TPU v7x, 32 devices: a whole 2x2x4 slice. The times are simulated.
32 devices in a mesh: tp: 2 (over y), dp: 4 (over z), rep: 4 (over x, core).
Axes of the slice: x: 2, y: 2, z: 4, core: 2. Of those that a mesh axis runs over, the one named last changes fastest.
Arguments:
- layer_input: bfloat16 [16, 1024, 768], P(('dp', 'rep'), 'tp'), may hold values from -6 to 6
- history: bfloat16 [4, 16, 1024, 768], P(None, ('dp', 'rep'), 'tp'), may hold values from -6 to 6
- cotangent: bfloat16 [16, 1024, 768], P(('dp', 'rep'), 'tp'), may hold values from -6 to 6
- lengths: int32 [16, 3], P(('dp', 'rep')), may hold values from 1 to 512, 1024 in all within a row
- dwa_weights: float32 [5], replicated, may hold values from 0.2 to 1
- gain_one: float32 [768], replicated, may hold values from 0.1 to 1.9
- bias_one: float32 [768], replicated, may hold values from -3 to 3
- w_qkv: bfloat16 [3, 768, 768], P(None, None, 'tp'), may hold values from -0.21875 to 0.21875
- w_out: bfloat16 [768, 768], P('tp'), may hold values from -1.75 to 1.75
- gain_two: float32 [768], replicated, may hold values from 0.1 to 1.9
- bias_two: float32 [768], replicated, may hold values from -3 to 3
- w_up: bfloat16 [768, 3072], P(None, 'tp'), may hold values from -0.21875 to 0.21875
- w_down: bfloat16 [3072, 768], P('tp'), may hold values from -0.109375 to 0.109375
Outputs:
- output: bfloat16 [16, 1024, 768], P(('dp', 'rep'), 'tp')
- grad_input: bfloat16 [16, 1024, 768], P(('dp', 'rep'), 'tp')
- grad_history: bfloat16 [4, 16, 1024, 768], P(None, ('dp', 'rep'), 'tp')
- grad_dwa: float32 [5], replicated
- grad_gain_one: float32 [768], replicated
- grad_bias_one: float32 [768], replicated
- grad_w_qkv: float32 [3, 768, 768], P(None, 'dp', 'tp')
- grad_w_out: float32 [768, 768], P('tp', 'dp')
- grad_gain_two: float32 [768], replicated
- grad_bias_two: float32 [768], replicated
- grad_w_up: float32 [768, 3072], P('dp', 'tp')
- grad_w_down: float32 [3072, 768], P('tp', 'dp')
Inputs may be any that keep to these rules, and one draw needn't show every extreme that they name: Row g lists in order the lengths of the 3 sequences packed into group g; they sum to 1024 and the largest of each row is 512.
All inputs are finite; a program needn't handle non-finite values.
Results may differ from a plain program's by a relative error of at most 0.02.
Values may be sent and summed in bfloat16 or wider, within the bound.
No kernel may reach another device: no remote copies, remote signals or barrier semaphores. Data moves between devices by JAX's collectives and lax.ppermute only.
A program may use at most 128 MiB of HBM per device.

v0:
```python
import functools
import itertools
import math

import jax
import jax.numpy as jnp
from jax import lax
from jax.experimental import pallas as pl
from jax.experimental.pallas import tpu as pltpu
from jax.sharding import Mesh, PartitionSpec as P

HEAD_DIM = 64
LONGEST = 512
NEG_FILL = -1e30
NORM_EPS = 1e-05
RATE = 3e6
ROOM = 60 << 20


def lasting(microseconds):
    return pl.CostEstimate(flops=0, transcendentals=0, bytes_accessed=int(microseconds * RATE))


BLOCK = 256
LANES = 128
NT = (((1,), (1,)), ((), ()))


def dot(a, b, dims=(((1,), (0,)), ((), ()))):
    return lax.dot_general(a, b, dims, preferred_element_type=jnp.float32)


def spans(whole, reach):
    back = -(-(reach - 1) // BLOCK)
    runs = []
    for i in range(whole // BLOCK):
        count = min(i, back) + 1
        if runs and runs[-1][2] == count:
            runs[-1][1] = i + 1
        else:
            runs.append([i, i + 1, count])
    return runs


def each_block(whole, reach, body):
    for first, last, count in spans(whole, reach):
        def step(at, carry, first=first, count=count):
            i = first + at // 2
            body(i, i + 1 - count, count * BLOCK, at % 2)
            return carry
        lax.fori_loop(0, 2 * (last - first), step, 0)


def attend_kernel(reach, start_ref, q_ref, k_ref, v_ref, out_ref, acc_ref):
    whole = q_ref.shape[0]
    lane = lax.broadcasted_iota(jnp.int32, (BLOCK, LANES), 1) // HEAD_DIM

    def body(i, first, count, head):
        at = pl.ds(pl.multiple_of(i * BLOCK, BLOCK), BLOCK)
        keys = pl.ds(pl.multiple_of(first * BLOCK, BLOCK), count)
        query = q_ref[at, :] * (HEAD_DIM**-0.5)
        query = jnp.where(lane == head, query, jnp.zeros_like(query))
        scores = dot(query, k_ref[keys, :], NT)
        key_at = first * BLOCK + lax.broadcasted_iota(jnp.int32, scores.shape, 1)
        query_at = i * BLOCK + lax.broadcasted_iota(jnp.int32, scores.shape, 0)
        allowed = (key_at >= start_ref[at, :1]) & (key_at <= query_at)
        scores = jnp.where(allowed, scores, NEG_FILL)
        exponent = jnp.exp(scores - jnp.max(scores, axis=1, keepdims=True))
        row_sum = jnp.sum(exponent, axis=1, keepdims=True)
        probs = (exponent * (1.0 / row_sum)).astype(jnp.bfloat16)
        mixed = dot(probs, v_ref[keys, :])

        @pl.when(head == 0)
        def _():
            acc_ref[...] = mixed

        @pl.when(head == 1)
        def _():
            out_ref[at, :] = jnp.where(lane == 0, acc_ref[...], mixed).astype(out_ref.dtype)

    each_block(whole, reach, body)


def attend(pair, start_column, projected, so_far, reach):
    count, whole, width = projected.shape

    def block(c):
        return pl.BlockSpec((None, whole, LANES), lambda i: (c, 0, pair))

    begun = [] if so_far is None else [so_far]
    kernel = attend_kernel if so_far is None else lambda reach, unused, *refs: attend_kernel(reach, *refs)
    return pl.pallas_call(
        functools.partial(kernel, reach),
        grid=(1,),
        in_specs=[pl.BlockSpec(memory_space=pl.ANY)] * len(begun)
        + [pl.BlockSpec((whole, LANES), lambda i: (0, 0)), block(0), block(1), block(2)],
        out_specs=pl.BlockSpec((whole, LANES), lambda i: (0, pair)),
        out_shape=jax.ShapeDtypeStruct((whole, width), jnp.bfloat16),
        scratch_shapes=[pltpu.VMEM((BLOCK, LANES), jnp.float32)],
        input_output_aliases={0: 0} if begun else {},
        compiler_params=pltpu.CompilerParams(vmem_limit_bytes=ROOM),
        cost_estimate=lasting(5),
    )(*begun, start_column, projected, projected, projected)


def turn_back(field, cos, sin):
    half = HEAD_DIM // 2
    lane = lax.broadcasted_iota(jnp.int32, field.shape, 1) % HEAD_DIM
    crossed = jnp.where(lane < half, pltpu.roll(field, LANES - half, 1), pltpu.roll(field, half, 1))
    return field * cos - crossed * sin


def attend_back_kernel(
    reach, start_ref, cos_ref, sin_ref, q_ref, k_ref, v_ref, g_ref, out_ref,
    key_acc, value_acc, query_acc,
):
    whole = q_ref.shape[0]
    lane = lax.broadcasted_iota(jnp.int32, (BLOCK, LANES), 1) // HEAD_DIM
    key_acc[...] = jnp.zeros_like(key_acc)
    value_acc[...] = jnp.zeros_like(value_acc)

    def body(i, first, count, head):
        at = pl.ds(pl.multiple_of(i * BLOCK, BLOCK), BLOCK)
        span = pl.ds(pl.multiple_of(first * BLOCK, BLOCK), count)
        query = q_ref[at, :] * (HEAD_DIM**-0.5)
        query = jnp.where(lane == head, query, jnp.zeros_like(query))
        grad = g_ref[at, :]
        grad = jnp.where(lane == head, grad, jnp.zeros_like(grad))
        keys = k_ref[span, :]
        scores = dot(keys, query, NT)
        key_at = first * BLOCK + lax.broadcasted_iota(jnp.int32, scores.shape, 0)
        query_at = i * BLOCK + lax.broadcasted_iota(jnp.int32, scores.shape, 1)
        allowed = (key_at >= start_ref[:1, at]) & (key_at <= query_at)
        scores = jnp.where(allowed, scores, NEG_FILL)
        exponent = jnp.exp(scores - jnp.max(scores, axis=0, keepdims=True))
        probs = exponent * (1.0 / jnp.sum(exponent, axis=0, keepdims=True))
        value_acc[span, :] += dot(probs.astype(jnp.bfloat16), grad)
        grad_probs = dot(v_ref[span, :], grad, NT)
        weighted = probs * grad_probs
        grad_scores = (weighted - probs * jnp.sum(weighted, axis=0, keepdims=True)).astype(jnp.bfloat16)
        key_acc[span, :] += dot(grad_scores, query)
        here = dot(grad_scores, keys, (((0,), (0,)), ((), ())))

        @pl.when(head == 0)
        def _():
            query_acc[...] = here

        @pl.when(head == 1)
        def _():
            both = jnp.where(lane == 0, query_acc[...], here) * (HEAD_DIM**-0.5)
            out_ref[0, at, :] = turn_back(both, cos_ref[at, :], sin_ref[at, :]).astype(out_ref.dtype)

    each_block(whole, reach, body)

    def finish(i, carry):
        at = pl.ds(pl.multiple_of(i * BLOCK, BLOCK), BLOCK)
        out_ref[1, at, :] = turn_back(key_acc[at, :], cos_ref[at, :], sin_ref[at, :]).astype(out_ref.dtype)
        out_ref[2, at, :] = value_acc[at, :].astype(out_ref.dtype)
        return carry

    lax.fori_loop(0, whole // BLOCK, finish, 0)


def attend_back(pair, start_row, cos, sin, projected, grad_mixed, so_far, reach):
    count, whole, width = projected.shape

    def block(c):
        return pl.BlockSpec((None, whole, LANES), lambda i: (c, 0, pair))

    table = pl.BlockSpec((whole, LANES), lambda i: (0, 0))
    begun = [] if so_far is None else [so_far]
    kernel = attend_back_kernel if so_far is None else lambda reach, unused, *refs: attend_back_kernel(reach, *refs)
    return pl.pallas_call(
        functools.partial(kernel, reach),
        grid=(1,),
        in_specs=[pl.BlockSpec(memory_space=pl.ANY)] * len(begun)
        + [
            pl.BlockSpec((8, whole), lambda i: (0, 0)),
            table,
            table,
            block(0),
            block(1),
            block(2),
            pl.BlockSpec((whole, LANES), lambda i: (0, pair)),
        ],
        out_specs=pl.BlockSpec((count, whole, LANES), lambda i: (0, 0, pair)),
        out_shape=jax.ShapeDtypeStruct((count, whole, width), jnp.bfloat16),
        scratch_shapes=[
            pltpu.VMEM((whole, LANES), jnp.float32),
            pltpu.VMEM((whole, LANES), jnp.float32),
            pltpu.VMEM((BLOCK, LANES), jnp.float32),
        ],
        input_output_aliases={0: 0} if begun else {},
        compiler_params=pltpu.CompilerParams(vmem_limit_bytes=ROOM),
        cost_estimate=lasting(9),
    )(*begun, start_row, cos, sin, projected, projected, projected, grad_mixed)


ROWS = 256


def norm_parts(field):
    centered = field - jnp.mean(field, axis=-1, keepdims=True)
    scale = lax.rsqrt(jnp.mean(centered * centered, axis=-1, keepdims=True) + NORM_EPS)
    return centered * scale, scale


def wide(ref, at):
    return ref[at, :].astype(jnp.float32)


def row_blocks(count, body):
    def step(i, carry):
        body(i, pl.ds(pl.multiple_of(i * ROWS, ROWS), ROWS))
        return carry

    lax.fori_loop(0, count // ROWS, step, 0)


def whole_spec(shape):
    return pl.BlockSpec(shape, lambda *at: (0,) * len(shape))


def turn(field, cos, sin):
    half = HEAD_DIM // 2
    lane = lax.broadcasted_iota(jnp.int32, field.shape, 1) % HEAD_DIM
    crossed = jnp.where(lane < half, pltpu.roll(field, LANES - half, 1), pltpu.roll(field, half, 1))
    return field * cos + crossed * sin


def project_kernel(
    flags, rows_ref, vectors, cos_ref, sin_ref, w_own, w_got, out_ref, turned_ref,
    weight_ref, norm_ref,
):
    whole = rows_ref.shape[0]
    step = pl.program_id(0)

    @pl.when(step == 0)
    def _():
        def body(i, at):
            unit, unused = norm_parts(wide(rows_ref, at))
            norm = unit * vectors[0:1, :] + vectors[1:2, :]
            norm_ref[at, :] = norm.astype(jnp.bfloat16)
            turned_ref[:, at] = norm.T.astype(jnp.bfloat16)

        row_blocks(whole, body)

    weight_ref[0] = jnp.where(flags[0] == 1, w_own[0], w_got[0])

    def body(i, at):
        field = dot(norm_ref[at, :], weight_ref[0])

        @pl.when(step < 2)
        def _():
            for p in range(field.shape[1] // LANES):
                lanes = slice(p * LANES, (p + 1) * LANES)
                out_ref[0, at, lanes] = turn(field[:, lanes], cos_ref[at, :], sin_ref[at, :]).astype(
                    jnp.bfloat16
                )

        @pl.when(step == 2)
        def _():
            out_ref[0, at, :] = field.astype(jnp.bfloat16)

    row_blocks(whole, body)


def project(flags, rows, vectors, cos, sin, w_own, w_got):
    whole, width = rows.shape
    count, unused, columns = w_own.shape
    weight = pl.BlockSpec((1, width, columns), lambda c, flags: (c, 0, 0))
    return pl.pallas_call(
        project_kernel,
        grid_spec=pltpu.PrefetchScalarGridSpec(
            num_scalar_prefetch=1,
            grid=(count,),
            in_specs=[
                whole_spec((whole, width)),
                whole_spec(vectors.shape),
                whole_spec((whole, LANES)),
                whole_spec((whole, LANES)),
                weight,
                weight,
            ],
            out_specs=[
                pl.BlockSpec((1, whole, columns), lambda c, flags: (c, 0, 0)),
                whole_spec((width, whole)),
                weight,
            ],
            scratch_shapes=[pltpu.VMEM((whole, width), jnp.bfloat16)],
        ),
        out_shape=[
            jax.ShapeDtypeStruct((count, whole, columns), jnp.bfloat16),
            jax.ShapeDtypeStruct((width, whole), jnp.bfloat16),
            jax.ShapeDtypeStruct(w_own.shape, jnp.bfloat16),
        ],
        compiler_params=pltpu.CompilerParams(vmem_limit_bytes=ROOM),
        cost_estimate=lasting(9),
    )(flags, rows, vectors, cos, sin, w_own, w_got)


HIDDEN = 256


def gelu_both(up):
    root = math.sqrt(2.0 / math.pi)
    square = up * up
    bent = jnp.tanh(root * up * (1.0 + 0.044715 * square))
    half = 0.5 * (1.0 + bent)
    slope = half + 0.5 * up * (1.0 - bent * bent) * (root * (1.0 + 3.0 * 0.044715 * square))
    return up * half, slope


def feed_kernel(early, flags, *refs):
    if early:
        weight_ref, rows_ref, own_ref, got_ref, cot_ref, vectors = refs[:6]
        up_own, down_own, got, norm, norm_t, grad, grad_t = refs[6:13]
    else:
        norm, norm_t, grad, grad_t, back_early, up_own, down_own, got = refs[:8]
    back_ref, act_ref, pieces_ref, down_ref, slope, up_w = refs[-6:]
    whole, width = norm.shape
    part = pieces_ref.shape[2]
    step = pl.program_id(0)

    @pl.when(step == 0)
    def _():
        up_w[...] = jnp.where(flags[0] == 1, up_own[...], got[:width])
        down_ref[...] = jnp.where(flags[0] == 1, down_own[...], got[width:])
        if early:

            def body(i, at):
                unit, unused = norm_parts(wide(rows_ref, at) + wide(own_ref, at) + wide(got_ref, at))
                field = unit * vectors[2:3, :] + vectors[3:4, :]
                norm[at, :] = field.astype(jnp.bfloat16)
                norm_t[:, at] = field.T.astype(jnp.bfloat16)
                field = wide(cot_ref, at) * weight_ref[weight_ref.shape[0] - 1]
                grad[at, :] = field.astype(jnp.bfloat16)
                grad_t[:, at] = field.T.astype(jnp.bfloat16)

            row_blocks(whole, body)

    hidden = pl.ds(pl.multiple_of(step * HIDDEN, HIDDEN), HIDDEN)
    up_block = up_w[:, hidden]
    down_block = down_ref[hidden, :]

    def body(i, at):
        value, rise = gelu_both(dot(norm[at, :], up_block))
        act_ref[at, :] = value.astype(jnp.bfloat16)
        slope[at, hidden] = (dot(grad[at, :], down_block, NT) * rise).astype(jnp.bfloat16)

    row_blocks(whole, body)

    def grads(i, at):
        fields = (dot(norm_t[at, :], slope[:, hidden]), dot(grad_t[at, :], act_ref[...]))
        for k, field in enumerate(fields):
            field = field.astype(jnp.bfloat16)
            for j in range(2 * part // HIDDEN):

                @pl.when(step == j)
                def _():
                    for p in range(2):
                        first, last = max(p * part, j * HIDDEN), min((p + 1) * part, (j + 1) * HIDDEN)
                        if first < last:
                            pieces_ref[2 * k + p, at, first - p * part : last - p * part] = field[
                                :, first - j * HIDDEN : last - j * HIDDEN
                            ]

    row_blocks(width, grads)

    @pl.when(step == pl.num_programs(0) - 1)
    def _():
        def body(i, at):
            back = dot(slope[at, :], up_w[...], NT)
            if not early:
                back = back + back_early[at, :]
            back_ref[at, :] = back.astype(back_ref.dtype)

        row_blocks(whole, body)


def feed(early, flags, head, w_up, w_down, got):
    whole, width = head[1].shape if early else head[0].shape
    hidden = w_up.shape[1] // 2
    steps = hidden // HIDDEN
    tokens = whole_spec((whole, width))
    turned = whole_spec((width, whole))
    index = 0 if early else 1
    low = jax.ShapeDtypeStruct((whole, width), jnp.bfloat16)
    low_turned = jax.ShapeDtypeStruct((width, whole), jnp.bfloat16)
    full = jax.ShapeDtypeStruct((whole, width), jnp.float32)
    if early:
        head_specs = [pl.BlockSpec(memory_space=pltpu.SMEM)] + [tokens] * 4
        head_specs = head_specs + [whole_spec(head[-1].shape)]
    else:
        head_specs = [tokens, turned, tokens, turned, tokens]
    return pl.pallas_call(
        functools.partial(feed_kernel, early),
        grid_spec=pltpu.PrefetchScalarGridSpec(
            num_scalar_prefetch=1,
            grid=(steps,),
            in_specs=head_specs
            + [
                pl.BlockSpec((width, hidden), lambda j, flags: (0, index)),
                pl.BlockSpec((hidden, width), lambda j, flags: (index, 0)),
                whole_spec(got.shape),
            ],
            out_specs=([tokens, turned, tokens, turned] if early else [])
            + [
                tokens,
                pl.BlockSpec((whole, HIDDEN), lambda j, flags: (0, j)),
                whole_spec((4, width, hidden // 2)),
                whole_spec((hidden, width)),
            ],
            scratch_shapes=[
                pltpu.VMEM((whole, hidden), jnp.bfloat16),
                pltpu.VMEM((width, hidden), jnp.bfloat16),
            ],
        ),
        out_shape=([low, low_turned, low, low_turned, full] if early else [low])
        + [
            jax.ShapeDtypeStruct((whole, hidden), jnp.bfloat16),
            jax.ShapeDtypeStruct((4, width, hidden // 2), jnp.bfloat16),
            jax.ShapeDtypeStruct((hidden, width), jnp.bfloat16),
        ],
        compiler_params=pltpu.CompilerParams(vmem_limit_bytes=ROOM),
        cost_estimate=lasting(20),
    )(flags, *head, w_up, w_down, got)


def lower_kernel(flags, act_early, act_late, early_ref, late_ref, rows_ref, own_ref, got_ref, keep_ref, send_ref):
    half = keep_ref.shape[0]
    first, second = early_ref[...], late_ref[...]

    def at_rows(near, i):
        return pl.ds(pl.multiple_of(near * half + i * ROWS, ROWS), ROWS)

    def send(i, at):
        here = at_rows(1 - flags[1], i)
        total = dot(act_early[here, :], first) + dot(act_late[here, :], second)
        send_ref[at, :] = total.astype(jnp.bfloat16)

    def keep(i, at):
        here = at_rows(flags[1], i)
        total = dot(act_early[here, :], first) + dot(act_late[here, :], second)
        keep_ref[at, :] = total + wide(rows_ref, here) + wide(own_ref, here) + wide(got_ref, here)

    row_blocks(half, send)
    row_blocks(half, keep)


def lower(flags, act_early, act_late, down_early, down_late, rows, own, got):
    whole, hidden = act_early.shape
    width = rows.shape[1]
    half = whole_spec((whole // 2, width))
    return pl.pallas_call(
        lower_kernel,
        grid_spec=pltpu.PrefetchScalarGridSpec(
            num_scalar_prefetch=1,
            grid=(1,),
            in_specs=[whole_spec((whole, hidden))] * 2
            + [whole_spec((hidden, width))] * 2
            + [whole_spec((whole, width))] * 3,
            out_specs=[half, half],
        ),
        out_shape=[
            jax.ShapeDtypeStruct((whole // 2, width), jnp.float32),
            jax.ShapeDtypeStruct((whole // 2, width), jnp.bfloat16),
        ],
        compiler_params=pltpu.CompilerParams(vmem_limit_bytes=ROOM),
        cost_estimate=lasting(7),
    )(flags, act_early, act_late, down_early, down_late, rows, own, got)


def middle_kernel(
    flags, weight_ref, rows_ref, own_ref, got_ref, cot_ref, back_own, back_got, vectors, mixed_ref,
    w_ref, grad_ref, gmixed_ref, gout_ref, sums_ref, turned,
):
    whole, width = rows_ref.shape
    weight = w_ref[...]
    gain = vectors[2:3, :]
    sums_ref[...] = jnp.zeros_like(sums_ref)

    def body(i, at):
        unit, scale = norm_parts(wide(rows_ref, at) + wide(own_ref, at) + wide(got_ref, at))
        back = wide(back_own, at) + wide(back_got, at)
        inner = back * gain
        mean = jnp.mean(inner, axis=-1, keepdims=True)
        slant = jnp.mean(inner * unit, axis=-1, keepdims=True)
        grad = wide(cot_ref, at) * weight_ref[weight_ref.shape[0] - 1] + scale * (inner - mean - unit * slant)
        low = grad.astype(jnp.bfloat16)
        grad_ref[at, :] = low
        turned[:, at] = grad.T.astype(jnp.bfloat16)
        gmixed_ref[at, :] = dot(low, weight, NT).astype(jnp.bfloat16)

        @pl.when((i * ROWS) // (whole // 2) == flags[1])
        def _():
            sums_ref[0:1, :] += jnp.sum(back * unit, axis=0, keepdims=True)
            sums_ref[1:2, :] += jnp.sum(back, axis=0, keepdims=True)

    row_blocks(whole, body)

    def grads(i, at):
        gout_ref[at, :] = dot(turned[at, :], mixed_ref[...]).astype(jnp.bfloat16)

    row_blocks(width, grads)


def middle(flags, weight, rows, own, got, cot, back_own, back_got, vectors, mixed, w_out):
    whole, width = rows.shape
    columns = mixed.shape[1]
    tokens = whole_spec((whole, width))
    narrow = whole_spec((whole, columns))
    projection = whole_spec((columns, width))
    return pl.pallas_call(
        middle_kernel,
        grid_spec=pltpu.PrefetchScalarGridSpec(
            num_scalar_prefetch=1,
            grid=(1,),
            in_specs=[pl.BlockSpec(memory_space=pltpu.SMEM)]
            + [tokens] * 6
            + [whole_spec(vectors.shape), narrow, projection],
            out_specs=[tokens, narrow, whole_spec((width, columns)), whole_spec((8, width))],
            scratch_shapes=[pltpu.VMEM((width, whole), jnp.bfloat16)],
        ),
        out_shape=[
            jax.ShapeDtypeStruct((whole, width), jnp.bfloat16),
            jax.ShapeDtypeStruct((whole, columns), jnp.bfloat16),
            jax.ShapeDtypeStruct((width, columns), jnp.bfloat16),
            jax.ShapeDtypeStruct((8, width), jnp.float32),
        ],
        compiler_params=pltpu.CompilerParams(vmem_limit_bytes=ROOM),
        cost_estimate=lasting(12),
    )(flags, weight, rows, own, got, cot, back_own, back_got, vectors, mixed, w_out)


def weigh_kernel(flags, turned_ref, grad_ref, out_grad_ref, *out_refs):
    last = grad_ref.shape[0]

    def grads(i, at):
        for j, out_ref in enumerate(out_refs):
            piece = flags[3 + j]

            @pl.when(piece < last)
            def _():
                out_ref[at, :] = dot(turned_ref[at, :], grad_ref[jnp.minimum(piece, last - 1)]).astype(
                    jnp.bfloat16
                )

            @pl.when(piece == last)
            def _():
                out_ref[at, :] = out_grad_ref[at, :]

    row_blocks(turned_ref.shape[0], grads)


def weigh(flags, turned, grad, out_grad):
    width, whole = turned.shape
    columns = grad.shape[2]
    piece = whole_spec((width, columns))
    return pl.pallas_call(
        weigh_kernel,
        grid_spec=pltpu.PrefetchScalarGridSpec(
            num_scalar_prefetch=1,
            grid=(1,),
            in_specs=[whole_spec((width, whole)), whole_spec(grad.shape), piece],
            out_specs=[piece] * 4,
        ),
        out_shape=[jax.ShapeDtypeStruct((width, columns), jnp.bfloat16)] * 4,
        compiler_params=pltpu.CompilerParams(vmem_limit_bytes=ROOM),
        cost_estimate=lasting(3),
    )(flags, turned, grad, out_grad)


def unproject_kernel(flags, grad_ref, weight, keep_ref, send_ref):
    half = keep_ref.shape[0]

    def side(near, out_ref):
        def body(i, at):
            from_rows = pl.ds(pl.multiple_of(near * half + i * ROWS, ROWS), ROWS)
            total = dot(grad_ref[0, from_rows, :], weight[0], NT)
            for c in range(1, grad_ref.shape[0]):
                total = total + dot(grad_ref[c, from_rows, :], weight[c], NT)
            out_ref[at, :] = total.astype(out_ref.dtype)

        row_blocks(half, body)

    side(1 - flags[1], send_ref)
    side(flags[1], keep_ref)


def unproject(flags, grad, weight):
    count, whole, columns = grad.shape
    width = weight.shape[1]
    half = whole_spec((whole // 2, width))
    return pl.pallas_call(
        unproject_kernel,
        grid_spec=pltpu.PrefetchScalarGridSpec(
            num_scalar_prefetch=1,
            grid=(1,),
            in_specs=[whole_spec(grad.shape), whole_spec((count, width, columns))],
            out_specs=[half, half],
        ),
        out_shape=[
            jax.ShapeDtypeStruct((whole // 2, width), jnp.float32),
            jax.ShapeDtypeStruct((whole // 2, width), jnp.bfloat16),
        ],
        compiler_params=pltpu.CompilerParams(vmem_limit_bytes=ROOM),
        cost_estimate=lasting(4),
    )(flags, grad, weight)


def last_kernel(
    flags, rows_ref, keep_ref, got_ref, resid_ref, vectors, block_keep, block_got, cot_ref, out_ref, sums_ref
):
    sums_ref[...] = jnp.zeros_like(sums_ref)

    def body(i, at):
        unit, scale = norm_parts(wide(rows_ref, at))
        back = keep_ref[at, :] + wide(got_ref, at)
        inner = back * vectors[0:1, :]
        mean = jnp.mean(inner, axis=-1, keepdims=True)
        slant = jnp.mean(inner * unit, axis=-1, keepdims=True)
        grad = wide(resid_ref, at) + scale * (inner - mean - unit * slant)
        out_ref[0, at, :] = grad.astype(jnp.bfloat16)
        block = block_keep[at, :] + wide(block_got, at)
        out_ref[1, at, :] = block.astype(jnp.bfloat16)
        sums_ref[0:1, :] += jnp.sum(back * unit, axis=0, keepdims=True)
        sums_ref[1:2, :] += jnp.sum(back, axis=0, keepdims=True)
        sums_ref[2:3, :] += jnp.sum(block * wide(cot_ref, at), axis=0, keepdims=True)

    row_blocks(rows_ref.shape[0], body)


def last(flags, rows, keep, got, resid, vectors, block_keep, block_got, cot):
    half, width = keep.shape
    mine = pl.BlockSpec((half, width), lambda i, flags: (flags[1], 0))
    tokens = whole_spec((half, width))
    return pl.pallas_call(
        last_kernel,
        grid_spec=pltpu.PrefetchScalarGridSpec(
            num_scalar_prefetch=1,
            grid=(1,),
            in_specs=[mine, tokens, tokens, mine, whole_spec(vectors.shape), tokens, tokens, mine],
            out_specs=[whole_spec((2, half, width)), whole_spec((8, width))],
        ),
        out_shape=[
            jax.ShapeDtypeStruct((2, half, width), jnp.bfloat16),
            jax.ShapeDtypeStruct((8, width), jnp.float32),
        ],
        compiler_params=pltpu.CompilerParams(vmem_limit_bytes=ROOM),
        cost_estimate=lasting(3),
    )(flags, rows, keep, got, resid, vectors, block_keep, block_got, cot)


def past_kernel(dwa_ref, hist_ref, cot_ref, grad_ref, part_ref, sums_ref):
    @pl.when(pl.program_id(0) == 0)
    def _():
        sums_ref[...] = jnp.zeros_like(sums_ref)

    grad = cot_ref[...].astype(jnp.float32)
    total = jnp.zeros_like(grad)
    for j in range(hist_ref.shape[0]):
        field = hist_ref[j].astype(jnp.float32)
        total += dwa_ref[j] * field
        grad_ref[j] = (dwa_ref[j] * grad).astype(jnp.bfloat16)
        sums_ref[j : j + 1, :] += jnp.sum(field * grad, axis=0, keepdims=True)
    part_ref[...] = total


def past(dwa, history, cot):
    count, rows, width = history.shape
    layers = pl.BlockSpec((count, ROWS, width), lambda i: (0, i, 0))
    tokens = pl.BlockSpec((ROWS, width), lambda i: (i, 0))
    return pl.pallas_call(
        past_kernel,
        grid=(rows // ROWS,),
        in_specs=[pl.BlockSpec(memory_space=pltpu.SMEM), layers, tokens],
        out_specs=[layers, tokens, whole_spec((8, width))],
        out_shape=[
            jax.ShapeDtypeStruct(history.shape, jnp.bfloat16),
            jax.ShapeDtypeStruct((rows, width), jnp.float32),
            jax.ShapeDtypeStruct((8, width), jnp.float32),
        ],
        compiler_params=pltpu.CompilerParams(vmem_limit_bytes=ROOM),
        cost_estimate=lasting(3),
    )(dwa, history, cot)


def present_kernel(flags, weight_ref, part_ref, own_ref, got_ref, out_ref, grad_ref):
    here = jnp.where(flags[0] == 1, own_ref[1], got_ref[1]).astype(jnp.float32)
    out_ref[...] = (part_ref[...] + weight_ref[weight_ref.shape[0] - 1] * here).astype(jnp.bfloat16)
    grad_ref[...] = jnp.where(flags[0] == 1, own_ref[0], got_ref[0])


def present(flags, weight, part, own, got):
    rows, width = part.shape
    scalars = pl.BlockSpec(memory_space=pltpu.SMEM)
    tokens = pl.BlockSpec((ROWS, width), lambda i: (i, 0))
    both = pl.BlockSpec((2, ROWS, width), lambda i: (0, i, 0))
    return pl.pallas_call(
        present_kernel,
        grid=(rows // ROWS,),
        in_specs=[scalars, scalars, tokens, both, both],
        out_specs=[tokens, tokens],
        out_shape=[jax.ShapeDtypeStruct((rows, width), jnp.bfloat16)] * 2,
        compiler_params=pltpu.CompilerParams(vmem_limit_bytes=ROOM),
        cost_estimate=lasting(2),
    )(flags, weight, part, own, got)


AXES = ("tp", "dp", "far", "near")


def moves(chosen, move):
    sizes = [lax.axis_size(name) for name in AXES]
    places = [place for place in itertools.product(*map(range, sizes)) if chosen(*place)]
    index = lambda place: functools.reduce(lambda at, step: at * step[0] + step[1], zip(sizes, place), 0)
    return [(index(place), index(move(*place))) for place in places]


def away(t, d, k, c):
    return t != c


def anyone(t, d, k, c):
    return True


def home(t, d, k, c):
    return t == c


def swap_diagonal(field):
    return lax.ppermute(field, AXES, moves(away, lambda t, d, k, c: (c, d, k, t)))


def send_to_owner(field, other_far, other_tp):
    return lax.ppermute(
        field,
        AXES,
        moves(
            away if not other_far and not other_tp else anyone,
            lambda t, d, k, c: (c, d, k ^ other_far, t ^ other_tp),
        ),
    )


def bring_home(field):
    return lax.ppermute(field, AXES, moves(away, lambda t, d, k, c: (c, d, k, c)))


def swap_far_home(field):
    return lax.ppermute(field, AXES, moves(home, lambda t, d, k, c: (t, d, 1 - k, c)))


def swap_far(field):
    return lax.ppermute(field, "far", [(0, 1), (1, 0)])


def swap_near(field):
    return lax.ppermute(field, "near", [(0, 1), (1, 0)])


def after(field, *others):
    return lax.optimization_barrier((field, *others))[0]


def ordered(own, other, first, axis=0):
    return jnp.where(
        first, jnp.concatenate([own, other], axis=axis), jnp.concatenate([other, own], axis=axis)
    )


def part_of(field, index, axis):
    size = field.shape[axis] // 2
    return lax.dynamic_slice_in_dim(field, index * size, size, axis)


def add(*fields):
    return sum(field.astype(jnp.float32) for field in fields).astype(jnp.bfloat16)


def scatter_plane(pieces):
    return lax.psum_scatter(pieces, ("tp", "far"), scatter_dimension=0, tiled=True)[0]


def scatter_rows(piece):
    return lax.psum_scatter(piece, "dp", scatter_dimension=0, tiled=True)


def gather(piece, part, far, same):
    pair = ordered(piece[None], bring_home(piece)[None], part == 0)
    pairs = ordered(pair[None], swap_far_home(pair)[None], far == 0)
    return jnp.where(same, pairs, swap_near(pairs))


def sum_everywhere(field):
    for name in ("near", "far", "tp", "dp"):
        size = lax.axis_size(name)
        bit = 1
        while bit < size:
            field = field + lax.ppermute(field, name, [(d, d ^ bit) for d in range(size)])
            bit *= 2
    return field


def local(
    layer_input,
    history,
    cotangent,
    lengths,
    dwa_weights,
    gain_one,
    bias_one,
    w_qkv,
    w_out,
    gain_two,
    bias_two,
    w_up,
    w_down,
):
    rows = layer_input.shape[1]
    whole = rows * lax.axis_size("tp")
    hist_count = history.shape[0]
    part, far, near = lax.axis_index("tp"), lax.axis_index("far"), lax.axis_index("near")
    same = near == part
    pieces = [2 * (far ^ a) + (part ^ b) for a in range(2) for b in range(2)]
    flags = jnp.stack([same.astype(jnp.int32), near, far, *pieces])

    input_got = swap_diagonal(layer_input[0])
    qkv_got = swap_diagonal(w_qkv)
    early_got = jnp.concatenate([part_of(w_up, 0, 1), part_of(w_down, 0, 0)], axis=0)
    late_got = jnp.concatenate([part_of(w_up, 1, 1), part_of(w_down, 1, 0)], axis=0)
    last_own = jnp.concatenate([w_out, cotangent[0]], axis=0)
    vectors = jnp.stack([gain_one, bias_one, gain_two, bias_two])

    own_lengths = jnp.where(same, lengths, swap_near(lengths))[0]
    seq_owner, token_place = positions(own_lengths, whole)
    seq_begin = jnp.arange(whole, dtype=jnp.int32) - token_place
    start_column = jnp.broadcast_to(seq_begin[:, None], (whole, LANES))
    start_row = jnp.broadcast_to(seq_begin[None, :], (8, whole))
    half_dim = HEAD_DIM // 2
    lane = jnp.arange(LANES, dtype=jnp.int32)
    frequency = jnp.exp((lane % half_dim).astype(jnp.float32) * (-math.log(10000.0) / half_dim))
    angles = token_place.astype(jnp.float32)[:, None] * frequency[None, :]
    cos_table = jnp.cos(angles)
    sin_table = jnp.sin(angles) * jnp.where(lane % HEAD_DIM < half_dim, -1.0, 1.0)[None, :]
    grad_history, past_sum, sums_past = past(dwa_weights, history[:, 0], cotangent[0])

    input_half = jnp.where(same, layer_input[0], input_got)
    layer_rows = ordered(input_half, swap_near(input_half), near == 0)
    layer_rows, last_own, early_got, late_got, vectors, past_sum, *tables = lax.optimization_barrier(
        (layer_rows, last_own, early_got, late_got, vectors, past_sum)
        + (cos_table, sin_table, start_column, start_row)
    )
    cos_table, sin_table, start_column, start_row = tables
    early_got = swap_diagonal(early_got)
    last_got = swap_diagonal(last_own)
    projected, norm_one_t, weight_qkv = project(
        flags, layer_rows, vectors, cos_table, sin_table, w_qkv, qkv_got
    )
    pairs = projected.shape[2] // LANES
    mixed = attend(0, start_column, projected, None, LONGEST)
    for pair in range(1, pairs):
        mixed = attend(pair, start_column, projected, mixed, LONGEST)
    late_got = swap_diagonal(after(late_got, mixed))
    last_got = jnp.where(same, last_own, last_got)
    weight_out = last_got[: w_out.shape[0]]
    attn = jnp.dot(mixed, weight_out, preferred_element_type=jnp.float32).astype(jnp.bfloat16)
    attn_got = swap_near(attn)
    cot_half = last_got[w_out.shape[0] :]
    cot_rows = ordered(cot_half, swap_near(cot_half), near == 0)
    head = (dwa_weights, layer_rows, attn, attn_got, cot_rows, vectors)
    *kept, act_early, early_pieces, down_early = feed(True, flags, head, w_up, w_down, early_got)
    early_sum = scatter_plane(after(early_pieces, late_got))
    back, act_late, late_pieces, down_late = feed(False, flags, kept, w_up, w_down, late_got)
    late_sum = scatter_plane(late_pieces)
    back_got = swap_near(back)
    grad_attn, grad_mixed, grad_out, sums_two = middle(
        flags,
        dwa_weights,
        layer_rows,
        attn,
        attn_got,
        cot_rows,
        back,
        back_got,
        vectors,
        mixed,
        weight_out,
    )

    grad_qkv = attend_back(0, start_row, cos_table, sin_table, projected, grad_mixed, None, LONGEST)
    for pair in range(1, pairs):
        grad_qkv = attend_back(
            pair, start_row, cos_table, sin_table, projected, grad_mixed, grad_qkv, LONGEST
        )
    owned = weigh(flags, norm_one_t, grad_qkv, grad_out)
    moved = [send_to_owner(owned[j], j // 2, j % 2) for j in range(4)]
    keep, send = unproject(flags, after(grad_qkv, owned[0]), weight_qkv)
    block_keep, block_send = lower(
        flags, after(act_early, send), act_late, down_early, down_late, layer_rows, attn, attn_got
    )
    feed_sum = scatter_rows(jnp.concatenate([after(early_sum, owned[0]), late_sum], axis=1))
    keep, send, block_keep, block_send, *moved = lax.optimization_barrier(
        (keep, send, block_keep, block_send, *moved)
    )
    ours, sums_one = last(
        flags,
        layer_rows,
        keep,
        swap_near(send),
        grad_attn,
        vectors,
        block_keep,
        swap_near(block_send),
        cot_rows,
    )
    attn_sum = scatter_rows(add(jnp.where(same, owned[0], moved[0]), *moved[1:]))
    theirs = swap_diagonal(ours)
    small = jnp.concatenate([sums_one[:3], sums_two[:2], sums_past[:hist_count]], axis=0)
    small = sum_everywhere(small)
    output, grad_input = present(flags, dwa_weights, past_sum, ours, after(theirs, small))
    feed_sum = after(feed_sum, output).reshape(feed_sum.shape[0], 2, -1).transpose(1, 0, 2)
    feed_all = gather(feed_sum, part, far, same)
    attn_sum = after(attn_sum, output)
    attn_pair = ordered(attn_sum[None], swap_near(attn_sum)[None], near == 0)
    attn_all = ordered(attn_pair, swap_far(attn_pair), far == 0)

    def columns_of(pieces):
        return pieces.transpose(2, 1, 0, 3).reshape(pieces.shape[2], -1).astype(jnp.float32)

    return (
        output[None],
        grad_input[None],
        grad_history[:, None],
        jnp.sum(jnp.concatenate([small[5:], small[2:3]], axis=0), axis=1),
        small[0],
        small[1],
        attn_all[:3].astype(jnp.float32),
        attn_all[3].astype(jnp.float32).T,
        small[3],
        small[4],
        columns_of(feed_all[:, 0]),
        columns_of(feed_all[:, 1]).T,
    )


def positions(seq_lengths, token_count):
    seq_ends = jnp.cumsum(seq_lengths)
    seq_starts = seq_ends - seq_lengths
    token_index = jnp.arange(token_count, dtype=jnp.int32)
    seq_owner = jnp.sum((token_index[:, None] >= seq_ends[None, :]).astype(jnp.int32), axis=1)
    picked = (
        seq_owner[:, None] == jnp.arange(seq_lengths.shape[0], dtype=jnp.int32)[None, :]
    ).astype(jnp.int32)
    seq_begin = jnp.sum(picked * seq_starts[None, :], axis=1)
    return (seq_owner, token_index - seq_begin)


def solution(mesh):
    tps, dps, reps = (mesh.shape[name] for name in ("tp", "dp", "rep"))
    split = Mesh(mesh.devices.reshape(tps, dps, reps // 2, 2), AXES)
    in_specs = (
        P(("dp", "far", "near"), "tp", None),
        P(None, ("dp", "far", "near"), "tp", None),
        P(("dp", "far", "near"), "tp", None),
        P(("dp", "far", "near"), None),
        P(),
        P(),
        P(),
        P(None, None, "tp"),
        P("tp", None),
        P(),
        P(),
        P(None, "tp"),
        P("tp", None),
    )
    out_specs = (
        P(("dp", "far", "near"), "tp", None),
        P(("dp", "far", "near"), "tp", None),
        P(None, ("dp", "far", "near"), "tp", None),
        P(),
        P(),
        P(),
        P(None, "dp", "tp"),
        P("tp", "dp"),
        P(),
        P(),
        P("dp", "tp"),
        P("tp", "dp"),
    )
    return jax.shard_map(local, mesh=split, in_specs=in_specs, out_specs=out_specs, check_vma=False)
```

profile of v0, /device:TPU:9, one launch (start us, length us, event | category | flops | bytes accessed | tf_op | source)
XLA Modules:
  0.0 340.8 jit_solution(12368787919847934580)
XLA Ops:
  8.0 3.1 collective-permute-start
  11.0 2.5 collective-permute-start.3
  13.6 3.0 fusion.9
  16.6 1.6 fusion.10
  18.7 4.3 %shard_map.220 = (bf16[4,512,768]{2,1,0:T(8,128)(2,1)}, f32[512,768]{1,0:T(8,128)}, f32[8,768]{1,0:T(8,128)}) custom-call(f32[5]{0:T(128)} %weight_ref.3, bf16[4,512,768]{2,1,0:T(8,128)(2,1)} %bitcast.61, bf16[512,768]{1,0:T(8,128)(2,1)} %bitcast.62), custom_call_target="tpu_custom_call" | custom-call | bytes 9000000 | tf_op jit(solution)/shard_map/pallas_call | solution.py:674
  23.6 4.0 %pad_maximum_fusion = (bf16[1536,768]{1,0:T(8,128)(2,1)}, bf16[1536,768]{1,0:T(8,128)(2,1)}) fusion(bf16[768,768]{1,0:T(8,128)(2,1)} %get-tuple-element.175, bf16[768,768]{1,0:T(8,128)(2,1)} %get-tuple-element.173, bf16[768,768]{1,0:T(8,128)(2,1)} %get-tuple-element.174, bf16[768,768]{1,0:T(8,128)(2,1)S(1)} %get-tuple-element.172), kind=kLoop, calls=%fused_computation | loop fusion | flops 9437184 | bytes 9437184 | tf_op jit(solution)/shard_map/concatenate | solution.py:832
  27.9 1.2 broadcast_select_fusion.5
  29.3 3.1 fusion
  32.4 1.8 maximum_select_fusion.rows_ref.refs_1_
  34.3 1.0 broadcast_in_dim.55.start_ref.refs_0_
  35.9 3.0 collective-permute-start.4
  39.6 2.5 collective-permute-start.7
  42.1 13.1 %shard_map.221 = (bf16[3,1024,384]{2,1,0:T(8,128)(2,1)}, bf16[768,1024]{1,0:T(8,128)(2,1)}, bf16[3,768,384]{2,1,0:T(8,128)(2,1)}) custom-call(s32[7]{0:T(128)} %stack.50.flags, bf16[1024,768]{1,0:T(8,128)(2,1)} %maximum_select_fusion.rows_ref.refs_1_, f32[4,768]{1,0:T(4,128)} %pad_maximum_fusion.5.vectors.refs_5_, ...), custom_call_target="tpu_custom_call" | custom-call | bytes 27000000 | tf_op jit(solution)/shard_map/pallas_call | solution.py:272
  55.2 7.5 %shard_map.222.unused = bf16[1024,384]{1,0:T(8,128)(2,1)} custom-call(s32[1024,128]{1,0:T(8,128)} %broadcast_in_dim.55.start_ref.refs_0_, bf16[3,1024,384]{2,1,0:T(8,128)(2,1)} %get-tuple-element.79.q_ref.k_ref.v_ref.refs_1_.refs_2_.refs_3_.refs_4_.refs_5_, bf16[3,1024,384]{2,1,0:T(8,128)(2,1)} %get-tuple-element.79.q_ref.k_ref.v_ref.refs_1_.refs_2_.refs_3_.refs_4_.refs_5_, ...), custom_call_target="tpu_custom_call" | custom-call | bytes 15000000 | tf_op jit(solution)/shard_map/pallas_call | solution.py:92
  62.7 7.5 %shard_map.223.unused = bf16[1024,384]{1,0:T(8,128)(2,1)} custom-call(bf16[1024,384]{1,0:T(8,128)(2,1)} %shard_map.222.unused, s32[1024,128]{1,0:T(8,128)} %broadcast_in_dim.55.start_ref.refs_0_, bf16[3,1024,384]{2,1,0:T(8,128)(2,1)} %get-tuple-element.79.q_ref.k_ref.v_ref.refs_1_.refs_2_.refs_3_.refs_4_.refs_5_, ...), custom_call_target="tpu_custom_call", output_to_operand_aliasing={{}: (0, {})} | custom-call | bytes 15000000 | tf_op jit(solution)/shard_map/pallas_call | solution.py:92
  70.2 7.5 %shard_map.224.mixed_ref = bf16[1024,384]{1,0:T(8,128)(2,1)} custom-call(bf16[1024,384]{1,0:T(8,128)(2,1)} %shard_map.223.unused, s32[1024,128]{1,0:T(8,128)} %broadcast_in_dim.55.start_ref.refs_0_, bf16[3,1024,384]{2,1,0:T(8,128)(2,1)} %get-tuple-element.79.q_ref.k_ref.v_ref.refs_1_.refs_2_.refs_3_.refs_4_.refs_5_, ...), custom_call_target="tpu_custom_call", output_to_operand_aliasing={{}: (0, {})} | custom-call | bytes 15000000 | tf_op jit(solution)/shard_map/pallas_call | solution.py:92
  77.7 15.4 %collective-permute-start.8 = (bf16[1536,768]{1,0:T(8,128)(2,1)}, bf16[1536,768]{1,0:T(8,128)(2,1)}, u32[]{:S(2)}, u32[]{:S(2)}) collective-permute-start(bf16[1536,768]{1,0:T(8,128)(2,1)} %get-tuple-element.89), channel_id=1, source_target_pairs={{1,16},{3,18},{5,20},{7,22},{9,24},{11,26},{13,28},{15,30},{16,1},... | collective-permute-start | bytes 7077896 | tf_op jit(solution)/shard_map/ppermute | solution.py:734
  93.3 1.0 convolution_convert_fusion.refs_2_.own_ref
  94.9 3.9 %collective-permute-done.6 = bf16[512,768]{1,0:T(8,128)(2,1)S(1)} collective-permute-done((bf16[512,768]{1,0:T(8,128)(2,1)S(1)}, bf16[512,768]{1,0:T(8,128)(2,1)S(1)}, u32[]{:S(2)}, u32[]{:S(2)}) %collective-permute-start.6) | collective-permute-done | bytes 786464 | tf_op jit(solution)/shard_map/ppermute | solution.py:761
  98.8 1.8 maximum_select_fusion.1.refs_4_.cot_ref
  100.7 1.2 copy-done.2
  101.8 24.9 %shard_map.225 = (bf16[1024,768]{1,0:T(8,128)(2,1)}, bf16[768,1024]{1,0:T(8,128)(2,1)}, bf16[1024,768]{1,0:T(8,128)(2,1)}, bf16[768,1024]{1,0:T(8,128)(2,1)}, f3...) custom-call(s32[7]{0:T(128)} %stack.50.flags, ...), custom_call_target="tpu_custom_call" | custom-call | bytes 60000000 | tf_op jit(solution)/shard_map/pallas_call | solution.py:396
  126.8 21.0 %shard_map.226 = (bf16[1024,768]{1,0:T(8,128)(2,1)}, bf16[1024,768]{1,0:T(8,128)(2,1)}, bf16[4,768,384]{2,1,0:T(8,128)(2,1)}, bf16[768,768]{1,0:T(8,128)(2,1)}) custom-call(s32[7]{0:T(128)} %stack.50.flags, bf16[1024,768]{1,0:T(8,128)(2,1)} %get-tuple-element.83.refs_0_, bf16[768,1024]{1,0:T(8,128)(2,1)} %get-tuple-element.84.refs_1_, ...), custom_call_target="tpu_custom_call" | custom-call | bytes 60000000 | tf_op jit(solution)/shard_map/pallas_call | solution.py:396
  147.9 1.3 copy-done.7
  149.4 1.9 slice.60.w_ref
  151.4 1.3 collective-permute-done.9.back_got
  152.7 1.2 copy-done.8
  153.9 12.0 %shard_map.227 = (bf16[1024,768]{1,0:T(8,128)(2,1)}, bf16[1024,384]{1,0:T(8,128)(2,1)}, bf16[768,384]{1,0:T(8,128)(2,1)}, f32[8,768]{1,0:T(8,128)}) custom-call(s32[7]{0:T(128)} %stack.50.flags, f32[5]{0:T(128)} %weight_ref.3, bf16[1024,768]{1,0:T(8,128)(2,1)} %maximum_select_fusion.rows_ref.refs_1_, bf16[1024,768]{1,0:T(8,128)(2,1)} %copy-done.1, ...), custom_call_target="tpu_custom_call" | custom-call | bytes 36000000 | tf_op jit(solution)/shard_map/pallas_call | solution.py:514
  165.8 11.6 %shard_map.228.unused = bf16[3,1024,384]{2,1,0:T(8,128)(2,1)} custom-call(s32[8,1024]{1,0:T(8,128)} %broadcast_in_dim.56.start_ref.refs_0_, f32[1024,128]{1,0:T(8,128)} %get-tuple-element.76.cos_ref.refs_1_, f32[1024,128]{1,0:T(8,128)} %get-tuple-element.77.sin_ref.refs_2_, ...), custom_call_target="tpu_custom_call" | custom-call | bytes 27000000 | tf_op jit(solution)/shard_map/pallas_call | solution.py:173
  177.4 11.7 %shard_map.229.unused = bf16[3,1024,384]{2,1,0:T(8,128)(2,1)} custom-call(bf16[3,1024,384]{2,1,0:T(8,128)(2,1)} %shard_map.228.unused, s32[8,1024]{1,0:T(8,128)} %broadcast_in_dim.56.start_ref.refs_0_, f32[1024,128]{1,0:T(8,128)} %get-tuple-element.76.cos_ref.refs_1_, f32[1024,128]{1,0:T(8,128)} %get-tuple-element.77.sin_ref.refs_2_, ...), custom_call_target="tpu_custom_call", output_to_operand_aliasing={{}: (0, {})} | custom-call | bytes 27000000 | tf_op jit(solution)/shard_map/pallas_call | solution.py:173
  189.1 11.7 %shard_map.230.grad_ref = bf16[3,1024,384]{2,1,0:T(8,128)(2,1)} custom-call(bf16[3,1024,384]{2,1,0:T(8,128)(2,1)} %shard_map.229.unused, s32[8,1024]{1,0:T(8,128)} %broadcast_in_dim.56.start_ref.refs_0_, f32[1024,128]{1,0:T(8,128)} %get-tuple-element.76.cos_ref.refs_1_, ...), custom_call_target="tpu_custom_call", output_to_operand_aliasing={{}: (0, {})} | custom-call | bytes 27000000 | tf_op jit(solution)/shard_map/pallas_call | solution.py:173
  200.8 8.5 %shard_map.231 = (bf16[768,384]{1,0:T(8,128)(2,1)}, bf16[768,384]{1,0:T(8,128)(2,1)}, bf16[768,384]{1,0:T(8,128)(2,1)}, bf16[768,384]{1,0:T(8,128)(2,1)}) custom-call(s32[7]{0:T(128)} %stack.50.flags, bf16[768,1024]{1,0:T(8,128)(2,1)} %get-tuple-element.92.turned_ref, bf16[3,1024,384]{2,1,0:T(8,128)(2,1)} %shard_map.230.grad_ref, ...), custom_call_target="tpu_custom_call" | custom-call | bytes 9000000 | tf_op jit(solution)/shard_map/pallas_call | solution.py:560
  209.3 2.5 collective-permute-start.10
  211.8 2.1 collective-permute-start.12
  214.2 2.4 pad_maximum_fusion.3
  216.9 7.2 %shard_map.232 = (f32[512,768]{1,0:T(8,128)}, bf16[512,768]{1,0:T(8,128)(2,1)}) custom-call(s32[7]{0:T(128)} %stack.50.flags, bf16[3,1024,384]{2,1,0:T(8,128)(2,1)} %shard_map.230.grad_ref, bf16[3,768,384]{2,1,0:T(8,128)(2,1)} %get-tuple-element.96.weight), custom_call_target="tpu_custom_call" | custom-call | bytes 12000000 | tf_op jit(solution)/shard_map/pallas_call | solution.py:595
  224.0 9.3 %shard_map.233 = (f32[512,768]{1,0:T(8,128)}, bf16[512,768]{1,0:T(8,128)(2,1)}) custom-call(s32[7]{0:T(128)} %stack.50.flags, bf16[1024,768]{1,0:T(8,128)(2,1)} %get-tuple-element.100.act_early, bf16[1024,768]{1,0:T(8,128)(2,1)} %get-tuple-element.101.act_late, bf16[768,768]{1,0:T(8,128)(2,1)} %get-tuple-element.102.early_ref, ...), custom_call_target="tpu_custom_call" | custom-call | bytes 21000000 | tf_op jit(solution)/shard_map/pallas_call | solution.py:455
  233.4 2.2 collective-permute-done.11
  235.5 5.5 %collective-permute-done.13 = bf16[768,384]{1,0:T(8,128)(2,1)S(1)} collective-permute-done((bf16[768,384]{1,0:T(8,128)(2,1)}, bf16[768,384]{1,0:T(8,128)(2,1)S(1)}, u32[]{:S(2)}, u32[]{:S(2)}) %collective-permute-start.13) | collective-permute-done | bytes 589856 | tf_op jit(solution)/shard_map/ppermute | solution.py:738
  242.4 1.8 collective-permute-done.14.got_ref
  244.1 1.3 collective-permute-done.15.block_got
  246.4 6.8 %shard_map.234 = (bf16[2,512,768]{2,1,0:T(8,128)(2,1)}, f32[8,768]{1,0:T(8,128)}) custom-call(s32[7]{0:T(128)} %stack.50.flags, bf16[1024,768]{1,0:T(8,128)(2,1)} %maximum_select_fusion.rows_ref.refs_1_, f32[512,768]{1,0:T(8,128)} %get-tuple-element.109.keep_ref, bf16[512,768]{1,0:T(8,128)(2,1)} %copy-done.10, ...), custom_call_target="tpu_custom_call" | custom-call | bytes 9000000 | tf_op jit(solution)/shard_map/pallas_call | solution.py:638
  253.2 2.7 collective-permute-start.16
  257.5 2.4 add_convert_fusion
  260.0 1.2 collective-permute-start.18
  261.3 1.8 collective-permute-done.18
  263.0 1.5 collective-permute-start.19
  264.5 10.0 %collective-permute-done.19 = f32[9,768]{1,0:T(8,128)S(1)} collective-permute-done((f32[9,768]{1,0:T(8,128)S(1)}, f32[9,768]{1,0:T(8,128)S(1)}, u32[]{:S(2)}, u32[]{:S(2)}) %collective-permute-start.19) | collective-permute-done | bytes 27680 | tf_op jit(solution)/shard_map/ppermute | solution.py:802
  274.6 4.5 %collective-permute-done.20 = f32[9,768]{1,0:T(8,128)S(1)} collective-permute-done((f32[9,768]{1,0:T(8,128)S(1)}, f32[9,768]{1,0:T(8,128)S(1)}, u32[]{:S(2)}, u32[]{:S(2)}) %collective-permute-start.20) | collective-permute-done | bytes 27680 | tf_op jit(solution)/shard_map/ppermute | solution.py:802
  279.1 1.6 collective-permute-start.21
  280.7 2.3 collective-permute-done.21
  283.0 1.1 copy-done.6
  284.1 3.3 shard_map.235
  287.5 1.0 reshape.159
  288.5 4.3 %collective-permute-start.24 = (bf16[2,192,384]{2,0,1:T(2,128)(2,1)S(1)}, bf16[2,192,384]{2,0,1:T(2,128)(2,1)S(1)}, u32[]{:S(2)}, u32[]{:S(2)}) collective-permute-start(bf16[2,192,384]{2,0,1:T(2,128)(2,1)S(1)} %bitcast.64), channel_id=1, source_target_pairs={{1,17},{3,19},{5,21},{7,23},{9,25},{11,27},{13,29},{15,31},{16,0},... | collective-permute-start | bytes 884744 | tf_op jit(solution)/shard_map/ppermute | solution.py:749
  292.8 3.6 %collective-permute-done.24 = bf16[2,192,384]{2,0,1:T(2,128)(2,1)S(1)} collective-permute-done((bf16[2,192,384]{2,0,1:T(2,128)(2,1)S(1)}, bf16[2,192,384]{2,0,1:T(2,128)(2,1)S(1)}, u32[]{:S(2)}, u32[]{:S(2)}) %collective-permute-start.24) | collective-permute-done | bytes 294944 | tf_op jit(solution)/shard_map/ppermute | solution.py:749
  298.3 6.5 %collective-permute-start.22 = (bf16[192,384]{1,0:T(8,128)(2,1)}, bf16[192,384]{1,0:T(8,128)(2,1)S(1)}, u32[]{:S(2)}, u32[]{:S(2)}) collective-permute-start(bf16[192,384]{1,0:T(8,128)(2,1)} %reduce-scatter.9.cloned.1.call-done), channel_id=1, source_target_pairs={{0,1},{1,0},{2,3},{3,2},{4,5},{5,4},{6,7},{7,6},{8,9},{9,8},{10,11... | collective-permute-start | bytes 442376 | tf_op jit(solution)/shard_map/ppermute | solution.py:761
  305.7 1.8 broadcast_select_fusion
  307.4 7.2 %collective-permute-start.26 = (bf16[2,2,2,192,384]{4,2,3,1,0:T(2,128)(2,1)S(1)}, bf16[2,2,2,192,384]{4,2,3,1,0:T(2,128)(2,1)S(1)}, u32[]{:S(2)}, u32[]{:S(2)}) collective-permute-start(bf16[2,2,2,192,384]{4,2,3,1,0:T(2,128)(2,1)S(1)} %broadcast_select_fusion), channel_id=1, source_target_pairs={{0,1},{1,0},{2,3},{3,2},{4,5},{5,4},{6,7},{7,6},{8,9},{9,8},{10,11... | collective-permute-start | bytes 3538952 | tf_op jit(solution)/shard_map/ppermute | solution.py:761
  314.7 1.3 collective-permute-start.23
  317.2 6.1 %collective-permute-done.23 = bf16[2,192,384]{2,1,0:T(8,128)(2,1)S(1)} collective-permute-done((bf16[2,192,384]{2,1,0:T(8,128)(2,1)S(1)}, bf16[2,192,384]{2,1,0:T(8,128)(2,1)S(1)}, u32[]{:S(2)}, u32[]{:S(2)}) %collective-permute-start.23) | collective-permute-done | bytes 294944 | tf_op jit(solution)/shard_map/ppermute | solution.py:757
  325.2 2.1 broadcast_select_fusion.1
  329.0 2.0 reshape.163
  331.9 2.0 reshape.161
  (121 shorter events, 17.7 us)
Async XLA Ops:
  7.2 207.1 %reduce-scatter.13.cloned.1.call-start = ((), (), s32[]{:S(2)}) async-start(), calls=%async_computation.6 | async-start | bytes 2949120
  7.2 20.4 %collective-permute-start.2 = (s32[1,3]{1,0:T(1,128)}, s32[1,3]{1,0:T(1,128)S(1)}, u32[]{:S(2)}, u32[]{:S(2)}) collective-permute-start(s32[1,3]{1,0:T(1,128)} %param.16), channel_id=1, source_target_pairs={{0,1},{1,0},{2,3},{3,2},{4,5},{5,4},{6,7},{7,6},{8,9},{9,8},{10,11... | collective-permute-start | bytes 44 | tf_op jit(solution)/shard_map/ppermute | solution.py:761
  8.0 19.9 %collective-permute-start = (bf16[512,768]{1,0:T(8,128)(2,1)}, bf16[512,768]{1,0:T(8,128)(2,1)}, u32[]{:S(2)}, u32[]{:S(2)}) collective-permute-start(bf16[512,768]{1,0:T(8,128)(2,1)} %bitcast.72), channel_id=1, source_target_pairs={{1,16},{3,18},{5,20},{7,22},{9,24},{11,26},{13,28},{15,30},{16,1},... | collective-permute-start | bytes 2359304 | tf_op jit(solution)/shard_map/ppermute | solution.py:734
  11.0 31.1 %collective-permute-start.3 = (bf16[3,768,384]{2,1,0:T(8,128)(2,1)}, bf16[3,768,384]{2,1,0:T(8,128)(2,1)}, u32[]{:S(2)}, u32[]{:S(2)}) collective-permute-start(bf16[3,768,384]{2,1,0:T(8,128)(2,1)} %w_own.1), channel_id=1, source_target_pairs={{1,16},{3,18},{5,20},{7,22},{9,24},{11,26},{13,28},{15,30},{16,1},... | collective-permute-start | bytes 5308424 | tf_op jit(solution)/shard_map/ppermute | solution.py:734
  13.5 3.0 copy-start
  16.6 1.6 copy-start.18
  16.6 1.6 copy-start.19
  16.6 1.6 copy-start.20
  16.6 1.6 copy-start.21
  16.6 1.6 copy-start.5
  16.6 2.0 copy-start.12
  23.5 4.1 %copy-start.22 = (s32[1,3]{1,0:T(1,128)S(1)}, s32[1,3]{1,0:T(1,128)}, u32[]{:S(2)}) copy-start(s32[1,3]{1,0:T(1,128)} %param.16) | copy-start | bytes 40
  23.6 4.3 %copy-start.9 = (bf16[1,512,768]{2,1,0:T(8,128)(2,1)S(1)}, bf16[1,512,768]{2,1,0:T(8,128)(2,1)}, u32[]{:S(2)}) copy-start(bf16[1,512,768]{2,1,0:T(8,128)(2,1)} %param.13) | copy-start | bytes 2359300
  29.1 3.3 collective-permute-start.1
  35.9 57.2 %collective-permute-start.4 = (bf16[896,768]{1,0:T(8,128)(2,1)S(1)}, bf16[896,768]{1,0:T(8,128)(2,1)S(1)}, u32[]{:S(2)}, u32[]{:S(2)}) collective-permute-start(bf16[896,768]{1,0:T(8,128)(2,1)S(1)} %pad_maximum_fusion.2), channel_id=1, source_target_pairs={{1,16},{3,18},{5,20},{7,22},{9,24},{11,26},{13,28},{15,30},{16,1},... | collective-permute-start | bytes 4128776 | tf_op jit(solution)/shard_map/ppermute | solution.py:734
  39.6 61.1 %collective-permute-start.7 = (bf16[1536,768]{1,0:T(8,128)(2,1)}, bf16[1536,768]{1,0:T(8,128)(2,1)}, u32[]{:S(2)}, u32[]{:S(2)}) collective-permute-start(bf16[1536,768]{1,0:T(8,128)(2,1)} %get-tuple-element.82), channel_id=1, source_target_pairs={{1,16},{3,18},{5,20},{7,22},{9,24},{11,26},{13,28},{15,30},{16,1},... | collective-permute-start | bytes 7077896 | tf_op jit(solution)/shard_map/ppermute | solution.py:734
  77.7 15.6 %copy-start.3 = (bf16[1024,384]{1,0:T(8,128)(2,1)S(1)}, bf16[1024,384]{1,0:T(8,128)(2,1)}, u32[]{:S(2)}) copy-start(bf16[1024,384]{1,0:T(8,128)(2,1)} %shard_map.224.mixed_ref) | copy-start | bytes 2359300
  77.7 49.1 %collective-permute-start.8 = (bf16[1536,768]{1,0:T(8,128)(2,1)}, bf16[1536,768]{1,0:T(8,128)(2,1)}, u32[]{:S(2)}, u32[]{:S(2)}) collective-permute-start(bf16[1536,768]{1,0:T(8,128)(2,1)} %get-tuple-element.89), channel_id=1, source_target_pairs={{1,16},{3,18},{5,20},{7,22},{9,24},{11,26},{13,28},{15,30},{16,1},... | collective-permute-start | bytes 7077896 | tf_op jit(solution)/shard_map/ppermute | solution.py:734
  93.2 1.1 copy-start.4
  94.2 6.4 %copy-start.1 = (bf16[1024,768]{1,0:T(8,128)(2,1)}, bf16[1024,768]{1,0:T(8,128)(2,1)S(1)}, u32[]{:S(2)}) copy-start(bf16[1024,768]{1,0:T(8,128)(2,1)S(1)} %convolution_convert_fusion.refs_2_.own_ref) | copy-start | bytes 4718596
  94.2 6.4 %collective-permute-start.5 = (bf16[1024,768]{1,0:T(8,128)(2,1)S(1)}, bf16[1024,768]{1,0:T(8,128)(2,1)S(1)}, u32[]{:S(2)}, u32[]{:S(2)}) collective-permute-start(bf16[1024,768]{1,0:T(8,128)(2,1)S(1)} %convolution_convert_fusion.refs_2_.own_ref), channel_id=1, source_target_pairs={{0,1},{1,0},{2,3},{3,2},{4,5},{5,4},{6,7},{7,6},{8,9},{9,8},{10,11... | collective-permute-start | bytes 4718600 | tf_op jit(solution)/shard_map/ppermute | solution.py:761
  94.4 4.5 %collective-permute-start.6 = (bf16[512,768]{1,0:T(8,128)(2,1)S(1)}, bf16[512,768]{1,0:T(8,128)(2,1)S(1)}, u32[]{:S(2)}, u32[]{:S(2)}) collective-permute-start(bf16[512,768]{1,0:T(8,128)(2,1)S(1)} %slice.61), channel_id=1, source_target_pairs={{0,1},{1,0},{2,3},{3,2},{4,5},{5,4},{6,7},{7,6},{8,9},{9,8},{10,11... | collective-permute-start | bytes 2359304 | tf_op jit(solution)/shard_map/ppermute | solution.py:761
  100.7 1.2 copy-start.2
  126.8 87.5 %reduce-scatter.15.cloned.1.call-start = ((), (), s32[]{:S(2)}) async-start(), calls=%async_computation.7 | async-start | bytes 2949120
  147.9 1.4 copy-start.7
  147.9 139.6 %reduce-scatter.11.cloned.1.call-start = ((), (), s32[]{:S(2)}) async-start(), calls=%async_computation.5 | async-start | bytes 1474560 | tf_op jit(solution)/shard_map/reduce_scatter | solution.py:788
  149.3 3.4 %collective-permute-start.9 = (bf16[1024,768]{1,0:T(8,128)(2,1)S(1)}, bf16[1024,768]{1,0:T(8,128)(2,1)S(1)}, u32[]{:S(2)}, u32[]{:S(2)}) collective-permute-start(bf16[1024,768]{1,0:T(8,128)(2,1)S(1)} %copy-done.7), channel_id=1, source_target_pairs={{0,1},{1,0},{2,3},{3,2},{4,5},{5,4},{6,7},{7,6},{8,9},{9,8},{10,11... | collective-permute-start | bytes 4718600 | tf_op jit(solution)/shard_map/ppermute | solution.py:761
  152.7 1.2 copy-start.8
  209.3 24.1 %collective-permute-start.10 = (bf16[768,384]{1,0:T(8,128)(2,1)}, bf16[768,384]{1,0:T(8,128)(2,1)S(1)}, u32[]{:S(2)}, u32[]{:S(2)}) collective-permute-start(bf16[768,384]{1,0:T(8,128)(2,1)} %get-tuple-element.94), channel_id=1, source_target_pairs={{1,16},{3,18},{5,20},{7,22},{9,24},{11,26},{13,28},{15,30},{16,1},... | collective-permute-start | bytes 1769480 | tf_op jit(solution)/shard_map/ppermute | solution.py:738
  211.8 23.8 %collective-permute-start.11 = (bf16[768,384]{1,0:T(8,128)(2,1)}, bf16[768,384]{1,0:T(8,128)(2,1)S(1)}, u32[]{:S(2)}, u32[]{:S(2)}) collective-permute-start(bf16[768,384]{1,0:T(8,128)(2,1)} %get-tuple-element.106), channel_id=1, source_target_pairs={{0,1},{1,17},{2,3},{3,19},{4,5},{5,21},{6,7},{7,23},{8,9},{9,25},{... | collective-permute-start | bytes 1769480 | tf_op jit(solution)/shard_map/ppermute | solution.py:738
  211.8 23.7 %collective-permute-start.12 = (bf16[768,384]{1,0:T(8,128)(2,1)}, bf16[768,384]{1,0:T(8,128)(2,1)S(1)}, u32[]{:S(2)}, u32[]{:S(2)}) collective-permute-start(bf16[768,384]{1,0:T(8,128)(2,1)} %get-tuple-element.107), channel_id=1, source_target_pairs={{0,2},{1,18},{2,0},{3,16},{4,6},{5,22},{6,4},{7,20},{8,10},{9,26},... | collective-permute-start | bytes 1769480 | tf_op jit(solution)/shard_map/ppermute | solution.py:738
  213.9 27.1 %collective-permute-start.13 = (bf16[768,384]{1,0:T(8,128)(2,1)}, bf16[768,384]{1,0:T(8,128)(2,1)S(1)}, u32[]{:S(2)}, u32[]{:S(2)}) collective-permute-start(bf16[768,384]{1,0:T(8,128)(2,1)} %get-tuple-element.108), channel_id=1, source_target_pairs={{0,3},{1,19},{2,1},{3,17},{4,7},{5,23},{6,5},{7,21},{8,11},{9,27},... | collective-permute-start | bytes 1769480 | tf_op jit(solution)/shard_map/ppermute | solution.py:738
  216.6 81.7 %reduce-scatter.9.cloned.1.call-start = ((), (), s32[]{:S(2)}) async-start(), calls=%async_computation.4 | async-start | bytes 737280 | tf_op jit(solution)/shard_map/reduce_scatter | solution.py:788
  224.0 17.8 %copy-start.23 = (bf16[512,768]{1,0:T(8,128)(2,1)S(1)}, bf16[512,768]{1,0:T(8,128)(2,1)}, u32[]{:S(2)}) copy-start(bf16[512,768]{1,0:T(8,128)(2,1)} %get-tuple-element.110) | copy-start | bytes 2359300
  235.5 5.5 %copy-start.14 = (bf16[768,384]{1,0:T(8,128)(2,1)}, bf16[768,384]{1,0:T(8,128)(2,1)S(1)}, u32[]{:S(2)}) copy-start(bf16[768,384]{1,0:T(8,128)(2,1)S(1)} %collective-permute-done.12) | copy-start | bytes 1769476
  241.0 0.8 copy-start.15
  241.9 2.3 collective-permute-start.14
  242.2 3.3 collective-permute-start.15
  244.1 1.3 copy-start.10
  245.5 0.9 copy-start.11
  246.4 9.5 %copy-start.17 = (f32[8,768]{1,0:T(8,128)S(1)}, f32[8,768]{1,0:T(8,128)}, u32[]{:S(2)}) copy-start(f32[8,768]{1,0:T(8,128)} %get-tuple-element.117) | copy-start | bytes 73732
  246.4 11.1 %copy-start.13 = (bf16[768,384]{1,0:T(8,128)(2,1)S(1)}, bf16[768,384]{1,0:T(8,128)(2,1)}, u32[]{:S(2)}) copy-start(bf16[768,384]{1,0:T(8,128)(2,1)} %get-tuple-element.94) | copy-start | bytes 1769476
  253.2 29.8 %collective-permute-start.16 = (bf16[2,512,768]{2,1,0:T(8,128)(2,1)}, bf16[2,512,768]{2,1,0:T(8,128)(2,1)S(1)}, u32[]{:S(2)}, u32[]{:S(2)}) collective-permute-start(bf16[2,512,768]{2,1,0:T(8,128)(2,1)} %get-tuple-element.114.own_ref), channel_id=1, source_target_pairs={{1,16},{3,18},{5,20},{7,22},{9,24},{11,26},{13,28},{15,30},{16,1},... | collective-permute-start | bytes 4718600 | tf_op jit(solution)/shard_map/ppermute | solution.py:734
  257.4 2.6 collective-permute-start.17
  260.0 3.0 collective-permute-start.18
  263.0 11.5 %collective-permute-start.19 = (f32[9,768]{1,0:T(8,128)S(1)}, f32[9,768]{1,0:T(8,128)S(1)}, u32[]{:S(2)}, u32[]{:S(2)}) collective-permute-start(f32[9,768]{1,0:T(8,128)S(1)} %add.69), channel_id=1, source_target_pairs={{0,16},{16,0},{1,17},{17,1},{2,18},{18,2},{3,19},{19,3},{4,20},{20... | collective-permute-start | bytes 82952 | tf_op jit(solution)/shard_map/ppermute | solution.py:802
  274.5 4.6 %collective-permute-start.20 = (f32[9,768]{1,0:T(8,128)S(1)}, f32[9,768]{1,0:T(8,128)S(1)}, u32[]{:S(2)}, u32[]{:S(2)}) collective-permute-start(f32[9,768]{1,0:T(8,128)S(1)} %add.70), channel_id=1, source_target_pairs={{0,4},{4,0},{8,12},{12,8},{1,5},{5,1},{9,13},{13,9},{2,6},{6,2},{1... | collective-permute-start | bytes 82952 | tf_op jit(solution)/shard_map/ppermute | solution.py:802
  279.1 3.9 %collective-permute-start.21 = (f32[9,768]{1,0:T(8,128)S(1)}, f32[9,768]{1,0:T(8,128)S(1)}, u32[]{:S(2)}, u32[]{:S(2)}) collective-permute-start(f32[9,768]{1,0:T(8,128)S(1)} %add.71), channel_id=1, source_target_pairs={{0,8},{4,12},{8,0},{12,4},{1,9},{5,13},{9,1},{13,5},{2,10},{6,14},... | collective-permute-start | bytes 82952 | tf_op jit(solution)/shard_map/ppermute | solution.py:802
  283.0 1.1 copy-start.6
  288.5 8.0 %collective-permute-start.24 = (bf16[2,192,384]{2,0,1:T(2,128)(2,1)S(1)}, bf16[2,192,384]{2,0,1:T(2,128)(2,1)S(1)}, u32[]{:S(2)}, u32[]{:S(2)}) collective-permute-start(bf16[2,192,384]{2,0,1:T(2,128)(2,1)S(1)} %bitcast.64), channel_id=1, source_target_pairs={{1,17},{3,19},{5,21},{7,23},{9,25},{11,27},{13,29},{15,31},{16,0},... | collective-permute-start | bytes 884744 | tf_op jit(solution)/shard_map/ppermute | solution.py:749
  297.3 8.4 %collective-permute-start.25 = (bf16[2,2,192,384]{3,1,2,0:T(2,128)(2,1)S(1)}, bf16[2,2,192,384]{3,1,2,0:T(2,128)(2,1)S(1)}, u32[]{:S(2)}, u32[]{:S(2)}) collective-permute-start(bf16[2,2,192,384]{3,1,2,0:T(2,128)(2,1)S(1)} %broadcast_select_fusion.3), channel_id=1, source_target_pairs={{0,2},{2,0},{4,6},{6,4},{8,10},{10,8},{12,14},{14,12},{17,19},{19,... | collective-permute-start | bytes 1769480 | tf_op jit(solution)/shard_map/ppermute | solution.py:753
  298.3 16.4 %collective-permute-start.22 = (bf16[192,384]{1,0:T(8,128)(2,1)}, bf16[192,384]{1,0:T(8,128)(2,1)S(1)}, u32[]{:S(2)}, u32[]{:S(2)}) collective-permute-start(bf16[192,384]{1,0:T(8,128)(2,1)} %reduce-scatter.9.cloned.1.call-done), channel_id=1, source_target_pairs={{0,1},{1,0},{2,3},{3,2},{4,5},{5,4},{6,7},{7,6},{8,9},{9,8},{10,11... | collective-permute-start | bytes 442376 | tf_op jit(solution)/shard_map/ppermute | solution.py:761
  304.8 9.8 %copy-start.16 = (bf16[192,384]{1,0:T(8,128)(2,1)S(1)}, bf16[192,384]{1,0:T(8,128)(2,1)}, u32[]{:S(2)}) copy-start(bf16[192,384]{1,0:T(8,128)(2,1)} %reduce-scatter.9.cloned.1.call-done) | copy-start | bytes 442372
  307.4 17.8 %collective-permute-start.26 = (bf16[2,2,2,192,384]{4,2,3,1,0:T(2,128)(2,1)S(1)}, bf16[2,2,2,192,384]{4,2,3,1,0:T(2,128)(2,1)S(1)}, u32[]{:S(2)}, u32[]{:S(2)}) collective-permute-start(bf16[2,2,2,192,384]{4,2,3,1,0:T(2,128)(2,1)S(1)} %broadcast_select_fusion), channel_id=1, source_target_pairs={{0,1},{1,0},{2,3},{3,2},{4,5},{5,4},{6,7},{7,6},{8,9},{9,8},{10,11... | collective-permute-start | bytes 3538952 | tf_op jit(solution)/shard_map/ppermute | solution.py:761
  314.7 8.7 %collective-permute-start.23 = (bf16[2,192,384]{2,1,0:T(8,128)(2,1)S(1)}, bf16[2,192,384]{2,1,0:T(8,128)(2,1)S(1)}, u32[]{:S(2)}, u32[]{:S(2)}) collective-permute-start(bf16[2,192,384]{2,1,0:T(8,128)(2,1)S(1)} %maximum_select_fusion.3), channel_id=1, source_target_pairs={{0,2},{2,0},{1,3},{3,1},{4,6},{6,4},{5,7},{7,5},{8,10},{10,8},{9,1... | collective-permute-start | bytes 884744 | tf_op jit(solution)/shard_map/ppermute | solution.py:757
Sparse Core Ops, SparseCore 0:
  126.9 37.3 reduce-scatter.12
  167.3 37.3 reduce-scatter.14
  216.7 27.6 reduce-scatter.10
  260.1 19.1 reduce-scatter.8
where the time goes:
time: 344 us; the launch traced here: 341 us
  Pallas kernels  168 us (49%)
  starting transfers between devices  61.3 us (18%)
  waiting for transfers between devices  44.4 us (13%)
  other arithmetic  26.9 us (8%)
  local copies, waits for them, and re-layouts  24.6 us (7%)
  between operations  14.8 us (4%)
    pallas_call x2, Pallas kernels, feed(): pl.pallas_call(functools.partial(feed_kernel, early), grid_spec=pltpu.Pre...  45.9 us
    pallas_call x3, Pallas kernels, attend_back(): pl.pallas_call(functools.partial(kernel, reach), grid=(1,), in_specs=[pl....  35 us
    ppermute x6, starting transfers between devices, swap_diagonal(): lax.ppermute(field, AXES, moves(away, lambda t, d, k, c: (c, d, k, t)))  29.2 us
    pallas_call x3, Pallas kernels, attend(): pl.pallas_call(functools.partial(kernel, reach), grid=(1,), in_specs=[pl....  22.5 us
    ppermute x5, waiting for transfers between devices, sum_everywhere(): lax.ppermute(field, name, [(d, d ^ bit) for d in range(size)])  18.5 us
    ppermute x9, starting transfers between devices, swap_near(): return lax.ppermute(field, 'near', [(0, 1), (1, 0)])  15.9 us
    pallas_call x1, Pallas kernels, project(): pl.pallas_call(project_kernel, grid_spec=pltpu.PrefetchScalarGridSpec(num...  13.1 us
    pallas_call x1, Pallas kernels, middle(): pl.pallas_call(middle_kernel, grid_spec=pltpu.PrefetchScalarGridSpec(num_...  12 us
  transfers between devices with their start and end apart: 31, of which 12 were waited for; matrix products, arithmetic and copies ran while one was open for 11% of the time, Pallas kernels for 49%

commit v1 on v0

--- a/solution.py
+++ b/solution.py
@@ -14,7 +14,7 @@
 NEG_FILL = -1e30
 NORM_EPS = 1e-05
 RATE = 3e6
-ROOM = 60 << 20
+MIB = 1 << 20
 
 
 def lasting(microseconds):
@@ -81,26 +81,22 @@
     each_block(whole, reach, body)
 
 
-def attend(pair, start_column, projected, so_far, reach):
+def attend(start_column, projected, reach):
     count, whole, width = projected.shape
 
     def block(c):
-        return pl.BlockSpec((None, whole, LANES), lambda i: (c, 0, pair))
-
-    begun = [] if so_far is None else [so_far]
-    kernel = attend_kernel if so_far is None else lambda reach, unused, *refs: attend_kernel(reach, *refs)
-    return pl.pallas_call(
-        functools.partial(kernel, reach),
-        grid=(1,),
-        in_specs=[pl.BlockSpec(memory_space=pl.ANY)] * len(begun)
-        + [pl.BlockSpec((whole, LANES), lambda i: (0, 0)), block(0), block(1), block(2)],
-        out_specs=pl.BlockSpec((whole, LANES), lambda i: (0, pair)),
+        return pl.BlockSpec((None, whole, LANES), lambda p: (c, 0, p))
+
+    return pl.pallas_call(
+        functools.partial(attend_kernel, reach),
+        grid=(width // LANES,),
+        in_specs=[pl.BlockSpec((whole, LANES), lambda p: (0, 0)), block(0), block(1), block(2)],
+        out_specs=pl.BlockSpec((whole, LANES), lambda p: (0, p)),
         out_shape=jax.ShapeDtypeStruct((whole, width), jnp.bfloat16),
         scratch_shapes=[pltpu.VMEM((BLOCK, LANES), jnp.float32)],
-        input_output_aliases={0: 0} if begun else {},
-        compiler_params=pltpu.CompilerParams(vmem_limit_bytes=ROOM),
-        cost_estimate=lasting(5),
-    )(*begun, start_column, projected, projected, projected)
+        compiler_params=pltpu.CompilerParams(vmem_limit_bytes=16 * MIB),
+        cost_estimate=lasting(17),
+    )(start_column, projected, projected, projected)
 
 
 def turn_back(field, cos, sin):
@@ -161,39 +157,35 @@
     lax.fori_loop(0, whole // BLOCK, finish, 0)
 
 
-def attend_back(pair, start_row, cos, sin, projected, grad_mixed, so_far, reach):
+def attend_back(start_row, cos, sin, projected, grad_mixed, reach):
     count, whole, width = projected.shape
 
     def block(c):
-        return pl.BlockSpec((None, whole, LANES), lambda i: (c, 0, pair))
-
-    table = pl.BlockSpec((whole, LANES), lambda i: (0, 0))
-    begun = [] if so_far is None else [so_far]
-    kernel = attend_back_kernel if so_far is None else lambda reach, unused, *refs: attend_back_kernel(reach, *refs)
-    return pl.pallas_call(
-        functools.partial(kernel, reach),
-        grid=(1,),
-        in_specs=[pl.BlockSpec(memory_space=pl.ANY)] * len(begun)
-        + [
-            pl.BlockSpec((8, whole), lambda i: (0, 0)),
+        return pl.BlockSpec((None, whole, LANES), lambda p: (c, 0, p))
+
+    table = pl.BlockSpec((whole, LANES), lambda p: (0, 0))
+    return pl.pallas_call(
+        functools.partial(attend_back_kernel, reach),
+        grid=(width // LANES,),
+        in_specs=[
+            pl.BlockSpec((8, whole), lambda p: (0, 0)),
             table,
             table,
             block(0),
             block(1),
             block(2),
-            pl.BlockSpec((whole, LANES), lambda i: (0, pair)),
+            pl.BlockSpec((whole, LANES), lambda p: (0, p)),
         ],
-        out_specs=pl.BlockSpec((count, whole, LANES), lambda i: (0, 0, pair)),
+        out_specs=pl.BlockSpec((count, whole, LANES), lambda p: (0, 0, p)),
         out_shape=jax.ShapeDtypeStruct((count, whole, width), jnp.bfloat16),
         scratch_shapes=[
             pltpu.VMEM((whole, LANES), jnp.float32),
             pltpu.VMEM((whole, LANES), jnp.float32),
             pltpu.VMEM((BLOCK, LANES), jnp.float32),
         ],
-        input_output_aliases={0: 0} if begun else {},
-        compiler_params=pltpu.CompilerParams(vmem_limit_bytes=ROOM),
-        cost_estimate=lasting(9),
-    )(*begun, start_row, cos, sin, projected, projected, projected, grad_mixed)
+        compiler_params=pltpu.CompilerParams(vmem_limit_bytes=20 * MIB),
+        cost_estimate=lasting(28),
+    )(start_row, cos, sin, projected, projected, projected, grad_mixed)
 
 
 ROWS = 256
@@ -294,7 +286,7 @@
             jax.ShapeDtypeStruct((width, whole), jnp.bfloat16),
             jax.ShapeDtypeStruct(w_own.shape, jnp.bfloat16),
         ],
-        compiler_params=pltpu.CompilerParams(vmem_limit_bytes=ROOM),
+        compiler_params=pltpu.CompilerParams(vmem_limit_bytes=24 * MIB),
         cost_estimate=lasting(9),
     )(flags, rows, vectors, cos, sin, w_own, w_got)
 
@@ -315,8 +307,9 @@
     if early:
         weight_ref, rows_ref, own_ref, got_ref, cot_ref, vectors = refs[:6]
         up_own, down_own, got, norm, norm_t, grad, grad_t = refs[6:13]
+        up_got, down_got = got.at[: norm.shape[1]], got.at[norm.shape[1] :]
     else:
-        norm, norm_t, grad, grad_t, back_early, up_own, down_own, got = refs[:8]
+        norm, norm_t, grad, grad_t, back_early, up_own, down_own, up_got, down_got = refs[:9]
     back_ref, act_ref, pieces_ref, down_ref, slope, up_w = refs[-6:]
     whole, width = norm.shape
     part = pieces_ref.shape[2]
@@ -324,8 +317,8 @@
 
     @pl.when(step == 0)
     def _():
-        up_w[...] = jnp.where(flags[0] == 1, up_own[...], got[:width])
-        down_ref[...] = jnp.where(flags[0] == 1, down_own[...], got[width:])
+        up_w[...] = jnp.where(flags[0] == 1, up_own[...], up_got[...])
+        down_ref[...] = jnp.where(flags[0] == 1, down_own[...], down_got[...])
         if early:
 
             def body(i, at):
@@ -378,7 +371,7 @@
         row_blocks(whole, body)
 
 
-def feed(early, flags, head, w_up, w_down, got):
+def feed(early, flags, head, w_up, w_down, *got):
     whole, width = head[1].shape if early else head[0].shape
     hidden = w_up.shape[1] // 2
     steps = hidden // HIDDEN
@@ -402,8 +395,8 @@
             + [
                 pl.BlockSpec((width, hidden), lambda j, flags: (0, index)),
                 pl.BlockSpec((hidden, width), lambda j, flags: (index, 0)),
-                whole_spec(got.shape),
-            ],
+            ]
+            + [whole_spec(field.shape) for field in got],
             out_specs=([tokens, turned, tokens, turned] if early else [])
             + [
                 tokens,
@@ -422,14 +415,17 @@
             jax.ShapeDtypeStruct((4, width, hidden // 2), jnp.bfloat16),
             jax.ShapeDtypeStruct((hidden, width), jnp.bfloat16),
         ],
-        compiler_params=pltpu.CompilerParams(vmem_limit_bytes=ROOM),
+        compiler_params=pltpu.CompilerParams(vmem_limit_bytes=52 * MIB),
         cost_estimate=lasting(20),
-    )(flags, *head, w_up, w_down, got)
-
-
-def lower_kernel(flags, act_early, act_late, early_ref, late_ref, rows_ref, own_ref, got_ref, keep_ref, send_ref):
+    )(flags, *head, w_up, w_down, *got)
+
+
+def lower_kernel(
+    flags, act_early, act_late, early_ref, late_ref, rows_ref, own_ref, got_ref, cot_ref, keep_ref, send_ref, sums_ref
+):
     half = keep_ref.shape[0]
     first, second = early_ref[...], late_ref[...]
+    sums_ref[...] = jnp.zeros_like(sums_ref)
 
     def at_rows(near, i):
         return pl.ds(pl.multiple_of(near * half + i * ROWS, ROWS), ROWS)
@@ -438,17 +434,20 @@
         here = at_rows(1 - flags[1], i)
         total = dot(act_early[here, :], first) + dot(act_late[here, :], second)
         send_ref[at, :] = total.astype(jnp.bfloat16)
+        sums_ref[0:1, :] += jnp.sum(total * wide(cot_ref, here), axis=0, keepdims=True)
 
     def keep(i, at):
         here = at_rows(flags[1], i)
         total = dot(act_early[here, :], first) + dot(act_late[here, :], second)
-        keep_ref[at, :] = total + wide(rows_ref, here) + wide(own_ref, here) + wide(got_ref, here)
+        total = total + wide(rows_ref, here) + wide(own_ref, here) + wide(got_ref, here)
+        keep_ref[at, :] = total
+        sums_ref[0:1, :] += jnp.sum(total * wide(cot_ref, here), axis=0, keepdims=True)
 
     row_blocks(half, send)
     row_blocks(half, keep)
 
 
-def lower(flags, act_early, act_late, down_early, down_late, rows, own, got):
+def lower(flags, act_early, act_late, down_early, down_late, rows, own, got, cot):
     whole, hidden = act_early.shape
     width = rows.shape[1]
     half = whole_spec((whole // 2, width))
@@ -459,16 +458,17 @@
             grid=(1,),
             in_specs=[whole_spec((whole, hidden))] * 2
             + [whole_spec((hidden, width))] * 2
-            + [whole_spec((whole, width))] * 3,
-            out_specs=[half, half],
+            + [whole_spec((whole, width))] * 4,
+            out_specs=[half, half, whole_spec((8, width))],
         ),
         out_shape=[
             jax.ShapeDtypeStruct((whole // 2, width), jnp.float32),
             jax.ShapeDtypeStruct((whole // 2, width), jnp.bfloat16),
+            jax.ShapeDtypeStruct((8, width), jnp.float32),
         ],
-        compiler_params=pltpu.CompilerParams(vmem_limit_bytes=ROOM),
-        cost_estimate=lasting(7),
-    )(flags, act_early, act_late, down_early, down_late, rows, own, got)
+        compiler_params=pltpu.CompilerParams(vmem_limit_bytes=28 * MIB),
+        cost_estimate=lasting(8),
+    )(flags, act_early, act_late, down_early, down_late, rows, own, got, cot)
 
 
 def middle_kernel(
@@ -528,7 +528,7 @@
             jax.ShapeDtypeStruct((width, columns), jnp.bfloat16),
             jax.ShapeDtypeStruct((8, width), jnp.float32),
         ],
-        compiler_params=pltpu.CompilerParams(vmem_limit_bytes=ROOM),
+        compiler_params=pltpu.CompilerParams(vmem_limit_bytes=36 * MIB),
         cost_estimate=lasting(12),
     )(flags, weight, rows, own, got, cot, back_own, back_got, vectors, mixed, w_out)
 
@@ -566,13 +566,14 @@
             out_specs=[piece] * 4,
         ),
         out_shape=[jax.ShapeDtypeStruct((width, columns), jnp.bfloat16)] * 4,
-        compiler_params=pltpu.CompilerParams(vmem_limit_bytes=ROOM),
+        compiler_params=pltpu.CompilerParams(vmem_limit_bytes=16 * MIB),
         cost_estimate=lasting(3),
     )(flags, turned, grad, out_grad)
 
 
-def unproject_kernel(flags, grad_ref, weight, keep_ref, send_ref):
+def unproject_kernel(flags, grad_ref, weight, rows_ref, keep_ref, send_ref, sums_ref):
     half = keep_ref.shape[0]
+    sums_ref[...] = jnp.zeros_like(sums_ref)
 
     def side(near, out_ref):
         def body(i, at):
@@ -581,6 +582,9 @@
             for c in range(1, grad_ref.shape[0]):
                 total = total + dot(grad_ref[c, from_rows, :], weight[c], NT)
             out_ref[at, :] = total.astype(out_ref.dtype)
+            unit, unused = norm_parts(wide(rows_ref, from_rows))
+            sums_ref[0:1, :] += jnp.sum(total * unit, axis=0, keepdims=True)
+            sums_ref[1:2, :] += jnp.sum(total, axis=0, keepdims=True)
 
         row_blocks(half, body)
 
@@ -588,7 +592,7 @@
     side(flags[1], keep_ref)
 
 
-def unproject(flags, grad, weight):
+def unproject(flags, grad, weight, rows):
     count, whole, columns = grad.shape
     width = weight.shape[1]
     half = whole_spec((whole // 2, width))
@@ -597,41 +601,33 @@
         grid_spec=pltpu.PrefetchScalarGridSpec(
             num_scalar_prefetch=1,
             grid=(1,),
-            in_specs=[whole_spec(grad.shape), whole_spec((count, width, columns))],
-            out_specs=[half, half],
+            in_specs=[whole_spec(grad.shape), whole_spec((count, width, columns)), whole_spec(rows.shape)],
+            out_specs=[half, half, whole_spec((8, width))],
         ),
         out_shape=[
             jax.ShapeDtypeStruct((whole // 2, width), jnp.float32),
             jax.ShapeDtypeStruct((whole // 2, width), jnp.bfloat16),
+            jax.ShapeDtypeStruct((8, width), jnp.float32),
         ],
-        compiler_params=pltpu.CompilerParams(vmem_limit_bytes=ROOM),
+        compiler_params=pltpu.CompilerParams(vmem_limit_bytes=20 * MIB),
         cost_estimate=lasting(4),
-    )(flags, grad, weight)
-
-
-def last_kernel(
-    flags, rows_ref, keep_ref, got_ref, resid_ref, vectors, block_keep, block_got, cot_ref, out_ref, sums_ref
-):
-    sums_ref[...] = jnp.zeros_like(sums_ref)
-
+    )(flags, grad, weight, rows)
+
+
+def last_kernel(flags, rows_ref, keep_ref, got_ref, resid_ref, vectors, block_keep, block_got, grad_ref, block_ref):
     def body(i, at):
         unit, scale = norm_parts(wide(rows_ref, at))
-        back = keep_ref[at, :] + wide(got_ref, at)
-        inner = back * vectors[0:1, :]
+        inner = (keep_ref[at, :] + wide(got_ref, at)) * vectors[0:1, :]
         mean = jnp.mean(inner, axis=-1, keepdims=True)
         slant = jnp.mean(inner * unit, axis=-1, keepdims=True)
         grad = wide(resid_ref, at) + scale * (inner - mean - unit * slant)
-        out_ref[0, at, :] = grad.astype(jnp.bfloat16)
-        block = block_keep[at, :] + wide(block_got, at)
-        out_ref[1, at, :] = block.astype(jnp.bfloat16)
-        sums_ref[0:1, :] += jnp.sum(back * unit, axis=0, keepdims=True)
-        sums_ref[1:2, :] += jnp.sum(back, axis=0, keepdims=True)
-        sums_ref[2:3, :] += jnp.sum(block * wide(cot_ref, at), axis=0, keepdims=True)
+        grad_ref[at, :] = grad.astype(jnp.bfloat16)
+        block_ref[at, :] = (block_keep[at, :] + wide(block_got, at)).astype(jnp.bfloat16)
 
     row_blocks(rows_ref.shape[0], body)
 
 
-def last(flags, rows, keep, got, resid, vectors, block_keep, block_got, cot):
+def last(flags, rows, keep, got, resid, vectors, block_keep, block_got):
     half, width = keep.shape
     mine = pl.BlockSpec((half, width), lambda i, flags: (flags[1], 0))
     tokens = whole_spec((half, width))
@@ -640,16 +636,13 @@
         grid_spec=pltpu.PrefetchScalarGridSpec(
             num_scalar_prefetch=1,
             grid=(1,),
-            in_specs=[mine, tokens, tokens, mine, whole_spec(vectors.shape), tokens, tokens, mine],
-            out_specs=[whole_spec((2, half, width)), whole_spec((8, width))],
+            in_specs=[mine, tokens, tokens, mine, whole_spec(vectors.shape), tokens, tokens],
+            out_specs=[tokens, tokens],
         ),
-        out_shape=[
-            jax.ShapeDtypeStruct((2, half, width), jnp.bfloat16),
-            jax.ShapeDtypeStruct((8, width), jnp.float32),
-        ],
-        compiler_params=pltpu.CompilerParams(vmem_limit_bytes=ROOM),
+        out_shape=[jax.ShapeDtypeStruct((half, width), jnp.bfloat16)] * 2,
+        compiler_params=pltpu.CompilerParams(vmem_limit_bytes=16 * MIB),
         cost_estimate=lasting(3),
-    )(flags, rows, keep, got, resid, vectors, block_keep, block_got, cot)
+    )(flags, rows, keep, got, resid, vectors, block_keep, block_got)
 
 
 def past_kernel(dwa_ref, hist_ref, cot_ref, grad_ref, part_ref, sums_ref):
@@ -681,31 +674,88 @@
             jax.ShapeDtypeStruct((rows, width), jnp.float32),
             jax.ShapeDtypeStruct((8, width), jnp.float32),
         ],
-        compiler_params=pltpu.CompilerParams(vmem_limit_bytes=ROOM),
+        compiler_params=pltpu.CompilerParams(vmem_limit_bytes=16 * MIB),
         cost_estimate=lasting(3),
     )(dwa, history, cot)
 
 
-def present_kernel(flags, weight_ref, part_ref, own_ref, got_ref, out_ref, grad_ref):
-    here = jnp.where(flags[0] == 1, own_ref[1], got_ref[1]).astype(jnp.float32)
+def present_kernel(flags, weight_ref, part_ref, grad_own, grad_got, block_own, block_got, out_ref, grad_ref):
+    here = jnp.where(flags[0] == 1, block_own[...], block_got[...]).astype(jnp.float32)
     out_ref[...] = (part_ref[...] + weight_ref[weight_ref.shape[0] - 1] * here).astype(jnp.bfloat16)
-    grad_ref[...] = jnp.where(flags[0] == 1, own_ref[0], got_ref[0])
-
-
-def present(flags, weight, part, own, got):
+    grad_ref[...] = jnp.where(flags[0] == 1, grad_own[...], grad_got[...])
+
+
+def present(flags, weight, part, grad_own, grad_got, block_own, block_got):
     rows, width = part.shape
     scalars = pl.BlockSpec(memory_space=pltpu.SMEM)
     tokens = pl.BlockSpec((ROWS, width), lambda i: (i, 0))
-    both = pl.BlockSpec((2, ROWS, width), lambda i: (0, i, 0))
     return pl.pallas_call(
         present_kernel,
         grid=(rows // ROWS,),
-        in_specs=[scalars, scalars, tokens, both, both],
+        in_specs=[scalars, scalars] + [tokens] * 5,
         out_specs=[tokens, tokens],
         out_shape=[jax.ShapeDtypeStruct((rows, width), jnp.bfloat16)] * 2,
-        compiler_params=pltpu.CompilerParams(vmem_limit_bytes=ROOM),
+        compiler_params=pltpu.CompilerParams(vmem_limit_bytes=12 * MIB),
         cost_estimate=lasting(2),
-    )(flags, weight, part, own, got)
+    )(flags, weight, part, grad_own, grad_got, block_own, block_got)
+
+
+def place_feed_kernel(flags, own_ref, got_ref, up_ref, down_ref):
+    part = own_ref.shape[-1]
+    far, tp = flags[2], flags[7]
+    for k in range(2):
+        for t, out_ref in enumerate((up_ref, down_ref)):
+            for half in range(2):
+                at = (2 * half + k) * part
+                here = [ref[k ^ far, t ^ tp, half].astype(jnp.float32) for ref in (own_ref, got_ref)]
+                out_ref[:, at : at + part] = jnp.where(flags[0] == 1, *here)
+
+
+def place_feed(flags, own, got):
+    rows, part = own.shape[-2:]
+    both = whole_spec(own.shape)
+    block = whole_spec((rows, 4 * part))
+    return pl.pallas_call(
+        place_feed_kernel,
+        grid_spec=pltpu.PrefetchScalarGridSpec(
+            num_scalar_prefetch=1, grid=(1,), in_specs=[both, both], out_specs=[block, block]
+        ),
+        out_shape=[jax.ShapeDtypeStruct((rows, 4 * part), jnp.float32)] * 2,
+        compiler_params=pltpu.CompilerParams(vmem_limit_bytes=16 * MIB),
+        cost_estimate=lasting(2),
+    )(flags, own, got)
+
+
+def place_attention_kernel(flags, own_ref, got_ref, qkv_ref, out_ref):
+    near, far = flags[1], flags[2]
+    for k in range(2):
+        for c in range(2):
+            here = [ref[c ^ near].astype(jnp.float32) for ref in (own_ref, got_ref)]
+            field = jnp.where(far == k, *here)
+            if 2 * k + c < 3:
+                qkv_ref[2 * k + c] = field
+            else:
+                out_ref[...] = field
+
+
+def place_attention(flags, own, got):
+    rows, part = own.shape[-2:]
+    both = whole_spec(own.shape)
+    return pl.pallas_call(
+        place_attention_kernel,
+        grid_spec=pltpu.PrefetchScalarGridSpec(
+            num_scalar_prefetch=1,
+            grid=(1,),
+            in_specs=[both, both],
+            out_specs=[whole_spec((3, rows, part)), whole_spec((rows, part))],
+        ),
+        out_shape=[
+            jax.ShapeDtypeStruct((3, rows, part), jnp.float32),
+            jax.ShapeDtypeStruct((rows, part), jnp.float32),
+        ],
+        compiler_params=pltpu.CompilerParams(vmem_limit_bytes=16 * MIB),
+        cost_estimate=lasting(1),
+    )(flags, own, got)
 
 
 AXES = ("tp", "dp", "far", "near")
@@ -788,19 +838,25 @@
     return lax.psum_scatter(piece, "dp", scatter_dimension=0, tiled=True)
 
 
-def gather(piece, part, far, same):
-    pair = ordered(piece[None], bring_home(piece)[None], part == 0)
-    pairs = ordered(pair[None], swap_far_home(pair)[None], far == 0)
-    return jnp.where(same, pairs, swap_near(pairs))
-
-
-def sum_everywhere(field):
-    for name in ("near", "far", "tp", "dp"):
-        size = lax.axis_size(name)
-        bit = 1
-        while bit < size:
-            field = field + lax.ppermute(field, name, [(d, d ^ bit) for d in range(size)])
-            bit *= 2
+def move_rows(block):
+    dps = lax.axis_size("dp")
+    if dps > 8:
+        return [scatter_rows(block)]
+    block = block.reshape(dps, block.shape[0] // dps, block.shape[1])
+    place = lax.axis_index("dp")
+    moved = [lax.dynamic_index_in_dim(block, place, 0, keepdims=False)]
+    for step in range(1, dps):
+        sent = lax.dynamic_index_in_dim(block, lax.rem(place + step, dps), 0, keepdims=False)
+        moved.append(lax.ppermute(sent, "dp", [(d, (d + step) % dps) for d in range(dps)]))
+    return moved
+
+
+def sum_over(field, name):
+    size = lax.axis_size(name)
+    bit = 1
+    while bit < size:
+        field = field + lax.ppermute(field, name, [(d, d ^ bit) for d in range(size)])
+        bit *= 2
     return field
 
 
@@ -825,12 +881,12 @@
     part, far, near = lax.axis_index("tp"), lax.axis_index("far"), lax.axis_index("near")
     same = near == part
     pieces = [2 * (far ^ a) + (part ^ b) for a in range(2) for b in range(2)]
-    flags = jnp.stack([same.astype(jnp.int32), near, far, *pieces])
+    flags = jnp.stack([same.astype(jnp.int32), near, far, *pieces, part])
 
     input_got = swap_diagonal(layer_input[0])
     qkv_got = swap_diagonal(w_qkv)
     early_got = jnp.concatenate([part_of(w_up, 0, 1), part_of(w_down, 0, 0)], axis=0)
-    late_got = jnp.concatenate([part_of(w_up, 1, 1), part_of(w_down, 1, 0)], axis=0)
+    late_up, late_down = part_of(w_up, 1, 1), part_of(w_down, 1, 0)
     last_own = jnp.concatenate([w_out, cotangent[0]], axis=0)
     vectors = jnp.stack([gain_one, bias_one, gain_two, bias_two])
 
@@ -849,8 +905,8 @@
 
     input_half = jnp.where(same, layer_input[0], input_got)
     layer_rows = ordered(input_half, swap_near(input_half), near == 0)
-    layer_rows, last_own, early_got, late_got, vectors, past_sum, *tables = lax.optimization_barrier(
-        (layer_rows, last_own, early_got, late_got, vectors, past_sum)
+    layer_rows, last_own, early_got, late_up, vectors, past_sum, *tables = lax.optimization_barrier(
+        (layer_rows, last_own, early_got, late_up, vectors, past_sum)
         + (cos_table, sin_table, start_column, start_row)
     )
     cos_table, sin_table, start_column, start_row = tables
@@ -859,11 +915,9 @@
     projected, norm_one_t, weight_qkv = project(
         flags, layer_rows, vectors, cos_table, sin_table, w_qkv, qkv_got
     )
-    pairs = projected.shape[2] // LANES
-    mixed = attend(0, start_column, projected, None, LONGEST)
-    for pair in range(1, pairs):
-        mixed = attend(pair, start_column, projected, mixed, LONGEST)
-    late_got = swap_diagonal(after(late_got, mixed))
+    mixed = attend(start_column, projected, LONGEST)
+    late_up = swap_diagonal(after(late_up, mixed))
+    late_down = swap_diagonal(after(late_down, mixed))
     last_got = jnp.where(same, last_own, last_got)
     weight_out = last_got[: w_out.shape[0]]
     attn = jnp.dot(mixed, weight_out, preferred_element_type=jnp.float32).astype(jnp.bfloat16)
@@ -872,8 +926,8 @@
     cot_rows = ordered(cot_half, swap_near(cot_half), near == 0)
     head = (dwa_weights, layer_rows, attn, attn_got, cot_rows, vectors)
     *kept, act_early, early_pieces, down_early = feed(True, flags, head, w_up, w_down, early_got)
-    early_sum = scatter_plane(after(early_pieces, late_got))
-    back, act_late, late_pieces, down_late = feed(False, flags, kept, w_up, w_down, late_got)
+    early_sum = scatter_plane(after(early_pieces, late_up, late_down))
+    back, act_late, late_pieces, down_late = feed(False, flags, kept, w_up, w_down, late_up, late_down)
     late_sum = scatter_plane(late_pieces)
     back_got = swap_near(back)
     grad_attn, grad_mixed, grad_out, sums_two = middle(
@@ -890,59 +944,61 @@
         weight_out,
     )
 
-    grad_qkv = attend_back(0, start_row, cos_table, sin_table, projected, grad_mixed, None, LONGEST)
-    for pair in range(1, pairs):
-        grad_qkv = attend_back(
-            pair, start_row, cos_table, sin_table, projected, grad_mixed, grad_qkv, LONGEST
-        )
+    grad_qkv = attend_back(start_row, cos_table, sin_table, projected, grad_mixed, LONGEST)
     owned = weigh(flags, norm_one_t, grad_qkv, grad_out)
     moved = [send_to_owner(owned[j], j // 2, j % 2) for j in range(4)]
-    keep, send = unproject(flags, after(grad_qkv, owned[0]), weight_qkv)
-    block_keep, block_send = lower(
-        flags, after(act_early, send), act_late, down_early, down_late, layer_rows, attn, attn_got
-    )
-    feed_sum = scatter_rows(jnp.concatenate([after(early_sum, owned[0]), late_sum], axis=1))
-    keep, send, block_keep, block_send, *moved = lax.optimization_barrier(
-        (keep, send, block_keep, block_send, *moved)
-    )
-    ours, sums_one = last(
-        flags,
-        layer_rows,
-        keep,
-        swap_near(send),
-        grad_attn,
-        vectors,
-        block_keep,
-        swap_near(block_send),
-        cot_rows,
-    )
-    attn_sum = scatter_rows(add(jnp.where(same, owned[0], moved[0]), *moved[1:]))
-    theirs = swap_diagonal(ours)
-    small = jnp.concatenate([sums_one[:3], sums_two[:2], sums_past[:hist_count]], axis=0)
-    small = sum_everywhere(small)
-    output, grad_input = present(flags, dwa_weights, past_sum, ours, after(theirs, small))
-    feed_sum = after(feed_sum, output).reshape(feed_sum.shape[0], 2, -1).transpose(1, 0, 2)
-    feed_all = gather(feed_sum, part, far, same)
-    attn_sum = after(attn_sum, output)
-    attn_pair = ordered(attn_sum[None], swap_near(attn_sum)[None], near == 0)
-    attn_all = ordered(attn_pair, swap_far(attn_pair), far == 0)
-
-    def columns_of(pieces):
-        return pieces.transpose(2, 1, 0, 3).reshape(pieces.shape[2], -1).astype(jnp.float32)
+    keep, send, sums_one = unproject(flags, after(grad_qkv, owned[0]), weight_qkv, layer_rows)
+    block_keep, block_send, sums_now = lower(
+        flags, act_early, act_late, down_early, down_late, layer_rows, attn, attn_got, after(cot_rows, send)
+    )
+    small = jnp.concatenate([sums_one[:2], sums_two[:2], sums_now[:1], sums_past[:hist_count]], axis=0)
+    early_sum = scatter_rows(after(early_sum, owned[0]))
+    for name in ("near", "dp", "tp", "far"):
+        small = sum_over(small, name)
+    small, keep, send, block_keep, block_send, *moved = lax.optimization_barrier(
+        (small, keep, send, block_keep, block_send, *moved)
+    )
+    attn_one = add(jnp.where(same, owned[0], moved[0]), *moved[1:])
+    attn_moved = move_rows(attn_one)
+    input_grad, block_half = last(
+        flags, layer_rows, after(keep, attn_one), swap_near(send), grad_attn, vectors, block_keep, swap_near(block_send)
+    )
+    input_moved = swap_diagonal(input_grad)
+    late_sum = scatter_rows(after(late_sum, attn_one))
+    input_grad, input_moved, block_half, *attn_moved = lax.optimization_barrier(
+        (input_grad, input_moved, block_half, *attn_moved)
+    )
+    block_moved = swap_diagonal(block_half)
+    attn_sum = add(*attn_moved)
+    attn_own = jnp.stack([attn_sum, swap_near(attn_sum)])
+    attn_got = swap_far(attn_own)
+    feed_sum = jnp.stack([after(early_sum, attn_sum), late_sum])
+    feed_home = bring_home(feed_sum)
+    block_moved, attn_own, attn_got, feed_sum, feed_home = lax.optimization_barrier(
+        (block_moved, attn_own, attn_got, feed_sum, feed_home)
+    )
+    feed_own = jnp.stack([feed_sum, feed_home])
+    feed_both = jnp.stack([feed_own, swap_far_home(feed_own)])
+    feed_got = swap_near(feed_both)
+    grad_w_qkv, grad_w_out = place_attention(flags, attn_own, attn_got)
+    grad_w_up, grad_w_down = place_feed(flags, feed_both, feed_got)
+    output, grad_input = present(
+        flags, dwa_weights, past_sum, input_grad, input_moved, block_half, block_moved
+    )
 
     return (
         output[None],
         grad_input[None],
         grad_history[:, None],
-        jnp.sum(jnp.concatenate([small[5:], small[2:3]], axis=0), axis=1),
+        jnp.sum(jnp.concatenate([small[5:], small[4:5]], axis=0), axis=1),
         small[0],
         small[1],
-        attn_all[:3].astype(jnp.float32),
-        attn_all[3].astype(jnp.float32).T,
+        grad_w_qkv,
+        grad_w_out.T,
+        small[2],
         small[3],
-        small[4],
-        columns_of(feed_all[:, 0]),
-        columns_of(feed_all[:, 1]).T,
+        grad_w_up,
+        grad_w_down.T,
     )
 
 

time: 344 us -> 305 us (0.89)
  Pallas kernels: 168 us -> 133 us
  other arithmetic: 26.9 us -> 16.6 us
  local copies, waits for them, and re-layouts: 24.6 us -> 31.4 us
    unnamed x48 -> x104, local copies, waits for them, and re-layouts: 6.88 us -> 23.2 us
    ppermute x5 -> x8, waiting for transfers between devices: 18.5 us -> 31.2 us  [the longest x3 19.2 us: move_rows(): lax.ppermute(sent, 'dp', [(d, (d + step) % dps) for d in range(dps)])]
    pallas_call x6 -> x4, Pallas kernels: 57.5 us -> 49.6 us  [the longest x1 28.6 us: attend_back(): pl.pallas_call(functools.partial(attend_back_kernel, reach), grid=(width...]
    ppermute x4, waiting for transfers between devices: 7.68 us -> 0.01 us  [send_to_owner(): lax.ppermute(field, AXES, moves(away if not other_far and (not other_tp)...]
    ppermute x5 -> x8, starting transfers between devices: 4.48 us -> 11.6 us  [the longest x5 6.67 us: sum_over(): lax.ppermute(field, name, [(d, d ^ bit) for d in range(size)])]
    pallas_call x1, Pallas kernels: 9.32 us -> 4.19 us  [lower(): pl.pallas_call(lower_kernel, grid_spec=pltpu.PrefetchScalarGridSpec(num_s...]
    pallas_call x1, Pallas kernels: 12 us -> 6.86 us  [middle(): pl.pallas_call(middle_kernel, grid_spec=pltpu.PrefetchScalarGridSpec(num_...]
    ppermute x6 -> x8, starting transfers between devices: 29.2 us -> 24.3 us  [swap_diagonal(): lax.ppermute(field, AXES, moves(away, lambda t, d, k, c: (c, d, k, t)))]
  transfers between devices with their start and end apart: 31 -> 36, of which waited for: 12 -> 15; matrix products, arithmetic and copies ran while one was open for 11% -> 8% of each run, Pallas kernels for 49% -> 43%
where the time goes in v1:
time: 305 us; the launch traced here: 304 us
  Pallas kernels  133 us (44%)
  starting transfers between devices  61 us (20%)
  waiting for transfers between devices  46.4 us (15%)
  local copies, waits for them, and re-layouts  31.4 us (10%)
  other arithmetic  16.6 us (5%)
  between operations  14.6 us (5%)
    pallas_call x2, Pallas kernels, feed(): pl.pallas_call(functools.partial(feed_kernel, early), grid_spec=pltpu.Pre...  45.2 us
    pallas_call x1, Pallas kernels, attend_back(): pl.pallas_call(functools.partial(attend_back_kernel, reach), grid=(width...  28.6 us
    ppermute x8, starting transfers between devices, swap_diagonal(): lax.ppermute(field, AXES, moves(away, lambda t, d, k, c: (c, d, k, t)))  24.3 us
    unnamed x104, local copies, waits for them, and re-layouts  23.2 us
    ppermute x3, waiting for transfers between devices, move_rows(): lax.ppermute(sent, 'dp', [(d, (d + step) % dps) for d in range(dps)])  19.2 us
    pallas_call x1, Pallas kernels, attend(): pl.pallas_call(functools.partial(attend_kernel, reach), grid=(width // LA...  17.2 us
    ppermute x9, starting transfers between devices, swap_near(): return lax.ppermute(field, 'near', [(0, 1), (1, 0)])  16.1 us
    ppermute x5, waiting for transfers between devices, sum_over(): lax.ppermute(field, name, [(d, d ^ bit) for d in range(size)])  12.1 us
  transfers between devices with their start and end apart: 36, of which 15 were waited for; matrix products, arithmetic and copies ran while one was open for 8% of the time, Pallas kernels for 43%

profile of v1, /device:TPU:9, one launch (start us, length us, event | category | flops | bytes accessed | tf_op | source)
XLA Modules:
  0.0 304.3 jit_solution(2794473276749331655)
XLA Ops:
  8.0 3.1 %collective-permute-start = (bf16[512,768]{1,0:T(8,128)(2,1)}, bf16[512,768]{1,0:T(8,128)(2,1)}, u32[]{:S(2)}, u32[]{:S(2)}) collective-permute-start(bf16[512,768]{1,0:T(8,128)(2,1)} %bitcast.55), channel_id=1, source_target_pairs={{1,16},{3,18},{5,20},{7,22},{9,24},{11,26},{13,28},{15,30},{16,1},... | collective-permute-start | bytes 2359304 | tf_op jit(solution)/shard_map/ppermute | solution.py:784
  11.0 2.5 collective-permute-start.3
  13.6 2.9 fusion.10
  19.1 3.0 shard_map.220
  23.3 1.2 pad_maximum_fusion.1
  24.4 1.5 pad_maximum_fusion
  26.3 1.2 broadcast_select_fusion.1
  27.7 1.9 fusion
  29.9 1.9 maximum_select_fusion.rows_ref.refs_1_
  32.8 3.0 %collective-permute-start.4 = (bf16[896,768]{1,0:T(8,128)(2,1)}, bf16[896,768]{1,0:T(8,128)(2,1)}, u32[]{:S(2)}, u32[]{:S(2)}) collective-permute-start(bf16[896,768]{1,0:T(8,128)(2,1)} %pad_maximum_fusion.1), channel_id=1, source_target_pairs={{1,16},{3,18},{5,20},{7,22},{9,24},{11,26},{13,28},{15,30},{16,1},... | collective-permute-start | bytes 4128776 | tf_op jit(solution)/shard_map/ppermute | solution.py:784
  35.8 2.5 collective-permute-start.7
  38.4 2.0 collective-permute-done.3.w_got
  40.4 1.2 copy-done.19
  41.7 1.4 copy-done
  43.1 1.5 copy-done.16
  44.6 1.5 copy-done.20
  46.0 9.3 %shard_map.221 = (bf16[3,1024,384]{2,1,0:T(8,128)(2,1)S(1)}, bf16[768,1024]{1,0:T(8,128)(2,1)S(1)}, bf16[3,768,384]{2,1,0:T(8,128)(2,1)S(1)}) custom-call(s32[8]{0:T(128)S(1)} %stack.90.flags, bf16[1024,768]{1,0:T(8,128)(2,1)S(1)} %copy-done, f32[4,768]{1,0:T(4,128)S(1)} %pad_maximum_fusion.7.vectors.refs_5_, f32[1024,128]{1,0:T(8,128)S(1)} %get-tuple-element.96.cos_ref, ...), custom_call_target="tpu_custom_call" | custom-call | bytes 27000000 | tf_op jit(solution)/shard_map/pallas_call | solution.py:264
  55.3 17.2 %shard_map.222.mixed_ref = bf16[1024,384]{1,0:T(8,128)(2,1)S(1)} custom-call(s32[1024,128]{1,0:T(8,128)S(1)} %copy-done.15, bf16[3,1024,384]{2,1,0:T(8,128)(2,1)S(1)} %get-tuple-element.99.q_ref.k_ref.v_ref, bf16[3,1024,384]{2,1,0:T(8,128)(2,1)S(1)} %get-tuple-element.99.q_ref.k_ref.v_ref, bf16[3,1024,384]{2,1,0:T(8,128)(2,1)S(1)} %get-tuple-element.99.q_ref.k_ref.v_ref), custom_call_target="tpu_custom_call" | custom-call | bytes 51000000 | tf_op jit(solution)/shard_map/pallas_call | solution.py:90
  72.6 1.8 broadcast_select_fusion
  76.1 3.1 %collective-permute-start.8 = (bf16[768,768]{1,0:T(8,128)(2,1)S(1)}, bf16[768,768]{1,0:T(8,128)(2,1)}, u32[]{:S(2)}, u32[]{:S(2)}) collective-permute-start(bf16[768,768]{1,0:T(8,128)(2,1)S(1)} %copy-done.44), channel_id=1, source_target_pairs={{1,16},{3,18},{5,20},{7,22},{9,24},{11,26},{13,28},{15,30},{16,1},... | collective-permute-start | bytes 3538952 | tf_op jit(solution)/shard_map/ppermute | solution.py:784
  79.2 2.7 collective-permute-start.9
  82.1 2.3 collective-permute-done.6
  84.3 1.8 maximum_select_fusion.1.refs_4_.cot_ref
  87.3 24.5 %shard_map.223 = (bf16[1024,768]{1,0:T(8,128)(2,1)}, bf16[768,1024]{1,0:T(8,128)(2,1)}, bf16[1024,768]{1,0:T(8,128)(2,1)}, bf16[768,1024]{1,0:T(8,128)(2,1)}, f3...) custom-call(s32[8]{0:T(128)S(1)} %stack.90.flags, ...), custom_call_target="tpu_custom_call" | custom-call | bytes 60000000 | tf_op jit(solution)/shard_map/pallas_call | solution.py:389
  113.0 20.6 %shard_map.224 = (bf16[1024,768]{1,0:T(8,128)(2,1)}, bf16[1024,768]{1,0:T(8,128)(2,1)}, bf16[4,768,384]{2,1,0:T(8,128)(2,1)}, bf16[768,768]{1,0:T(8,128)(2,1)S(1)}) custom-call(s32[8]{0:T(128)S(1)} %stack.90.flags, bf16[1024,768]{1,0:T(8,128)(2,1)} %get-tuple-element.103.refs_0_, bf16[768,1024]{1,0:T(8,128)(2,1)} %get-tuple-element.104.refs_1_, ...), custom_call_target="tpu_custom_call" | custom-call | bytes 60000000 | tf_op jit(solution)/shard_map/pallas_call | solution.py:389
  136.1 2.3 collective-permute-done.10.back_got
  138.4 1.4 copy-done.1
  139.8 1.4 copy-done.3
  141.2 1.8 copy-done.6
  143.0 1.4 copy-done.9
  144.4 1.4 copy-done.31
  145.8 6.9 %shard_map.225 = (bf16[1024,768]{1,0:T(8,128)(2,1)S(1)}, bf16[1024,384]{1,0:T(8,128)(2,1)S(1)}, bf16[768,384]{1,0:T(8,128)(2,1)S(1)}, f32[8,768]{1,0:T(8,128)S(1)}) custom-call(s32[8]{0:T(128)S(1)} %stack.90.flags, f32[5]{0:T(128)S(1)} %copy-done.38, bf16[1024,768]{1,0:T(8,128)(2,1)S(1)} %copy-done.1, bf16[1024,768]{1,0:T(8,128)(2,1)S(1)} %copy-done.6, ...), custom_call_target="tpu_custom_call" | custom-call | bytes 36000000 | tf_op jit(solution)/shard_map/pallas_call | solution.py:514
  152.7 28.6 %shard_map.226.grad_ref = bf16[3,1024,384]{2,1,0:T(8,128)(2,1)S(1)} custom-call(s32[8,1024]{1,0:T(8,128)S(1)} %broadcast_in_dim.21.start_ref, f32[1024,128]{1,0:T(8,128)S(1)} %get-tuple-element.96.cos_ref, f32[1024,128]{1,0:T(8,128)S(1)} %get-tuple-element.97.sin_ref, bf16[3,1024,384]{2,1,0:T(8,128)(2,1)S(1)} %get-tuple-element.99.q_ref.k_ref.v_ref, ...), custom_call_target="tpu_custom_call" | custom-call | bytes 84000000 | tf_op jit(solution)/shard_map/pallas_call | solution.py:167
  181.4 6.1 %shard_map.227 = (bf16[768,384]{1,0:T(8,128)(2,1)}, bf16[768,384]{1,0:T(8,128)(2,1)}, bf16[768,384]{1,0:T(8,128)(2,1)}, bf16[768,384]{1,0:T(8,128)(2,1)}) custom-call(s32[8]{0:T(128)S(1)} %stack.90.flags, bf16[768,1024]{1,0:T(8,128)(2,1)S(1)} %copy-done.24, bf16[3,1024,384]{2,1,0:T(8,128)(2,1)S(1)} %shard_map.226.grad_ref, ...), custom_call_target="tpu_custom_call" | custom-call | bytes 9000000 | tf_op jit(solution)/shard_map/pallas_call | solution.py:560
  187.5 3.0 collective-permute-start.16
  190.5 1.7 collective-permute-start.18
  192.5 4.0 %shard_map.228 = (f32[512,768]{1,0:T(8,128)S(1)}, bf16[512,768]{1,0:T(8,128)(2,1)S(1)}, f32[8,768]{1,0:T(8,128)S(1)}) custom-call(s32[8]{0:T(128)S(1)} %stack.90.flags, bf16[3,1024,384]{2,1,0:T(8,128)(2,1)S(1)} %shard_map.226.grad_ref, bf16[3,768,384]{2,1,0:T(8,128)(2,1)S(1)} %copy-done.18, bf16[1024,768]{1,0:T(8,128)(2,1)S(1)} %copy-done.1), custom_call_target="tpu_custom_call" | custom-call | bytes 12000000 | tf_op jit(solution)/shard_map/pallas_call | solution.py:599
  197.4 4.2 %shard_map.229 = (f32[512,768]{1,0:T(8,128)S(1)}, bf16[512,768]{1,0:T(8,128)(2,1)S(1)}, f32[8,768]{1,0:T(8,128)S(1)}) custom-call(s32[8]{0:T(128)S(1)} %stack.90.flags, bf16[1024,768]{1,0:T(8,128)(2,1)S(1)} %copy-done.29, bf16[1024,768]{1,0:T(8,128)(2,1)S(1)} %copy-done.30, bf16[768,768]{1,0:T(8,128)(2,1)S(1)} %copy-done.33, ...), custom_call_target="tpu_custom_call" | custom-call | bytes 24000000 | tf_op jit(solution)/shard_map/pallas_call | solution.py:454
  205.1 3.3 %collective-permute-done.12 = f32[9,768]{1,0:T(8,128)S(1)} collective-permute-done((f32[9,768]{1,0:T(8,128)S(1)}, f32[9,768]{1,0:T(8,128)S(1)}, u32[]{:S(2)}, u32[]{:S(2)}) %collective-permute-start.12) | collective-permute-done | bytes 27680 | tf_op jit(solution)/shard_map/ppermute | solution.py:858
  208.4 2.3 collective-permute-start.13
  210.7 3.3 %collective-permute-done.13 = f32[9,768]{1,0:T(8,128)S(1)} collective-permute-done((f32[9,768]{1,0:T(8,128)S(1)}, f32[9,768]{1,0:T(8,128)S(1)}, u32[]{:S(2)}, u32[]{:S(2)}) %collective-permute-start.13) | collective-permute-done | bytes 27680 | tf_op jit(solution)/shard_map/ppermute | solution.py:858
  214.1 2.4 collective-permute-start.14
  216.4 2.9 collective-permute-done.14
  219.3 1.5 collective-permute-start.15
  220.8 1.7 collective-permute-done.15
  222.6 2.0 collective-permute-start.20
  224.8 2.8 add_convert_fusion
  227.9 2.8 shard_map.230
  231.6 4.0 %collective-permute-start.22 = (bf16[512,768]{1,0:T(8,128)(2,1)}, bf16[512,768]{1,0:T(8,128)(2,1)S(1)}, u32[]{:S(2)}, u32[]{:S(2)}) collective-permute-start(bf16[512,768]{1,0:T(8,128)(2,1)} %get-tuple-element.146.grad_own), channel_id=1, source_target_pairs={{1,16},{3,18},{5,20},{7,22},{9,24},{11,26},{13,28},{15,30},{16,1},... | collective-permute-start | bytes 2359304 | tf_op jit(solution)/shard_map/ppermute | solution.py:784
  235.7 1.2 dynamic-slice_bitcast_fusion
  237.3 3.2 %collective-permute-start.24 = (bf16[192,384]{1,0:T(8,128)(2,1)S(1)}, bf16[192,384]{1,0:T(8,128)(2,1)S(1)}, u32[]{:S(2)}, u32[]{:S(2)}) collective-permute-start(bf16[192,384]{1,0:T(8,128)(2,1)S(1)} %get-tuple-element.219), channel_id=1, source_target_pairs={{0,8},{4,12},{8,0},{12,4},{1,9},{5,13},{9,1},{13,5},{2,10},{6,14},... | collective-permute-start | bytes 442376 | tf_op jit(solution)/shard_map/ppermute | solution.py:850
  240.5 1.4 collective-permute-start.25
  241.9 13.0 %collective-permute-done.24 = bf16[192,384]{1,0:T(8,128)(2,1)S(1)} collective-permute-done((bf16[192,384]{1,0:T(8,128)(2,1)S(1)}, bf16[192,384]{1,0:T(8,128)(2,1)S(1)}, u32[]{:S(2)}, u32[]{:S(2)}) %collective-permute-start.24) | collective-permute-done | bytes 147488 | tf_op jit(solution)/shard_map/ppermute | solution.py:850
  254.8 6.2 %collective-permute-done.25 = bf16[192,384]{1,0:T(8,128)(2,1)S(1)} collective-permute-done((bf16[192,384]{1,0:T(8,128)(2,1)S(1)}, bf16[192,384]{1,0:T(8,128)(2,1)S(1)}, u32[]{:S(2)}, u32[]{:S(2)}) %collective-permute-start.25) | collective-permute-done | bytes 147488 | tf_op jit(solution)/shard_map/ppermute | solution.py:850
  261.0 3.5 %collective-permute-start.26 = (bf16[512,768]{1,0:T(8,128)(2,1)S(1)}, bf16[512,768]{1,0:T(8,128)(2,1)S(1)}, u32[]{:S(2)}, u32[]{:S(2)}) collective-permute-start(bf16[512,768]{1,0:T(8,128)(2,1)S(1)} %copy-done.37), channel_id=1, source_target_pairs={{1,16},{3,18},{5,20},{7,22},{9,24},{11,26},{13,28},{15,30},{16,1},... | collective-permute-start | bytes 2359304 | tf_op jit(solution)/shard_map/ppermute | solution.py:784
  264.7 1.4 collective-permute-done.27
  266.1 1.3 collective-permute-start.28
  268.4 1.8 collective-permute-start.29
  270.2 4.4 %collective-permute-done.28.got_ref = bf16[2,192,384]{2,1,0:T(8,128)(2,1)S(1)} collective-permute-done((bf16[2,192,384]{2,1,0:T(8,128)(2,1)S(1)}, bf16[2,192,384]{2,1,0:T(8,128)(2,1)S(1)}, u32[]{:S(2)}, u32[]{:S(2)}) %collective-permute-start.28) | collective-permute-done | bytes 294944 | tf_op jit(solution)/shard_map/ppermute | solution.py:807
  274.6 1.9 collective-permute-done.29
  277.7 12.7 %collective-permute-start.31 = (bf16[2,2,2,192,384]{4,3,2,1,0:T(8,128)(2,1)S(1)}, bf16[2,2,2,192,384]{4,3,2,1,0:T(8,128)(2,1)S(1)}, u32[]{:S(2)}, u32[]{:S(2)}) collective-permute-start(bf16[2,2,2,192,384]{4,3,2,1,0:T(8,128)(2,1)S(1)} %pad_maximum_fusion.2.own_ref), channel_id=1, source_target_pairs={{0,1},{1,0},{2,3},{3,2},{4,5},{5,4},{6,7},{7,6},{8,9},{9,8},{10,11... | collective-permute-start | bytes 3538952 | tf_op jit(solution)/shard_map/ppermute | solution.py:811
  291.7 1.6 shard_map.232
  293.3 2.3 shard_map.231
  295.6 2.1 shard_map.233
  (177 shorter events, 22.8 us)
Async XLA Ops:
  7.2 196.9 %reduce-scatter.13.cloned.1.call-start = ((), (), s32[]{:S(2)}) async-start(), calls=%async_computation.6 | async-start | bytes 2949120
  7.2 18.8 %collective-permute-start.2 = (s32[1,3]{1,0:T(1,128)}, s32[1,3]{1,0:T(1,128)S(1)}, u32[]{:S(2)}, u32[]{:S(2)}) collective-permute-start(s32[1,3]{1,0:T(1,128)} %param.16), channel_id=1, source_target_pairs={{0,1},{1,0},{2,3},{3,2},{4,5},{5,4},{6,7},{7,6},{8,9},{9,8},{10,11... | collective-permute-start | bytes 44 | tf_op jit(solution)/shard_map/ppermute | solution.py:811
  8.0 18.3 %collective-permute-start = (bf16[512,768]{1,0:T(8,128)(2,1)}, bf16[512,768]{1,0:T(8,128)(2,1)}, u32[]{:S(2)}, u32[]{:S(2)}) collective-permute-start(bf16[512,768]{1,0:T(8,128)(2,1)} %bitcast.55), channel_id=1, source_target_pairs={{1,16},{3,18},{5,20},{7,22},{9,24},{11,26},{13,28},{15,30},{16,1},... | collective-permute-start | bytes 2359304 | tf_op jit(solution)/shard_map/ppermute | solution.py:784
  11.0 29.4 %collective-permute-start.3 = (bf16[3,768,384]{2,1,0:T(8,128)(2,1)}, bf16[3,768,384]{2,1,0:T(8,128)(2,1)S(1)}, u32[]{:S(2)}, u32[]{:S(2)}) collective-permute-start(bf16[3,768,384]{2,1,0:T(8,128)(2,1)} %w_own.1), channel_id=1, source_target_pairs={{1,16},{3,18},{5,20},{7,22},{9,24},{11,26},{13,28},{15,30},{16,1},... | collective-permute-start | bytes 5308424 | tf_op jit(solution)/shard_map/ppermute | solution.py:784
  13.6 3.0 copy-start.41
  16.5 2.4 copy-start.13
  16.6 2.5 copy-start.14
  16.6 2.5 copy-start.38
  19.1 4.2 %copy-start.46 = (bf16[384,768]{1,0:T(8,128)(2,1)S(1)}, bf16[384,768]{1,0:T(8,128)(2,1)}, u32[]{:S(2)}) copy-start(bf16[384,768]{1,0:T(8,128)(2,1)} %param.21) | copy-start | bytes 1769476
  24.4 1.8 copy-start.45
  27.5 2.4 collective-permute-start.1
  32.8 39.8 %collective-permute-start.4 = (bf16[896,768]{1,0:T(8,128)(2,1)}, bf16[896,768]{1,0:T(8,128)(2,1)}, u32[]{:S(2)}, u32[]{:S(2)}) collective-permute-start(bf16[896,768]{1,0:T(8,128)(2,1)} %pad_maximum_fusion.1), channel_id=1, source_target_pairs={{1,16},{3,18},{5,20},{7,22},{9,24},{11,26},{13,28},{15,30},{16,1},... | collective-permute-start | bytes 4128776 | tf_op jit(solution)/shard_map/ppermute | solution.py:784
  35.8 50.3 %collective-permute-start.7 = (bf16[1536,768]{1,0:T(8,128)(2,1)}, bf16[1536,768]{1,0:T(8,128)(2,1)}, u32[]{:S(2)}, u32[]{:S(2)}) collective-permute-start(bf16[1536,768]{1,0:T(8,128)(2,1)} %pad_maximum_fusion), channel_id=1, source_target_pairs={{1,16},{3,18},{5,20},{7,22},{9,24},{11,26},{13,28},{15,30},{16,1},... | collective-permute-start | bytes 7077896 | tf_op jit(solution)/shard_map/ppermute | solution.py:784
  46.0 9.3 %copy-start.15 = (s32[1024,128]{1,0:T(8,128)S(1)}, s32[1024,128]{1,0:T(8,128)}, u32[]{:S(2)}) copy-start(s32[1024,128]{1,0:T(8,128)} %broadcast_in_dim.20.start_ref) | copy-start | bytes 1572868
  55.3 17.2 %copy-start.17 = (bf16[3,768,384]{2,1,0:T(8,128)(2,1)}, bf16[3,768,384]{2,1,0:T(8,128)(2,1)S(1)}, u32[]{:S(2)}) copy-start(bf16[3,768,384]{2,1,0:T(8,128)(2,1)S(1)} %get-tuple-element.117.weight) | copy-start | bytes 5308420
  55.3 17.2 %copy-start.23 = (bf16[768,1024]{1,0:T(8,128)(2,1)}, bf16[768,1024]{1,0:T(8,128)(2,1)S(1)}, u32[]{:S(2)}) copy-start(bf16[768,1024]{1,0:T(8,128)(2,1)S(1)} %get-tuple-element.113.turned_ref) | copy-start | bytes 4718596
  74.4 7.6 %copy-start.42 = (bf16[896,768]{1,0:T(8,128)(2,1)}, bf16[896,768]{1,0:T(8,128)(2,1)S(1)}, u32[]{:S(2)}) copy-start(bf16[896,768]{1,0:T(8,128)(2,1)S(1)} %broadcast_select_fusion) | copy-start | bytes 4128772
  74.4 4.8 %copy-start.43 = (bf16[768,768]{1,0:T(8,128)(2,1)S(1)}, bf16[768,768]{1,0:T(8,128)(2,1)}, u32[]{:S(2)}) copy-start(bf16[768,768]{1,0:T(8,128)(2,1)} %get-tuple-element.110) | copy-start | bytes 3538948
  75.4 10.8 %copy-start.5 = (bf16[1024,768]{1,0:T(8,128)(2,1)}, bf16[1024,768]{1,0:T(8,128)(2,1)S(1)}, u32[]{:S(2)}) copy-start(bf16[1024,768]{1,0:T(8,128)(2,1)S(1)} %convolution_convert_fusion.refs_2_.own_ref) | copy-start | bytes 4718596
  75.4 10.8 %collective-permute-start.5 = (bf16[1024,768]{1,0:T(8,128)(2,1)S(1)}, bf16[1024,768]{1,0:T(8,128)(2,1)S(1)}, u32[]{:S(2)}, u32[]{:S(2)}) collective-permute-start(bf16[1024,768]{1,0:T(8,128)(2,1)S(1)} %convolution_convert_fusion.refs_2_.own_ref), channel_id=1, source_target_pairs={{0,1},{1,0},{2,3},{3,2},{4,5},{5,4},{6,7},{7,6},{8,9},{9,8},{10,11... | collective-permute-start | bytes 4718600 | tf_op jit(solution)/shard_map/ppermute | solution.py:811
  76.1 36.8 %collective-permute-start.8 = (bf16[768,768]{1,0:T(8,128)(2,1)S(1)}, bf16[768,768]{1,0:T(8,128)(2,1)}, u32[]{:S(2)}, u32[]{:S(2)}) collective-permute-start(bf16[768,768]{1,0:T(8,128)(2,1)S(1)} %copy-done.44), channel_id=1, source_target_pairs={{1,16},{3,18},{5,20},{7,22},{9,24},{11,26},{13,28},{15,30},{16,1},... | collective-permute-start | bytes 3538952 | tf_op jit(solution)/shard_map/ppermute | solution.py:784
  79.2 33.7 %collective-permute-start.9 = (bf16[768,768]{1,0:T(8,128)(2,1)S(1)}, bf16[768,768]{1,0:T(8,128)(2,1)}, u32[]{:S(2)}, u32[]{:S(2)}) collective-permute-start(bf16[768,768]{1,0:T(8,128)(2,1)S(1)} %copy-done.43), channel_id=1, source_target_pairs={{1,16},{3,18},{5,20},{7,22},{9,24},{11,26},{13,28},{15,30},{16,1},... | collective-permute-start | bytes 3538952 | tf_op jit(solution)/shard_map/ppermute | solution.py:784
  82.0 2.4 collective-permute-start.6
  112.9 122.7 %reduce-scatter.15.cloned.1.call-start = ((), (), s32[]{:S(2)}) async-start(), calls=%async_computation.7 | async-start | bytes 2949120
  134.7 132.7 %reduce-scatter.9.cloned.1.call-start = ((), (), s32[]{:S(2)}) async-start(), calls=%async_computation.4 | async-start | bytes 737280 | tf_op jit(solution)/shard_map/reduce_scatter | solution.py:838
  134.7 3.7 %copy-start.12 = (bf16[1024,384]{1,0:T(8,128)(2,1)S(1)}, bf16[1024,384]{1,0:T(8,128)(2,1)}, u32[]{:S(2)}) copy-start(bf16[1024,384]{1,0:T(8,128)(2,1)} %copy-done.11) | copy-start | bytes 2359300
  134.7 3.7 %collective-permute-start.10 = (bf16[1024,768]{1,0:T(8,128)(2,1)}, bf16[1024,768]{1,0:T(8,128)(2,1)S(1)}, u32[]{:S(2)}, u32[]{:S(2)}) collective-permute-start(bf16[1024,768]{1,0:T(8,128)(2,1)} %get-tuple-element.111.back_own), channel_id=1, source_target_pairs={{0,1},{1,0},{2,3},{3,2},{4,5},{5,4},{6,7},{7,6},{8,9},{9,8},{10,11... | collective-permute-start | bytes 4718600 | tf_op jit(solution)/shard_map/ppermute | solution.py:811
  152.7 28.7 %copy-start.25 = (bf16[1024,768]{1,0:T(8,128)(2,1)}, bf16[1024,768]{1,0:T(8,128)(2,1)S(1)}, u32[]{:S(2)}) copy-start(bf16[1024,768]{1,0:T(8,128)(2,1)S(1)} %get-tuple-element.141.resid_ref) | copy-start | bytes 4718596
  152.7 28.7 %copy-start.24 = (bf16[768,1024]{1,0:T(8,128)(2,1)S(1)}, bf16[768,1024]{1,0:T(8,128)(2,1)}, u32[]{:S(2)}) copy-start(bf16[768,1024]{1,0:T(8,128)(2,1)} %copy-done.23) | copy-start | bytes 4718596
  152.7 44.6 %copy-start.30 = (bf16[1024,768]{1,0:T(8,128)(2,1)S(1)}, bf16[1024,768]{1,0:T(8,128)(2,1)}, u32[]{:S(2)}) copy-start(bf16[1024,768]{1,0:T(8,128)(2,1)} %get-tuple-element.121.act_late) | copy-start | bytes 4718596
  152.7 44.6 %copy-start.33 = (bf16[768,768]{1,0:T(8,128)(2,1)S(1)}, bf16[768,768]{1,0:T(8,128)(2,1)}, u32[]{:S(2)}) copy-start(bf16[768,768]{1,0:T(8,128)(2,1)} %copy-done.32) | copy-start | bytes 3538948
  152.7 44.6 %copy-start.35 = (bf16[768,768]{1,0:T(8,128)(2,1)S(1)}, bf16[768,768]{1,0:T(8,128)(2,1)}, u32[]{:S(2)}) copy-start(bf16[768,768]{1,0:T(8,128)(2,1)} %copy-done.34) | copy-start | bytes 3538948
  181.4 11.1 %copy-start.18 = (bf16[3,768,384]{2,1,0:T(8,128)(2,1)S(1)}, bf16[3,768,384]{2,1,0:T(8,128)(2,1)}, u32[]{:S(2)}) copy-start(bf16[3,768,384]{2,1,0:T(8,128)(2,1)} %copy-done.17) | copy-start | bytes 5308420
  181.4 15.9 %copy-start.10 = (bf16[1024,768]{1,0:T(8,128)(2,1)S(1)}, bf16[1024,768]{1,0:T(8,128)(2,1)}, u32[]{:S(2)}) copy-start(bf16[1024,768]{1,0:T(8,128)(2,1)} %copy-done.8) | copy-start | bytes 4718596
  181.4 15.9 %copy-start.29 = (bf16[1024,768]{1,0:T(8,128)(2,1)S(1)}, bf16[1024,768]{1,0:T(8,128)(2,1)}, u32[]{:S(2)}) copy-start(bf16[1024,768]{1,0:T(8,128)(2,1)} %get-tuple-element.120.act_early) | copy-start | bytes 4718596
  187.5 35.1 %collective-permute-start.16 = (bf16[768,384]{1,0:T(8,128)(2,1)}, bf16[768,384]{1,0:T(8,128)(2,1)}, u32[]{:S(2)}, u32[]{:S(2)}) collective-permute-start(bf16[768,384]{1,0:T(8,128)(2,1)} %get-tuple-element.115), channel_id=1, source_target_pairs={{1,16},{3,18},{5,20},{7,22},{9,24},{11,26},{13,28},{15,30},{16,1},... | collective-permute-start | bytes 1769480 | tf_op jit(solution)/shard_map/ppermute | solution.py:788
  190.4 32.1 %collective-permute-start.17 = (bf16[768,384]{1,0:T(8,128)(2,1)}, bf16[768,384]{1,0:T(8,128)(2,1)}, u32[]{:S(2)}, u32[]{:S(2)}) collective-permute-start(bf16[768,384]{1,0:T(8,128)(2,1)} %get-tuple-element.131), channel_id=1, source_target_pairs={{0,1},{1,17},{2,3},{3,19},{4,5},{5,21},{6,7},{7,23},{8,9},{9,25},{... | collective-permute-start | bytes 1769480 | tf_op jit(solution)/shard_map/ppermute | solution.py:788
  190.5 32.1 %collective-permute-start.18 = (bf16[768,384]{1,0:T(8,128)(2,1)}, bf16[768,384]{1,0:T(8,128)(2,1)}, u32[]{:S(2)}, u32[]{:S(2)}) collective-permute-start(bf16[768,384]{1,0:T(8,128)(2,1)} %get-tuple-element.132), channel_id=1, source_target_pairs={{0,2},{1,18},{2,0},{3,16},{4,6},{5,22},{6,4},{7,20},{8,10},{9,26},... | collective-permute-start | bytes 1769480 | tf_op jit(solution)/shard_map/ppermute | solution.py:788
  192.2 30.4 %collective-permute-start.19 = (bf16[768,384]{1,0:T(8,128)(2,1)}, bf16[768,384]{1,0:T(8,128)(2,1)}, u32[]{:S(2)}, u32[]{:S(2)}) collective-permute-start(bf16[768,384]{1,0:T(8,128)(2,1)} %get-tuple-element.133), channel_id=1, source_target_pairs={{0,3},{1,19},{2,1},{3,17},{4,7},{5,23},{6,5},{7,21},{8,11},{9,27},... | collective-permute-start | bytes 1769480 | tf_op jit(solution)/shard_map/ppermute | solution.py:788
  192.4 4.9 %copy-start.2 = (bf16[1024,768]{1,0:T(8,128)(2,1)S(1)}, bf16[1024,768]{1,0:T(8,128)(2,1)}, u32[]{:S(2)}) copy-start(bf16[1024,768]{1,0:T(8,128)(2,1)} %maximum_select_fusion.rows_ref.refs_1_) | copy-start | bytes 4718596
  192.5 4.9 %copy-start.4 = (bf16[1024,768]{1,0:T(8,128)(2,1)S(1)}, bf16[1024,768]{1,0:T(8,128)(2,1)}, u32[]{:S(2)}) copy-start(bf16[1024,768]{1,0:T(8,128)(2,1)} %maximum_select_fusion.1.refs_4_.cot_ref) | copy-start | bytes 4718596
  192.5 4.9 %copy-start.7 = (bf16[1024,768]{1,0:T(8,128)(2,1)S(1)}, bf16[1024,768]{1,0:T(8,128)(2,1)}, u32[]{:S(2)}) copy-start(bf16[1024,768]{1,0:T(8,128)(2,1)} %copy-done.5) | copy-start | bytes 4718596
  203.7 1.3 collective-permute-start.11
  204.1 63.2 %reduce-scatter.11.cloned.1.call-start = ((), (), s32[]{:S(2)}) async-start(), calls=%async_computation.5 | async-start | bytes 737280 | tf_op jit(solution)/shard_map/reduce_scatter | solution.py:838
  205.0 3.4 %collective-permute-start.12 = (f32[9,768]{1,0:T(8,128)S(1)}, f32[9,768]{1,0:T(8,128)S(1)}, u32[]{:S(2)}, u32[]{:S(2)}) collective-permute-start(f32[9,768]{1,0:T(8,128)S(1)} %fusion.7), channel_id=1, source_target_pairs={{0,4},{4,0},{8,12},{12,8},{1,5},{5,1},{9,13},{13,9},{2,6},{6,2},{1... | collective-permute-start | bytes 82952 | tf_op jit(solution)/shard_map/ppermute | solution.py:858
  208.4 5.7 %collective-permute-start.13 = (f32[9,768]{1,0:T(8,128)S(1)}, f32[9,768]{1,0:T(8,128)S(1)}, u32[]{:S(2)}, u32[]{:S(2)}) collective-permute-start(f32[9,768]{1,0:T(8,128)S(1)} %add.100), channel_id=1, source_target_pairs={{0,8},{4,12},{8,0},{12,4},{1,9},{5,13},{9,1},{13,5},{2,10},{6,14},... | collective-permute-start | bytes 82952 | tf_op jit(solution)/shard_map/ppermute | solution.py:858
  214.1 5.2 %collective-permute-start.14 = (f32[9,768]{1,0:T(8,128)S(1)}, f32[9,768]{1,0:T(8,128)S(1)}, u32[]{:S(2)}, u32[]{:S(2)}) collective-permute-start(f32[9,768]{1,0:T(8,128)S(1)} %add.101), channel_id=1, source_target_pairs={{0,16},{16,0},{1,17},{17,1},{2,18},{18,2},{3,19},{19,3},{4,20},{20... | collective-permute-start | bytes 82952 | tf_op jit(solution)/shard_map/ppermute | solution.py:858
  219.3 3.2 %collective-permute-start.15 = (f32[9,768]{1,0:T(8,128)S(1)}, f32[9,768]{1,0:T(8,128)S(1)}, u32[]{:S(2)}, u32[]{:S(2)}) collective-permute-start(f32[9,768]{1,0:T(8,128)S(1)} %add.102), channel_id=1, source_target_pairs={{0,2},{2,0},{1,3},{3,1},{4,6},{6,4},{5,7},{7,5},{8,10},{10,8},{9,1... | collective-permute-start | bytes 82952 | tf_op jit(solution)/shard_map/ppermute | solution.py:858
  222.6 5.3 %copy-start.26 = (bf16[1024,768]{1,0:T(8,128)(2,1)S(1)}, bf16[1024,768]{1,0:T(8,128)(2,1)}, u32[]{:S(2)}) copy-start(bf16[1024,768]{1,0:T(8,128)(2,1)} %copy-done.25) | copy-start | bytes 4718596
  222.6 5.3 %copy-start.28 = (f32[512,768]{1,0:T(8,128)S(1)}, f32[512,768]{1,0:T(8,128)}, u32[]{:S(2)}) copy-start(f32[512,768]{1,0:T(8,128)} %copy-done.27) | copy-start | bytes 4718596
  222.6 4.9 %collective-permute-start.20 = (bf16[512,768]{1,0:T(8,128)(2,1)}, bf16[512,768]{1,0:T(8,128)(2,1)S(1)}, u32[]{:S(2)}, u32[]{:S(2)}) collective-permute-start(bf16[512,768]{1,0:T(8,128)(2,1)} %copy-done.39), channel_id=1, source_target_pairs={{0,1},{1,0},{2,3},{3,2},{4,5},{5,4},{6,7},{7,6},{8,9},{9,8},{10,11... | collective-permute-start | bytes 2359304 | tf_op jit(solution)/shard_map/ppermute | solution.py:811
  224.7 3.2 %collective-permute-start.21 = (bf16[512,768]{1,0:T(8,128)(2,1)}, bf16[512,768]{1,0:T(8,128)(2,1)S(1)}, u32[]{:S(2)}, u32[]{:S(2)}) collective-permute-start(bf16[512,768]{1,0:T(8,128)(2,1)} %copy-done.40), channel_id=1, source_target_pairs={{0,1},{1,0},{2,3},{3,2},{4,5},{5,4},{6,7},{7,6},{8,9},{9,8},{10,11... | collective-permute-start | bytes 2359304 | tf_op jit(solution)/shard_map/ppermute | solution.py:811
  231.6 29.4 %copy-start.37 = (bf16[512,768]{1,0:T(8,128)(2,1)S(1)}, bf16[512,768]{1,0:T(8,128)(2,1)}, u32[]{:S(2)}) copy-start(bf16[512,768]{1,0:T(8,128)(2,1)} %copy-done.36) | copy-start | bytes 2359300
  231.6 29.4 %collective-permute-start.22 = (bf16[512,768]{1,0:T(8,128)(2,1)}, bf16[512,768]{1,0:T(8,128)(2,1)S(1)}, u32[]{:S(2)}, u32[]{:S(2)}) collective-permute-start(bf16[512,768]{1,0:T(8,128)(2,1)} %get-tuple-element.146.grad_own), channel_id=1, source_target_pairs={{1,16},{3,18},{5,20},{7,22},{9,24},{11,26},{13,28},{15,30},{16,1},... | collective-permute-start | bytes 2359304 | tf_op jit(solution)/shard_map/ppermute | solution.py:784
  236.9 4.9 %collective-permute-start.23 = (bf16[192,384]{1,0:T(8,128)(2,1)S(1)}, bf16[192,384]{1,0:T(8,128)(2,1)S(1)}, u32[]{:S(2)}, u32[]{:S(2)}) collective-permute-start(bf16[192,384]{1,0:T(8,128)(2,1)S(1)} %get-tuple-element.220), channel_id=1, source_target_pairs={{0,4},{4,8},{8,12},{12,0},{1,5},{5,9},{9,13},{13,1},{2,6},{6,10},{... | collective-permute-start | bytes 442376 | tf_op jit(solution)/shard_map/ppermute | solution.py:850
  237.3 17.6 %collective-permute-start.24 = (bf16[192,384]{1,0:T(8,128)(2,1)S(1)}, bf16[192,384]{1,0:T(8,128)(2,1)S(1)}, u32[]{:S(2)}, u32[]{:S(2)}) collective-permute-start(bf16[192,384]{1,0:T(8,128)(2,1)S(1)} %get-tuple-element.219), channel_id=1, source_target_pairs={{0,8},{4,12},{8,0},{12,4},{1,9},{5,13},{9,1},{13,5},{2,10},{6,14},... | collective-permute-start | bytes 442376 | tf_op jit(solution)/shard_map/ppermute | solution.py:850
  240.5 20.5 %collective-permute-start.25 = (bf16[192,384]{1,0:T(8,128)(2,1)S(1)}, bf16[192,384]{1,0:T(8,128)(2,1)S(1)}, u32[]{:S(2)}, u32[]{:S(2)}) collective-permute-start(bf16[192,384]{1,0:T(8,128)(2,1)S(1)} %get-tuple-element.218), channel_id=1, source_target_pairs={{0,12},{4,0},{8,4},{12,8},{1,13},{5,1},{9,5},{13,9},{2,14},{6,2},{... | collective-permute-start | bytes 442376 | tf_op jit(solution)/shard_map/ppermute | solution.py:850
  261.0 13.6 %collective-permute-start.26 = (bf16[512,768]{1,0:T(8,128)(2,1)S(1)}, bf16[512,768]{1,0:T(8,128)(2,1)S(1)}, u32[]{:S(2)}, u32[]{:S(2)}) collective-permute-start(bf16[512,768]{1,0:T(8,128)(2,1)S(1)} %copy-done.37), channel_id=1, source_target_pairs={{1,16},{3,18},{5,20},{7,22},{9,24},{11,26},{13,28},{15,30},{16,1},... | collective-permute-start | bytes 2359304 | tf_op jit(solution)/shard_map/ppermute | solution.py:784
  264.6 1.4 collective-permute-start.27
  266.1 8.5 %collective-permute-start.28 = (bf16[2,192,384]{2,1,0:T(8,128)(2,1)S(1)}, bf16[2,192,384]{2,1,0:T(8,128)(2,1)S(1)}, u32[]{:S(2)}, u32[]{:S(2)}) collective-permute-start(bf16[2,192,384]{2,1,0:T(8,128)(2,1)S(1)} %pad_maximum_fusion.4.own_ref), channel_id=1, source_target_pairs={{0,2},{2,0},{1,3},{3,1},{4,6},{6,4},{5,7},{7,5},{8,10},{10,8},{9,1... | collective-permute-start | bytes 884744 | tf_op jit(solution)/shard_map/ppermute | solution.py:807
  268.4 8.2 %collective-permute-start.29 = (bf16[2,192,384]{2,1,0:T(8,128)(2,1)S(1)}, bf16[2,192,384]{2,1,0:T(8,128)(2,1)S(1)}, u32[]{:S(2)}, u32[]{:S(2)}) collective-permute-start(bf16[2,192,384]{2,1,0:T(8,128)(2,1)S(1)} %pad_maximum_fusion.5), channel_id=1, source_target_pairs={{1,17},{3,19},{5,21},{7,23},{9,25},{11,27},{13,29},{15,31},{16,0},... | collective-permute-start | bytes 884744 | tf_op jit(solution)/shard_map/ppermute | solution.py:799
  276.7 16.6 %copy-start.22 = (f32[512,768]{1,0:T(8,128)S(1)}, f32[512,768]{1,0:T(8,128)}, u32[]{:S(2)}) copy-start(f32[512,768]{1,0:T(8,128)} %copy-done.21) | copy-start | bytes 4718596
  276.7 0.8 collective-permute-start.30
  277.7 17.9 %collective-permute-start.31 = (bf16[2,2,2,192,384]{4,3,2,1,0:T(8,128)(2,1)S(1)}, bf16[2,2,2,192,384]{4,3,2,1,0:T(8,128)(2,1)S(1)}, u32[]{:S(2)}, u32[]{:S(2)}) collective-permute-start(bf16[2,2,2,192,384]{4,3,2,1,0:T(8,128)(2,1)S(1)} %pad_maximum_fusion.2.own_ref), channel_id=1, source_target_pairs={{0,1},{1,0},{2,3},{3,2},{4,5},{5,4},{6,7},{7,6},{8,9},{9,8},{10,11... | collective-permute-start | bytes 3538952 | tf_op jit(solution)/shard_map/ppermute | solution.py:811
  (24 other events, 31.2 us)
Sparse Core Ops, SparseCore 0:
  113.0 37.9 reduce-scatter.12
  154.1 37.3 reduce-scatter.14
  204.2 20.2 reduce-scatter.8
  235.8 25.9 reduce-scatter.10

commit v2 on v1

v2 whole, which is shorter than its diff:
```python
import functools
import itertools
import math

import jax
import jax.numpy as jnp
from jax import lax
from jax.experimental import pallas as pl
from jax.experimental.pallas import tpu as pltpu
from jax.sharding import Mesh, PartitionSpec as P

HEAD_DIM = 64
LONGEST = 512
NEG_FILL = -1e30
NORM_EPS = 1e-05
RATE = 3e6
ROOM = 60 << 20


def lasting(microseconds):
    return pl.CostEstimate(flops=0, transcendentals=0, bytes_accessed=int(microseconds * RATE))


BLOCK = 256
LANES = 128
NT = (((1,), (1,)), ((), ()))


def dot(a, b, dims=(((1,), (0,)), ((), ()))):
    return lax.dot_general(a, b, dims, preferred_element_type=jnp.float32)


def spans(whole, reach):
    back = -(-(reach - 1) // BLOCK)
    runs = []
    for i in range(whole // BLOCK):
        count = min(i, back) + 1
        if runs and runs[-1][2] == count:
            runs[-1][1] = i + 1
        else:
            runs.append([i, i + 1, count])
    return runs


def each_block(whole, reach, body):
    for first, last, count in spans(whole, reach):

        def step(i, carry, count=count):
            body(i, i + 1 - count, count)
            return carry

        lax.fori_loop(first, last, step, 0)


def block_at(i, count=1):
    return pl.ds(pl.multiple_of(i * BLOCK, BLOCK), count * BLOCK)


def head_query(q_ref, apart_ref, i, head):
    lane = lax.broadcasted_iota(jnp.int32, (BLOCK, LANES), 1) // HEAD_DIM
    query = q_ref[block_at(i), :] * (HEAD_DIM**-0.5)
    query = jnp.where(lane == head, query, jnp.zeros_like(query))
    return query, jnp.concatenate([query, apart_ref[block_at(i), :]], axis=1)


def attend_kernel(reach, apart_ref, member_ref, q_ref, k_ref, v_ref, out_ref, keys):
    whole = q_ref.shape[0]
    lane = lax.broadcasted_iota(jnp.int32, (BLOCK, LANES), 1) // HEAD_DIM
    keys[:, :LANES] = k_ref[...]
    keys[:, LANES:] = member_ref[...]

    def one(i, first, count, head):
        unused, query = head_query(q_ref, apart_ref, i, head)
        own = dot(query, keys[block_at(i), :], NT)
        key_at = lax.broadcasted_iota(jnp.int32, own.shape, 1)
        query_at = lax.broadcasted_iota(jnp.int32, own.shape, 0)
        scores = jnp.where(key_at <= query_at, own, NEG_FILL)
        if count > 1:
            scores = jnp.concatenate([dot(query, keys[block_at(first, count - 1), :], NT), scores], axis=1)
        exponent = jnp.exp(scores - jnp.max(scores, axis=1, keepdims=True))
        row_sum = jnp.sum(exponent, axis=1, keepdims=True)
        return dot(exponent.astype(jnp.bfloat16), v_ref[block_at(first, count), :]) * (1.0 / row_sum)

    def body(i, first, count):
        mixed = [one(i, first, count, head) for head in range(2)]
        out_ref[block_at(i), :] = jnp.where(lane == 0, *mixed).astype(out_ref.dtype)

    each_block(whole, reach, body)


def attend(apart, member, projected, reach):
    count, whole, width = projected.shape

    def block(c):
        return pl.BlockSpec((None, whole, LANES), lambda p: (c, 0, p))

    table = pl.BlockSpec((whole, LANES), lambda p: (0, 0))
    return pl.pallas_call(
        functools.partial(attend_kernel, reach),
        grid=(width // LANES,),
        in_specs=[table, table, block(0), block(1), block(2)],
        out_specs=pl.BlockSpec((whole, LANES), lambda p: (0, p)),
        out_shape=jax.ShapeDtypeStruct((whole, width), jnp.bfloat16),
        scratch_shapes=[pltpu.VMEM((whole, 2 * LANES), jnp.bfloat16)],
        compiler_params=pltpu.CompilerParams(vmem_limit_bytes=ROOM),
        cost_estimate=lasting(12),
    )(apart, member, projected, projected, projected)


def turn_back(field, cos, sin):
    half = HEAD_DIM // 2
    lane = lax.broadcasted_iota(jnp.int32, field.shape, 1) % HEAD_DIM
    crossed = jnp.where(lane < half, pltpu.roll(field, LANES - half, 1), pltpu.roll(field, half, 1))
    return field * cos - crossed * sin


def attend_back_kernel(
    reach, apart_ref, member_ref, cos_ref, sin_ref, q_ref, k_ref, v_ref, g_ref, out_ref, keys, keys_t, key_acc, value_acc
):
    whole = q_ref.shape[0]
    lane = lax.broadcasted_iota(jnp.int32, (BLOCK, LANES), 1) // HEAD_DIM
    keys[:, :LANES] = k_ref[...]
    keys[:, LANES:] = member_ref[...]
    keys_t[...] = k_ref[...].astype(jnp.float32).T.astype(jnp.bfloat16)
    key_acc[...] = jnp.zeros_like(key_acc)
    value_acc[...] = jnp.zeros_like(value_acc)

    def one(i, first, count, head):
        span = block_at(first, count)
        plain, query = head_query(q_ref, apart_ref, i, head)
        grad = g_ref[block_at(i), :]
        grad = jnp.where(lane == head, grad, jnp.zeros_like(grad))
        own = dot(keys[block_at(i), :], query, NT)
        key_at = lax.broadcasted_iota(jnp.int32, own.shape, 0)
        query_at = lax.broadcasted_iota(jnp.int32, own.shape, 1)
        scores = jnp.where(key_at <= query_at, own, NEG_FILL)
        if count > 1:
            scores = jnp.concatenate([dot(keys[block_at(first, count - 1), :], query, NT), scores], axis=0)
        exponent = jnp.exp(scores - jnp.max(scores, axis=0, keepdims=True))
        probs = exponent * (1.0 / jnp.sum(exponent, axis=0, keepdims=True))
        grad_values = dot(probs.astype(jnp.bfloat16), grad)
        weighted = probs * dot(v_ref[span, :], grad, NT)
        grad_scores = (weighted - probs * jnp.sum(weighted, axis=0, keepdims=True)).astype(jnp.bfloat16)
        here = dot(keys_t[:, span], grad_scores)
        return grad_values, dot(grad_scores, plain), here

    def body(i, first, count):
        span, at = block_at(first, count), block_at(i)
        values, keys_, queries = zip(*[one(i, first, count, head) for head in range(2)])
        value_acc[span, :] += values[0] + values[1]
        key_acc[span, :] += keys_[0] + keys_[1]
        row = lax.broadcasted_iota(jnp.int32, queries[0].shape, 0) // HEAD_DIM
        both = jnp.where(row == 0, *queries).T * (HEAD_DIM**-0.5)
        out_ref[0, at, :] = turn_back(both, cos_ref[at, :], sin_ref[at, :]).astype(out_ref.dtype)

    each_block(whole, reach, body)

    def finish(i, carry):
        at = block_at(i)
        out_ref[1, at, :] = turn_back(key_acc[at, :], cos_ref[at, :], sin_ref[at, :]).astype(out_ref.dtype)
        out_ref[2, at, :] = value_acc[at, :].astype(out_ref.dtype)
        return carry

    lax.fori_loop(0, whole // BLOCK, finish, 0)


def attend_back(apart, member, cos, sin, projected, grad_mixed, reach):
    count, whole, width = projected.shape

    def block(c):
        return pl.BlockSpec((None, whole, LANES), lambda p: (c, 0, p))

    table = pl.BlockSpec((whole, LANES), lambda p: (0, 0))
    return pl.pallas_call(
        functools.partial(attend_back_kernel, reach),
        grid=(width // LANES,),
        in_specs=[table] * 4 + [block(0), block(1), block(2), pl.BlockSpec((whole, LANES), lambda p: (0, p))],
        out_specs=pl.BlockSpec((count, whole, LANES), lambda p: (0, 0, p)),
        out_shape=jax.ShapeDtypeStruct((count, whole, width), jnp.bfloat16),
        scratch_shapes=[
            pltpu.VMEM((whole, 2 * LANES), jnp.bfloat16),
            pltpu.VMEM((LANES, whole), jnp.bfloat16),
            pltpu.VMEM((whole, LANES), jnp.float32),
            pltpu.VMEM((whole, LANES), jnp.float32),
        ],
        compiler_params=pltpu.CompilerParams(vmem_limit_bytes=ROOM),
        cost_estimate=lasting(22),
    )(apart, member, cos, sin, projected, projected, projected, grad_mixed)


ROWS = 256


def norm_parts(field):
    centered = field - jnp.mean(field, axis=-1, keepdims=True)
    scale = lax.rsqrt(jnp.mean(centered * centered, axis=-1, keepdims=True) + NORM_EPS)
    return centered * scale, scale


def wide(ref, at):
    return ref[at, :].astype(jnp.float32)


def row_blocks(count, body):
    def step(i, carry):
        body(i, pl.ds(pl.multiple_of(i * ROWS, ROWS), ROWS))
        return carry

    lax.fori_loop(0, count // ROWS, step, 0)


TALL = 512


def streamed(kernel, steps, scalars, fields, outs, scratch, microseconds):
    def spec(shape, block=None, at=None):
        if block is None:
            return pl.BlockSpec(shape, lambda i, *scalars: (0,) * len(shape))
        return pl.BlockSpec(block, at)

    fields = [field if isinstance(field, tuple) else (field,) for field in fields]
    return pl.pallas_call(
        kernel,
        grid_spec=pltpu.PrefetchScalarGridSpec(
            num_scalar_prefetch=len(scalars),
            grid=(steps,),
            in_specs=[spec(field[0].shape, *field[1:]) for field in fields],
            out_specs=[spec(out[0], *out[2:]) for out in outs],
            scratch_shapes=[pltpu.VMEM(shape, dtype) for shape, dtype in scratch],
        ),
        out_shape=[jax.ShapeDtypeStruct(*out[:2]) for out in outs],
        compiler_params=pltpu.CompilerParams(vmem_limit_bytes=ROOM),
        cost_estimate=lasting(microseconds),
    )(*scalars, *[field[0] for field in fields])


def by_rows(field, rows, shift=None):
    if shift is None:
        return field, (rows, field.shape[1]), lambda i, *scalars: (i, 0)
    return field, (rows, field.shape[1]), lambda i, *scalars: (shift(i, *scalars), 0)


def whole_spec(shape):
    return pl.BlockSpec(shape, lambda *at: (0,) * len(shape))


def turn(field, cos, sin):
    half = HEAD_DIM // 2
    lane = lax.broadcasted_iota(jnp.int32, field.shape, 1) % HEAD_DIM
    crossed = jnp.where(lane < half, pltpu.roll(field, LANES - half, 1), pltpu.roll(field, half, 1))
    return field * cos + crossed * sin


def project_kernel(flags, rows_ref, cos_ref, sin_ref, vectors, w_own, w_got, out_ref, turned_ref, weight_ref):
    @pl.when(pl.program_id(0) == 0)
    def _():
        weight_ref[...] = jnp.where(flags[0] == 1, w_own[...], w_got[...])

    unit, unused = norm_parts(rows_ref[...].astype(jnp.float32))
    norm = unit * vectors[0:1, :] + vectors[1:2, :]
    turned_ref[...] = norm.T.astype(jnp.bfloat16)
    norm = norm.astype(jnp.bfloat16)
    for c in range(weight_ref.shape[0]):
        field = dot(norm, weight_ref[c])
        if c == 2:
            out_ref[c] = field.astype(jnp.bfloat16)
        else:
            for p in range(field.shape[1] // LANES):
                lanes = slice(p * LANES, (p + 1) * LANES)
                out_ref[c, :, lanes] = turn(field[:, lanes], cos_ref[...], sin_ref[...]).astype(jnp.bfloat16)


def project(flags, rows, vectors, cos, sin, w_own, w_got):
    whole, width = rows.shape
    count, unused, columns = w_own.shape
    low = jnp.bfloat16
    return streamed(
        project_kernel,
        whole // ROWS,
        [flags],
        [by_rows(rows, ROWS), by_rows(cos, ROWS), by_rows(sin, ROWS), vectors, w_own, w_got],
        [
            ((count, whole, columns), low, (count, ROWS, columns), lambda i, flags: (0, i, 0)),
            ((width, whole), low, (width, ROWS), lambda i, flags: (0, i)),
            (w_own.shape, low),
        ],
        [],
        8,
    )


def gelu_both(up):
    root = math.sqrt(2.0 / math.pi)
    square = up * up
    bent = jnp.tanh(root * up * (1.0 + 0.044715 * square))
    half = 0.5 * (1.0 + bent)
    slope = half + 0.5 * up * (1.0 - bent * bent) * (root * (1.0 + 3.0 * 0.044715 * square))
    return up * half, slope


def feed_kernel(early, *refs):
    if early:
        flags, weight_ref, rows_ref, own_ref, got_ref, cot_ref, vectors, up_own, down_own, got = refs[:10]
        norm, norm_t, grad, grad_t = refs[10:14]
        up_got, down_got = got.at[: norm.shape[1]], got.at[norm.shape[1] :]
    else:
        flags, norm, norm_t, grad, grad_t, up_own, down_own, up_got, down_got = refs[:9]
    back_ref, act_ref, pieces_ref, down_ref, up_w, up_sum, down_sum = refs[-7:]
    part = pieces_ref.shape[2]
    step, last = pl.program_id(0), pl.num_programs(0) - 1

    @pl.when(step == 0)
    def _():
        up_w[...] = jnp.where(flags[0] == 1, up_own[...], up_got[...])
        down_ref[...] = jnp.where(flags[0] == 1, down_own[...], down_got[...])

    if early:

        def head(i, at):
            unit, unused = norm_parts(wide(rows_ref, at) + wide(own_ref, at) + wide(got_ref, at))
            field = unit * vectors[2:3, :] + vectors[3:4, :]
            norm[at, :] = field.astype(jnp.bfloat16)
            norm_t[:, at] = field.T.astype(jnp.bfloat16)
            field = wide(cot_ref, at) * weight_ref[weight_ref.shape[0] - 1]
            grad[at, :] = field.astype(jnp.bfloat16)
            grad_t[:, at] = field.T.astype(jnp.bfloat16)

        row_blocks(norm.shape[0], head)
    value, rise = gelu_both(dot(norm[...], up_w[...]))
    act_ref[...] = value.astype(jnp.bfloat16)
    slope = (dot(grad[...], down_ref[...], NT) * rise).astype(jnp.bfloat16)
    back_ref[...] = dot(slope, up_w[...], NT).astype(jnp.bfloat16)

    def grads(i, at):
        fields = (dot(norm_t[at, :], slope), dot(grad_t[at, :], act_ref[...]))
        for k, (field, total) in enumerate(zip(fields, (up_sum, down_sum))):

            @pl.when(step == 0)
            def _():
                total[at, :] = field

            @pl.when(step == last)
            def _():
                low = (total[at, :] + field).astype(jnp.bfloat16)
                for p in range(2):
                    pieces_ref[2 * k + p, at, :] = low[:, p * part : (p + 1) * part]

    row_blocks(norm_t.shape[0], grads)


def feed(early, scalars, fields, w_up, w_down, *got):
    whole, width = fields[0].shape
    hidden = w_up.shape[1] // 2
    rows = whole // 2
    half = 0 if early else 1
    low = jnp.bfloat16

    def across(i, *scalars):
        return (0, i)

    tokens = ((whole, width), low, (rows, width), lambda i, *scalars: (i, 0))
    turned = ((width, whole), low, (width, rows), across)
    if early:
        operands = [by_rows(field, rows) for field in fields[:4]] + [fields[4]]
        outs = [tokens, turned, tokens, turned]
    else:
        operands = [by_rows(fields[0], rows), (fields[1], (width, rows), across)]
        operands += [by_rows(fields[2], rows), (fields[3], (width, rows), across)]
        outs = []
    operands += [
        (w_up, (width, hidden), lambda i, *scalars: (0, half)),
        (w_down, (hidden, width), lambda i, *scalars: (half, 0)),
        *got,
    ]
    outs += [
        tokens,
        ((whole, hidden), low, (rows, hidden), lambda i, *scalars: (i, 0)),
        ((4, width, hidden // 2), low),
        ((hidden, width), low),
    ]
    sums = ((width, hidden), jnp.float32)
    return streamed(
        functools.partial(feed_kernel, early), 2, scalars, operands, outs, [((width, hidden), low), sums, sums], 17
    )


def lower_kernel(flags, act_early, act_late, rows_ref, own_ref, got_ref, cot_ref, early_ref, late_ref, keep_ref, send_ref, sums_ref):
    step, half = pl.program_id(0), pl.num_programs(0) // 2

    @pl.when(step == 0)
    def _():
        sums_ref[...] = jnp.zeros_like(sums_ref)

    total = dot(act_early[...], early_ref[...]) + dot(act_late[...], late_ref[...])
    cot = cot_ref[...].astype(jnp.float32)

    @pl.when(step < half)
    def _():
        send_ref[...] = total.astype(jnp.bfloat16)
        sums_ref[0:1, :] += jnp.sum(total * cot, axis=0, keepdims=True)

    @pl.when(step >= half)
    def _():
        parts = [ref[...].astype(jnp.float32) for ref in (rows_ref, own_ref, got_ref)]
        block = total + parts[0] + parts[1] + parts[2]
        keep_ref[...] = block
        sums_ref[0:1, :] += jnp.sum(block * cot, axis=0, keepdims=True)


def theirs_first(steps):
    return lambda i, flags, *more: lax.rem((1 - flags[1]) * (steps // 2) + i, steps)


def halves(steps, rows, width):
    keep = (rows, width), lambda i, *scalars: (jnp.maximum(i - steps // 2, 0), 0)
    send = (rows, width), lambda i, *scalars: (jnp.minimum(i, steps // 2 - 1), 0)
    return keep, send


def lower(flags, act_early, act_late, down_early, down_late, rows, own, got, cot):
    whole, width = rows.shape
    steps = whole // ROWS
    order = theirs_first(steps)
    keep, send = halves(steps, ROWS, width)
    shape = (whole // 2, width)
    return streamed(
        lower_kernel,
        steps,
        [flags],
        [by_rows(field, ROWS, order) for field in (act_early, act_late, rows, own, got, cot)] + [down_early, down_late],
        [(shape, jnp.float32, *keep), (shape, jnp.bfloat16, *send), ((8, width), jnp.float32)],
        [],
        6,
    )


def middle_kernel(
    flags, weight_ref, rows_ref, own_ref, got_ref, cot_ref, early_own, early_got, late_own, late_got, mixed_ref,
    vectors, w_ref, grad_ref, gmixed_ref, gout_ref, sums_ref, gout,
):
    step, last = pl.program_id(0), pl.num_programs(0) - 1
    unit, scale = norm_parts(sum(ref[...].astype(jnp.float32) for ref in (rows_ref, own_ref, got_ref)))
    back = sum(ref[...].astype(jnp.float32) for ref in (early_own, early_got, late_own, late_got))
    inner = back * vectors[2:3, :]
    mean = jnp.mean(inner, axis=-1, keepdims=True)
    slant = jnp.mean(inner * unit, axis=-1, keepdims=True)
    cot = cot_ref[...].astype(jnp.float32) * weight_ref[weight_ref.shape[0] - 1]
    grad = cot + scale * (inner - mean - unit * slant)
    low = grad.astype(jnp.bfloat16)
    grad_ref[...] = low
    gmixed_ref[...] = dot(low, w_ref[...], NT).astype(jnp.bfloat16)
    part = dot(grad.T.astype(jnp.bfloat16), mixed_ref[...])

    @pl.when(step == 0)
    def _():
        gout[...] = part
        sums_ref[...] = jnp.zeros_like(sums_ref)

    @pl.when(step > 0)
    def _():
        gout[...] += part

    @pl.when(step == last)
    def _():
        gout_ref[...] = gout[...].astype(jnp.bfloat16)

    @pl.when(step // ((last + 1) // 2) == flags[1])
    def _():
        sums_ref[0:1, :] += jnp.sum(back * unit, axis=0, keepdims=True)
        sums_ref[1:2, :] += jnp.sum(back, axis=0, keepdims=True)


def middle(flags, weight, fields, mixed, vectors, w_out):
    whole, width = fields[0].shape
    columns = mixed.shape[1]
    low = jnp.bfloat16
    in_order = lambda i, *scalars: (i, 0)
    return streamed(
        middle_kernel,
        whole // ROWS,
        [flags, weight],
        [by_rows(field, ROWS) for field in (*fields, mixed)] + [vectors, w_out],
        [
            ((whole, width), low, (ROWS, width), in_order),
            ((whole, columns), low, (ROWS, columns), in_order),
            ((width, columns), low),
            ((8, width), jnp.float32),
        ],
        [((width, columns), jnp.float32)],
        8,
    )


def weigh_kernel(flags, turned_ref, out_grad_ref, grad_ref, *out_refs):
    last = grad_ref.shape[0]
    for j, out_ref in enumerate(out_refs):
        piece = flags[3 + j]

        @pl.when(piece < last)
        def _():
            out_ref[...] = dot(turned_ref[...], grad_ref[jnp.minimum(piece, last - 1)]).astype(jnp.bfloat16)

        @pl.when(piece == last)
        def _():
            out_ref[...] = out_grad_ref[...]


def weigh(flags, turned, grad, out_grad):
    width, columns = turned.shape[0], grad.shape[2]
    piece = ((width, columns), jnp.bfloat16, (ROWS, columns), lambda i, flags: (i, 0))
    return streamed(
        weigh_kernel, width // ROWS, [flags], [by_rows(turned, ROWS), by_rows(out_grad, ROWS), grad], [piece] * 4, [], 4
    )


def unproject_kernel(flags, grad_ref, rows_ref, weight, keep_ref, send_ref, sums_ref):
    step, half = pl.program_id(0), pl.num_programs(0) // 2
    total = dot(grad_ref[0], weight[0], NT)
    for c in range(1, grad_ref.shape[0]):
        total = total + dot(grad_ref[c], weight[c], NT)
    unit, unused = norm_parts(rows_ref[...].astype(jnp.float32))

    @pl.when(step == 0)
    def _():
        sums_ref[...] = jnp.zeros_like(sums_ref)

    sums_ref[0:1, :] += jnp.sum(total * unit, axis=0, keepdims=True)
    sums_ref[1:2, :] += jnp.sum(total, axis=0, keepdims=True)

    @pl.when(step < half)
    def _():
        send_ref[...] = total.astype(jnp.bfloat16)

    @pl.when(step >= half)
    def _():
        keep_ref[...] = total


def unproject(flags, grad, weight, rows):
    whole, width = rows.shape
    count, unused, columns = grad.shape
    steps = whole // ROWS
    order = theirs_first(steps)
    keep, send = halves(steps, ROWS, width)
    shape = (whole // 2, width)
    return streamed(
        unproject_kernel,
        steps,
        [flags],
        [(grad, (count, ROWS, columns), lambda i, flags: (0, order(i, flags), 0)), by_rows(rows, ROWS, order), weight],
        [(shape, jnp.float32, *keep), (shape, jnp.bfloat16, *send), ((8, width), jnp.float32)],
        [],
        5,
    )


def last_kernel(flags, rows_ref, resid_ref, keep_ref, got_ref, block_keep, block_got, vectors, grad_ref, block_ref):
    unit, scale = norm_parts(rows_ref[...].astype(jnp.float32))
    inner = (keep_ref[...] + got_ref[...].astype(jnp.float32)) * vectors[0:1, :]
    mean = jnp.mean(inner, axis=-1, keepdims=True)
    slant = jnp.mean(inner * unit, axis=-1, keepdims=True)
    grad = resid_ref[...].astype(jnp.float32) + scale * (inner - mean - unit * slant)
    grad_ref[...] = grad.astype(jnp.bfloat16)
    block_ref[...] = (block_keep[...] + block_got[...].astype(jnp.float32)).astype(jnp.bfloat16)


def last(flags, rows, resid, keep, got, block_keep, block_got, vectors):
    half, width = keep.shape
    steps = half // ROWS

    def mine(i, flags):
        return flags[1] * steps + i

    out = ((half, width), jnp.bfloat16, (ROWS, width), lambda i, flags: (i, 0))
    fields = [by_rows(rows, ROWS, mine), by_rows(resid, ROWS, mine)]
    fields += [by_rows(field, ROWS) for field in (keep, got, block_keep, block_got)]
    return streamed(last_kernel, steps, [flags], fields + [vectors], [out] * 2, [], 3)


def past_kernel(dwa_ref, hist_ref, cot_ref, grad_ref, part_ref, sums_ref):
    @pl.when(pl.program_id(0) == 0)
    def _():
        sums_ref[...] = jnp.zeros_like(sums_ref)

    grad = cot_ref[...].astype(jnp.float32)
    total = jnp.zeros_like(grad)
    for j in range(hist_ref.shape[0]):
        field = hist_ref[j].astype(jnp.float32)
        total += dwa_ref[j] * field
        grad_ref[j] = (dwa_ref[j] * grad).astype(jnp.bfloat16)
        sums_ref[j : j + 1, :] += jnp.sum(field * grad, axis=0, keepdims=True)
    part_ref[...] = total


def past(dwa, history, cot):
    count, rows, width = history.shape
    layers = pl.BlockSpec((count, ROWS, width), lambda i: (0, i, 0))
    tokens = pl.BlockSpec((ROWS, width), lambda i: (i, 0))
    return pl.pallas_call(
        past_kernel,
        grid=(rows // ROWS,),
        in_specs=[pl.BlockSpec(memory_space=pltpu.SMEM), layers, tokens],
        out_specs=[layers, tokens, whole_spec((8, width))],
        out_shape=[
            jax.ShapeDtypeStruct(history.shape, jnp.bfloat16),
            jax.ShapeDtypeStruct((rows, width), jnp.float32),
            jax.ShapeDtypeStruct((8, width), jnp.float32),
        ],
        compiler_params=pltpu.CompilerParams(vmem_limit_bytes=ROOM),
        cost_estimate=lasting(3),
    )(dwa, history, cot)


def present_kernel(flags, weight_ref, part_ref, grad_own, grad_got, block_own, block_got, out_ref, grad_ref):
    here = jnp.where(flags[0] == 1, block_own[...], block_got[...]).astype(jnp.float32)
    out_ref[...] = (part_ref[...] + weight_ref[weight_ref.shape[0] - 1] * here).astype(jnp.bfloat16)
    grad_ref[...] = jnp.where(flags[0] == 1, grad_own[...], grad_got[...])


def present(flags, weight, part, grad_own, grad_got, block_own, block_got):
    rows, width = part.shape
    scalars = pl.BlockSpec(memory_space=pltpu.SMEM)
    tokens = pl.BlockSpec((ROWS, width), lambda i: (i, 0))
    return pl.pallas_call(
        present_kernel,
        grid=(rows // ROWS,),
        in_specs=[scalars, scalars] + [tokens] * 5,
        out_specs=[tokens, tokens],
        out_shape=[jax.ShapeDtypeStruct((rows, width), jnp.bfloat16)] * 2,
        compiler_params=pltpu.CompilerParams(vmem_limit_bytes=ROOM),
        cost_estimate=lasting(2),
    )(flags, weight, part, grad_own, grad_got, block_own, block_got)


def place_feed_kernel(flags, own_ref, got_ref, up_ref, down_ref):
    part = own_ref.shape[-1]
    far, tp = flags[2], flags[7]
    for k in range(2):
        for t, out_ref in enumerate((up_ref, down_ref)):
            for half in range(2):
                at = (2 * half + k) * part
                here = [ref[k ^ far, t ^ tp, half].astype(jnp.float32) for ref in (own_ref, got_ref)]
                out_ref[:, at : at + part] = jnp.where(flags[0] == 1, *here)


def place_feed(flags, own, got):
    rows, part = own.shape[-2:]
    both = whole_spec(own.shape)
    block = whole_spec((rows, 4 * part))
    return pl.pallas_call(
        place_feed_kernel,
        grid_spec=pltpu.PrefetchScalarGridSpec(
            num_scalar_prefetch=1, grid=(1,), in_specs=[both, both], out_specs=[block, block]
        ),
        out_shape=[jax.ShapeDtypeStruct((rows, 4 * part), jnp.float32)] * 2,
        compiler_params=pltpu.CompilerParams(vmem_limit_bytes=ROOM),
        cost_estimate=lasting(2),
    )(flags, own, got)


def place_attention_kernel(flags, own_ref, got_ref, qkv_ref, out_ref):
    near, far = flags[1], flags[2]
    for k in range(2):
        for c in range(2):
            here = [ref[c ^ near].astype(jnp.float32) for ref in (own_ref, got_ref)]
            field = jnp.where(far == k, *here)
            if 2 * k + c < 3:
                qkv_ref[2 * k + c] = field
            else:
                out_ref[...] = field


def place_attention(flags, own, got):
    rows, part = own.shape[-2:]
    both = whole_spec(own.shape)
    return pl.pallas_call(
        place_attention_kernel,
        grid_spec=pltpu.PrefetchScalarGridSpec(
            num_scalar_prefetch=1,
            grid=(1,),
            in_specs=[both, both],
            out_specs=[whole_spec((3, rows, part)), whole_spec((rows, part))],
        ),
        out_shape=[
            jax.ShapeDtypeStruct((3, rows, part), jnp.float32),
            jax.ShapeDtypeStruct((rows, part), jnp.float32),
        ],
        compiler_params=pltpu.CompilerParams(vmem_limit_bytes=ROOM),
        cost_estimate=lasting(1),
    )(flags, own, got)


AXES = ("tp", "dp", "far", "near")


def moves(chosen, move):
    sizes = [lax.axis_size(name) for name in AXES]
    places = [place for place in itertools.product(*map(range, sizes)) if chosen(*place)]
    index = lambda place: functools.reduce(lambda at, step: at * step[0] + step[1], zip(sizes, place), 0)
    return [(index(place), index(move(*place))) for place in places]


def away(t, d, k, c):
    return t != c


def anyone(t, d, k, c):
    return True


def home(t, d, k, c):
    return t == c


def swap_diagonal(field):
    return lax.ppermute(field, AXES, moves(away, lambda t, d, k, c: (c, d, k, t)))


def send_to_owner(field, other_far, other_tp):
    return lax.ppermute(
        field,
        AXES,
        moves(
            away if not other_far and not other_tp else anyone,
            lambda t, d, k, c: (c, d, k ^ other_far, t ^ other_tp),
        ),
    )


def bring_home(field):
    return lax.ppermute(field, AXES, moves(away, lambda t, d, k, c: (c, d, k, c)))


def swap_far_home(field):
    return lax.ppermute(field, AXES, moves(home, lambda t, d, k, c: (t, d, 1 - k, c)))


def swap_far(field):
    return lax.ppermute(field, "far", [(0, 1), (1, 0)])


def swap_near(field):
    return lax.ppermute(field, "near", [(0, 1), (1, 0)])


def after(field, *others):
    return lax.optimization_barrier((field, *others))[0]


def ordered(own, other, first, axis=0):
    return jnp.where(
        first, jnp.concatenate([own, other], axis=axis), jnp.concatenate([other, own], axis=axis)
    )


def part_of(field, index, axis):
    size = field.shape[axis] // 2
    return lax.dynamic_slice_in_dim(field, index * size, size, axis)


def add(*fields):
    return sum(field.astype(jnp.float32) for field in fields).astype(jnp.bfloat16)


def scatter_plane(pieces):
    return lax.psum_scatter(pieces, ("tp", "far"), scatter_dimension=0, tiled=True)[0]


def scatter_rows(piece):
    return lax.psum_scatter(piece, "dp", scatter_dimension=0, tiled=True)


def move_rows(block):
    dps = lax.axis_size("dp")
    if dps > 8:
        return [scatter_rows(block)]
    block = block.reshape(dps, block.shape[0] // dps, block.shape[1])
    place = lax.axis_index("dp")
    moved = [lax.dynamic_index_in_dim(block, place, 0, keepdims=False)]
    for step in range(1, dps):
        sent = lax.dynamic_index_in_dim(block, lax.rem(place + step, dps), 0, keepdims=False)
        moved.append(lax.ppermute(sent, "dp", [(d, (d + step) % dps) for d in range(dps)]))
    return moved


def sum_over(field, name):
    size = lax.axis_size(name)
    bit = 1
    while bit < size:
        field = field + lax.ppermute(field, name, [(d, d ^ bit) for d in range(size)])
        bit *= 2
    return field


def local(
    layer_input,
    history,
    cotangent,
    lengths,
    dwa_weights,
    gain_one,
    bias_one,
    w_qkv,
    w_out,
    gain_two,
    bias_two,
    w_up,
    w_down,
):
    rows = layer_input.shape[1]
    whole = rows * lax.axis_size("tp")
    hist_count = history.shape[0]
    part, far, near = lax.axis_index("tp"), lax.axis_index("far"), lax.axis_index("near")
    same = near == part
    pieces = [2 * (far ^ a) + (part ^ b) for a in range(2) for b in range(2)]
    flags = jnp.stack([same.astype(jnp.int32), near, far, *pieces, part])

    input_got = swap_diagonal(layer_input[0])
    qkv_got = swap_diagonal(w_qkv)
    early_got = jnp.concatenate([part_of(w_up, 0, 1), part_of(w_down, 0, 0)], axis=0)
    late_up, late_down = part_of(w_up, 1, 1), part_of(w_down, 1, 0)
    last_own = jnp.concatenate([w_out, cotangent[0]], axis=0)
    vectors = jnp.stack([gain_one, bias_one, gain_two, bias_two])

    own_lengths = jnp.where(same, lengths, swap_near(lengths))[0]
    seq_owner, token_place = positions(own_lengths, whole)
    lane = jnp.arange(LANES, dtype=jnp.int32)
    member = seq_owner[:, None] == lane[None, :]
    apart = jnp.where(member | (lane >= lengths.shape[1])[None, :], 0.0, NEG_FILL).astype(jnp.bfloat16)
    member = member.astype(jnp.bfloat16)
    half_dim = HEAD_DIM // 2
    frequency = jnp.exp((lane % half_dim).astype(jnp.float32) * (-math.log(10000.0) / half_dim))
    angles = token_place.astype(jnp.float32)[:, None] * frequency[None, :]
    cos_table = jnp.cos(angles)
    sin_table = jnp.sin(angles) * jnp.where(lane % HEAD_DIM < half_dim, -1.0, 1.0)[None, :]
    grad_history, past_sum, sums_past = past(dwa_weights, history[:, 0], cotangent[0])

    input_half = jnp.where(same, layer_input[0], input_got)
    layer_rows = ordered(input_half, swap_near(input_half), near == 0)
    layer_rows, last_own, early_got, late_up, vectors, past_sum, *tables = lax.optimization_barrier(
        (layer_rows, last_own, early_got, late_up, vectors, past_sum)
        + (cos_table, sin_table, apart, member)
    )
    cos_table, sin_table, apart, member = tables
    early_got = swap_diagonal(early_got)
    last_got = swap_diagonal(last_own)
    projected, norm_one_t, weight_qkv = project(
        flags, layer_rows, vectors, cos_table, sin_table, w_qkv, qkv_got
    )
    mixed = attend(apart, member, projected, LONGEST)
    late_up = swap_diagonal(after(late_up, mixed))
    late_down = swap_diagonal(after(late_down, mixed))
    last_got = jnp.where(same, last_own, last_got)
    weight_out = last_got[: w_out.shape[0]]
    attn = jnp.dot(mixed, weight_out, preferred_element_type=jnp.float32).astype(jnp.bfloat16)
    attn_got = swap_near(attn)
    cot_half = last_got[w_out.shape[0] :]
    cot_rows = ordered(cot_half, swap_near(cot_half), near == 0)
    scalars = [flags, dwa_weights]
    fields = [layer_rows, attn, attn_got, cot_rows, vectors]
    *kept, back_early, act_early, early_pieces, down_early = feed(True, scalars, fields, w_up, w_down, early_got)
    early_sum = scatter_plane(after(early_pieces, late_up, late_down))
    back_late, act_late, late_pieces, down_late = feed(False, [flags], kept, w_up, w_down, late_up, late_down)
    late_sum = scatter_plane(late_pieces)
    fields = [layer_rows, attn, attn_got, cot_rows, back_early, swap_near(back_early), back_late, swap_near(back_late)]
    grad_attn, grad_mixed, grad_out, sums_two = middle(flags, dwa_weights, fields, mixed, vectors, weight_out)
    grad_qkv = attend_back(apart, member, cos_table, sin_table, projected, grad_mixed, LONGEST)
    owned = weigh(flags, norm_one_t, grad_qkv, grad_out)
    moved = [send_to_owner(owned[j], j // 2, j % 2) for j in range(4)]
    keep, send, sums_one = unproject(flags, after(grad_qkv, owned[0]), weight_qkv, layer_rows)
    block_keep, block_send, sums_now = lower(
        flags, act_early, act_late, down_early, down_late, layer_rows, attn, attn_got, after(cot_rows, send)
    )
    small = jnp.concatenate([sums_one[:2], sums_two[:2], sums_now[:1], sums_past[:hist_count]], axis=0)
    early_sum = scatter_rows(after(early_sum, owned[0]))
    for name in ("near", "dp", "tp", "far"):
        small = sum_over(small, name)
    small, keep, send, block_keep, block_send, *moved = lax.optimization_barrier(
        (small, keep, send, block_keep, block_send, *moved)
    )
    attn_one = add(jnp.where(same, owned[0], moved[0]), *moved[1:])
    attn_moved = move_rows(attn_one)
    input_grad, block_half = last(
        flags, layer_rows, grad_attn, after(keep, attn_one), swap_near(send), block_keep, swap_near(block_send), vectors
    )
    input_moved = swap_diagonal(input_grad)
    late_sum = scatter_rows(after(late_sum, attn_one))
    input_grad, input_moved, block_half, *attn_moved = lax.optimization_barrier(
        (input_grad, input_moved, block_half, *attn_moved)
    )
    block_moved = swap_diagonal(block_half)
    attn_sum = add(*attn_moved)
    attn_own = jnp.stack([attn_sum, swap_near(attn_sum)])
    attn_got = swap_far(attn_own)
    feed_sum = jnp.stack([after(early_sum, attn_sum), late_sum])
    feed_home = bring_home(feed_sum)
    block_moved, attn_own, attn_got, feed_sum, feed_home = lax.optimization_barrier(
        (block_moved, attn_own, attn_got, feed_sum, feed_home)
    )
    feed_own = jnp.stack([feed_sum, feed_home])
    feed_both = jnp.stack([feed_own, swap_far_home(feed_own)])
    feed_got = swap_near(feed_both)
    grad_w_qkv, grad_w_out = place_attention(flags, attn_own, attn_got)
    grad_w_up, grad_w_down = place_feed(flags, feed_both, feed_got)
    output, grad_input = present(
        flags, dwa_weights, past_sum, input_grad, input_moved, block_half, block_moved
    )

    return (
        output[None],
        grad_input[None],
        grad_history[:, None],
        jnp.sum(jnp.concatenate([small[5:], small[4:5]], axis=0), axis=1),
        small[0],
        small[1],
        grad_w_qkv,
        grad_w_out.T,
        small[2],
        small[3],
        grad_w_up,
        grad_w_down.T,
    )


def positions(seq_lengths, token_count):
    seq_ends = jnp.cumsum(seq_lengths)
    seq_starts = seq_ends - seq_lengths
    token_index = jnp.arange(token_count, dtype=jnp.int32)
    seq_owner = jnp.sum((token_index[:, None] >= seq_ends[None, :]).astype(jnp.int32), axis=1)
    picked = (
        seq_owner[:, None] == jnp.arange(seq_lengths.shape[0], dtype=jnp.int32)[None, :]
    ).astype(jnp.int32)
    seq_begin = jnp.sum(picked * seq_starts[None, :], axis=1)
    return (seq_owner, token_index - seq_begin)


def solution(mesh):
    tps, dps, reps = (mesh.shape[name] for name in ("tp", "dp", "rep"))
    split = Mesh(mesh.devices.reshape(tps, dps, reps // 2, 2), AXES)
    in_specs = (
        P(("dp", "far", "near"), "tp", None),
        P(None, ("dp", "far", "near"), "tp", None),
        P(("dp", "far", "near"), "tp", None),
        P(("dp", "far", "near"), None),
        P(),
        P(),
        P(),
        P(None, None, "tp"),
        P("tp", None),
        P(),
        P(),
        P(None, "tp"),
        P("tp", None),
    )
    out_specs = (
        P(("dp", "far", "near"), "tp", None),
        P(("dp", "far", "near"), "tp", None),
        P(None, ("dp", "far", "near"), "tp", None),
        P(),
        P(),
        P(),
        P(None, "dp", "tp"),
        P("tp", "dp"),
        P(),
        P(),
        P("dp", "tp"),
        P("tp", "dp"),
    )
    return jax.shard_map(local, mesh=split, in_specs=in_specs, out_specs=out_specs, check_vma=False)
```

time: 305 us -> 303 us (level)
  local copies, waits for them, and re-layouts: 31.4 us -> 18.1 us
  waiting for transfers between devices: 46.4 us -> 53.9 us
    unnamed x104 -> x42, local copies, waits for them, and re-layouts: 23.2 us -> 5.67 us
    ppermute x8, waiting for transfers between devices: 2.06 us -> 10.5 us  [swap_diagonal(): lax.ppermute(field, AXES, moves(away, lambda t, d, k, c: (c, d, k, t)))]
    pallas_call x8, Pallas kernels: 78.3 us -> 84.7 us  [streamed(): pl.pallas_call(kernel, grid_spec=pltpu.PrefetchScalarGridSpec(num_scalar_...]
    pallas_call x1, Pallas kernels: 28.6 us -> 23.1 us  [attend_back(): pl.pallas_call(functools.partial(attend_back_kernel, reach), grid=(width...]
    pallas_call x1, Pallas kernels: 17.2 us -> 12.7 us  [attend(): pl.pallas_call(functools.partial(attend_kernel, reach), grid=(width // LA...]
    ppermute x9 -> x10, starting transfers between devices: 16.1 us -> 17.9 us  [swap_near(): return lax.ppermute(field, 'near', [(0, 1), (1, 0)])]
    ppermute x9 -> x10, waiting for transfers between devices: 6.62 us -> 7.83 us  [swap_near(): return lax.ppermute(field, 'near', [(0, 1), (1, 0)])]
  transfers between devices with their start and end apart: 36 -> 37, of which waited for: 15 -> 18; matrix products, arithmetic and copies ran while one was open for 8% -> 10% of each run, Pallas kernels for 43% -> 43%
where the time goes in v2:
time: 303 us; the launch traced here: 301 us
  Pallas kernels  135 us (45%)
  starting transfers between devices  62.5 us (21%)
  waiting for transfers between devices  53.9 us (18%)
  local copies, waits for them, and re-layouts  18.1 us (6%)
  other arithmetic  16.4 us (5%)
  between operations  14.3 us (5%)
    pallas_call x8, Pallas kernels, streamed(): pl.pallas_call(kernel, grid_spec=pltpu.PrefetchScalarGridSpec(num_scalar_...  84.7 us
    pallas_call x1, Pallas kernels, attend_back(): pl.pallas_call(functools.partial(attend_back_kernel, reach), grid=(width...  23.1 us
    ppermute x8, starting transfers between devices, swap_diagonal(): lax.ppermute(field, AXES, moves(away, lambda t, d, k, c: (c, d, k, t)))  23 us
    ppermute x3, waiting for transfers between devices, move_rows(): lax.ppermute(sent, 'dp', [(d, (d + step) % dps) for d in range(dps)])  18.5 us
    ppermute x10, starting transfers between devices, swap_near(): return lax.ppermute(field, 'near', [(0, 1), (1, 0)])  17.9 us
    pallas_call x1, Pallas kernels, attend(): pl.pallas_call(functools.partial(attend_kernel, reach), grid=(width // LA...  12.7 us
    ppermute x5, waiting for transfers between devices, sum_over(): lax.ppermute(field, name, [(d, d ^ bit) for d in range(size)])  12.2 us
    ppermute x8, waiting for transfers between devices, swap_diagonal(): lax.ppermute(field, AXES, moves(away, lambda t, d, k, c: (c, d, k, t)))  10.5 us
  transfers between devices with their start and end apart: 37, of which 18 were waited for; matrix products, arithmetic and copies ran while one was open for 10% of the time, Pallas kernels for 43%

profile of v2, /device:TPU:9, one launch (start us, length us, event | category | flops | bytes accessed | tf_op | source)
XLA Modules:
  0.0 301.1 jit_solution(16524639780087624789)
XLA Ops:
  8.0 3.1 %collective-permute-start = (bf16[512,768]{1,0:T(8,128)(2,1)}, bf16[512,768]{1,0:T(8,128)(2,1)}, u32[]{:S(2)}, u32[]{:S(2)}) collective-permute-start(bf16[512,768]{1,0:T(8,128)(2,1)} %bitcast.55), channel_id=1, source_target_pairs={{1,16},{3,18},{5,20},{7,22},{9,24},{11,26},{13,28},{15,30},{16,1},... | collective-permute-start | bytes 2359304 | tf_op jit(solution)/shard_map/ppermute | solution.py:716
  11.0 2.5 collective-permute-start.3
  16.3 2.9 fusion.12
  19.3 1.2 fusion.11
  21.1 1.6 pad_maximum_fusion
  22.7 4.4 %shard_map.220 = (bf16[4,512,768]{2,1,0:T(8,128)(2,1)}, f32[512,768]{1,0:T(8,128)}, f32[8,768]{1,0:T(8,128)}) custom-call(f32[5]{0:T(128)} %weight_ref.3, bf16[4,512,768]{2,1,0:T(8,128)(2,1)} %bitcast.50, bf16[512,768]{1,0:T(8,128)(2,1)} %bitcast.51), custom_call_target="tpu_custom_call" | custom-call | bytes 9000000 | tf_op jit(solution)/shard_map/pallas_call | solution.py:599
  28.1 1.2 broadcast_select_fusion.1
  29.4 3.1 %fusion = (f32[1024,128]{1,0:T(8,128)}, f32[1024,128]{1,0:T(8,128)}) fusion(f32[128]{0:T(128)S(1)} %get-tuple-element.225, f32[128]{0:T(128)S(1)} %get-tuple-element.226, f32[1024]{0:T(1024)S(1)} %subtract_convert_fusion), kind=kLoop, calls=%fused_computation.12 | loop fusion | flops 262144 | bytes 1053696 | tf_op jit(solution)/shard_map/mul | solution.py:835
  34.3 1.8 maximum_select_fusion.rows_ref.refs_2_
  36.1 3.0 %collective-permute-start.4 = (bf16[896,768]{1,0:T(8,128)(2,1)S(1)}, bf16[896,768]{1,0:T(8,128)(2,1)S(1)}, u32[]{:S(2)}, u32[]{:S(2)}) collective-permute-start(bf16[896,768]{1,0:T(8,128)(2,1)S(1)} %pad_maximum_fusion.1), channel_id=1, source_target_pairs={{1,16},{3,18},{5,20},{7,22},{9,24},{11,26},{13,28},{15,30},{16,1},... | collective-permute-start | bytes 4128776 | tf_op jit(solution)/shard_map/ppermute | solution.py:716
  39.1 2.5 collective-permute-start.7
  42.3 9.4 %shard_map.221 = (bf16[3,1024,384]{2,1,0:T(8,128)(2,1)}, bf16[768,1024]{1,0:T(8,128)(2,1)}, bf16[3,768,384]{2,1,0:T(8,128)(2,1)}) custom-call(s32[8]{0:T(128)} %stack.90.flags.refs_0_, bf16[1024,768]{1,0:T(8,128)(2,1)} %maximum_select_fusion.rows_ref.refs_2_, f32[1024,128]{1,0:T(8,128)} %get-tuple-element.97.cos_ref, f32[1024,128]{1,0:T(8,128)} %get-tuple-element.98.sin_ref, ...), custom_call_target="tpu_custom_call" | custom-call | bytes 24000000 | tf_op jit(solution)/shard_map/pallas_call | solution.py:222
  51.7 12.7 %shard_map.222.mixed_ref = bf16[1024,384]{1,0:T(8,128)(2,1)} custom-call(bf16[1024,128]{1,0:T(8,128)(2,1)} %select_convert_fusion.apart_ref, bf16[1024,128]{1,0:T(8,128)(2,1)} %fusion.1.member_ref, bf16[3,1024,384]{2,1,0:T(8,128)(2,1)} %get-tuple-element.100.q_ref.k_ref.v_ref, bf16[3,1024,384]{2,1,0:T(8,128)(2,1)} %get-tuple-element.100.q_ref.k_ref.v_ref, ...), custom_call_target="tpu_custom_call" | custom-call | bytes 36000000 | tf_op jit(solution)/shard_map/pallas_call | solution.py:98
  64.5 1.0 copy-done.5
  65.5 1.0 convolution_convert_fusion.refs_3_.own_ref
  66.6 3.1 %collective-permute-start.9 = (bf16[768,768]{1,0:T(8,128)(2,1)}, bf16[768,768]{1,0:T(8,128)(2,1)}, u32[]{:S(2)}, u32[]{:S(2)}) collective-permute-start(bf16[768,768]{1,0:T(8,128)(2,1)} %get-tuple-element.109), channel_id=1, source_target_pairs={{1,16},{3,18},{5,20},{7,22},{9,24},{11,26},{13,28},{15,30},{16,1},... | collective-permute-start | bytes 3538952 | tf_op jit(solution)/shard_map/ppermute | solution.py:716
  69.6 2.7 collective-permute-start.10
  72.5 2.3 collective-permute-done.6
  74.7 1.9 maximum_select_fusion.1.refs_5_.cot_ref
  76.6 4.5 %collective-permute-done.7.refs_9_ = bf16[1536,768]{1,0:T(8,128)(2,1)} collective-permute-done((bf16[1536,768]{1,0:T(8,128)(2,1)}, bf16[1536,768]{1,0:T(8,128)(2,1)}, u32[]{:S(2)}, u32[]{:S(2)}) %collective-permute-start.7) | collective-permute-done | bytes 2359328 | tf_op jit(solution)/shard_map/ppermute | solution.py:716
  81.1 1.2 copy-done.2
  82.2 18.8 %shard_map.223 = (bf16[1024,768]{1,0:T(8,128)(2,1)}, bf16[768,1024]{1,0:T(8,128)(2,1)}, bf16[1024,768]{1,0:T(8,128)(2,1)}, bf16[768,1024]{1,0:T(8,128)(2,1)}, bf...) custom-call(s32[8]{0:T(128)} %stack.90.flags.refs_0_, ...), custom_call_target="tpu_custom_call" | custom-call | bytes 51000000 | tf_op jit(solution)/shard_map/pallas_call | solution.py:222
  101.0 5.3 %collective-permute-done.10.refs_8_ = bf16[768,768]{1,0:T(8,128)(2,1)} collective-permute-done((bf16[768,768]{1,0:T(8,128)(2,1)}, bf16[768,768]{1,0:T(8,128)(2,1)}, u32[]{:S(2)}, u32[]{:S(2)}) %collective-permute-start.10) | collective-permute-done | bytes 1179680 | tf_op jit(solution)/shard_map/ppermute | solution.py:716
  106.4 15.3 %shard_map.224 = (bf16[1024,768]{1,0:T(8,128)(2,1)}, bf16[1024,768]{1,0:T(8,128)(2,1)}, bf16[4,768,384]{2,1,0:T(8,128)(2,1)}, bf16[768,768]{1,0:T(8,128)(2,1)}) custom-call(s32[8]{0:T(128)} %stack.90.flags.refs_0_, bf16[1024,768]{1,0:T(8,128)(2,1)} %get-tuple-element.104.refs_1_, bf16[768,1024]{1,0:T(8,128)(2,1)} %get-tuple-element.105.refs_2_, ...), custom_call_target="tpu_custom_call" | custom-call | bytes 51000000 | tf_op jit(solution)/shard_map/pallas_call | solution.py:222
  122.1 1.0 copy-done.7
  123.2 1.9 slice.48.w_ref
  125.7 2.2 collective-permute-done.8.early_got
  127.9 11.4 %shard_map.225 = (bf16[1024,768]{1,0:T(8,128)(2,1)}, bf16[1024,384]{1,0:T(8,128)(2,1)}, bf16[768,384]{1,0:T(8,128)(2,1)}, f32[8,768]{1,0:T(8,128)}) custom-call(s32[8]{0:T(128)} %stack.90.flags.refs_0_, f32[5]{0:T(128)} %weight_ref.3, bf16[1024,768]{1,0:T(8,128)(2,1)} %maximum_select_fusion.rows_ref.refs_2_, bf16[1024,768]{1,0:T(8,128)(2,1)} %copy-done.1, ...), custom_call_target="tpu_custom_call" | custom-call | bytes 24000000 | tf_op jit(solution)/shard_map/pallas_call | solution.py:222
  139.3 23.1 %shard_map.226.grad_ref = bf16[3,1024,384]{2,1,0:T(8,128)(2,1)} custom-call(bf16[1024,128]{1,0:T(8,128)(2,1)} %select_convert_fusion.apart_ref, bf16[1024,128]{1,0:T(8,128)(2,1)} %fusion.1.member_ref, f32[1024,128]{1,0:T(8,128)} %get-tuple-element.97.cos_ref, f32[1024,128]{1,0:T(8,128)} %get-tuple-element.98.sin_ref, ...), custom_call_target="tpu_custom_call" | custom-call | bytes 66000000 | tf_op jit(solution)/shard_map/pallas_call | solution.py:174
  162.4 7.8 %shard_map.227 = (bf16[768,384]{1,0:T(8,128)(2,1)}, bf16[768,384]{1,0:T(8,128)(2,1)}, bf16[768,384]{1,0:T(8,128)(2,1)}, bf16[768,384]{1,0:T(8,128)(2,1)}) custom-call(s32[8]{0:T(128)} %stack.90.flags.refs_0_, bf16[768,1024]{1,0:T(8,128)(2,1)} %get-tuple-element.114.turned_ref, bf16[768,384]{1,0:T(8,128)(2,1)} %get-tuple-element.115.out_grad_ref, ...), custom_call_target="tpu_custom_call" | custom-call | bytes 12000000 | tf_op jit(solution)/shard_map/pallas_call | solution.py:222
  170.3 0.9 collective-permute-start.18
  171.2 2.0 collective-permute-start.19
  173.2 2.5 collective-permute-start.17
  176.5 7.9 %shard_map.228 = (f32[512,768]{1,0:T(8,128)}, bf16[512,768]{1,0:T(8,128)(2,1)}, f32[8,768]{1,0:T(8,128)}) custom-call(s32[8]{0:T(128)} %stack.90.flags.refs_0_, bf16[3,1024,384]{2,1,0:T(8,128)(2,1)} %shard_map.226.grad_ref, bf16[1024,768]{1,0:T(8,128)(2,1)} %maximum_select_fusion.rows_ref.refs_2_, bf16[3,768,384]{2,1,0:T(8,128)(2,1)} %get-tuple-element.118.weight), custom_call_target="tpu_custom_call" | custom-call | bytes 15000000 | tf_op jit(solution)/shard_map/pallas_call | solution.py:222
  185.2 9.2 %shard_map.229 = (f32[512,768]{1,0:T(8,128)}, bf16[512,768]{1,0:T(8,128)(2,1)}, f32[8,768]{1,0:T(8,128)}) custom-call(s32[8]{0:T(128)} %stack.90.flags.refs_0_, bf16[1024,768]{1,0:T(8,128)(2,1)} %get-tuple-element.121.act_early, bf16[1024,768]{1,0:T(8,128)(2,1)} %get-tuple-element.122.act_late, bf16[1024,768]{1,0:T(8,128)(2,1)} %maximum_select_fusion.rows_ref.refs_2_, ...), custom_call_target="tpu_custom_call" | custom-call | bytes 18000000 | tf_op jit(solution)/shard_map/pallas_call | solution.py:222
  195.4 1.1 collective-permute-done.12
  196.6 3.3 %collective-permute-done.13 = f32[9,768]{1,0:T(8,128)S(1)} collective-permute-done((f32[9,768]{1,0:T(8,128)S(1)}, f32[9,768]{1,0:T(8,128)S(1)}, u32[]{:S(2)}, u32[]{:S(2)}) %collective-permute-start.13) | collective-permute-done | bytes 27680 | tf_op jit(solution)/shard_map/ppermute | solution.py:790
  199.9 2.3 collective-permute-start.14
  202.2 4.2 %collective-permute-done.14 = f32[9,768]{1,0:T(8,128)S(1)} collective-permute-done((f32[9,768]{1,0:T(8,128)S(1)}, f32[9,768]{1,0:T(8,128)S(1)}, u32[]{:S(2)}, u32[]{:S(2)}) %collective-permute-start.14) | collective-permute-done | bytes 27680 | tf_op jit(solution)/shard_map/ppermute | solution.py:790
  206.4 1.2 collective-permute-start.15
  207.7 1.7 collective-permute-done.15
  209.4 1.7 collective-permute-start.16
  211.1 1.9 collective-permute-done.16
  213.0 3.1 %collective-permute-start.21 = (bf16[512,768]{1,0:T(8,128)(2,1)}, bf16[512,768]{1,0:T(8,128)(2,1)S(1)}, u32[]{:S(2)}, u32[]{:S(2)}) collective-permute-start(bf16[512,768]{1,0:T(8,128)(2,1)} %get-tuple-element.141), channel_id=1, source_target_pairs={{0,1},{1,0},{2,3},{3,2},{4,5},{5,4},{6,7},{7,6},{8,9},{9,8},{10,11... | collective-permute-start | bytes 2359304 | tf_op jit(solution)/shard_map/ppermute | solution.py:743
  216.2 1.8 add_convert_fusion
  218.2 1.1 collective-permute-done.22.block_got
  220.2 4.9 %shard_map.230 = (bf16[512,768]{1,0:T(8,128)(2,1)}, bf16[512,768]{1,0:T(8,128)(2,1)}) custom-call(s32[8]{0:T(128)} %stack.90.flags.refs_0_, bf16[1024,768]{1,0:T(8,128)(2,1)} %maximum_select_fusion.rows_ref.refs_2_, bf16[1024,768]{1,0:T(8,128)(2,1)} %get-tuple-element.112.resid_ref, f32[512,768]{1,0:T(8,128)} %get-tuple-element.140.keep_ref, ...), custom_call_target="tpu_custom_call" | custom-call | bytes 9000000 | tf_op jit(solution)/shard_map/pallas_call | solution.py:222
  225.2 3.5 %collective-permute-start.23 = (bf16[512,768]{1,0:T(8,128)(2,1)}, bf16[512,768]{1,0:T(8,128)(2,1)S(1)}, u32[]{:S(2)}, u32[]{:S(2)}) collective-permute-start(bf16[512,768]{1,0:T(8,128)(2,1)} %get-tuple-element.146.grad_own), channel_id=1, source_target_pairs={{1,16},{3,18},{5,20},{7,22},{9,24},{11,26},{13,28},{15,30},{16,1},... | collective-permute-start | bytes 2359304 | tf_op jit(solution)/shard_map/ppermute | solution.py:716
  229.4 2.7 collective-permute-start.25
  232.2 2.3 collective-permute-start.24
  234.5 11.8 %collective-permute-done.25 = bf16[192,384]{1,0:T(8,128)(2,1)S(1)} collective-permute-done((bf16[192,384]{1,0:T(8,128)(2,1)S(1)}, bf16[192,384]{1,0:T(8,128)(2,1)S(1)}, u32[]{:S(2)}, u32[]{:S(2)}) %collective-permute-start.25) | collective-permute-done | bytes 147488 | tf_op jit(solution)/shard_map/ppermute | solution.py:782
  246.3 6.7 %collective-permute-done.24 = bf16[192,384]{1,0:T(8,128)(2,1)S(1)} collective-permute-done((bf16[192,384]{1,0:T(8,128)(2,1)S(1)}, bf16[192,384]{1,0:T(8,128)(2,1)S(1)}, u32[]{:S(2)}, u32[]{:S(2)}) %collective-permute-start.24) | collective-permute-done | bytes 147488 | tf_op jit(solution)/shard_map/ppermute | solution.py:782
  253.0 2.6 collective-permute-start.27
  255.8 1.4 collective-permute-done.28
  257.2 1.0 collective-permute-start.29
  258.1 1.0 pad_maximum_fusion.5
  259.1 3.1 %collective-permute-start.30 = (bf16[2,192,384]{2,1,0:T(8,128)(2,1)S(1)}, bf16[2,192,384]{2,1,0:T(8,128)(2,1)S(1)}, u32[]{:S(2)}, u32[]{:S(2)}) collective-permute-start(bf16[2,192,384]{2,1,0:T(8,128)(2,1)S(1)} %pad_maximum_fusion.5), channel_id=1, source_target_pairs={{1,17},{3,19},{5,21},{7,23},{9,25},{11,27},{13,29},{15,31},{16,0},... | collective-permute-start | bytes 884744 | tf_op jit(solution)/shard_map/ppermute | solution.py:731
  262.2 3.4 %collective-permute-done.29.got_ref = bf16[2,192,384]{2,1,0:T(8,128)(2,1)S(1)} collective-permute-done((bf16[2,192,384]{2,1,0:T(8,128)(2,1)S(1)}, bf16[2,192,384]{2,1,0:T(8,128)(2,1)S(1)}, u32[]{:S(2)}, u32[]{:S(2)}) %collective-permute-start.29) | collective-permute-done | bytes 294944 | tf_op jit(solution)/shard_map/ppermute | solution.py:739
  266.4 1.3 collective-permute-done.30
  268.7 13.6 %collective-permute-start.32 = (bf16[2,2,2,192,384]{4,3,2,1,0:T(8,128)(2,1)S(1)}, bf16[2,2,2,192,384]{4,3,2,1,0:T(8,128)(2,1)S(1)}, u32[]{:S(2)}, u32[]{:S(2)}) collective-permute-start(bf16[2,2,2,192,384]{4,3,2,1,0:T(8,128)(2,1)S(1)} %pad_maximum_fusion.2.own_ref), channel_id=1, source_target_pairs={{0,1},{1,0},{2,3},{3,2},{4,5},{5,4},{6,7},{7,6},{8,9},{9,8},{10,11... | collective-permute-start | bytes 3538952 | tf_op jit(solution)/shard_map/ppermute | solution.py:743
  283.5 2.8 shard_map.232
  286.3 3.3 %shard_map.231 = (bf16[512,768]{1,0:T(8,128)(2,1)}, bf16[512,768]{1,0:T(8,128)(2,1)}) custom-call(s32[8]{0:T(128)} %stack.90.flags.refs_0_, f32[5]{0:T(128)} %weight_ref.3, f32[512,768]{1,0:T(8,128)} %get-tuple-element.93.part_ref, bf16[512,768]{1,0:T(8,128)(2,1)} %get-tuple-element.146.grad_own, bf16[512,768]{1,0:T(8,128)(2,1)} %copy-done.13, ...), custom_call_target="tpu_custom_call" | custom-call | bytes 6000000 | tf_op jit(solution)/shard_map/pallas_call | solution.py:624
  289.7 1.0 copy-done.9
  290.7 3.9 %shard_map.233 = (f32[192,1536]{1,0:T(8,128)}, f32[192,1536]{1,0:T(8,128)}) custom-call(s32[8]{0:T(128)} %stack.90.flags.refs_0_, bf16[2,2,2,192,384]{4,3,2,1,0:T(8,128)(2,1)} %copy-done.4, bf16[2,2,2,192,384]{4,3,2,1,0:T(8,128)(2,1)} %copy-done.9), custom_call_target="tpu_custom_call" | custom-call | bytes 6000000 | tf_op jit(solution)/shard_map/pallas_call | solution.py:650
  (118 shorter events, 16.7 us)
Async XLA Ops:
  7.2 188.1 %reduce-scatter.13.cloned.1.call-start = ((), (), s32[]{:S(2)}) async-start(), calls=%async_computation.6 | async-start | bytes 2949120
  7.2 20.5 %collective-permute-start.2 = (s32[1,3]{1,0:T(1,128)}, s32[1,3]{1,0:T(1,128)S(1)}, u32[]{:S(2)}, u32[]{:S(2)}) collective-permute-start(s32[1,3]{1,0:T(1,128)} %param.16), channel_id=1, source_target_pairs={{0,1},{1,0},{2,3},{3,2},{4,5},{5,4},{6,7},{7,6},{8,9},{9,8},{10,11... | collective-permute-start | bytes 44 | tf_op jit(solution)/shard_map/ppermute | solution.py:743
  8.0 20.1 %collective-permute-start = (bf16[512,768]{1,0:T(8,128)(2,1)}, bf16[512,768]{1,0:T(8,128)(2,1)}, u32[]{:S(2)}, u32[]{:S(2)}) collective-permute-start(bf16[512,768]{1,0:T(8,128)(2,1)} %bitcast.55), channel_id=1, source_target_pairs={{1,16},{3,18},{5,20},{7,22},{9,24},{11,26},{13,28},{15,30},{16,1},... | collective-permute-start | bytes 2359304 | tf_op jit(solution)/shard_map/ppermute | solution.py:716
  11.0 31.3 %collective-permute-start.3 = (bf16[3,768,384]{2,1,0:T(8,128)(2,1)}, bf16[3,768,384]{2,1,0:T(8,128)(2,1)}, u32[]{:S(2)}, u32[]{:S(2)}) collective-permute-start(bf16[3,768,384]{2,1,0:T(8,128)(2,1)} %w_own.1), channel_id=1, source_target_pairs={{1,16},{3,18},{5,20},{7,22},{9,24},{11,26},{13,28},{15,30},{16,1},... | collective-permute-start | bytes 5308424 | tf_op jit(solution)/shard_map/ppermute | solution.py:716
  16.3 2.9 copy-start
  19.3 1.3 copy-start.6
  19.3 1.7 copy-start.16
  22.7 5.0 %copy-start.20 = (s32[1,3]{1,0:T(1,128)S(1)}, s32[1,3]{1,0:T(1,128)}, u32[]{:S(2)}) copy-start(s32[1,3]{1,0:T(1,128)} %param.16) | copy-start | bytes 40
  22.7 5.4 %copy-start.11 = (bf16[1,512,768]{2,1,0:T(8,128)(2,1)S(1)}, bf16[1,512,768]{2,1,0:T(8,128)(2,1)}, u32[]{:S(2)}) copy-start(bf16[1,512,768]{2,1,0:T(8,128)(2,1)} %param.13) | copy-start | bytes 2359300
  29.3 5.0 %collective-permute-start.1 = (bf16[512,768]{1,0:T(8,128)(2,1)S(1)}, bf16[512,768]{1,0:T(8,128)(2,1)S(1)}, u32[]{:S(2)}, u32[]{:S(2)}) collective-permute-start(bf16[512,768]{1,0:T(8,128)(2,1)S(1)} %broadcast_select_fusion.1), channel_id=1, source_target_pairs={{0,1},{1,0},{2,3},{3,2},{4,5},{5,4},{6,7},{7,6},{8,9},{9,8},{10,11... | collective-permute-start | bytes 2359304 | tf_op jit(solution)/shard_map/ppermute | solution.py:743
  36.1 28.3 %collective-permute-start.4 = (bf16[896,768]{1,0:T(8,128)(2,1)S(1)}, bf16[896,768]{1,0:T(8,128)(2,1)S(1)}, u32[]{:S(2)}, u32[]{:S(2)}) collective-permute-start(bf16[896,768]{1,0:T(8,128)(2,1)S(1)} %pad_maximum_fusion.1), channel_id=1, source_target_pairs={{1,16},{3,18},{5,20},{7,22},{9,24},{11,26},{13,28},{15,30},{16,1},... | collective-permute-start | bytes 4128776 | tf_op jit(solution)/shard_map/ppermute | solution.py:716
  39.1 41.9 %collective-permute-start.7 = (bf16[1536,768]{1,0:T(8,128)(2,1)}, bf16[1536,768]{1,0:T(8,128)(2,1)}, u32[]{:S(2)}, u32[]{:S(2)}) collective-permute-start(bf16[1536,768]{1,0:T(8,128)(2,1)} %pad_maximum_fusion), channel_id=1, source_target_pairs={{1,16},{3,18},{5,20},{7,22},{9,24},{11,26},{13,28},{15,30},{16,1},... | collective-permute-start | bytes 7077896 | tf_op jit(solution)/shard_map/ppermute | solution.py:716
  64.4 1.1 copy-start.5
  65.5 6.9 %copy-start.3 = (bf16[896,768]{1,0:T(8,128)(2,1)}, bf16[896,768]{1,0:T(8,128)(2,1)S(1)}, u32[]{:S(2)}) copy-start(bf16[896,768]{1,0:T(8,128)(2,1)S(1)} %broadcast_select_fusion) | copy-start | bytes 4128772
  66.5 10.1 %copy-start.1 = (bf16[1024,768]{1,0:T(8,128)(2,1)}, bf16[1024,768]{1,0:T(8,128)(2,1)S(1)}, u32[]{:S(2)}) copy-start(bf16[1024,768]{1,0:T(8,128)(2,1)S(1)} %convolution_convert_fusion.refs_3_.own_ref) | copy-start | bytes 4718596
  66.5 14.6 %collective-permute-start.5 = (bf16[1024,768]{1,0:T(8,128)(2,1)S(1)}, bf16[1024,768]{1,0:T(8,128)(2,1)S(1)}, u32[]{:S(2)}, u32[]{:S(2)}) collective-permute-start(bf16[1024,768]{1,0:T(8,128)(2,1)S(1)} %convolution_convert_fusion.refs_3_.own_ref), channel_id=1, source_target_pairs={{0,1},{1,0},{2,3},{3,2},{4,5},{5,4},{6,7},{7,6},{8,9},{9,8},{10,11... | collective-permute-start | bytes 4718600 | tf_op jit(solution)/shard_map/ppermute | solution.py:743
  66.6 34.4 %collective-permute-start.9 = (bf16[768,768]{1,0:T(8,128)(2,1)}, bf16[768,768]{1,0:T(8,128)(2,1)}, u32[]{:S(2)}, u32[]{:S(2)}) collective-permute-start(bf16[768,768]{1,0:T(8,128)(2,1)} %get-tuple-element.109), channel_id=1, source_target_pairs={{1,16},{3,18},{5,20},{7,22},{9,24},{11,26},{13,28},{15,30},{16,1},... | collective-permute-start | bytes 3538952 | tf_op jit(solution)/shard_map/ppermute | solution.py:716
  69.6 36.7 %collective-permute-start.10 = (bf16[768,768]{1,0:T(8,128)(2,1)}, bf16[768,768]{1,0:T(8,128)(2,1)}, u32[]{:S(2)}, u32[]{:S(2)}) collective-permute-start(bf16[768,768]{1,0:T(8,128)(2,1)} %get-tuple-element.110), channel_id=1, source_target_pairs={{1,16},{3,18},{5,20},{7,22},{9,24},{11,26},{13,28},{15,30},{16,1},... | collective-permute-start | bytes 3538952 | tf_op jit(solution)/shard_map/ppermute | solution.py:716
  72.4 2.4 collective-permute-start.6
  81.1 1.2 copy-start.2
  106.4 122.3 %reduce-scatter.15.cloned.1.call-start = ((), (), s32[]{:S(2)}) async-start(), calls=%async_computation.7 | async-start | bytes 2949120
  121.7 1.4 copy-start.7
  121.8 136.3 %reduce-scatter.9.cloned.1.call-start = ((), (), s32[]{:S(2)}) async-start(), calls=%async_computation.4 | async-start | bytes 737280 | tf_op jit(solution)/shard_map/reduce_scatter | solution.py:770
  122.1 3.7 %collective-permute-start.11 = (bf16[1024,768]{1,0:T(8,128)(2,1)}, bf16[1024,768]{1,0:T(8,128)(2,1)S(1)}, u32[]{:S(2)}, u32[]{:S(2)}) collective-permute-start(bf16[1024,768]{1,0:T(8,128)(2,1)} %get-tuple-element.111.late_own), channel_id=1, source_target_pairs={{0,1},{1,0},{2,3},{3,2},{4,5},{5,4},{6,7},{7,6},{8,9},{9,8},{10,11... | collective-permute-start | bytes 4718600 | tf_op jit(solution)/shard_map/ppermute | solution.py:743
  123.2 4.8 %collective-permute-start.8 = (bf16[1024,768]{1,0:T(8,128)(2,1)S(1)}, bf16[1024,768]{1,0:T(8,128)(2,1)}, u32[]{:S(2)}, u32[]{:S(2)}) collective-permute-start(bf16[1024,768]{1,0:T(8,128)(2,1)S(1)} %copy-done.7), channel_id=1, source_target_pairs={{0,1},{1,0},{2,3},{3,2},{4,5},{5,4},{6,7},{7,6},{8,9},{9,8},{10,11... | collective-permute-start | bytes 4718600 | tf_op jit(solution)/shard_map/ppermute | solution.py:743
  125.7 2.2 copy-start.8
  162.4 13.3 %copy-start.19 = (f32[8,768]{1,0:T(8,128)S(1)}, f32[8,768]{1,0:T(8,128)}, u32[]{:S(2)}) copy-start(f32[8,768]{1,0:T(8,128)} %get-tuple-element.128) | copy-start | bytes 73732
  170.3 42.7 %collective-permute-start.18 = (bf16[768,384]{1,0:T(8,128)(2,1)}, bf16[768,384]{1,0:T(8,128)(2,1)S(1)}, u32[]{:S(2)}, u32[]{:S(2)}) collective-permute-start(bf16[768,384]{1,0:T(8,128)(2,1)} %get-tuple-element.132), channel_id=1, source_target_pairs={{0,1},{1,17},{2,3},{3,19},{4,5},{5,21},{6,7},{7,23},{8,9},{9,25},{... | collective-permute-start | bytes 1769480 | tf_op jit(solution)/shard_map/ppermute | solution.py:720
  171.2 41.8 %collective-permute-start.19 = (bf16[768,384]{1,0:T(8,128)(2,1)}, bf16[768,384]{1,0:T(8,128)(2,1)}, u32[]{:S(2)}, u32[]{:S(2)}) collective-permute-start(bf16[768,384]{1,0:T(8,128)(2,1)} %get-tuple-element.133), channel_id=1, source_target_pairs={{0,2},{1,18},{2,0},{3,16},{4,6},{5,22},{6,4},{7,20},{8,10},{9,26},... | collective-permute-start | bytes 1769480 | tf_op jit(solution)/shard_map/ppermute | solution.py:720
  173.2 39.8 %collective-permute-start.20 = (bf16[768,384]{1,0:T(8,128)(2,1)}, bf16[768,384]{1,0:T(8,128)(2,1)}, u32[]{:S(2)}, u32[]{:S(2)}) collective-permute-start(bf16[768,384]{1,0:T(8,128)(2,1)} %get-tuple-element.134), channel_id=1, source_target_pairs={{0,3},{1,19},{2,1},{3,17},{4,7},{5,23},{6,5},{7,21},{8,11},{9,27},... | collective-permute-start | bytes 1769480 | tf_op jit(solution)/shard_map/ppermute | solution.py:720
  173.2 39.8 %collective-permute-start.17 = (bf16[768,384]{1,0:T(8,128)(2,1)}, bf16[768,384]{1,0:T(8,128)(2,1)}, u32[]{:S(2)}, u32[]{:S(2)}) collective-permute-start(bf16[768,384]{1,0:T(8,128)(2,1)} %get-tuple-element.116), channel_id=1, source_target_pairs={{1,16},{3,18},{5,20},{7,22},{9,24},{11,26},{13,28},{15,30},{16,1},... | collective-permute-start | bytes 1769480 | tf_op jit(solution)/shard_map/ppermute | solution.py:720
  194.3 21.9 %copy-start.17 = (bf16[768,384]{1,0:T(8,128)(2,1)S(1)}, bf16[768,384]{1,0:T(8,128)(2,1)}, u32[]{:S(2)}) copy-start(bf16[768,384]{1,0:T(8,128)(2,1)} %get-tuple-element.116) | copy-start | bytes 1769476
  195.2 1.3 collective-permute-start.12
  195.3 62.8 %reduce-scatter.11.cloned.1.call-start = ((), (), s32[]{:S(2)}) async-start(), calls=%async_computation.5 | async-start | bytes 737280 | tf_op jit(solution)/shard_map/reduce_scatter | solution.py:770
  196.5 3.4 %collective-permute-start.13 = (f32[9,768]{1,0:T(8,128)S(1)}, f32[9,768]{1,0:T(8,128)S(1)}, u32[]{:S(2)}, u32[]{:S(2)}) collective-permute-start(f32[9,768]{1,0:T(8,128)S(1)} %fusion.8), channel_id=1, source_target_pairs={{0,4},{4,0},{8,12},{12,8},{1,5},{5,1},{9,13},{13,9},{2,6},{6,2},{1... | collective-permute-start | bytes 82952 | tf_op jit(solution)/shard_map/ppermute | solution.py:790
  199.9 6.5 %collective-permute-start.14 = (f32[9,768]{1,0:T(8,128)S(1)}, f32[9,768]{1,0:T(8,128)S(1)}, u32[]{:S(2)}, u32[]{:S(2)}) collective-permute-start(f32[9,768]{1,0:T(8,128)S(1)} %add.100), channel_id=1, source_target_pairs={{0,8},{4,12},{8,0},{12,4},{1,9},{5,13},{9,1},{13,5},{2,10},{6,14},... | collective-permute-start | bytes 82952 | tf_op jit(solution)/shard_map/ppermute | solution.py:790
  206.4 2.9 collective-permute-start.15
  209.4 3.6 %collective-permute-start.16 = (f32[9,768]{1,0:T(8,128)S(1)}, f32[9,768]{1,0:T(8,128)S(1)}, u32[]{:S(2)}, u32[]{:S(2)}) collective-permute-start(f32[9,768]{1,0:T(8,128)S(1)} %add.102), channel_id=1, source_target_pairs={{0,2},{2,0},{1,3},{3,1},{4,6},{6,4},{5,7},{7,5},{8,10},{10,8},{9,1... | collective-permute-start | bytes 82952 | tf_op jit(solution)/shard_map/ppermute | solution.py:790
  213.0 5.2 %collective-permute-start.21 = (bf16[512,768]{1,0:T(8,128)(2,1)}, bf16[512,768]{1,0:T(8,128)(2,1)S(1)}, u32[]{:S(2)}, u32[]{:S(2)}) collective-permute-start(bf16[512,768]{1,0:T(8,128)(2,1)} %get-tuple-element.141), channel_id=1, source_target_pairs={{0,1},{1,0},{2,3},{3,2},{4,5},{5,4},{6,7},{7,6},{8,9},{9,8},{10,11... | collective-permute-start | bytes 2359304 | tf_op jit(solution)/shard_map/ppermute | solution.py:743
  216.1 3.2 %collective-permute-start.22 = (bf16[512,768]{1,0:T(8,128)(2,1)}, bf16[512,768]{1,0:T(8,128)(2,1)S(1)}, u32[]{:S(2)}, u32[]{:S(2)}) collective-permute-start(bf16[512,768]{1,0:T(8,128)(2,1)} %get-tuple-element.143), channel_id=1, source_target_pairs={{0,1},{1,0},{2,3},{3,2},{4,5},{5,4},{6,7},{7,6},{8,9},{9,8},{10,11... | collective-permute-start | bytes 2359304 | tf_op jit(solution)/shard_map/ppermute | solution.py:743
  218.2 1.1 copy-start.14
  219.4 0.9 copy-start.15
  225.2 27.8 %copy-start.12 = (bf16[512,768]{1,0:T(8,128)(2,1)S(1)}, bf16[512,768]{1,0:T(8,128)(2,1)}, u32[]{:S(2)}) copy-start(bf16[512,768]{1,0:T(8,128)(2,1)} %get-tuple-element.148.block_own) | copy-start | bytes 2359300
  225.2 27.8 %collective-permute-start.23 = (bf16[512,768]{1,0:T(8,128)(2,1)}, bf16[512,768]{1,0:T(8,128)(2,1)S(1)}, u32[]{:S(2)}, u32[]{:S(2)}) collective-permute-start(bf16[512,768]{1,0:T(8,128)(2,1)} %get-tuple-element.146.grad_own), channel_id=1, source_target_pairs={{1,16},{3,18},{5,20},{7,22},{9,24},{11,26},{13,28},{15,30},{16,1},... | collective-permute-start | bytes 2359304 | tf_op jit(solution)/shard_map/ppermute | solution.py:716
  228.9 5.6 %collective-permute-start.26 = (bf16[192,384]{1,0:T(8,128)(2,1)S(1)}, bf16[192,384]{1,0:T(8,128)(2,1)S(1)}, u32[]{:S(2)}, u32[]{:S(2)}) collective-permute-start(bf16[192,384]{1,0:T(8,128)(2,1)S(1)} %get-tuple-element.218), channel_id=1, source_target_pairs={{0,12},{4,0},{8,4},{12,8},{1,13},{5,1},{9,5},{13,9},{2,14},{6,2},{... | collective-permute-start | bytes 442376 | tf_op jit(solution)/shard_map/ppermute | solution.py:782
  229.4 16.9 %collective-permute-start.25 = (bf16[192,384]{1,0:T(8,128)(2,1)S(1)}, bf16[192,384]{1,0:T(8,128)(2,1)S(1)}, u32[]{:S(2)}, u32[]{:S(2)}) collective-permute-start(bf16[192,384]{1,0:T(8,128)(2,1)S(1)} %get-tuple-element.219), channel_id=1, source_target_pairs={{0,8},{4,12},{8,0},{12,4},{1,9},{5,13},{9,1},{13,5},{2,10},{6,14},... | collective-permute-start | bytes 442376 | tf_op jit(solution)/shard_map/ppermute | solution.py:782
  232.2 20.8 %collective-permute-start.24 = (bf16[192,384]{1,0:T(8,128)(2,1)S(1)}, bf16[192,384]{1,0:T(8,128)(2,1)S(1)}, u32[]{:S(2)}, u32[]{:S(2)}) collective-permute-start(bf16[192,384]{1,0:T(8,128)(2,1)S(1)} %get-tuple-element.220), channel_id=1, source_target_pairs={{0,4},{4,8},{8,12},{12,0},{1,5},{5,9},{9,13},{13,1},{2,6},{6,10},{... | collective-permute-start | bytes 442376 | tf_op jit(solution)/shard_map/ppermute | solution.py:782
  253.0 14.8 %copy-start.13 = (bf16[512,768]{1,0:T(8,128)(2,1)}, bf16[512,768]{1,0:T(8,128)(2,1)S(1)}, u32[]{:S(2)}) copy-start(bf16[512,768]{1,0:T(8,128)(2,1)S(1)} %collective-permute-done.23.grad_got) | copy-start | bytes 2359300
  253.0 13.4 %collective-permute-start.27 = (bf16[512,768]{1,0:T(8,128)(2,1)S(1)}, bf16[512,768]{1,0:T(8,128)(2,1)}, u32[]{:S(2)}, u32[]{:S(2)}) collective-permute-start(bf16[512,768]{1,0:T(8,128)(2,1)S(1)} %copy-done.12), channel_id=1, source_target_pairs={{1,16},{3,18},{5,20},{7,22},{9,24},{11,26},{13,28},{15,30},{16,1},... | collective-permute-start | bytes 2359304 | tf_op jit(solution)/shard_map/ppermute | solution.py:716
  255.7 1.4 collective-permute-start.28
  257.1 11.5 %copy-start.10 = (bf16[2,192,384]{2,1,0:T(8,128)(2,1)}, bf16[2,192,384]{2,1,0:T(8,128)(2,1)S(1)}, u32[]{:S(2)}) copy-start(bf16[2,192,384]{2,1,0:T(8,128)(2,1)S(1)} %pad_maximum_fusion.4.own_ref) | copy-start | bytes 884740
  257.2 8.5 %collective-permute-start.29 = (bf16[2,192,384]{2,1,0:T(8,128)(2,1)S(1)}, bf16[2,192,384]{2,1,0:T(8,128)(2,1)S(1)}, u32[]{:S(2)}, u32[]{:S(2)}) collective-permute-start(bf16[2,192,384]{2,1,0:T(8,128)(2,1)S(1)} %pad_maximum_fusion.4.own_ref), channel_id=1, source_target_pairs={{0,2},{2,0},{1,3},{3,1},{4,6},{6,4},{5,7},{7,5},{8,10},{10,8},{9,1... | collective-permute-start | bytes 884744 | tf_op jit(solution)/shard_map/ppermute | solution.py:739
  259.1 8.5 %collective-permute-start.30 = (bf16[2,192,384]{2,1,0:T(8,128)(2,1)S(1)}, bf16[2,192,384]{2,1,0:T(8,128)(2,1)S(1)}, u32[]{:S(2)}, u32[]{:S(2)}) collective-permute-start(bf16[2,192,384]{2,1,0:T(8,128)(2,1)S(1)} %pad_maximum_fusion.5), channel_id=1, source_target_pairs={{1,17},{3,19},{5,21},{7,23},{9,25},{11,27},{13,29},{15,31},{16,0},... | collective-permute-start | bytes 884744 | tf_op jit(solution)/shard_map/ppermute | solution.py:731
  265.7 3.0 copy-start.18
  267.8 0.7 collective-permute-start.31
  268.7 21.0 %copy-start.4 = (bf16[2,2,2,192,384]{4,3,2,1,0:T(8,128)(2,1)}, bf16[2,2,2,192,384]{4,3,2,1,0:T(8,128)(2,1)S(1)}, u32[]{:S(2)}) copy-start(bf16[2,2,2,192,384]{4,3,2,1,0:T(8,128)(2,1)S(1)} %pad_maximum_fusion.2.own_ref) | copy-start | bytes 3538948
  268.7 21.0 %collective-permute-start.32 = (bf16[2,2,2,192,384]{4,3,2,1,0:T(8,128)(2,1)S(1)}, bf16[2,2,2,192,384]{4,3,2,1,0:T(8,128)(2,1)S(1)}, u32[]{:S(2)}, u32[]{:S(2)}) collective-permute-start(bf16[2,2,2,192,384]{4,3,2,1,0:T(8,128)(2,1)S(1)} %pad_maximum_fusion.2.own_ref), channel_id=1, source_target_pairs={{0,1},{1,0},{2,3},{3,2},{4,5},{5,4},{6,7},{7,6},{8,9},{9,8},{10,11... | collective-permute-start | bytes 3538952 | tf_op jit(solution)/shard_map/ppermute | solution.py:743
  289.7 1.0 copy-start.9
Sparse Core Ops, SparseCore 0:
  106.5 37.8 reduce-scatter.12
  147.5 44.2 reduce-scatter.14
  195.4 19.5 reduce-scatter.8
  228.9 24.0 reduce-scatter.10

commit v3 on v2

--- a/solution.py
+++ b/solution.py
@@ -15,6 +15,7 @@
 NORM_EPS = 1e-05
 RATE = 3e6
 ROOM = 60 << 20
+SNUG = 18 << 20
 
 
 def lasting(microseconds):
@@ -212,7 +213,7 @@
 TALL = 512
 
 
-def streamed(kernel, steps, scalars, fields, outs, scratch, microseconds):
+def streamed(kernel, steps, scalars, fields, outs, scratch, microseconds, room=ROOM):
     def spec(shape, block=None, at=None):
         if block is None:
             return pl.BlockSpec(shape, lambda i, *scalars: (0,) * len(shape))
@@ -229,7 +230,7 @@
             scratch_shapes=[pltpu.VMEM(shape, dtype) for shape, dtype in scratch],
         ),
         out_shape=[jax.ShapeDtypeStruct(*out[:2]) for out in outs],
-        compiler_params=pltpu.CompilerParams(vmem_limit_bytes=ROOM),
+        compiler_params=pltpu.CompilerParams(vmem_limit_bytes=room),
         cost_estimate=lasting(microseconds),
     )(*scalars, *[field[0] for field in fields])
 
@@ -431,6 +432,7 @@
         [(shape, jnp.float32, *keep), (shape, jnp.bfloat16, *send), ((8, width), jnp.float32)],
         [],
         6,
+        SNUG,
     )
 
 
@@ -551,17 +553,18 @@
         [(shape, jnp.float32, *keep), (shape, jnp.bfloat16, *send), ((8, width), jnp.float32)],
         [],
         5,
-    )
-
-
-def last_kernel(flags, rows_ref, resid_ref, keep_ref, got_ref, block_keep, block_got, vectors, grad_ref, block_ref):
+        SNUG,
+    )
+
+
+def last_kernel(flags, rows_ref, resid_ref, keep_ref, got_ref, block_keep, block_got, vectors, out_ref):
     unit, scale = norm_parts(rows_ref[...].astype(jnp.float32))
     inner = (keep_ref[...] + got_ref[...].astype(jnp.float32)) * vectors[0:1, :]
     mean = jnp.mean(inner, axis=-1, keepdims=True)
     slant = jnp.mean(inner * unit, axis=-1, keepdims=True)
     grad = resid_ref[...].astype(jnp.float32) + scale * (inner - mean - unit * slant)
-    grad_ref[...] = grad.astype(jnp.bfloat16)
-    block_ref[...] = (block_keep[...] + block_got[...].astype(jnp.float32)).astype(jnp.bfloat16)
+    out_ref[0] = grad.astype(jnp.bfloat16)
+    out_ref[1] = (block_keep[...] + block_got[...].astype(jnp.float32)).astype(jnp.bfloat16)
 
 
 def last(flags, rows, resid, keep, got, block_keep, block_got, vectors):
@@ -571,10 +574,10 @@
     def mine(i, flags):
         return flags[1] * steps + i
 
-    out = ((half, width), jnp.bfloat16, (ROWS, width), lambda i, flags: (i, 0))
+    out = ((2, half, width), jnp.bfloat16, (2, ROWS, width), lambda i, flags: (0, i, 0))
     fields = [by_rows(rows, ROWS, mine), by_rows(resid, ROWS, mine)]
     fields += [by_rows(field, ROWS) for field in (keep, got, block_keep, block_got)]
-    return streamed(last_kernel, steps, [flags], fields + [vectors], [out] * 2, [], 3)
+    return streamed(last_kernel, steps, [flags], fields + [vectors], [out], [], 3, SNUG)[0]
 
 
 def past_kernel(dwa_ref, hist_ref, cot_ref, grad_ref, part_ref, sums_ref):
@@ -611,83 +614,40 @@
     )(dwa, history, cot)
 
 
-def present_kernel(flags, weight_ref, part_ref, grad_own, grad_got, block_own, block_got, out_ref, grad_ref):
-    here = jnp.where(flags[0] == 1, block_own[...], block_got[...]).astype(jnp.float32)
+def present_kernel(flags, weight_ref, part_ref, own_ref, got_ref, out_ref, grad_ref):
+    here = jnp.where(flags[0] == 1, own_ref[1], got_ref[1]).astype(jnp.float32)
     out_ref[...] = (part_ref[...] + weight_ref[weight_ref.shape[0] - 1] * here).astype(jnp.bfloat16)
-    grad_ref[...] = jnp.where(flags[0] == 1, grad_own[...], grad_got[...])
-
-
-def present(flags, weight, part, grad_own, grad_got, block_own, block_got):
+    grad_ref[...] = jnp.where(flags[0] == 1, own_ref[0], got_ref[0])
+
+
+def present(flags, weight, part, own, got):
     rows, width = part.shape
-    scalars = pl.BlockSpec(memory_space=pltpu.SMEM)
-    tokens = pl.BlockSpec((ROWS, width), lambda i: (i, 0))
-    return pl.pallas_call(
-        present_kernel,
-        grid=(rows // ROWS,),
-        in_specs=[scalars, scalars] + [tokens] * 5,
-        out_specs=[tokens, tokens],
-        out_shape=[jax.ShapeDtypeStruct((rows, width), jnp.bfloat16)] * 2,
-        compiler_params=pltpu.CompilerParams(vmem_limit_bytes=ROOM),
-        cost_estimate=lasting(2),
-    )(flags, weight, part, grad_own, grad_got, block_own, block_got)
-
-
-def place_feed_kernel(flags, own_ref, got_ref, up_ref, down_ref):
-    part = own_ref.shape[-1]
-    far, tp = flags[2], flags[7]
+    both = (2, ROWS, width), lambda i, *scalars: (0, i, 0)
+    out = ((rows, width), jnp.bfloat16, (ROWS, width), lambda i, *scalars: (i, 0))
+    fields = [by_rows(part, ROWS), (own, *both), (got, *both)]
+    return streamed(present_kernel, rows // ROWS, [flags, weight], fields, [out] * 2, [], 2, SNUG)
+
+
+def place_kernel(flags, here_ref, there_ref, qkv_ref, out_ref, up_ref, down_ref):
+    near, far = flags[1], flags[2]
+    part = out_ref.shape[1]
     for k in range(2):
-        for t, out_ref in enumerate((up_ref, down_ref)):
+        for c in range(2):
+            field = jnp.where(near == c, here_ref[k ^ far], there_ref[k ^ far]).astype(jnp.float32)
+            if 2 * k + c < 3:
+                qkv_ref[2 * k + c] = field[:, :part]
+            else:
+                out_ref[...] = field[:, :part]
             for half in range(2):
                 at = (2 * half + k) * part
-                here = [ref[k ^ far, t ^ tp, half].astype(jnp.float32) for ref in (own_ref, got_ref)]
-                out_ref[:, at : at + part] = jnp.where(flags[0] == 1, *here)
-
-
-def place_feed(flags, own, got):
-    rows, part = own.shape[-2:]
-    both = whole_spec(own.shape)
-    block = whole_spec((rows, 4 * part))
-    return pl.pallas_call(
-        place_feed_kernel,
-        grid_spec=pltpu.PrefetchScalarGridSpec(
-            num_scalar_prefetch=1, grid=(1,), in_specs=[both, both], out_specs=[block, block]
-        ),
-        out_shape=[jax.ShapeDtypeStruct((rows, 4 * part), jnp.float32)] * 2,
-        compiler_params=pltpu.CompilerParams(vmem_limit_bytes=ROOM),
-        cost_estimate=lasting(2),
-    )(flags, own, got)
-
-
-def place_attention_kernel(flags, own_ref, got_ref, qkv_ref, out_ref):
-    near, far = flags[1], flags[2]
-    for k in range(2):
-        for c in range(2):
-            here = [ref[c ^ near].astype(jnp.float32) for ref in (own_ref, got_ref)]
-            field = jnp.where(far == k, *here)
-            if 2 * k + c < 3:
-                qkv_ref[2 * k + c] = field
-            else:
-                out_ref[...] = field
-
-
-def place_attention(flags, own, got):
-    rows, part = own.shape[-2:]
-    both = whole_spec(own.shape)
-    return pl.pallas_call(
-        place_attention_kernel,
-        grid_spec=pltpu.PrefetchScalarGridSpec(
-            num_scalar_prefetch=1,
-            grid=(1,),
-            in_specs=[both, both],
-            out_specs=[whole_spec((3, rows, part)), whole_spec((rows, part))],
-        ),
-        out_shape=[
-            jax.ShapeDtypeStruct((3, rows, part), jnp.float32),
-            jax.ShapeDtypeStruct((rows, part), jnp.float32),
-        ],
-        compiler_params=pltpu.CompilerParams(vmem_limit_bytes=ROOM),
-        cost_estimate=lasting(1),
-    )(flags, own, got)
+                (up_ref, down_ref)[c][:, at : at + part] = field[:, (1 + half) * part : (2 + half) * part]
+
+
+def place(flags, here, there):
+    rows, part = here.shape[1], here.shape[2] // 3
+    outs = [((3, rows, part), jnp.float32), ((rows, part), jnp.float32)]
+    outs += [((rows, 4 * part), jnp.float32)] * 2
+    return streamed(place_kernel, 1, [flags], [here, there], outs, [], 3, SNUG)
 
 
 AXES = ("tp", "dp", "far", "near")
@@ -706,10 +666,6 @@
 
 def anyone(t, d, k, c):
     return True
-
-
-def home(t, d, k, c):
-    return t == c
 
 
 def swap_diagonal(field):
@@ -725,14 +681,6 @@
             lambda t, d, k, c: (c, d, k ^ other_far, t ^ other_tp),
         ),
     )
-
-
-def bring_home(field):
-    return lax.ppermute(field, AXES, moves(away, lambda t, d, k, c: (c, d, k, c)))
-
-
-def swap_far_home(field):
-    return lax.ppermute(field, AXES, moves(home, lambda t, d, k, c: (t, d, 1 - k, c)))
 
 
 def swap_far(field):
@@ -872,39 +820,29 @@
         flags, act_early, act_late, down_early, down_late, layer_rows, attn, attn_got, after(cot_rows, send)
     )
     small = jnp.concatenate([sums_one[:2], sums_two[:2], sums_now[:1], sums_past[:hist_count]], axis=0)
-    early_sum = scatter_rows(after(early_sum, owned[0]))
-    for name in ("near", "dp", "tp", "far"):
+    for name in ("near", "dp"):
         small = sum_over(small, name)
     small, keep, send, block_keep, block_send, *moved = lax.optimization_barrier(
         (small, keep, send, block_keep, block_send, *moved)
     )
     attn_one = add(jnp.where(same, owned[0], moved[0]), *moved[1:])
     attn_moved = move_rows(attn_one)
-    input_grad, block_half = last(
-        flags, layer_rows, grad_attn, after(keep, attn_one), swap_near(send), block_keep, swap_near(block_send), vectors
-    )
-    input_moved = swap_diagonal(input_grad)
-    late_sum = scatter_rows(after(late_sum, attn_one))
-    input_grad, input_moved, block_half, *attn_moved = lax.optimization_barrier(
-        (input_grad, input_moved, block_half, *attn_moved)
-    )
-    block_moved = swap_diagonal(block_half)
+    feed_sum = scatter_rows(jnp.concatenate([after(early_sum, attn_one), late_sum], axis=1))
+    ours = last(
+        flags, layer_rows, grad_attn, keep, swap_near(send), block_keep, swap_near(block_send), vectors
+    )
+    for name in ("tp", "far"):
+        small = sum_over(small, name)
+    small, ours, *attn_moved = lax.optimization_barrier((small, ours, *attn_moved))
+    theirs = swap_diagonal(ours)
+    feed_sum = after(feed_sum, small)
+    feed_got = swap_diagonal(feed_sum)
     attn_sum = add(*attn_moved)
-    attn_own = jnp.stack([attn_sum, swap_near(attn_sum)])
-    attn_got = swap_far(attn_own)
-    feed_sum = jnp.stack([after(early_sum, attn_sum), late_sum])
-    feed_home = bring_home(feed_sum)
-    block_moved, attn_own, attn_got, feed_sum, feed_home = lax.optimization_barrier(
-        (block_moved, attn_own, attn_got, feed_sum, feed_home)
-    )
-    feed_own = jnp.stack([feed_sum, feed_home])
-    feed_both = jnp.stack([feed_own, swap_far_home(feed_own)])
-    feed_got = swap_near(feed_both)
-    grad_w_qkv, grad_w_out = place_attention(flags, attn_own, attn_got)
-    grad_w_up, grad_w_down = place_feed(flags, feed_both, feed_got)
-    output, grad_input = present(
-        flags, dwa_weights, past_sum, input_grad, input_moved, block_half, block_moved
-    )
+    blocks = jnp.concatenate([attn_sum, jnp.where(same, feed_sum, feed_got)], axis=1)
+    here = jnp.stack([blocks, swap_far(blocks)])
+    output, grad_input = present(flags, dwa_weights, past_sum, ours, theirs)
+    here = after(here, output)
+    grad_w_qkv, grad_w_out, grad_w_up, grad_w_down = place(flags, here, swap_near(here))
 
     return (
         output[None],

time: 303 us -> 296 us (0.977)
  starting transfers between devices: 62.5 us -> 43.9 us
  local copies, waits for them, and re-layouts: 18.1 us -> 34.2 us
  Pallas kernels: 135 us -> 121 us
  waiting for transfers between devices: 53.9 us -> 58.9 us
  other arithmetic: 16.4 us -> 19.8 us
    unnamed x42 -> x74, local copies, waits for them, and re-layouts: 5.67 us -> 23.2 us
    ppermute x8, waiting for transfers between devices: 10.5 us -> 25.3 us  [swap_diagonal(): lax.ppermute(field, AXES, moves(away, lambda t, d, k, c: (c, d, k, t)))]
    ppermute x10 -> x9, starting transfers between devices: 17.9 us -> 3.11 us  [swap_near(): return lax.ppermute(field, 'near', [(0, 1), (1, 0)])]
    pallas_call x3 -> x0, Pallas kernels: 9.99 us -> none  [the longest x1 3.86 us: place_feed(): pl.pallas_call(place_feed_kernel, grid_spec=pltpu.PrefetchScalarGridSpec(...]
    ppermute x5, waiting for transfers between devices: 12.2 us -> 8.23 us  [sum_over(): lax.ppermute(field, name, [(d, d ^ bit) for d in range(size)])]
    pallas_call x8 -> x10, Pallas kernels: 84.7 us -> 80.8 us  [streamed(): pl.pallas_call(kernel, grid_spec=pltpu.PrefetchScalarGridSpec(num_scalar_...]
    ppermute x3, waiting for transfers between devices: 18.5 us -> 14.7 us  [move_rows(): lax.ppermute(sent, 'dp', [(d, (d + step) % dps) for d in range(dps)])]
    ppermute x2 -> x0, starting transfers between devices: 3.79 us -> none  [the longest x1 3.09 us: bring_home(): lax.ppermute(field, AXES, moves(away, lambda t, d, k, c: (c, d, k, c)))]
  transfers between devices with their start and end apart: 37 -> 33, of which waited for: 18 -> 15; matrix products, arithmetic and copies ran while one was open for 10% -> 10% of each run, Pallas kernels for 43% -> 40%
where the time goes in v3:
time: 296 us; the launch traced here: 293 us
  Pallas kernels  121 us (41%)
  waiting for transfers between devices  58.9 us (20%)
  starting transfers between devices  43.9 us (15%)
  local copies, waits for them, and re-layouts  34.2 us (12%)
  other arithmetic  19.8 us (7%)
  between operations  14.3 us (5%)
    pallas_call x10, Pallas kernels, streamed(): pl.pallas_call(kernel, grid_spec=pltpu.PrefetchScalarGridSpec(num_scalar_...  80.8 us
    ppermute x8, waiting for transfers between devices, swap_diagonal(): lax.ppermute(field, AXES, moves(away, lambda t, d, k, c: (c, d, k, t)))  25.3 us
    ppermute x8, starting transfers between devices, swap_diagonal(): lax.ppermute(field, AXES, moves(away, lambda t, d, k, c: (c, d, k, t)))  24.1 us
    unnamed x74, local copies, waits for them, and re-layouts  23.2 us
    pallas_call x1, Pallas kernels, attend_back(): pl.pallas_call(functools.partial(attend_back_kernel, reach), grid=(width...  23.1 us
    ppermute x3, waiting for transfers between devices, move_rows(): lax.ppermute(sent, 'dp', [(d, (d + step) % dps) for d in range(dps)])  14.7 us
    pallas_call x1, Pallas kernels, attend(): pl.pallas_call(functools.partial(attend_kernel, reach), grid=(width // LA...  12.7 us
    ppermute x5, waiting for transfers between devices, sum_over(): lax.ppermute(field, name, [(d, d ^ bit) for d in range(size)])  8.23 us
  transfers between devices with their start and end apart: 33, of which 15 were waited for; matrix products, arithmetic and copies ran while one was open for 10% of the time, Pallas kernels for 40%

profile of v3, /device:TPU:9, one launch (start us, length us, event | category | flops | bytes accessed | tf_op | source)
XLA Modules:
  0.0 292.8 jit_solution(16460245989459512799)
XLA Ops:
  8.0 3.1 %collective-permute-start = (bf16[512,768]{1,0:T(8,128)(2,1)}, bf16[512,768]{1,0:T(8,128)(2,1)}, u32[]{:S(2)}, u32[]{:S(2)}) collective-permute-start(bf16[512,768]{1,0:T(8,128)(2,1)} %bitcast.48), channel_id=1, source_target_pairs={{1,16},{3,18},{5,20},{7,22},{9,24},{11,26},{13,28},{15,30},{16,1},... | collective-permute-start | bytes 2359304 | tf_op jit(solution)/shard_map/ppermute | solution.py:672
  11.0 2.5 collective-permute-start.3
  16.3 2.9 %fusion.12 = (bf16[768,768]{1,0:T(8,128)(2,1)}, bf16[768,768]{1,0:T(8,128)(2,1)S(1)}) fusion(bf16[768,1536]{1,0:T(8,128)(2,1)} %refs_5_.1), kind=kLoop, calls=%fused_computation.51 | loop fusion | bytes 4718592 | tf_op jit(solution)/shard_map/dynamic_slice | solution.py:706
  19.3 1.2 fusion.11
  21.1 1.5 pad_maximum_fusion
  22.6 4.3 %shard_map.220 = (bf16[4,512,768]{2,1,0:T(8,128)(2,1)}, f32[512,768]{1,0:T(8,128)}, f32[8,768]{1,0:T(8,128)}) custom-call(f32[5]{0:T(128)} %weight_ref.3, bf16[4,512,768]{2,1,0:T(8,128)(2,1)} %bitcast.44, bf16[512,768]{1,0:T(8,128)(2,1)} %bitcast.45), custom_call_target="tpu_custom_call" | custom-call | bytes 9000000 | tf_op jit(solution)/shard_map/pallas_call | solution.py:602
  27.9 1.5 broadcast_select_fusion.1
  29.5 3.1 %fusion = (f32[1024,128]{1,0:T(8,128)}, f32[1024,128]{1,0:T(8,128)}) fusion(f32[128]{0:T(128)S(1)} %get-tuple-element.207, f32[128]{0:T(128)S(1)} %get-tuple-element.208, f32[1024]{0:T(1024)S(1)} %subtract_convert_fusion), kind=kLoop, calls=%fused_computation.12 | loop fusion | flops 262144 | bytes 1053696 | tf_op jit(solution)/shard_map/mul | solution.py:783
  34.4 1.8 maximum_select_fusion.rows_ref.refs_2_
  36.2 3.0 %collective-permute-start.4 = (bf16[896,768]{1,0:T(8,128)(2,1)S(1)}, bf16[896,768]{1,0:T(8,128)(2,1)}, u32[]{:S(2)}, u32[]{:S(2)}) collective-permute-start(bf16[896,768]{1,0:T(8,128)(2,1)S(1)} %pad_maximum_fusion.1), channel_id=1, source_target_pairs={{1,16},{3,18},{5,20},{7,22},{9,24},{11,26},{13,28},{15,30},{16,1},... | collective-permute-start | bytes 4128776 | tf_op jit(solution)/shard_map/ppermute | solution.py:672
  39.3 2.5 collective-permute-start.7
  42.4 1.3 copy-done.29
  43.7 9.4 %shard_map.221 = (bf16[3,1024,384]{2,1,0:T(8,128)(2,1)}, bf16[768,1024]{1,0:T(8,128)(2,1)}, bf16[3,768,384]{2,1,0:T(8,128)(2,1)}) custom-call(s32[8]{0:T(128)} %stack.63.flags.refs_0_, bf16[1024,768]{1,0:T(8,128)(2,1)} %maximum_select_fusion.rows_ref.refs_2_, f32[1024,128]{1,0:T(8,128)} %get-tuple-element.87.cos_ref, f32[1024,128]{1,0:T(8,128)} %get-tuple-element.88.sin_ref, ...), custom_call_target="tpu_custom_call" | custom-call | bytes 24000000 | tf_op jit(solution)/shard_map/pallas_call | solution.py:223
  53.2 12.7 %shard_map.222.mixed_ref = bf16[1024,384]{1,0:T(8,128)(2,1)} custom-call(bf16[1024,128]{1,0:T(8,128)(2,1)} %select_convert_fusion.apart_ref, bf16[1024,128]{1,0:T(8,128)(2,1)} %fusion.1.member_ref, bf16[3,1024,384]{2,1,0:T(8,128)(2,1)} %get-tuple-element.91.q_ref.k_ref.v_ref, bf16[3,1024,384]{2,1,0:T(8,128)(2,1)} %get-tuple-element.91.q_ref.k_ref.v_ref, ...), custom_call_target="tpu_custom_call" | custom-call | bytes 36000000 | tf_op jit(solution)/shard_map/pallas_call | solution.py:99
  65.9 1.6 broadcast_select_fusion
  68.5 3.1 %collective-permute-start.9 = (bf16[768,768]{1,0:T(8,128)(2,1)}, bf16[768,768]{1,0:T(8,128)(2,1)}, u32[]{:S(2)}, u32[]{:S(2)}) collective-permute-start(bf16[768,768]{1,0:T(8,128)(2,1)} %get-tuple-element.100), channel_id=1, source_target_pairs={{1,16},{3,18},{5,20},{7,22},{9,24},{11,26},{13,28},{15,30},{16,1},... | collective-permute-start | bytes 3538952 | tf_op jit(solution)/shard_map/ppermute | solution.py:672
  71.6 2.7 collective-permute-start.10
  74.4 2.3 collective-permute-done.6
  76.7 1.8 maximum_select_fusion.1.refs_5_.cot_ref
  78.5 2.7 collective-permute-done.7.refs_9_
  81.3 1.2 copy-done.5
  82.4 18.7 %shard_map.223 = (bf16[1024,768]{1,0:T(8,128)(2,1)}, bf16[768,1024]{1,0:T(8,128)(2,1)}, bf16[1024,768]{1,0:T(8,128)(2,1)}, bf16[768,1024]{1,0:T(8,128)(2,1)}, bf...) custom-call(s32[8]{0:T(128)} %stack.63.flags.refs_0_, ...), custom_call_target="tpu_custom_call" | custom-call | bytes 51000000 | tf_op jit(solution)/shard_map/pallas_call | solution.py:223
  101.1 5.4 %collective-permute-done.10.refs_8_ = bf16[768,768]{1,0:T(8,128)(2,1)} collective-permute-done((bf16[768,768]{1,0:T(8,128)(2,1)}, bf16[768,768]{1,0:T(8,128)(2,1)}, u32[]{:S(2)}, u32[]{:S(2)}) %collective-permute-start.10) | collective-permute-done | bytes 1179680 | tf_op jit(solution)/shard_map/ppermute | solution.py:672
  106.6 15.3 %shard_map.224 = (bf16[1024,768]{1,0:T(8,128)(2,1)}, bf16[1024,768]{1,0:T(8,128)(2,1)}, bf16[4,768,384]{2,1,0:T(8,128)(2,1)}, bf16[768,768]{1,0:T(8,128)(2,1)}) custom-call(s32[8]{0:T(128)} %stack.63.flags.refs_0_, bf16[1024,768]{1,0:T(8,128)(2,1)} %get-tuple-element.95.refs_1_, bf16[768,1024]{1,0:T(8,128)(2,1)} %get-tuple-element.96.refs_2_, ...), custom_call_target="tpu_custom_call" | custom-call | bytes 51000000 | tf_op jit(solution)/shard_map/pallas_call | solution.py:223
  124.2 1.9 collective-permute-done.11.late_got
  126.0 2.0 collective-permute-done.8.early_got
  128.1 11.4 %shard_map.225 = (bf16[1024,768]{1,0:T(8,128)(2,1)}, bf16[1024,384]{1,0:T(8,128)(2,1)}, bf16[768,384]{1,0:T(8,128)(2,1)}, f32[8,768]{1,0:T(8,128)}) custom-call(s32[8]{0:T(128)} %stack.63.flags.refs_0_, f32[5]{0:T(128)} %weight_ref.3, bf16[1024,768]{1,0:T(8,128)(2,1)} %maximum_select_fusion.rows_ref.refs_2_, bf16[1024,768]{1,0:T(8,128)(2,1)} %copy-done.3, ...), custom_call_target="tpu_custom_call" | custom-call | bytes 24000000 | tf_op jit(solution)/shard_map/pallas_call | solution.py:223
  139.5 23.1 %shard_map.226.grad_ref = bf16[3,1024,384]{2,1,0:T(8,128)(2,1)} custom-call(bf16[1024,128]{1,0:T(8,128)(2,1)} %select_convert_fusion.apart_ref, bf16[1024,128]{1,0:T(8,128)(2,1)} %fusion.1.member_ref, f32[1024,128]{1,0:T(8,128)} %get-tuple-element.87.cos_ref, f32[1024,128]{1,0:T(8,128)} %get-tuple-element.88.sin_ref, ...), custom_call_target="tpu_custom_call" | custom-call | bytes 66000000 | tf_op jit(solution)/shard_map/pallas_call | solution.py:175
  162.6 8.1 %shard_map.227 = (bf16[768,384]{1,0:T(8,128)(2,1)}, bf16[768,384]{1,0:T(8,128)(2,1)}, bf16[768,384]{1,0:T(8,128)(2,1)}, bf16[768,384]{1,0:T(8,128)(2,1)}) custom-call(s32[8]{0:T(128)} %stack.63.flags.refs_0_, bf16[768,1024]{1,0:T(8,128)(2,1)} %get-tuple-element.104.turned_ref, bf16[768,384]{1,0:T(8,128)(2,1)} %get-tuple-element.105.out_grad_ref, ...), custom_call_target="tpu_custom_call" | custom-call | bytes 12000000 | tf_op jit(solution)/shard_map/pallas_call | solution.py:223
  171.5 2.0 collective-permute-start.17
  173.6 2.6 collective-permute-start.15
  177.0 1.7 copy-done.2
  178.6 5.7 %shard_map.228 = (f32[512,768]{1,0:T(8,128)S(1)}, bf16[512,768]{1,0:T(8,128)(2,1)}, f32[8,768]{1,0:T(8,128)S(1)}) custom-call(s32[8]{0:T(128)S(1)} %copy-done.23, bf16[3,1024,384]{2,1,0:T(8,128)(2,1)S(1)} %copy-done.2, bf16[1024,768]{1,0:T(8,128)(2,1)S(1)} %copy-done, bf16[3,768,384]{2,1,0:T(8,128)(2,1)S(1)} %copy-done.7), custom_call_target="tpu_custom_call" | custom-call | bytes 15000000 | tf_op jit(solution)/shard_map/pallas_call | solution.py:223
  184.3 1.2 copy-done.10
  185.5 1.4 copy-done.14
  186.9 1.4 copy-done.15
  188.3 1.3 copy-done.16
  189.6 1.3 copy-done.17
  190.9 4.6 %shard_map.229 = (f32[512,768]{1,0:T(8,128)S(1)}, bf16[512,768]{1,0:T(8,128)(2,1)S(1)}, f32[8,768]{1,0:T(8,128)S(1)}) custom-call(s32[8]{0:T(128)S(1)} %copy-done.23, bf16[1024,768]{1,0:T(8,128)(2,1)S(1)} %copy-done.14, bf16[1024,768]{1,0:T(8,128)(2,1)S(1)} %copy-done.15, bf16[1024,768]{1,0:T(8,128)(2,1)S(1)} %copy-done, bf16[1024,768]{1,0:T(8,128)(2,1)S(1)} %copy-done.4, ...), custom_call_target="tpu_custom_call" | custom-call | bytes 18000000 | tf_op jit(solution)/shard_map/pallas_call | solution.py:223
  195.5 1.1 copy-done.12
  197.6 1.2 collective-permute-done.12
  199.0 3.2 %collective-permute-done.13 = f32[9,768]{1,0:T(8,128)S(1)} collective-permute-done((f32[9,768]{1,0:T(8,128)S(1)}, f32[9,768]{1,0:T(8,128)S(1)}, u32[]{:S(2)}, u32[]{:S(2)}) %collective-permute-start.13) | collective-permute-done | bytes 27680 | tf_op jit(solution)/shard_map/ppermute | solution.py:738
  202.2 2.3 collective-permute-start.14
  204.5 1.8 collective-permute-done.14
  206.4 1.2 add_convert_fusion
  207.6 2.4 pad_maximum_fusion.2
  210.0 1.9 collective-permute-start.21
  213.0 1.9 collective-permute-done.19
  215.0 1.3 collective-permute-start.20
  216.2 1.2 dynamic-slice_bitcast_fusion
  217.7 2.6 collective-permute-start.24
  220.3 2.3 collective-permute-start.23
  224.3 1.4 copy-done.9
  225.8 1.4 copy-done.11
  227.2 1.4 copy-done.13
  230.9 2.0 shard_map.230.own_ref
  232.9 4.9 %collective-permute-done.24 = bf16[192,384]{1,0:T(8,128)(2,1)S(1)} collective-permute-done((bf16[192,384]{1,0:T(8,128)(2,1)S(1)}, bf16[192,384]{1,0:T(8,128)(2,1)S(1)}, u32[]{:S(2)}, u32[]{:S(2)}) %collective-permute-start.24) | collective-permute-done | bytes 147488 | tf_op jit(solution)/shard_map/ppermute | solution.py:730
  237.8 9.8 %collective-permute-done.23 = bf16[192,384]{1,0:T(8,128)(2,1)S(1)} collective-permute-done((bf16[192,384]{1,0:T(8,128)(2,1)S(1)}, bf16[192,384]{1,0:T(8,128)(2,1)S(1)}, u32[]{:S(2)}, u32[]{:S(2)}) %collective-permute-start.23) | collective-permute-done | bytes 147488 | tf_op jit(solution)/shard_map/ppermute | solution.py:730
  248.2 4.3 %collective-permute-start.26 = (bf16[2,512,768]{2,1,0:T(8,128)(2,1)S(1)}, bf16[2,512,768]{2,1,0:T(8,128)(2,1)}, u32[]{:S(2)}, u32[]{:S(2)}) collective-permute-start(bf16[2,512,768]{2,1,0:T(8,128)(2,1)S(1)} %shard_map.230.own_ref), channel_id=1, source_target_pairs={{1,16},{3,18},{5,20},{7,22},{9,24},{11,26},{13,28},{15,30},{16,1},... | collective-permute-start | bytes 4718600 | tf_op jit(solution)/shard_map/ppermute | solution.py:672
  252.7 2.9 collective-permute-start.27
  256.7 17.2 %collective-permute-done.27 = bf16[192,768]{1,0:T(8,128)(2,1)S(1)} collective-permute-done((bf16[192,768]{1,0:T(8,128)(2,1)}, bf16[192,768]{1,0:T(8,128)(2,1)S(1)}, u32[]{:S(2)}, u32[]{:S(2)}) %collective-permute-start.27) | collective-permute-done | bytes 294944 | tf_op jit(solution)/shard_map/ppermute | solution.py:672
  274.9 3.0 %shard_map.231 = (bf16[512,768]{1,0:T(8,128)(2,1)}, bf16[512,768]{1,0:T(8,128)(2,1)}) custom-call(s32[8]{0:T(128)S(1)} %copy-done.23, f32[5]{0:T(128)S(1)} %copy-done.24, f32[512,768]{1,0:T(8,128)S(1)} %copy-done.8, bf16[2,512,768]{2,1,0:T(8,128)(2,1)S(1)} %shard_map.230.own_ref, bf16[2,512,768]{2,1,0:T(8,128)(2,1)} %collective-permute-done.26.got_ref), custom_call_target="tpu_custom_call" | custom-call | bytes 6000000 | tf_op jit(solution)/shard_map/pallas_call | solution.py:223
  278.0 3.2 %collective-permute-done.28 = bf16[192,1152]{1,0:T(8,128)(2,1)S(1)} collective-permute-done((bf16[192,1152]{1,0:T(8,128)(2,1)S(1)}, bf16[192,1152]{1,0:T(8,128)(2,1)S(1)}, u32[]{:S(2)}, u32[]{:S(2)}) %collective-permute-start.28) | collective-permute-done | bytes 442400 | tf_op jit(solution)/shard_map/ppermute | solution.py:687
  283.8 2.5 shard_map.232
  (140 shorter events, 24.8 us)
Async XLA Ops:
  7.2 200.5 %reduce-scatter.10.cloned.1.call-start = ((), (), s32[]{:S(2)}) async-start(), calls=%async_computation.4 | async-start | bytes 2949120
  7.2 20.3 %collective-permute-start.2 = (s32[1,3]{1,0:T(1,128)}, s32[1,3]{1,0:T(1,128)S(1)}, u32[]{:S(2)}, u32[]{:S(2)}) collective-permute-start(s32[1,3]{1,0:T(1,128)} %param.16), channel_id=1, source_target_pairs={{0,1},{1,0},{2,3},{3,2},{4,5},{5,4},{6,7},{7,6},{8,9},{9,8},{10,11... | collective-permute-start | bytes 44 | tf_op jit(solution)/shard_map/ppermute | solution.py:691
  8.0 20.0 %collective-permute-start = (bf16[512,768]{1,0:T(8,128)(2,1)}, bf16[512,768]{1,0:T(8,128)(2,1)}, u32[]{:S(2)}, u32[]{:S(2)}) collective-permute-start(bf16[512,768]{1,0:T(8,128)(2,1)} %bitcast.48), channel_id=1, source_target_pairs={{1,16},{3,18},{5,20},{7,22},{9,24},{11,26},{13,28},{15,30},{16,1},... | collective-permute-start | bytes 2359304 | tf_op jit(solution)/shard_map/ppermute | solution.py:672
  11.0 31.4 %collective-permute-start.3 = (bf16[3,768,384]{2,1,0:T(8,128)(2,1)}, bf16[3,768,384]{2,1,0:T(8,128)(2,1)S(1)}, u32[]{:S(2)}, u32[]{:S(2)}) collective-permute-start(bf16[3,768,384]{2,1,0:T(8,128)(2,1)} %w_own.1), channel_id=1, source_target_pairs={{1,16},{3,18},{5,20},{7,22},{9,24},{11,26},{13,28},{15,30},{16,1},... | collective-permute-start | bytes 5308424 | tf_op jit(solution)/shard_map/ppermute | solution.py:672
  16.3 2.9 %copy-start.26 = (bf16[1536,768]{1,0:T(8,128)(2,1)S(1)}, bf16[1536,768]{1,0:T(8,128)(2,1)}, u32[]{:S(2)}) copy-start(bf16[1536,768]{1,0:T(8,128)(2,1)} %refs_6_.1) | copy-start | bytes 7077892
  19.3 1.3 copy-start.28
  19.3 1.7 copy-start.31
  22.6 4.9 %copy-start.36 = (s32[1,3]{1,0:T(1,128)S(1)}, s32[1,3]{1,0:T(1,128)}, u32[]{:S(2)}) copy-start(s32[1,3]{1,0:T(1,128)} %param.16) | copy-start | bytes 40
  29.4 5.0 %collective-permute-start.1 = (bf16[512,768]{1,0:T(8,128)(2,1)S(1)}, bf16[512,768]{1,0:T(8,128)(2,1)S(1)}, u32[]{:S(2)}, u32[]{:S(2)}) collective-permute-start(bf16[512,768]{1,0:T(8,128)(2,1)S(1)} %broadcast_select_fusion.1), channel_id=1, source_target_pairs={{0,1},{1,0},{2,3},{3,2},{4,5},{5,4},{6,7},{7,6},{8,9},{9,8},{10,11... | collective-permute-start | bytes 2359304 | tf_op jit(solution)/shard_map/ppermute | solution.py:691
  36.2 29.6 %collective-permute-start.4 = (bf16[896,768]{1,0:T(8,128)(2,1)S(1)}, bf16[896,768]{1,0:T(8,128)(2,1)}, u32[]{:S(2)}, u32[]{:S(2)}) collective-permute-start(bf16[896,768]{1,0:T(8,128)(2,1)S(1)} %pad_maximum_fusion.1), channel_id=1, source_target_pairs={{1,16},{3,18},{5,20},{7,22},{9,24},{11,26},{13,28},{15,30},{16,1},... | collective-permute-start | bytes 4128776 | tf_op jit(solution)/shard_map/ppermute | solution.py:672
  39.3 41.9 %collective-permute-start.7 = (bf16[1536,768]{1,0:T(8,128)(2,1)}, bf16[1536,768]{1,0:T(8,128)(2,1)}, u32[]{:S(2)}, u32[]{:S(2)}) collective-permute-start(bf16[1536,768]{1,0:T(8,128)(2,1)} %pad_maximum_fusion), channel_id=1, source_target_pairs={{1,16},{3,18},{5,20},{7,22},{9,24},{11,26},{13,28},{15,30},{16,1},... | collective-permute-start | bytes 7077896 | tf_op jit(solution)/shard_map/ppermute | solution.py:672
  42.4 1.3 copy-start.29
  65.9 1.6 copy-start.27
  68.4 10.1 %copy-start.3 = (bf16[1024,768]{1,0:T(8,128)(2,1)}, bf16[1024,768]{1,0:T(8,128)(2,1)S(1)}, u32[]{:S(2)}) copy-start(bf16[1024,768]{1,0:T(8,128)(2,1)S(1)} %convolution_convert_fusion.refs_3_.own_ref) | copy-start | bytes 4718596
  68.4 12.8 %collective-permute-start.5 = (bf16[1024,768]{1,0:T(8,128)(2,1)S(1)}, bf16[1024,768]{1,0:T(8,128)(2,1)S(1)}, u32[]{:S(2)}, u32[]{:S(2)}) collective-permute-start(bf16[1024,768]{1,0:T(8,128)(2,1)S(1)} %convolution_convert_fusion.refs_3_.own_ref), channel_id=1, source_target_pairs={{0,1},{1,0},{2,3},{3,2},{4,5},{5,4},{6,7},{7,6},{8,9},{9,8},{10,11... | collective-permute-start | bytes 4718600 | tf_op jit(solution)/shard_map/ppermute | solution.py:691
  68.5 32.6 %collective-permute-start.9 = (bf16[768,768]{1,0:T(8,128)(2,1)}, bf16[768,768]{1,0:T(8,128)(2,1)}, u32[]{:S(2)}, u32[]{:S(2)}) collective-permute-start(bf16[768,768]{1,0:T(8,128)(2,1)} %get-tuple-element.100), channel_id=1, source_target_pairs={{1,16},{3,18},{5,20},{7,22},{9,24},{11,26},{13,28},{15,30},{16,1},... | collective-permute-start | bytes 3538952 | tf_op jit(solution)/shard_map/ppermute | solution.py:672
  71.6 34.9 %collective-permute-start.10 = (bf16[768,768]{1,0:T(8,128)(2,1)}, bf16[768,768]{1,0:T(8,128)(2,1)}, u32[]{:S(2)}, u32[]{:S(2)}) collective-permute-start(bf16[768,768]{1,0:T(8,128)(2,1)} %get-tuple-element.101), channel_id=1, source_target_pairs={{1,16},{3,18},{5,20},{7,22},{9,24},{11,26},{13,28},{15,30},{16,1},... | collective-permute-start | bytes 3538952 | tf_op jit(solution)/shard_map/ppermute | solution.py:672
  74.3 2.4 collective-permute-start.6
  81.3 1.2 copy-start.5
  106.6 101.1 %reduce-scatter.12.cloned.1.call-start = ((), (), s32[]{:S(2)}) async-start(), calls=%async_computation.5 | async-start | bytes 2949120
  121.9 1.4 copy-start.30
  121.9 130.7 %reduce-scatter.8.cloned.1.call-start = ((), (), s32[]{:S(2)}) async-start(), calls=%async_computation.3 | async-start | bytes 1474560 | tf_op jit(solution)/shard_map/reduce_scatter | solution.py:718
  122.2 3.8 %collective-permute-start.11 = (bf16[1024,768]{1,0:T(8,128)(2,1)}, bf16[1024,768]{1,0:T(8,128)(2,1)}, u32[]{:S(2)}, u32[]{:S(2)}) collective-permute-start(bf16[1024,768]{1,0:T(8,128)(2,1)} %get-tuple-element.102.late_own), channel_id=1, source_target_pairs={{0,1},{1,0},{2,3},{3,2},{4,5},{5,4},{6,7},{7,6},{8,9},{9,8},{10,11... | collective-permute-start | bytes 4718600 | tf_op jit(solution)/shard_map/ppermute | solution.py:691
  123.3 4.8 %collective-permute-start.8 = (bf16[1024,768]{1,0:T(8,128)(2,1)S(1)}, bf16[1024,768]{1,0:T(8,128)(2,1)}, u32[]{:S(2)}, u32[]{:S(2)}) collective-permute-start(bf16[1024,768]{1,0:T(8,128)(2,1)S(1)} %copy-done.30), channel_id=1, source_target_pairs={{0,1},{1,0},{2,3},{3,2},{4,5},{5,4},{6,7},{7,6},{8,9},{9,8},{10,11... | collective-permute-start | bytes 4718600 | tf_op jit(solution)/shard_map/ppermute | solution.py:691
  162.6 13.6 %copy-start.35 = (f32[8,768]{1,0:T(8,128)S(1)}, f32[8,768]{1,0:T(8,128)}, u32[]{:S(2)}) copy-start(f32[8,768]{1,0:T(8,128)} %get-tuple-element.118) | copy-start | bytes 73732
  162.6 14.4 %copy-start = (bf16[1024,768]{1,0:T(8,128)(2,1)S(1)}, bf16[1024,768]{1,0:T(8,128)(2,1)}, u32[]{:S(2)}) copy-start(bf16[1024,768]{1,0:T(8,128)(2,1)} %maximum_select_fusion.rows_ref.refs_2_) | copy-start | bytes 4718596
  162.6 14.4 %copy-start.7 = (bf16[3,768,384]{2,1,0:T(8,128)(2,1)S(1)}, bf16[3,768,384]{2,1,0:T(8,128)(2,1)}, u32[]{:S(2)}) copy-start(bf16[3,768,384]{2,1,0:T(8,128)(2,1)} %get-tuple-element.108.weight) | copy-start | bytes 5308420
  162.6 14.4 %copy-start.23 = (s32[8]{0:T(128)S(1)}, s32[8]{0:T(128)}, u32[]{:S(2)}) copy-start(s32[8]{0:T(128)} %stack.63.flags.refs_0_) | copy-start | bytes 100
  170.7 35.7 %collective-permute-start.16 = (bf16[768,384]{1,0:T(8,128)(2,1)}, bf16[768,384]{1,0:T(8,128)(2,1)S(1)}, u32[]{:S(2)}, u32[]{:S(2)}) collective-permute-start(bf16[768,384]{1,0:T(8,128)(2,1)} %get-tuple-element.122), channel_id=1, source_target_pairs={{0,1},{1,17},{2,3},{3,19},{4,5},{5,21},{6,7},{7,23},{8,9},{9,25},{... | collective-permute-start | bytes 1769480 | tf_op jit(solution)/shard_map/ppermute | solution.py:676
  171.5 34.9 %collective-permute-start.17 = (bf16[768,384]{1,0:T(8,128)(2,1)}, bf16[768,384]{1,0:T(8,128)(2,1)S(1)}, u32[]{:S(2)}, u32[]{:S(2)}) collective-permute-start(bf16[768,384]{1,0:T(8,128)(2,1)} %get-tuple-element.123), channel_id=1, source_target_pairs={{0,2},{1,18},{2,0},{3,16},{4,6},{5,22},{6,4},{7,20},{8,10},{9,26},... | collective-permute-start | bytes 1769480 | tf_op jit(solution)/shard_map/ppermute | solution.py:676
  173.6 32.9 %collective-permute-start.18 = (bf16[768,384]{1,0:T(8,128)(2,1)}, bf16[768,384]{1,0:T(8,128)(2,1)S(1)}, u32[]{:S(2)}, u32[]{:S(2)}) collective-permute-start(bf16[768,384]{1,0:T(8,128)(2,1)} %get-tuple-element.124), channel_id=1, source_target_pairs={{0,3},{1,19},{2,1},{3,17},{4,7},{5,23},{6,5},{7,21},{8,11},{9,27},... | collective-permute-start | bytes 1769480 | tf_op jit(solution)/shard_map/ppermute | solution.py:676
  173.6 32.9 %collective-permute-start.15 = (bf16[768,384]{1,0:T(8,128)(2,1)}, bf16[768,384]{1,0:T(8,128)(2,1)S(1)}, u32[]{:S(2)}, u32[]{:S(2)}) collective-permute-start(bf16[768,384]{1,0:T(8,128)(2,1)} %get-tuple-element.106), channel_id=1, source_target_pairs={{1,16},{3,18},{5,20},{7,22},{9,24},{11,26},{13,28},{15,30},{16,1},... | collective-permute-start | bytes 1769480 | tf_op jit(solution)/shard_map/ppermute | solution.py:676
  177.0 1.7 copy-start.2
  178.6 6.9 %copy-start.1 = (bf16[1024,768]{1,0:T(8,128)(2,1)S(1)}, bf16[1024,768]{1,0:T(8,128)(2,1)}, u32[]{:S(2)}) copy-start(bf16[1024,768]{1,0:T(8,128)(2,1)} %maximum_select_fusion.1.refs_5_.cot_ref) | copy-start | bytes 4718596
  178.6 6.9 %copy-start.4 = (bf16[1024,768]{1,0:T(8,128)(2,1)S(1)}, bf16[1024,768]{1,0:T(8,128)(2,1)}, u32[]{:S(2)}) copy-start(bf16[1024,768]{1,0:T(8,128)(2,1)} %copy-done.3) | copy-start | bytes 4718596
  178.6 6.9 %copy-start.6 = (bf16[1024,768]{1,0:T(8,128)(2,1)S(1)}, bf16[1024,768]{1,0:T(8,128)(2,1)}, u32[]{:S(2)}) copy-start(bf16[1024,768]{1,0:T(8,128)(2,1)} %copy-done.5) | copy-start | bytes 4718596
  184.3 1.2 copy-start.10
  185.5 1.4 copy-start.14
  186.9 1.4 copy-start.15
  188.3 1.3 copy-start.16
  189.6 1.3 copy-start.17
  190.9 15.5 %copy-start.32 = (bf16[768,384]{1,0:T(8,128)(2,1)S(1)}, bf16[768,384]{1,0:T(8,128)(2,1)}, u32[]{:S(2)}) copy-start(bf16[768,384]{1,0:T(8,128)(2,1)} %get-tuple-element.106) | copy-start | bytes 1769476
  195.5 1.1 copy-start.12
  197.6 1.3 collective-permute-start.12
  198.9 3.3 %collective-permute-start.13 = (f32[9,768]{1,0:T(8,128)S(1)}, f32[9,768]{1,0:T(8,128)S(1)}, u32[]{:S(2)}, u32[]{:S(2)}) collective-permute-start(f32[9,768]{1,0:T(8,128)S(1)} %fusion.8), channel_id=1, source_target_pairs={{0,4},{4,0},{8,12},{12,8},{1,5},{5,1},{9,13},{13,9},{2,6},{6,2},{1... | collective-permute-start | bytes 82952 | tf_op jit(solution)/shard_map/ppermute | solution.py:738
  202.2 4.2 %collective-permute-start.14 = (f32[9,768]{1,0:T(8,128)S(1)}, f32[9,768]{1,0:T(8,128)S(1)}, u32[]{:S(2)}, u32[]{:S(2)}) collective-permute-start(f32[9,768]{1,0:T(8,128)S(1)} %add.98), channel_id=1, source_target_pairs={{0,8},{4,12},{8,0},{12,4},{1,9},{5,13},{9,1},{13,5},{2,10},{6,14},... | collective-permute-start | bytes 82952 | tf_op jit(solution)/shard_map/ppermute | solution.py:738
  210.0 14.3 %copy-start.22 = (f32[4,768]{1,0:T(4,128)S(1)}, f32[4,768]{1,0:T(4,128)}, u32[]{:S(2)}) copy-start(f32[4,768]{1,0:T(4,128)} %pad_maximum_fusion.6.vectors.refs_6_) | copy-start | bytes 36868
  210.0 12.5 %collective-permute-start.21 = (bf16[512,768]{1,0:T(8,128)(2,1)}, bf16[512,768]{1,0:T(8,128)(2,1)S(1)}, u32[]{:S(2)}, u32[]{:S(2)}) collective-permute-start(bf16[512,768]{1,0:T(8,128)(2,1)} %get-tuple-element.128), channel_id=1, source_target_pairs={{0,1},{1,0},{2,3},{3,2},{4,5},{5,4},{6,7},{7,6},{8,9},{9,8},{10,11... | collective-permute-start | bytes 2359304 | tf_op jit(solution)/shard_map/ppermute | solution.py:691
  212.0 11.5 %collective-permute-start.22 = (bf16[512,768]{1,0:T(8,128)(2,1)}, bf16[512,768]{1,0:T(8,128)(2,1)S(1)}, u32[]{:S(2)}, u32[]{:S(2)}) collective-permute-start(bf16[512,768]{1,0:T(8,128)(2,1)} %copy-done.25), channel_id=1, source_target_pairs={{0,1},{1,0},{2,3},{3,2},{4,5},{5,4},{6,7},{7,6},{8,9},{9,8},{10,11... | collective-permute-start | bytes 2359304 | tf_op jit(solution)/shard_map/ppermute | solution.py:691
  212.0 2.9 %collective-permute-start.19 = (f32[9,768]{1,0:T(8,128)S(1)}, f32[9,768]{1,0:T(8,128)S(1)}, u32[]{:S(2)}, u32[]{:S(2)}) collective-permute-start(f32[9,768]{1,0:T(8,128)S(1)} %add.99), channel_id=1, source_target_pairs={{0,16},{16,0},{1,17},{17,1},{2,18},{18,2},{3,19},{19,3},{4,20},{20... | collective-permute-start | bytes 82952 | tf_op jit(solution)/shard_map/ppermute | solution.py:738
  215.0 5.3 %collective-permute-start.20 = (f32[9,768]{1,0:T(8,128)S(1)}, f32[9,768]{1,0:T(8,128)S(1)}, u32[]{:S(2)}, u32[]{:S(2)}) collective-permute-start(f32[9,768]{1,0:T(8,128)S(1)} %add.100), channel_id=1, source_target_pairs={{0,2},{2,0},{1,3},{3,1},{4,6},{6,4},{5,7},{7,5},{8,10},{10,8},{9,1... | collective-permute-start | bytes 82952 | tf_op jit(solution)/shard_map/ppermute | solution.py:738
  217.4 15.5 %collective-permute-start.25 = (bf16[192,384]{1,0:T(8,128)(2,1)S(1)}, bf16[192,384]{1,0:T(8,128)(2,1)S(1)}, u32[]{:S(2)}, u32[]{:S(2)}) collective-permute-start(bf16[192,384]{1,0:T(8,128)(2,1)S(1)} %get-tuple-element.198), channel_id=1, source_target_pairs={{0,12},{4,0},{8,4},{12,8},{1,13},{5,1},{9,5},{13,9},{2,14},{6,2},{... | collective-permute-start | bytes 442376 | tf_op jit(solution)/shard_map/ppermute | solution.py:730
  217.7 20.1 %collective-permute-start.24 = (bf16[192,384]{1,0:T(8,128)(2,1)S(1)}, bf16[192,384]{1,0:T(8,128)(2,1)S(1)}, u32[]{:S(2)}, u32[]{:S(2)}) collective-permute-start(bf16[192,384]{1,0:T(8,128)(2,1)S(1)} %get-tuple-element.199), channel_id=1, source_target_pairs={{0,8},{4,12},{8,0},{12,4},{1,9},{5,13},{9,1},{13,5},{2,10},{6,14},... | collective-permute-start | bytes 442376 | tf_op jit(solution)/shard_map/ppermute | solution.py:730
  220.3 27.3 %collective-permute-start.23 = (bf16[192,384]{1,0:T(8,128)(2,1)S(1)}, bf16[192,384]{1,0:T(8,128)(2,1)S(1)}, u32[]{:S(2)}, u32[]{:S(2)}) collective-permute-start(bf16[192,384]{1,0:T(8,128)(2,1)S(1)} %get-tuple-element.200), channel_id=1, source_target_pairs={{0,4},{4,8},{8,12},{12,0},{1,5},{5,9},{9,13},{13,1},{2,6},{6,10},{... | collective-permute-start | bytes 442376 | tf_op jit(solution)/shard_map/ppermute | solution.py:730
  224.3 1.4 copy-start.9
  225.8 1.4 copy-start.11
  227.2 1.4 copy-start.13
  232.9 42.0 %copy-start.8 = (f32[512,768]{1,0:T(8,128)S(1)}, f32[512,768]{1,0:T(8,128)}, u32[]{:S(2)}) copy-start(f32[512,768]{1,0:T(8,128)} %get-tuple-element.84.part_ref) | copy-start | bytes 4718596
  232.9 42.0 %copy-start.24 = (f32[5]{0:T(128)S(1)}, f32[5]{0:T(128)}, u32[]{:S(2)}) copy-start(f32[5]{0:T(128)} %weight_ref.3) | copy-start | bytes 64
  237.8 9.8 %copy-start.33 = (bf16[192,384]{1,0:T(8,128)(2,1)}, bf16[192,384]{1,0:T(8,128)(2,1)S(1)}, u32[]{:S(2)}) copy-start(bf16[192,384]{1,0:T(8,128)(2,1)S(1)} %collective-permute-done.24) | copy-start | bytes 442372
  248.2 26.7 %collective-permute-start.26 = (bf16[2,512,768]{2,1,0:T(8,128)(2,1)S(1)}, bf16[2,512,768]{2,1,0:T(8,128)(2,1)}, u32[]{:S(2)}, u32[]{:S(2)}) collective-permute-start(bf16[2,512,768]{2,1,0:T(8,128)(2,1)S(1)} %shard_map.230.own_ref), channel_id=1, source_target_pairs={{1,16},{3,18},{5,20},{7,22},{9,24},{11,26},{13,28},{15,30},{16,1},... | collective-permute-start | bytes 4718600 | tf_op jit(solution)/shard_map/ppermute | solution.py:672
  252.7 21.1 %collective-permute-start.27 = (bf16[192,768]{1,0:T(8,128)(2,1)}, bf16[192,768]{1,0:T(8,128)(2,1)S(1)}, u32[]{:S(2)}, u32[]{:S(2)}) collective-permute-start(bf16[192,768]{1,0:T(8,128)(2,1)} %reduce-scatter.8.cloned.1.call-done), channel_id=1, source_target_pairs={{1,16},{3,18},{5,20},{7,22},{9,24},{11,26},{13,28},{15,30},{16,1},... | collective-permute-start | bytes 884744 | tf_op jit(solution)/shard_map/ppermute | solution.py:672
  273.9 7.2 %collective-permute-start.28 = (bf16[192,1152]{1,0:T(8,128)(2,1)S(1)}, bf16[192,1152]{1,0:T(8,128)(2,1)S(1)}, u32[]{:S(2)}, u32[]{:S(2)}) collective-permute-start(bf16[192,1152]{1,0:T(8,128)(2,1)S(1)} %get-tuple-element.203), channel_id=1, source_target_pairs={{0,2},{2,0},{1,3},{3,1},{4,6},{6,4},{5,7},{7,5},{8,10},{10,8},{9,1... | collective-permute-start | bytes 1327112 | tf_op jit(solution)/shard_map/ppermute | solution.py:687
  281.3 2.5 collective-permute-start.29
  (6 other events, 5.6 us)
Sparse Core Ops, SparseCore 0:
  106.7 37.8 reduce-scatter.9
  147.7 44.2 reduce-scatter.11
  210.1 42.4 reduce-scatter.7

commit v4 on v3

--- a/solution.py
+++ b/solution.py
@@ -819,29 +819,29 @@
     block_keep, block_send, sums_now = lower(
         flags, act_early, act_late, down_early, down_late, layer_rows, attn, attn_got, after(cot_rows, send)
     )
-    small = jnp.concatenate([sums_one[:2], sums_two[:2], sums_now[:1], sums_past[:hist_count]], axis=0)
-    for name in ("near", "dp"):
-        small = sum_over(small, name)
-    small, keep, send, block_keep, block_send, *moved = lax.optimization_barrier(
-        (small, keep, send, block_keep, block_send, *moved)
+    early_sum = scatter_rows(after(early_sum, owned[0]))
+    keep, send, block_keep, block_send, *moved = lax.optimization_barrier(
+        (keep, send, block_keep, block_send, *moved)
     )
     attn_one = add(jnp.where(same, owned[0], moved[0]), *moved[1:])
     attn_moved = move_rows(attn_one)
-    feed_sum = scatter_rows(jnp.concatenate([after(early_sum, attn_one), late_sum], axis=1))
+    late_sum = scatter_rows(after(late_sum, attn_one))
     ours = last(
         flags, layer_rows, grad_attn, keep, swap_near(send), block_keep, swap_near(block_send), vectors
     )
-    for name in ("tp", "far"):
+    small = jnp.concatenate([sums_one[:2], sums_two[:2], sums_now[:1], sums_past[:hist_count]], axis=0)
+    small = after(small, attn_one)
+    for name in ("near", "tp", "far"):
         small = sum_over(small, name)
     small, ours, *attn_moved = lax.optimization_barrier((small, ours, *attn_moved))
-    theirs = swap_diagonal(ours)
-    feed_sum = after(feed_sum, small)
+    feed_sum = jnp.concatenate([after(early_sum, small), late_sum], axis=1)
     feed_got = swap_diagonal(feed_sum)
+    theirs = swap_diagonal(after(ours, feed_got))
+    small = sum_over(small, "dp")
     attn_sum = add(*attn_moved)
     blocks = jnp.concatenate([attn_sum, jnp.where(same, feed_sum, feed_got)], axis=1)
     here = jnp.stack([blocks, swap_far(blocks)])
     output, grad_input = present(flags, dwa_weights, past_sum, ours, theirs)
-    here = after(here, output)
     grad_w_qkv, grad_w_out, grad_w_up, grad_w_down = place(flags, here, swap_near(here))
 
     return (

time: 296 us -> 285 us (0.963)
  waiting for transfers between devices: 58.9 us -> 53.2 us
  other arithmetic: 19.8 us -> 14.6 us
    ppermute x4, waiting for transfers between devices: 0.01 us -> 9.64 us  [send_to_owner(): lax.ppermute(field, AXES, moves(away if not other_far and (not other_tp)...]
    ppermute x8, waiting for transfers between devices: 25.3 us -> 18.1 us  [swap_diagonal(): lax.ppermute(field, AXES, moves(away, lambda t, d, k, c: (c, d, k, t)))]
    ppermute x3, waiting for transfers between devices: 14.7 us -> 7.84 us  [move_rows(): lax.ppermute(sent, 'dp', [(d, (d + step) % dps) for d in range(dps)])]
    unnamed x74 -> x79, local copies, waits for them, and re-layouts: 23.2 us -> 23 us
  transfers between devices with their start and end apart: 33 -> 34, of which waited for: 15 -> 15; matrix products, arithmetic and copies ran while one was open for 10% -> 10% of each run, Pallas kernels for 40% -> 42%
where the time goes in v4:
time: 285 us; the launch traced here: 283 us
  Pallas kernels  120 us (42%)
  waiting for transfers between devices  53.2 us (19%)
  starting transfers between devices  43.5 us (15%)
  local copies, waits for them, and re-layouts  36 us (13%)
  other arithmetic  14.6 us (5%)
  between operations  14.3 us (5%)
    pallas_call x10, Pallas kernels, streamed(): pl.pallas_call(kernel, grid_spec=pltpu.PrefetchScalarGridSpec(num_scalar_...  79.7 us
    ppermute x8, starting transfers between devices, swap_diagonal(): lax.ppermute(field, AXES, moves(away, lambda t, d, k, c: (c, d, k, t)))  24.2 us
    pallas_call x1, Pallas kernels, attend_back(): pl.pallas_call(functools.partial(attend_back_kernel, reach), grid=(width...  23.1 us
    unnamed x79, local copies, waits for them, and re-layouts  23 us
    ppermute x8, waiting for transfers between devices, swap_diagonal(): lax.ppermute(field, AXES, moves(away, lambda t, d, k, c: (c, d, k, t)))  18.1 us
    pallas_call x1, Pallas kernels, attend(): pl.pallas_call(functools.partial(attend_kernel, reach), grid=(width // LA...  12.7 us
    ppermute x4, waiting for transfers between devices, send_to_owner(): lax.ppermute(field, AXES, moves(away if not other_far and (not other_tp)...  9.64 us
    ppermute x3, waiting for transfers between devices, move_rows(): lax.ppermute(sent, 'dp', [(d, (d + step) % dps) for d in range(dps)])  7.84 us
  transfers between devices with their start and end apart: 34, of which 15 were waited for; matrix products, arithmetic and copies ran while one was open for 10% of the time, Pallas kernels for 42%

profile of v4, /device:TPU:9, one launch (start us, length us, event | category | flops | bytes accessed | tf_op | source)
XLA Modules:
  0.0 282.5 jit_solution(9826396753894960120)
XLA Ops:
  8.0 3.1 %collective-permute-start = (bf16[512,768]{1,0:T(8,128)(2,1)}, bf16[512,768]{1,0:T(8,128)(2,1)S(1)}, u32[]{:S(2)}, u32[]{:S(2)}) collective-permute-start(bf16[512,768]{1,0:T(8,128)(2,1)} %bitcast.48), channel_id=1, source_target_pairs={{1,16},{3,18},{5,20},{7,22},{9,24},{11,26},{13,28},{15,30},{16,1},... | collective-permute-start | bytes 2359304 | tf_op jit(solution)/shard_map/ppermute | solution.py:672
  11.0 2.5 collective-permute-start.3
  16.3 2.9 %fusion.11 = (bf16[768,768]{1,0:T(8,128)(2,1)}, bf16[768,768]{1,0:T(8,128)(2,1)S(1)}) fusion(bf16[768,1536]{1,0:T(8,128)(2,1)} %refs_5_.1), kind=kLoop, calls=%fused_computation.51 | loop fusion | bytes 4718592 | tf_op jit(solution)/shard_map/dynamic_slice | solution.py:706
  19.3 1.2 fusion.10
  21.1 1.5 pad_maximum_fusion
  22.6 4.4 %shard_map.220 = (bf16[4,512,768]{2,1,0:T(8,128)(2,1)}, f32[512,768]{1,0:T(8,128)}, f32[8,768]{1,0:T(8,128)}) custom-call(f32[5]{0:T(128)} %weight_ref.3, bf16[4,512,768]{2,1,0:T(8,128)(2,1)} %bitcast.44, bf16[512,768]{1,0:T(8,128)(2,1)} %bitcast.45), custom_call_target="tpu_custom_call" | custom-call | bytes 9000000 | tf_op jit(solution)/shard_map/pallas_call | solution.py:602
  28.2 3.1 %fusion = (f32[1024,128]{1,0:T(8,128)}, f32[1024,128]{1,0:T(8,128)}) fusion(f32[128]{0:T(128)S(1)} %get-tuple-element.209, f32[128]{0:T(128)S(1)} %get-tuple-element.210, f32[1024]{0:T(1024)S(1)} %subtract_convert_fusion), kind=kLoop, calls=%fused_computation.11 | loop fusion | flops 262144 | bytes 1053696 | tf_op jit(solution)/shard_map/mul | solution.py:783
  33.2 1.8 maximum_select_fusion.rows_ref.refs_2_
  35.0 3.0 %collective-permute-start.4 = (bf16[896,768]{1,0:T(8,128)(2,1)S(1)}, bf16[896,768]{1,0:T(8,128)(2,1)S(1)}, u32[]{:S(2)}, u32[]{:S(2)}) collective-permute-start(bf16[896,768]{1,0:T(8,128)(2,1)S(1)} %pad_maximum_fusion.1), channel_id=1, source_target_pairs={{1,16},{3,18},{5,20},{7,22},{9,24},{11,26},{13,28},{15,30},{16,1},... | collective-permute-start | bytes 4128776 | tf_op jit(solution)/shard_map/ppermute | solution.py:672
  38.1 2.5 collective-permute-start.7
  41.3 9.4 %shard_map.221 = (bf16[3,1024,384]{2,1,0:T(8,128)(2,1)}, bf16[768,1024]{1,0:T(8,128)(2,1)}, bf16[3,768,384]{2,1,0:T(8,128)(2,1)}) custom-call(s32[8]{0:T(128)} %stack.63.flags.refs_0_, bf16[1024,768]{1,0:T(8,128)(2,1)} %maximum_select_fusion.rows_ref.refs_2_, f32[1024,128]{1,0:T(8,128)} %get-tuple-element.88.cos_ref, f32[1024,128]{1,0:T(8,128)} %get-tuple-element.89.sin_ref, ...), custom_call_target="tpu_custom_call" | custom-call | bytes 24000000 | tf_op jit(solution)/shard_map/pallas_call | solution.py:223
  50.7 12.7 %shard_map.222.mixed_ref = bf16[1024,384]{1,0:T(8,128)(2,1)} custom-call(bf16[1024,128]{1,0:T(8,128)(2,1)} %select_convert_fusion.apart_ref, bf16[1024,128]{1,0:T(8,128)(2,1)} %fusion.1.member_ref, bf16[3,1024,384]{2,1,0:T(8,128)(2,1)} %get-tuple-element.92.q_ref.k_ref.v_ref, bf16[3,1024,384]{2,1,0:T(8,128)(2,1)} %get-tuple-element.92.q_ref.k_ref.v_ref, ...), custom_call_target="tpu_custom_call" | custom-call | bytes 36000000 | tf_op jit(solution)/shard_map/pallas_call | solution.py:99
  65.6 3.1 %collective-permute-start.9 = (bf16[768,768]{1,0:T(8,128)(2,1)}, bf16[768,768]{1,0:T(8,128)(2,1)}, u32[]{:S(2)}, u32[]{:S(2)}) collective-permute-start(bf16[768,768]{1,0:T(8,128)(2,1)} %get-tuple-element.101), channel_id=1, source_target_pairs={{1,16},{3,18},{5,20},{7,22},{9,24},{11,26},{13,28},{15,30},{16,1},... | collective-permute-start | bytes 3538952 | tf_op jit(solution)/shard_map/ppermute | solution.py:672
  68.6 2.7 collective-permute-start.10
  71.5 2.3 collective-permute-done.6
  73.8 1.8 maximum_select_fusion.1.refs_5_.cot_ref
  75.6 5.0 %collective-permute-done.7.refs_9_ = bf16[1536,768]{1,0:T(8,128)(2,1)} collective-permute-done((bf16[1536,768]{1,0:T(8,128)(2,1)}, bf16[1536,768]{1,0:T(8,128)(2,1)}, u32[]{:S(2)}, u32[]{:S(2)}) %collective-permute-start.7) | collective-permute-done | bytes 2359328 | tf_op jit(solution)/shard_map/ppermute | solution.py:672
  80.6 1.1 copy-done.5
  81.7 18.7 %shard_map.223 = (bf16[1024,768]{1,0:T(8,128)(2,1)}, bf16[768,1024]{1,0:T(8,128)(2,1)}, bf16[1024,768]{1,0:T(8,128)(2,1)}, bf16[768,1024]{1,0:T(8,128)(2,1)}, bf...) custom-call(s32[8]{0:T(128)} %stack.63.flags.refs_0_, ...), custom_call_target="tpu_custom_call" | custom-call | bytes 51000000 | tf_op jit(solution)/shard_map/pallas_call | solution.py:223
  100.4 5.4 %collective-permute-done.10.refs_8_ = bf16[768,768]{1,0:T(8,128)(2,1)} collective-permute-done((bf16[768,768]{1,0:T(8,128)(2,1)}, bf16[768,768]{1,0:T(8,128)(2,1)}, u32[]{:S(2)}, u32[]{:S(2)}) %collective-permute-start.10) | collective-permute-done | bytes 1179680 | tf_op jit(solution)/shard_map/ppermute | solution.py:672
  105.9 15.3 %shard_map.224 = (bf16[1024,768]{1,0:T(8,128)(2,1)}, bf16[1024,768]{1,0:T(8,128)(2,1)}, bf16[4,768,384]{2,1,0:T(8,128)(2,1)}, bf16[768,768]{1,0:T(8,128)(2,1)}) custom-call(s32[8]{0:T(128)} %stack.63.flags.refs_0_, bf16[1024,768]{1,0:T(8,128)(2,1)} %get-tuple-element.96.refs_1_, bf16[768,1024]{1,0:T(8,128)(2,1)} %get-tuple-element.97.refs_2_, ...), custom_call_target="tpu_custom_call" | custom-call | bytes 51000000 | tf_op jit(solution)/shard_map/pallas_call | solution.py:223
  122.6 1.9 slice.48.w_ref
  125.2 2.2 collective-permute-done.8.early_got
  127.4 11.4 %shard_map.225 = (bf16[1024,768]{1,0:T(8,128)(2,1)}, bf16[1024,384]{1,0:T(8,128)(2,1)}, bf16[768,384]{1,0:T(8,128)(2,1)}, f32[8,768]{1,0:T(8,128)}) custom-call(s32[8]{0:T(128)} %stack.63.flags.refs_0_, f32[5]{0:T(128)} %weight_ref.3, bf16[1024,768]{1,0:T(8,128)(2,1)} %maximum_select_fusion.rows_ref.refs_2_, bf16[1024,768]{1,0:T(8,128)(2,1)} %copy-done.3, ...), custom_call_target="tpu_custom_call" | custom-call | bytes 24000000 | tf_op jit(solution)/shard_map/pallas_call | solution.py:223
  138.8 23.1 %shard_map.226.grad_ref = bf16[3,1024,384]{2,1,0:T(8,128)(2,1)} custom-call(bf16[1024,128]{1,0:T(8,128)(2,1)} %select_convert_fusion.apart_ref, bf16[1024,128]{1,0:T(8,128)(2,1)} %fusion.1.member_ref, f32[1024,128]{1,0:T(8,128)} %get-tuple-element.88.cos_ref, f32[1024,128]{1,0:T(8,128)} %get-tuple-element.89.sin_ref, ...), custom_call_target="tpu_custom_call" | custom-call | bytes 66000000 | tf_op jit(solution)/shard_map/pallas_call | solution.py:175
  161.9 8.1 %shard_map.227 = (bf16[768,384]{1,0:T(8,128)(2,1)}, bf16[768,384]{1,0:T(8,128)(2,1)}, bf16[768,384]{1,0:T(8,128)(2,1)}, bf16[768,384]{1,0:T(8,128)(2,1)}) custom-call(s32[8]{0:T(128)} %stack.63.flags.refs_0_, bf16[768,1024]{1,0:T(8,128)(2,1)} %get-tuple-element.105.turned_ref, bf16[768,384]{1,0:T(8,128)(2,1)} %get-tuple-element.106.out_grad_ref, ...), custom_call_target="tpu_custom_call" | custom-call | bytes 12000000 | tf_op jit(solution)/shard_map/pallas_call | solution.py:223
  171.0 2.0 collective-permute-start.14
  173.0 2.6 collective-permute-start.12
  175.6 1.7 copy-done.2
  177.3 5.7 %shard_map.228 = (f32[512,768]{1,0:T(8,128)S(1)}, bf16[512,768]{1,0:T(8,128)(2,1)}, f32[8,768]{1,0:T(8,128)S(1)}) custom-call(s32[8]{0:T(128)S(1)} %copy-done.23, bf16[3,1024,384]{2,1,0:T(8,128)(2,1)S(1)} %copy-done.2, bf16[1024,768]{1,0:T(8,128)(2,1)S(1)} %copy-done, bf16[3,768,384]{2,1,0:T(8,128)(2,1)S(1)} %copy-done.7), custom_call_target="tpu_custom_call" | custom-call | bytes 15000000 | tf_op jit(solution)/shard_map/pallas_call | solution.py:223
  183.0 1.1 copy-done.10
  184.1 1.4 copy-done.14
  185.6 1.4 copy-done.15
  187.0 1.3 copy-done.16
  188.3 1.3 copy-done.17
  189.5 4.5 %shard_map.229 = (f32[512,768]{1,0:T(8,128)S(1)}, bf16[512,768]{1,0:T(8,128)(2,1)S(1)}, f32[8,768]{1,0:T(8,128)S(1)}) custom-call(s32[8]{0:T(128)S(1)} %copy-done.23, bf16[1024,768]{1,0:T(8,128)(2,1)S(1)} %copy-done.14, bf16[1024,768]{1,0:T(8,128)(2,1)S(1)} %copy-done.15, bf16[1024,768]{1,0:T(8,128)(2,1)S(1)} %copy-done, bf16[1024,768]{1,0:T(8,128)(2,1)S(1)} %copy-done.4, ...), custom_call_target="tpu_custom_call" | custom-call | bytes 18000000 | tf_op jit(solution)/shard_map/pallas_call | solution.py:223
  194.1 1.2 copy-done.12
  195.3 9.6 %collective-permute-done.15 = bf16[768,384]{1,0:T(8,128)(2,1)S(1)} collective-permute-done((bf16[768,384]{1,0:T(8,128)(2,1)}, bf16[768,384]{1,0:T(8,128)(2,1)S(1)}, u32[]{:S(2)}, u32[]{:S(2)}) %collective-permute-start.15) | collective-permute-done | bytes 589856 | tf_op jit(solution)/shard_map/ppermute | solution.py:676
  204.9 1.2 add_convert_fusion
  206.2 1.3 collective-permute-start.19
  208.9 1.8 collective-permute-done.16
  211.4 2.2 collective-permute-done.17
  213.6 1.2 collective-permute-start.18
  214.8 1.2 dynamic-slice_bitcast_fusion
  216.6 1.9 collective-permute-start.22
  218.5 2.2 collective-permute-start.21
  222.5 1.4 copy-done.9
  223.9 1.4 copy-done.11
  225.3 1.4 copy-done.13
  226.7 1.1 copy-done.19
  229.0 2.0 shard_map.230.own_ref
  231.1 7.8 %collective-permute-done.21 = bf16[192,384]{1,0:T(8,128)(2,1)S(1)} collective-permute-done((bf16[192,384]{1,0:T(8,128)(2,1)S(1)}, bf16[192,384]{1,0:T(8,128)(2,1)S(1)}, u32[]{:S(2)}, u32[]{:S(2)}) %collective-permute-start.21) | collective-permute-done | bytes 147488 | tf_op jit(solution)/shard_map/ppermute | solution.py:730
  240.5 1.7 reduce-scatter.11.cloned.1.call-done
  243.2 3.8 %collective-permute-start.24 = (bf16[192,768]{1,0:T(8,128)(2,1)S(1)}, bf16[192,768]{1,0:T(8,128)(2,1)S(1)}, u32[]{:S(2)}, u32[]{:S(2)}) collective-permute-start(bf16[192,768]{1,0:T(8,128)(2,1)S(1)} %constant_dynamic-update-slice_fusion), channel_id=1, source_target_pairs={{1,16},{3,18},{5,20},{7,22},{9,24},{11,26},{13,28},{15,30},{16,1},... | collective-permute-start | bytes 884744 | tf_op jit(solution)/shard_map/ppermute | solution.py:672
  248.0 3.6 %collective-permute-done.24 = bf16[192,768]{1,0:T(8,128)(2,1)S(1)} collective-permute-done((bf16[192,768]{1,0:T(8,128)(2,1)S(1)}, bf16[192,768]{1,0:T(8,128)(2,1)S(1)}, u32[]{:S(2)}, u32[]{:S(2)}) %collective-permute-start.24) | collective-permute-done | bytes 294944 | tf_op jit(solution)/shard_map/ppermute | solution.py:672
  252.2 3.6 %collective-permute-start.25 = (bf16[2,512,768]{2,1,0:T(8,128)(2,1)S(1)}, bf16[2,512,768]{2,1,0:T(8,128)(2,1)S(1)}, u32[]{:S(2)}, u32[]{:S(2)}) collective-permute-start(bf16[2,512,768]{2,1,0:T(8,128)(2,1)S(1)} %shard_map.230.own_ref), channel_id=1, source_target_pairs={{1,16},{3,18},{5,20},{7,22},{9,24},{11,26},{13,28},{15,30},{16,1},... | collective-permute-start | bytes 4718600 | tf_op jit(solution)/shard_map/ppermute | solution.py:672
  255.8 3.1 %collective-permute-done.28 = bf16[192,1152]{1,0:T(8,128)(2,1)S(1)} collective-permute-done((bf16[192,1152]{1,0:T(8,128)(2,1)S(1)}, bf16[192,1152]{1,0:T(8,128)(2,1)S(1)}, u32[]{:S(2)}, u32[]{:S(2)}) %collective-permute-start.28) | collective-permute-done | bytes 442400 | tf_op jit(solution)/shard_map/ppermute | solution.py:687
  259.1 1.6 collective-permute-start.26
  260.7 1.5 collective-permute-done.26
  262.2 1.7 collective-permute-start.27
  263.9 2.2 collective-permute-done.27
  267.4 2.5 shard_map.232
  269.9 4.0 %collective-permute-done.25.got_ref = bf16[2,512,768]{2,1,0:T(8,128)(2,1)S(1)} collective-permute-done((bf16[2,512,768]{2,1,0:T(8,128)(2,1)S(1)}, bf16[2,512,768]{2,1,0:T(8,128)(2,1)S(1)}, u32[]{:S(2)}, u32[]{:S(2)}) %collective-permute-start.25) | collective-permute-done | bytes 1572896 | tf_op jit(solution)/shard_map/ppermute | solution.py:672
  273.9 2.1 shard_map.231
  (148 shorter events, 24.5 us)
Async XLA Ops:
  7.2 162.8 %reduce-scatter.13.cloned.1.call-start = ((), (), s32[]{:S(2)}) async-start(), calls=%async_computation.6 | async-start | bytes 2949120
  7.2 20.4 %collective-permute-start.2 = (s32[1,3]{1,0:T(1,128)}, s32[1,3]{1,0:T(1,128)S(1)}, u32[]{:S(2)}, u32[]{:S(2)}) collective-permute-start(s32[1,3]{1,0:T(1,128)} %param.16), channel_id=1, source_target_pairs={{0,1},{1,0},{2,3},{3,2},{4,5},{5,4},{6,7},{7,6},{8,9},{9,8},{10,11... | collective-permute-start | bytes 44 | tf_op jit(solution)/shard_map/ppermute | solution.py:691
  8.0 20.1 %collective-permute-start = (bf16[512,768]{1,0:T(8,128)(2,1)}, bf16[512,768]{1,0:T(8,128)(2,1)S(1)}, u32[]{:S(2)}, u32[]{:S(2)}) collective-permute-start(bf16[512,768]{1,0:T(8,128)(2,1)} %bitcast.48), channel_id=1, source_target_pairs={{1,16},{3,18},{5,20},{7,22},{9,24},{11,26},{13,28},{15,30},{16,1},... | collective-permute-start | bytes 2359304 | tf_op jit(solution)/shard_map/ppermute | solution.py:672
  11.0 30.3 %collective-permute-start.3 = (bf16[3,768,384]{2,1,0:T(8,128)(2,1)}, bf16[3,768,384]{2,1,0:T(8,128)(2,1)}, u32[]{:S(2)}, u32[]{:S(2)}) collective-permute-start(bf16[3,768,384]{2,1,0:T(8,128)(2,1)} %w_own.1), channel_id=1, source_target_pairs={{1,16},{3,18},{5,20},{7,22},{9,24},{11,26},{13,28},{15,30},{16,1},... | collective-permute-start | bytes 5308424 | tf_op jit(solution)/shard_map/ppermute | solution.py:672
  16.3 2.9 %copy-start.26 = (bf16[1536,768]{1,0:T(8,128)(2,1)S(1)}, bf16[1536,768]{1,0:T(8,128)(2,1)}, u32[]{:S(2)}) copy-start(bf16[1536,768]{1,0:T(8,128)(2,1)} %refs_6_.1) | copy-start | bytes 7077892
  19.3 1.3 copy-start.29
  19.3 1.7 copy-start.33
  22.6 5.0 %copy-start.38 = (s32[1,3]{1,0:T(1,128)S(1)}, s32[1,3]{1,0:T(1,128)}, u32[]{:S(2)}) copy-start(s32[1,3]{1,0:T(1,128)} %param.16) | copy-start | bytes 40
  22.6 5.4 %copy-start.32 = (bf16[1,512,768]{2,1,0:T(8,128)(2,1)S(1)}, bf16[1,512,768]{2,1,0:T(8,128)(2,1)}, u32[]{:S(2)}) copy-start(bf16[1,512,768]{2,1,0:T(8,128)(2,1)} %param.13) | copy-start | bytes 2359300
  28.1 5.0 %collective-permute-start.1 = (bf16[512,768]{1,0:T(8,128)(2,1)S(1)}, bf16[512,768]{1,0:T(8,128)(2,1)S(1)}, u32[]{:S(2)}, u32[]{:S(2)}) collective-permute-start(bf16[512,768]{1,0:T(8,128)(2,1)S(1)} %broadcast_select_fusion.1), channel_id=1, source_target_pairs={{0,1},{1,0},{2,3},{3,2},{4,5},{5,4},{6,7},{7,6},{8,9},{9,8},{10,11... | collective-permute-start | bytes 2359304 | tf_op jit(solution)/shard_map/ppermute | solution.py:691
  35.0 28.4 %collective-permute-start.4 = (bf16[896,768]{1,0:T(8,128)(2,1)S(1)}, bf16[896,768]{1,0:T(8,128)(2,1)S(1)}, u32[]{:S(2)}, u32[]{:S(2)}) collective-permute-start(bf16[896,768]{1,0:T(8,128)(2,1)S(1)} %pad_maximum_fusion.1), channel_id=1, source_target_pairs={{1,16},{3,18},{5,20},{7,22},{9,24},{11,26},{13,28},{15,30},{16,1},... | collective-permute-start | bytes 4128776 | tf_op jit(solution)/shard_map/ppermute | solution.py:672
  38.1 42.5 %collective-permute-start.7 = (bf16[1536,768]{1,0:T(8,128)(2,1)}, bf16[1536,768]{1,0:T(8,128)(2,1)}, u32[]{:S(2)}, u32[]{:S(2)}) collective-permute-start(bf16[1536,768]{1,0:T(8,128)(2,1)} %pad_maximum_fusion), channel_id=1, source_target_pairs={{1,16},{3,18},{5,20},{7,22},{9,24},{11,26},{13,28},{15,30},{16,1},... | collective-permute-start | bytes 7077896 | tf_op jit(solution)/shard_map/ppermute | solution.py:672
  64.5 6.9 %copy-start.27 = (bf16[896,768]{1,0:T(8,128)(2,1)}, bf16[896,768]{1,0:T(8,128)(2,1)S(1)}, u32[]{:S(2)}) copy-start(bf16[896,768]{1,0:T(8,128)(2,1)S(1)} %broadcast_select_fusion) | copy-start | bytes 4128772
  65.5 10.1 %copy-start.3 = (bf16[1024,768]{1,0:T(8,128)(2,1)}, bf16[1024,768]{1,0:T(8,128)(2,1)S(1)}, u32[]{:S(2)}) copy-start(bf16[1024,768]{1,0:T(8,128)(2,1)S(1)} %convolution_convert_fusion.refs_3_.own_ref) | copy-start | bytes 4718596
  65.5 15.1 %collective-permute-start.5 = (bf16[1024,768]{1,0:T(8,128)(2,1)S(1)}, bf16[1024,768]{1,0:T(8,128)(2,1)S(1)}, u32[]{:S(2)}, u32[]{:S(2)}) collective-permute-start(bf16[1024,768]{1,0:T(8,128)(2,1)S(1)} %convolution_convert_fusion.refs_3_.own_ref), channel_id=1, source_target_pairs={{0,1},{1,0},{2,3},{3,2},{4,5},{5,4},{6,7},{7,6},{8,9},{9,8},{10,11... | collective-permute-start | bytes 4718600 | tf_op jit(solution)/shard_map/ppermute | solution.py:691
  65.6 34.8 %collective-permute-start.9 = (bf16[768,768]{1,0:T(8,128)(2,1)}, bf16[768,768]{1,0:T(8,128)(2,1)}, u32[]{:S(2)}, u32[]{:S(2)}) collective-permute-start(bf16[768,768]{1,0:T(8,128)(2,1)} %get-tuple-element.101), channel_id=1, source_target_pairs={{1,16},{3,18},{5,20},{7,22},{9,24},{11,26},{13,28},{15,30},{16,1},... | collective-permute-start | bytes 3538952 | tf_op jit(solution)/shard_map/ppermute | solution.py:672
  68.6 37.2 %collective-permute-start.10 = (bf16[768,768]{1,0:T(8,128)(2,1)}, bf16[768,768]{1,0:T(8,128)(2,1)}, u32[]{:S(2)}, u32[]{:S(2)}) collective-permute-start(bf16[768,768]{1,0:T(8,128)(2,1)} %get-tuple-element.102), channel_id=1, source_target_pairs={{1,16},{3,18},{5,20},{7,22},{9,24},{11,26},{13,28},{15,30},{16,1},... | collective-permute-start | bytes 3538952 | tf_op jit(solution)/shard_map/ppermute | solution.py:672
  71.4 2.4 collective-permute-start.6
  105.9 100.3 %reduce-scatter.15.cloned.1.call-start = ((), (), s32[]{:S(2)}) async-start(), calls=%async_computation.7 | async-start | bytes 2949120
  121.2 1.4 copy-start.30
  121.3 118.3 %reduce-scatter.9.cloned.1.call-start = ((), (), s32[]{:S(2)}) async-start(), calls=%async_computation.4 | async-start | bytes 737280 | tf_op jit(solution)/shard_map/reduce_scatter | solution.py:718
  121.5 3.7 %collective-permute-start.11 = (bf16[1024,768]{1,0:T(8,128)(2,1)}, bf16[1024,768]{1,0:T(8,128)(2,1)S(1)}, u32[]{:S(2)}, u32[]{:S(2)}) collective-permute-start(bf16[1024,768]{1,0:T(8,128)(2,1)} %get-tuple-element.103.late_own), channel_id=1, source_target_pairs={{0,1},{1,0},{2,3},{3,2},{4,5},{5,4},{6,7},{7,6},{8,9},{9,8},{10,11... | collective-permute-start | bytes 4718600 | tf_op jit(solution)/shard_map/ppermute | solution.py:691
  122.6 4.8 %collective-permute-start.8 = (bf16[1024,768]{1,0:T(8,128)(2,1)S(1)}, bf16[1024,768]{1,0:T(8,128)(2,1)}, u32[]{:S(2)}, u32[]{:S(2)}) collective-permute-start(bf16[1024,768]{1,0:T(8,128)(2,1)S(1)} %copy-done.30), channel_id=1, source_target_pairs={{0,1},{1,0},{2,3},{3,2},{4,5},{5,4},{6,7},{7,6},{8,9},{9,8},{10,11... | collective-permute-start | bytes 4718600 | tf_op jit(solution)/shard_map/ppermute | solution.py:691
  125.2 2.2 copy-start.31
  161.9 13.7 %copy-start = (bf16[1024,768]{1,0:T(8,128)(2,1)S(1)}, bf16[1024,768]{1,0:T(8,128)(2,1)}, u32[]{:S(2)}) copy-start(bf16[1024,768]{1,0:T(8,128)(2,1)} %maximum_select_fusion.rows_ref.refs_2_) | copy-start | bytes 4718596
  161.9 13.7 %copy-start.7 = (bf16[3,768,384]{2,1,0:T(8,128)(2,1)S(1)}, bf16[3,768,384]{2,1,0:T(8,128)(2,1)}, u32[]{:S(2)}) copy-start(bf16[3,768,384]{2,1,0:T(8,128)(2,1)} %get-tuple-element.109.weight) | copy-start | bytes 5308420
  161.9 13.7 %copy-start.23 = (s32[8]{0:T(128)S(1)}, s32[8]{0:T(128)}, u32[]{:S(2)}) copy-start(s32[8]{0:T(128)} %stack.63.flags.refs_0_) | copy-start | bytes 100
  170.0 72.2 %reduce-scatter.11.cloned.1.call-start = ((), (), s32[]{:S(2)}) async-start(), calls=%async_computation.5 | async-start | bytes 737280 | tf_op jit(solution)/shard_map/reduce_scatter | solution.py:718
  170.1 25.2 %collective-permute-start.13 = (bf16[768,384]{1,0:T(8,128)(2,1)}, bf16[768,384]{1,0:T(8,128)(2,1)S(1)}, u32[]{:S(2)}, u32[]{:S(2)}) collective-permute-start(bf16[768,384]{1,0:T(8,128)(2,1)} %get-tuple-element.123), channel_id=1, source_target_pairs={{0,1},{1,17},{2,3},{3,19},{4,5},{5,21},{6,7},{7,23},{8,9},{9,25},{... | collective-permute-start | bytes 1769480 | tf_op jit(solution)/shard_map/ppermute | solution.py:676
  171.0 24.3 %collective-permute-start.14 = (bf16[768,384]{1,0:T(8,128)(2,1)}, bf16[768,384]{1,0:T(8,128)(2,1)S(1)}, u32[]{:S(2)}, u32[]{:S(2)}) collective-permute-start(bf16[768,384]{1,0:T(8,128)(2,1)} %get-tuple-element.124), channel_id=1, source_target_pairs={{0,2},{1,18},{2,0},{3,16},{4,6},{5,22},{6,4},{7,20},{8,10},{9,26},... | collective-permute-start | bytes 1769480 | tf_op jit(solution)/shard_map/ppermute | solution.py:676
  173.0 31.9 %collective-permute-start.15 = (bf16[768,384]{1,0:T(8,128)(2,1)}, bf16[768,384]{1,0:T(8,128)(2,1)S(1)}, u32[]{:S(2)}, u32[]{:S(2)}) collective-permute-start(bf16[768,384]{1,0:T(8,128)(2,1)} %get-tuple-element.125), channel_id=1, source_target_pairs={{0,3},{1,19},{2,1},{3,17},{4,7},{5,23},{6,5},{7,21},{8,11},{9,27},... | collective-permute-start | bytes 1769480 | tf_op jit(solution)/shard_map/ppermute | solution.py:676
  173.0 31.9 %collective-permute-start.12 = (bf16[768,384]{1,0:T(8,128)(2,1)}, bf16[768,384]{1,0:T(8,128)(2,1)S(1)}, u32[]{:S(2)}, u32[]{:S(2)}) collective-permute-start(bf16[768,384]{1,0:T(8,128)(2,1)} %get-tuple-element.107), channel_id=1, source_target_pairs={{1,16},{3,18},{5,20},{7,22},{9,24},{11,26},{13,28},{15,30},{16,1},... | collective-permute-start | bytes 1769480 | tf_op jit(solution)/shard_map/ppermute | solution.py:676
  175.6 1.7 copy-start.2
  177.3 6.8 %copy-start.1 = (bf16[1024,768]{1,0:T(8,128)(2,1)S(1)}, bf16[1024,768]{1,0:T(8,128)(2,1)}, u32[]{:S(2)}) copy-start(bf16[1024,768]{1,0:T(8,128)(2,1)} %maximum_select_fusion.1.refs_5_.cot_ref) | copy-start | bytes 4718596
  177.3 6.8 %copy-start.4 = (bf16[1024,768]{1,0:T(8,128)(2,1)S(1)}, bf16[1024,768]{1,0:T(8,128)(2,1)}, u32[]{:S(2)}) copy-start(bf16[1024,768]{1,0:T(8,128)(2,1)} %copy-done.3) | copy-start | bytes 4718596
  177.3 6.8 %copy-start.6 = (bf16[1024,768]{1,0:T(8,128)(2,1)S(1)}, bf16[1024,768]{1,0:T(8,128)(2,1)}, u32[]{:S(2)}) copy-start(bf16[1024,768]{1,0:T(8,128)(2,1)} %copy-done.5) | copy-start | bytes 4718596
  184.1 1.4 copy-start.14
  185.6 1.4 copy-start.15
  187.0 1.3 copy-start.16
  188.3 1.3 copy-start.17
  189.5 15.4 %copy-start.34 = (bf16[768,384]{1,0:T(8,128)(2,1)S(1)}, bf16[768,384]{1,0:T(8,128)(2,1)}, u32[]{:S(2)}) copy-start(bf16[768,384]{1,0:T(8,128)(2,1)} %get-tuple-element.107) | copy-start | bytes 1769476
  195.3 9.6 %copy-start.25 = (bf16[512,768]{1,0:T(8,128)(2,1)}, bf16[512,768]{1,0:T(8,128)(2,1)S(1)}, u32[]{:S(2)}) copy-start(bf16[512,768]{1,0:T(8,128)(2,1)S(1)} %get-tuple-element.135) | copy-start | bytes 2359300
  204.9 2.7 copy-start.37
  206.2 16.3 %copy-start.22 = (f32[4,768]{1,0:T(4,128)S(1)}, f32[4,768]{1,0:T(4,128)}, u32[]{:S(2)}) copy-start(f32[4,768]{1,0:T(4,128)} %pad_maximum_fusion.5.vectors.refs_6_) | copy-start | bytes 36868
  206.2 14.5 %collective-permute-start.19 = (bf16[512,768]{1,0:T(8,128)(2,1)}, bf16[512,768]{1,0:T(8,128)(2,1)S(1)}, u32[]{:S(2)}, u32[]{:S(2)}) collective-permute-start(bf16[512,768]{1,0:T(8,128)(2,1)} %get-tuple-element.133), channel_id=1, source_target_pairs={{0,1},{1,0},{2,3},{3,2},{4,5},{5,4},{6,7},{7,6},{8,9},{9,8},{10,11... | collective-permute-start | bytes 2359304 | tf_op jit(solution)/shard_map/ppermute | solution.py:691
  207.5 14.1 %collective-permute-start.20 = (bf16[512,768]{1,0:T(8,128)(2,1)}, bf16[512,768]{1,0:T(8,128)(2,1)S(1)}, u32[]{:S(2)}, u32[]{:S(2)}) collective-permute-start(bf16[512,768]{1,0:T(8,128)(2,1)} %copy-done.25), channel_id=1, source_target_pairs={{0,1},{1,0},{2,3},{3,2},{4,5},{5,4},{6,7},{7,6},{8,9},{9,8},{10,11... | collective-permute-start | bytes 2359304 | tf_op jit(solution)/shard_map/ppermute | solution.py:691
  208.4 2.2 collective-permute-start.16
  210.7 2.9 %collective-permute-start.17 = (f32[9,768]{1,0:T(8,128)S(1)}, f32[9,768]{1,0:T(8,128)S(1)}, u32[]{:S(2)}, u32[]{:S(2)}) collective-permute-start(f32[9,768]{1,0:T(8,128)S(1)} %add.102), channel_id=1, source_target_pairs={{0,16},{16,0},{1,17},{17,1},{2,18},{18,2},{3,19},{19,3},{4,20},{20... | collective-permute-start | bytes 82952 | tf_op jit(solution)/shard_map/ppermute | solution.py:738
  213.6 4.9 %collective-permute-start.18 = (f32[9,768]{1,0:T(8,128)S(1)}, f32[9,768]{1,0:T(8,128)S(1)}, u32[]{:S(2)}, u32[]{:S(2)}) collective-permute-start(f32[9,768]{1,0:T(8,128)S(1)} %add.103), channel_id=1, source_target_pairs={{0,2},{2,0},{1,3},{3,1},{4,6},{6,4},{5,7},{7,5},{8,10},{10,8},{9,1... | collective-permute-start | bytes 82952 | tf_op jit(solution)/shard_map/ppermute | solution.py:738
  216.0 15.1 %collective-permute-start.23 = (bf16[192,384]{1,0:T(8,128)(2,1)S(1)}, bf16[192,384]{1,0:T(8,128)(2,1)S(1)}, u32[]{:S(2)}, u32[]{:S(2)}) collective-permute-start(bf16[192,384]{1,0:T(8,128)(2,1)S(1)} %get-tuple-element.200), channel_id=1, source_target_pairs={{0,12},{4,0},{8,4},{12,8},{1,13},{5,1},{9,5},{13,9},{2,14},{6,2},{... | collective-permute-start | bytes 442376 | tf_op jit(solution)/shard_map/ppermute | solution.py:730
  216.6 14.5 %collective-permute-start.22 = (bf16[192,384]{1,0:T(8,128)(2,1)S(1)}, bf16[192,384]{1,0:T(8,128)(2,1)S(1)}, u32[]{:S(2)}, u32[]{:S(2)}) collective-permute-start(bf16[192,384]{1,0:T(8,128)(2,1)S(1)} %get-tuple-element.201), channel_id=1, source_target_pairs={{0,8},{4,12},{8,0},{12,4},{1,9},{5,13},{9,1},{13,5},{2,10},{6,14},... | collective-permute-start | bytes 442376 | tf_op jit(solution)/shard_map/ppermute | solution.py:730
  218.5 20.4 %collective-permute-start.21 = (bf16[192,384]{1,0:T(8,128)(2,1)S(1)}, bf16[192,384]{1,0:T(8,128)(2,1)S(1)}, u32[]{:S(2)}, u32[]{:S(2)}) collective-permute-start(bf16[192,384]{1,0:T(8,128)(2,1)S(1)} %get-tuple-element.202), channel_id=1, source_target_pairs={{0,4},{4,8},{8,12},{12,0},{1,5},{5,9},{9,13},{13,1},{2,6},{6,10},{... | collective-permute-start | bytes 442376 | tf_op jit(solution)/shard_map/ppermute | solution.py:730
  222.5 1.4 copy-start.9
  223.9 1.4 copy-start.11
  225.3 1.4 copy-start.13
  231.1 7.8 %copy-start.35 = (bf16[192,384]{1,0:T(8,128)(2,1)}, bf16[192,384]{1,0:T(8,128)(2,1)S(1)}, u32[]{:S(2)}) copy-start(bf16[192,384]{1,0:T(8,128)(2,1)S(1)} %collective-permute-done.22) | copy-start | bytes 442372
  243.2 8.5 %collective-permute-start.24 = (bf16[192,768]{1,0:T(8,128)(2,1)S(1)}, bf16[192,768]{1,0:T(8,128)(2,1)S(1)}, u32[]{:S(2)}, u32[]{:S(2)}) collective-permute-start(bf16[192,768]{1,0:T(8,128)(2,1)S(1)} %constant_dynamic-update-slice_fusion), channel_id=1, source_target_pairs={{1,16},{3,18},{5,20},{7,22},{9,24},{11,26},{13,28},{15,30},{16,1},... | collective-permute-start | bytes 884744 | tf_op jit(solution)/shard_map/ppermute | solution.py:672
  251.7 7.2 %collective-permute-start.28 = (bf16[192,1152]{1,0:T(8,128)(2,1)S(1)}, bf16[192,1152]{1,0:T(8,128)(2,1)S(1)}, u32[]{:S(2)}, u32[]{:S(2)}) collective-permute-start(bf16[192,1152]{1,0:T(8,128)(2,1)S(1)} %get-tuple-element.205), channel_id=1, source_target_pairs={{0,2},{2,0},{1,3},{3,1},{4,6},{6,4},{5,7},{7,5},{8,10},{10,8},{9,1... | collective-permute-start | bytes 1327112 | tf_op jit(solution)/shard_map/ppermute | solution.py:687
  252.2 21.7 %collective-permute-start.25 = (bf16[2,512,768]{2,1,0:T(8,128)(2,1)S(1)}, bf16[2,512,768]{2,1,0:T(8,128)(2,1)S(1)}, u32[]{:S(2)}, u32[]{:S(2)}) collective-permute-start(bf16[2,512,768]{2,1,0:T(8,128)(2,1)S(1)} %shard_map.230.own_ref), channel_id=1, source_target_pairs={{1,16},{3,18},{5,20},{7,22},{9,24},{11,26},{13,28},{15,30},{16,1},... | collective-permute-start | bytes 4718600 | tf_op jit(solution)/shard_map/ppermute | solution.py:672
  258.9 15.0 %copy-start.8 = (f32[512,768]{1,0:T(8,128)S(1)}, f32[512,768]{1,0:T(8,128)}, u32[]{:S(2)}) copy-start(f32[512,768]{1,0:T(8,128)} %get-tuple-element.85.part_ref) | copy-start | bytes 4718596
  259.0 15.0 %copy-start.24 = (f32[5]{0:T(128)S(1)}, f32[5]{0:T(128)}, u32[]{:S(2)}) copy-start(f32[5]{0:T(128)} %weight_ref.3) | copy-start | bytes 64
  259.0 8.3 %collective-permute-start.29 = (bf16[2,192,1152]{2,1,0:T(8,128)(2,1)S(1)}, bf16[2,192,1152]{2,1,0:T(8,128)(2,1)S(1)}, u32[]{:S(2)}, u32[]{:S(2)}) collective-permute-start(bf16[2,192,1152]{2,1,0:T(8,128)(2,1)S(1)} %pad_maximum_fusion.2.here_ref), channel_id=1, source_target_pairs={{0,1},{1,0},{2,3},{3,2},{4,5},{5,4},{6,7},{7,6},{8,9},{9,8},{10,11... | collective-permute-start | bytes 2654216 | tf_op jit(solution)/shard_map/ppermute | solution.py:691
  259.1 3.0 %collective-permute-start.26 = (f32[9,768]{1,0:T(8,128)S(1)}, f32[9,768]{1,0:T(8,128)S(1)}, u32[]{:S(2)}, u32[]{:S(2)}) collective-permute-start(f32[9,768]{1,0:T(8,128)S(1)} %add.104), channel_id=1, source_target_pairs={{0,4},{4,0},{8,12},{12,8},{1,5},{5,1},{9,13},{13,9},{2,6},{6,2},{1... | collective-permute-start | bytes 82952 | tf_op jit(solution)/shard_map/ppermute | solution.py:738
  262.2 3.9 %collective-permute-start.27 = (f32[9,768]{1,0:T(8,128)S(1)}, f32[9,768]{1,0:T(8,128)S(1)}, u32[]{:S(2)}, u32[]{:S(2)}) collective-permute-start(f32[9,768]{1,0:T(8,128)S(1)} %add.112), channel_id=1, source_target_pairs={{0,8},{4,12},{8,0},{12,4},{1,9},{5,13},{9,1},{13,5},{2,10},{6,14},... | collective-permute-start | bytes 82952 | tf_op jit(solution)/shard_map/ppermute | solution.py:738
  (9 other events, 9.3 us)
Sparse Core Ops, SparseCore 0:
  106.0 37.8 reduce-scatter.12
  147.0 44.2 reduce-scatter.14
  193.6 17.8 reduce-scatter.8
  213.7 28.4 reduce-scatter.10

commit v5 on v4

--- a/solution.py
+++ b/solution.py
@@ -302,12 +302,13 @@
 def feed_kernel(early, *refs):
     if early:
         flags, weight_ref, rows_ref, own_ref, got_ref, cot_ref, vectors, up_own, down_own, got = refs[:10]
-        norm, norm_t, grad, grad_t = refs[10:14]
+        norm, norm_t, grad, grad_t, back_ref, act_ref, down_ref, pieces = refs[10:18]
         up_got, down_got = got.at[: norm.shape[1]], got.at[norm.shape[1] :]
     else:
-        flags, norm, norm_t, grad, grad_t, up_own, down_own, up_got, down_got = refs[:9]
-    back_ref, act_ref, pieces_ref, down_ref, up_w, up_sum, down_sum = refs[-7:]
-    part = pieces_ref.shape[2]
+        flags, norm, norm_t, grad, grad_t, back_early, up_own, down_own, up_got, down_got = refs[:10]
+        back_ref, act_ref, down_ref, *pieces = refs[10:17]
+    up_w, up_sum, down_sum = refs[-3:]
+    part = up_w.shape[1] // 2
     step, last = pl.program_id(0), pl.num_programs(0) - 1
 
     @pl.when(step == 0)
@@ -330,7 +331,21 @@
     value, rise = gelu_both(dot(norm[...], up_w[...]))
     act_ref[...] = value.astype(jnp.bfloat16)
     slope = (dot(grad[...], down_ref[...], NT) * rise).astype(jnp.bfloat16)
-    back_ref[...] = dot(slope, up_w[...], NT).astype(jnp.bfloat16)
+    back = dot(slope, up_w[...], NT)
+    if not early:
+        back = back + back_early[...].astype(jnp.float32)
+    back_ref[...] = back.astype(jnp.bfloat16)
+
+    def store(p, at, low):
+        if early:
+            pieces[p, at, :] = low
+            return
+        slot = 2 * (flags[2] ^ (p % 2)) + (flags[7] ^ (p // 2))
+        for j, piece in enumerate(pieces):
+
+            @pl.when(slot == j)
+            def _():
+                piece[at, :] = low
 
     def grads(i, at):
         fields = (dot(norm_t[at, :], slope), dot(grad_t[at, :], act_ref[...]))
@@ -344,7 +359,7 @@
             def _():
                 low = (total[at, :] + field).astype(jnp.bfloat16)
                 for p in range(2):
-                    pieces_ref[2 * k + p, at, :] = low[:, p * part : (p + 1) * part]
+                    store(2 * k + p, at, low[:, p * part : (p + 1) * part])
 
     row_blocks(norm_t.shape[0], grads)
 
@@ -364,85 +379,86 @@
     if early:
         operands = [by_rows(field, rows) for field in fields[:4]] + [fields[4]]
         outs = [tokens, turned, tokens, turned]
+        pieces = [((4, width, hidden // 2), low)]
     else:
         operands = [by_rows(fields[0], rows), (fields[1], (width, rows), across)]
-        operands += [by_rows(fields[2], rows), (fields[3], (width, rows), across)]
+        operands += [by_rows(fields[2], rows), (fields[3], (width, rows), across), by_rows(fields[4], rows)]
         outs = []
+        pieces = [((width, hidden // 2), low)] * 4
     operands += [
         (w_up, (width, hidden), lambda i, *scalars: (0, half)),
         (w_down, (hidden, width), lambda i, *scalars: (half, 0)),
         *got,
     ]
-    outs += [
-        tokens,
-        ((whole, hidden), low, (rows, hidden), lambda i, *scalars: (i, 0)),
-        ((4, width, hidden // 2), low),
-        ((hidden, width), low),
-    ]
+    outs += [tokens, ((whole, hidden), low, (rows, hidden), lambda i, *scalars: (i, 0)), ((hidden, width), low)]
     sums = ((width, hidden), jnp.float32)
     return streamed(
-        functools.partial(feed_kernel, early), 2, scalars, operands, outs, [((width, hidden), low), sums, sums], 17
-    )
-
-
-def lower_kernel(flags, act_early, act_late, rows_ref, own_ref, got_ref, cot_ref, early_ref, late_ref, keep_ref, send_ref, sums_ref):
-    step, half = pl.program_id(0), pl.num_programs(0) // 2
+        functools.partial(feed_kernel, early), 2, scalars, operands, outs + pieces, [((width, hidden), low), sums, sums], 17
+    )
+
+
+def lower_kernel(
+    flags, act_early, act_late, rows_ref, own_ref, got_ref, cot_ref, early_ref, late_ref, keep_ref, first, second, sums_ref
+):
+    step = pl.program_id(0)
+    total = dot(act_early[...], early_ref[...]) + dot(act_late[...], late_ref[...])
+    cot = cot_ref[...].astype(jnp.float32)
 
     @pl.when(step == 0)
     def _():
         sums_ref[...] = jnp.zeros_like(sums_ref)
 
-    total = dot(act_early[...], early_ref[...]) + dot(act_late[...], late_ref[...])
-    cot = cot_ref[...].astype(jnp.float32)
-
-    @pl.when(step < half)
+    send_or_keep(
+        total,
+        total + sum(ref[...].astype(jnp.float32) for ref in (rows_ref, own_ref, got_ref)),
+        first,
+        second,
+        keep_ref,
+    )
+    mine = jnp.where(step < pl.num_programs(0) // 2, 0.0, 1.0)
+    block = total + mine * sum(ref[...].astype(jnp.float32) for ref in (rows_ref, own_ref, got_ref))
+    sums_ref[0:1, :] += jnp.sum(block * cot, axis=0, keepdims=True)
+
+
+def send_or_keep(sent, kept, first, second, keep_ref):
+    step = pl.program_id(0)
+    for j, ref in enumerate((first, second)):
+
+        @pl.when(step == j)
+        def _():
+            ref[...] = sent.astype(ref.dtype)
+
+    @pl.when(step >= 2)
     def _():
-        send_ref[...] = total.astype(jnp.bfloat16)
-        sums_ref[0:1, :] += jnp.sum(total * cot, axis=0, keepdims=True)
-
-    @pl.when(step >= half)
-    def _():
-        parts = [ref[...].astype(jnp.float32) for ref in (rows_ref, own_ref, got_ref)]
-        block = total + parts[0] + parts[1] + parts[2]
-        keep_ref[...] = block
-        sums_ref[0:1, :] += jnp.sum(block * cot, axis=0, keepdims=True)
-
-
-def theirs_first(steps):
-    return lambda i, flags, *more: lax.rem((1 - flags[1]) * (steps // 2) + i, steps)
-
-
-def halves(steps, rows, width):
-    keep = (rows, width), lambda i, *scalars: (jnp.maximum(i - steps // 2, 0), 0)
-    send = (rows, width), lambda i, *scalars: (jnp.minimum(i, steps // 2 - 1), 0)
-    return keep, send
+        keep_ref[...] = kept
+
+
+def theirs_first(i, flags, *more):
+    return lax.rem((1 - flags[1]) * 2 + i, 4)
+
+
+def sent_and_kept(whole, width):
+    rows = whole // 4
+    keep = ((2 * rows, width), jnp.float32, (rows, width), lambda i, *scalars: (jnp.maximum(i - 2, 0), 0))
+    send = ((rows, width), jnp.bfloat16)
+    return [keep, send, send, ((8, width), jnp.float32)]
 
 
 def lower(flags, act_early, act_late, down_early, down_late, rows, own, got, cot):
     whole, width = rows.shape
-    steps = whole // ROWS
-    order = theirs_first(steps)
-    keep, send = halves(steps, ROWS, width)
-    shape = (whole // 2, width)
+    fields = [by_rows(field, whole // 4, theirs_first) for field in (act_early, act_late, rows, own, got, cot)]
     return streamed(
-        lower_kernel,
-        steps,
-        [flags],
-        [by_rows(field, ROWS, order) for field in (act_early, act_late, rows, own, got, cot)] + [down_early, down_late],
-        [(shape, jnp.float32, *keep), (shape, jnp.bfloat16, *send), ((8, width), jnp.float32)],
-        [],
-        6,
-        SNUG,
+        lower_kernel, 4, [flags], fields + [down_early, down_late], sent_and_kept(whole, width), [], 6, SNUG
     )
 
 
 def middle_kernel(
-    flags, weight_ref, rows_ref, own_ref, got_ref, cot_ref, early_own, early_got, late_own, late_got, mixed_ref,
+    flags, weight_ref, rows_ref, own_ref, got_ref, cot_ref, back_own, back_got, mixed_ref,
     vectors, w_ref, grad_ref, gmixed_ref, gout_ref, sums_ref, gout,
 ):
     step, last = pl.program_id(0), pl.num_programs(0) - 1
     unit, scale = norm_parts(sum(ref[...].astype(jnp.float32) for ref in (rows_ref, own_ref, got_ref)))
-    back = sum(ref[...].astype(jnp.float32) for ref in (early_own, early_got, late_own, late_got))
+    back = sum(ref[...].astype(jnp.float32) for ref in (back_own, back_got))
     inner = back * vectors[2:3, :]
     mean = jnp.mean(inner, axis=-1, keepdims=True)
     slant = jnp.mean(inner * unit, axis=-1, keepdims=True)
@@ -515,69 +531,54 @@
     )
 
 
-def unproject_kernel(flags, grad_ref, rows_ref, weight, keep_ref, send_ref, sums_ref):
-    step, half = pl.program_id(0), pl.num_programs(0) // 2
+def unproject_kernel(flags, grad_ref, rows_ref, weight, keep_ref, first, second, sums_ref):
     total = dot(grad_ref[0], weight[0], NT)
     for c in range(1, grad_ref.shape[0]):
         total = total + dot(grad_ref[c], weight[c], NT)
     unit, unused = norm_parts(rows_ref[...].astype(jnp.float32))
 
-    @pl.when(step == 0)
+    @pl.when(pl.program_id(0) == 0)
     def _():
         sums_ref[...] = jnp.zeros_like(sums_ref)
 
     sums_ref[0:1, :] += jnp.sum(total * unit, axis=0, keepdims=True)
     sums_ref[1:2, :] += jnp.sum(total, axis=0, keepdims=True)
-
-    @pl.when(step < half)
-    def _():
-        send_ref[...] = total.astype(jnp.bfloat16)
-
-    @pl.when(step >= half)
-    def _():
-        keep_ref[...] = total
+    send_or_keep(total, total, first, second, keep_ref)
 
 
 def unproject(flags, grad, weight, rows):
     whole, width = rows.shape
     count, unused, columns = grad.shape
-    steps = whole // ROWS
-    order = theirs_first(steps)
-    keep, send = halves(steps, ROWS, width)
-    shape = (whole // 2, width)
-    return streamed(
-        unproject_kernel,
-        steps,
-        [flags],
-        [(grad, (count, ROWS, columns), lambda i, flags: (0, order(i, flags), 0)), by_rows(rows, ROWS, order), weight],
-        [(shape, jnp.float32, *keep), (shape, jnp.bfloat16, *send), ((8, width), jnp.float32)],
-        [],
-        5,
-        SNUG,
-    )
-
-
-def last_kernel(flags, rows_ref, resid_ref, keep_ref, got_ref, block_keep, block_got, vectors, out_ref):
+    grads = (grad, (count, whole // 4, columns), lambda i, flags: (0, theirs_first(i, flags), 0))
+    fields = [grads, by_rows(rows, whole // 4, theirs_first), weight]
+    return streamed(unproject_kernel, 4, [flags], fields, sent_and_kept(whole, width), [], 5, SNUG)
+
+
+def last_kernel(
+    flags, rows_ref, resid_ref, keep_ref, block_keep, got_first, got_second, block_first, block_second, vectors, out_ref
+):
+    first = pl.program_id(0) == 0
     unit, scale = norm_parts(rows_ref[...].astype(jnp.float32))
-    inner = (keep_ref[...] + got_ref[...].astype(jnp.float32)) * vectors[0:1, :]
+    got = jnp.where(first, got_first[...], got_second[...]).astype(jnp.float32)
+    inner = (keep_ref[...] + got) * vectors[0:1, :]
     mean = jnp.mean(inner, axis=-1, keepdims=True)
     slant = jnp.mean(inner * unit, axis=-1, keepdims=True)
     grad = resid_ref[...].astype(jnp.float32) + scale * (inner - mean - unit * slant)
     out_ref[0] = grad.astype(jnp.bfloat16)
-    out_ref[1] = (block_keep[...] + block_got[...].astype(jnp.float32)).astype(jnp.bfloat16)
-
-
-def last(flags, rows, resid, keep, got, block_keep, block_got, vectors):
+    got = jnp.where(first, block_first[...], block_second[...]).astype(jnp.float32)
+    out_ref[1] = (block_keep[...] + got).astype(jnp.bfloat16)
+
+
+def last(flags, rows, resid, keep, block_keep, got, vectors):
     half, width = keep.shape
-    steps = half // ROWS
+    size = half // 2
 
     def mine(i, flags):
-        return flags[1] * steps + i
-
-    out = ((2, half, width), jnp.bfloat16, (2, ROWS, width), lambda i, flags: (0, i, 0))
-    fields = [by_rows(rows, ROWS, mine), by_rows(resid, ROWS, mine)]
-    fields += [by_rows(field, ROWS) for field in (keep, got, block_keep, block_got)]
-    return streamed(last_kernel, steps, [flags], fields + [vectors], [out], [], 3, SNUG)[0]
+        return flags[1] * 2 + i
+
+    out = ((2, half, width), jnp.bfloat16, (2, size, width), lambda i, flags: (0, i, 0))
+    fields = [by_rows(rows, size, mine), by_rows(resid, size, mine), by_rows(keep, size), by_rows(block_keep, size)]
+    return streamed(last_kernel, 2, [flags], fields + [*got, vectors], [out], [], 3)[0]
 
 
 def past_kernel(dwa_ref, hist_ref, cot_ref, grad_ref, part_ref, sums_ref):
@@ -806,40 +807,44 @@
     cot_rows = ordered(cot_half, swap_near(cot_half), near == 0)
     scalars = [flags, dwa_weights]
     fields = [layer_rows, attn, attn_got, cot_rows, vectors]
-    *kept, back_early, act_early, early_pieces, down_early = feed(True, scalars, fields, w_up, w_down, early_got)
+    *kept, back, act_early, down_early, early_pieces = feed(True, scalars, fields, w_up, w_down, early_got)
     early_sum = scatter_plane(after(early_pieces, late_up, late_down))
-    back_late, act_late, late_pieces, down_late = feed(False, [flags], kept, w_up, w_down, late_up, late_down)
-    late_sum = scatter_plane(late_pieces)
-    fields = [layer_rows, attn, attn_got, cot_rows, back_early, swap_near(back_early), back_late, swap_near(back_late)]
+    back, act_late, down_late, *late_owned = feed(
+        False, [flags], [*kept, back], w_up, w_down, late_up, late_down
+    )
+    late_moved = [send_to_owner(late_owned[j], j // 2, j % 2) for j in range(4)]
+    fields = [layer_rows, attn, attn_got, cot_rows, back, swap_near(back)]
     grad_attn, grad_mixed, grad_out, sums_two = middle(flags, dwa_weights, fields, mixed, vectors, weight_out)
     grad_qkv = attend_back(apart, member, cos_table, sin_table, projected, grad_mixed, LONGEST)
+    grad_qkv, *late_moved = lax.optimization_barrier((grad_qkv, *late_moved))
     owned = weigh(flags, norm_one_t, grad_qkv, grad_out)
     moved = [send_to_owner(owned[j], j // 2, j % 2) for j in range(4)]
-    keep, send, sums_one = unproject(flags, after(grad_qkv, owned[0]), weight_qkv, layer_rows)
-    block_keep, block_send, sums_now = lower(
-        flags, act_early, act_late, down_early, down_late, layer_rows, attn, attn_got, after(cot_rows, send)
-    )
-    early_sum = scatter_rows(after(early_sum, owned[0]))
-    keep, send, block_keep, block_send, *moved = lax.optimization_barrier(
-        (keep, send, block_keep, block_send, *moved)
-    )
+    late_sum = add(jnp.where(same, late_owned[0], after(late_moved[0], owned[0])), *late_moved[1:])
+    feed_sum = scatter_rows(jnp.concatenate([early_sum, late_sum], axis=1))
+    keep, *send, sums_one = unproject(flags, after(grad_qkv, owned[0]), weight_qkv, layer_rows)
+    block_keep, *block_send, sums_now = lower(
+        flags, act_early, act_late, down_early, down_late, layer_rows, attn, attn_got, after(cot_rows, keep)
+    )
+    sent = [*send, *block_send]
+    keep, block_keep, *arrived = lax.optimization_barrier((keep, block_keep, *sent, *moved))
+    sent, moved = arrived[:4], arrived[4:]
     attn_one = add(jnp.where(same, owned[0], moved[0]), *moved[1:])
     attn_moved = move_rows(attn_one)
-    late_sum = scatter_rows(after(late_sum, attn_one))
-    ours = last(
-        flags, layer_rows, grad_attn, keep, swap_near(send), block_keep, swap_near(block_send), vectors
-    )
+    got = [swap_near(field) for field in sent]
+    ours = last(flags, layer_rows, grad_attn, after(keep, attn_one), block_keep, got, vectors)
+    early_sum, late_sum = jnp.split(after(feed_sum, attn_one), 2, axis=1)
+    early_got = swap_diagonal(early_sum)
     small = jnp.concatenate([sums_one[:2], sums_two[:2], sums_now[:1], sums_past[:hist_count]], axis=0)
-    small = after(small, attn_one)
+    small = after(small, ours)
     for name in ("near", "tp", "far"):
         small = sum_over(small, name)
-    small, ours, *attn_moved = lax.optimization_barrier((small, ours, *attn_moved))
-    feed_sum = jnp.concatenate([after(early_sum, small), late_sum], axis=1)
-    feed_got = swap_diagonal(feed_sum)
-    theirs = swap_diagonal(after(ours, feed_got))
+    small, ours, late_sum, early_sum, early_got, *attn_moved = lax.optimization_barrier(
+        (small, ours, late_sum, early_sum, early_got, *attn_moved)
+    )
+    theirs = swap_diagonal(ours)
     small = sum_over(small, "dp")
     attn_sum = add(*attn_moved)
-    blocks = jnp.concatenate([attn_sum, jnp.where(same, feed_sum, feed_got)], axis=1)
+    blocks = jnp.concatenate([attn_sum, jnp.where(same, early_sum, early_got), late_sum], axis=1)
     here = jnp.stack([blocks, swap_far(blocks)])
     output, grad_input = present(flags, dwa_weights, past_sum, ours, theirs)
     grad_w_qkv, grad_w_out, grad_w_up, grad_w_down = place(flags, here, swap_near(here))

time: 285 us -> 270 us (0.947)
  waiting for transfers between devices: 53.2 us -> 32.3 us
  local copies, waits for them, and re-layouts: 36 us -> 23.3 us
  other arithmetic: 14.6 us -> 20.6 us
  starting transfers between devices: 43.5 us -> 49.2 us
  Pallas kernels: 120 us -> 125 us
    unnamed x79 -> x80, local copies, waits for them, and re-layouts: 23 us -> 13.6 us
    ppermute x3, waiting for transfers between devices: 7.84 us -> 0.01 us  [move_rows(): lax.ppermute(sent, 'dp', [(d, (d + step) % dps) for d in range(dps)])]
    ppermute x8, waiting for transfers between devices: 18.1 us -> 11.6 us  [swap_diagonal(): lax.ppermute(field, AXES, moves(away, lambda t, d, k, c: (c, d, k, t)))]
    pallas_call x10, Pallas kernels: 79.7 us -> 84.9 us  [streamed(): pl.pallas_call(kernel, grid_spec=pltpu.PrefetchScalarGridSpec(num_scalar_...]
    ppermute x4 -> x8, waiting for transfers between devices: 9.64 us -> 4.99 us  [send_to_owner(): lax.ppermute(field, AXES, moves(away if not other_far and (not other_tp)...]
    ppermute x4 -> x8, starting transfers between devices: 5.52 us -> 9.98 us  [send_to_owner(): lax.ppermute(field, AXES, moves(away if not other_far and (not other_tp)...]
    ppermute x5, waiting for transfers between devices: 7.63 us -> 10.8 us  [sum_over(): lax.ppermute(field, name, [(d, d ^ bit) for d in range(size)])]
    ppermute x9 -> x10, starting transfers between devices: 2.52 us -> 5.41 us  [swap_near(): return lax.ppermute(field, 'near', [(0, 1), (1, 0)])]
  transfers between devices with their start and end apart: 34 -> 37, of which waited for: 15 -> 12; matrix products, arithmetic and copies ran while one was open for 10% -> 11% of each run, Pallas kernels for 42% -> 46%
where the time goes in v5:
time: 270 us; the launch traced here: 266 us
  Pallas kernels  125 us (46%)
  starting transfers between devices  49.2 us (18%)
  waiting for transfers between devices  32.3 us (12%)
  local copies, waits for them, and re-layouts  23.3 us (9%)
  other arithmetic  20.6 us (8%)
  between operations  14.8 us (5%)
    pallas_call x10, Pallas kernels, streamed(): pl.pallas_call(kernel, grid_spec=pltpu.PrefetchScalarGridSpec(num_scalar_...  84.9 us
    ppermute x8, starting transfers between devices, swap_diagonal(): lax.ppermute(field, AXES, moves(away, lambda t, d, k, c: (c, d, k, t)))  25.2 us
    pallas_call x1, Pallas kernels, attend_back(): pl.pallas_call(functools.partial(attend_back_kernel, reach), grid=(width...  23.1 us
    unnamed x80, local copies, waits for them, and re-layouts  13.6 us
    pallas_call x1, Pallas kernels, attend(): pl.pallas_call(functools.partial(attend_kernel, reach), grid=(width // LA...  12.7 us
    ppermute x8, waiting for transfers between devices, swap_diagonal(): lax.ppermute(field, AXES, moves(away, lambda t, d, k, c: (c, d, k, t)))  11.6 us
    ppermute x5, waiting for transfers between devices, sum_over(): lax.ppermute(field, name, [(d, d ^ bit) for d in range(size)])  10.8 us
    ppermute x8, starting transfers between devices, send_to_owner(): lax.ppermute(field, AXES, moves(away if not other_far and (not other_tp)...  9.98 us
  transfers between devices with their start and end apart: 37, of which 12 were waited for; matrix products, arithmetic and copies ran while one was open for 11% of the time, Pallas kernels for 46%

profile of v5, /device:TPU:9, one launch (start us, length us, event | category | flops | bytes accessed | tf_op | source)
XLA Modules:
  0.0 266.0 jit_solution(6552230590080116608)
XLA Ops:
  8.0 3.1 %collective-permute-start = (bf16[512,768]{1,0:T(8,128)(2,1)}, bf16[512,768]{1,0:T(8,128)(2,1)}, u32[]{:S(2)}, u32[]{:S(2)}) collective-permute-start(bf16[512,768]{1,0:T(8,128)(2,1)} %bitcast.47), channel_id=1, source_target_pairs={{1,16},{3,18},{5,20},{7,22},{9,24},{11,26},{13,28},{15,30},{16,1},... | collective-permute-start | bytes 2359304 | tf_op jit(solution)/shard_map/ppermute | solution.py:673
  11.0 2.5 collective-permute-start.3
  13.6 2.9 %fusion.10 = (bf16[768,768]{1,0:T(8,128)(2,1)}, bf16[768,768]{1,0:T(8,128)(2,1)S(1)}) fusion(bf16[1536,768]{1,0:T(8,128)(2,1)} %refs_7_.3), kind=kLoop, calls=%fused_computation.50 | loop fusion | bytes 4718592 | tf_op jit(solution)/shard_map/dynamic_slice | solution.py:707
  16.6 1.6 fusion.11
  18.6 4.3 %shard_map.220 = (bf16[4,512,768]{2,1,0:T(8,128)(2,1)}, f32[512,768]{1,0:T(8,128)}, f32[8,768]{1,0:T(8,128)}) custom-call(f32[5]{0:T(128)} %weight_ref.3, bf16[4,512,768]{2,1,0:T(8,128)(2,1)} %bitcast.43, bf16[512,768]{1,0:T(8,128)(2,1)} %bitcast.44), custom_call_target="tpu_custom_call" | custom-call | bytes 9000000 | tf_op jit(solution)/shard_map/pallas_call | solution.py:603
  22.9 2.9 %pad_maximum_fusion = bf16[1536,768]{1,0:T(8,128)(2,1)} fusion(bf16[768,768]{1,0:T(8,128)(2,1)S(1)} %get-tuple-element.225, bf16[768,768]{1,0:T(8,128)(2,1)} %get-tuple-element.227), kind=kLoop, calls=%fused_computation | loop fusion | flops 4718592 | bytes 4718592 | tf_op jit(solution)/shard_map/concatenate | solution.py:769
  26.9 1.2 broadcast_select_fusion.1
  28.2 3.1 %fusion = (f32[1024,128]{1,0:T(8,128)}, f32[1024,128]{1,0:T(8,128)}) fusion(f32[128]{0:T(128)S(1)} %get-tuple-element.239, f32[128]{0:T(128)S(1)} %get-tuple-element.240, f32[1024]{0:T(1024)S(1)} %subtract_convert_fusion), kind=kLoop, calls=%fused_computation.13 | loop fusion | flops 262144 | bytes 1053696 | tf_op jit(solution)/shard_map/mul | solution.py:784
  33.1 1.8 maximum_select_fusion.rows_ref.refs_2_
  35.0 3.0 %collective-permute-start.4 = (bf16[896,768]{1,0:T(8,128)(2,1)S(1)}, bf16[896,768]{1,0:T(8,128)(2,1)S(1)}, u32[]{:S(2)}, u32[]{:S(2)}) collective-permute-start(bf16[896,768]{1,0:T(8,128)(2,1)S(1)} %pad_maximum_fusion.1), channel_id=1, source_target_pairs={{1,16},{3,18},{5,20},{7,22},{9,24},{11,26},{13,28},{15,30},{16,1},... | collective-permute-start | bytes 4128776 | tf_op jit(solution)/shard_map/ppermute | solution.py:673
  38.0 2.5 collective-permute-start.7
  41.2 9.5 %shard_map.221 = (bf16[3,1024,384]{2,1,0:T(8,128)(2,1)}, bf16[768,1024]{1,0:T(8,128)(2,1)}, bf16[3,768,384]{2,1,0:T(8,128)(2,1)}) custom-call(s32[8]{0:T(128)} %stack.63.flags.refs_0_, bf16[1024,768]{1,0:T(8,128)(2,1)} %maximum_select_fusion.rows_ref.refs_2_, f32[1024,128]{1,0:T(8,128)} %get-tuple-element.102.cos_ref, ...), custom_call_target="tpu_custom_call" | custom-call | bytes 24000000 | tf_op jit(solution)/shard_map/pallas_call | solution.py:223
  50.7 12.7 %shard_map.222.mixed_ref = bf16[1024,384]{1,0:T(8,128)(2,1)} custom-call(bf16[1024,128]{1,0:T(8,128)(2,1)} %select_convert_fusion.apart_ref, bf16[1024,128]{1,0:T(8,128)(2,1)} %fusion.1.member_ref, bf16[3,1024,384]{2,1,0:T(8,128)(2,1)} %get-tuple-element.106.q_ref.k_ref.v_ref, bf16[3,1024,384]{2,1,0:T(8,128)(2,1)} %get-tuple-element.106.q_ref.k_ref.v_ref, ...), custom_call_target="tpu_custom_call" | custom-call | bytes 36000000 | tf_op jit(solution)/shard_map/pallas_call | solution.py:99
  65.6 3.1 %collective-permute-start.8 = (bf16[768,768]{1,0:T(8,128)(2,1)}, bf16[768,768]{1,0:T(8,128)(2,1)S(1)}, u32[]{:S(2)}, u32[]{:S(2)}) collective-permute-start(bf16[768,768]{1,0:T(8,128)(2,1)} %get-tuple-element.115), channel_id=1, source_target_pairs={{1,16},{3,18},{5,20},{7,22},{9,24},{11,26},{13,28},{15,30},{16,1},... | collective-permute-start | bytes 3538952 | tf_op jit(solution)/shard_map/ppermute | solution.py:673
  68.6 2.7 %collective-permute-start.9 = (bf16[768,768]{1,0:T(8,128)(2,1)}, bf16[768,768]{1,0:T(8,128)(2,1)S(1)}, u32[]{:S(2)}, u32[]{:S(2)}) collective-permute-start(bf16[768,768]{1,0:T(8,128)(2,1)} %get-tuple-element.116), channel_id=1, source_target_pairs={{1,16},{3,18},{5,20},{7,22},{9,24},{11,26},{13,28},{15,30},{16,1},... | collective-permute-start | bytes 3538952 | tf_op jit(solution)/shard_map/ppermute | solution.py:673
  71.5 2.3 collective-permute-done.6
  73.7 1.8 maximum_select_fusion.1.refs_5_.cot_ref
  75.6 5.0 %collective-permute-done.7.refs_9_ = bf16[1536,768]{1,0:T(8,128)(2,1)} collective-permute-done((bf16[1536,768]{1,0:T(8,128)(2,1)}, bf16[1536,768]{1,0:T(8,128)(2,1)}, u32[]{:S(2)}, u32[]{:S(2)}) %collective-permute-start.7) | collective-permute-done | bytes 2359328 | tf_op jit(solution)/shard_map/ppermute | solution.py:673
  80.6 1.2 copy-done.5
  81.7 18.7 %shard_map.223 = (bf16[1024,768]{1,0:T(8,128)(2,1)}, bf16[768,1024]{1,0:T(8,128)(2,1)}, bf16[1024,768]{1,0:T(8,128)(2,1)}, bf16[768,1024]{1,0:T(8,128)(2,1)}, bf...) custom-call(s32[8]{0:T(128)} %stack.63.flags.refs_0_, ...), custom_call_target="tpu_custom_call" | custom-call | bytes 51000000 | tf_op jit(solution)/shard_map/pallas_call | solution.py:223
  100.5 5.2 %collective-permute-done.9.refs_9_ = bf16[768,768]{1,0:T(8,128)(2,1)S(1)} collective-permute-done((bf16[768,768]{1,0:T(8,128)(2,1)}, bf16[768,768]{1,0:T(8,128)(2,1)S(1)}, u32[]{:S(2)}, u32[]{:S(2)}) %collective-permute-start.9) | collective-permute-done | bytes 1179680 | tf_op jit(solution)/shard_map/ppermute | solution.py:673
  106.8 16.2 %shard_map.224 = (bf16[1024,768]{1,0:T(8,128)(2,1)}, bf16[1024,768]{1,0:T(8,128)(2,1)}, bf16[768,768]{1,0:T(8,128)(2,1)}, bf16[768,384]{1,0:T(8,128)(2,1)}, bf16...) custom-call(s32[8]{0:T(128)} %stack.63.flags.refs_0_, ...), custom_call_target="tpu_custom_call" | custom-call | bytes 51000000 | tf_op jit(solution)/shard_map/pallas_call | solution.py:223
  123.1 3.1 %collective-permute-start.11 = (bf16[768,384]{1,0:T(8,128)(2,1)}, bf16[768,384]{1,0:T(8,128)(2,1)S(1)}, u32[]{:S(2)}, u32[]{:S(2)}) collective-permute-start(bf16[768,384]{1,0:T(8,128)(2,1)} %get-tuple-element.119), channel_id=1, source_target_pairs={{1,16},{3,18},{5,20},{7,22},{9,24},{11,26},{13,28},{15,30},{16,1},... | collective-permute-start | bytes 1769480 | tf_op jit(solution)/shard_map/ppermute | solution.py:677
  126.2 1.6 collective-permute-start.13
  128.1 1.9 slice.48.w_ref
  130.0 1.2 copy-done.23
  131.2 10.1 %shard_map.225 = (bf16[1024,768]{1,0:T(8,128)(2,1)}, bf16[1024,384]{1,0:T(8,128)(2,1)}, bf16[768,384]{1,0:T(8,128)(2,1)}, f32[8,768]{1,0:T(8,128)}) custom-call(s32[8]{0:T(128)} %stack.63.flags.refs_0_, f32[5]{0:T(128)} %weight_ref.3, bf16[1024,768]{1,0:T(8,128)(2,1)} %maximum_select_fusion.rows_ref.refs_2_, bf16[1024,768]{1,0:T(8,128)(2,1)} %copy-done.3, ...), custom_call_target="tpu_custom_call" | custom-call | bytes 24000000 | tf_op jit(solution)/shard_map/pallas_call | solution.py:223
  141.3 23.1 %shard_map.226.grad_ref = bf16[3,1024,384]{2,1,0:T(8,128)(2,1)} custom-call(bf16[1024,128]{1,0:T(8,128)(2,1)} %select_convert_fusion.apart_ref, bf16[1024,128]{1,0:T(8,128)(2,1)} %fusion.1.member_ref, f32[1024,128]{1,0:T(8,128)} %get-tuple-element.102.cos_ref, f32[1024,128]{1,0:T(8,128)} %get-tuple-element.103.sin_ref, ...), custom_call_target="tpu_custom_call" | custom-call | bytes 66000000 | tf_op jit(solution)/shard_map/pallas_call | solution.py:175
  164.4 7.8 %shard_map.227 = (bf16[768,384]{1,0:T(8,128)(2,1)}, bf16[768,384]{1,0:T(8,128)(2,1)}, bf16[768,384]{1,0:T(8,128)(2,1)}, bf16[768,384]{1,0:T(8,128)(2,1)}) custom-call(s32[8]{0:T(128)} %stack.63.flags.refs_0_, bf16[768,1024]{1,0:T(8,128)(2,1)} %get-tuple-element.124.turned_ref, bf16[768,384]{1,0:T(8,128)(2,1)} %get-tuple-element.125.out_grad_ref, ...), custom_call_target="tpu_custom_call" | custom-call | bytes 12000000 | tf_op jit(solution)/shard_map/pallas_call | solution.py:223
  172.2 1.2 add_convert_fusion
  173.4 2.5 pad_maximum_fusion.2
  175.9 3.7 %collective-permute-start.15 = (bf16[768,384]{1,0:T(8,128)(2,1)}, bf16[768,384]{1,0:T(8,128)(2,1)}, u32[]{:S(2)}, u32[]{:S(2)}) collective-permute-start(bf16[768,384]{1,0:T(8,128)(2,1)} %get-tuple-element.126), channel_id=1, source_target_pairs={{1,16},{3,18},{5,20},{7,22},{9,24},{11,26},{13,28},{15,30},{16,1},... | collective-permute-start | bytes 1769480 | tf_op jit(solution)/shard_map/ppermute | solution.py:677
  179.7 1.0 collective-permute-start.17
  181.0 1.7 copy-done.2
  182.7 5.9 %shard_map.228 = (f32[512,768]{1,0:T(8,128)S(1)}, bf16[256,768]{1,0:T(8,128)(2,1)}, bf16[256,768]{1,0:T(8,128)(2,1)}, f32[8,768]{1,0:T(8,128)S(1)}) custom-call(s32[8]{0:T(128)S(1)} %copy-done.16, bf16[3,1024,384]{2,1,0:T(8,128)(2,1)S(1)} %copy-done.2, bf16[1024,768]{1,0:T(8,128)(2,1)S(1)} %copy-done, bf16[3,768,384]{2,1,0:T(8,128)(2,1)S(1)} %copy-done.8), custom_call_target="tpu_custom_call" | custom-call | bytes 15000000 | tf_op jit(solution)/shard_map/pallas_call | solution.py:223
  188.6 1.2 copy-done.10
  189.7 1.4 copy-done.12
  191.1 1.4 copy-done.13
  192.6 1.3 copy-done.14
  193.8 1.3 copy-done.15
  195.1 6.9 %shard_map.229 = (f32[512,768]{1,0:T(8,128)S(1)}, bf16[256,768]{1,0:T(8,128)(2,1)S(1)}, bf16[256,768]{1,0:T(8,128)(2,1)S(1)}, f32[8,768]{1,0:T(8,128)S(1)}) custom-call(s32[8]{0:T(128)S(1)} %copy-done.16, bf16[1024,768]{1,0:T(8,128)(2,1)S(1)} %copy-done.12, bf16[1024,768]{1,0:T(8,128)(2,1)S(1)} %copy-done.13, bf16[1024,768]{1,0:T(8,128)(2,1)S(1)} %copy-done, ...), custom_call_target="tpu_custom_call" | custom-call | bytes 18000000 | tf_op jit(solution)/shard_map/pallas_call | solution.py:223
  202.8 2.8 %collective-permute-done.16 = bf16[768,384]{1,0:T(8,128)(2,1)} collective-permute-done((bf16[768,384]{1,0:T(8,128)(2,1)}, bf16[768,384]{1,0:T(8,128)(2,1)}, u32[]{:S(2)}, u32[]{:S(2)}) %collective-permute-start.16) | collective-permute-done | bytes 589856 | tf_op jit(solution)/shard_map/ppermute | solution.py:677
  205.7 2.2 collective-permute-done.18
  208.8 2.0 add_convert_fusion.1
  210.9 1.3 collective-permute-start.27
  212.3 1.0 fusion.12
  213.3 1.1 collective-permute-start.28
  214.4 1.4 collective-permute-start.29
  215.8 2.8 %collective-permute-start.26 = (bf16[192,384]{1,0:T(8,128)(2,1)S(1)}, bf16[192,384]{1,0:T(8,128)(2,1)S(1)}, u32[]{:S(2)}, u32[]{:S(2)}) collective-permute-start(bf16[192,384]{1,0:T(8,128)(2,1)S(1)} %get-tuple-element.177), channel_id=1, source_target_pairs={{1,16},{3,18},{5,20},{7,22},{9,24},{11,26},{13,28},{15,30},{16,1},... | collective-permute-start | bytes 442376 | tf_op jit(solution)/shard_map/ppermute | solution.py:673
  219.4 5.2 %shard_map.230.own_ref = bf16[2,512,768]{2,1,0:T(8,128)(2,1)} custom-call(s32[8]{0:T(128)} %stack.63.flags.refs_0_, bf16[1024,768]{1,0:T(8,128)(2,1)} %maximum_select_fusion.rows_ref.refs_2_, bf16[1024,768]{1,0:T(8,128)(2,1)} %get-tuple-element.139.resid_ref, f32[512,768]{1,0:T(8,128)} %copy-done.10, f32[512,768]{1,0:T(8,128)} %copy-done.11, ...), custom_call_target="tpu_custom_call" | custom-call | bytes 9000000 | tf_op jit(solution)/shard_map/pallas_call | solution.py:223
  224.7 1.2 collective-permute-done.23
  226.8 2.1 collective-permute-done.24
  228.9 1.3 collective-permute-start.25
  230.2 1.7 collective-permute-done.25
  232.2 1.3 collective-permute-start.33
  233.5 5.6 %collective-permute-start.30 = (bf16[2,512,768]{2,1,0:T(8,128)(2,1)S(1)}, bf16[2,512,768]{2,1,0:T(8,128)(2,1)S(1)}, u32[]{:S(2)}, u32[]{:S(2)}) collective-permute-start(bf16[2,512,768]{2,1,0:T(8,128)(2,1)S(1)} %copy-done.7), channel_id=1, source_target_pairs={{1,16},{3,18},{5,20},{7,22},{9,24},{11,26},{13,28},{15,30},{16,1},... | collective-permute-start | bytes 4718600 | tf_op jit(solution)/shard_map/ppermute | solution.py:673
  239.0 2.5 collective-permute-done.33
  241.6 3.4 %collective-permute-start.34 = (bf16[2,192,1152]{2,1,0:T(8,128)(2,1)S(1)}, bf16[2,192,1152]{2,1,0:T(8,128)(2,1)S(1)}, u32[]{:S(2)}, u32[]{:S(2)}) collective-permute-start(bf16[2,192,1152]{2,1,0:T(8,128)(2,1)S(1)} %pad_maximum_fusion.3.here_ref), channel_id=1, source_target_pairs={{0,1},{1,0},{2,3},{3,2},{4,5},{5,4},{6,7},{7,6},{8,9},{9,8},{10,11... | collective-permute-start | bytes 2654216 | tf_op jit(solution)/shard_map/ppermute | solution.py:692
  245.0 1.1 collective-permute-start.31
  246.1 1.9 collective-permute-done.31
  248.1 3.9 %collective-permute-done.32 = f32[9,768]{1,0:T(8,128)S(1)} collective-permute-done((f32[9,768]{1,0:T(8,128)S(1)}, f32[9,768]{1,0:T(8,128)S(1)}, u32[]{:S(2)}, u32[]{:S(2)}) %collective-permute-start.32) | collective-permute-done | bytes 27680 | tf_op jit(solution)/shard_map/ppermute | solution.py:739
  253.3 2.5 shard_map.232
  255.8 1.4 collective-permute-done.30.got_ref
  257.1 2.1 shard_map.231
  (155 shorter events, 14.1 us)
Async XLA Ops:
  7.2 166.2 %reduce-scatter.7.cloned.1.call-start = ((), (), s32[]{:S(2)}) async-start(), calls=%async_computation.3 | async-start | bytes 2949120
  7.2 19.2 %collective-permute-start.2 = (s32[1,3]{1,0:T(1,128)}, s32[1,3]{1,0:T(1,128)S(1)}, u32[]{:S(2)}, u32[]{:S(2)}) collective-permute-start(s32[1,3]{1,0:T(1,128)} %param.16), channel_id=1, source_target_pairs={{0,1},{1,0},{2,3},{3,2},{4,5},{5,4},{6,7},{7,6},{8,9},{9,8},{10,11... | collective-permute-start | bytes 44 | tf_op jit(solution)/shard_map/ppermute | solution.py:692
  8.0 18.9 %collective-permute-start = (bf16[512,768]{1,0:T(8,128)(2,1)}, bf16[512,768]{1,0:T(8,128)(2,1)}, u32[]{:S(2)}, u32[]{:S(2)}) collective-permute-start(bf16[512,768]{1,0:T(8,128)(2,1)} %bitcast.47), channel_id=1, source_target_pairs={{1,16},{3,18},{5,20},{7,22},{9,24},{11,26},{13,28},{15,30},{16,1},... | collective-permute-start | bytes 2359304 | tf_op jit(solution)/shard_map/ppermute | solution.py:673
  11.0 30.2 %collective-permute-start.3 = (bf16[3,768,384]{2,1,0:T(8,128)(2,1)}, bf16[3,768,384]{2,1,0:T(8,128)(2,1)}, u32[]{:S(2)}, u32[]{:S(2)}) collective-permute-start(bf16[3,768,384]{2,1,0:T(8,128)(2,1)} %w_own.1), channel_id=1, source_target_pairs={{1,16},{3,18},{5,20},{7,22},{9,24},{11,26},{13,28},{15,30},{16,1},... | collective-permute-start | bytes 5308424 | tf_op jit(solution)/shard_map/ppermute | solution.py:673
  13.6 3.0 %copy-start.19 = (bf16[768,1536]{1,0:T(8,128)(2,1)S(1)}, bf16[768,1536]{1,0:T(8,128)(2,1)}, u32[]{:S(2)}) copy-start(bf16[768,1536]{1,0:T(8,128)(2,1)} %refs_6_.1) | copy-start | bytes 7077892
  16.5 1.7 copy-start.38
  16.5 1.7 copy-start.22
  16.6 2.0 copy-start.27
  22.9 3.6 %copy-start.39 = (s32[1,3]{1,0:T(1,128)S(1)}, s32[1,3]{1,0:T(1,128)}, u32[]{:S(2)}) copy-start(s32[1,3]{1,0:T(1,128)} %param.16) | copy-start | bytes 40
  22.9 4.0 %copy-start.26 = (bf16[1,512,768]{2,1,0:T(8,128)(2,1)S(1)}, bf16[1,512,768]{2,1,0:T(8,128)(2,1)}, u32[]{:S(2)}) copy-start(bf16[1,512,768]{2,1,0:T(8,128)(2,1)} %param.13) | copy-start | bytes 2359300
  28.1 5.0 %collective-permute-start.1 = (bf16[512,768]{1,0:T(8,128)(2,1)S(1)}, bf16[512,768]{1,0:T(8,128)(2,1)S(1)}, u32[]{:S(2)}, u32[]{:S(2)}) collective-permute-start(bf16[512,768]{1,0:T(8,128)(2,1)S(1)} %broadcast_select_fusion.1), channel_id=1, source_target_pairs={{0,1},{1,0},{2,3},{3,2},{4,5},{5,4},{6,7},{7,6},{8,9},{9,8},{10,11... | collective-permute-start | bytes 2359304 | tf_op jit(solution)/shard_map/ppermute | solution.py:692
  35.0 28.4 %collective-permute-start.4 = (bf16[896,768]{1,0:T(8,128)(2,1)S(1)}, bf16[896,768]{1,0:T(8,128)(2,1)S(1)}, u32[]{:S(2)}, u32[]{:S(2)}) collective-permute-start(bf16[896,768]{1,0:T(8,128)(2,1)S(1)} %pad_maximum_fusion.1), channel_id=1, source_target_pairs={{1,16},{3,18},{5,20},{7,22},{9,24},{11,26},{13,28},{15,30},{16,1},... | collective-permute-start | bytes 4128776 | tf_op jit(solution)/shard_map/ppermute | solution.py:673
  38.0 42.6 %collective-permute-start.7 = (bf16[1536,768]{1,0:T(8,128)(2,1)}, bf16[1536,768]{1,0:T(8,128)(2,1)}, u32[]{:S(2)}, u32[]{:S(2)}) collective-permute-start(bf16[1536,768]{1,0:T(8,128)(2,1)} %pad_maximum_fusion), channel_id=1, source_target_pairs={{1,16},{3,18},{5,20},{7,22},{9,24},{11,26},{13,28},{15,30},{16,1},... | collective-permute-start | bytes 7077896 | tf_op jit(solution)/shard_map/ppermute | solution.py:673
  64.5 6.9 %copy-start.20 = (bf16[896,768]{1,0:T(8,128)(2,1)}, bf16[896,768]{1,0:T(8,128)(2,1)S(1)}, u32[]{:S(2)}) copy-start(bf16[896,768]{1,0:T(8,128)(2,1)S(1)} %broadcast_select_fusion) | copy-start | bytes 4128772
  65.5 10.1 %copy-start.3 = (bf16[1024,768]{1,0:T(8,128)(2,1)}, bf16[1024,768]{1,0:T(8,128)(2,1)S(1)}, u32[]{:S(2)}) copy-start(bf16[1024,768]{1,0:T(8,128)(2,1)S(1)} %convolution_convert_fusion.refs_3_.own_ref) | copy-start | bytes 4718596
  65.5 15.1 %collective-permute-start.5 = (bf16[1024,768]{1,0:T(8,128)(2,1)S(1)}, bf16[1024,768]{1,0:T(8,128)(2,1)S(1)}, u32[]{:S(2)}, u32[]{:S(2)}) collective-permute-start(bf16[1024,768]{1,0:T(8,128)(2,1)S(1)} %convolution_convert_fusion.refs_3_.own_ref), channel_id=1, source_target_pairs={{0,1},{1,0},{2,3},{3,2},{4,5},{5,4},{6,7},{7,6},{8,9},{9,8},{10,11... | collective-permute-start | bytes 4718600 | tf_op jit(solution)/shard_map/ppermute | solution.py:692
  65.6 34.9 %collective-permute-start.8 = (bf16[768,768]{1,0:T(8,128)(2,1)}, bf16[768,768]{1,0:T(8,128)(2,1)S(1)}, u32[]{:S(2)}, u32[]{:S(2)}) collective-permute-start(bf16[768,768]{1,0:T(8,128)(2,1)} %get-tuple-element.115), channel_id=1, source_target_pairs={{1,16},{3,18},{5,20},{7,22},{9,24},{11,26},{13,28},{15,30},{16,1},... | collective-permute-start | bytes 3538952 | tf_op jit(solution)/shard_map/ppermute | solution.py:673
  68.6 37.1 %collective-permute-start.9 = (bf16[768,768]{1,0:T(8,128)(2,1)}, bf16[768,768]{1,0:T(8,128)(2,1)S(1)}, u32[]{:S(2)}, u32[]{:S(2)}) collective-permute-start(bf16[768,768]{1,0:T(8,128)(2,1)} %get-tuple-element.116), channel_id=1, source_target_pairs={{1,16},{3,18},{5,20},{7,22},{9,24},{11,26},{13,28},{15,30},{16,1},... | collective-permute-start | bytes 3538952 | tf_op jit(solution)/shard_map/ppermute | solution.py:673
  71.4 2.4 collective-permute-start.6
  100.5 5.3 %copy-start.24 = (bf16[768,768]{1,0:T(8,128)(2,1)}, bf16[768,768]{1,0:T(8,128)(2,1)S(1)}, u32[]{:S(2)}) copy-start(bf16[768,768]{1,0:T(8,128)(2,1)S(1)} %collective-permute-done.8.refs_8_) | copy-start | bytes 3538948
  105.8 106.5 %reduce-scatter.5.cloned.1.call-start = ((), (), s32[]{:S(2)}) async-start(), calls=%async_computation.2 | async-start | bytes 1474560 | tf_op jit(solution)/shard_map/reduce_scatter | solution.py:719
  123.0 7.0 %collective-permute-start.10 = (bf16[1024,768]{1,0:T(8,128)(2,1)}, bf16[1024,768]{1,0:T(8,128)(2,1)S(1)}, u32[]{:S(2)}, u32[]{:S(2)}) collective-permute-start(bf16[1024,768]{1,0:T(8,128)(2,1)} %get-tuple-element.117.back_own), channel_id=1, source_target_pairs={{0,1},{1,0},{2,3},{3,2},{4,5},{5,4},{6,7},{7,6},{8,9},{9,8},{10,11... | collective-permute-start | bytes 4718600 | tf_op jit(solution)/shard_map/ppermute | solution.py:692
  123.1 41.3 %collective-permute-start.11 = (bf16[768,384]{1,0:T(8,128)(2,1)}, bf16[768,384]{1,0:T(8,128)(2,1)S(1)}, u32[]{:S(2)}, u32[]{:S(2)}) collective-permute-start(bf16[768,384]{1,0:T(8,128)(2,1)} %get-tuple-element.119), channel_id=1, source_target_pairs={{1,16},{3,18},{5,20},{7,22},{9,24},{11,26},{13,28},{15,30},{16,1},... | collective-permute-start | bytes 1769480 | tf_op jit(solution)/shard_map/ppermute | solution.py:677
  126.2 38.2 %collective-permute-start.12 = (bf16[768,384]{1,0:T(8,128)(2,1)}, bf16[768,384]{1,0:T(8,128)(2,1)S(1)}, u32[]{:S(2)}, u32[]{:S(2)}) collective-permute-start(bf16[768,384]{1,0:T(8,128)(2,1)} %get-tuple-element.120), channel_id=1, source_target_pairs={{0,1},{1,17},{2,3},{3,19},{4,5},{5,21},{6,7},{7,23},{8,9},{9,25},{... | collective-permute-start | bytes 1769480 | tf_op jit(solution)/shard_map/ppermute | solution.py:677
  126.2 38.2 %collective-permute-start.13 = (bf16[768,384]{1,0:T(8,128)(2,1)}, bf16[768,384]{1,0:T(8,128)(2,1)S(1)}, u32[]{:S(2)}, u32[]{:S(2)}) collective-permute-start(bf16[768,384]{1,0:T(8,128)(2,1)} %get-tuple-element.121), channel_id=1, source_target_pairs={{0,2},{1,18},{2,0},{3,16},{4,6},{5,22},{6,4},{7,20},{8,10},{9,26},... | collective-permute-start | bytes 1769480 | tf_op jit(solution)/shard_map/ppermute | solution.py:677
  127.8 36.7 %collective-permute-start.14 = (bf16[768,384]{1,0:T(8,128)(2,1)}, bf16[768,384]{1,0:T(8,128)(2,1)S(1)}, u32[]{:S(2)}, u32[]{:S(2)}) collective-permute-start(bf16[768,384]{1,0:T(8,128)(2,1)} %get-tuple-element.122), channel_id=1, source_target_pairs={{0,3},{1,19},{2,1},{3,17},{4,7},{5,23},{6,5},{7,21},{8,11},{9,27},... | collective-permute-start | bytes 1769480 | tf_op jit(solution)/shard_map/ppermute | solution.py:677
  164.4 7.8 %copy-start.29 = (bf16[768,384]{1,0:T(8,128)(2,1)S(1)}, bf16[768,384]{1,0:T(8,128)(2,1)}, u32[]{:S(2)}) copy-start(bf16[768,384]{1,0:T(8,128)(2,1)} %get-tuple-element.119) | copy-start | bytes 1769476
  173.4 7.6 %copy-start.34 = (f32[8,768]{1,0:T(8,128)S(1)}, f32[8,768]{1,0:T(8,128)}, u32[]{:S(2)}) copy-start(f32[8,768]{1,0:T(8,128)} %get-tuple-element.138) | copy-start | bytes 73732
  173.4 7.6 %copy-start = (bf16[1024,768]{1,0:T(8,128)(2,1)S(1)}, bf16[1024,768]{1,0:T(8,128)(2,1)}, u32[]{:S(2)}) copy-start(bf16[1024,768]{1,0:T(8,128)(2,1)} %maximum_select_fusion.rows_ref.refs_2_) | copy-start | bytes 4718596
  173.4 7.6 %copy-start.8 = (bf16[3,768,384]{2,1,0:T(8,128)(2,1)S(1)}, bf16[3,768,384]{2,1,0:T(8,128)(2,1)}, u32[]{:S(2)}) copy-start(bf16[3,768,384]{2,1,0:T(8,128)(2,1)} %get-tuple-element.128.weight) | copy-start | bytes 5308420
  173.4 7.6 %copy-start.16 = (s32[8]{0:T(128)S(1)}, s32[8]{0:T(128)}, u32[]{:S(2)}) copy-start(s32[8]{0:T(128)} %stack.63.flags.refs_0_) | copy-start | bytes 100
  175.9 26.9 %collective-permute-start.15 = (bf16[768,384]{1,0:T(8,128)(2,1)}, bf16[768,384]{1,0:T(8,128)(2,1)}, u32[]{:S(2)}, u32[]{:S(2)}) collective-permute-start(bf16[768,384]{1,0:T(8,128)(2,1)} %get-tuple-element.126), channel_id=1, source_target_pairs={{1,16},{3,18},{5,20},{7,22},{9,24},{11,26},{13,28},{15,30},{16,1},... | collective-permute-start | bytes 1769480 | tf_op jit(solution)/shard_map/ppermute | solution.py:677
  179.7 26.0 %collective-permute-start.16 = (bf16[768,384]{1,0:T(8,128)(2,1)}, bf16[768,384]{1,0:T(8,128)(2,1)}, u32[]{:S(2)}, u32[]{:S(2)}) collective-permute-start(bf16[768,384]{1,0:T(8,128)(2,1)} %get-tuple-element.145), channel_id=1, source_target_pairs={{0,1},{1,17},{2,3},{3,19},{4,5},{5,21},{6,7},{7,23},{8,9},{9,25},{... | collective-permute-start | bytes 1769480 | tf_op jit(solution)/shard_map/ppermute | solution.py:677
  179.7 26.0 %collective-permute-start.17 = (bf16[768,384]{1,0:T(8,128)(2,1)}, bf16[768,384]{1,0:T(8,128)(2,1)}, u32[]{:S(2)}, u32[]{:S(2)}) collective-permute-start(bf16[768,384]{1,0:T(8,128)(2,1)} %get-tuple-element.146), channel_id=1, source_target_pairs={{0,2},{1,18},{2,0},{3,16},{4,6},{5,22},{6,4},{7,20},{8,10},{9,26},... | collective-permute-start | bytes 1769480 | tf_op jit(solution)/shard_map/ppermute | solution.py:677
  180.7 27.2 %collective-permute-start.18 = (bf16[768,384]{1,0:T(8,128)(2,1)}, bf16[768,384]{1,0:T(8,128)(2,1)}, u32[]{:S(2)}, u32[]{:S(2)}) collective-permute-start(bf16[768,384]{1,0:T(8,128)(2,1)} %get-tuple-element.147), channel_id=1, source_target_pairs={{0,3},{1,19},{2,1},{3,17},{4,7},{5,23},{6,5},{7,21},{8,11},{9,27},... | collective-permute-start | bytes 1769480 | tf_op jit(solution)/shard_map/ppermute | solution.py:677
  181.0 1.7 copy-start.2
  182.7 7.0 %copy-start.1 = (bf16[1024,768]{1,0:T(8,128)(2,1)S(1)}, bf16[1024,768]{1,0:T(8,128)(2,1)}, u32[]{:S(2)}) copy-start(bf16[1024,768]{1,0:T(8,128)(2,1)} %maximum_select_fusion.1.refs_5_.cot_ref) | copy-start | bytes 4718596
  182.7 7.0 %copy-start.4 = (bf16[1024,768]{1,0:T(8,128)(2,1)S(1)}, bf16[1024,768]{1,0:T(8,128)(2,1)}, u32[]{:S(2)}) copy-start(bf16[1024,768]{1,0:T(8,128)(2,1)} %copy-done.3) | copy-start | bytes 4718596
  182.7 7.0 %copy-start.6 = (bf16[1024,768]{1,0:T(8,128)(2,1)S(1)}, bf16[1024,768]{1,0:T(8,128)(2,1)}, u32[]{:S(2)}) copy-start(bf16[1024,768]{1,0:T(8,128)(2,1)} %copy-done.5) | copy-start | bytes 4718596
  195.1 13.7 %copy-start.28 = (bf16[768,384]{1,0:T(8,128)(2,1)S(1)}, bf16[768,384]{1,0:T(8,128)(2,1)}, u32[]{:S(2)}) copy-start(bf16[768,384]{1,0:T(8,128)(2,1)} %get-tuple-element.126) | copy-start | bytes 1769476
  202.0 8.8 %copy-start.11 = (f32[512,768]{1,0:T(8,128)}, f32[512,768]{1,0:T(8,128)S(1)}, u32[]{:S(2)}) copy-start(f32[512,768]{1,0:T(8,128)S(1)} %get-tuple-element.154.block_keep) | copy-start | bytes 4718596
  207.8 5.5 %collective-permute-start.19 = (bf16[256,768]{1,0:T(8,128)(2,1)}, bf16[256,768]{1,0:T(8,128)(2,1)S(1)}, u32[]{:S(2)}, u32[]{:S(2)}) collective-permute-start(bf16[256,768]{1,0:T(8,128)(2,1)} %get-tuple-element.155), channel_id=1, source_target_pairs={{0,1},{1,0},{2,3},{3,2},{4,5},{5,4},{6,7},{7,6},{8,9},{9,8},{10,11... | collective-permute-start | bytes 1179656 | tf_op jit(solution)/shard_map/ppermute | solution.py:692
  208.2 6.2 %collective-permute-start.20 = (bf16[256,768]{1,0:T(8,128)(2,1)}, bf16[256,768]{1,0:T(8,128)(2,1)S(1)}, u32[]{:S(2)}, u32[]{:S(2)}) collective-permute-start(bf16[256,768]{1,0:T(8,128)(2,1)} %get-tuple-element.156), channel_id=1, source_target_pairs={{0,1},{1,0},{2,3},{3,2},{4,5},{5,4},{6,7},{7,6},{8,9},{9,8},{10,11... | collective-permute-start | bytes 1179656 | tf_op jit(solution)/shard_map/ppermute | solution.py:692
  208.3 7.5 %collective-permute-start.21 = (bf16[256,768]{1,0:T(8,128)(2,1)S(1)}, bf16[256,768]{1,0:T(8,128)(2,1)S(1)}, u32[]{:S(2)}, u32[]{:S(2)}) collective-permute-start(bf16[256,768]{1,0:T(8,128)(2,1)S(1)} %get-tuple-element.157), channel_id=1, source_target_pairs={{0,1},{1,0},{2,3},{3,2},{4,5},{5,4},{6,7},{7,6},{8,9},{9,8},{10,11... | collective-permute-start | bytes 1179656 | tf_op jit(solution)/shard_map/ppermute | solution.py:692
  208.7 10.0 %collective-permute-start.22 = (bf16[256,768]{1,0:T(8,128)(2,1)S(1)}, bf16[256,768]{1,0:T(8,128)(2,1)S(1)}, u32[]{:S(2)}, u32[]{:S(2)}) collective-permute-start(bf16[256,768]{1,0:T(8,128)(2,1)S(1)} %get-tuple-element.158), channel_id=1, source_target_pairs={{0,1},{1,0},{2,3},{3,2},{4,5},{5,4},{6,7},{7,6},{8,9},{9,8},{10,11... | collective-permute-start | bytes 1179656 | tf_op jit(solution)/shard_map/ppermute | solution.py:692
  210.9 21.0 %collective-permute-start.27 = (bf16[192,384]{1,0:T(8,128)(2,1)S(1)}, bf16[192,384]{1,0:T(8,128)(2,1)S(1)}, u32[]{:S(2)}, u32[]{:S(2)}) collective-permute-start(bf16[192,384]{1,0:T(8,128)(2,1)S(1)} %get-tuple-element.230), channel_id=1, source_target_pairs={{0,4},{4,8},{8,12},{12,0},{1,5},{5,9},{9,13},{13,1},{2,6},{6,10},{... | collective-permute-start | bytes 442376 | tf_op jit(solution)/shard_map/ppermute | solution.py:731
  213.3 5.4 %copy-start.30 = (bf16[256,768]{1,0:T(8,128)(2,1)}, bf16[256,768]{1,0:T(8,128)(2,1)S(1)}, u32[]{:S(2)}) copy-start(bf16[256,768]{1,0:T(8,128)(2,1)S(1)} %collective-permute-done.19.got_first) | copy-start | bytes 1179652
  213.3 18.7 %collective-permute-start.28 = (bf16[192,384]{1,0:T(8,128)(2,1)S(1)}, bf16[192,384]{1,0:T(8,128)(2,1)S(1)}, u32[]{:S(2)}, u32[]{:S(2)}) collective-permute-start(bf16[192,384]{1,0:T(8,128)(2,1)S(1)} %get-tuple-element.229), channel_id=1, source_target_pairs={{0,8},{4,12},{8,0},{12,4},{1,9},{5,13},{9,1},{13,5},{2,10},{6,14},... | collective-permute-start | bytes 442376 | tf_op jit(solution)/shard_map/ppermute | solution.py:731
  214.4 4.3 %copy-start.31 = (bf16[256,768]{1,0:T(8,128)(2,1)}, bf16[256,768]{1,0:T(8,128)(2,1)S(1)}, u32[]{:S(2)}) copy-start(bf16[256,768]{1,0:T(8,128)(2,1)S(1)} %collective-permute-done.20.got_second) | copy-start | bytes 1179652
  214.4 17.5 %collective-permute-start.29 = (bf16[192,384]{1,0:T(8,128)(2,1)S(1)}, bf16[192,384]{1,0:T(8,128)(2,1)S(1)}, u32[]{:S(2)}, u32[]{:S(2)}) collective-permute-start(bf16[192,384]{1,0:T(8,128)(2,1)S(1)} %get-tuple-element.228), channel_id=1, source_target_pairs={{0,12},{4,0},{8,4},{12,8},{1,13},{5,1},{9,5},{13,9},{2,14},{6,2},{... | collective-permute-start | bytes 442376 | tf_op jit(solution)/shard_map/ppermute | solution.py:731
  215.8 2.9 %copy-start.32 = (bf16[256,768]{1,0:T(8,128)(2,1)}, bf16[256,768]{1,0:T(8,128)(2,1)S(1)}, u32[]{:S(2)}) copy-start(bf16[256,768]{1,0:T(8,128)(2,1)S(1)} %collective-permute-done.21.block_first) | copy-start | bytes 1179652
  215.8 16.1 %collective-permute-start.26 = (bf16[192,384]{1,0:T(8,128)(2,1)S(1)}, bf16[192,384]{1,0:T(8,128)(2,1)S(1)}, u32[]{:S(2)}, u32[]{:S(2)}) collective-permute-start(bf16[192,384]{1,0:T(8,128)(2,1)S(1)} %get-tuple-element.177), channel_id=1, source_target_pairs={{1,16},{3,18},{5,20},{7,22},{9,24},{11,26},{13,28},{15,30},{16,1},... | collective-permute-start | bytes 442376 | tf_op jit(solution)/shard_map/ppermute | solution.py:673
  224.7 8.8 %copy-start.7 = (bf16[2,512,768]{2,1,0:T(8,128)(2,1)S(1)}, bf16[2,512,768]{2,1,0:T(8,128)(2,1)}, u32[]{:S(2)}) copy-start(bf16[2,512,768]{2,1,0:T(8,128)(2,1)} %shard_map.230.own_ref) | copy-start | bytes 4718596
  224.7 1.2 collective-permute-start.23
  225.9 3.0 %collective-permute-start.24 = (f32[9,768]{1,0:T(8,128)S(1)}, f32[9,768]{1,0:T(8,128)S(1)}, u32[]{:S(2)}, u32[]{:S(2)}) collective-permute-start(f32[9,768]{1,0:T(8,128)S(1)} %add.107), channel_id=1, source_target_pairs={{0,16},{16,0},{1,17},{17,1},{2,18},{18,2},{3,19},{19,3},{4,20},{20... | collective-permute-start | bytes 82952 | tf_op jit(solution)/shard_map/ppermute | solution.py:739
  228.9 3.0 %collective-permute-start.25 = (f32[9,768]{1,0:T(8,128)S(1)}, f32[9,768]{1,0:T(8,128)S(1)}, u32[]{:S(2)}, u32[]{:S(2)}) collective-permute-start(f32[9,768]{1,0:T(8,128)S(1)} %add.108), channel_id=1, source_target_pairs={{0,2},{2,0},{1,3},{3,1},{4,6},{6,4},{5,7},{7,5},{8,10},{10,8},{9,1... | collective-permute-start | bytes 82952 | tf_op jit(solution)/shard_map/ppermute | solution.py:739
  232.1 21.1 %copy-start.17 = (s32[8]{0:T(128)S(1)}, s32[8]{0:T(128)}, u32[]{:S(2)}) copy-start(s32[8]{0:T(128)} %stack.63.flags.refs_0_) | copy-start | bytes 100
  232.2 9.3 %collective-permute-start.33 = (bf16[192,1152]{1,0:T(8,128)(2,1)S(1)}, bf16[192,1152]{1,0:T(8,128)(2,1)S(1)}, u32[]{:S(2)}, u32[]{:S(2)}) collective-permute-start(bf16[192,1152]{1,0:T(8,128)(2,1)S(1)} %get-tuple-element.233), channel_id=1, source_target_pairs={{0,2},{2,0},{1,3},{3,1},{4,6},{6,4},{5,7},{7,5},{8,10},{10,8},{9,1... | collective-permute-start | bytes 1327112 | tf_op jit(solution)/shard_map/ppermute | solution.py:688
  233.5 23.7 %collective-permute-start.30 = (bf16[2,512,768]{2,1,0:T(8,128)(2,1)S(1)}, bf16[2,512,768]{2,1,0:T(8,128)(2,1)S(1)}, u32[]{:S(2)}, u32[]{:S(2)}) collective-permute-start(bf16[2,512,768]{2,1,0:T(8,128)(2,1)S(1)} %copy-done.7), channel_id=1, source_target_pairs={{1,16},{3,18},{5,20},{7,22},{9,24},{11,26},{13,28},{15,30},{16,1},... | collective-permute-start | bytes 4718600 | tf_op jit(solution)/shard_map/ppermute | solution.py:673
  241.5 15.6 %copy-start.9 = (f32[512,768]{1,0:T(8,128)S(1)}, f32[512,768]{1,0:T(8,128)}, u32[]{:S(2)}) copy-start(f32[512,768]{1,0:T(8,128)} %get-tuple-element.99.part_ref) | copy-start | bytes 4718596
  241.5 15.6 %copy-start.18 = (f32[5]{0:T(128)S(1)}, f32[5]{0:T(128)}, u32[]{:S(2)}) copy-start(f32[5]{0:T(128)} %weight_ref.3) | copy-start | bytes 64
  241.6 11.6 %collective-permute-start.34 = (bf16[2,192,1152]{2,1,0:T(8,128)(2,1)S(1)}, bf16[2,192,1152]{2,1,0:T(8,128)(2,1)S(1)}, u32[]{:S(2)}, u32[]{:S(2)}) collective-permute-start(bf16[2,192,1152]{2,1,0:T(8,128)(2,1)S(1)} %pad_maximum_fusion.3.here_ref), channel_id=1, source_target_pairs={{0,1},{1,0},{2,3},{3,2},{4,5},{5,4},{6,7},{7,6},{8,9},{9,8},{10,11... | collective-permute-start | bytes 2654216 | tf_op jit(solution)/shard_map/ppermute | solution.py:692
  245.0 3.0 %collective-permute-start.31 = (f32[9,768]{1,0:T(8,128)S(1)}, f32[9,768]{1,0:T(8,128)S(1)}, u32[]{:S(2)}, u32[]{:S(2)}) collective-permute-start(f32[9,768]{1,0:T(8,128)S(1)} %add.109), channel_id=1, source_target_pairs={{0,4},{4,0},{8,12},{12,8},{1,5},{5,1},{9,13},{13,9},{2,6},{6,2},{1... | collective-permute-start | bytes 82952 | tf_op jit(solution)/shard_map/ppermute | solution.py:739
  248.0 4.0 %collective-permute-start.32 = (f32[9,768]{1,0:T(8,128)S(1)}, f32[9,768]{1,0:T(8,128)S(1)}, u32[]{:S(2)}, u32[]{:S(2)}) collective-permute-start(f32[9,768]{1,0:T(8,128)S(1)} %add.120), channel_id=1, source_target_pairs={{0,8},{4,12},{8,0},{12,4},{1,9},{5,13},{9,1},{13,5},{2,10},{6,14},... | collective-permute-start | bytes 82952 | tf_op jit(solution)/shard_map/ppermute | solution.py:739
  (13 other events, 16.8 us)
Sparse Core Ops, SparseCore 0:
  105.9 44.8 reduce-scatter.6
  176.1 28.2 reduce-scatter.4

commit v6 on v5

--- a/solution.py
+++ b/solution.py
@@ -116,8 +116,10 @@
 
 
 def attend_back_kernel(
-    reach, apart_ref, member_ref, cos_ref, sin_ref, q_ref, k_ref, v_ref, g_ref, out_ref, keys, keys_t, key_acc, value_acc
+    reach, flags, apart_ref, member_ref, cos_ref, sin_ref, q_ref, k_ref, v_ref, g_ref, turned_ref, out_grad_ref,
+    out_ref, *refs,
 ):
+    owned, (keys, keys_t, key_acc, value_acc) = refs[:4], refs[4:]
     whole = q_ref.shape[0]
     lane = lax.broadcasted_iota(jnp.int32, (BLOCK, LANES), 1) // HEAD_DIM
     keys[:, :LANES] = k_ref[...]
@@ -164,29 +166,53 @@
 
     lax.fori_loop(0, whole // BLOCK, finish, 0)
 
-
-def attend_back(apart, member, cos, sin, projected, grad_mixed, reach):
+    def store(piece, at, low):
+        slot = 2 * (flags[2] ^ (piece // 2)) + (flags[3] ^ (piece % 2))
+        for j, ref in enumerate(owned):
+
+            @pl.when(slot == j)
+            def _():
+                ref[at, :] = low
+
+    def weigh(i, carry):
+        at = block_at(i)
+        rows = turned_ref[at, :]
+        both = dot(rows, jnp.concatenate([out_ref[0], out_ref[1]], axis=1)).astype(jnp.bfloat16)
+        store(0, at, both[:, :LANES])
+        store(1, at, both[:, LANES:])
+        store(2, at, dot(rows, out_ref[2]).astype(jnp.bfloat16))
+        store(3, at, out_grad_ref[at, :])
+        return carry
+
+    lax.fori_loop(0, turned_ref.shape[0] // BLOCK, weigh, 0)
+
+
+def attend_back(flags, apart, member, cos, sin, projected, grad_mixed, turned, out_grad, reach):
     count, whole, width = projected.shape
+    depth = turned.shape[0]
 
     def block(c):
-        return pl.BlockSpec((None, whole, LANES), lambda p: (c, 0, p))
-
-    table = pl.BlockSpec((whole, LANES), lambda p: (0, 0))
-    return pl.pallas_call(
+        return projected, (None, whole, LANES), lambda p, flags: (c, 0, p)
+
+    def columns(field):
+        return field, (field.shape[0], LANES), lambda p, flags: (0, p)
+
+    low = jnp.bfloat16
+    piece = ((depth, width), low, (depth, LANES), lambda p, flags: (0, p))
+    return streamed(
         functools.partial(attend_back_kernel, reach),
-        grid=(width // LANES,),
-        in_specs=[table] * 4 + [block(0), block(1), block(2), pl.BlockSpec((whole, LANES), lambda p: (0, p))],
-        out_specs=pl.BlockSpec((count, whole, LANES), lambda p: (0, 0, p)),
-        out_shape=jax.ShapeDtypeStruct((count, whole, width), jnp.bfloat16),
-        scratch_shapes=[
-            pltpu.VMEM((whole, 2 * LANES), jnp.bfloat16),
-            pltpu.VMEM((LANES, whole), jnp.bfloat16),
-            pltpu.VMEM((whole, LANES), jnp.float32),
-            pltpu.VMEM((whole, LANES), jnp.float32),
+        width // LANES,
+        [flags],
+        [apart, member, cos, sin, block(0), block(1), block(2), columns(grad_mixed), turned, columns(out_grad)],
+        [((count, whole, width), low, (count, whole, LANES), lambda p, flags: (0, 0, p))] + [piece] * 4,
+        [
+            ((whole, 2 * LANES), low),
+            ((LANES, whole), low),
+            ((whole, LANES), jnp.float32),
+            ((whole, LANES), jnp.float32),
         ],
-        compiler_params=pltpu.CompilerParams(vmem_limit_bytes=ROOM),
-        cost_estimate=lasting(22),
-    )(apart, member, cos, sin, projected, projected, projected, grad_mixed)
+        28,
+    )
 
 
 ROWS = 256
@@ -252,10 +278,13 @@
     return field * cos + crossed * sin
 
 
-def project_kernel(flags, rows_ref, cos_ref, sin_ref, vectors, w_own, w_got, out_ref, turned_ref, weight_ref):
+def project_kernel(flags, rows_ref, cos_ref, sin_ref, vectors, w_own, w_near, w_far, out_ref, turned_ref, weight_ref):
     @pl.when(pl.program_id(0) == 0)
     def _():
-        weight_ref[...] = jnp.where(flags[0] == 1, w_own[...], w_got[...])
+        half = w_near.shape[1]
+        for index, got in ((flags[2], w_near), (1 - flags[2], w_far)):
+            at = pl.ds(pl.multiple_of(index * half, half), half)
+            weight_ref[:, at, :] = jnp.where(flags[0] == 1, w_own[:, at, :], got[...])
 
     unit, unused = norm_parts(rows_ref[...].astype(jnp.float32))
     norm = unit * vectors[0:1, :] + vectors[1:2, :]
@@ -271,7 +300,7 @@
                 out_ref[c, :, lanes] = turn(field[:, lanes], cos_ref[...], sin_ref[...]).astype(jnp.bfloat16)
 
 
-def project(flags, rows, vectors, cos, sin, w_own, w_got):
+def project(flags, rows, vectors, cos, sin, w_own, w_near, w_far):
     whole, width = rows.shape
     count, unused, columns = w_own.shape
     low = jnp.bfloat16
@@ -279,7 +308,7 @@
         project_kernel,
         whole // ROWS,
         [flags],
-        [by_rows(rows, ROWS), by_rows(cos, ROWS), by_rows(sin, ROWS), vectors, w_own, w_got],
+        [by_rows(rows, ROWS), by_rows(cos, ROWS), by_rows(sin, ROWS), vectors, w_own, w_near, w_far],
         [
             ((count, whole, columns), low, (count, ROWS, columns), lambda i, flags: (0, i, 0)),
             ((width, whole), low, (width, ROWS), lambda i, flags: (0, i)),
@@ -340,7 +369,7 @@
         if early:
             pieces[p, at, :] = low
             return
-        slot = 2 * (flags[2] ^ (p % 2)) + (flags[7] ^ (p // 2))
+        slot = 2 * (flags[2] ^ (p % 2)) + (flags[3] ^ (p // 2))
         for j, piece in enumerate(pieces):
 
             @pl.when(slot == j)
@@ -488,7 +517,7 @@
         sums_ref[1:2, :] += jnp.sum(back, axis=0, keepdims=True)
 
 
-def middle(flags, weight, fields, mixed, vectors, w_out):
+def middle(flags, weight, fields, mixed, vectors, bundle):
     whole, width = fields[0].shape
     columns = mixed.shape[1]
     low = jnp.bfloat16
@@ -497,7 +526,8 @@
         middle_kernel,
         whole // ROWS,
         [flags, weight],
-        [by_rows(field, ROWS) for field in (*fields, mixed)] + [vectors, w_out],
+        [by_rows(field, ROWS) for field in (*fields, mixed)]
+        + [vectors, (bundle, (columns, width), lambda i, *scalars: (0, 0))],
         [
             ((whole, width), low, (ROWS, width), in_order),
             ((whole, columns), low, (ROWS, columns), in_order),
@@ -506,28 +536,6 @@
         ],
         [((width, columns), jnp.float32)],
         8,
-    )
-
-
-def weigh_kernel(flags, turned_ref, out_grad_ref, grad_ref, *out_refs):
-    last = grad_ref.shape[0]
-    for j, out_ref in enumerate(out_refs):
-        piece = flags[3 + j]
-
-        @pl.when(piece < last)
-        def _():
-            out_ref[...] = dot(turned_ref[...], grad_ref[jnp.minimum(piece, last - 1)]).astype(jnp.bfloat16)
-
-        @pl.when(piece == last)
-        def _():
-            out_ref[...] = out_grad_ref[...]
-
-
-def weigh(flags, turned, grad, out_grad):
-    width, columns = turned.shape[0], grad.shape[2]
-    piece = ((width, columns), jnp.bfloat16, (ROWS, columns), lambda i, flags: (i, 0))
-    return streamed(
-        weigh_kernel, width // ROWS, [flags], [by_rows(turned, ROWS), by_rows(out_grad, ROWS), grad], [piece] * 4, [], 4
     )
 
 
@@ -682,6 +690,10 @@
             lambda t, d, k, c: (c, d, k ^ other_far, t ^ other_tp),
         ),
     )
+
+
+def swap_far_away(field):
+    return lax.ppermute(field, AXES, moves(away, lambda t, d, k, c: (t, d, 1 - k, c)))
 
 
 def swap_far(field):
@@ -761,11 +773,11 @@
     hist_count = history.shape[0]
     part, far, near = lax.axis_index("tp"), lax.axis_index("far"), lax.axis_index("near")
     same = near == part
-    pieces = [2 * (far ^ a) + (part ^ b) for a in range(2) for b in range(2)]
-    flags = jnp.stack([same.astype(jnp.int32), near, far, *pieces, part])
+    flags = jnp.stack([same.astype(jnp.int32), near, far, part])
 
     input_got = swap_diagonal(layer_input[0])
-    qkv_got = swap_diagonal(w_qkv)
+    qkv_near = swap_diagonal(part_of(w_qkv, far, 1))
+    qkv_far = swap_far_away(qkv_near)
     early_got = jnp.concatenate([part_of(w_up, 0, 1), part_of(w_down, 0, 0)], axis=0)
     late_up, late_down = part_of(w_up, 1, 1), part_of(w_down, 1, 0)
     last_own = jnp.concatenate([w_out, cotangent[0]], axis=0)
@@ -794,7 +806,7 @@
     early_got = swap_diagonal(early_got)
     last_got = swap_diagonal(last_own)
     projected, norm_one_t, weight_qkv = project(
-        flags, layer_rows, vectors, cos_table, sin_table, w_qkv, qkv_got
+        flags, layer_rows, vectors, cos_table, sin_table, w_qkv, qkv_near, qkv_far
     )
     mixed = attend(apart, member, projected, LONGEST)
     late_up = swap_diagonal(after(late_up, mixed))
@@ -814,14 +826,15 @@
     )
     late_moved = [send_to_owner(late_owned[j], j // 2, j % 2) for j in range(4)]
     fields = [layer_rows, attn, attn_got, cot_rows, back, swap_near(back)]
-    grad_attn, grad_mixed, grad_out, sums_two = middle(flags, dwa_weights, fields, mixed, vectors, weight_out)
-    grad_qkv = attend_back(apart, member, cos_table, sin_table, projected, grad_mixed, LONGEST)
+    grad_attn, grad_mixed, grad_out, sums_two = middle(flags, dwa_weights, fields, mixed, vectors, last_got)
+    grad_qkv, *owned = attend_back(
+        flags, apart, member, cos_table, sin_table, projected, grad_mixed, norm_one_t, grad_out, LONGEST
+    )
     grad_qkv, *late_moved = lax.optimization_barrier((grad_qkv, *late_moved))
-    owned = weigh(flags, norm_one_t, grad_qkv, grad_out)
     moved = [send_to_owner(owned[j], j // 2, j % 2) for j in range(4)]
-    late_sum = add(jnp.where(same, late_owned[0], after(late_moved[0], owned[0])), *late_moved[1:])
-    feed_sum = scatter_rows(jnp.concatenate([early_sum, late_sum], axis=1))
-    keep, *send, sums_one = unproject(flags, after(grad_qkv, owned[0]), weight_qkv, layer_rows)
+    early_sum = scatter_rows(after(early_sum, grad_qkv))
+    late_sum = scatter_rows(add(jnp.where(same, late_owned[0], late_moved[0]), *late_moved[1:]))
+    keep, *send, sums_one = unproject(flags, grad_qkv, weight_qkv, layer_rows)
     block_keep, *block_send, sums_now = lower(
         flags, act_early, act_late, down_early, down_late, layer_rows, attn, attn_got, after(cot_rows, keep)
     )
@@ -832,7 +845,7 @@
     attn_moved = move_rows(attn_one)
     got = [swap_near(field) for field in sent]
     ours = last(flags, layer_rows, grad_attn, after(keep, attn_one), block_keep, got, vectors)
-    early_sum, late_sum = jnp.split(after(feed_sum, attn_one), 2, axis=1)
+    early_sum = after(early_sum, attn_one)
     early_got = swap_diagonal(early_sum)
     small = jnp.concatenate([sums_one[:2], sums_two[:2], sums_now[:1], sums_past[:hist_count]], axis=0)
     small = after(small, ours)

time: 270 us -> 271 us (level)
  waiting for transfers between devices: 32.3 us -> 28.1 us
    pallas_call x10, Pallas kernels: 84.9 us -> 110 us  [streamed(): pl.pallas_call(kernel, grid_spec=pltpu.PrefetchScalarGridSpec(num_scalar_...]
    pallas_call x1 -> x0, Pallas kernels: 23.1 us -> none  [attend_back(): pl.pallas_call(functools.partial(attend_back_kernel, reach), grid=(width...]
    ppermute x8, waiting for transfers between devices: 11.6 us -> 0.82 us  [swap_diagonal(): lax.ppermute(field, AXES, moves(away, lambda t, d, k, c: (c, d, k, t)))]
    ppermute x0 -> x1, waiting for transfers between devices: none -> 7.51 us  [swap_far_away(): lax.ppermute(field, AXES, moves(away, lambda t, d, k, c: (t, d, 1 - k, c)))]
    ppermute x8, waiting for transfers between devices: 4.99 us -> 1.76 us  [send_to_owner(): lax.ppermute(field, AXES, moves(away if not other_far and (not other_tp)...]
    ppermute x0 -> x1, starting transfers between devices: none -> 3.12 us  [swap_far_away(): lax.ppermute(field, AXES, moves(away, lambda t, d, k, c: (t, d, 1 - k, c)))]
    dynamic_slice x2 -> x3, local copies, waits for them, and re-layouts: 4.54 us -> 6.68 us  [part_of(): return lax.dynamic_slice_in_dim(field, index * size, size, axis)]
    unnamed x80 -> x86, local copies, waits for them, and re-layouts: 13.6 us -> 13.7 us
  transfers between devices with their start and end apart: 37 -> 39, of which waited for: 12 -> 11; matrix products, arithmetic and copies ran while one was open for 11% -> 11% of each run, Pallas kernels for 46% -> 47%
where the time goes in v6:
time: 271 us; the launch traced here: 266 us
  Pallas kernels  127 us (47%)
  starting transfers between devices  51.9 us (19%)
  waiting for transfers between devices  28.1 us (10%)
  local copies, waits for them, and re-layouts  22 us (8%)
  other arithmetic  21.5 us (8%)
  between operations  14.6 us (5%)
    pallas_call x10, Pallas kernels, streamed(): pl.pallas_call(kernel, grid_spec=pltpu.PrefetchScalarGridSpec(num_scalar_...  110 us
    ppermute x8, starting transfers between devices, swap_diagonal(): lax.ppermute(field, AXES, moves(away, lambda t, d, k, c: (c, d, k, t)))  25.2 us
    unnamed x86, local copies, waits for them, and re-layouts  13.7 us
    pallas_call x1, Pallas kernels, attend(): pl.pallas_call(functools.partial(attend_kernel, reach), grid=(width // LA...  12.7 us
    ppermute x5, waiting for transfers between devices, sum_over(): lax.ppermute(field, name, [(d, d ^ bit) for d in range(size)])  11.8 us
    ppermute x8, starting transfers between devices, send_to_owner(): lax.ppermute(field, AXES, moves(away if not other_far and (not other_tp)...  10.5 us
    ppermute x1, waiting for transfers between devices, swap_far_away(): lax.ppermute(field, AXES, moves(away, lambda t, d, k, c: (t, d, 1 - k, c)))  7.51 us
    dynamic_slice x3, local copies, waits for them, and re-layouts, part_of(): return lax.dynamic_slice_in_dim(field, index * size, size, axis)  6.68 us
  transfers between devices with their start and end apart: 39, of which 11 were waited for; matrix products, arithmetic and copies ran while one was open for 11% of the time, Pallas kernels for 47%

profile of v6, /device:TPU:9, one launch (start us, length us, event | category | flops | bytes accessed | tf_op | source)
XLA Modules:
  0.0 266.3 jit_solution(16660482142398249198)
XLA Ops:
  8.0 3.1 %collective-permute-start = (bf16[512,768]{1,0:T(8,128)(2,1)}, bf16[512,768]{1,0:T(8,128)(2,1)}, u32[]{:S(2)}, u32[]{:S(2)}) collective-permute-start(bf16[512,768]{1,0:T(8,128)(2,1)} %bitcast.43), channel_id=1, source_target_pairs={{1,16},{3,18},{5,20},{7,22},{9,24},{11,26},{13,28},{15,30},{16,1},... | collective-permute-start | bytes 2359304 | tf_op jit(solution)/shard_map/ppermute | solution.py:681
  11.0 2.2 constant_dynamic-slice_fusion
  13.2 2.5 collective-permute-start.3
  15.7 2.9 %fusion.10 = (bf16[768,768]{1,0:T(8,128)(2,1)}, bf16[768,768]{1,0:T(8,128)(2,1)S(1)}) fusion(bf16[1536,768]{1,0:T(8,128)(2,1)} %refs_7_.3), kind=kLoop, calls=%fused_computation.51 | loop fusion | bytes 4718592 | tf_op jit(solution)/shard_map/dynamic_slice | solution.py:719
  18.7 1.6 fusion.11
  20.8 4.3 %shard_map.220 = (bf16[4,512,768]{2,1,0:T(8,128)(2,1)}, f32[512,768]{1,0:T(8,128)}, f32[8,768]{1,0:T(8,128)}) custom-call(f32[5]{0:T(128)} %weight_ref.3, bf16[4,512,768]{2,1,0:T(8,128)(2,1)} %bitcast.39, bf16[512,768]{1,0:T(8,128)(2,1)} %bitcast.40), custom_call_target="tpu_custom_call" | custom-call | bytes 9000000 | tf_op jit(solution)/shard_map/pallas_call | solution.py:611
  25.1 3.0 %pad_maximum_fusion = bf16[1536,768]{1,0:T(8,128)(2,1)} fusion(bf16[768,768]{1,0:T(8,128)(2,1)S(1)} %get-tuple-element.225, bf16[768,768]{1,0:T(8,128)(2,1)} %get-tuple-element.227), kind=kLoop, calls=%fused_computation | loop fusion | flops 4718592 | bytes 4718592 | tf_op jit(solution)/shard_map/concatenate | solution.py:781
  29.1 1.2 broadcast_select_fusion.1
  30.4 3.1 %fusion.1 = (f32[1024,128]{1,0:T(8,128)}, f32[1024,128]{1,0:T(8,128)}) fusion(f32[128]{0:T(128)S(1)} %get-tuple-element.237, f32[128]{0:T(128)S(1)} %get-tuple-element.238, f32[1024]{0:T(1024)S(1)} %subtract_convert_fusion), kind=kLoop, calls=%fused_computation.13 | loop fusion | flops 262144 | bytes 1053696 | tf_op jit(solution)/shard_map/mul | solution.py:796
  33.5 0.9 fusion.2.member_ref
  34.4 0.9 select_convert_fusion.apart_ref
  35.3 1.8 maximum_select_fusion.rows_ref.refs_2_
  37.1 3.0 %collective-permute-start.5 = (bf16[896,768]{1,0:T(8,128)(2,1)S(1)}, bf16[896,768]{1,0:T(8,128)(2,1)S(1)}, u32[]{:S(2)}, u32[]{:S(2)}) collective-permute-start(bf16[896,768]{1,0:T(8,128)(2,1)S(1)} %pad_maximum_fusion.1), channel_id=1, source_target_pairs={{1,16},{3,18},{5,20},{7,22},{9,24},{11,26},{13,28},{15,30},{16,1},... | collective-permute-start | bytes 4128776 | tf_op jit(solution)/shard_map/ppermute | solution.py:681
  40.2 3.1 %collective-permute-start.4 = (bf16[3,384,384]{2,1,0:T(8,128)(2,1)}, bf16[3,384,384]{2,1,0:T(8,128)(2,1)}, u32[]{:S(2)}, u32[]{:S(2)}) collective-permute-start(bf16[3,384,384]{2,1,0:T(8,128)(2,1)} %collective-permute-done.3.w_near), channel_id=1, source_target_pairs={{1,3},{3,1},{5,7},{7,5},{9,11},{11,9},{13,15},{15,13},{16,18},{18,... | collective-permute-start | bytes 2654216 | tf_op jit(solution)/shard_map/ppermute | solution.py:696
  43.3 2.8 %collective-permute-start.8 = (bf16[1536,768]{1,0:T(8,128)(2,1)}, bf16[1536,768]{1,0:T(8,128)(2,1)}, u32[]{:S(2)}, u32[]{:S(2)}) collective-permute-start(bf16[1536,768]{1,0:T(8,128)(2,1)} %pad_maximum_fusion), channel_id=1, source_target_pairs={{1,16},{3,18},{5,20},{7,22},{9,24},{11,26},{13,28},{15,30},{16,1},... | collective-permute-start | bytes 7077896 | tf_op jit(solution)/shard_map/ppermute | solution.py:681
  46.8 7.5 %collective-permute-done.4.w_far = bf16[3,384,384]{2,1,0:T(8,128)(2,1)} collective-permute-done((bf16[3,384,384]{2,1,0:T(8,128)(2,1)}, bf16[3,384,384]{2,1,0:T(8,128)(2,1)}, u32[]{:S(2)}, u32[]{:S(2)}) %collective-permute-start.4) | collective-permute-done | bytes 884768 | tf_op jit(solution)/shard_map/ppermute | solution.py:696
  54.3 9.6 %shard_map.221 = (bf16[3,1024,384]{2,1,0:T(8,128)(2,1)}, bf16[768,1024]{1,0:T(8,128)(2,1)}, bf16[3,768,384]{2,1,0:T(8,128)(2,1)}) custom-call(s32[4]{0:T(128)} %pad_add_fusion.flags.refs_0_, bf16[1024,768]{1,0:T(8,128)(2,1)} %maximum_select_fusion.rows_ref.refs_2_, f32[1024,128]{1,0:T(8,128)} %get-tuple-element.102.cos_ref, ...), custom_call_target="tpu_custom_call" | custom-call | bytes 24000000 | tf_op jit(solution)/shard_map/pallas_call | solution.py:249
  63.9 12.7 %shard_map.222.mixed_ref = bf16[1024,384]{1,0:T(8,128)(2,1)} custom-call(bf16[1024,128]{1,0:T(8,128)(2,1)} %select_convert_fusion.apart_ref, bf16[1024,128]{1,0:T(8,128)(2,1)} %fusion.2.member_ref, bf16[3,1024,384]{2,1,0:T(8,128)(2,1)} %get-tuple-element.106.q_ref.k_ref.v_ref, bf16[3,1024,384]{2,1,0:T(8,128)(2,1)} %get-tuple-element.106.q_ref.k_ref.v_ref, ...), custom_call_target="tpu_custom_call" | custom-call | bytes 36000000 | tf_op jit(solution)/shard_map/pallas_call | solution.py:99
  76.7 1.0 copy-done.21
  77.7 1.0 convolution_convert_fusion.refs_3_.own_ref
  78.8 3.7 %collective-permute-start.9 = (bf16[768,768]{1,0:T(8,128)(2,1)}, bf16[768,768]{1,0:T(8,128)(2,1)S(1)}, u32[]{:S(2)}, u32[]{:S(2)}) collective-permute-start(bf16[768,768]{1,0:T(8,128)(2,1)} %get-tuple-element.115), channel_id=1, source_target_pairs={{1,16},{3,18},{5,20},{7,22},{9,24},{11,26},{13,28},{15,30},{16,1},... | collective-permute-start | bytes 3538952 | tf_op jit(solution)/shard_map/ppermute | solution.py:681
  82.4 2.1 collective-permute-start.10
  84.7 2.3 collective-permute-done.7
  86.9 1.8 maximum_select_fusion.1.refs_5_.cot_ref
  88.8 1.2 copy-done.4
  90.0 18.7 %shard_map.223 = (bf16[1024,768]{1,0:T(8,128)(2,1)}, bf16[768,1024]{1,0:T(8,128)(2,1)}, bf16[1024,768]{1,0:T(8,128)(2,1)}, bf16[768,1024]{1,0:T(8,128)(2,1)}, bf...) custom-call(s32[4]{0:T(128)} %pad_add_fusion.flags.refs_0_, ...), custom_call_target="tpu_custom_call" | custom-call | bytes 51000000 | tf_op jit(solution)/shard_map/pallas_call | solution.py:249
  110.2 16.3 %shard_map.224 = (bf16[1024,768]{1,0:T(8,128)(2,1)}, bf16[1024,768]{1,0:T(8,128)(2,1)}, bf16[768,768]{1,0:T(8,128)(2,1)}, bf16[768,384]{1,0:T(8,128)(2,1)}, bf16...) custom-call(s32[4]{0:T(128)} %pad_add_fusion.flags.refs_0_, ...), custom_call_target="tpu_custom_call" | custom-call | bytes 51000000 | tf_op jit(solution)/shard_map/pallas_call | solution.py:249
  126.6 3.6 %collective-permute-start.12 = (bf16[768,384]{1,0:T(8,128)(2,1)}, bf16[768,384]{1,0:T(8,128)(2,1)S(1)}, u32[]{:S(2)}, u32[]{:S(2)}) collective-permute-start(bf16[768,384]{1,0:T(8,128)(2,1)} %get-tuple-element.122), channel_id=1, source_target_pairs={{1,16},{3,18},{5,20},{7,22},{9,24},{11,26},{13,28},{15,30},{16,1},... | collective-permute-start | bytes 1769480 | tf_op jit(solution)/shard_map/ppermute | solution.py:685
  130.3 1.0 collective-permute-start.14
  131.6 1.1 copy-done.23
  132.7 10.2 %shard_map.225 = (bf16[1024,768]{1,0:T(8,128)(2,1)}, bf16[1024,384]{1,0:T(8,128)(2,1)}, bf16[768,384]{1,0:T(8,128)(2,1)}, f32[8,768]{1,0:T(8,128)}) custom-call(s32[4]{0:T(128)} %pad_add_fusion.flags.refs_0_, f32[5]{0:T(128)} %weight_ref.3, bf16[1024,768]{1,0:T(8,128)(2,1)} %maximum_select_fusion.rows_ref.refs_2_, bf16[1024,768]{1,0:T(8,128)(2,1)} %copy-done.2, ...), custom_call_target="tpu_custom_call" | custom-call | bytes 24000000 | tf_op jit(solution)/shard_map/pallas_call | solution.py:249
  142.9 32.9 %shard_map.226 = (bf16[3,1024,384]{2,1,0:T(8,128)(2,1)}, bf16[768,384]{1,0:T(8,128)(2,1)}, bf16[768,384]{1,0:T(8,128)(2,1)}, bf16[768,384]{1,0:T(8,128)(2,1)}, bf16[768,384]{1,0:T(8,128)(2,1)}) custom-call(s32[4]{0:T(128)} %pad_add_fusion.flags.refs_0_, bf16[1024,128]{1,0:T(8,128)(2,1)} %select_convert_fusion.apart_ref, bf16[1024,128]{1,0:T(8,128)(2,1)} %fusion.2.member_ref, ...), custom_call_target="tpu_custom_call" | custom-call | bytes 84000000 | tf_op jit(solution)/shard_map/pallas_call | solution.py:249
  176.0 4.2 %collective-permute-start.16 = (bf16[768,384]{1,0:T(8,128)(2,1)}, bf16[768,384]{1,0:T(8,128)(2,1)}, u32[]{:S(2)}, u32[]{:S(2)}) collective-permute-start(bf16[768,384]{1,0:T(8,128)(2,1)} %get-tuple-element.144), channel_id=1, source_target_pairs={{1,16},{3,18},{5,20},{7,22},{9,24},{11,26},{13,28},{15,30},{16,1},... | collective-permute-start | bytes 1769480 | tf_op jit(solution)/shard_map/ppermute | solution.py:685
  180.2 1.0 collective-permute-start.18
  181.6 3.0 %add_convert_fusion = bf16[768,384]{1,0:T(8,128)(2,1)} fusion(bf16[768,384]{1,0:T(8,128)(2,1)} %copy-done.31, bf16[768,384]{1,0:T(8,128)(2,1)} %copy-done.30, bf16[768,384]{1,0:T(8,128)(2,1)} %collective-permute-done.13, bf16[768,384]{1,0:T(8,128)(2,1)} %get-tuple-element.122, bf16[768,384]{1,0:T(8,128)(2,1)} %copy-done.29, pred[]{:T(512)S(6)} %eq.36), kind=kLoop, calls=%fused_computation.6 | loop fusion | flops 2654208 | bytes 3538945 | tf_op jit(solution)/shard_map/convert_element_type | solution.py:723
  184.7 1.7 copy-done.7
  186.4 5.9 %shard_map.227 = (f32[512,768]{1,0:T(8,128)S(1)}, bf16[256,768]{1,0:T(8,128)(2,1)}, bf16[256,768]{1,0:T(8,128)(2,1)}, f32[8,768]{1,0:T(8,128)S(1)}) custom-call(s32[4]{0:T(128)S(1)} %copy-done.16, bf16[3,1024,384]{2,1,0:T(8,128)(2,1)S(1)} %copy-done.7, bf16[1024,768]{1,0:T(8,128)(2,1)S(1)} %copy-done, bf16[3,768,384]{2,1,0:T(8,128)(2,1)S(1)} %copy-done.8), custom_call_target="tpu_custom_call" | custom-call | bytes 15000000 | tf_op jit(solution)/shard_map/pallas_call | solution.py:249
  192.3 1.2 copy-done.10
  193.5 1.4 copy-done.12
  194.9 1.4 copy-done.13
  196.3 1.3 copy-done.14
  197.6 1.3 copy-done.15
  198.9 6.9 %shard_map.228 = (f32[512,768]{1,0:T(8,128)S(1)}, bf16[256,768]{1,0:T(8,128)(2,1)S(1)}, bf16[256,768]{1,0:T(8,128)(2,1)S(1)}, f32[8,768]{1,0:T(8,128)S(1)}) custom-call(s32[4]{0:T(128)S(1)} %copy-done.16, bf16[1024,768]{1,0:T(8,128)(2,1)S(1)} %copy-done.12, bf16[1024,768]{1,0:T(8,128)(2,1)S(1)} %copy-done.13, bf16[1024,768]{1,0:T(8,128)(2,1)S(1)} %copy-done, ...), custom_call_target="tpu_custom_call" | custom-call | bytes 18000000 | tf_op jit(solution)/shard_map/pallas_call | solution.py:249
  206.6 1.7 collective-permute-done.19
  209.4 2.0 add_convert_fusion.1
  211.4 1.3 collective-permute-start.28
  212.8 1.1 collective-permute-start.29
  213.9 1.3 collective-permute-start.30
  215.3 3.5 %collective-permute-start.27 = (bf16[192,384]{1,0:T(8,128)(2,1)}, bf16[192,384]{1,0:T(8,128)(2,1)S(1)}, u32[]{:S(2)}, u32[]{:S(2)}) collective-permute-start(bf16[192,384]{1,0:T(8,128)(2,1)} %reduce-scatter.8.cloned.1.call-done), channel_id=1, source_target_pairs={{1,16},{3,18},{5,20},{7,22},{9,24},{11,26},{13,28},{15,30},{16,1},... | collective-permute-start | bytes 442376 | tf_op jit(solution)/shard_map/ppermute | solution.py:681
  219.5 5.4 %shard_map.229.own_ref = bf16[2,512,768]{2,1,0:T(8,128)(2,1)} custom-call(s32[4]{0:T(128)} %pad_add_fusion.flags.refs_0_, bf16[1024,768]{1,0:T(8,128)(2,1)} %maximum_select_fusion.rows_ref.refs_2_, bf16[1024,768]{1,0:T(8,128)(2,1)} %get-tuple-element.138.resid_ref, f32[512,768]{1,0:T(8,128)} %copy-done.10, f32[512,768]{1,0:T(8,128)} %copy-done.11, ...), custom_call_target="tpu_custom_call" | custom-call | bytes 9000000 | tf_op jit(solution)/shard_map/pallas_call | solution.py:249
  225.0 1.2 collective-permute-done.24
  226.4 3.1 %collective-permute-done.25 = f32[9,768]{1,0:T(8,128)S(1)} collective-permute-done((f32[9,768]{1,0:T(8,128)S(1)}, f32[9,768]{1,0:T(8,128)S(1)}, u32[]{:S(2)}, u32[]{:S(2)}) %collective-permute-start.25) | collective-permute-done | bytes 27680 | tf_op jit(solution)/shard_map/ppermute | solution.py:751
  229.5 1.2 collective-permute-start.26
  230.7 1.8 collective-permute-done.26
  232.7 1.0 fusion.9
  233.7 1.2 collective-permute-start.34
  234.9 4.7 %collective-permute-start.31 = (bf16[2,512,768]{2,1,0:T(8,128)(2,1)S(1)}, bf16[2,512,768]{2,1,0:T(8,128)(2,1)S(1)}, u32[]{:S(2)}, u32[]{:S(2)}) collective-permute-start(bf16[2,512,768]{2,1,0:T(8,128)(2,1)S(1)} %copy-done.6), channel_id=1, source_target_pairs={{1,16},{3,18},{5,20},{7,22},{9,24},{11,26},{13,28},{15,30},{16,1},... | collective-permute-start | bytes 4718600 | tf_op jit(solution)/shard_map/ppermute | solution.py:681
  239.6 3.8 %collective-permute-done.34 = bf16[192,1152]{1,0:T(8,128)(2,1)S(1)} collective-permute-done((bf16[192,1152]{1,0:T(8,128)(2,1)S(1)}, bf16[192,1152]{1,0:T(8,128)(2,1)S(1)}, u32[]{:S(2)}, u32[]{:S(2)}) %collective-permute-start.34) | collective-permute-done | bytes 442400 | tf_op jit(solution)/shard_map/ppermute | solution.py:700
  243.4 3.1 %collective-permute-start.35 = (bf16[2,192,1152]{2,1,0:T(8,128)(2,1)S(1)}, bf16[2,192,1152]{2,1,0:T(8,128)(2,1)S(1)}, u32[]{:S(2)}, u32[]{:S(2)}) collective-permute-start(bf16[2,192,1152]{2,1,0:T(8,128)(2,1)S(1)} %pad_maximum_fusion.2.here_ref), channel_id=1, source_target_pairs={{0,1},{1,0},{2,3},{3,2},{4,5},{5,4},{6,7},{7,6},{8,9},{9,8},{10,11... | collective-permute-start | bytes 2654216 | tf_op jit(solution)/shard_map/ppermute | solution.py:704
  246.5 0.8 collective-permute-start.32
  247.3 2.2 collective-permute-done.32
  249.9 3.6 %collective-permute-done.33 = f32[9,768]{1,0:T(8,128)S(1)} collective-permute-done((f32[9,768]{1,0:T(8,128)S(1)}, f32[9,768]{1,0:T(8,128)S(1)}, u32[]{:S(2)}, u32[]{:S(2)}) %collective-permute-start.33) | collective-permute-done | bytes 27680 | tf_op jit(solution)/shard_map/ppermute | solution.py:751
  254.8 2.5 shard_map.231
  257.7 2.1 shard_map.230
  (163 shorter events, 11.1 us)
Async XLA Ops:
  7.2 168.7 %reduce-scatter.10.cloned.1.call-start = ((), (), s32[]{:S(2)}) async-start(), calls=%async_computation.5 | async-start | bytes 2949120
  7.2 21.4 %collective-permute-start.2 = (s32[1,3]{1,0:T(1,128)}, s32[1,3]{1,0:T(1,128)S(1)}, u32[]{:S(2)}, u32[]{:S(2)}) collective-permute-start(s32[1,3]{1,0:T(1,128)} %param.16), channel_id=1, source_target_pairs={{0,1},{1,0},{2,3},{3,2},{4,5},{5,4},{6,7},{7,6},{8,9},{9,8},{10,11... | collective-permute-start | bytes 44 | tf_op jit(solution)/shard_map/ppermute | solution.py:704
  8.0 21.1 %collective-permute-start = (bf16[512,768]{1,0:T(8,128)(2,1)}, bf16[512,768]{1,0:T(8,128)(2,1)}, u32[]{:S(2)}, u32[]{:S(2)}) collective-permute-start(bf16[512,768]{1,0:T(8,128)(2,1)} %bitcast.43), channel_id=1, source_target_pairs={{1,16},{3,18},{5,20},{7,22},{9,24},{11,26},{13,28},{15,30},{16,1},... | collective-permute-start | bytes 2359304 | tf_op jit(solution)/shard_map/ppermute | solution.py:681
  13.2 27.0 %collective-permute-start.3 = (bf16[3,384,384]{2,1,0:T(8,128)(2,1)}, bf16[3,384,384]{2,1,0:T(8,128)(2,1)}, u32[]{:S(2)}, u32[]{:S(2)}) collective-permute-start(bf16[3,384,384]{2,1,0:T(8,128)(2,1)} %constant_dynamic-slice_fusion), channel_id=1, source_target_pairs={{1,16},{3,18},{5,20},{7,22},{9,24},{11,26},{13,28},{15,30},{16,1},... | collective-permute-start | bytes 2654216 | tf_op jit(solution)/shard_map/ppermute | solution.py:681
  15.7 3.0 %copy-start.19 = (bf16[768,1536]{1,0:T(8,128)(2,1)S(1)}, bf16[768,1536]{1,0:T(8,128)(2,1)}, u32[]{:S(2)}) copy-start(bf16[768,1536]{1,0:T(8,128)(2,1)} %refs_6_.1) | copy-start | bytes 7077892
  25.0 3.6 %copy-start.42 = (s32[1,3]{1,0:T(1,128)S(1)}, s32[1,3]{1,0:T(1,128)}, u32[]{:S(2)}) copy-start(s32[1,3]{1,0:T(1,128)} %param.16) | copy-start | bytes 40
  25.0 4.0 %copy-start.26 = (bf16[1,512,768]{2,1,0:T(8,128)(2,1)S(1)}, bf16[1,512,768]{2,1,0:T(8,128)(2,1)}, u32[]{:S(2)}) copy-start(bf16[1,512,768]{2,1,0:T(8,128)(2,1)} %param.13) | copy-start | bytes 2359300
  30.3 5.0 %collective-permute-start.1 = (bf16[512,768]{1,0:T(8,128)(2,1)S(1)}, bf16[512,768]{1,0:T(8,128)(2,1)S(1)}, u32[]{:S(2)}, u32[]{:S(2)}) collective-permute-start(bf16[512,768]{1,0:T(8,128)(2,1)S(1)} %broadcast_select_fusion.1), channel_id=1, source_target_pairs={{0,1},{1,0},{2,3},{3,2},{4,5},{5,4},{6,7},{7,6},{8,9},{9,8},{10,11... | collective-permute-start | bytes 2359304 | tf_op jit(solution)/shard_map/ppermute | solution.py:704
  37.1 39.4 %collective-permute-start.5 = (bf16[896,768]{1,0:T(8,128)(2,1)S(1)}, bf16[896,768]{1,0:T(8,128)(2,1)S(1)}, u32[]{:S(2)}, u32[]{:S(2)}) collective-permute-start(bf16[896,768]{1,0:T(8,128)(2,1)S(1)} %pad_maximum_fusion.1), channel_id=1, source_target_pairs={{1,16},{3,18},{5,20},{7,22},{9,24},{11,26},{13,28},{15,30},{16,1},... | collective-permute-start | bytes 4128776 | tf_op jit(solution)/shard_map/ppermute | solution.py:681
  40.2 14.1 %collective-permute-start.4 = (bf16[3,384,384]{2,1,0:T(8,128)(2,1)}, bf16[3,384,384]{2,1,0:T(8,128)(2,1)}, u32[]{:S(2)}, u32[]{:S(2)}) collective-permute-start(bf16[3,384,384]{2,1,0:T(8,128)(2,1)} %collective-permute-done.3.w_near), channel_id=1, source_target_pairs={{1,3},{3,1},{5,7},{7,5},{9,11},{11,9},{13,15},{15,13},{16,18},{18,... | collective-permute-start | bytes 2654216 | tf_op jit(solution)/shard_map/ppermute | solution.py:696
  43.3 45.5 %collective-permute-start.8 = (bf16[1536,768]{1,0:T(8,128)(2,1)}, bf16[1536,768]{1,0:T(8,128)(2,1)}, u32[]{:S(2)}, u32[]{:S(2)}) collective-permute-start(bf16[1536,768]{1,0:T(8,128)(2,1)} %pad_maximum_fusion), channel_id=1, source_target_pairs={{1,16},{3,18},{5,20},{7,22},{9,24},{11,26},{13,28},{15,30},{16,1},... | collective-permute-start | bytes 7077896 | tf_op jit(solution)/shard_map/ppermute | solution.py:681
  77.7 6.9 %copy-start.20 = (bf16[896,768]{1,0:T(8,128)(2,1)}, bf16[896,768]{1,0:T(8,128)(2,1)S(1)}, u32[]{:S(2)}) copy-start(bf16[896,768]{1,0:T(8,128)(2,1)S(1)} %broadcast_select_fusion.w_ref) | copy-start | bytes 4128772
  78.7 10.1 %copy-start.2 = (bf16[1024,768]{1,0:T(8,128)(2,1)}, bf16[1024,768]{1,0:T(8,128)(2,1)S(1)}, u32[]{:S(2)}) copy-start(bf16[1024,768]{1,0:T(8,128)(2,1)S(1)} %convolution_convert_fusion.refs_3_.own_ref) | copy-start | bytes 4718596
  78.7 10.1 %collective-permute-start.6 = (bf16[1024,768]{1,0:T(8,128)(2,1)S(1)}, bf16[1024,768]{1,0:T(8,128)(2,1)S(1)}, u32[]{:S(2)}, u32[]{:S(2)}) collective-permute-start(bf16[1024,768]{1,0:T(8,128)(2,1)S(1)} %convolution_convert_fusion.refs_3_.own_ref), channel_id=1, source_target_pairs={{0,1},{1,0},{2,3},{3,2},{4,5},{5,4},{6,7},{7,6},{8,9},{9,8},{10,11... | collective-permute-start | bytes 4718600 | tf_op jit(solution)/shard_map/ppermute | solution.py:704
  78.8 29.9 %collective-permute-start.9 = (bf16[768,768]{1,0:T(8,128)(2,1)}, bf16[768,768]{1,0:T(8,128)(2,1)S(1)}, u32[]{:S(2)}, u32[]{:S(2)}) collective-permute-start(bf16[768,768]{1,0:T(8,128)(2,1)} %get-tuple-element.115), channel_id=1, source_target_pairs={{1,16},{3,18},{5,20},{7,22},{9,24},{11,26},{13,28},{15,30},{16,1},... | collective-permute-start | bytes 3538952 | tf_op jit(solution)/shard_map/ppermute | solution.py:681
  82.4 26.7 %collective-permute-start.10 = (bf16[768,768]{1,0:T(8,128)(2,1)}, bf16[768,768]{1,0:T(8,128)(2,1)S(1)}, u32[]{:S(2)}, u32[]{:S(2)}) collective-permute-start(bf16[768,768]{1,0:T(8,128)(2,1)} %get-tuple-element.116), channel_id=1, source_target_pairs={{1,16},{3,18},{5,20},{7,22},{9,24},{11,26},{13,28},{15,30},{16,1},... | collective-permute-start | bytes 3538952 | tf_op jit(solution)/shard_map/ppermute | solution.py:681
  84.6 2.4 collective-permute-start.7
  109.2 103.6 %reduce-scatter.8.cloned.1.call-start = ((), (), s32[]{:S(2)}) async-start(), calls=%async_computation.4 | async-start | bytes 737280 | tf_op jit(solution)/shard_map/reduce_scatter | solution.py:731
  126.4 5.1 %collective-permute-start.11 = (bf16[1024,768]{1,0:T(8,128)(2,1)}, bf16[1024,768]{1,0:T(8,128)(2,1)S(1)}, u32[]{:S(2)}, u32[]{:S(2)}) collective-permute-start(bf16[1024,768]{1,0:T(8,128)(2,1)} %get-tuple-element.117.back_own), channel_id=1, source_target_pairs={{0,1},{1,0},{2,3},{3,2},{4,5},{5,4},{6,7},{7,6},{8,9},{9,8},{10,11... | collective-permute-start | bytes 4718600 | tf_op jit(solution)/shard_map/ppermute | solution.py:704
  126.6 49.2 %collective-permute-start.12 = (bf16[768,384]{1,0:T(8,128)(2,1)}, bf16[768,384]{1,0:T(8,128)(2,1)S(1)}, u32[]{:S(2)}, u32[]{:S(2)}) collective-permute-start(bf16[768,384]{1,0:T(8,128)(2,1)} %get-tuple-element.122), channel_id=1, source_target_pairs={{1,16},{3,18},{5,20},{7,22},{9,24},{11,26},{13,28},{15,30},{16,1},... | collective-permute-start | bytes 1769480 | tf_op jit(solution)/shard_map/ppermute | solution.py:685
  130.2 45.6 %collective-permute-start.13 = (bf16[768,384]{1,0:T(8,128)(2,1)}, bf16[768,384]{1,0:T(8,128)(2,1)}, u32[]{:S(2)}, u32[]{:S(2)}) collective-permute-start(bf16[768,384]{1,0:T(8,128)(2,1)} %get-tuple-element.123), channel_id=1, source_target_pairs={{0,1},{1,17},{2,3},{3,19},{4,5},{5,21},{6,7},{7,23},{8,9},{9,25},{... | collective-permute-start | bytes 1769480 | tf_op jit(solution)/shard_map/ppermute | solution.py:685
  130.3 45.6 %collective-permute-start.14 = (bf16[768,384]{1,0:T(8,128)(2,1)}, bf16[768,384]{1,0:T(8,128)(2,1)S(1)}, u32[]{:S(2)}, u32[]{:S(2)}) collective-permute-start(bf16[768,384]{1,0:T(8,128)(2,1)} %get-tuple-element.124), channel_id=1, source_target_pairs={{0,2},{1,18},{2,0},{3,16},{4,6},{5,22},{6,4},{7,20},{8,10},{9,26},... | collective-permute-start | bytes 1769480 | tf_op jit(solution)/shard_map/ppermute | solution.py:685
  131.2 44.6 %collective-permute-start.15 = (bf16[768,384]{1,0:T(8,128)(2,1)}, bf16[768,384]{1,0:T(8,128)(2,1)S(1)}, u32[]{:S(2)}, u32[]{:S(2)}) collective-permute-start(bf16[768,384]{1,0:T(8,128)(2,1)} %get-tuple-element.125), channel_id=1, source_target_pairs={{0,3},{1,19},{2,1},{3,17},{4,7},{5,23},{6,5},{7,21},{8,11},{9,27},... | collective-permute-start | bytes 1769480 | tf_op jit(solution)/shard_map/ppermute | solution.py:685
  175.8 5.4 %copy-start.29 = (bf16[768,384]{1,0:T(8,128)(2,1)}, bf16[768,384]{1,0:T(8,128)(2,1)S(1)}, u32[]{:S(2)}) copy-start(bf16[768,384]{1,0:T(8,128)(2,1)S(1)} %collective-permute-done.12) | copy-start | bytes 1769476
  175.8 5.3 %copy-start.30 = (bf16[768,384]{1,0:T(8,128)(2,1)}, bf16[768,384]{1,0:T(8,128)(2,1)S(1)}, u32[]{:S(2)}) copy-start(bf16[768,384]{1,0:T(8,128)(2,1)S(1)} %collective-permute-done.14) | copy-start | bytes 1769476
  175.9 5.3 %copy-start.31 = (bf16[768,384]{1,0:T(8,128)(2,1)}, bf16[768,384]{1,0:T(8,128)(2,1)S(1)}, u32[]{:S(2)}) copy-start(bf16[768,384]{1,0:T(8,128)(2,1)S(1)} %collective-permute-done.15) | copy-start | bytes 1769476
  175.9 56.6 %reduce-scatter.6.cloned.1.call-start = ((), (), s32[]{:S(2)}) async-start(), calls=%async_computation.3 | async-start | bytes 737280 | tf_op jit(solution)/shard_map/reduce_scatter | solution.py:731
  176.0 30.6 %collective-permute-start.16 = (bf16[768,384]{1,0:T(8,128)(2,1)}, bf16[768,384]{1,0:T(8,128)(2,1)}, u32[]{:S(2)}, u32[]{:S(2)}) collective-permute-start(bf16[768,384]{1,0:T(8,128)(2,1)} %get-tuple-element.144), channel_id=1, source_target_pairs={{1,16},{3,18},{5,20},{7,22},{9,24},{11,26},{13,28},{15,30},{16,1},... | collective-permute-start | bytes 1769480 | tf_op jit(solution)/shard_map/ppermute | solution.py:685
  180.2 26.4 %collective-permute-start.17 = (bf16[768,384]{1,0:T(8,128)(2,1)}, bf16[768,384]{1,0:T(8,128)(2,1)}, u32[]{:S(2)}, u32[]{:S(2)}) collective-permute-start(bf16[768,384]{1,0:T(8,128)(2,1)} %get-tuple-element.145), channel_id=1, source_target_pairs={{0,1},{1,17},{2,3},{3,19},{4,5},{5,21},{6,7},{7,23},{8,9},{9,25},{... | collective-permute-start | bytes 1769480 | tf_op jit(solution)/shard_map/ppermute | solution.py:685
  180.2 26.4 %collective-permute-start.18 = (bf16[768,384]{1,0:T(8,128)(2,1)}, bf16[768,384]{1,0:T(8,128)(2,1)}, u32[]{:S(2)}, u32[]{:S(2)}) collective-permute-start(bf16[768,384]{1,0:T(8,128)(2,1)} %get-tuple-element.146), channel_id=1, source_target_pairs={{0,2},{1,18},{2,0},{3,16},{4,6},{5,22},{6,4},{7,20},{8,10},{9,26},... | collective-permute-start | bytes 1769480 | tf_op jit(solution)/shard_map/ppermute | solution.py:685
  181.2 3.5 %copy-start.37 = (f32[8,768]{1,0:T(8,128)S(1)}, f32[8,768]{1,0:T(8,128)}, u32[]{:S(2)}) copy-start(f32[8,768]{1,0:T(8,128)} %get-tuple-element.137) | copy-start | bytes 73732
  181.2 3.5 %copy-start = (bf16[1024,768]{1,0:T(8,128)(2,1)S(1)}, bf16[1024,768]{1,0:T(8,128)(2,1)}, u32[]{:S(2)}) copy-start(bf16[1024,768]{1,0:T(8,128)(2,1)} %maximum_select_fusion.rows_ref.refs_2_) | copy-start | bytes 4718596
  181.2 3.5 %copy-start.8 = (bf16[3,768,384]{2,1,0:T(8,128)(2,1)S(1)}, bf16[3,768,384]{2,1,0:T(8,128)(2,1)}, u32[]{:S(2)}) copy-start(bf16[3,768,384]{2,1,0:T(8,128)(2,1)} %get-tuple-element.127.weight) | copy-start | bytes 5308420
  181.2 3.5 %copy-start.16 = (s32[4]{0:T(128)S(1)}, s32[4]{0:T(128)}, u32[]{:S(2)}) copy-start(s32[4]{0:T(128)} %pad_add_fusion.flags.refs_0_) | copy-start | bytes 52
  181.2 27.1 %collective-permute-start.19 = (bf16[768,384]{1,0:T(8,128)(2,1)}, bf16[768,384]{1,0:T(8,128)(2,1)}, u32[]{:S(2)}, u32[]{:S(2)}) collective-permute-start(bf16[768,384]{1,0:T(8,128)(2,1)} %get-tuple-element.147), channel_id=1, source_target_pairs={{0,3},{1,19},{2,1},{3,17},{4,7},{5,23},{6,5},{7,21},{8,11},{9,27},... | collective-permute-start | bytes 1769480 | tf_op jit(solution)/shard_map/ppermute | solution.py:685
  186.4 7.1 %copy-start.1 = (bf16[1024,768]{1,0:T(8,128)(2,1)S(1)}, bf16[1024,768]{1,0:T(8,128)(2,1)}, u32[]{:S(2)}) copy-start(bf16[1024,768]{1,0:T(8,128)(2,1)} %maximum_select_fusion.1.refs_5_.cot_ref) | copy-start | bytes 4718596
  186.4 7.1 %copy-start.3 = (bf16[1024,768]{1,0:T(8,128)(2,1)S(1)}, bf16[1024,768]{1,0:T(8,128)(2,1)}, u32[]{:S(2)}) copy-start(bf16[1024,768]{1,0:T(8,128)(2,1)} %copy-done.2) | copy-start | bytes 4718596
  186.4 7.1 %copy-start.5 = (bf16[1024,768]{1,0:T(8,128)(2,1)S(1)}, bf16[1024,768]{1,0:T(8,128)(2,1)}, u32[]{:S(2)}) copy-start(bf16[1024,768]{1,0:T(8,128)(2,1)} %copy-done.4) | copy-start | bytes 4718596
  198.9 10.5 %copy-start.28 = (bf16[768,384]{1,0:T(8,128)(2,1)S(1)}, bf16[768,384]{1,0:T(8,128)(2,1)}, u32[]{:S(2)}) copy-start(bf16[768,384]{1,0:T(8,128)(2,1)} %get-tuple-element.144) | copy-start | bytes 1769476
  205.8 5.6 %copy-start.11 = (f32[512,768]{1,0:T(8,128)}, f32[512,768]{1,0:T(8,128)S(1)}, u32[]{:S(2)}) copy-start(f32[512,768]{1,0:T(8,128)S(1)} %get-tuple-element.154.block_keep) | copy-start | bytes 4718596
  208.3 4.4 %collective-permute-start.20 = (bf16[256,768]{1,0:T(8,128)(2,1)}, bf16[256,768]{1,0:T(8,128)(2,1)S(1)}, u32[]{:S(2)}, u32[]{:S(2)}) collective-permute-start(bf16[256,768]{1,0:T(8,128)(2,1)} %get-tuple-element.155), channel_id=1, source_target_pairs={{0,1},{1,0},{2,3},{3,2},{4,5},{5,4},{6,7},{7,6},{8,9},{9,8},{10,11... | collective-permute-start | bytes 1179656 | tf_op jit(solution)/shard_map/ppermute | solution.py:704
  208.7 5.2 %collective-permute-start.21 = (bf16[256,768]{1,0:T(8,128)(2,1)}, bf16[256,768]{1,0:T(8,128)(2,1)S(1)}, u32[]{:S(2)}, u32[]{:S(2)}) collective-permute-start(bf16[256,768]{1,0:T(8,128)(2,1)} %get-tuple-element.156), channel_id=1, source_target_pairs={{0,1},{1,0},{2,3},{3,2},{4,5},{5,4},{6,7},{7,6},{8,9},{9,8},{10,11... | collective-permute-start | bytes 1179656 | tf_op jit(solution)/shard_map/ppermute | solution.py:704
  208.8 6.4 %collective-permute-start.22 = (bf16[256,768]{1,0:T(8,128)(2,1)S(1)}, bf16[256,768]{1,0:T(8,128)(2,1)S(1)}, u32[]{:S(2)}, u32[]{:S(2)}) collective-permute-start(bf16[256,768]{1,0:T(8,128)(2,1)S(1)} %get-tuple-element.157), channel_id=1, source_target_pairs={{0,1},{1,0},{2,3},{3,2},{4,5},{5,4},{6,7},{7,6},{8,9},{9,8},{10,11... | collective-permute-start | bytes 1179656 | tf_op jit(solution)/shard_map/ppermute | solution.py:704
  209.2 9.5 %collective-permute-start.23 = (bf16[256,768]{1,0:T(8,128)(2,1)S(1)}, bf16[256,768]{1,0:T(8,128)(2,1)S(1)}, u32[]{:S(2)}, u32[]{:S(2)}) collective-permute-start(bf16[256,768]{1,0:T(8,128)(2,1)S(1)} %get-tuple-element.158), channel_id=1, source_target_pairs={{0,1},{1,0},{2,3},{3,2},{4,5},{5,4},{6,7},{7,6},{8,9},{9,8},{10,11... | collective-permute-start | bytes 1179656 | tf_op jit(solution)/shard_map/ppermute | solution.py:704
  211.4 21.1 %collective-permute-start.28 = (bf16[192,384]{1,0:T(8,128)(2,1)S(1)}, bf16[192,384]{1,0:T(8,128)(2,1)S(1)}, u32[]{:S(2)}, u32[]{:S(2)}) collective-permute-start(bf16[192,384]{1,0:T(8,128)(2,1)S(1)} %get-tuple-element.230), channel_id=1, source_target_pairs={{0,4},{4,8},{8,12},{12,0},{1,5},{5,9},{9,13},{13,1},{2,6},{6,10},{... | collective-permute-start | bytes 442376 | tf_op jit(solution)/shard_map/ppermute | solution.py:743
  212.8 6.0 %copy-start.32 = (bf16[256,768]{1,0:T(8,128)(2,1)}, bf16[256,768]{1,0:T(8,128)(2,1)S(1)}, u32[]{:S(2)}) copy-start(bf16[256,768]{1,0:T(8,128)(2,1)S(1)} %collective-permute-done.20.got_first) | copy-start | bytes 1179652
  212.8 19.8 %collective-permute-start.29 = (bf16[192,384]{1,0:T(8,128)(2,1)S(1)}, bf16[192,384]{1,0:T(8,128)(2,1)S(1)}, u32[]{:S(2)}, u32[]{:S(2)}) collective-permute-start(bf16[192,384]{1,0:T(8,128)(2,1)S(1)} %get-tuple-element.229), channel_id=1, source_target_pairs={{0,8},{4,12},{8,0},{12,4},{1,9},{5,13},{9,1},{13,5},{2,10},{6,14},... | collective-permute-start | bytes 442376 | tf_op jit(solution)/shard_map/ppermute | solution.py:743
  213.9 4.9 %copy-start.33 = (bf16[256,768]{1,0:T(8,128)(2,1)}, bf16[256,768]{1,0:T(8,128)(2,1)S(1)}, u32[]{:S(2)}) copy-start(bf16[256,768]{1,0:T(8,128)(2,1)S(1)} %collective-permute-done.21.got_second) | copy-start | bytes 1179652
  213.9 18.6 %collective-permute-start.30 = (bf16[192,384]{1,0:T(8,128)(2,1)S(1)}, bf16[192,384]{1,0:T(8,128)(2,1)S(1)}, u32[]{:S(2)}, u32[]{:S(2)}) collective-permute-start(bf16[192,384]{1,0:T(8,128)(2,1)S(1)} %get-tuple-element.228), channel_id=1, source_target_pairs={{0,12},{4,0},{8,4},{12,8},{1,13},{5,1},{9,5},{13,9},{2,14},{6,2},{... | collective-permute-start | bytes 442376 | tf_op jit(solution)/shard_map/ppermute | solution.py:743
  215.3 3.5 %copy-start.34 = (bf16[256,768]{1,0:T(8,128)(2,1)}, bf16[256,768]{1,0:T(8,128)(2,1)S(1)}, u32[]{:S(2)}) copy-start(bf16[256,768]{1,0:T(8,128)(2,1)S(1)} %collective-permute-done.22.block_first) | copy-start | bytes 1179652
  215.3 17.3 %collective-permute-start.27 = (bf16[192,384]{1,0:T(8,128)(2,1)}, bf16[192,384]{1,0:T(8,128)(2,1)S(1)}, u32[]{:S(2)}, u32[]{:S(2)}) collective-permute-start(bf16[192,384]{1,0:T(8,128)(2,1)} %reduce-scatter.8.cloned.1.call-done), channel_id=1, source_target_pairs={{1,16},{3,18},{5,20},{7,22},{9,24},{11,26},{13,28},{15,30},{16,1},... | collective-permute-start | bytes 442376 | tf_op jit(solution)/shard_map/ppermute | solution.py:681
  219.5 13.1 %copy-start.36 = (bf16[192,384]{1,0:T(8,128)(2,1)S(1)}, bf16[192,384]{1,0:T(8,128)(2,1)}, u32[]{:S(2)}) copy-start(bf16[192,384]{1,0:T(8,128)(2,1)} %reduce-scatter.8.cloned.1.call-done) | copy-start | bytes 442372
  224.9 10.0 %copy-start.6 = (bf16[2,512,768]{2,1,0:T(8,128)(2,1)S(1)}, bf16[2,512,768]{2,1,0:T(8,128)(2,1)}, u32[]{:S(2)}) copy-start(bf16[2,512,768]{2,1,0:T(8,128)(2,1)} %shard_map.229.own_ref) | copy-start | bytes 4718596
  224.9 1.2 collective-permute-start.24
  226.2 3.3 %collective-permute-start.25 = (f32[9,768]{1,0:T(8,128)S(1)}, f32[9,768]{1,0:T(8,128)S(1)}, u32[]{:S(2)}, u32[]{:S(2)}) collective-permute-start(f32[9,768]{1,0:T(8,128)S(1)} %add.97), channel_id=1, source_target_pairs={{0,16},{16,0},{1,17},{17,1},{2,18},{18,2},{3,19},{19,3},{4,20},{20... | collective-permute-start | bytes 82952 | tf_op jit(solution)/shard_map/ppermute | solution.py:751
  229.5 3.0 %collective-permute-start.26 = (f32[9,768]{1,0:T(8,128)S(1)}, f32[9,768]{1,0:T(8,128)S(1)}, u32[]{:S(2)}, u32[]{:S(2)}) collective-permute-start(f32[9,768]{1,0:T(8,128)S(1)} %add.98), channel_id=1, source_target_pairs={{0,2},{2,0},{1,3},{3,1},{4,6},{6,4},{5,7},{7,5},{8,10},{10,8},{9,1... | collective-permute-start | bytes 82952 | tf_op jit(solution)/shard_map/ppermute | solution.py:751
  232.7 22.1 %copy-start.17 = (s32[4]{0:T(128)S(1)}, s32[4]{0:T(128)}, u32[]{:S(2)}) copy-start(s32[4]{0:T(128)} %pad_add_fusion.flags.refs_0_) | copy-start | bytes 52
  233.7 9.6 %collective-permute-start.34 = (bf16[192,1152]{1,0:T(8,128)(2,1)S(1)}, bf16[192,1152]{1,0:T(8,128)(2,1)S(1)}, u32[]{:S(2)}, u32[]{:S(2)}) collective-permute-start(bf16[192,1152]{1,0:T(8,128)(2,1)S(1)} %get-tuple-element.233), channel_id=1, source_target_pairs={{0,2},{2,0},{1,3},{3,1},{4,6},{6,4},{5,7},{7,5},{8,10},{10,8},{9,1... | collective-permute-start | bytes 1327112 | tf_op jit(solution)/shard_map/ppermute | solution.py:700
  234.9 22.8 %collective-permute-start.31 = (bf16[2,512,768]{2,1,0:T(8,128)(2,1)S(1)}, bf16[2,512,768]{2,1,0:T(8,128)(2,1)S(1)}, u32[]{:S(2)}, u32[]{:S(2)}) collective-permute-start(bf16[2,512,768]{2,1,0:T(8,128)(2,1)S(1)} %copy-done.6), channel_id=1, source_target_pairs={{1,16},{3,18},{5,20},{7,22},{9,24},{11,26},{13,28},{15,30},{16,1},... | collective-permute-start | bytes 4718600 | tf_op jit(solution)/shard_map/ppermute | solution.py:681
  243.3 14.3 %copy-start.9 = (f32[512,768]{1,0:T(8,128)S(1)}, f32[512,768]{1,0:T(8,128)}, u32[]{:S(2)}) copy-start(f32[512,768]{1,0:T(8,128)} %get-tuple-element.99.part_ref) | copy-start | bytes 4718596
  243.3 14.3 %copy-start.18 = (f32[5]{0:T(128)S(1)}, f32[5]{0:T(128)}, u32[]{:S(2)}) copy-start(f32[5]{0:T(128)} %weight_ref.3) | copy-start | bytes 64
  243.4 11.3 %collective-permute-start.35 = (bf16[2,192,1152]{2,1,0:T(8,128)(2,1)S(1)}, bf16[2,192,1152]{2,1,0:T(8,128)(2,1)S(1)}, u32[]{:S(2)}, u32[]{:S(2)}) collective-permute-start(bf16[2,192,1152]{2,1,0:T(8,128)(2,1)S(1)} %pad_maximum_fusion.2.here_ref), channel_id=1, source_target_pairs={{0,1},{1,0},{2,3},{3,2},{4,5},{5,4},{6,7},{7,6},{8,9},{9,8},{10,11... | collective-permute-start | bytes 2654216 | tf_op jit(solution)/shard_map/ppermute | solution.py:704
  246.5 3.0 %collective-permute-start.32 = (f32[9,768]{1,0:T(8,128)S(1)}, f32[9,768]{1,0:T(8,128)S(1)}, u32[]{:S(2)}, u32[]{:S(2)}) collective-permute-start(f32[9,768]{1,0:T(8,128)S(1)} %add.99), channel_id=1, source_target_pairs={{0,4},{4,0},{8,12},{12,8},{1,5},{5,1},{9,13},{13,9},{2,6},{6,2},{1... | collective-permute-start | bytes 82952 | tf_op jit(solution)/shard_map/ppermute | solution.py:751
  249.5 4.0 %collective-permute-start.33 = (f32[9,768]{1,0:T(8,128)S(1)}, f32[9,768]{1,0:T(8,128)S(1)}, u32[]{:S(2)}, u32[]{:S(2)}) collective-permute-start(f32[9,768]{1,0:T(8,128)S(1)} %add.110), channel_id=1, source_target_pairs={{0,8},{4,12},{8,0},{12,4},{1,9},{5,13},{9,1},{13,5},{2,10},{6,14},... | collective-permute-start | bytes 82952 | tf_op jit(solution)/shard_map/ppermute | solution.py:751
  (18 other events, 24.7 us)
Sparse Core Ops, SparseCore 0:
  109.3 45.3 reduce-scatter.9
  176.0 20.0 reduce-scatter.7
  199.0 28.7 reduce-scatter.5

commit v7 on v5

--- a/solution.py
+++ b/solution.py
@@ -252,10 +252,13 @@
     return field * cos + crossed * sin
 
 
-def project_kernel(flags, rows_ref, cos_ref, sin_ref, vectors, w_own, w_got, out_ref, turned_ref, weight_ref):
+def project_kernel(flags, rows_ref, cos_ref, sin_ref, vectors, w_own, w_near, w_far, out_ref, turned_ref, weight_ref):
     @pl.when(pl.program_id(0) == 0)
     def _():
-        weight_ref[...] = jnp.where(flags[0] == 1, w_own[...], w_got[...])
+        half = w_near.shape[1]
+        for index, got in ((flags[2], w_near), (1 - flags[2], w_far)):
+            at = pl.ds(pl.multiple_of(index * half, half), half)
+            weight_ref[:, at, :] = jnp.where(flags[0] == 1, w_own[:, at, :], got[...])
 
     unit, unused = norm_parts(rows_ref[...].astype(jnp.float32))
     norm = unit * vectors[0:1, :] + vectors[1:2, :]
@@ -271,7 +274,7 @@
                 out_ref[c, :, lanes] = turn(field[:, lanes], cos_ref[...], sin_ref[...]).astype(jnp.bfloat16)
 
 
-def project(flags, rows, vectors, cos, sin, w_own, w_got):
+def project(flags, rows, vectors, cos, sin, w_own, w_near, w_far):
     whole, width = rows.shape
     count, unused, columns = w_own.shape
     low = jnp.bfloat16
@@ -279,7 +282,7 @@
         project_kernel,
         whole // ROWS,
         [flags],
-        [by_rows(rows, ROWS), by_rows(cos, ROWS), by_rows(sin, ROWS), vectors, w_own, w_got],
+        [by_rows(rows, ROWS), by_rows(cos, ROWS), by_rows(sin, ROWS), vectors, w_own, w_near, w_far],
         [
             ((count, whole, columns), low, (count, ROWS, columns), lambda i, flags: (0, i, 0)),
             ((width, whole), low, (width, ROWS), lambda i, flags: (0, i)),
@@ -301,8 +304,8 @@
 
 def feed_kernel(early, *refs):
     if early:
-        flags, weight_ref, rows_ref, own_ref, got_ref, cot_ref, vectors, up_own, down_own, got = refs[:10]
-        norm, norm_t, grad, grad_t, back_ref, act_ref, down_ref, pieces = refs[10:18]
+        flags, weight_ref, rows_ref, own_ref, got_ref, cot_here, cot_there, vectors, up_own, down_own, got = refs[:11]
+        norm, norm_t, grad, grad_t, back_ref, act_ref, down_ref, pieces = refs[11:19]
         up_got, down_got = got.at[: norm.shape[1]], got.at[norm.shape[1] :]
     else:
         flags, norm, norm_t, grad, grad_t, back_early, up_own, down_own, up_got, down_got = refs[:10]
@@ -323,7 +326,8 @@
             field = unit * vectors[2:3, :] + vectors[3:4, :]
             norm[at, :] = field.astype(jnp.bfloat16)
             norm_t[:, at] = field.T.astype(jnp.bfloat16)
-            field = wide(cot_ref, at) * weight_ref[weight_ref.shape[0] - 1]
+            cot = jnp.where(flags[1] == step, cot_here[at, :], cot_there[at, :])
+            field = cot.astype(jnp.float32) * weight_ref[weight_ref.shape[0] - 1]
             grad[at, :] = field.astype(jnp.bfloat16)
             grad_t[:, at] = field.T.astype(jnp.bfloat16)
 
@@ -340,7 +344,7 @@
         if early:
             pieces[p, at, :] = low
             return
-        slot = 2 * (flags[2] ^ (p % 2)) + (flags[7] ^ (p // 2))
+        slot = 2 * (flags[2] ^ (p % 2)) + (flags[3] ^ (p // 2))
         for j, piece in enumerate(pieces):
 
             @pl.when(slot == j)
@@ -377,7 +381,7 @@
     tokens = ((whole, width), low, (rows, width), lambda i, *scalars: (i, 0))
     turned = ((width, whole), low, (width, rows), across)
     if early:
-        operands = [by_rows(field, rows) for field in fields[:4]] + [fields[4]]
+        operands = [by_rows(field, rows) for field in fields[:3]] + [*fields[3:]]
         outs = [tokens, turned, tokens, turned]
         pieces = [((4, width, hidden // 2), low)]
     else:
@@ -453,7 +457,7 @@
 
 
 def middle_kernel(
-    flags, weight_ref, rows_ref, own_ref, got_ref, cot_ref, back_own, back_got, mixed_ref,
+    flags, rows_ref, own_ref, got_ref, cot_ref, back_own, back_got, mixed_ref,
     vectors, w_ref, grad_ref, gmixed_ref, gout_ref, sums_ref, gout,
 ):
     step, last = pl.program_id(0), pl.num_programs(0) - 1
@@ -462,8 +466,7 @@
     inner = back * vectors[2:3, :]
     mean = jnp.mean(inner, axis=-1, keepdims=True)
     slant = jnp.mean(inner * unit, axis=-1, keepdims=True)
-    cot = cot_ref[...].astype(jnp.float32) * weight_ref[weight_ref.shape[0] - 1]
-    grad = cot + scale * (inner - mean - unit * slant)
+    grad = cot_ref[...].astype(jnp.float32) + scale * (inner - mean - unit * slant)
     low = grad.astype(jnp.bfloat16)
     grad_ref[...] = low
     gmixed_ref[...] = dot(low, w_ref[...], NT).astype(jnp.bfloat16)
@@ -488,7 +491,7 @@
         sums_ref[1:2, :] += jnp.sum(back, axis=0, keepdims=True)
 
 
-def middle(flags, weight, fields, mixed, vectors, w_out):
+def middle(flags, fields, mixed, vectors, bundle):
     whole, width = fields[0].shape
     columns = mixed.shape[1]
     low = jnp.bfloat16
@@ -496,8 +499,9 @@
     return streamed(
         middle_kernel,
         whole // ROWS,
-        [flags, weight],
-        [by_rows(field, ROWS) for field in (*fields, mixed)] + [vectors, w_out],
+        [flags],
+        [by_rows(field, ROWS) for field in (*fields, mixed)]
+        + [vectors, (bundle, (columns, width), lambda i, *scalars: (0, 0))],
         [
             ((whole, width), low, (ROWS, width), in_order),
             ((whole, columns), low, (ROWS, columns), in_order),
@@ -512,7 +516,7 @@
 def weigh_kernel(flags, turned_ref, out_grad_ref, grad_ref, *out_refs):
     last = grad_ref.shape[0]
     for j, out_ref in enumerate(out_refs):
-        piece = flags[3 + j]
+        piece = 2 * (flags[2] ^ (j // 2)) + (flags[3] ^ (j % 2))
 
         @pl.when(piece < last)
         def _():
@@ -554,30 +558,25 @@
     return streamed(unproject_kernel, 4, [flags], fields, sent_and_kept(whole, width), [], 5, SNUG)
 
 
-def last_kernel(
-    flags, rows_ref, resid_ref, keep_ref, block_keep, got_first, got_second, block_first, block_second, vectors, out_ref
-):
-    first = pl.program_id(0) == 0
+def last_kernel(flags, rows_ref, resid_ref, keep_ref, got_first, got_second, vectors, out_ref):
     unit, scale = norm_parts(rows_ref[...].astype(jnp.float32))
-    got = jnp.where(first, got_first[...], got_second[...]).astype(jnp.float32)
+    got = jnp.where(pl.program_id(0) == 0, got_first[...], got_second[...]).astype(jnp.float32)
     inner = (keep_ref[...] + got) * vectors[0:1, :]
     mean = jnp.mean(inner, axis=-1, keepdims=True)
     slant = jnp.mean(inner * unit, axis=-1, keepdims=True)
     grad = resid_ref[...].astype(jnp.float32) + scale * (inner - mean - unit * slant)
-    out_ref[0] = grad.astype(jnp.bfloat16)
-    got = jnp.where(first, block_first[...], block_second[...]).astype(jnp.float32)
-    out_ref[1] = (block_keep[...] + got).astype(jnp.bfloat16)
-
-
-def last(flags, rows, resid, keep, block_keep, got, vectors):
+    out_ref[...] = grad.astype(jnp.bfloat16)
+
+
+def last(flags, rows, resid, keep, got, vectors):
     half, width = keep.shape
     size = half // 2
 
     def mine(i, flags):
         return flags[1] * 2 + i
 
-    out = ((2, half, width), jnp.bfloat16, (2, size, width), lambda i, flags: (0, i, 0))
-    fields = [by_rows(rows, size, mine), by_rows(resid, size, mine), by_rows(keep, size), by_rows(block_keep, size)]
+    out = ((half, width), jnp.bfloat16, (size, width), lambda i, flags: (i, 0))
+    fields = [by_rows(rows, size, mine), by_rows(resid, size, mine), by_rows(keep, size)]
     return streamed(last_kernel, 2, [flags], fields + [*got, vectors], [out], [], 3)[0]
 
 
@@ -615,17 +614,16 @@
     )(dwa, history, cot)
 
 
-def present_kernel(flags, weight_ref, part_ref, own_ref, got_ref, out_ref, grad_ref):
-    here = jnp.where(flags[0] == 1, own_ref[1], got_ref[1]).astype(jnp.float32)
+def present_kernel(flags, weight_ref, part_ref, grad_own, grad_got, block_own, block_got, out_ref, grad_ref):
+    here = jnp.where(flags[0] == 1, block_own[...], block_got[...]).astype(jnp.float32)
     out_ref[...] = (part_ref[...] + weight_ref[weight_ref.shape[0] - 1] * here).astype(jnp.bfloat16)
-    grad_ref[...] = jnp.where(flags[0] == 1, own_ref[0], got_ref[0])
-
-
-def present(flags, weight, part, own, got):
-    rows, width = part.shape
-    both = (2, ROWS, width), lambda i, *scalars: (0, i, 0)
+    grad_ref[...] = jnp.where(flags[0] == 1, grad_own[...], grad_got[...])
+
+
+def present(flags, weight, *fields):
+    rows, width = fields[0].shape
     out = ((rows, width), jnp.bfloat16, (ROWS, width), lambda i, *scalars: (i, 0))
-    fields = [by_rows(part, ROWS), (own, *both), (got, *both)]
+    fields = [by_rows(field, ROWS) for field in fields]
     return streamed(present_kernel, rows // ROWS, [flags, weight], fields, [out] * 2, [], 2, SNUG)
 
 
@@ -682,6 +680,10 @@
             lambda t, d, k, c: (c, d, k ^ other_far, t ^ other_tp),
         ),
     )
+
+
+def swap_far_away(field):
+    return lax.ppermute(field, AXES, moves(away, lambda t, d, k, c: (t, d, 1 - k, c)))
 
 
 def swap_far(field):
@@ -761,11 +763,11 @@
     hist_count = history.shape[0]
     part, far, near = lax.axis_index("tp"), lax.axis_index("far"), lax.axis_index("near")
     same = near == part
-    pieces = [2 * (far ^ a) + (part ^ b) for a in range(2) for b in range(2)]
-    flags = jnp.stack([same.astype(jnp.int32), near, far, *pieces, part])
+    flags = jnp.stack([same.astype(jnp.int32), near, far, part])
 
     input_got = swap_diagonal(layer_input[0])
-    qkv_got = swap_diagonal(w_qkv)
+    qkv_near = swap_diagonal(part_of(w_qkv, far, 1))
+    qkv_far = swap_far_away(qkv_near)
     early_got = jnp.concatenate([part_of(w_up, 0, 1), part_of(w_down, 0, 0)], axis=0)
     late_up, late_down = part_of(w_up, 1, 1), part_of(w_down, 1, 0)
     last_own = jnp.concatenate([w_out, cotangent[0]], axis=0)
@@ -786,44 +788,42 @@
 
     input_half = jnp.where(same, layer_input[0], input_got)
     layer_rows = ordered(input_half, swap_near(input_half), near == 0)
-    layer_rows, last_own, early_got, late_up, vectors, past_sum, *tables = lax.optimization_barrier(
-        (layer_rows, last_own, early_got, late_up, vectors, past_sum)
-        + (cos_table, sin_table, apart, member)
-    )
-    cos_table, sin_table, apart, member = tables
-    early_got = swap_diagonal(early_got)
-    last_got = swap_diagonal(last_own)
+    layer_rows, vectors, past_sum, cos_table, sin_table, apart, member = lax.optimization_barrier(
+        (layer_rows, vectors, past_sum, cos_table, sin_table, apart, member)
+    )
+    early_got = swap_diagonal(after(early_got, input_got))
+    last_got = swap_diagonal(after(last_own, input_got))
     projected, norm_one_t, weight_qkv = project(
-        flags, layer_rows, vectors, cos_table, sin_table, w_qkv, qkv_got
+        flags, layer_rows, vectors, cos_table, sin_table, w_qkv, qkv_near, qkv_far
     )
     mixed = attend(apart, member, projected, LONGEST)
     late_up = swap_diagonal(after(late_up, mixed))
     late_down = swap_diagonal(after(late_down, mixed))
-    last_got = jnp.where(same, last_own, last_got)
+    last_got = jnp.where(same, last_own, after(last_got, mixed))
     weight_out = last_got[: w_out.shape[0]]
     attn = jnp.dot(mixed, weight_out, preferred_element_type=jnp.float32).astype(jnp.bfloat16)
     attn_got = swap_near(attn)
     cot_half = last_got[w_out.shape[0] :]
-    cot_rows = ordered(cot_half, swap_near(cot_half), near == 0)
     scalars = [flags, dwa_weights]
-    fields = [layer_rows, attn, attn_got, cot_rows, vectors]
+    fields = [layer_rows, attn, attn_got, cot_half, swap_near(cot_half), vectors]
     *kept, back, act_early, down_early, early_pieces = feed(True, scalars, fields, w_up, w_down, early_got)
     early_sum = scatter_plane(after(early_pieces, late_up, late_down))
     back, act_late, down_late, *late_owned = feed(
         False, [flags], [*kept, back], w_up, w_down, late_up, late_down
     )
     late_moved = [send_to_owner(late_owned[j], j // 2, j % 2) for j in range(4)]
-    fields = [layer_rows, attn, attn_got, cot_rows, back, swap_near(back)]
-    grad_attn, grad_mixed, grad_out, sums_two = middle(flags, dwa_weights, fields, mixed, vectors, weight_out)
+    grad_down = kept[2]
+    fields = [layer_rows, attn, attn_got, grad_down, back, swap_near(back)]
+    grad_attn, grad_mixed, grad_out, sums_two = middle(flags, fields, mixed, vectors, last_got)
     grad_qkv = attend_back(apart, member, cos_table, sin_table, projected, grad_mixed, LONGEST)
     grad_qkv, *late_moved = lax.optimization_barrier((grad_qkv, *late_moved))
     owned = weigh(flags, norm_one_t, grad_qkv, grad_out)
     moved = [send_to_owner(owned[j], j // 2, j % 2) for j in range(4)]
-    late_sum = add(jnp.where(same, late_owned[0], after(late_moved[0], owned[0])), *late_moved[1:])
-    feed_sum = scatter_rows(jnp.concatenate([early_sum, late_sum], axis=1))
+    early_sum = scatter_rows(after(early_sum, grad_qkv))
+    late_sum = scatter_rows(add(jnp.where(same, late_owned[0], after(late_moved[0], owned[0])), *late_moved[1:]))
     keep, *send, sums_one = unproject(flags, after(grad_qkv, owned[0]), weight_qkv, layer_rows)
     block_keep, *block_send, sums_now = lower(
-        flags, act_early, act_late, down_early, down_late, layer_rows, attn, attn_got, after(cot_rows, keep)
+        flags, act_early, act_late, down_early, down_late, layer_rows, attn, attn_got, after(grad_down, keep)
     )
     sent = [*send, *block_send]
     keep, block_keep, *arrived = lax.optimization_barrier((keep, block_keep, *sent, *moved))
@@ -831,29 +831,34 @@
     attn_one = add(jnp.where(same, owned[0], moved[0]), *moved[1:])
     attn_moved = move_rows(attn_one)
     got = [swap_near(field) for field in sent]
-    ours = last(flags, layer_rows, grad_attn, after(keep, attn_one), block_keep, got, vectors)
-    early_sum, late_sum = jnp.split(after(feed_sum, attn_one), 2, axis=1)
+    block_half = add(block_keep, jnp.concatenate(got[2:], axis=0))
+    block_moved = swap_diagonal(block_half)
+    input_grad = last(flags, layer_rows, grad_attn, after(keep, attn_one), got[:2], vectors)
+    early_sum = after(early_sum, attn_one)
     early_got = swap_diagonal(early_sum)
     small = jnp.concatenate([sums_one[:2], sums_two[:2], sums_now[:1], sums_past[:hist_count]], axis=0)
-    small = after(small, ours)
-    for name in ("near", "tp", "far"):
+    small = after(small, input_grad)
+    for name in ("tp", "far"):
         small = sum_over(small, name)
-    small, ours, late_sum, early_sum, early_got, *attn_moved = lax.optimization_barrier(
-        (small, ours, late_sum, early_sum, early_got, *attn_moved)
-    )
-    theirs = swap_diagonal(ours)
-    small = sum_over(small, "dp")
+    small, input_grad, block_moved, late_sum, early_sum, early_got, *attn_moved = lax.optimization_barrier(
+        (small, input_grad, block_moved, late_sum, early_sum, early_got, *attn_moved)
+    )
+    input_moved = swap_diagonal(input_grad)
+    for name in ("near", "dp"):
+        small = sum_over(small, name)
     attn_sum = add(*attn_moved)
     blocks = jnp.concatenate([attn_sum, jnp.where(same, early_sum, early_got), late_sum], axis=1)
     here = jnp.stack([blocks, swap_far(blocks)])
-    output, grad_input = present(flags, dwa_weights, past_sum, ours, theirs)
+    output, grad_input = present(
+        flags, dwa_weights, past_sum, input_grad, input_moved, block_half, block_moved
+    )
     grad_w_qkv, grad_w_out, grad_w_up, grad_w_down = place(flags, here, swap_near(here))
 
     return (
         output[None],
         grad_input[None],
         grad_history[:, None],
-        jnp.sum(jnp.concatenate([small[5:], small[4:5]], axis=0), axis=1),
+        jnp.sum(jnp.concatenate([small[5:], small[4:5] / dwa_weights[hist_count]], axis=0), axis=1),
         small[0],
         small[1],
         grad_w_qkv,

time: 270 us -> 278 us (1.030)
  starting transfers between devices: 49.2 us -> 58.7 us
  waiting for transfers between devices: 32.3 us -> 28 us
    ppermute x8 -> x9, waiting for transfers between devices: 11.6 us -> 1.31 us  [swap_diagonal(): lax.ppermute(field, AXES, moves(away, lambda t, d, k, c: (c, d, k, t)))]
    ppermute x1, waiting for transfers between devices: 2.49 us -> 9.39 us  [swap_far(): return lax.ppermute(field, 'far', [(0, 1), (1, 0)])]
    ppermute x3, waiting for transfers between devices: 0.01 us -> 5.55 us  [move_rows(): lax.ppermute(sent, 'dp', [(d, (d + step) % dps) for d in range(dps)])]
    ppermute x8, waiting for transfers between devices: 4.99 us -> 0.93 us  [send_to_owner(): lax.ppermute(field, AXES, moves(away if not other_far and (not other_tp)...]
    unnamed x80 -> x104, local copies, waits for them, and re-layouts: 13.6 us -> 16.9 us
    ppermute x5, waiting for transfers between devices: 10.8 us -> 7.62 us  [sum_over(): lax.ppermute(field, name, [(d, d ^ bit) for d in range(size)])]
    ppermute x0 -> x1, starting transfers between devices: none -> 3.12 us  [swap_far_away(): lax.ppermute(field, AXES, moves(away, lambda t, d, k, c: (t, d, 1 - k, c)))]
    ppermute x5, starting transfers between devices: 3.36 us -> 6.45 us  [sum_over(): lax.ppermute(field, name, [(d, d ^ bit) for d in range(size)])]
  transfers between devices with their start and end apart: 37 -> 40, of which waited for: 12 -> 13; matrix products, arithmetic and copies ran while one was open for 11% -> 11% of each run, Pallas kernels for 46% -> 45%
where the time goes in v7:
time: 278 us; the launch traced here: 273 us
  Pallas kernels  124 us (45%)
  starting transfers between devices  58.7 us (21%)
  waiting for transfers between devices  28 us (10%)
  local copies, waits for them, and re-layouts  23.9 us (9%)
  other arithmetic  22.8 us (8%)
  between operations  14.6 us (5%)
    pallas_call x10, Pallas kernels, streamed(): pl.pallas_call(kernel, grid_spec=pltpu.PrefetchScalarGridSpec(num_scalar_...  83.9 us
    ppermute x9, starting transfers between devices, swap_diagonal(): lax.ppermute(field, AXES, moves(away, lambda t, d, k, c: (c, d, k, t)))  26.9 us
    pallas_call x1, Pallas kernels, attend_back(): pl.pallas_call(functools.partial(attend_back_kernel, reach), grid=(width...  23.1 us
    unnamed x104, local copies, waits for them, and re-layouts  16.9 us
    pallas_call x1, Pallas kernels, attend(): pl.pallas_call(functools.partial(attend_kernel, reach), grid=(width // LA...  12.8 us
    ppermute x8, starting transfers between devices, send_to_owner(): lax.ppermute(field, AXES, moves(away if not other_far and (not other_tp)...  12 us
    ppermute x1, waiting for transfers between devices, swap_far(): return lax.ppermute(field, 'far', [(0, 1), (1, 0)])  9.39 us
    ppermute x5, waiting for transfers between devices, sum_over(): lax.ppermute(field, name, [(d, d ^ bit) for d in range(size)])  7.62 us
  transfers between devices with their start and end apart: 40, of which 13 were waited for; matrix products, arithmetic and copies ran while one was open for 11% of the time, Pallas kernels for 45%

profile of v7, /device:TPU:9, one launch (start us, length us, event | category | flops | bytes accessed | tf_op | source)
XLA Modules:
  0.0 273.0 jit_solution(7632566804101148215)
XLA Ops:
  8.0 3.2 %collective-permute-start = (bf16[512,768]{1,0:T(8,128)(2,1)}, bf16[512,768]{1,0:T(8,128)(2,1)}, u32[]{:S(2)}, u32[]{:S(2)}) collective-permute-start(bf16[512,768]{1,0:T(8,128)(2,1)} %bitcast.45), channel_id=1, source_target_pairs={{1,16},{3,18},{5,20},{7,22},{9,24},{11,26},{13,28},{15,30},{16,1},... | collective-permute-start | bytes 2359304 | tf_op jit(solution)/shard_map/ppermute | solution.py:671
  11.2 2.2 constant_dynamic-slice_fusion
  13.4 2.5 collective-permute-start.3
  17.0 2.3 pad_maximum_fusion.1
  19.3 3.3 %fusion.10 = (bf16[768,768]{1,0:T(8,128)(2,1)}, bf16[768,768]{1,0:T(8,128)(2,1)S(1)}, bf16[768,768]{1,0:T(8,128)(2,1)S(1)}, bf16[768,768]{1,0:T(8,128)(2,1)}) fusion(bf16[1536,768]{1,0:T(8,128)(2,1)} %refs_7_.1, bf16[768,1536]{1,0:T(8,128)(2,1)S(1)} %copy-done.22), kind=kLoop, calls=%fused_computation.52 | loop fusion | bytes 9437184 | tf_op jit(solution)/shard_map/dynamic_slice | solution.py:709
  22.6 1.6 pad_maximum_fusion
  24.2 4.4 %shard_map.220 = (bf16[4,512,768]{2,1,0:T(8,128)(2,1)}, f32[512,768]{1,0:T(8,128)}, f32[8,768]{1,0:T(8,128)}) custom-call(f32[5]{0:T(128)} %weight_ref.1, bf16[4,512,768]{2,1,0:T(8,128)(2,1)} %bitcast.43, bf16[512,768]{1,0:T(8,128)(2,1)} %bitcast.40), custom_call_target="tpu_custom_call" | custom-call | bytes 9000000 | tf_op jit(solution)/shard_map/pallas_call | solution.py:602
  30.2 3.2 %collective-permute-start.5 = (bf16[896,768]{1,0:T(8,128)(2,1)S(1)}, bf16[896,768]{1,0:T(8,128)(2,1)S(1)}, u32[]{:S(2)}, u32[]{:S(2)}) collective-permute-start(bf16[896,768]{1,0:T(8,128)(2,1)S(1)} %copy-done.30), channel_id=1, source_target_pairs={{1,16},{3,18},{5,20},{7,22},{9,24},{11,26},{13,28},{15,30},{16,1},... | collective-permute-start | bytes 4128776 | tf_op jit(solution)/shard_map/ppermute | solution.py:671
  33.5 1.2 broadcast_select_fusion.1
  34.8 3.1 %collective-permute-start.4 = (bf16[3,384,384]{2,1,0:T(8,128)(2,1)}, bf16[3,384,384]{2,1,0:T(8,128)(2,1)S(1)}, u32[]{:S(2)}, u32[]{:S(2)}) collective-permute-start(bf16[3,384,384]{2,1,0:T(8,128)(2,1)} %collective-permute-done.3.w_near), channel_id=1, source_target_pairs={{1,3},{3,1},{5,7},{7,5},{9,11},{11,9},{13,15},{15,13},{16,18},{18,... | collective-permute-start | bytes 2654216 | tf_op jit(solution)/shard_map/ppermute | solution.py:686
  37.9 1.6 select_convert_fusion.apart_ref
  39.5 3.7 %fusion.1 = (f32[1024,128]{1,0:T(8,128)}, f32[1024,128]{1,0:T(8,128)}) fusion(f32[128]{0:T(128)} %get-tuple-element.241, f32[128]{0:T(128)} %get-tuple-element.242, f32[1024]{0:T(1024)S(1)} %subtract_convert_fusion), kind=kLoop, calls=%fused_computation.13 | loop fusion | flops 262144 | bytes 1053696 | tf_op jit(solution)/shard_map/mul | solution.py:786
  43.2 2.6 collective-permute-start.8
  46.8 1.9 maximum_select_fusion.rows_ref.refs_2_
  49.7 9.6 %shard_map.221 = (bf16[3,1024,384]{2,1,0:T(8,128)(2,1)}, bf16[768,1024]{1,0:T(8,128)(2,1)}, bf16[3,768,384]{2,1,0:T(8,128)(2,1)}) custom-call(s32[4]{0:T(128)} %pad_add_fusion.flags.refs_0_, bf16[1024,768]{1,0:T(8,128)(2,1)} %maximum_select_fusion.rows_ref.refs_2_, f32[1024,128]{1,0:T(8,128)} %get-tuple-element.104.cos_ref, ...), custom_call_target="tpu_custom_call" | custom-call | bytes 24000000 | tf_op jit(solution)/shard_map/pallas_call | solution.py:223
  59.3 12.8 %shard_map.222.mixed_ref = bf16[1024,384]{1,0:T(8,128)(2,1)} custom-call(bf16[1024,128]{1,0:T(8,128)(2,1)} %select_convert_fusion.apart_ref, bf16[1024,128]{1,0:T(8,128)(2,1)} %fusion.2.member_ref, bf16[3,1024,384]{2,1,0:T(8,128)(2,1)} %get-tuple-element.108.q_ref.k_ref.v_ref, bf16[3,1024,384]{2,1,0:T(8,128)(2,1)} %get-tuple-element.108.q_ref.k_ref.v_ref, ...), custom_call_target="tpu_custom_call" | custom-call | bytes 36000000 | tf_op jit(solution)/shard_map/pallas_call | solution.py:99
  74.3 3.5 %collective-permute-start.9 = (bf16[768,768]{1,0:T(8,128)(2,1)}, bf16[768,768]{1,0:T(8,128)(2,1)}, u32[]{:S(2)}, u32[]{:S(2)}) collective-permute-start(bf16[768,768]{1,0:T(8,128)(2,1)} %get-tuple-element.117), channel_id=1, source_target_pairs={{1,16},{3,18},{5,20},{7,22},{9,24},{11,26},{13,28},{15,30},{16,1},... | collective-permute-start | bytes 3538952 | tf_op jit(solution)/shard_map/ppermute | solution.py:671
  77.8 2.2 collective-permute-start.10
  80.2 2.3 collective-permute-done.7.refs_6_
  83.4 1.2 copy-done.5
  84.5 18.9 %shard_map.223 = (bf16[1024,768]{1,0:T(8,128)(2,1)}, bf16[768,1024]{1,0:T(8,128)(2,1)}, bf16[1024,768]{1,0:T(8,128)(2,1)}, bf16[768,1024]{1,0:T(8,128)(2,1)}, bf...) custom-call(s32[4]{0:T(128)} %pad_add_fusion.flags.refs_0_, ...), custom_call_target="tpu_custom_call" | custom-call | bytes 51000000 | tf_op jit(solution)/shard_map/pallas_call | solution.py:223
  103.5 1.3 collective-permute-done.10.refs_9_
  104.8 16.3 %shard_map.224 = (bf16[1024,768]{1,0:T(8,128)(2,1)}, bf16[1024,768]{1,0:T(8,128)(2,1)}, bf16[768,768]{1,0:T(8,128)(2,1)}, bf16[768,384]{1,0:T(8,128)(2,1)}, bf16...) custom-call(s32[4]{0:T(128)} %pad_add_fusion.flags.refs_0_, ...), custom_call_target="tpu_custom_call" | custom-call | bytes 51000000 | tf_op jit(solution)/shard_map/pallas_call | solution.py:223
  121.2 1.7 collective-permute-start.13
  122.9 1.3 collective-permute-start.14
  124.3 3.5 %collective-permute-start.12 = (bf16[768,384]{1,0:T(8,128)(2,1)}, bf16[768,384]{1,0:T(8,128)(2,1)S(1)}, u32[]{:S(2)}, u32[]{:S(2)}) collective-permute-start(bf16[768,384]{1,0:T(8,128)(2,1)} %get-tuple-element.121), channel_id=1, source_target_pairs={{1,16},{3,18},{5,20},{7,22},{9,24},{11,26},{13,28},{15,30},{16,1},... | collective-permute-start | bytes 1769480 | tf_op jit(solution)/shard_map/ppermute | solution.py:675
  127.8 1.2 copy-done.29
  129.0 10.0 %shard_map.225 = (bf16[1024,768]{1,0:T(8,128)(2,1)}, bf16[1024,384]{1,0:T(8,128)(2,1)}, bf16[768,384]{1,0:T(8,128)(2,1)}, f32[8,768]{1,0:T(8,128)}) custom-call(s32[4]{0:T(128)} %pad_add_fusion.flags.refs_0_, bf16[1024,768]{1,0:T(8,128)(2,1)} %maximum_select_fusion.rows_ref.refs_2_, bf16[1024,768]{1,0:T(8,128)(2,1)} %copy-done.3, ...), custom_call_target="tpu_custom_call" | custom-call | bytes 24000000 | tf_op jit(solution)/shard_map/pallas_call | solution.py:223
  139.0 23.1 %shard_map.226.grad_ref = bf16[3,1024,384]{2,1,0:T(8,128)(2,1)} custom-call(bf16[1024,128]{1,0:T(8,128)(2,1)} %select_convert_fusion.apart_ref, bf16[1024,128]{1,0:T(8,128)(2,1)} %fusion.2.member_ref, f32[1024,128]{1,0:T(8,128)} %get-tuple-element.104.cos_ref, f32[1024,128]{1,0:T(8,128)} %get-tuple-element.105.sin_ref, ...), custom_call_target="tpu_custom_call" | custom-call | bytes 66000000 | tf_op jit(solution)/shard_map/pallas_call | solution.py:175
  163.6 7.9 %shard_map.227 = (bf16[768,384]{1,0:T(8,128)(2,1)}, bf16[768,384]{1,0:T(8,128)(2,1)}, bf16[768,384]{1,0:T(8,128)(2,1)}, bf16[768,384]{1,0:T(8,128)(2,1)}) custom-call(s32[4]{0:T(128)} %pad_add_fusion.flags.refs_0_, bf16[768,1024]{1,0:T(8,128)(2,1)} %get-tuple-element.126.turned_ref, bf16[768,384]{1,0:T(8,128)(2,1)} %get-tuple-element.127.out_grad_ref, ...), custom_call_target="tpu_custom_call" | custom-call | bytes 12000000 | tf_op jit(solution)/shard_map/pallas_call | solution.py:223
  171.5 1.4 collective-permute-start.18
  173.3 3.7 %collective-permute-start.16 = (bf16[768,384]{1,0:T(8,128)(2,1)}, bf16[768,384]{1,0:T(8,128)(2,1)}, u32[]{:S(2)}, u32[]{:S(2)}) collective-permute-start(bf16[768,384]{1,0:T(8,128)(2,1)} %get-tuple-element.128), channel_id=1, source_target_pairs={{1,16},{3,18},{5,20},{7,22},{9,24},{11,26},{13,28},{15,30},{16,1},... | collective-permute-start | bytes 1769480 | tf_op jit(solution)/shard_map/ppermute | solution.py:675
  177.0 1.7 copy-done.1
  178.7 5.0 %shard_map.228 = (f32[512,768]{1,0:T(8,128)S(1)}, bf16[256,768]{1,0:T(8,128)(2,1)S(1)}, bf16[256,768]{1,0:T(8,128)(2,1)S(1)}, f32[8,768]{1,0:T(8,128)S(1)}) custom-call(s32[4]{0:T(128)S(1)} %copy-done.15, bf16[3,1024,384]{2,1,0:T(8,128)(2,1)S(1)} %copy-done.1, bf16[1024,768]{1,0:T(8,128)(2,1)S(1)} %copy-done, bf16[3,768,384]{2,1,0:T(8,128)(2,1)S(1)} %copy-done.8), custom_call_target="tpu_custom_call" | custom-call | bytes 15000000 | tf_op jit(solution)/shard_map/pallas_call | solution.py:223
  183.7 1.2 copy-done.10
  186.4 1.4 copy-done.11
  187.8 1.4 copy-done.12
  189.2 1.3 copy-done.13
  190.5 1.3 copy-done.14
  191.8 7.4 %shard_map.229 = (f32[512,768]{1,0:T(8,128)S(1)}, bf16[256,768]{1,0:T(8,128)(2,1)}, bf16[256,768]{1,0:T(8,128)(2,1)}, f32[8,768]{1,0:T(8,128)S(1)}) custom-call(s32[4]{0:T(128)S(1)} %copy-done.15, bf16[1024,768]{1,0:T(8,128)(2,1)S(1)} %copy-done.11, bf16[1024,768]{1,0:T(8,128)(2,1)S(1)} %copy-done.12, bf16[1024,768]{1,0:T(8,128)(2,1)S(1)} %copy-done, ...), custom_call_target="tpu_custom_call" | custom-call | bytes 18000000 | tf_op jit(solution)/shard_map/pallas_call | solution.py:223
  200.6 1.2 add_convert_fusion.1
  202.8 2.4 collective-permute-start.26
  206.5 2.0 add_convert_fusion.2
  209.4 4.3 %shard_map.230.grad_own = bf16[512,768]{1,0:T(8,128)(2,1)} custom-call(s32[4]{0:T(128)} %pad_add_fusion.flags.refs_0_, bf16[1024,768]{1,0:T(8,128)(2,1)} %maximum_select_fusion.rows_ref.refs_2_, bf16[1024,768]{1,0:T(8,128)(2,1)} %get-tuple-element.141.resid_ref, f32[512,768]{1,0:T(8,128)} %copy-done.10, bf16[256,768]{1,0:T(8,128)(2,1)} %copy-done.44, ...), custom_call_target="tpu_custom_call" | custom-call | bytes 9000000 | tf_op jit(solution)/shard_map/pallas_call | solution.py:223
  213.7 1.1 collective-permute-start.22
  214.8 2.5 collective-permute-done.22
  217.3 1.8 collective-permute-start.23
  219.4 2.3 collective-permute-start.29
  221.7 2.2 collective-permute-start.28
  223.9 4.5 %collective-permute-start.27 = (bf16[192,384]{1,0:T(8,128)(2,1)}, bf16[192,384]{1,0:T(8,128)(2,1)S(1)}, u32[]{:S(2)}, u32[]{:S(2)}) collective-permute-start(bf16[192,384]{1,0:T(8,128)(2,1)} %reduce-scatter.8.cloned.1.call-done), channel_id=1, source_target_pairs={{1,16},{3,18},{5,20},{7,22},{9,24},{11,26},{13,28},{15,30},{16,1},... | collective-permute-start | bytes 442376 | tf_op jit(solution)/shard_map/ppermute | solution.py:671
  228.4 2.0 collective-permute-done.29
  230.4 3.5 %collective-permute-done.28 = bf16[192,384]{1,0:T(8,128)(2,1)S(1)} collective-permute-done((bf16[192,384]{1,0:T(8,128)(2,1)S(1)}, bf16[192,384]{1,0:T(8,128)(2,1)S(1)}, u32[]{:S(2)}, u32[]{:S(2)}) %collective-permute-start.28) | collective-permute-done | bytes 147488 | tf_op jit(solution)/shard_map/ppermute | solution.py:733
  234.1 1.1 fusion.9
  235.4 9.4 %collective-permute-done.35 = bf16[192,1152]{1,0:T(8,128)(2,1)S(1)} collective-permute-done((bf16[192,1152]{1,0:T(8,128)(2,1)S(1)}, bf16[192,1152]{1,0:T(8,128)(2,1)S(1)}, u32[]{:S(2)}, u32[]{:S(2)}) %collective-permute-start.35) | collective-permute-done | bytes 442400 | tf_op jit(solution)/shard_map/ppermute | solution.py:690
  244.9 3.2 %collective-permute-start.36 = (bf16[2,192,1152]{2,1,0:T(8,128)(2,1)S(1)}, bf16[2,192,1152]{2,1,0:T(8,128)(2,1)S(1)}, u32[]{:S(2)}, u32[]{:S(2)}) collective-permute-start(bf16[2,192,1152]{2,1,0:T(8,128)(2,1)S(1)} %pad_maximum_fusion.2.here_ref), channel_id=1, source_target_pairs={{0,1},{1,0},{2,3},{3,2},{4,5},{5,4},{6,7},{7,6},{8,9},{9,8},{10,11... | collective-permute-start | bytes 2654216 | tf_op jit(solution)/shard_map/ppermute | solution.py:694
  248.1 2.8 %collective-permute-start.31 = (bf16[512,768]{1,0:T(8,128)(2,1)S(1)}, bf16[512,768]{1,0:T(8,128)(2,1)S(1)}, u32[]{:S(2)}, u32[]{:S(2)}) collective-permute-start(bf16[512,768]{1,0:T(8,128)(2,1)S(1)} %copy-done.7), channel_id=1, source_target_pairs={{1,16},{3,18},{5,20},{7,22},{9,24},{11,26},{13,28},{15,30},{16,1},... | collective-permute-start | bytes 2359304 | tf_op jit(solution)/shard_map/ppermute | solution.py:671
  250.9 1.2 collective-permute-done.32
  252.2 2.0 collective-permute-start.33
  254.2 2.0 collective-permute-done.33
  256.2 1.5 collective-permute-start.34
  258.3 1.9 collective-permute-done.34
  260.2 1.3 slice_reduce_fusion
  262.1 1.9 shard_map.231
  264.0 2.5 shard_map.232
  (184 shorter events, 18.7 us)
Async XLA Ops:
  7.2 9.8 %copy-start.47 = (f32[768]{0:T(1024)S(1)}, f32[768]{0:T(1024)}, u32[]{:S(2)}) copy-start(f32[768]{0:T(1024)} %param.18) | copy-start | bytes 9220
  7.2 9.8 %copy-start.48 = (f32[768]{0:T(1024)S(1)}, f32[768]{0:T(1024)}, u32[]{:S(2)}) copy-start(f32[768]{0:T(1024)} %param.19) | copy-start | bytes 9220
  7.2 9.8 %copy-start.49 = (f32[768]{0:T(1024)S(1)}, f32[768]{0:T(1024)}, u32[]{:S(2)}) copy-start(f32[768]{0:T(1024)} %param.22) | copy-start | bytes 9220
  7.2 9.8 %copy-start.50 = (f32[768]{0:T(1024)S(1)}, f32[768]{0:T(1024)}, u32[]{:S(2)}) copy-start(f32[768]{0:T(1024)} %param.23) | copy-start | bytes 9220
  7.2 9.8 %copy-start.24 = (bf16[1,512,768]{2,1,0:T(8,128)(2,1)S(1)}, bf16[1,512,768]{2,1,0:T(8,128)(2,1)}, u32[]{:S(2)}) copy-start(bf16[1,512,768]{2,1,0:T(8,128)(2,1)} %param.15) | copy-start | bytes 2359300
  7.2 155.0 %reduce-scatter.10.cloned.1.call-start = ((), (), s32[]{:S(2)}) async-start(), calls=%async_computation.5 | async-start | bytes 2949120
  7.3 22.6 %collective-permute-start.2 = (s32[1,3]{1,0:T(1,128)}, s32[1,3]{1,0:T(1,128)S(1)}, u32[]{:S(2)}, u32[]{:S(2)}) collective-permute-start(s32[1,3]{1,0:T(1,128)} %param.16), channel_id=1, source_target_pairs={{0,1},{1,0},{2,3},{3,2},{4,5},{5,4},{6,7},{7,6},{8,9},{9,8},{10,11... | collective-permute-start | bytes 44 | tf_op jit(solution)/shard_map/ppermute | solution.py:694
  8.0 22.2 %collective-permute-start = (bf16[512,768]{1,0:T(8,128)(2,1)}, bf16[512,768]{1,0:T(8,128)(2,1)}, u32[]{:S(2)}, u32[]{:S(2)}) collective-permute-start(bf16[512,768]{1,0:T(8,128)(2,1)} %bitcast.45), channel_id=1, source_target_pairs={{1,16},{3,18},{5,20},{7,22},{9,24},{11,26},{13,28},{15,30},{16,1},... | collective-permute-start | bytes 2359304 | tf_op jit(solution)/shard_map/ppermute | solution.py:671
  13.4 21.4 %collective-permute-start.3 = (bf16[3,384,384]{2,1,0:T(8,128)(2,1)}, bf16[3,384,384]{2,1,0:T(8,128)(2,1)}, u32[]{:S(2)}, u32[]{:S(2)}) collective-permute-start(bf16[3,384,384]{2,1,0:T(8,128)(2,1)} %constant_dynamic-slice_fusion), channel_id=1, source_target_pairs={{1,16},{3,18},{5,20},{7,22},{9,24},{11,26},{13,28},{15,30},{16,1},... | collective-permute-start | bytes 2654216 | tf_op jit(solution)/shard_map/ppermute | solution.py:671
  24.2 9.2 %copy-start.32 = (bf16[1,512,768]{2,1,0:T(8,128)(2,1)S(1)}, bf16[1,512,768]{2,1,0:T(8,128)(2,1)}, u32[]{:S(2)}) copy-start(bf16[1,512,768]{2,1,0:T(8,128)(2,1)} %param.13) | copy-start | bytes 2359300
  30.2 41.8 %collective-permute-start.5 = (bf16[896,768]{1,0:T(8,128)(2,1)S(1)}, bf16[896,768]{1,0:T(8,128)(2,1)S(1)}, u32[]{:S(2)}, u32[]{:S(2)}) collective-permute-start(bf16[896,768]{1,0:T(8,128)(2,1)S(1)} %copy-done.30), channel_id=1, source_target_pairs={{1,16},{3,18},{5,20},{7,22},{9,24},{11,26},{13,28},{15,30},{16,1},... | collective-permute-start | bytes 4128776 | tf_op jit(solution)/shard_map/ppermute | solution.py:671
  34.7 12.1 %collective-permute-start.1 = (bf16[512,768]{1,0:T(8,128)(2,1)S(1)}, bf16[512,768]{1,0:T(8,128)(2,1)S(1)}, u32[]{:S(2)}, u32[]{:S(2)}) collective-permute-start(bf16[512,768]{1,0:T(8,128)(2,1)S(1)} %broadcast_select_fusion.1), channel_id=1, source_target_pairs={{0,1},{1,0},{2,3},{3,2},{4,5},{5,4},{6,7},{7,6},{8,9},{9,8},{10,11... | collective-permute-start | bytes 2359304 | tf_op jit(solution)/shard_map/ppermute | solution.py:694
  34.8 14.0 %collective-permute-start.4 = (bf16[3,384,384]{2,1,0:T(8,128)(2,1)}, bf16[3,384,384]{2,1,0:T(8,128)(2,1)S(1)}, u32[]{:S(2)}, u32[]{:S(2)}) collective-permute-start(bf16[3,384,384]{2,1,0:T(8,128)(2,1)} %collective-permute-done.3.w_near), channel_id=1, source_target_pairs={{1,3},{3,1},{5,7},{7,5},{9,11},{11,9},{13,15},{15,13},{16,18},{18,... | collective-permute-start | bytes 2654216 | tf_op jit(solution)/shard_map/ppermute | solution.py:686
  43.2 39.3 %collective-permute-start.8 = (bf16[1536,768]{1,0:T(8,128)(2,1)}, bf16[1536,768]{1,0:T(8,128)(2,1)}, u32[]{:S(2)}, u32[]{:S(2)}) collective-permute-start(bf16[1536,768]{1,0:T(8,128)(2,1)} %pad_maximum_fusion), channel_id=1, source_target_pairs={{1,16},{3,18},{5,20},{7,22},{9,24},{11,26},{13,28},{15,30},{16,1},... | collective-permute-start | bytes 7077896 | tf_op jit(solution)/shard_map/ppermute | solution.py:671
  59.3 12.8 %copy-start.25 = (bf16[1,512,768]{2,1,0:T(8,128)(2,1)S(1)}, bf16[1,512,768]{2,1,0:T(8,128)(2,1)}, u32[]{:S(2)}) copy-start(bf16[1,512,768]{2,1,0:T(8,128)(2,1)} %param.15) | copy-start | bytes 2359300
  59.3 12.8 %copy-start.28 = (bf16[384,768]{1,0:T(8,128)(2,1)S(1)}, bf16[384,768]{1,0:T(8,128)(2,1)}, u32[]{:S(2)}) copy-start(bf16[384,768]{1,0:T(8,128)(2,1)} %param.21) | copy-start | bytes 1769476
  74.2 8.3 %copy-start.3 = (bf16[1024,768]{1,0:T(8,128)(2,1)}, bf16[1024,768]{1,0:T(8,128)(2,1)S(1)}, u32[]{:S(2)}) copy-start(bf16[1024,768]{1,0:T(8,128)(2,1)S(1)} %convolution_convert_fusion.refs_3_.own_ref) | copy-start | bytes 4718596
  74.2 8.3 %collective-permute-start.6 = (bf16[1024,768]{1,0:T(8,128)(2,1)S(1)}, bf16[1024,768]{1,0:T(8,128)(2,1)S(1)}, u32[]{:S(2)}, u32[]{:S(2)}) collective-permute-start(bf16[1024,768]{1,0:T(8,128)(2,1)S(1)} %convolution_convert_fusion.refs_3_.own_ref), channel_id=1, source_target_pairs={{0,1},{1,0},{2,3},{3,2},{4,5},{5,4},{6,7},{7,6},{8,9},{9,8},{10,11... | collective-permute-start | bytes 4718600 | tf_op jit(solution)/shard_map/ppermute | solution.py:694
  74.3 29.2 %collective-permute-start.9 = (bf16[768,768]{1,0:T(8,128)(2,1)}, bf16[768,768]{1,0:T(8,128)(2,1)}, u32[]{:S(2)}, u32[]{:S(2)}) collective-permute-start(bf16[768,768]{1,0:T(8,128)(2,1)} %get-tuple-element.117), channel_id=1, source_target_pairs={{1,16},{3,18},{5,20},{7,22},{9,24},{11,26},{13,28},{15,30},{16,1},... | collective-permute-start | bytes 3538952 | tf_op jit(solution)/shard_map/ppermute | solution.py:671
  77.8 27.0 %collective-permute-start.10 = (bf16[768,768]{1,0:T(8,128)(2,1)}, bf16[768,768]{1,0:T(8,128)(2,1)}, u32[]{:S(2)}, u32[]{:S(2)}) collective-permute-start(bf16[768,768]{1,0:T(8,128)(2,1)} %get-tuple-element.118), channel_id=1, source_target_pairs={{1,16},{3,18},{5,20},{7,22},{9,24},{11,26},{13,28},{15,30},{16,1},... | collective-permute-start | bytes 3538952 | tf_op jit(solution)/shard_map/ppermute | solution.py:671
  80.1 2.4 collective-permute-start.7
  104.8 119.1 %reduce-scatter.8.cloned.1.call-start = ((), (), s32[]{:S(2)}) async-start(), calls=%async_computation.4 | async-start | bytes 737280 | tf_op jit(solution)/shard_map/reduce_scatter | solution.py:721
  121.1 6.6 %collective-permute-start.11 = (bf16[1024,768]{1,0:T(8,128)(2,1)}, bf16[1024,768]{1,0:T(8,128)(2,1)S(1)}, u32[]{:S(2)}, u32[]{:S(2)}) collective-permute-start(bf16[1024,768]{1,0:T(8,128)(2,1)} %get-tuple-element.119.back_own), channel_id=1, source_target_pairs={{0,1},{1,0},{2,3},{3,2},{4,5},{5,4},{6,7},{7,6},{8,9},{9,8},{10,11... | collective-permute-start | bytes 4718600 | tf_op jit(solution)/shard_map/ppermute | solution.py:694
  121.2 40.9 %collective-permute-start.13 = (bf16[768,384]{1,0:T(8,128)(2,1)}, bf16[768,384]{1,0:T(8,128)(2,1)S(1)}, u32[]{:S(2)}, u32[]{:S(2)}) collective-permute-start(bf16[768,384]{1,0:T(8,128)(2,1)} %get-tuple-element.122), channel_id=1, source_target_pairs={{0,1},{1,17},{2,3},{3,19},{4,5},{5,21},{6,7},{7,23},{8,9},{9,25},{... | collective-permute-start | bytes 1769480 | tf_op jit(solution)/shard_map/ppermute | solution.py:675
  122.9 39.2 %collective-permute-start.14 = (bf16[768,384]{1,0:T(8,128)(2,1)}, bf16[768,384]{1,0:T(8,128)(2,1)S(1)}, u32[]{:S(2)}, u32[]{:S(2)}) collective-permute-start(bf16[768,384]{1,0:T(8,128)(2,1)} %get-tuple-element.123), channel_id=1, source_target_pairs={{0,2},{1,18},{2,0},{3,16},{4,6},{5,22},{6,4},{7,20},{8,10},{9,26},... | collective-permute-start | bytes 1769480 | tf_op jit(solution)/shard_map/ppermute | solution.py:675
  124.3 37.9 %collective-permute-start.15 = (bf16[768,384]{1,0:T(8,128)(2,1)}, bf16[768,384]{1,0:T(8,128)(2,1)S(1)}, u32[]{:S(2)}, u32[]{:S(2)}) collective-permute-start(bf16[768,384]{1,0:T(8,128)(2,1)} %get-tuple-element.124), channel_id=1, source_target_pairs={{0,3},{1,19},{2,1},{3,17},{4,7},{5,23},{6,5},{7,21},{8,11},{9,27},... | collective-permute-start | bytes 1769480 | tf_op jit(solution)/shard_map/ppermute | solution.py:675
  124.3 37.9 %collective-permute-start.12 = (bf16[768,384]{1,0:T(8,128)(2,1)}, bf16[768,384]{1,0:T(8,128)(2,1)S(1)}, u32[]{:S(2)}, u32[]{:S(2)}) collective-permute-start(bf16[768,384]{1,0:T(8,128)(2,1)} %get-tuple-element.121), channel_id=1, source_target_pairs={{1,16},{3,18},{5,20},{7,22},{9,24},{11,26},{13,28},{15,30},{16,1},... | collective-permute-start | bytes 1769480 | tf_op jit(solution)/shard_map/ppermute | solution.py:675
  162.3 71.7 %reduce-scatter.6.cloned.1.call-start = ((), (), s32[]{:S(2)}) async-start(), calls=%async_computation.3 | async-start | bytes 737280 | tf_op jit(solution)/shard_map/reduce_scatter | solution.py:721
  163.6 13.4 %copy-start = (bf16[1024,768]{1,0:T(8,128)(2,1)S(1)}, bf16[1024,768]{1,0:T(8,128)(2,1)}, u32[]{:S(2)}) copy-start(bf16[1024,768]{1,0:T(8,128)(2,1)} %maximum_select_fusion.rows_ref.refs_2_) | copy-start | bytes 4718596
  163.6 13.5 %copy-start.8 = (bf16[3,768,384]{2,1,0:T(8,128)(2,1)S(1)}, bf16[3,768,384]{2,1,0:T(8,128)(2,1)}, u32[]{:S(2)}) copy-start(bf16[3,768,384]{2,1,0:T(8,128)(2,1)} %get-tuple-element.130.weight) | copy-start | bytes 5308420
  163.6 13.5 %copy-start.15 = (s32[4]{0:T(128)S(1)}, s32[4]{0:T(128)}, u32[]{:S(2)}) copy-start(s32[4]{0:T(128)} %pad_add_fusion.flags.refs_0_) | copy-start | bytes 52
  171.5 27.7 %collective-permute-start.17 = (bf16[768,384]{1,0:T(8,128)(2,1)}, bf16[768,384]{1,0:T(8,128)(2,1)}, u32[]{:S(2)}, u32[]{:S(2)}) collective-permute-start(bf16[768,384]{1,0:T(8,128)(2,1)} %get-tuple-element.147), channel_id=1, source_target_pairs={{0,1},{1,17},{2,3},{3,19},{4,5},{5,21},{6,7},{7,23},{8,9},{9,25},{... | collective-permute-start | bytes 1769480 | tf_op jit(solution)/shard_map/ppermute | solution.py:675
  171.5 27.7 %collective-permute-start.18 = (bf16[768,384]{1,0:T(8,128)(2,1)}, bf16[768,384]{1,0:T(8,128)(2,1)}, u32[]{:S(2)}, u32[]{:S(2)}) collective-permute-start(bf16[768,384]{1,0:T(8,128)(2,1)} %get-tuple-element.148), channel_id=1, source_target_pairs={{0,2},{1,18},{2,0},{3,16},{4,6},{5,22},{6,4},{7,20},{8,10},{9,26},... | collective-permute-start | bytes 1769480 | tf_op jit(solution)/shard_map/ppermute | solution.py:675
  172.9 27.2 %collective-permute-start.19 = (bf16[768,384]{1,0:T(8,128)(2,1)}, bf16[768,384]{1,0:T(8,128)(2,1)}, u32[]{:S(2)}, u32[]{:S(2)}) collective-permute-start(bf16[768,384]{1,0:T(8,128)(2,1)} %get-tuple-element.149), channel_id=1, source_target_pairs={{0,3},{1,19},{2,1},{3,17},{4,7},{5,23},{6,5},{7,21},{8,11},{9,27},... | collective-permute-start | bytes 1769480 | tf_op jit(solution)/shard_map/ppermute | solution.py:675
  173.3 26.8 %collective-permute-start.16 = (bf16[768,384]{1,0:T(8,128)(2,1)}, bf16[768,384]{1,0:T(8,128)(2,1)}, u32[]{:S(2)}, u32[]{:S(2)}) collective-permute-start(bf16[768,384]{1,0:T(8,128)(2,1)} %get-tuple-element.128), channel_id=1, source_target_pairs={{1,16},{3,18},{5,20},{7,22},{9,24},{11,26},{13,28},{15,30},{16,1},... | collective-permute-start | bytes 1769480 | tf_op jit(solution)/shard_map/ppermute | solution.py:675
  178.7 7.7 %copy-start.2 = (bf16[1024,768]{1,0:T(8,128)(2,1)S(1)}, bf16[1024,768]{1,0:T(8,128)(2,1)}, u32[]{:S(2)}) copy-start(bf16[1024,768]{1,0:T(8,128)(2,1)} %get-tuple-element.136.refs_3_.cot_ref) | copy-start | bytes 4718596
  178.7 7.7 %copy-start.4 = (bf16[1024,768]{1,0:T(8,128)(2,1)S(1)}, bf16[1024,768]{1,0:T(8,128)(2,1)}, u32[]{:S(2)}) copy-start(bf16[1024,768]{1,0:T(8,128)(2,1)} %copy-done.3) | copy-start | bytes 4718596
  178.7 7.7 %copy-start.6 = (bf16[1024,768]{1,0:T(8,128)(2,1)S(1)}, bf16[1024,768]{1,0:T(8,128)(2,1)}, u32[]{:S(2)}) copy-start(bf16[1024,768]{1,0:T(8,128)(2,1)} %copy-done.5) | copy-start | bytes 4718596
  191.8 8.8 %copy-start.34 = (bf16[768,384]{1,0:T(8,128)(2,1)S(1)}, bf16[768,384]{1,0:T(8,128)(2,1)}, u32[]{:S(2)}) copy-start(bf16[768,384]{1,0:T(8,128)(2,1)} %get-tuple-element.121) | copy-start | bytes 1769476
  191.8 8.8 %copy-start.36 = (bf16[768,384]{1,0:T(8,128)(2,1)S(1)}, bf16[768,384]{1,0:T(8,128)(2,1)}, u32[]{:S(2)}) copy-start(bf16[768,384]{1,0:T(8,128)(2,1)} %copy-done.35) | copy-start | bytes 1769476
  191.8 8.8 %copy-start.38 = (bf16[768,384]{1,0:T(8,128)(2,1)S(1)}, bf16[768,384]{1,0:T(8,128)(2,1)}, u32[]{:S(2)}) copy-start(bf16[768,384]{1,0:T(8,128)(2,1)} %copy-done.37) | copy-start | bytes 1769476
  191.8 8.8 %copy-start.40 = (bf16[768,384]{1,0:T(8,128)(2,1)S(1)}, bf16[768,384]{1,0:T(8,128)(2,1)}, u32[]{:S(2)}) copy-start(bf16[768,384]{1,0:T(8,128)(2,1)} %copy-done.39) | copy-start | bytes 1769476
  191.8 8.8 %copy-start.42 = (bf16[768,384]{1,0:T(8,128)(2,1)S(1)}, bf16[768,384]{1,0:T(8,128)(2,1)}, u32[]{:S(2)}) copy-start(bf16[768,384]{1,0:T(8,128)(2,1)} %copy-done.41) | copy-start | bytes 1769476
  200.1 2.0 collective-permute-start.24
  200.5 2.1 collective-permute-start.25
  202.8 31.2 %collective-permute-start.26 = (bf16[512,768]{1,0:T(8,128)(2,1)S(1)}, bf16[512,768]{1,0:T(8,128)(2,1)S(1)}, u32[]{:S(2)}, u32[]{:S(2)}) collective-permute-start(bf16[512,768]{1,0:T(8,128)(2,1)S(1)} %add_convert_fusion.block_own), channel_id=1, source_target_pairs={{1,16},{3,18},{5,20},{7,22},{9,24},{11,26},{13,28},{15,30},{16,1},... | collective-permute-start | bytes 2359304 | tf_op jit(solution)/shard_map/ppermute | solution.py:671
  205.9 2.6 collective-permute-start.20
  206.0 2.5 collective-permute-start.21
  213.7 3.6 %collective-permute-start.22 = (f32[9,768]{1,0:T(8,128)S(1)}, f32[9,768]{1,0:T(8,128)S(1)}, u32[]{:S(2)}, u32[]{:S(2)}) collective-permute-start(f32[9,768]{1,0:T(8,128)S(1)} %pad_maximum_fusion.4), channel_id=1, source_target_pairs={{0,16},{16,0},{1,17},{17,1},{2,18},{18,2},{3,19},{19,3},{4,20},{20... | collective-permute-start | bytes 82952 | tf_op jit(solution)/shard_map/ppermute | solution.py:741
  217.3 6.6 %collective-permute-start.23 = (f32[9,768]{1,0:T(8,128)S(1)}, f32[9,768]{1,0:T(8,128)S(1)}, u32[]{:S(2)}, u32[]{:S(2)}) collective-permute-start(f32[9,768]{1,0:T(8,128)S(1)} %add.100), channel_id=1, source_target_pairs={{0,2},{2,0},{1,3},{3,1},{4,6},{6,4},{5,7},{7,5},{8,10},{10,8},{9,1... | collective-permute-start | bytes 82952 | tf_op jit(solution)/shard_map/ppermute | solution.py:741
  219.2 9.3 %collective-permute-start.30 = (bf16[192,384]{1,0:T(8,128)(2,1)S(1)}, bf16[192,384]{1,0:T(8,128)(2,1)S(1)}, u32[]{:S(2)}, u32[]{:S(2)}) collective-permute-start(bf16[192,384]{1,0:T(8,128)(2,1)S(1)} %get-tuple-element.232), channel_id=1, source_target_pairs={{0,12},{4,0},{8,4},{12,8},{1,13},{5,1},{9,5},{13,9},{2,14},{6,2},{... | collective-permute-start | bytes 442376 | tf_op jit(solution)/shard_map/ppermute | solution.py:733
  219.4 11.0 %collective-permute-start.29 = (bf16[192,384]{1,0:T(8,128)(2,1)S(1)}, bf16[192,384]{1,0:T(8,128)(2,1)S(1)}, u32[]{:S(2)}, u32[]{:S(2)}) collective-permute-start(bf16[192,384]{1,0:T(8,128)(2,1)S(1)} %get-tuple-element.233), channel_id=1, source_target_pairs={{0,8},{4,12},{8,0},{12,4},{1,9},{5,13},{9,1},{13,5},{2,10},{6,14},... | collective-permute-start | bytes 442376 | tf_op jit(solution)/shard_map/ppermute | solution.py:733
  221.7 12.3 %collective-permute-start.28 = (bf16[192,384]{1,0:T(8,128)(2,1)S(1)}, bf16[192,384]{1,0:T(8,128)(2,1)S(1)}, u32[]{:S(2)}, u32[]{:S(2)}) collective-permute-start(bf16[192,384]{1,0:T(8,128)(2,1)S(1)} %get-tuple-element.234), channel_id=1, source_target_pairs={{0,4},{4,8},{8,12},{12,0},{1,5},{5,9},{9,13},{13,1},{2,6},{6,10},{... | collective-permute-start | bytes 442376 | tf_op jit(solution)/shard_map/ppermute | solution.py:733
  223.9 10.1 %collective-permute-start.27 = (bf16[192,384]{1,0:T(8,128)(2,1)}, bf16[192,384]{1,0:T(8,128)(2,1)S(1)}, u32[]{:S(2)}, u32[]{:S(2)}) collective-permute-start(bf16[192,384]{1,0:T(8,128)(2,1)} %reduce-scatter.8.cloned.1.call-done), channel_id=1, source_target_pairs={{1,16},{3,18},{5,20},{7,22},{9,24},{11,26},{13,28},{15,30},{16,1},... | collective-permute-start | bytes 442376 | tf_op jit(solution)/shard_map/ppermute | solution.py:671
  234.1 14.0 %copy-start.7 = (bf16[512,768]{1,0:T(8,128)(2,1)S(1)}, bf16[512,768]{1,0:T(8,128)(2,1)}, u32[]{:S(2)}) copy-start(bf16[512,768]{1,0:T(8,128)(2,1)} %shard_map.230.grad_own) | copy-start | bytes 2359300
  234.1 23.6 %copy-start.17 = (f32[5]{0:T(128)S(1)}, f32[5]{0:T(128)}, u32[]{:S(2)}) copy-start(f32[5]{0:T(128)} %weight_ref.1) | copy-start | bytes 64
  234.1 28.0 %copy-start.9 = (f32[512,768]{1,0:T(8,128)S(1)}, f32[512,768]{1,0:T(8,128)}, u32[]{:S(2)}) copy-start(f32[512,768]{1,0:T(8,128)} %get-tuple-element.101.part_ref) | copy-start | bytes 4718596
  234.1 28.0 %copy-start.16 = (s32[4]{0:T(128)S(1)}, s32[4]{0:T(128)}, u32[]{:S(2)}) copy-start(s32[4]{0:T(128)} %pad_add_fusion.flags.refs_0_) | copy-start | bytes 52
  235.3 9.5 %collective-permute-start.35 = (bf16[192,1152]{1,0:T(8,128)(2,1)S(1)}, bf16[192,1152]{1,0:T(8,128)(2,1)S(1)}, u32[]{:S(2)}, u32[]{:S(2)}) collective-permute-start(bf16[192,1152]{1,0:T(8,128)(2,1)S(1)} %get-tuple-element.237), channel_id=1, source_target_pairs={{0,2},{2,0},{1,3},{3,1},{4,6},{6,4},{5,7},{7,5},{8,10},{10,8},{9,1... | collective-permute-start | bytes 1327112 | tf_op jit(solution)/shard_map/ppermute | solution.py:690
  244.9 19.1 %collective-permute-start.36 = (bf16[2,192,1152]{2,1,0:T(8,128)(2,1)S(1)}, bf16[2,192,1152]{2,1,0:T(8,128)(2,1)S(1)}, u32[]{:S(2)}, u32[]{:S(2)}) collective-permute-start(bf16[2,192,1152]{2,1,0:T(8,128)(2,1)S(1)} %pad_maximum_fusion.2.here_ref), channel_id=1, source_target_pairs={{0,1},{1,0},{2,3},{3,2},{4,5},{5,4},{6,7},{7,6},{8,9},{9,8},{10,11... | collective-permute-start | bytes 2654216 | tf_op jit(solution)/shard_map/ppermute | solution.py:694
  248.1 14.0 %collective-permute-start.31 = (bf16[512,768]{1,0:T(8,128)(2,1)S(1)}, bf16[512,768]{1,0:T(8,128)(2,1)S(1)}, u32[]{:S(2)}, u32[]{:S(2)}) collective-permute-start(bf16[512,768]{1,0:T(8,128)(2,1)S(1)} %copy-done.7), channel_id=1, source_target_pairs={{1,16},{3,18},{5,20},{7,22},{9,24},{11,26},{13,28},{15,30},{16,1},... | collective-permute-start | bytes 2359304 | tf_op jit(solution)/shard_map/ppermute | solution.py:671
  250.8 1.3 collective-permute-start.32
  252.2 4.0 %collective-permute-start.33 = (f32[9,768]{1,0:T(8,128)S(1)}, f32[9,768]{1,0:T(8,128)S(1)}, u32[]{:S(2)}, u32[]{:S(2)}) collective-permute-start(f32[9,768]{1,0:T(8,128)S(1)} %add.113), channel_id=1, source_target_pairs={{0,4},{4,0},{8,12},{12,8},{1,5},{5,1},{9,13},{13,9},{2,6},{6,2},{1... | collective-permute-start | bytes 82952 | tf_op jit(solution)/shard_map/ppermute | solution.py:741
  256.2 4.0 %collective-permute-start.34 = (f32[9,768]{1,0:T(8,128)S(1)}, f32[9,768]{1,0:T(8,128)S(1)}, u32[]{:S(2)}, u32[]{:S(2)}) collective-permute-start(f32[9,768]{1,0:T(8,128)S(1)} %add.114), channel_id=1, source_target_pairs={{0,8},{4,12},{8,0},{12,4},{1,9},{5,13},{9,1},{13,5},{2,10},{6,14},... | collective-permute-start | bytes 82952 | tf_op jit(solution)/shard_map/ppermute | solution.py:741
  (28 other events, 64.1 us)
Sparse Core Ops, SparseCore 0:
  104.9 47.3 reduce-scatter.9
  162.4 18.1 reduce-scatter.7
  201.9 18.5 reduce-scatter.5

commit v8 on v7

--- a/solution.py
+++ b/solution.py
@@ -558,25 +558,30 @@
     return streamed(unproject_kernel, 4, [flags], fields, sent_and_kept(whole, width), [], 5, SNUG)
 
 
-def last_kernel(flags, rows_ref, resid_ref, keep_ref, got_first, got_second, vectors, out_ref):
+def last_kernel(
+    flags, rows_ref, resid_ref, keep_ref, block_keep, got_first, got_second, block_first, block_second, vectors, out_ref
+):
+    first = pl.program_id(0) == 0
     unit, scale = norm_parts(rows_ref[...].astype(jnp.float32))
-    got = jnp.where(pl.program_id(0) == 0, got_first[...], got_second[...]).astype(jnp.float32)
+    got = jnp.where(first, got_first[...], got_second[...]).astype(jnp.float32)
     inner = (keep_ref[...] + got) * vectors[0:1, :]
     mean = jnp.mean(inner, axis=-1, keepdims=True)
     slant = jnp.mean(inner * unit, axis=-1, keepdims=True)
     grad = resid_ref[...].astype(jnp.float32) + scale * (inner - mean - unit * slant)
-    out_ref[...] = grad.astype(jnp.bfloat16)
-
-
-def last(flags, rows, resid, keep, got, vectors):
+    out_ref[0] = grad.astype(jnp.bfloat16)
+    got = jnp.where(first, block_first[...], block_second[...]).astype(jnp.float32)
+    out_ref[1] = (block_keep[...] + got).astype(jnp.bfloat16)
+
+
+def last(flags, rows, resid, keep, block_keep, got, vectors):
     half, width = keep.shape
     size = half // 2
 
     def mine(i, flags):
         return flags[1] * 2 + i
 
-    out = ((half, width), jnp.bfloat16, (size, width), lambda i, flags: (i, 0))
-    fields = [by_rows(rows, size, mine), by_rows(resid, size, mine), by_rows(keep, size)]
+    out = ((2, half, width), jnp.bfloat16, (2, size, width), lambda i, flags: (0, i, 0))
+    fields = [by_rows(rows, size, mine), by_rows(resid, size, mine), by_rows(keep, size), by_rows(block_keep, size)]
     return streamed(last_kernel, 2, [flags], fields + [*got, vectors], [out], [], 3)[0]
 
 
@@ -614,16 +619,17 @@
     )(dwa, history, cot)
 
 
-def present_kernel(flags, weight_ref, part_ref, grad_own, grad_got, block_own, block_got, out_ref, grad_ref):
-    here = jnp.where(flags[0] == 1, block_own[...], block_got[...]).astype(jnp.float32)
+def present_kernel(flags, weight_ref, part_ref, own_ref, got_ref, out_ref, grad_ref):
+    here = jnp.where(flags[0] == 1, own_ref[1], got_ref[1]).astype(jnp.float32)
     out_ref[...] = (part_ref[...] + weight_ref[weight_ref.shape[0] - 1] * here).astype(jnp.bfloat16)
-    grad_ref[...] = jnp.where(flags[0] == 1, grad_own[...], grad_got[...])
-
-
-def present(flags, weight, *fields):
-    rows, width = fields[0].shape
+    grad_ref[...] = jnp.where(flags[0] == 1, own_ref[0], got_ref[0])
+
+
+def present(flags, weight, part, own, got):
+    rows, width = part.shape
+    both = (2, ROWS, width), lambda i, *scalars: (0, i, 0)
     out = ((rows, width), jnp.bfloat16, (ROWS, width), lambda i, *scalars: (i, 0))
-    fields = [by_rows(field, ROWS) for field in fields]
+    fields = [by_rows(part, ROWS), (own, *both), (got, *both)]
     return streamed(present_kernel, rows // ROWS, [flags, weight], fields, [out] * 2, [], 2, SNUG)
 
 
@@ -831,27 +837,22 @@
     attn_one = add(jnp.where(same, owned[0], moved[0]), *moved[1:])
     attn_moved = move_rows(attn_one)
     got = [swap_near(field) for field in sent]
-    block_half = add(block_keep, jnp.concatenate(got[2:], axis=0))
-    block_moved = swap_diagonal(block_half)
-    input_grad = last(flags, layer_rows, grad_attn, after(keep, attn_one), got[:2], vectors)
+    ours = last(flags, layer_rows, grad_attn, after(keep, attn_one), block_keep, got, vectors)
     early_sum = after(early_sum, attn_one)
     early_got = swap_diagonal(early_sum)
     small = jnp.concatenate([sums_one[:2], sums_two[:2], sums_now[:1], sums_past[:hist_count]], axis=0)
-    small = after(small, input_grad)
-    for name in ("tp", "far"):
+    small = after(small, ours)
+    for name in ("near", "tp", "far"):
         small = sum_over(small, name)
-    small, input_grad, block_moved, late_sum, early_sum, early_got, *attn_moved = lax.optimization_barrier(
-        (small, input_grad, block_moved, late_sum, early_sum, early_got, *attn_moved)
-    )
-    input_moved = swap_diagonal(input_grad)
-    for name in ("near", "dp"):
-        small = sum_over(small, name)
+    small, ours, late_sum, early_sum, early_got, *attn_moved = lax.optimization_barrier(
+        (small, ours, late_sum, early_sum, early_got, *attn_moved)
+    )
+    theirs = swap_diagonal(ours)
+    small = sum_over(small, "dp")
     attn_sum = add(*attn_moved)
     blocks = jnp.concatenate([attn_sum, jnp.where(same, early_sum, early_got), late_sum], axis=1)
     here = jnp.stack([blocks, swap_far(blocks)])
-    output, grad_input = present(
-        flags, dwa_weights, past_sum, input_grad, input_moved, block_half, block_moved
-    )
+    output, grad_input = present(flags, dwa_weights, past_sum, ours, theirs)
     grad_w_qkv, grad_w_out, grad_w_up, grad_w_down = place(flags, here, swap_near(here))
 
     return (

time: 278 us -> 265 us (0.953)
  starting transfers between devices: 58.7 us -> 52.2 us
  waiting for transfers between devices: 28 us -> 22.4 us
  local copies, waits for them, and re-layouts: 23.9 us -> 21 us
    ppermute x3, waiting for transfers between devices: 5.55 us -> 0.01 us  [move_rows(): lax.ppermute(sent, 'dp', [(d, (d + step) % dps) for d in range(dps)])]
    ppermute x5, starting transfers between devices: 6.45 us -> 1.03 us  [sum_over(): lax.ppermute(field, name, [(d, d ^ bit) for d in range(size)])]
    ppermute x1, waiting for transfers between devices: 9.39 us -> 4.3 us  [swap_far(): return lax.ppermute(field, 'far', [(0, 1), (1, 0)])]
    ppermute x5, waiting for transfers between devices: 7.62 us -> 12.5 us  [sum_over(): lax.ppermute(field, name, [(d, d ^ bit) for d in range(size)])]
    unnamed x104 -> x94, local copies, waits for them, and re-layouts: 16.9 us -> 14.1 us
    ppermute x9 -> x8, starting transfers between devices: 26.9 us -> 26 us  [swap_diagonal(): lax.ppermute(field, AXES, moves(away, lambda t, d, k, c: (c, d, k, t)))]
  transfers between devices with their start and end apart: 40 -> 39, of which waited for: 13 -> 10; matrix products, arithmetic and copies ran while one was open for 11% -> 12% of each run, Pallas kernels for 45% -> 47%
where the time goes in v8:
time: 265 us; the launch traced here: 261 us
  Pallas kernels  126 us (48%)
  starting transfers between devices  52.2 us (20%)
  other arithmetic  24 us (9%)
  waiting for transfers between devices  22.4 us (8%)
  local copies, waits for them, and re-layouts  21 us (8%)
  between operations  14.6 us (6%)
    pallas_call x10, Pallas kernels, streamed(): pl.pallas_call(kernel, grid_spec=pltpu.PrefetchScalarGridSpec(num_scalar_...  85.2 us
    ppermute x8, starting transfers between devices, swap_diagonal(): lax.ppermute(field, AXES, moves(away, lambda t, d, k, c: (c, d, k, t)))  26 us
    pallas_call x1, Pallas kernels, attend_back(): pl.pallas_call(functools.partial(attend_back_kernel, reach), grid=(width...  23.1 us
    unnamed x94, local copies, waits for them, and re-layouts  14.1 us
    pallas_call x1, Pallas kernels, attend(): pl.pallas_call(functools.partial(attend_kernel, reach), grid=(width // LA...  12.8 us
    ppermute x5, waiting for transfers between devices, sum_over(): lax.ppermute(field, name, [(d, d ^ bit) for d in range(size)])  12.5 us
    ppermute x8, starting transfers between devices, send_to_owner(): lax.ppermute(field, AXES, moves(away if not other_far and (not other_tp)...  11.5 us
    ppermute x10, starting transfers between devices, swap_near(): return lax.ppermute(field, 'near', [(0, 1), (1, 0)])  5.52 us
  transfers between devices with their start and end apart: 39, of which 10 were waited for; matrix products, arithmetic and copies ran while one was open for 12% of the time, Pallas kernels for 47%

profile of v8, /device:TPU:9, one launch (start us, length us, event | category | flops | bytes accessed | tf_op | source)
XLA Modules:
  0.0 260.8 jit_solution(3268047114236339858)
XLA Ops:
  8.0 3.2 %collective-permute-start = (bf16[512,768]{1,0:T(8,128)(2,1)}, bf16[512,768]{1,0:T(8,128)(2,1)}, u32[]{:S(2)}, u32[]{:S(2)}) collective-permute-start(bf16[512,768]{1,0:T(8,128)(2,1)} %bitcast.45), channel_id=1, source_target_pairs={{1,16},{3,18},{5,20},{7,22},{9,24},{11,26},{13,28},{15,30},{16,1},... | collective-permute-start | bytes 2359304 | tf_op jit(solution)/shard_map/ppermute | solution.py:677
  11.2 2.2 constant_dynamic-slice_fusion
  13.4 2.5 collective-permute-start.3
  17.0 2.3 pad_maximum_fusion.1
  19.3 3.3 %fusion.10 = (bf16[768,768]{1,0:T(8,128)(2,1)}, bf16[768,768]{1,0:T(8,128)(2,1)S(1)}, bf16[768,768]{1,0:T(8,128)(2,1)S(1)}, bf16[768,768]{1,0:T(8,128)(2,1)}) fusion(bf16[1536,768]{1,0:T(8,128)(2,1)} %refs_7_.1, bf16[768,1536]{1,0:T(8,128)(2,1)S(1)} %copy-done.19), kind=kLoop, calls=%fused_computation.51 | loop fusion | bytes 9437184 | tf_op jit(solution)/shard_map/dynamic_slice | solution.py:715
  22.6 1.6 pad_maximum_fusion
  24.2 4.4 %shard_map.220 = (bf16[4,512,768]{2,1,0:T(8,128)(2,1)}, f32[512,768]{1,0:T(8,128)}, f32[8,768]{1,0:T(8,128)}) custom-call(f32[5]{0:T(128)} %weight_ref.1, bf16[4,512,768]{2,1,0:T(8,128)(2,1)} %bitcast.43, bf16[512,768]{1,0:T(8,128)(2,1)} %bitcast.40), custom_call_target="tpu_custom_call" | custom-call | bytes 9000000 | tf_op jit(solution)/shard_map/pallas_call | solution.py:607
  30.3 3.2 %collective-permute-start.5 = (bf16[896,768]{1,0:T(8,128)(2,1)S(1)}, bf16[896,768]{1,0:T(8,128)(2,1)S(1)}, u32[]{:S(2)}, u32[]{:S(2)}) collective-permute-start(bf16[896,768]{1,0:T(8,128)(2,1)S(1)} %copy-done.27), channel_id=1, source_target_pairs={{1,16},{3,18},{5,20},{7,22},{9,24},{11,26},{13,28},{15,30},{16,1},... | collective-permute-start | bytes 4128776 | tf_op jit(solution)/shard_map/ppermute | solution.py:677
  33.5 1.2 broadcast_select_fusion.1
  34.8 3.1 %collective-permute-start.4 = (bf16[3,384,384]{2,1,0:T(8,128)(2,1)}, bf16[3,384,384]{2,1,0:T(8,128)(2,1)S(1)}, u32[]{:S(2)}, u32[]{:S(2)}) collective-permute-start(bf16[3,384,384]{2,1,0:T(8,128)(2,1)} %collective-permute-done.3.w_near), channel_id=1, source_target_pairs={{1,3},{3,1},{5,7},{7,5},{9,11},{11,9},{13,15},{15,13},{16,18},{18,... | collective-permute-start | bytes 2654216 | tf_op jit(solution)/shard_map/ppermute | solution.py:692
  37.9 1.6 select_convert_fusion.apart_ref
  39.5 3.7 %fusion.1 = (f32[1024,128]{1,0:T(8,128)}, f32[1024,128]{1,0:T(8,128)}) fusion(f32[128]{0:T(128)} %get-tuple-element.239, f32[128]{0:T(128)} %get-tuple-element.240, f32[1024]{0:T(1024)S(1)} %subtract_convert_fusion), kind=kLoop, calls=%fused_computation.12 | loop fusion | flops 262144 | bytes 1053696 | tf_op jit(solution)/shard_map/mul | solution.py:792
  43.2 2.6 %collective-permute-start.8 = (bf16[1536,768]{1,0:T(8,128)(2,1)}, bf16[1536,768]{1,0:T(8,128)(2,1)}, u32[]{:S(2)}, u32[]{:S(2)}) collective-permute-start(bf16[1536,768]{1,0:T(8,128)(2,1)} %pad_maximum_fusion), channel_id=1, source_target_pairs={{1,16},{3,18},{5,20},{7,22},{9,24},{11,26},{13,28},{15,30},{16,1},... | collective-permute-start | bytes 7077896 | tf_op jit(solution)/shard_map/ppermute | solution.py:677
  45.9 0.9 fusion.2.member_ref
  46.8 1.9 maximum_select_fusion.rows_ref.refs_2_
  48.8 0.9 copy-done.28
  49.7 9.6 %shard_map.221 = (bf16[3,1024,384]{2,1,0:T(8,128)(2,1)}, bf16[768,1024]{1,0:T(8,128)(2,1)}, bf16[3,768,384]{2,1,0:T(8,128)(2,1)}) custom-call(s32[4]{0:T(128)} %pad_add_fusion.flags.refs_0_, bf16[1024,768]{1,0:T(8,128)(2,1)} %maximum_select_fusion.rows_ref.refs_2_, f32[1024,128]{1,0:T(8,128)} %get-tuple-element.103.cos_ref, ...), custom_call_target="tpu_custom_call" | custom-call | bytes 24000000 | tf_op jit(solution)/shard_map/pallas_call | solution.py:223
  59.3 12.8 %shard_map.222.mixed_ref = bf16[1024,384]{1,0:T(8,128)(2,1)} custom-call(bf16[1024,128]{1,0:T(8,128)(2,1)} %select_convert_fusion.apart_ref, bf16[1024,128]{1,0:T(8,128)(2,1)} %fusion.2.member_ref, bf16[3,1024,384]{2,1,0:T(8,128)(2,1)} %get-tuple-element.107.q_ref.k_ref.v_ref, bf16[3,1024,384]{2,1,0:T(8,128)(2,1)} %get-tuple-element.107.q_ref.k_ref.v_ref, ...), custom_call_target="tpu_custom_call" | custom-call | bytes 36000000 | tf_op jit(solution)/shard_map/pallas_call | solution.py:99
  73.3 1.0 convolution_convert_fusion.refs_3_.own_ref
  74.3 3.5 %collective-permute-start.9 = (bf16[768,768]{1,0:T(8,128)(2,1)}, bf16[768,768]{1,0:T(8,128)(2,1)}, u32[]{:S(2)}, u32[]{:S(2)}) collective-permute-start(bf16[768,768]{1,0:T(8,128)(2,1)} %get-tuple-element.116), channel_id=1, source_target_pairs={{1,16},{3,18},{5,20},{7,22},{9,24},{11,26},{13,28},{15,30},{16,1},... | collective-permute-start | bytes 3538952 | tf_op jit(solution)/shard_map/ppermute | solution.py:677
  77.9 2.2 collective-permute-start.10
  80.2 2.3 collective-permute-done.7.refs_6_
  82.5 0.9 copy-done.30
  83.4 1.2 copy-done.5
  84.6 18.9 %shard_map.223 = (bf16[1024,768]{1,0:T(8,128)(2,1)}, bf16[768,1024]{1,0:T(8,128)(2,1)}, bf16[1024,768]{1,0:T(8,128)(2,1)}, bf16[768,1024]{1,0:T(8,128)(2,1)}, bf...) custom-call(s32[4]{0:T(128)} %pad_add_fusion.flags.refs_0_, ...), custom_call_target="tpu_custom_call" | custom-call | bytes 51000000 | tf_op jit(solution)/shard_map/pallas_call | solution.py:223
  103.5 1.3 collective-permute-done.10.refs_9_
  104.9 16.3 %shard_map.224 = (bf16[1024,768]{1,0:T(8,128)(2,1)}, bf16[1024,768]{1,0:T(8,128)(2,1)}, bf16[768,768]{1,0:T(8,128)(2,1)}, bf16[768,384]{1,0:T(8,128)(2,1)}, bf16...) custom-call(s32[4]{0:T(128)} %pad_add_fusion.flags.refs_0_, ...), custom_call_target="tpu_custom_call" | custom-call | bytes 51000000 | tf_op jit(solution)/shard_map/pallas_call | solution.py:223
  121.2 1.7 collective-permute-start.13
  123.0 1.3 collective-permute-start.14
  124.3 3.5 %collective-permute-start.12 = (bf16[768,384]{1,0:T(8,128)(2,1)}, bf16[768,384]{1,0:T(8,128)(2,1)S(1)}, u32[]{:S(2)}, u32[]{:S(2)}) collective-permute-start(bf16[768,384]{1,0:T(8,128)(2,1)} %get-tuple-element.120), channel_id=1, source_target_pairs={{1,16},{3,18},{5,20},{7,22},{9,24},{11,26},{13,28},{15,30},{16,1},... | collective-permute-start | bytes 1769480 | tf_op jit(solution)/shard_map/ppermute | solution.py:681
  127.7 1.2 copy-done.26
  129.0 10.1 %shard_map.225 = (bf16[1024,768]{1,0:T(8,128)(2,1)}, bf16[1024,384]{1,0:T(8,128)(2,1)}, bf16[768,384]{1,0:T(8,128)(2,1)}, f32[8,768]{1,0:T(8,128)}) custom-call(s32[4]{0:T(128)} %pad_add_fusion.flags.refs_0_, bf16[1024,768]{1,0:T(8,128)(2,1)} %maximum_select_fusion.rows_ref.refs_2_, bf16[1024,768]{1,0:T(8,128)(2,1)} %copy-done.3, ...), custom_call_target="tpu_custom_call" | custom-call | bytes 24000000 | tf_op jit(solution)/shard_map/pallas_call | solution.py:223
  139.1 23.1 %shard_map.226.grad_ref = bf16[3,1024,384]{2,1,0:T(8,128)(2,1)} custom-call(bf16[1024,128]{1,0:T(8,128)(2,1)} %select_convert_fusion.apart_ref, bf16[1024,128]{1,0:T(8,128)(2,1)} %fusion.2.member_ref, f32[1024,128]{1,0:T(8,128)} %get-tuple-element.103.cos_ref, f32[1024,128]{1,0:T(8,128)} %get-tuple-element.104.sin_ref, ...), custom_call_target="tpu_custom_call" | custom-call | bytes 66000000 | tf_op jit(solution)/shard_map/pallas_call | solution.py:175
  162.3 7.6 %shard_map.227 = (bf16[768,384]{1,0:T(8,128)(2,1)}, bf16[768,384]{1,0:T(8,128)(2,1)}, bf16[768,384]{1,0:T(8,128)(2,1)}, bf16[768,384]{1,0:T(8,128)(2,1)}) custom-call(s32[4]{0:T(128)} %pad_add_fusion.flags.refs_0_, bf16[768,1024]{1,0:T(8,128)(2,1)} %get-tuple-element.125.turned_ref, bf16[768,384]{1,0:T(8,128)(2,1)} %get-tuple-element.126.out_grad_ref, ...), custom_call_target="tpu_custom_call" | custom-call | bytes 12000000 | tf_op jit(solution)/shard_map/pallas_call | solution.py:223
  170.0 2.4 collective-permute-start.16
  172.4 1.5 collective-permute-start.18
  174.0 1.1 collective-permute-start.19
  175.0 2.8 %add_convert_fusion = bf16[768,384]{1,0:T(8,128)(2,1)} fusion(bf16[768,384]{1,0:T(8,128)(2,1)} %copy-done.34, bf16[768,384]{1,0:T(8,128)(2,1)} %copy-done.33, bf16[768,384]{1,0:T(8,128)(2,1)} %copy-done.32, bf16[768,384]{1,0:T(8,128)(2,1)} %get-tuple-element.120, bf16[768,384]{1,0:T(8,128)(2,1)} %copy-done.35, pred[]{:T(512)S(6)} %eq.35), kind=kLoop, calls=%fused_computation.5 | loop fusion | flops 2654208 | bytes 3538945 | tf_op jit(solution)/shard_map/convert_element_type | solution.py:719
  178.7 1.7 copy-done.1
  180.4 5.9 %shard_map.228 = (f32[512,768]{1,0:T(8,128)S(1)}, bf16[256,768]{1,0:T(8,128)(2,1)}, bf16[256,768]{1,0:T(8,128)(2,1)}, f32[8,768]{1,0:T(8,128)S(1)}) custom-call(s32[4]{0:T(128)S(1)} %copy-done.16, bf16[3,1024,384]{2,1,0:T(8,128)(2,1)S(1)} %copy-done.1, bf16[1024,768]{1,0:T(8,128)(2,1)S(1)} %copy-done, bf16[3,768,384]{2,1,0:T(8,128)(2,1)S(1)} %copy-done.8), custom_call_target="tpu_custom_call" | custom-call | bytes 15000000 | tf_op jit(solution)/shard_map/pallas_call | solution.py:223
  186.2 1.2 copy-done.10
  187.5 1.4 copy-done.12
  188.9 1.4 copy-done.13
  190.3 1.3 copy-done.14
  191.5 1.3 copy-done.15
  192.8 6.9 %shard_map.229 = (f32[512,768]{1,0:T(8,128)S(1)}, bf16[256,768]{1,0:T(8,128)(2,1)S(1)}, bf16[256,768]{1,0:T(8,128)(2,1)S(1)}, f32[8,768]{1,0:T(8,128)S(1)}) custom-call(s32[4]{0:T(128)S(1)} %copy-done.16, bf16[1024,768]{1,0:T(8,128)(2,1)S(1)} %copy-done.12, bf16[1024,768]{1,0:T(8,128)(2,1)S(1)} %copy-done.13, bf16[1024,768]{1,0:T(8,128)(2,1)S(1)} %copy-done, ...), custom_call_target="tpu_custom_call" | custom-call | bytes 18000000 | tf_op jit(solution)/shard_map/pallas_call | solution.py:223
  199.8 1.8 collective-permute-done.19
  202.7 2.0 add_convert_fusion.1
  205.0 2.3 collective-permute-start.29
  207.4 2.2 collective-permute-start.28
  209.5 3.9 %collective-permute-start.27 = (bf16[192,384]{1,0:T(8,128)(2,1)}, bf16[192,384]{1,0:T(8,128)(2,1)S(1)}, u32[]{:S(2)}, u32[]{:S(2)}) collective-permute-start(bf16[192,384]{1,0:T(8,128)(2,1)} %reduce-scatter.8.cloned.1.call-done), channel_id=1, source_target_pairs={{1,16},{3,18},{5,20},{7,22},{9,24},{11,26},{13,28},{15,30},{16,1},... | collective-permute-start | bytes 442376 | tf_op jit(solution)/shard_map/ppermute | solution.py:677
  214.3 5.4 %shard_map.230.own_ref = bf16[2,512,768]{2,1,0:T(8,128)(2,1)} custom-call(s32[4]{0:T(128)} %pad_add_fusion.flags.refs_0_, bf16[1024,768]{1,0:T(8,128)(2,1)} %maximum_select_fusion.rows_ref.refs_2_, bf16[1024,768]{1,0:T(8,128)(2,1)} %get-tuple-element.140.resid_ref, f32[512,768]{1,0:T(8,128)} %copy-done.10, f32[512,768]{1,0:T(8,128)} %copy-done.11, ...), custom_call_target="tpu_custom_call" | custom-call | bytes 9000000 | tf_op jit(solution)/shard_map/pallas_call | solution.py:223
  219.7 1.2 collective-permute-done.24
  221.0 2.9 %collective-permute-done.25 = f32[9,768]{1,0:T(8,128)S(1)} collective-permute-done((f32[9,768]{1,0:T(8,128)S(1)}, f32[9,768]{1,0:T(8,128)S(1)}, u32[]{:S(2)}, u32[]{:S(2)}) %collective-permute-start.25) | collective-permute-done | bytes 27680 | tf_op jit(solution)/shard_map/ppermute | solution.py:747
  224.1 2.8 %collective-permute-done.26 = f32[9,768]{1,0:T(8,128)S(1)} collective-permute-done((f32[9,768]{1,0:T(8,128)S(1)}, f32[9,768]{1,0:T(8,128)S(1)}, u32[]{:S(2)}, u32[]{:S(2)}) %collective-permute-start.26) | collective-permute-done | bytes 27680 | tf_op jit(solution)/shard_map/ppermute | solution.py:747
  227.1 1.0 fusion.9
  228.3 4.8 %collective-permute-start.31 = (bf16[2,512,768]{2,1,0:T(8,128)(2,1)S(1)}, bf16[2,512,768]{2,1,0:T(8,128)(2,1)S(1)}, u32[]{:S(2)}, u32[]{:S(2)}) collective-permute-start(bf16[2,512,768]{2,1,0:T(8,128)(2,1)S(1)} %copy-done.7), channel_id=1, source_target_pairs={{1,16},{3,18},{5,20},{7,22},{9,24},{11,26},{13,28},{15,30},{16,1},... | collective-permute-start | bytes 4718600 | tf_op jit(solution)/shard_map/ppermute | solution.py:677
  233.2 4.3 %collective-permute-done.34 = bf16[192,1152]{1,0:T(8,128)(2,1)S(1)} collective-permute-done((bf16[192,1152]{1,0:T(8,128)(2,1)S(1)}, bf16[192,1152]{1,0:T(8,128)(2,1)S(1)}, u32[]{:S(2)}, u32[]{:S(2)}) %collective-permute-start.34) | collective-permute-done | bytes 442400 | tf_op jit(solution)/shard_map/ppermute | solution.py:696
  237.6 3.4 %collective-permute-start.35 = (bf16[2,192,1152]{2,1,0:T(8,128)(2,1)S(1)}, bf16[2,192,1152]{2,1,0:T(8,128)(2,1)S(1)}, u32[]{:S(2)}, u32[]{:S(2)}) collective-permute-start(bf16[2,192,1152]{2,1,0:T(8,128)(2,1)S(1)} %pad_maximum_fusion.2.here_ref), channel_id=1, source_target_pairs={{0,1},{1,0},{2,3},{3,2},{4,5},{5,4},{6,7},{7,6},{8,9},{9,8},{10,11... | collective-permute-start | bytes 2654216 | tf_op jit(solution)/shard_map/ppermute | solution.py:700
  240.9 3.0 %collective-permute-done.32 = f32[9,768]{1,0:T(8,128)S(1)} collective-permute-done((f32[9,768]{1,0:T(8,128)S(1)}, f32[9,768]{1,0:T(8,128)S(1)}, u32[]{:S(2)}, u32[]{:S(2)}) %collective-permute-start.32) | collective-permute-done | bytes 27680 | tf_op jit(solution)/shard_map/ppermute | solution.py:747
  245.2 2.6 collective-permute-done.33
  247.8 1.3 slice_reduce_fusion
  249.7 2.5 shard_map.232
  252.2 2.1 shard_map.231
  (171 shorter events, 11.1 us)
Async XLA Ops:
  7.2 9.8 %copy-start.42 = (f32[768]{0:T(1024)S(1)}, f32[768]{0:T(1024)}, u32[]{:S(2)}) copy-start(f32[768]{0:T(1024)} %param.18) | copy-start | bytes 9220
  7.2 9.8 %copy-start.43 = (f32[768]{0:T(1024)S(1)}, f32[768]{0:T(1024)}, u32[]{:S(2)}) copy-start(f32[768]{0:T(1024)} %param.19) | copy-start | bytes 9220
  7.2 9.8 %copy-start.44 = (f32[768]{0:T(1024)S(1)}, f32[768]{0:T(1024)}, u32[]{:S(2)}) copy-start(f32[768]{0:T(1024)} %param.22) | copy-start | bytes 9220
  7.2 9.8 %copy-start.45 = (f32[768]{0:T(1024)S(1)}, f32[768]{0:T(1024)}, u32[]{:S(2)}) copy-start(f32[768]{0:T(1024)} %param.23) | copy-start | bytes 9220
  7.2 9.8 %copy-start.21 = (bf16[1,512,768]{2,1,0:T(8,128)(2,1)S(1)}, bf16[1,512,768]{2,1,0:T(8,128)(2,1)}, u32[]{:S(2)}) copy-start(bf16[1,512,768]{2,1,0:T(8,128)(2,1)} %param.15) | copy-start | bytes 2359300
  7.2 155.0 %reduce-scatter.10.cloned.1.call-start = ((), (), s32[]{:S(2)}) async-start(), calls=%async_computation.5 | async-start | bytes 2949120
  7.3 22.6 %collective-permute-start.2 = (s32[1,3]{1,0:T(1,128)}, s32[1,3]{1,0:T(1,128)S(1)}, u32[]{:S(2)}, u32[]{:S(2)}) collective-permute-start(s32[1,3]{1,0:T(1,128)} %param.16), channel_id=1, source_target_pairs={{0,1},{1,0},{2,3},{3,2},{4,5},{5,4},{6,7},{7,6},{8,9},{9,8},{10,11... | collective-permute-start | bytes 44 | tf_op jit(solution)/shard_map/ppermute | solution.py:700
  8.0 22.2 %collective-permute-start = (bf16[512,768]{1,0:T(8,128)(2,1)}, bf16[512,768]{1,0:T(8,128)(2,1)}, u32[]{:S(2)}, u32[]{:S(2)}) collective-permute-start(bf16[512,768]{1,0:T(8,128)(2,1)} %bitcast.45), channel_id=1, source_target_pairs={{1,16},{3,18},{5,20},{7,22},{9,24},{11,26},{13,28},{15,30},{16,1},... | collective-permute-start | bytes 2359304 | tf_op jit(solution)/shard_map/ppermute | solution.py:677
  13.4 21.4 %collective-permute-start.3 = (bf16[3,384,384]{2,1,0:T(8,128)(2,1)}, bf16[3,384,384]{2,1,0:T(8,128)(2,1)}, u32[]{:S(2)}, u32[]{:S(2)}) collective-permute-start(bf16[3,384,384]{2,1,0:T(8,128)(2,1)} %constant_dynamic-slice_fusion), channel_id=1, source_target_pairs={{1,16},{3,18},{5,20},{7,22},{9,24},{11,26},{13,28},{15,30},{16,1},... | collective-permute-start | bytes 2654216 | tf_op jit(solution)/shard_map/ppermute | solution.py:677
  24.2 9.3 %copy-start.29 = (bf16[1,512,768]{2,1,0:T(8,128)(2,1)S(1)}, bf16[1,512,768]{2,1,0:T(8,128)(2,1)}, u32[]{:S(2)}) copy-start(bf16[1,512,768]{2,1,0:T(8,128)(2,1)} %param.13) | copy-start | bytes 2359300
  30.3 41.9 %collective-permute-start.5 = (bf16[896,768]{1,0:T(8,128)(2,1)S(1)}, bf16[896,768]{1,0:T(8,128)(2,1)S(1)}, u32[]{:S(2)}, u32[]{:S(2)}) collective-permute-start(bf16[896,768]{1,0:T(8,128)(2,1)S(1)} %copy-done.27), channel_id=1, source_target_pairs={{1,16},{3,18},{5,20},{7,22},{9,24},{11,26},{13,28},{15,30},{16,1},... | collective-permute-start | bytes 4128776 | tf_op jit(solution)/shard_map/ppermute | solution.py:677
  34.7 12.1 %collective-permute-start.1 = (bf16[512,768]{1,0:T(8,128)(2,1)S(1)}, bf16[512,768]{1,0:T(8,128)(2,1)S(1)}, u32[]{:S(2)}, u32[]{:S(2)}) collective-permute-start(bf16[512,768]{1,0:T(8,128)(2,1)S(1)} %broadcast_select_fusion.1), channel_id=1, source_target_pairs={{0,1},{1,0},{2,3},{3,2},{4,5},{5,4},{6,7},{7,6},{8,9},{9,8},{10,11... | collective-permute-start | bytes 2359304 | tf_op jit(solution)/shard_map/ppermute | solution.py:700
  34.8 14.0 %collective-permute-start.4 = (bf16[3,384,384]{2,1,0:T(8,128)(2,1)}, bf16[3,384,384]{2,1,0:T(8,128)(2,1)S(1)}, u32[]{:S(2)}, u32[]{:S(2)}) collective-permute-start(bf16[3,384,384]{2,1,0:T(8,128)(2,1)} %collective-permute-done.3.w_near), channel_id=1, source_target_pairs={{1,3},{3,1},{5,7},{7,5},{9,11},{11,9},{13,15},{15,13},{16,18},{18,... | collective-permute-start | bytes 2654216 | tf_op jit(solution)/shard_map/ppermute | solution.py:692
  43.2 39.3 %collective-permute-start.8 = (bf16[1536,768]{1,0:T(8,128)(2,1)}, bf16[1536,768]{1,0:T(8,128)(2,1)}, u32[]{:S(2)}, u32[]{:S(2)}) collective-permute-start(bf16[1536,768]{1,0:T(8,128)(2,1)} %pad_maximum_fusion), channel_id=1, source_target_pairs={{1,16},{3,18},{5,20},{7,22},{9,24},{11,26},{13,28},{15,30},{16,1},... | collective-permute-start | bytes 7077896 | tf_op jit(solution)/shard_map/ppermute | solution.py:677
  59.3 12.8 %copy-start.22 = (bf16[1,512,768]{2,1,0:T(8,128)(2,1)S(1)}, bf16[1,512,768]{2,1,0:T(8,128)(2,1)}, u32[]{:S(2)}) copy-start(bf16[1,512,768]{2,1,0:T(8,128)(2,1)} %param.15) | copy-start | bytes 2359300
  59.3 12.8 %copy-start.25 = (bf16[384,768]{1,0:T(8,128)(2,1)S(1)}, bf16[384,768]{1,0:T(8,128)(2,1)}, u32[]{:S(2)}) copy-start(bf16[384,768]{1,0:T(8,128)(2,1)} %param.21) | copy-start | bytes 1769476
  73.2 6.9 %copy-start.20 = (bf16[896,768]{1,0:T(8,128)(2,1)}, bf16[896,768]{1,0:T(8,128)(2,1)S(1)}, u32[]{:S(2)}) copy-start(bf16[896,768]{1,0:T(8,128)(2,1)S(1)} %broadcast_select_fusion.w_ref) | copy-start | bytes 4128772
  74.2 8.3 %copy-start.3 = (bf16[1024,768]{1,0:T(8,128)(2,1)}, bf16[1024,768]{1,0:T(8,128)(2,1)S(1)}, u32[]{:S(2)}) copy-start(bf16[1024,768]{1,0:T(8,128)(2,1)S(1)} %convolution_convert_fusion.refs_3_.own_ref) | copy-start | bytes 4718596
  74.2 8.3 %collective-permute-start.6 = (bf16[1024,768]{1,0:T(8,128)(2,1)S(1)}, bf16[1024,768]{1,0:T(8,128)(2,1)S(1)}, u32[]{:S(2)}, u32[]{:S(2)}) collective-permute-start(bf16[1024,768]{1,0:T(8,128)(2,1)S(1)} %convolution_convert_fusion.refs_3_.own_ref), channel_id=1, source_target_pairs={{0,1},{1,0},{2,3},{3,2},{4,5},{5,4},{6,7},{7,6},{8,9},{9,8},{10,11... | collective-permute-start | bytes 4718600 | tf_op jit(solution)/shard_map/ppermute | solution.py:700
  74.3 29.1 %collective-permute-start.9 = (bf16[768,768]{1,0:T(8,128)(2,1)}, bf16[768,768]{1,0:T(8,128)(2,1)}, u32[]{:S(2)}, u32[]{:S(2)}) collective-permute-start(bf16[768,768]{1,0:T(8,128)(2,1)} %get-tuple-element.116), channel_id=1, source_target_pairs={{1,16},{3,18},{5,20},{7,22},{9,24},{11,26},{13,28},{15,30},{16,1},... | collective-permute-start | bytes 3538952 | tf_op jit(solution)/shard_map/ppermute | solution.py:677
  77.9 26.9 %collective-permute-start.10 = (bf16[768,768]{1,0:T(8,128)(2,1)}, bf16[768,768]{1,0:T(8,128)(2,1)}, u32[]{:S(2)}, u32[]{:S(2)}) collective-permute-start(bf16[768,768]{1,0:T(8,128)(2,1)} %get-tuple-element.117), channel_id=1, source_target_pairs={{1,16},{3,18},{5,20},{7,22},{9,24},{11,26},{13,28},{15,30},{16,1},... | collective-permute-start | bytes 3538952 | tf_op jit(solution)/shard_map/ppermute | solution.py:677
  80.2 2.4 collective-permute-start.7
  104.8 100.2 %reduce-scatter.8.cloned.1.call-start = ((), (), s32[]{:S(2)}) async-start(), calls=%async_computation.4 | async-start | bytes 737280 | tf_op jit(solution)/shard_map/reduce_scatter | solution.py:727
  121.2 6.6 %collective-permute-start.11 = (bf16[1024,768]{1,0:T(8,128)(2,1)}, bf16[1024,768]{1,0:T(8,128)(2,1)S(1)}, u32[]{:S(2)}, u32[]{:S(2)}) collective-permute-start(bf16[1024,768]{1,0:T(8,128)(2,1)} %get-tuple-element.118.back_own), channel_id=1, source_target_pairs={{0,1},{1,0},{2,3},{3,2},{4,5},{5,4},{6,7},{7,6},{8,9},{9,8},{10,11... | collective-permute-start | bytes 4718600 | tf_op jit(solution)/shard_map/ppermute | solution.py:700
  121.2 40.9 %collective-permute-start.13 = (bf16[768,384]{1,0:T(8,128)(2,1)}, bf16[768,384]{1,0:T(8,128)(2,1)S(1)}, u32[]{:S(2)}, u32[]{:S(2)}) collective-permute-start(bf16[768,384]{1,0:T(8,128)(2,1)} %get-tuple-element.121), channel_id=1, source_target_pairs={{0,1},{1,17},{2,3},{3,19},{4,5},{5,21},{6,7},{7,23},{8,9},{9,25},{... | collective-permute-start | bytes 1769480 | tf_op jit(solution)/shard_map/ppermute | solution.py:681
  123.0 39.2 %collective-permute-start.14 = (bf16[768,384]{1,0:T(8,128)(2,1)}, bf16[768,384]{1,0:T(8,128)(2,1)S(1)}, u32[]{:S(2)}, u32[]{:S(2)}) collective-permute-start(bf16[768,384]{1,0:T(8,128)(2,1)} %get-tuple-element.122), channel_id=1, source_target_pairs={{0,2},{1,18},{2,0},{3,16},{4,6},{5,22},{6,4},{7,20},{8,10},{9,26},... | collective-permute-start | bytes 1769480 | tf_op jit(solution)/shard_map/ppermute | solution.py:681
  124.3 37.9 %collective-permute-start.15 = (bf16[768,384]{1,0:T(8,128)(2,1)}, bf16[768,384]{1,0:T(8,128)(2,1)S(1)}, u32[]{:S(2)}, u32[]{:S(2)}) collective-permute-start(bf16[768,384]{1,0:T(8,128)(2,1)} %get-tuple-element.123), channel_id=1, source_target_pairs={{0,3},{1,19},{2,1},{3,17},{4,7},{5,23},{6,5},{7,21},{8,11},{9,27},... | collective-permute-start | bytes 1769480 | tf_op jit(solution)/shard_map/ppermute | solution.py:681
  124.3 37.9 %collective-permute-start.12 = (bf16[768,384]{1,0:T(8,128)(2,1)}, bf16[768,384]{1,0:T(8,128)(2,1)S(1)}, u32[]{:S(2)}, u32[]{:S(2)}) collective-permute-start(bf16[768,384]{1,0:T(8,128)(2,1)} %get-tuple-element.120), channel_id=1, source_target_pairs={{1,16},{3,18},{5,20},{7,22},{9,24},{11,26},{13,28},{15,30},{16,1},... | collective-permute-start | bytes 1769480 | tf_op jit(solution)/shard_map/ppermute | solution.py:681
  162.2 11.8 %copy-start.32 = (bf16[768,384]{1,0:T(8,128)(2,1)}, bf16[768,384]{1,0:T(8,128)(2,1)S(1)}, u32[]{:S(2)}) copy-start(bf16[768,384]{1,0:T(8,128)(2,1)S(1)} %collective-permute-done.13) | copy-start | bytes 1769476
  162.2 11.8 %copy-start.33 = (bf16[768,384]{1,0:T(8,128)(2,1)}, bf16[768,384]{1,0:T(8,128)(2,1)S(1)}, u32[]{:S(2)}) copy-start(bf16[768,384]{1,0:T(8,128)(2,1)S(1)} %collective-permute-done.14) | copy-start | bytes 1769476
  162.2 7.8 %copy-start.34 = (bf16[768,384]{1,0:T(8,128)(2,1)}, bf16[768,384]{1,0:T(8,128)(2,1)S(1)}, u32[]{:S(2)}) copy-start(bf16[768,384]{1,0:T(8,128)(2,1)S(1)} %collective-permute-done.15) | copy-start | bytes 1769476
  162.2 7.8 %copy-start.35 = (bf16[768,384]{1,0:T(8,128)(2,1)}, bf16[768,384]{1,0:T(8,128)(2,1)S(1)}, u32[]{:S(2)}) copy-start(bf16[768,384]{1,0:T(8,128)(2,1)S(1)} %collective-permute-done.12) | copy-start | bytes 1769476
  162.3 64.7 %reduce-scatter.6.cloned.1.call-start = ((), (), s32[]{:S(2)}) async-start(), calls=%async_computation.3 | async-start | bytes 737280 | tf_op jit(solution)/shard_map/reduce_scatter | solution.py:727
  170.0 31.6 %collective-permute-start.16 = (bf16[768,384]{1,0:T(8,128)(2,1)}, bf16[768,384]{1,0:T(8,128)(2,1)}, u32[]{:S(2)}, u32[]{:S(2)}) collective-permute-start(bf16[768,384]{1,0:T(8,128)(2,1)} %get-tuple-element.127), channel_id=1, source_target_pairs={{1,16},{3,18},{5,20},{7,22},{9,24},{11,26},{13,28},{15,30},{16,1},... | collective-permute-start | bytes 1769480 | tf_op jit(solution)/shard_map/ppermute | solution.py:681
  172.4 27.4 %collective-permute-start.17 = (bf16[768,384]{1,0:T(8,128)(2,1)}, bf16[768,384]{1,0:T(8,128)(2,1)}, u32[]{:S(2)}, u32[]{:S(2)}) collective-permute-start(bf16[768,384]{1,0:T(8,128)(2,1)} %get-tuple-element.146), channel_id=1, source_target_pairs={{0,1},{1,17},{2,3},{3,19},{4,5},{5,21},{6,7},{7,23},{8,9},{9,25},{... | collective-permute-start | bytes 1769480 | tf_op jit(solution)/shard_map/ppermute | solution.py:681
  172.4 27.4 %collective-permute-start.18 = (bf16[768,384]{1,0:T(8,128)(2,1)}, bf16[768,384]{1,0:T(8,128)(2,1)}, u32[]{:S(2)}, u32[]{:S(2)}) collective-permute-start(bf16[768,384]{1,0:T(8,128)(2,1)} %get-tuple-element.147), channel_id=1, source_target_pairs={{0,2},{1,18},{2,0},{3,16},{4,6},{5,22},{6,4},{7,20},{8,10},{9,26},... | collective-permute-start | bytes 1769480 | tf_op jit(solution)/shard_map/ppermute | solution.py:681
  174.0 27.6 %collective-permute-start.19 = (bf16[768,384]{1,0:T(8,128)(2,1)}, bf16[768,384]{1,0:T(8,128)(2,1)}, u32[]{:S(2)}, u32[]{:S(2)}) collective-permute-start(bf16[768,384]{1,0:T(8,128)(2,1)} %get-tuple-element.148), channel_id=1, source_target_pairs={{0,3},{1,19},{2,1},{3,17},{4,7},{5,23},{6,5},{7,21},{8,11},{9,27},... | collective-permute-start | bytes 1769480 | tf_op jit(solution)/shard_map/ppermute | solution.py:681
  180.4 7.1 %copy-start.2 = (bf16[1024,768]{1,0:T(8,128)(2,1)S(1)}, bf16[1024,768]{1,0:T(8,128)(2,1)}, u32[]{:S(2)}) copy-start(bf16[1024,768]{1,0:T(8,128)(2,1)} %get-tuple-element.135.refs_3_.cot_ref) | copy-start | bytes 4718596
  180.4 7.1 %copy-start.4 = (bf16[1024,768]{1,0:T(8,128)(2,1)S(1)}, bf16[1024,768]{1,0:T(8,128)(2,1)}, u32[]{:S(2)}) copy-start(bf16[1024,768]{1,0:T(8,128)(2,1)} %copy-done.3) | copy-start | bytes 4718596
  180.4 7.1 %copy-start.6 = (bf16[1024,768]{1,0:T(8,128)(2,1)S(1)}, bf16[1024,768]{1,0:T(8,128)(2,1)}, u32[]{:S(2)}) copy-start(bf16[1024,768]{1,0:T(8,128)(2,1)} %copy-done.5) | copy-start | bytes 4718596
  192.8 9.9 %copy-start.31 = (bf16[768,384]{1,0:T(8,128)(2,1)S(1)}, bf16[768,384]{1,0:T(8,128)(2,1)}, u32[]{:S(2)}) copy-start(bf16[768,384]{1,0:T(8,128)(2,1)} %get-tuple-element.127) | copy-start | bytes 1769476
  201.6 3.5 %collective-permute-start.20 = (bf16[256,768]{1,0:T(8,128)(2,1)}, bf16[256,768]{1,0:T(8,128)(2,1)S(1)}, u32[]{:S(2)}, u32[]{:S(2)}) collective-permute-start(bf16[256,768]{1,0:T(8,128)(2,1)} %get-tuple-element.156), channel_id=1, source_target_pairs={{0,1},{1,0},{2,3},{3,2},{4,5},{5,4},{6,7},{7,6},{8,9},{9,8},{10,11... | collective-permute-start | bytes 1179656 | tf_op jit(solution)/shard_map/ppermute | solution.py:700
  202.2 5.2 %collective-permute-start.21 = (bf16[256,768]{1,0:T(8,128)(2,1)}, bf16[256,768]{1,0:T(8,128)(2,1)S(1)}, u32[]{:S(2)}, u32[]{:S(2)}) collective-permute-start(bf16[256,768]{1,0:T(8,128)(2,1)} %get-tuple-element.157), channel_id=1, source_target_pairs={{0,1},{1,0},{2,3},{3,2},{4,5},{5,4},{6,7},{7,6},{8,9},{9,8},{10,11... | collective-permute-start | bytes 1179656 | tf_op jit(solution)/shard_map/ppermute | solution.py:700
  202.2 7.3 %collective-permute-start.22 = (bf16[256,768]{1,0:T(8,128)(2,1)S(1)}, bf16[256,768]{1,0:T(8,128)(2,1)S(1)}, u32[]{:S(2)}, u32[]{:S(2)}) collective-permute-start(bf16[256,768]{1,0:T(8,128)(2,1)S(1)} %get-tuple-element.158), channel_id=1, source_target_pairs={{0,1},{1,0},{2,3},{3,2},{4,5},{5,4},{6,7},{7,6},{8,9},{9,8},{10,11... | collective-permute-start | bytes 1179656 | tf_op jit(solution)/shard_map/ppermute | solution.py:700
  202.7 10.8 %collective-permute-start.23 = (bf16[256,768]{1,0:T(8,128)(2,1)S(1)}, bf16[256,768]{1,0:T(8,128)(2,1)S(1)}, u32[]{:S(2)}, u32[]{:S(2)}) collective-permute-start(bf16[256,768]{1,0:T(8,128)(2,1)S(1)} %get-tuple-element.159), channel_id=1, source_target_pairs={{0,1},{1,0},{2,3},{3,2},{4,5},{5,4},{6,7},{7,6},{8,9},{9,8},{10,11... | collective-permute-start | bytes 1179656 | tf_op jit(solution)/shard_map/ppermute | solution.py:700
  204.8 22.1 %collective-permute-start.30 = (bf16[192,384]{1,0:T(8,128)(2,1)S(1)}, bf16[192,384]{1,0:T(8,128)(2,1)S(1)}, u32[]{:S(2)}, u32[]{:S(2)}) collective-permute-start(bf16[192,384]{1,0:T(8,128)(2,1)S(1)} %get-tuple-element.230), channel_id=1, source_target_pairs={{0,12},{4,0},{8,4},{12,8},{1,13},{5,1},{9,5},{13,9},{2,14},{6,2},{... | collective-permute-start | bytes 442376 | tf_op jit(solution)/shard_map/ppermute | solution.py:739
  205.0 8.5 %copy-start.36 = (bf16[256,768]{1,0:T(8,128)(2,1)}, bf16[256,768]{1,0:T(8,128)(2,1)S(1)}, u32[]{:S(2)}) copy-start(bf16[256,768]{1,0:T(8,128)(2,1)S(1)} %collective-permute-done.20.got_first) | copy-start | bytes 1179652
  205.0 21.9 %collective-permute-start.29 = (bf16[192,384]{1,0:T(8,128)(2,1)S(1)}, bf16[192,384]{1,0:T(8,128)(2,1)S(1)}, u32[]{:S(2)}, u32[]{:S(2)}) collective-permute-start(bf16[192,384]{1,0:T(8,128)(2,1)S(1)} %get-tuple-element.231), channel_id=1, source_target_pairs={{0,8},{4,12},{8,0},{12,4},{1,9},{5,13},{9,1},{13,5},{2,10},{6,14},... | collective-permute-start | bytes 442376 | tf_op jit(solution)/shard_map/ppermute | solution.py:739
  207.4 6.2 %copy-start.37 = (bf16[256,768]{1,0:T(8,128)(2,1)}, bf16[256,768]{1,0:T(8,128)(2,1)S(1)}, u32[]{:S(2)}) copy-start(bf16[256,768]{1,0:T(8,128)(2,1)S(1)} %collective-permute-done.21.got_second) | copy-start | bytes 1179652
  207.4 19.6 %collective-permute-start.28 = (bf16[192,384]{1,0:T(8,128)(2,1)S(1)}, bf16[192,384]{1,0:T(8,128)(2,1)S(1)}, u32[]{:S(2)}, u32[]{:S(2)}) collective-permute-start(bf16[192,384]{1,0:T(8,128)(2,1)S(1)} %get-tuple-element.232), channel_id=1, source_target_pairs={{0,4},{4,8},{8,12},{12,0},{1,5},{5,9},{9,13},{13,1},{2,6},{6,10},{... | collective-permute-start | bytes 442376 | tf_op jit(solution)/shard_map/ppermute | solution.py:739
  209.5 17.4 %collective-permute-start.27 = (bf16[192,384]{1,0:T(8,128)(2,1)}, bf16[192,384]{1,0:T(8,128)(2,1)S(1)}, u32[]{:S(2)}, u32[]{:S(2)}) collective-permute-start(bf16[192,384]{1,0:T(8,128)(2,1)} %reduce-scatter.8.cloned.1.call-done), channel_id=1, source_target_pairs={{1,16},{3,18},{5,20},{7,22},{9,24},{11,26},{13,28},{15,30},{16,1},... | collective-permute-start | bytes 442376 | tf_op jit(solution)/shard_map/ppermute | solution.py:677
  214.3 12.7 %copy-start.40 = (bf16[192,384]{1,0:T(8,128)(2,1)S(1)}, bf16[192,384]{1,0:T(8,128)(2,1)}, u32[]{:S(2)}) copy-start(bf16[192,384]{1,0:T(8,128)(2,1)} %reduce-scatter.8.cloned.1.call-done) | copy-start | bytes 442372
  219.6 8.7 %copy-start.7 = (bf16[2,512,768]{2,1,0:T(8,128)(2,1)S(1)}, bf16[2,512,768]{2,1,0:T(8,128)(2,1)}, u32[]{:S(2)}) copy-start(bf16[2,512,768]{2,1,0:T(8,128)(2,1)} %shard_map.230.own_ref) | copy-start | bytes 4718596
  219.6 1.2 collective-permute-start.24
  220.9 3.0 %collective-permute-start.25 = (f32[9,768]{1,0:T(8,128)S(1)}, f32[9,768]{1,0:T(8,128)S(1)}, u32[]{:S(2)}, u32[]{:S(2)}) collective-permute-start(f32[9,768]{1,0:T(8,128)S(1)} %add.97), channel_id=1, source_target_pairs={{0,16},{16,0},{1,17},{17,1},{2,18},{18,2},{3,19},{19,3},{4,20},{20... | collective-permute-start | bytes 82952 | tf_op jit(solution)/shard_map/ppermute | solution.py:747
  223.9 3.0 %collective-permute-start.26 = (f32[9,768]{1,0:T(8,128)S(1)}, f32[9,768]{1,0:T(8,128)S(1)}, u32[]{:S(2)}, u32[]{:S(2)}) collective-permute-start(f32[9,768]{1,0:T(8,128)S(1)} %add.98), channel_id=1, source_target_pairs={{0,2},{2,0},{1,3},{3,1},{4,6},{6,4},{5,7},{7,5},{8,10},{10,8},{9,1... | collective-permute-start | bytes 82952 | tf_op jit(solution)/shard_map/ppermute | solution.py:747
  227.1 17.5 %copy-start.18 = (f32[5]{0:T(128)S(1)}, f32[5]{0:T(128)}, u32[]{:S(2)}) copy-start(f32[5]{0:T(128)} %weight_ref.1) | copy-start | bytes 64
  227.1 22.6 %copy-start.17 = (s32[4]{0:T(128)S(1)}, s32[4]{0:T(128)}, u32[]{:S(2)}) copy-start(s32[4]{0:T(128)} %pad_add_fusion.flags.refs_0_) | copy-start | bytes 52
  228.1 9.3 %collective-permute-start.34 = (bf16[192,1152]{1,0:T(8,128)(2,1)S(1)}, bf16[192,1152]{1,0:T(8,128)(2,1)S(1)}, u32[]{:S(2)}, u32[]{:S(2)}) collective-permute-start(bf16[192,1152]{1,0:T(8,128)(2,1)S(1)} %get-tuple-element.235), channel_id=1, source_target_pairs={{0,2},{2,0},{1,3},{3,1},{4,6},{6,4},{5,7},{7,5},{8,10},{10,8},{9,1... | collective-permute-start | bytes 1327112 | tf_op jit(solution)/shard_map/ppermute | solution.py:696
  228.3 23.9 %collective-permute-start.31 = (bf16[2,512,768]{2,1,0:T(8,128)(2,1)S(1)}, bf16[2,512,768]{2,1,0:T(8,128)(2,1)S(1)}, u32[]{:S(2)}, u32[]{:S(2)}) collective-permute-start(bf16[2,512,768]{2,1,0:T(8,128)(2,1)S(1)} %copy-done.7), channel_id=1, source_target_pairs={{1,16},{3,18},{5,20},{7,22},{9,24},{11,26},{13,28},{15,30},{16,1},... | collective-permute-start | bytes 4718600 | tf_op jit(solution)/shard_map/ppermute | solution.py:677
  237.5 14.8 %copy-start.9 = (f32[512,768]{1,0:T(8,128)S(1)}, f32[512,768]{1,0:T(8,128)}, u32[]{:S(2)}) copy-start(f32[512,768]{1,0:T(8,128)} %get-tuple-element.100.part_ref) | copy-start | bytes 4718596
  237.6 12.2 %collective-permute-start.35 = (bf16[2,192,1152]{2,1,0:T(8,128)(2,1)S(1)}, bf16[2,192,1152]{2,1,0:T(8,128)(2,1)S(1)}, u32[]{:S(2)}, u32[]{:S(2)}) collective-permute-start(bf16[2,192,1152]{2,1,0:T(8,128)(2,1)S(1)} %pad_maximum_fusion.2.here_ref), channel_id=1, source_target_pairs={{0,1},{1,0},{2,3},{3,2},{4,5},{5,4},{6,7},{7,6},{8,9},{9,8},{10,11... | collective-permute-start | bytes 2654216 | tf_op jit(solution)/shard_map/ppermute | solution.py:700
  240.9 3.0 %collective-permute-start.32 = (f32[9,768]{1,0:T(8,128)S(1)}, f32[9,768]{1,0:T(8,128)S(1)}, u32[]{:S(2)}, u32[]{:S(2)}) collective-permute-start(f32[9,768]{1,0:T(8,128)S(1)} %add.99), channel_id=1, source_target_pairs={{0,4},{4,0},{8,12},{12,8},{1,5},{5,1},{9,13},{13,9},{2,6},{6,2},{1... | collective-permute-start | bytes 82952 | tf_op jit(solution)/shard_map/ppermute | solution.py:747
  243.9 3.9 %collective-permute-start.33 = (f32[9,768]{1,0:T(8,128)S(1)}, f32[9,768]{1,0:T(8,128)S(1)}, u32[]{:S(2)}, u32[]{:S(2)}) collective-permute-start(f32[9,768]{1,0:T(8,128)S(1)} %add.110), channel_id=1, source_target_pairs={{0,8},{4,12},{8,0},{12,4},{1,9},{5,13},{9,1},{13,5},{2,10},{6,14},... | collective-permute-start | bytes 82952 | tf_op jit(solution)/shard_map/ppermute | solution.py:747
  (22 other events, 61.4 us)
Sparse Core Ops, SparseCore 0:
  104.9 47.4 reduce-scatter.9
  162.4 18.2 reduce-scatter.7
  183.5 20.2 reduce-scatter.5

commit v9 on v8

--- a/solution.py
+++ b/solution.py
@@ -64,7 +64,7 @@
     return query, jnp.concatenate([query, apart_ref[block_at(i), :]], axis=1)
 
 
-def attend_kernel(reach, apart_ref, member_ref, q_ref, k_ref, v_ref, out_ref, keys):
+def attend_kernel(reach, apart_ref, member_ref, q_ref, k_ref, v_ref, out_ref, logs_ref, keys):
     whole = q_ref.shape[0]
     lane = lax.broadcasted_iota(jnp.int32, (BLOCK, LANES), 1) // HEAD_DIM
     keys[:, :LANES] = k_ref[...]
@@ -78,13 +78,18 @@
         scores = jnp.where(key_at <= query_at, own, NEG_FILL)
         if count > 1:
             scores = jnp.concatenate([dot(query, keys[block_at(first, count - 1), :], NT), scores], axis=1)
-        exponent = jnp.exp(scores - jnp.max(scores, axis=1, keepdims=True))
+        row_max = jnp.max(scores, axis=1, keepdims=True)
+        exponent = jnp.exp(scores - row_max)
         row_sum = jnp.sum(exponent, axis=1, keepdims=True)
-        return dot(exponent.astype(jnp.bfloat16), v_ref[block_at(first, count), :]) * (1.0 / row_sum)
+        mixed = dot(exponent.astype(jnp.bfloat16), v_ref[block_at(first, count), :]) * (1.0 / row_sum)
+        return mixed, row_max + jnp.log(row_sum)
 
     def body(i, first, count):
-        mixed = [one(i, first, count, head) for head in range(2)]
+        mixed, logs = zip(*[one(i, first, count, head) for head in range(2)])
         out_ref[block_at(i), :] = jnp.where(lane == 0, *mixed).astype(out_ref.dtype)
+        turned = jnp.where(lane == 0, *logs).T
+        for head in range(2):
+            logs_ref[head : head + 1, block_at(i)] = turned[head * HEAD_DIM : head * HEAD_DIM + 1]
 
     each_block(whole, reach, body)
 
@@ -100,8 +105,14 @@
         functools.partial(attend_kernel, reach),
         grid=(width // LANES,),
         in_specs=[table, table, block(0), block(1), block(2)],
-        out_specs=pl.BlockSpec((whole, LANES), lambda p: (0, p)),
-        out_shape=jax.ShapeDtypeStruct((whole, width), jnp.bfloat16),
+        out_specs=[
+            pl.BlockSpec((whole, LANES), lambda p: (0, p)),
+            pl.BlockSpec((None, 8, whole), lambda p: (p, 0, 0)),
+        ],
+        out_shape=[
+            jax.ShapeDtypeStruct((whole, width), jnp.bfloat16),
+            jax.ShapeDtypeStruct((width // LANES, 8, whole), jnp.float32),
+        ],
         scratch_shapes=[pltpu.VMEM((whole, 2 * LANES), jnp.bfloat16)],
         compiler_params=pltpu.CompilerParams(vmem_limit_bytes=ROOM),
         cost_estimate=lasting(12),
@@ -116,7 +127,8 @@
 
 
 def attend_back_kernel(
-    reach, apart_ref, member_ref, cos_ref, sin_ref, q_ref, k_ref, v_ref, g_ref, out_ref, keys, keys_t, key_acc, value_acc
+    reach, apart_ref, member_ref, cos_ref, sin_ref, q_ref, k_ref, v_ref, g_ref, mixed_ref, logs_ref, out_ref,
+    keys, keys_t, key_acc, value_acc
 ):
     whole = q_ref.shape[0]
     lane = lax.broadcasted_iota(jnp.int32, (BLOCK, LANES), 1) // HEAD_DIM
@@ -137,11 +149,13 @@
         scores = jnp.where(key_at <= query_at, own, NEG_FILL)
         if count > 1:
             scores = jnp.concatenate([dot(keys[block_at(first, count - 1), :], query, NT), scores], axis=0)
-        exponent = jnp.exp(scores - jnp.max(scores, axis=0, keepdims=True))
-        probs = exponent * (1.0 / jnp.sum(exponent, axis=0, keepdims=True))
+        probs = jnp.exp(scores - logs_ref[head : head + 1, block_at(i)])
         grad_values = dot(probs.astype(jnp.bfloat16), grad)
-        weighted = probs * dot(v_ref[span, :], grad, NT)
-        grad_scores = (weighted - probs * jnp.sum(weighted, axis=0, keepdims=True)).astype(jnp.bfloat16)
+        product = grad.astype(jnp.float32) * mixed_ref[block_at(i), :].astype(jnp.float32)
+        high = product.astype(jnp.bfloat16)
+        ones = jnp.ones((8, LANES), jnp.bfloat16)
+        row_dot = dot(ones, high, NT) + dot(ones, (product - high.astype(jnp.float32)).astype(jnp.bfloat16), NT)
+        grad_scores = (probs * (dot(v_ref[span, :], grad, NT) - row_dot[:1])).astype(jnp.bfloat16)
         here = dot(keys_t[:, span], grad_scores)
         return grad_values, dot(grad_scores, plain), here
 
@@ -165,7 +179,7 @@
     lax.fori_loop(0, whole // BLOCK, finish, 0)
 
 
-def attend_back(apart, member, cos, sin, projected, grad_mixed, reach):
+def attend_back(apart, member, cos, sin, projected, grad_mixed, mixed, logs, reach):
     count, whole, width = projected.shape
 
     def block(c):
@@ -175,7 +189,10 @@
     return pl.pallas_call(
         functools.partial(attend_back_kernel, reach),
         grid=(width // LANES,),
-        in_specs=[table] * 4 + [block(0), block(1), block(2), pl.BlockSpec((whole, LANES), lambda p: (0, p))],
+        in_specs=[table] * 4
+        + [block(0), block(1), block(2)]
+        + [pl.BlockSpec((whole, LANES), lambda p: (0, p))] * 2
+        + [pl.BlockSpec((None, 8, whole), lambda p: (p, 0, 0))],
         out_specs=pl.BlockSpec((count, whole, LANES), lambda p: (0, 0, p)),
         out_shape=jax.ShapeDtypeStruct((count, whole, width), jnp.bfloat16),
         scratch_shapes=[
@@ -186,7 +203,7 @@
         ],
         compiler_params=pltpu.CompilerParams(vmem_limit_bytes=ROOM),
         cost_estimate=lasting(22),
-    )(apart, member, cos, sin, projected, projected, projected, grad_mixed)
+    )(apart, member, cos, sin, projected, projected, projected, grad_mixed, mixed, logs)
 
 
 ROWS = 256
@@ -252,13 +269,17 @@
     return field * cos + crossed * sin
 
 
+def join_rows(flags, own, near, far, out):
+    half = near.shape[1]
+    for index, got in ((flags[2], near), (1 - flags[2], far)):
+        at = pl.ds(pl.multiple_of(index * half, half), half)
+        out[:, at, :] = jnp.where(flags[0] == 1, own[:, at, :], got[...])
+
+
 def project_kernel(flags, rows_ref, cos_ref, sin_ref, vectors, w_own, w_near, w_far, out_ref, turned_ref, weight_ref):
     @pl.when(pl.program_id(0) == 0)
     def _():
-        half = w_near.shape[1]
-        for index, got in ((flags[2], w_near), (1 - flags[2], w_far)):
-            at = pl.ds(pl.multiple_of(index * half, half), half)
-            weight_ref[:, at, :] = jnp.where(flags[0] == 1, w_own[:, at, :], got[...])
+        join_rows(flags, w_own, w_near, w_far, weight_ref)
 
     unit, unused = norm_parts(rows_ref[...].astype(jnp.float32))
     norm = unit * vectors[0:1, :] + vectors[1:2, :]
@@ -286,9 +307,8 @@
         [
             ((count, whole, columns), low, (count, ROWS, columns), lambda i, flags: (0, i, 0)),
             ((width, whole), low, (width, ROWS), lambda i, flags: (0, i)),
-            (w_own.shape, low),
         ],
-        [],
+        [(w_own.shape, low)],
         8,
     )
 
@@ -535,7 +555,11 @@
     )
 
 
-def unproject_kernel(flags, grad_ref, rows_ref, weight, keep_ref, first, second, sums_ref):
+def unproject_kernel(flags, grad_ref, rows_ref, w_own, w_near, w_far, keep_ref, first, second, sums_ref, weight):
+    @pl.when(pl.program_id(0) == 0)
+    def _():
+        join_rows(flags, w_own, w_near, w_far, weight)
+
     total = dot(grad_ref[0], weight[0], NT)
     for c in range(1, grad_ref.shape[0]):
         total = total + dot(grad_ref[c], weight[c], NT)
@@ -550,12 +574,13 @@
     send_or_keep(total, total, first, second, keep_ref)
 
 
-def unproject(flags, grad, weight, rows):
+def unproject(flags, grad, weights, rows):
     whole, width = rows.shape
     count, unused, columns = grad.shape
     grads = (grad, (count, whole // 4, columns), lambda i, flags: (0, theirs_first(i, flags), 0))
-    fields = [grads, by_rows(rows, whole // 4, theirs_first), weight]
-    return streamed(unproject_kernel, 4, [flags], fields, sent_and_kept(whole, width), [], 5, SNUG)
+    fields = [grads, by_rows(rows, whole // 4, theirs_first), *weights]
+    scratch = [((count, width, columns), jnp.bfloat16)]
+    return streamed(unproject_kernel, 4, [flags], fields, sent_and_kept(whole, width), scratch, 5, SNUG + (4 << 20))
 
 
 def last_kernel(
@@ -799,10 +824,10 @@
     )
     early_got = swap_diagonal(after(early_got, input_got))
     last_got = swap_diagonal(after(last_own, input_got))
-    projected, norm_one_t, weight_qkv = project(
+    projected, norm_one_t = project(
         flags, layer_rows, vectors, cos_table, sin_table, w_qkv, qkv_near, qkv_far
     )
-    mixed = attend(apart, member, projected, LONGEST)
+    mixed, logs = attend(apart, member, projected, LONGEST)
     late_up = swap_diagonal(after(late_up, mixed))
     late_down = swap_diagonal(after(late_down, mixed))
     last_got = jnp.where(same, last_own, after(last_got, mixed))
@@ -821,13 +846,17 @@
     grad_down = kept[2]
     fields = [layer_rows, attn, attn_got, grad_down, back, swap_near(back)]
     grad_attn, grad_mixed, grad_out, sums_two = middle(flags, fields, mixed, vectors, last_got)
-    grad_qkv = attend_back(apart, member, cos_table, sin_table, projected, grad_mixed, LONGEST)
+    grad_qkv = attend_back(
+        apart, member, cos_table, sin_table, projected, grad_mixed, mixed, logs, LONGEST
+    )
     grad_qkv, *late_moved = lax.optimization_barrier((grad_qkv, *late_moved))
     owned = weigh(flags, norm_one_t, grad_qkv, grad_out)
     moved = [send_to_owner(owned[j], j // 2, j % 2) for j in range(4)]
     early_sum = scatter_rows(after(early_sum, grad_qkv))
     late_sum = scatter_rows(add(jnp.where(same, late_owned[0], after(late_moved[0], owned[0])), *late_moved[1:]))
-    keep, *send, sums_one = unproject(flags, after(grad_qkv, owned[0]), weight_qkv, layer_rows)
+    keep, *send, sums_one = unproject(
+        flags, after(grad_qkv, owned[0]), (w_qkv, qkv_near, qkv_far), layer_rows
+    )
     block_keep, *block_send, sums_now = lower(
         flags, act_early, act_late, down_early, down_late, layer_rows, attn, attn_got, after(grad_down, keep)
     )

time: 265 us -> 262 us (0.989)
  Pallas kernels: 126 us -> 122 us
    pallas_call x1, Pallas kernels: 23.1 us -> 19.6 us  [attend_back(): pl.pallas_call(functools.partial(attend_back_kernel, reach), grid=(width...]
    unnamed x94 -> x98, local copies, waits for them, and re-layouts: 14.1 us -> 12.9 us
where the time goes in v9:
time: 262 us; the launch traced here: 257 us
  Pallas kernels  122 us (47%)
  starting transfers between devices  53.2 us (20%)
  other arithmetic  23.5 us (9%)
  waiting for transfers between devices  23.2 us (9%)
  local copies, waits for them, and re-layouts  19.9 us (8%)
  between operations  14.7 us (6%)
    pallas_call x10, Pallas kernels, streamed(): pl.pallas_call(kernel, grid_spec=pltpu.PrefetchScalarGridSpec(num_scalar_...  85 us
    ppermute x8, starting transfers between devices, swap_diagonal(): lax.ppermute(field, AXES, moves(away, lambda t, d, k, c: (c, d, k, t)))  26.1 us
    pallas_call x1, Pallas kernels, attend_back(): pl.pallas_call(functools.partial(attend_back_kernel, reach), grid=(width...  19.6 us
    pallas_call x1, Pallas kernels, attend(): pl.pallas_call(functools.partial(attend_kernel, reach), grid=(width // LA...  13 us
    unnamed x98, local copies, waits for them, and re-layouts  12.9 us
    ppermute x5, waiting for transfers between devices, sum_over(): lax.ppermute(field, name, [(d, d ^ bit) for d in range(size)])  12 us
    ppermute x8, starting transfers between devices, send_to_owner(): lax.ppermute(field, AXES, moves(away if not other_far and (not other_tp)...  11.7 us
    dynamic_slice x2, local copies, waits for them, and re-layouts, part_of(): return lax.dynamic_slice_in_dim(field, index * size, size, axis)  5.51 us
  transfers between devices with their start and end apart: 39, of which 10 were waited for; matrix products, arithmetic and copies ran while one was open for 12% of the time, Pallas kernels for 47%

profile of v9, /device:TPU:9, one launch (start us, length us, event | category | flops | bytes accessed | tf_op | source)
XLA Modules:
  0.0 257.4 jit_solution(9595892425387780772)
XLA Ops:
  8.0 3.1 %collective-permute-start = (bf16[512,768]{1,0:T(8,128)(2,1)}, bf16[512,768]{1,0:T(8,128)(2,1)}, u32[]{:S(2)}, u32[]{:S(2)}) collective-permute-start(bf16[512,768]{1,0:T(8,128)(2,1)} %bitcast.45), channel_id=1, source_target_pairs={{1,16},{3,18},{5,20},{7,22},{9,24},{11,26},{13,28},{15,30},{16,1},... | collective-permute-start | bytes 2359304 | tf_op jit(solution)/shard_map/ppermute | solution.py:702
  11.1 2.2 constant_dynamic-slice_fusion
  13.2 2.6 %collective-permute-start.3 = (bf16[3,384,384]{2,1,0:T(8,128)(2,1)}, bf16[3,384,384]{2,1,0:T(8,128)(2,1)S(1)}, u32[]{:S(2)}, u32[]{:S(2)}) collective-permute-start(bf16[3,384,384]{2,1,0:T(8,128)(2,1)} %constant_dynamic-slice_fusion), channel_id=1, source_target_pairs={{1,16},{3,18},{5,20},{7,22},{9,24},{11,26},{13,28},{15,30},{16,1},... | collective-permute-start | bytes 2654216 | tf_op jit(solution)/shard_map/ppermute | solution.py:702
  16.0 2.5 pad_maximum_fusion.1
  18.5 3.3 %fusion.10 = (bf16[768,768]{1,0:T(8,128)(2,1)}, bf16[768,768]{1,0:T(8,128)(2,1)S(1)}, bf16[768,768]{1,0:T(8,128)(2,1)S(1)}, bf16[768,768]{1,0:T(8,128)(2,1)}) fusion(bf16[1536,768]{1,0:T(8,128)(2,1)} %refs_7_.1, bf16[768,1536]{1,0:T(8,128)(2,1)S(1)} %copy-done.23), kind=kLoop, calls=%fused_computation.51 | loop fusion | bytes 9437184 | tf_op jit(solution)/shard_map/dynamic_slice | solution.py:740
  21.8 1.6 pad_maximum_fusion
  23.4 4.4 %shard_map.220 = (bf16[4,512,768]{2,1,0:T(8,128)(2,1)}, f32[512,768]{1,0:T(8,128)}, f32[8,768]{1,0:T(8,128)}) custom-call(f32[5]{0:T(128)} %weight_ref.1, bf16[4,512,768]{2,1,0:T(8,128)(2,1)} %bitcast.43, bf16[512,768]{1,0:T(8,128)(2,1)} %bitcast.41), custom_call_target="tpu_custom_call" | custom-call | bytes 9000000 | tf_op jit(solution)/shard_map/pallas_call | solution.py:632
  29.5 3.1 %collective-permute-start.5 = (bf16[896,768]{1,0:T(8,128)(2,1)S(1)}, bf16[896,768]{1,0:T(8,128)(2,1)}, u32[]{:S(2)}, u32[]{:S(2)}) collective-permute-start(bf16[896,768]{1,0:T(8,128)(2,1)S(1)} %copy-done.30), channel_id=1, source_target_pairs={{1,16},{3,18},{5,20},{7,22},{9,24},{11,26},{13,28},{15,30},{16,1},... | collective-permute-start | bytes 4128776 | tf_op jit(solution)/shard_map/ppermute | solution.py:702
  32.6 1.2 broadcast_select_fusion.1
  33.9 3.1 %collective-permute-start.4 = (bf16[3,384,384]{2,1,0:T(8,128)(2,1)S(1)}, bf16[3,384,384]{2,1,0:T(8,128)(2,1)S(1)}, u32[]{:S(2)}, u32[]{:S(2)}) collective-permute-start(bf16[3,384,384]{2,1,0:T(8,128)(2,1)S(1)} %collective-permute-done.3.w_near), channel_id=1, source_target_pairs={{1,3},{3,1},{5,7},{7,5},{9,11},{11,9},{13,15},{15,13},{16,18},{18,... | collective-permute-start | bytes 2654216 | tf_op jit(solution)/shard_map/ppermute | solution.py:717
  37.0 0.9 select_convert_fusion.apart_ref
  38.0 3.0 %fusion.1 = (f32[1024,128]{1,0:T(8,128)}, f32[1024,128]{1,0:T(8,128)}) fusion(f32[128]{0:T(128)S(1)} %get-tuple-element.241, f32[128]{0:T(128)S(1)} %get-tuple-element.242, f32[1024]{0:T(1024)S(1)} %subtract_convert_fusion), kind=kLoop, calls=%fused_computation.12 | loop fusion | flops 262144 | bytes 1053696 | tf_op jit(solution)/shard_map/mul | solution.py:817
  41.0 2.8 %collective-permute-start.8 = (bf16[1536,768]{1,0:T(8,128)(2,1)}, bf16[1536,768]{1,0:T(8,128)(2,1)}, u32[]{:S(2)}, u32[]{:S(2)}) collective-permute-start(bf16[1536,768]{1,0:T(8,128)(2,1)} %pad_maximum_fusion), channel_id=1, source_target_pairs={{1,16},{3,18},{5,20},{7,22},{9,24},{11,26},{13,28},{15,30},{16,1},... | collective-permute-start | bytes 7077896 | tf_op jit(solution)/shard_map/ppermute | solution.py:702
  43.8 0.9 fusion.2.member_ref
  44.7 1.8 maximum_select_fusion.rows_ref.refs_2_
  46.5 1.2 collective-permute-done.4.w_far
  47.7 0.9 copy-done.11
  48.6 9.0 %shard_map.221 = (bf16[3,1024,384]{2,1,0:T(8,128)(2,1)}, bf16[768,1024]{1,0:T(8,128)(2,1)}) custom-call(s32[4]{0:T(128)} %pad_add_fusion.flags.refs_0_, bf16[1024,768]{1,0:T(8,128)(2,1)} %maximum_select_fusion.rows_ref.refs_2_, f32[1024,128]{1,0:T(8,128)} %get-tuple-element.104.cos_ref, f32[1024,128]{1,0:T(8,128)} %get-tuple-element.105.sin_ref, ...), custom_call_target="tpu_custom_call" | custom-call | bytes 24000000 | tf_op jit(solution)/shard_map/pallas_call | solution.py:240
  57.6 13.0 %shard_map.222 = (bf16[1024,384]{1,0:T(8,128)(2,1)}, f32[3,8,1024]{2,1,0:T(8,128)}) custom-call(bf16[1024,128]{1,0:T(8,128)(2,1)} %select_convert_fusion.apart_ref, bf16[1024,128]{1,0:T(8,128)(2,1)} %fusion.2.member_ref, bf16[3,1024,384]{2,1,0:T(8,128)(2,1)} %get-tuple-element.108.q_ref.k_ref.v_ref, ...), custom_call_target="tpu_custom_call" | custom-call | bytes 36000000 | tf_op jit(solution)/shard_map/pallas_call | solution.py:104
  70.7 1.7 broadcast_select_fusion.w_ref
  72.5 1.0 convolution_convert_fusion.refs_3_.own_ref
  73.5 3.6 %collective-permute-start.9 = (bf16[768,768]{1,0:T(8,128)(2,1)}, bf16[768,768]{1,0:T(8,128)(2,1)}, u32[]{:S(2)}, u32[]{:S(2)}) collective-permute-start(bf16[768,768]{1,0:T(8,128)(2,1)} %get-tuple-element.118), channel_id=1, source_target_pairs={{1,16},{3,18},{5,20},{7,22},{9,24},{11,26},{13,28},{15,30},{16,1},... | collective-permute-start | bytes 3538952 | tf_op jit(solution)/shard_map/ppermute | solution.py:702
  77.2 2.1 collective-permute-start.10
  79.5 2.3 collective-permute-done.7.refs_6_
  82.6 1.1 copy-done.5
  83.8 18.9 %shard_map.223 = (bf16[1024,768]{1,0:T(8,128)(2,1)}, bf16[768,1024]{1,0:T(8,128)(2,1)}, bf16[1024,768]{1,0:T(8,128)(2,1)}, bf16[768,1024]{1,0:T(8,128)(2,1)}, bf...) custom-call(s32[4]{0:T(128)} %pad_add_fusion.flags.refs_0_, ...), custom_call_target="tpu_custom_call" | custom-call | bytes 51000000 | tf_op jit(solution)/shard_map/pallas_call | solution.py:240
  102.7 1.3 collective-permute-done.10.refs_9_
  104.1 16.3 %shard_map.224 = (bf16[1024,768]{1,0:T(8,128)(2,1)}, bf16[1024,768]{1,0:T(8,128)(2,1)}, bf16[768,768]{1,0:T(8,128)(2,1)}, bf16[768,384]{1,0:T(8,128)(2,1)}, bf16...) custom-call(s32[4]{0:T(128)} %pad_add_fusion.flags.refs_0_, ...), custom_call_target="tpu_custom_call" | custom-call | bytes 51000000 | tf_op jit(solution)/shard_map/pallas_call | solution.py:240
  120.5 1.8 collective-permute-start.13
  122.3 1.2 collective-permute-start.14
  123.6 3.6 %collective-permute-start.12 = (bf16[768,384]{1,0:T(8,128)(2,1)}, bf16[768,384]{1,0:T(8,128)(2,1)S(1)}, u32[]{:S(2)}, u32[]{:S(2)}) collective-permute-start(bf16[768,384]{1,0:T(8,128)(2,1)} %get-tuple-element.123), channel_id=1, source_target_pairs={{1,16},{3,18},{5,20},{7,22},{9,24},{11,26},{13,28},{15,30},{16,1},... | collective-permute-start | bytes 1769480 | tf_op jit(solution)/shard_map/ppermute | solution.py:706
  127.1 1.2 copy-done.29
  128.3 10.0 %shard_map.225 = (bf16[1024,768]{1,0:T(8,128)(2,1)}, bf16[1024,384]{1,0:T(8,128)(2,1)}, bf16[768,384]{1,0:T(8,128)(2,1)}, f32[8,768]{1,0:T(8,128)}) custom-call(s32[4]{0:T(128)} %pad_add_fusion.flags.refs_0_, bf16[1024,768]{1,0:T(8,128)(2,1)} %maximum_select_fusion.rows_ref.refs_2_, bf16[1024,768]{1,0:T(8,128)(2,1)} %copy-done.3, ...), custom_call_target="tpu_custom_call" | custom-call | bytes 24000000 | tf_op jit(solution)/shard_map/pallas_call | solution.py:240
  138.3 19.6 %shard_map.226.grad_ref = bf16[3,1024,384]{2,1,0:T(8,128)(2,1)} custom-call(bf16[1024,128]{1,0:T(8,128)(2,1)} %select_convert_fusion.apart_ref, bf16[1024,128]{1,0:T(8,128)(2,1)} %fusion.2.member_ref, f32[1024,128]{1,0:T(8,128)} %get-tuple-element.104.cos_ref, f32[1024,128]{1,0:T(8,128)} %get-tuple-element.105.sin_ref, ...), custom_call_target="tpu_custom_call" | custom-call | bytes 66000000 | tf_op jit(solution)/shard_map/pallas_call | solution.py:189
  158.2 7.7 %shard_map.227 = (bf16[768,384]{1,0:T(8,128)(2,1)}, bf16[768,384]{1,0:T(8,128)(2,1)}, bf16[768,384]{1,0:T(8,128)(2,1)}, bf16[768,384]{1,0:T(8,128)(2,1)}) custom-call(s32[4]{0:T(128)} %pad_add_fusion.flags.refs_0_, bf16[768,1024]{1,0:T(8,128)(2,1)} %get-tuple-element.128.turned_ref, bf16[768,384]{1,0:T(8,128)(2,1)} %get-tuple-element.129.out_grad_ref, ...), custom_call_target="tpu_custom_call" | custom-call | bytes 12000000 | tf_op jit(solution)/shard_map/pallas_call | solution.py:240
  165.9 3.1 %collective-permute-start.16 = (bf16[768,384]{1,0:T(8,128)(2,1)}, bf16[768,384]{1,0:T(8,128)(2,1)}, u32[]{:S(2)}, u32[]{:S(2)}) collective-permute-start(bf16[768,384]{1,0:T(8,128)(2,1)} %get-tuple-element.130), channel_id=1, source_target_pairs={{1,16},{3,18},{5,20},{7,22},{9,24},{11,26},{13,28},{15,30},{16,1},... | collective-permute-start | bytes 1769480 | tf_op jit(solution)/shard_map/ppermute | solution.py:706
  169.0 1.6 collective-permute-start.18
  170.9 3.0 %add_convert_fusion = bf16[768,384]{1,0:T(8,128)(2,1)} fusion(bf16[768,384]{1,0:T(8,128)(2,1)} %copy-done.36, bf16[768,384]{1,0:T(8,128)(2,1)} %copy-done.35, bf16[768,384]{1,0:T(8,128)(2,1)} %copy-done.34, bf16[768,384]{1,0:T(8,128)(2,1)} %get-tuple-element.123, bf16[768,384]{1,0:T(8,128)(2,1)} %copy-done.37, pred[]{:T(512)S(6)} %eq.35), kind=kLoop, calls=%fused_computation.5 | loop fusion | flops 2654208 | bytes 3538945 | tf_op jit(solution)/shard_map/convert_element_type | solution.py:744
  174.7 1.7 copy-done.1
  176.4 1.2 copy-done.10
  177.6 1.2 copy-done.12
  178.8 6.2 %shard_map.228 = (f32[512,768]{1,0:T(8,128)S(1)}, bf16[256,768]{1,0:T(8,128)(2,1)}, bf16[256,768]{1,0:T(8,128)(2,1)}, f32[8,768]{1,0:T(8,128)S(1)}) custom-call(s32[4]{0:T(128)S(1)} %copy-done.20, bf16[3,1024,384]{2,1,0:T(8,128)(2,1)S(1)} %copy-done.1, bf16[1024,768]{1,0:T(8,128)(2,1)S(1)} %copy-done, bf16[3,768,384]{2,1,0:T(8,128)(2,1)S(1)} %copy-done.7, ...), custom_call_target="tpu_custom_call" | custom-call | bytes 15000000 | tf_op jit(solution)/shard_map/pallas_call | solution.py:240
  185.0 1.2 copy-done.14
  186.2 1.4 copy-done.17
  187.6 1.3 copy-done.19
  188.9 6.9 %shard_map.229 = (f32[512,768]{1,0:T(8,128)S(1)}, bf16[256,768]{1,0:T(8,128)(2,1)S(1)}, bf16[256,768]{1,0:T(8,128)(2,1)S(1)}, f32[8,768]{1,0:T(8,128)S(1)}) custom-call(s32[4]{0:T(128)S(1)} %copy-done.20, bf16[1024,768]{1,0:T(8,128)(2,1)S(1)} %copy-done.16, bf16[1024,768]{1,0:T(8,128)(2,1)S(1)} %copy-done.17, bf16[1024,768]{1,0:T(8,128)(2,1)S(1)} %copy-done, ...), custom_call_target="tpu_custom_call" | custom-call | bytes 18000000 | tf_op jit(solution)/shard_map/pallas_call | solution.py:240
  195.8 2.1 collective-permute-done.19
  198.9 2.0 add_convert_fusion.1
  201.5 1.8 collective-permute-start.29
  203.3 2.2 collective-permute-start.28
  205.6 4.4 %collective-permute-start.27 = (bf16[192,384]{1,0:T(8,128)(2,1)}, bf16[192,384]{1,0:T(8,128)(2,1)S(1)}, u32[]{:S(2)}, u32[]{:S(2)}) collective-permute-start(bf16[192,384]{1,0:T(8,128)(2,1)} %reduce-scatter.8.cloned.1.call-done), channel_id=1, source_target_pairs={{1,16},{3,18},{5,20},{7,22},{9,24},{11,26},{13,28},{15,30},{16,1},... | collective-permute-start | bytes 442376 | tf_op jit(solution)/shard_map/ppermute | solution.py:702
  210.8 5.4 %shard_map.230.own_ref = bf16[2,512,768]{2,1,0:T(8,128)(2,1)} custom-call(s32[4]{0:T(128)} %pad_add_fusion.flags.refs_0_, bf16[1024,768]{1,0:T(8,128)(2,1)} %maximum_select_fusion.rows_ref.refs_2_, bf16[1024,768]{1,0:T(8,128)(2,1)} %get-tuple-element.142.resid_ref, f32[512,768]{1,0:T(8,128)} %copy-done.14, f32[512,768]{1,0:T(8,128)} %copy-done.15, ...), custom_call_target="tpu_custom_call" | custom-call | bytes 9000000 | tf_op jit(solution)/shard_map/pallas_call | solution.py:240
  216.2 1.2 collective-permute-done.24
  217.5 2.9 %collective-permute-done.25 = f32[9,768]{1,0:T(8,128)S(1)} collective-permute-done((f32[9,768]{1,0:T(8,128)S(1)}, f32[9,768]{1,0:T(8,128)S(1)}, u32[]{:S(2)}, u32[]{:S(2)}) %collective-permute-start.25) | collective-permute-done | bytes 27680 | tf_op jit(solution)/shard_map/ppermute | solution.py:772
  221.1 2.3 collective-permute-done.26
  223.7 1.0 fusion.9
  225.4 4.5 %collective-permute-start.31 = (bf16[2,512,768]{2,1,0:T(8,128)(2,1)S(1)}, bf16[2,512,768]{2,1,0:T(8,128)(2,1)S(1)}, u32[]{:S(2)}, u32[]{:S(2)}) collective-permute-start(bf16[2,512,768]{2,1,0:T(8,128)(2,1)S(1)} %copy-done.8), channel_id=1, source_target_pairs={{1,16},{3,18},{5,20},{7,22},{9,24},{11,26},{13,28},{15,30},{16,1},... | collective-permute-start | bytes 4718600 | tf_op jit(solution)/shard_map/ppermute | solution.py:702
  229.8 4.2 %collective-permute-done.34 = bf16[192,1152]{1,0:T(8,128)(2,1)S(1)} collective-permute-done((bf16[192,1152]{1,0:T(8,128)(2,1)S(1)}, bf16[192,1152]{1,0:T(8,128)(2,1)S(1)}, u32[]{:S(2)}, u32[]{:S(2)}) %collective-permute-start.34) | collective-permute-done | bytes 442400 | tf_op jit(solution)/shard_map/ppermute | solution.py:721
  234.1 3.4 %collective-permute-start.35 = (bf16[2,192,1152]{2,1,0:T(8,128)(2,1)S(1)}, bf16[2,192,1152]{2,1,0:T(8,128)(2,1)S(1)}, u32[]{:S(2)}, u32[]{:S(2)}) collective-permute-start(bf16[2,192,1152]{2,1,0:T(8,128)(2,1)S(1)} %pad_maximum_fusion.2.here_ref), channel_id=1, source_target_pairs={{0,1},{1,0},{2,3},{3,2},{4,5},{5,4},{6,7},{7,6},{8,9},{9,8},{10,11... | collective-permute-start | bytes 2654216 | tf_op jit(solution)/shard_map/ppermute | solution.py:725
  237.5 3.0 %collective-permute-done.32 = f32[9,768]{1,0:T(8,128)S(1)} collective-permute-done((f32[9,768]{1,0:T(8,128)S(1)}, f32[9,768]{1,0:T(8,128)S(1)}, u32[]{:S(2)}, u32[]{:S(2)}) %collective-permute-start.32) | collective-permute-done | bytes 27680 | tf_op jit(solution)/shard_map/ppermute | solution.py:772
  241.8 2.6 collective-permute-done.33
  244.4 1.3 slice_reduce_fusion
  246.3 2.5 shard_map.232
  248.8 2.1 shard_map.231
  (175 shorter events, 11.2 us)
Async XLA Ops:
  7.2 8.7 %copy-start.44 = (f32[768]{0:T(1024)S(1)}, f32[768]{0:T(1024)}, u32[]{:S(2)}) copy-start(f32[768]{0:T(1024)} %param.18) | copy-start | bytes 9220
  7.2 8.8 %copy-start.45 = (f32[768]{0:T(1024)S(1)}, f32[768]{0:T(1024)}, u32[]{:S(2)}) copy-start(f32[768]{0:T(1024)} %param.19) | copy-start | bytes 9220
  7.2 8.8 %copy-start.46 = (f32[768]{0:T(1024)S(1)}, f32[768]{0:T(1024)}, u32[]{:S(2)}) copy-start(f32[768]{0:T(1024)} %param.22) | copy-start | bytes 9220
  7.2 8.8 %copy-start.47 = (f32[768]{0:T(1024)S(1)}, f32[768]{0:T(1024)}, u32[]{:S(2)}) copy-start(f32[768]{0:T(1024)} %param.23) | copy-start | bytes 9220
  7.2 150.9 %reduce-scatter.10.cloned.1.call-start = ((), (), s32[]{:S(2)}) async-start(), calls=%async_computation.5 | async-start | bytes 2949120
  7.3 21.8 %collective-permute-start.2 = (s32[1,3]{1,0:T(1,128)}, s32[1,3]{1,0:T(1,128)S(1)}, u32[]{:S(2)}, u32[]{:S(2)}) collective-permute-start(s32[1,3]{1,0:T(1,128)} %param.16), channel_id=1, source_target_pairs={{0,1},{1,0},{2,3},{3,2},{4,5},{5,4},{6,7},{7,6},{8,9},{9,8},{10,11... | collective-permute-start | bytes 44 | tf_op jit(solution)/shard_map/ppermute | solution.py:725
  8.0 21.5 %collective-permute-start = (bf16[512,768]{1,0:T(8,128)(2,1)}, bf16[512,768]{1,0:T(8,128)(2,1)}, u32[]{:S(2)}, u32[]{:S(2)}) collective-permute-start(bf16[512,768]{1,0:T(8,128)(2,1)} %bitcast.45), channel_id=1, source_target_pairs={{1,16},{3,18},{5,20},{7,22},{9,24},{11,26},{13,28},{15,30},{16,1},... | collective-permute-start | bytes 2359304 | tf_op jit(solution)/shard_map/ppermute | solution.py:702
  13.2 20.6 %collective-permute-start.3 = (bf16[3,384,384]{2,1,0:T(8,128)(2,1)}, bf16[3,384,384]{2,1,0:T(8,128)(2,1)S(1)}, u32[]{:S(2)}, u32[]{:S(2)}) collective-permute-start(bf16[3,384,384]{2,1,0:T(8,128)(2,1)} %constant_dynamic-slice_fusion), channel_id=1, source_target_pairs={{1,16},{3,18},{5,20},{7,22},{9,24},{11,26},{13,28},{15,30},{16,1},... | collective-permute-start | bytes 2654216 | tf_op jit(solution)/shard_map/ppermute | solution.py:702
  23.4 9.1 %copy-start.31 = (bf16[1,512,768]{2,1,0:T(8,128)(2,1)S(1)}, bf16[1,512,768]{2,1,0:T(8,128)(2,1)}, u32[]{:S(2)}) copy-start(bf16[1,512,768]{2,1,0:T(8,128)(2,1)} %param.13) | copy-start | bytes 2359300
  29.5 41.2 %collective-permute-start.5 = (bf16[896,768]{1,0:T(8,128)(2,1)S(1)}, bf16[896,768]{1,0:T(8,128)(2,1)}, u32[]{:S(2)}, u32[]{:S(2)}) collective-permute-start(bf16[896,768]{1,0:T(8,128)(2,1)S(1)} %copy-done.30), channel_id=1, source_target_pairs={{1,16},{3,18},{5,20},{7,22},{9,24},{11,26},{13,28},{15,30},{16,1},... | collective-permute-start | bytes 4128776 | tf_op jit(solution)/shard_map/ppermute | solution.py:702
  33.8 10.9 %collective-permute-start.1 = (bf16[512,768]{1,0:T(8,128)(2,1)S(1)}, bf16[512,768]{1,0:T(8,128)(2,1)S(1)}, u32[]{:S(2)}, u32[]{:S(2)}) collective-permute-start(bf16[512,768]{1,0:T(8,128)(2,1)S(1)} %broadcast_select_fusion.1), channel_id=1, source_target_pairs={{0,1},{1,0},{2,3},{3,2},{4,5},{5,4},{6,7},{7,6},{8,9},{9,8},{10,11... | collective-permute-start | bytes 2359304 | tf_op jit(solution)/shard_map/ppermute | solution.py:725
  33.9 12.6 %copy-start.9 = (bf16[3,384,384]{2,1,0:T(8,128)(2,1)}, bf16[3,384,384]{2,1,0:T(8,128)(2,1)S(1)}, u32[]{:S(2)}) copy-start(bf16[3,384,384]{2,1,0:T(8,128)(2,1)S(1)} %collective-permute-done.3.w_near) | copy-start | bytes 2654212
  33.9 13.8 %collective-permute-start.4 = (bf16[3,384,384]{2,1,0:T(8,128)(2,1)S(1)}, bf16[3,384,384]{2,1,0:T(8,128)(2,1)S(1)}, u32[]{:S(2)}, u32[]{:S(2)}) collective-permute-start(bf16[3,384,384]{2,1,0:T(8,128)(2,1)S(1)} %collective-permute-done.3.w_near), channel_id=1, source_target_pairs={{1,3},{3,1},{5,7},{7,5},{9,11},{11,9},{13,15},{15,13},{16,18},{18,... | collective-permute-start | bytes 2654216 | tf_op jit(solution)/shard_map/ppermute | solution.py:717
  41.0 41.6 %collective-permute-start.8 = (bf16[1536,768]{1,0:T(8,128)(2,1)}, bf16[1536,768]{1,0:T(8,128)(2,1)}, u32[]{:S(2)}, u32[]{:S(2)}) collective-permute-start(bf16[1536,768]{1,0:T(8,128)(2,1)} %pad_maximum_fusion), channel_id=1, source_target_pairs={{1,16},{3,18},{5,20},{7,22},{9,24},{11,26},{13,28},{15,30},{16,1},... | collective-permute-start | bytes 7077896 | tf_op jit(solution)/shard_map/ppermute | solution.py:702
  57.6 13.1 %copy-start.25 = (bf16[1,512,768]{2,1,0:T(8,128)(2,1)S(1)}, bf16[1,512,768]{2,1,0:T(8,128)(2,1)}, u32[]{:S(2)}) copy-start(bf16[1,512,768]{2,1,0:T(8,128)(2,1)} %param.15) | copy-start | bytes 2359300
  57.6 13.1 %copy-start.28 = (bf16[384,768]{1,0:T(8,128)(2,1)S(1)}, bf16[384,768]{1,0:T(8,128)(2,1)}, u32[]{:S(2)}) copy-start(bf16[384,768]{1,0:T(8,128)(2,1)} %param.21) | copy-start | bytes 1769476
  73.4 9.2 %copy-start.3 = (bf16[1024,768]{1,0:T(8,128)(2,1)}, bf16[1024,768]{1,0:T(8,128)(2,1)S(1)}, u32[]{:S(2)}) copy-start(bf16[1024,768]{1,0:T(8,128)(2,1)S(1)} %convolution_convert_fusion.refs_3_.own_ref) | copy-start | bytes 4718596
  73.4 9.2 %collective-permute-start.6 = (bf16[1024,768]{1,0:T(8,128)(2,1)S(1)}, bf16[1024,768]{1,0:T(8,128)(2,1)S(1)}, u32[]{:S(2)}, u32[]{:S(2)}) collective-permute-start(bf16[1024,768]{1,0:T(8,128)(2,1)S(1)} %convolution_convert_fusion.refs_3_.own_ref), channel_id=1, source_target_pairs={{0,1},{1,0},{2,3},{3,2},{4,5},{5,4},{6,7},{7,6},{8,9},{9,8},{10,11... | collective-permute-start | bytes 4718600 | tf_op jit(solution)/shard_map/ppermute | solution.py:725
  73.5 29.2 %collective-permute-start.9 = (bf16[768,768]{1,0:T(8,128)(2,1)}, bf16[768,768]{1,0:T(8,128)(2,1)}, u32[]{:S(2)}, u32[]{:S(2)}) collective-permute-start(bf16[768,768]{1,0:T(8,128)(2,1)} %get-tuple-element.118), channel_id=1, source_target_pairs={{1,16},{3,18},{5,20},{7,22},{9,24},{11,26},{13,28},{15,30},{16,1},... | collective-permute-start | bytes 3538952 | tf_op jit(solution)/shard_map/ppermute | solution.py:702
  77.2 26.8 %collective-permute-start.10 = (bf16[768,768]{1,0:T(8,128)(2,1)}, bf16[768,768]{1,0:T(8,128)(2,1)}, u32[]{:S(2)}, u32[]{:S(2)}) collective-permute-start(bf16[768,768]{1,0:T(8,128)(2,1)} %get-tuple-element.119), channel_id=1, source_target_pairs={{1,16},{3,18},{5,20},{7,22},{9,24},{11,26},{13,28},{15,30},{16,1},... | collective-permute-start | bytes 3538952 | tf_op jit(solution)/shard_map/ppermute | solution.py:702
  79.4 2.4 collective-permute-start.7
  104.0 97.5 %reduce-scatter.8.cloned.1.call-start = ((), (), s32[]{:S(2)}) async-start(), calls=%async_computation.4 | async-start | bytes 737280 | tf_op jit(solution)/shard_map/reduce_scatter | solution.py:752
  120.4 6.7 %collective-permute-start.11 = (bf16[1024,768]{1,0:T(8,128)(2,1)}, bf16[1024,768]{1,0:T(8,128)(2,1)S(1)}, u32[]{:S(2)}, u32[]{:S(2)}) collective-permute-start(bf16[1024,768]{1,0:T(8,128)(2,1)} %get-tuple-element.120.back_own), channel_id=1, source_target_pairs={{0,1},{1,0},{2,3},{3,2},{4,5},{5,4},{6,7},{7,6},{8,9},{9,8},{10,11... | collective-permute-start | bytes 4718600 | tf_op jit(solution)/shard_map/ppermute | solution.py:725
  120.5 37.5 %collective-permute-start.13 = (bf16[768,384]{1,0:T(8,128)(2,1)}, bf16[768,384]{1,0:T(8,128)(2,1)S(1)}, u32[]{:S(2)}, u32[]{:S(2)}) collective-permute-start(bf16[768,384]{1,0:T(8,128)(2,1)} %get-tuple-element.124), channel_id=1, source_target_pairs={{0,1},{1,17},{2,3},{3,19},{4,5},{5,21},{6,7},{7,23},{8,9},{9,25},{... | collective-permute-start | bytes 1769480 | tf_op jit(solution)/shard_map/ppermute | solution.py:706
  122.3 35.7 %collective-permute-start.14 = (bf16[768,384]{1,0:T(8,128)(2,1)}, bf16[768,384]{1,0:T(8,128)(2,1)S(1)}, u32[]{:S(2)}, u32[]{:S(2)}) collective-permute-start(bf16[768,384]{1,0:T(8,128)(2,1)} %get-tuple-element.125), channel_id=1, source_target_pairs={{0,2},{1,18},{2,0},{3,16},{4,6},{5,22},{6,4},{7,20},{8,10},{9,26},... | collective-permute-start | bytes 1769480 | tf_op jit(solution)/shard_map/ppermute | solution.py:706
  123.6 34.5 %collective-permute-start.15 = (bf16[768,384]{1,0:T(8,128)(2,1)}, bf16[768,384]{1,0:T(8,128)(2,1)S(1)}, u32[]{:S(2)}, u32[]{:S(2)}) collective-permute-start(bf16[768,384]{1,0:T(8,128)(2,1)} %get-tuple-element.126), channel_id=1, source_target_pairs={{0,3},{1,19},{2,1},{3,17},{4,7},{5,23},{6,5},{7,21},{8,11},{9,27},... | collective-permute-start | bytes 1769480 | tf_op jit(solution)/shard_map/ppermute | solution.py:706
  123.6 34.5 %collective-permute-start.12 = (bf16[768,384]{1,0:T(8,128)(2,1)}, bf16[768,384]{1,0:T(8,128)(2,1)S(1)}, u32[]{:S(2)}, u32[]{:S(2)}) collective-permute-start(bf16[768,384]{1,0:T(8,128)(2,1)} %get-tuple-element.123), channel_id=1, source_target_pairs={{1,16},{3,18},{5,20},{7,22},{9,24},{11,26},{13,28},{15,30},{16,1},... | collective-permute-start | bytes 1769480 | tf_op jit(solution)/shard_map/ppermute | solution.py:706
  158.0 7.8 %copy-start.34 = (bf16[768,384]{1,0:T(8,128)(2,1)}, bf16[768,384]{1,0:T(8,128)(2,1)S(1)}, u32[]{:S(2)}) copy-start(bf16[768,384]{1,0:T(8,128)(2,1)S(1)} %collective-permute-done.13) | copy-start | bytes 1769476
  158.0 7.8 %copy-start.35 = (bf16[768,384]{1,0:T(8,128)(2,1)}, bf16[768,384]{1,0:T(8,128)(2,1)S(1)}, u32[]{:S(2)}) copy-start(bf16[768,384]{1,0:T(8,128)(2,1)S(1)} %collective-permute-done.14) | copy-start | bytes 1769476
  158.1 7.8 %copy-start.36 = (bf16[768,384]{1,0:T(8,128)(2,1)}, bf16[768,384]{1,0:T(8,128)(2,1)S(1)}, u32[]{:S(2)}) copy-start(bf16[768,384]{1,0:T(8,128)(2,1)S(1)} %collective-permute-done.15) | copy-start | bytes 1769476
  158.1 7.8 %copy-start.37 = (bf16[768,384]{1,0:T(8,128)(2,1)}, bf16[768,384]{1,0:T(8,128)(2,1)S(1)}, u32[]{:S(2)}) copy-start(bf16[768,384]{1,0:T(8,128)(2,1)S(1)} %collective-permute-done.12) | copy-start | bytes 1769476
  158.1 65.4 %reduce-scatter.6.cloned.1.call-start = ((), (), s32[]{:S(2)}) async-start(), calls=%async_computation.3 | async-start | bytes 737280 | tf_op jit(solution)/shard_map/reduce_scatter | solution.py:752
  165.9 32.0 %collective-permute-start.16 = (bf16[768,384]{1,0:T(8,128)(2,1)}, bf16[768,384]{1,0:T(8,128)(2,1)}, u32[]{:S(2)}, u32[]{:S(2)}) collective-permute-start(bf16[768,384]{1,0:T(8,128)(2,1)} %get-tuple-element.130), channel_id=1, source_target_pairs={{1,16},{3,18},{5,20},{7,22},{9,24},{11,26},{13,28},{15,30},{16,1},... | collective-permute-start | bytes 1769480 | tf_op jit(solution)/shard_map/ppermute | solution.py:706
  168.9 26.8 %collective-permute-start.17 = (bf16[768,384]{1,0:T(8,128)(2,1)}, bf16[768,384]{1,0:T(8,128)(2,1)}, u32[]{:S(2)}, u32[]{:S(2)}) collective-permute-start(bf16[768,384]{1,0:T(8,128)(2,1)} %get-tuple-element.148), channel_id=1, source_target_pairs={{0,1},{1,17},{2,3},{3,19},{4,5},{5,21},{6,7},{7,23},{8,9},{9,25},{... | collective-permute-start | bytes 1769480 | tf_op jit(solution)/shard_map/ppermute | solution.py:706
  169.0 26.8 %collective-permute-start.18 = (bf16[768,384]{1,0:T(8,128)(2,1)}, bf16[768,384]{1,0:T(8,128)(2,1)}, u32[]{:S(2)}, u32[]{:S(2)}) collective-permute-start(bf16[768,384]{1,0:T(8,128)(2,1)} %get-tuple-element.149), channel_id=1, source_target_pairs={{0,2},{1,18},{2,0},{3,16},{4,6},{5,22},{6,4},{7,20},{8,10},{9,26},... | collective-permute-start | bytes 1769480 | tf_op jit(solution)/shard_map/ppermute | solution.py:706
  170.6 27.3 %collective-permute-start.19 = (bf16[768,384]{1,0:T(8,128)(2,1)}, bf16[768,384]{1,0:T(8,128)(2,1)}, u32[]{:S(2)}, u32[]{:S(2)}) collective-permute-start(bf16[768,384]{1,0:T(8,128)(2,1)} %get-tuple-element.150), channel_id=1, source_target_pairs={{0,3},{1,19},{2,1},{3,17},{4,7},{5,23},{6,5},{7,21},{8,11},{9,27},... | collective-permute-start | bytes 1769480 | tf_op jit(solution)/shard_map/ppermute | solution.py:706
  178.7 7.4 %copy-start.2 = (bf16[1024,768]{1,0:T(8,128)(2,1)S(1)}, bf16[1024,768]{1,0:T(8,128)(2,1)}, u32[]{:S(2)}) copy-start(bf16[1024,768]{1,0:T(8,128)(2,1)} %get-tuple-element.137.refs_3_.cot_ref) | copy-start | bytes 4718596
  178.7 7.4 %copy-start.4 = (bf16[1024,768]{1,0:T(8,128)(2,1)S(1)}, bf16[1024,768]{1,0:T(8,128)(2,1)}, u32[]{:S(2)}) copy-start(bf16[1024,768]{1,0:T(8,128)(2,1)} %copy-done.3) | copy-start | bytes 4718596
  178.7 7.4 %copy-start.6 = (bf16[1024,768]{1,0:T(8,128)(2,1)S(1)}, bf16[1024,768]{1,0:T(8,128)(2,1)}, u32[]{:S(2)}) copy-start(bf16[1024,768]{1,0:T(8,128)(2,1)} %copy-done.5) | copy-start | bytes 4718596
  178.8 7.4 %copy-start.16 = (bf16[1024,768]{1,0:T(8,128)(2,1)S(1)}, bf16[1024,768]{1,0:T(8,128)(2,1)}, u32[]{:S(2)}) copy-start(bf16[1024,768]{1,0:T(8,128)(2,1)} %get-tuple-element.134.act_early) | copy-start | bytes 4718596
  178.8 7.4 %copy-start.18 = (bf16[768,768]{1,0:T(8,128)(2,1)S(1)}, bf16[768,768]{1,0:T(8,128)(2,1)}, u32[]{:S(2)}) copy-start(bf16[768,768]{1,0:T(8,128)(2,1)} %get-tuple-element.138.early_ref) | copy-start | bytes 3538948
  188.9 10.1 %copy-start.33 = (bf16[768,384]{1,0:T(8,128)(2,1)S(1)}, bf16[768,384]{1,0:T(8,128)(2,1)}, u32[]{:S(2)}) copy-start(bf16[768,384]{1,0:T(8,128)(2,1)} %get-tuple-element.130) | copy-start | bytes 1769476
  197.9 3.6 %collective-permute-start.20 = (bf16[256,768]{1,0:T(8,128)(2,1)}, bf16[256,768]{1,0:T(8,128)(2,1)S(1)}, u32[]{:S(2)}, u32[]{:S(2)}) collective-permute-start(bf16[256,768]{1,0:T(8,128)(2,1)} %get-tuple-element.158), channel_id=1, source_target_pairs={{0,1},{1,0},{2,3},{3,2},{4,5},{5,4},{6,7},{7,6},{8,9},{9,8},{10,11... | collective-permute-start | bytes 1179656 | tf_op jit(solution)/shard_map/ppermute | solution.py:725
  198.1 5.3 %collective-permute-start.21 = (bf16[256,768]{1,0:T(8,128)(2,1)}, bf16[256,768]{1,0:T(8,128)(2,1)S(1)}, u32[]{:S(2)}, u32[]{:S(2)}) collective-permute-start(bf16[256,768]{1,0:T(8,128)(2,1)} %get-tuple-element.159), channel_id=1, source_target_pairs={{0,1},{1,0},{2,3},{3,2},{4,5},{5,4},{6,7},{7,6},{8,9},{9,8},{10,11... | collective-permute-start | bytes 1179656 | tf_op jit(solution)/shard_map/ppermute | solution.py:725
  198.4 7.2 %collective-permute-start.22 = (bf16[256,768]{1,0:T(8,128)(2,1)S(1)}, bf16[256,768]{1,0:T(8,128)(2,1)S(1)}, u32[]{:S(2)}, u32[]{:S(2)}) collective-permute-start(bf16[256,768]{1,0:T(8,128)(2,1)S(1)} %get-tuple-element.160), channel_id=1, source_target_pairs={{0,1},{1,0},{2,3},{3,2},{4,5},{5,4},{6,7},{7,6},{8,9},{9,8},{10,11... | collective-permute-start | bytes 1179656 | tf_op jit(solution)/shard_map/ppermute | solution.py:725
  198.6 11.4 %collective-permute-start.23 = (bf16[256,768]{1,0:T(8,128)(2,1)S(1)}, bf16[256,768]{1,0:T(8,128)(2,1)S(1)}, u32[]{:S(2)}, u32[]{:S(2)}) collective-permute-start(bf16[256,768]{1,0:T(8,128)(2,1)S(1)} %get-tuple-element.161), channel_id=1, source_target_pairs={{0,1},{1,0},{2,3},{3,2},{4,5},{5,4},{6,7},{7,6},{8,9},{9,8},{10,11... | collective-permute-start | bytes 1179656 | tf_op jit(solution)/shard_map/ppermute | solution.py:725
  201.0 22.5 %collective-permute-start.30 = (bf16[192,384]{1,0:T(8,128)(2,1)S(1)}, bf16[192,384]{1,0:T(8,128)(2,1)S(1)}, u32[]{:S(2)}, u32[]{:S(2)}) collective-permute-start(bf16[192,384]{1,0:T(8,128)(2,1)S(1)} %get-tuple-element.232), channel_id=1, source_target_pairs={{0,12},{4,0},{8,4},{12,8},{1,13},{5,1},{9,5},{13,9},{2,14},{6,2},{... | collective-permute-start | bytes 442376 | tf_op jit(solution)/shard_map/ppermute | solution.py:764
  201.5 8.5 %copy-start.38 = (bf16[256,768]{1,0:T(8,128)(2,1)}, bf16[256,768]{1,0:T(8,128)(2,1)S(1)}, u32[]{:S(2)}) copy-start(bf16[256,768]{1,0:T(8,128)(2,1)S(1)} %collective-permute-done.20.got_first) | copy-start | bytes 1179652
  201.5 22.0 %collective-permute-start.29 = (bf16[192,384]{1,0:T(8,128)(2,1)S(1)}, bf16[192,384]{1,0:T(8,128)(2,1)S(1)}, u32[]{:S(2)}, u32[]{:S(2)}) collective-permute-start(bf16[192,384]{1,0:T(8,128)(2,1)S(1)} %get-tuple-element.233), channel_id=1, source_target_pairs={{0,8},{4,12},{8,0},{12,4},{1,9},{5,13},{9,1},{13,5},{2,10},{6,14},... | collective-permute-start | bytes 442376 | tf_op jit(solution)/shard_map/ppermute | solution.py:764
  203.3 20.1 %collective-permute-start.28 = (bf16[192,384]{1,0:T(8,128)(2,1)S(1)}, bf16[192,384]{1,0:T(8,128)(2,1)S(1)}, u32[]{:S(2)}, u32[]{:S(2)}) collective-permute-start(bf16[192,384]{1,0:T(8,128)(2,1)S(1)} %get-tuple-element.234), channel_id=1, source_target_pairs={{0,4},{4,8},{8,12},{12,0},{1,5},{5,9},{9,13},{13,1},{2,6},{6,10},{... | collective-permute-start | bytes 442376 | tf_op jit(solution)/shard_map/ppermute | solution.py:764
  205.6 18.0 %collective-permute-start.27 = (bf16[192,384]{1,0:T(8,128)(2,1)}, bf16[192,384]{1,0:T(8,128)(2,1)S(1)}, u32[]{:S(2)}, u32[]{:S(2)}) collective-permute-start(bf16[192,384]{1,0:T(8,128)(2,1)} %reduce-scatter.8.cloned.1.call-done), channel_id=1, source_target_pairs={{1,16},{3,18},{5,20},{7,22},{9,24},{11,26},{13,28},{15,30},{16,1},... | collective-permute-start | bytes 442376 | tf_op jit(solution)/shard_map/ppermute | solution.py:702
  210.8 12.8 %copy-start.42 = (bf16[192,384]{1,0:T(8,128)(2,1)S(1)}, bf16[192,384]{1,0:T(8,128)(2,1)}, u32[]{:S(2)}) copy-start(bf16[192,384]{1,0:T(8,128)(2,1)} %reduce-scatter.8.cloned.1.call-done) | copy-start | bytes 442372
  216.2 9.2 %copy-start.8 = (bf16[2,512,768]{2,1,0:T(8,128)(2,1)S(1)}, bf16[2,512,768]{2,1,0:T(8,128)(2,1)}, u32[]{:S(2)}) copy-start(bf16[2,512,768]{2,1,0:T(8,128)(2,1)} %shard_map.230.own_ref) | copy-start | bytes 4718596
  216.2 1.2 collective-permute-start.24
  217.4 3.0 %collective-permute-start.25 = (f32[9,768]{1,0:T(8,128)S(1)}, f32[9,768]{1,0:T(8,128)S(1)}, u32[]{:S(2)}, u32[]{:S(2)}) collective-permute-start(f32[9,768]{1,0:T(8,128)S(1)} %add.97), channel_id=1, source_target_pairs={{0,16},{16,0},{1,17},{17,1},{2,18},{18,2},{3,19},{19,3},{4,20},{20... | collective-permute-start | bytes 82952 | tf_op jit(solution)/shard_map/ppermute | solution.py:772
  220.5 3.0 %collective-permute-start.26 = (f32[9,768]{1,0:T(8,128)S(1)}, f32[9,768]{1,0:T(8,128)S(1)}, u32[]{:S(2)}, u32[]{:S(2)}) collective-permute-start(f32[9,768]{1,0:T(8,128)S(1)} %add.98), channel_id=1, source_target_pairs={{0,2},{2,0},{1,3},{3,1},{4,6},{6,4},{5,7},{7,5},{8,10},{10,8},{9,1... | collective-permute-start | bytes 82952 | tf_op jit(solution)/shard_map/ppermute | solution.py:772
  223.7 17.5 %copy-start.22 = (f32[5]{0:T(128)S(1)}, f32[5]{0:T(128)}, u32[]{:S(2)}) copy-start(f32[5]{0:T(128)} %weight_ref.1) | copy-start | bytes 64
  223.7 22.6 %copy-start.21 = (s32[4]{0:T(128)S(1)}, s32[4]{0:T(128)}, u32[]{:S(2)}) copy-start(s32[4]{0:T(128)} %pad_add_fusion.flags.refs_0_) | copy-start | bytes 52
  224.7 9.3 %collective-permute-start.34 = (bf16[192,1152]{1,0:T(8,128)(2,1)S(1)}, bf16[192,1152]{1,0:T(8,128)(2,1)S(1)}, u32[]{:S(2)}, u32[]{:S(2)}) collective-permute-start(bf16[192,1152]{1,0:T(8,128)(2,1)S(1)} %get-tuple-element.237), channel_id=1, source_target_pairs={{0,2},{2,0},{1,3},{3,1},{4,6},{6,4},{5,7},{7,5},{8,10},{10,8},{9,1... | collective-permute-start | bytes 1327112 | tf_op jit(solution)/shard_map/ppermute | solution.py:721
  225.4 23.4 %collective-permute-start.31 = (bf16[2,512,768]{2,1,0:T(8,128)(2,1)S(1)}, bf16[2,512,768]{2,1,0:T(8,128)(2,1)S(1)}, u32[]{:S(2)}, u32[]{:S(2)}) collective-permute-start(bf16[2,512,768]{2,1,0:T(8,128)(2,1)S(1)} %copy-done.8), channel_id=1, source_target_pairs={{1,16},{3,18},{5,20},{7,22},{9,24},{11,26},{13,28},{15,30},{16,1},... | collective-permute-start | bytes 4718600 | tf_op jit(solution)/shard_map/ppermute | solution.py:702
  234.0 14.8 %copy-start.13 = (f32[512,768]{1,0:T(8,128)S(1)}, f32[512,768]{1,0:T(8,128)}, u32[]{:S(2)}) copy-start(f32[512,768]{1,0:T(8,128)} %get-tuple-element.101.part_ref) | copy-start | bytes 4718596
  234.1 12.2 %collective-permute-start.35 = (bf16[2,192,1152]{2,1,0:T(8,128)(2,1)S(1)}, bf16[2,192,1152]{2,1,0:T(8,128)(2,1)S(1)}, u32[]{:S(2)}, u32[]{:S(2)}) collective-permute-start(bf16[2,192,1152]{2,1,0:T(8,128)(2,1)S(1)} %pad_maximum_fusion.2.here_ref), channel_id=1, source_target_pairs={{0,1},{1,0},{2,3},{3,2},{4,5},{5,4},{6,7},{7,6},{8,9},{9,8},{10,11... | collective-permute-start | bytes 2654216 | tf_op jit(solution)/shard_map/ppermute | solution.py:725
  237.5 3.0 %collective-permute-start.32 = (f32[9,768]{1,0:T(8,128)S(1)}, f32[9,768]{1,0:T(8,128)S(1)}, u32[]{:S(2)}, u32[]{:S(2)}) collective-permute-start(f32[9,768]{1,0:T(8,128)S(1)} %add.99), channel_id=1, source_target_pairs={{0,4},{4,0},{8,12},{12,8},{1,5},{5,1},{9,13},{13,9},{2,6},{6,2},{1... | collective-permute-start | bytes 82952 | tf_op jit(solution)/shard_map/ppermute | solution.py:772
  240.4 3.9 %collective-permute-start.33 = (f32[9,768]{1,0:T(8,128)S(1)}, f32[9,768]{1,0:T(8,128)S(1)}, u32[]{:S(2)}, u32[]{:S(2)}) collective-permute-start(f32[9,768]{1,0:T(8,128)S(1)} %add.110), channel_id=1, source_target_pairs={{0,8},{4,12},{8,0},{12,4},{1,9},{5,13},{9,1},{13,5},{2,10},{6,14},... | collective-permute-start | bytes 82952 | tf_op jit(solution)/shard_map/ppermute | solution.py:772
  (24 other events, 73.9 us)
Sparse Core Ops, SparseCore 0:
  104.2 47.4 reduce-scatter.9
  158.2 18.5 reduce-scatter.7
  179.7 20.3 reduce-scatter.5

commit v10 on v9

--- a/solution.py
+++ b/solution.py
@@ -326,10 +326,10 @@
     if early:
         flags, weight_ref, rows_ref, own_ref, got_ref, cot_here, cot_there, vectors, up_own, down_own, got = refs[:11]
         norm, norm_t, grad, grad_t, back_ref, act_ref, down_ref, pieces = refs[11:19]
-        up_got, down_got = got.at[: norm.shape[1]], got.at[norm.shape[1] :]
     else:
-        flags, norm, norm_t, grad, grad_t, back_early, up_own, down_own, up_got, down_got = refs[:10]
-        back_ref, act_ref, down_ref, *pieces = refs[10:17]
+        flags, norm, norm_t, grad, grad_t, back_early, up_own, down_own, got = refs[:9]
+        back_ref, act_ref, down_ref, *pieces = refs[9:16]
+    up_got, down_got = got.at[: norm.shape[1]], got.at[norm.shape[1] :]
     up_w, up_sum, down_sum = refs[-3:]
     part = up_w.shape[1] // 2
     step, last = pl.program_id(0), pl.num_programs(0) - 1
@@ -388,7 +388,7 @@
     row_blocks(norm_t.shape[0], grads)
 
 
-def feed(early, scalars, fields, w_up, w_down, *got):
+def feed(early, scalars, fields, w_up, w_down, got):
     whole, width = fields[0].shape
     hidden = w_up.shape[1] // 2
     rows = whole // 2
@@ -412,7 +412,7 @@
     operands += [
         (w_up, (width, hidden), lambda i, *scalars: (0, half)),
         (w_down, (hidden, width), lambda i, *scalars: (half, 0)),
-        *got,
+        got,
     ]
     outs += [tokens, ((whole, hidden), low, (rows, hidden), lambda i, *scalars: (i, 0)), ((hidden, width), low)]
     sums = ((width, hidden), jnp.float32)
@@ -800,7 +800,7 @@
     qkv_near = swap_diagonal(part_of(w_qkv, far, 1))
     qkv_far = swap_far_away(qkv_near)
     early_got = jnp.concatenate([part_of(w_up, 0, 1), part_of(w_down, 0, 0)], axis=0)
-    late_up, late_down = part_of(w_up, 1, 1), part_of(w_down, 1, 0)
+    late_got = jnp.concatenate([part_of(w_up, 1, 1), part_of(w_down, 1, 0)], axis=0)
     last_own = jnp.concatenate([w_out, cotangent[0]], axis=0)
     vectors = jnp.stack([gain_one, bias_one, gain_two, bias_two])
 
@@ -828,8 +828,7 @@
         flags, layer_rows, vectors, cos_table, sin_table, w_qkv, qkv_near, qkv_far
     )
     mixed, logs = attend(apart, member, projected, LONGEST)
-    late_up = swap_diagonal(after(late_up, mixed))
-    late_down = swap_diagonal(after(late_down, mixed))
+    late_got = swap_diagonal(after(late_got, mixed))
     last_got = jnp.where(same, last_own, after(last_got, mixed))
     weight_out = last_got[: w_out.shape[0]]
     attn = jnp.dot(mixed, weight_out, preferred_element_type=jnp.float32).astype(jnp.bfloat16)
@@ -838,9 +837,9 @@
     scalars = [flags, dwa_weights]
     fields = [layer_rows, attn, attn_got, cot_half, swap_near(cot_half), vectors]
     *kept, back, act_early, down_early, early_pieces = feed(True, scalars, fields, w_up, w_down, early_got)
-    early_sum = scatter_plane(after(early_pieces, late_up, late_down))
+    early_sum = scatter_plane(after(early_pieces, late_got))
     back, act_late, down_late, *late_owned = feed(
-        False, [flags], [*kept, back], w_up, w_down, late_up, late_down
+        False, [flags], [*kept, back], w_up, w_down, late_got
     )
     late_moved = [send_to_owner(late_owned[j], j // 2, j % 2) for j in range(4)]
     grad_down = kept[2]
@@ -871,13 +870,14 @@
     early_got = swap_diagonal(early_sum)
     small = jnp.concatenate([sums_one[:2], sums_two[:2], sums_now[:1], sums_past[:hist_count]], axis=0)
     small = after(small, ours)
-    for name in ("near", "tp", "far"):
+    for name in ("tp", "far"):
         small = sum_over(small, name)
-    small, ours, late_sum, early_sum, early_got, *attn_moved = lax.optimization_barrier(
-        (small, ours, late_sum, early_sum, early_got, *attn_moved)
-    )
     theirs = swap_diagonal(ours)
-    small = sum_over(small, "dp")
+    small, late_sum, early_sum, early_got, *attn_moved = lax.optimization_barrier(
+        (small, late_sum, early_sum, early_got, *attn_moved)
+    )
+    for name in ("near", "dp"):
+        small = sum_over(small, name)
     attn_sum = add(*attn_moved)
     blocks = jnp.concatenate([attn_sum, jnp.where(same, early_sum, early_got), late_sum], axis=1)
     here = jnp.stack([blocks, swap_far(blocks)])

time: 262 us -> 263 us (level)
  starting transfers between devices: 53.2 us -> 48.9 us
  other arithmetic: 23.5 us -> 26.2 us
    ppermute x1, waiting for transfers between devices: 4.19 us -> 8.52 us  [swap_far(): return lax.ppermute(field, 'far', [(0, 1), (1, 0)])]
    ppermute x8 -> x7, starting transfers between devices: 26.1 us -> 23.1 us  [swap_diagonal(): lax.ppermute(field, AXES, moves(away, lambda t, d, k, c: (c, d, k, t)))]
    ppermute x10, starting transfers between devices: 5.41 us -> 2.73 us  [swap_near(): return lax.ppermute(field, 'near', [(0, 1), (1, 0)])]
    unnamed x98 -> x100, local copies, waits for them, and re-layouts: 12.9 us -> 13.6 us
  transfers between devices with their start and end apart: 39 -> 38, of which waited for: 10 -> 8; matrix products, arithmetic and copies ran while one was open for 12% -> 13% of each run, Pallas kernels for 47% -> 46%
where the time goes in v10:
time: 263 us; the launch traced here: 258 us
  Pallas kernels  122 us (46%)
  starting transfers between devices  48.9 us (19%)
  other arithmetic  26.2 us (10%)
  waiting for transfers between devices  25.4 us (10%)
  local copies, waits for them, and re-layouts  19.9 us (8%)
  between operations  14.7 us (6%)
    pallas_call x10, Pallas kernels, streamed(): pl.pallas_call(kernel, grid_spec=pltpu.PrefetchScalarGridSpec(num_scalar_...  85.2 us
    ppermute x7, starting transfers between devices, swap_diagonal(): lax.ppermute(field, AXES, moves(away, lambda t, d, k, c: (c, d, k, t)))  23.1 us
    pallas_call x1, Pallas kernels, attend_back(): pl.pallas_call(functools.partial(attend_back_kernel, reach), grid=(width...  19.6 us
    unnamed x100, local copies, waits for them, and re-layouts  13.6 us
    pallas_call x1, Pallas kernels, attend(): pl.pallas_call(functools.partial(attend_kernel, reach), grid=(width // LA...  13.1 us
    ppermute x8, starting transfers between devices, send_to_owner(): lax.ppermute(field, AXES, moves(away if not other_far and (not other_tp)...  10.7 us
    ppermute x5, waiting for transfers between devices, sum_over(): lax.ppermute(field, name, [(d, d ^ bit) for d in range(size)])  9.87 us
    ppermute x1, waiting for transfers between devices, swap_far(): return lax.ppermute(field, 'far', [(0, 1), (1, 0)])  8.52 us
  transfers between devices with their start and end apart: 38, of which 8 were waited for; matrix products, arithmetic and copies ran while one was open for 13% of the time, Pallas kernels for 46%

profile of v10, /device:TPU:9, one launch (start us, length us, event | category | flops | bytes accessed | tf_op | source)
XLA Modules:
  0.0 258.4 jit_solution(3734849241332828373)
XLA Ops:
  8.0 3.1 %collective-permute-start = (bf16[512,768]{1,0:T(8,128)(2,1)}, bf16[512,768]{1,0:T(8,128)(2,1)}, u32[]{:S(2)}, u32[]{:S(2)}) collective-permute-start(bf16[512,768]{1,0:T(8,128)(2,1)} %bitcast.45), channel_id=1, source_target_pairs={{1,16},{3,18},{5,20},{7,22},{9,24},{11,26},{13,28},{15,30},{16,1},... | collective-permute-start | bytes 2359304 | tf_op jit(solution)/shard_map/ppermute | solution.py:702
  11.1 2.2 constant_dynamic-slice_fusion
  13.2 2.6 %collective-permute-start.3 = (bf16[3,384,384]{2,1,0:T(8,128)(2,1)}, bf16[3,384,384]{2,1,0:T(8,128)(2,1)S(1)}, u32[]{:S(2)}, u32[]{:S(2)}) collective-permute-start(bf16[3,384,384]{2,1,0:T(8,128)(2,1)} %constant_dynamic-slice_fusion), channel_id=1, source_target_pairs={{1,16},{3,18},{5,20},{7,22},{9,24},{11,26},{13,28},{15,30},{16,1},... | collective-permute-start | bytes 2654216 | tf_op jit(solution)/shard_map/ppermute | solution.py:702
  16.0 2.5 pad_maximum_fusion.2
  18.5 1.9 fusion.10
  20.4 1.6 pad_maximum_fusion.1
  22.0 1.6 pad_maximum_fusion
  23.6 4.4 %shard_map.220 = (bf16[4,512,768]{2,1,0:T(8,128)(2,1)}, f32[512,768]{1,0:T(8,128)}, f32[8,768]{1,0:T(8,128)}) custom-call(f32[5]{0:T(128)} %weight_ref.1, bf16[4,512,768]{2,1,0:T(8,128)(2,1)} %bitcast.43, bf16[512,768]{1,0:T(8,128)(2,1)} %bitcast.41), custom_call_target="tpu_custom_call" | custom-call | bytes 9000000 | tf_op jit(solution)/shard_map/pallas_call | solution.py:632
  29.6 3.1 %collective-permute-start.5 = (bf16[896,768]{1,0:T(8,128)(2,1)S(1)}, bf16[896,768]{1,0:T(8,128)(2,1)}, u32[]{:S(2)}, u32[]{:S(2)}) collective-permute-start(bf16[896,768]{1,0:T(8,128)(2,1)S(1)} %copy-done.30), channel_id=1, source_target_pairs={{1,16},{3,18},{5,20},{7,22},{9,24},{11,26},{13,28},{15,30},{16,1},... | collective-permute-start | bytes 4128776 | tf_op jit(solution)/shard_map/ppermute | solution.py:702
  32.7 1.2 broadcast_select_fusion.1
  34.0 3.1 %collective-permute-start.4 = (bf16[3,384,384]{2,1,0:T(8,128)(2,1)S(1)}, bf16[3,384,384]{2,1,0:T(8,128)(2,1)S(1)}, u32[]{:S(2)}, u32[]{:S(2)}) collective-permute-start(bf16[3,384,384]{2,1,0:T(8,128)(2,1)S(1)} %collective-permute-done.3.w_near), channel_id=1, source_target_pairs={{1,3},{3,1},{5,7},{7,5},{9,11},{11,9},{13,15},{15,13},{16,18},{18,... | collective-permute-start | bytes 2654216 | tf_op jit(solution)/shard_map/ppermute | solution.py:717
  37.1 0.9 fusion.2.member_ref
  38.1 0.9 select_convert_fusion.apart_ref
  39.0 3.1 %fusion.1 = (f32[1024,128]{1,0:T(8,128)}, f32[1024,128]{1,0:T(8,128)}) fusion(f32[128]{0:T(128)S(1)} %get-tuple-element.237, f32[128]{0:T(128)S(1)} %get-tuple-element.238, f32[1024]{0:T(1024)S(1)} %subtract_convert_fusion), kind=kLoop, calls=%fused_computation.13 | loop fusion | flops 262144 | bytes 1053696 | tf_op jit(solution)/shard_map/mul | solution.py:817
  42.0 2.8 %collective-permute-start.8 = (bf16[1536,768]{1,0:T(8,128)(2,1)}, bf16[1536,768]{1,0:T(8,128)(2,1)}, u32[]{:S(2)}, u32[]{:S(2)}) collective-permute-start(bf16[1536,768]{1,0:T(8,128)(2,1)} %pad_maximum_fusion), channel_id=1, source_target_pairs={{1,16},{3,18},{5,20},{7,22},{9,24},{11,26},{13,28},{15,30},{16,1},... | collective-permute-start | bytes 7077896 | tf_op jit(solution)/shard_map/ppermute | solution.py:702
  44.8 1.9 maximum_select_fusion.rows_ref.refs_2_
  46.7 1.1 collective-permute-done.4.w_far
  47.8 0.9 copy-done.11
  48.7 9.0 %shard_map.221 = (bf16[3,1024,384]{2,1,0:T(8,128)(2,1)}, bf16[768,1024]{1,0:T(8,128)(2,1)}) custom-call(s32[4]{0:T(128)} %pad_add_fusion.flags.refs_0_, bf16[1024,768]{1,0:T(8,128)(2,1)} %maximum_select_fusion.rows_ref.refs_2_, f32[1024,128]{1,0:T(8,128)} %get-tuple-element.103.cos_ref, f32[1024,128]{1,0:T(8,128)} %get-tuple-element.104.sin_ref, ...), custom_call_target="tpu_custom_call" | custom-call | bytes 24000000 | tf_op jit(solution)/shard_map/pallas_call | solution.py:240
  57.7 13.1 %shard_map.222 = (bf16[1024,384]{1,0:T(8,128)(2,1)}, f32[3,8,1024]{2,1,0:T(8,128)}) custom-call(bf16[1024,128]{1,0:T(8,128)(2,1)} %select_convert_fusion.apart_ref, bf16[1024,128]{1,0:T(8,128)(2,1)} %fusion.2.member_ref, bf16[3,1024,384]{2,1,0:T(8,128)(2,1)} %get-tuple-element.106.q_ref.k_ref.v_ref, ...), custom_call_target="tpu_custom_call" | custom-call | bytes 36000000 | tf_op jit(solution)/shard_map/pallas_call | solution.py:104
  70.8 4.0 %collective-permute-start.9 = (bf16[1536,768]{1,0:T(8,128)(2,1)}, bf16[1536,768]{1,0:T(8,128)(2,1)}, u32[]{:S(2)}, u32[]{:S(2)}) collective-permute-start(bf16[1536,768]{1,0:T(8,128)(2,1)} %pad_maximum_fusion.1), channel_id=1, source_target_pairs={{1,16},{3,18},{5,20},{7,22},{9,24},{11,26},{13,28},{15,30},{16,1},... | collective-permute-start | bytes 7077896 | tf_op jit(solution)/shard_map/ppermute | solution.py:702
  74.8 1.7 broadcast_select_fusion.w_ref
  76.4 1.0 convolution_convert_fusion.refs_3_.own_ref
  78.1 3.9 %collective-permute-done.7.refs_6_ = bf16[512,768]{1,0:T(8,128)(2,1)S(1)} collective-permute-done((bf16[512,768]{1,0:T(8,128)(2,1)S(1)}, bf16[512,768]{1,0:T(8,128)(2,1)S(1)}, u32[]{:S(2)}, u32[]{:S(2)}) %collective-permute-start.7) | collective-permute-done | bytes 786464 | tf_op jit(solution)/shard_map/ppermute | solution.py:725
  82.9 1.2 copy-done.5
  84.1 19.0 %shard_map.223 = (bf16[1024,768]{1,0:T(8,128)(2,1)}, bf16[768,1024]{1,0:T(8,128)(2,1)}, bf16[1024,768]{1,0:T(8,128)(2,1)}, bf16[768,1024]{1,0:T(8,128)(2,1)}, bf...) custom-call(s32[4]{0:T(128)} %pad_add_fusion.flags.refs_0_, ...), custom_call_target="tpu_custom_call" | custom-call | bytes 51000000 | tf_op jit(solution)/shard_map/pallas_call | solution.py:240
  103.2 16.3 %shard_map.224 = (bf16[1024,768]{1,0:T(8,128)(2,1)}, bf16[1024,768]{1,0:T(8,128)(2,1)}, bf16[768,768]{1,0:T(8,128)(2,1)}, bf16[768,384]{1,0:T(8,128)(2,1)}, bf16...) custom-call(s32[4]{0:T(128)} %pad_add_fusion.flags.refs_0_, ...), custom_call_target="tpu_custom_call" | custom-call | bytes 51000000 | tf_op jit(solution)/shard_map/pallas_call | solution.py:240
  119.8 2.9 %collective-permute-start.13 = (bf16[768,384]{1,0:T(8,128)(2,1)}, bf16[768,384]{1,0:T(8,128)(2,1)S(1)}, u32[]{:S(2)}, u32[]{:S(2)}) collective-permute-start(bf16[768,384]{1,0:T(8,128)(2,1)} %get-tuple-element.123), channel_id=1, source_target_pairs={{0,2},{1,18},{2,0},{3,16},{4,6},{5,22},{6,4},{7,20},{8,10},{9,26},... | collective-permute-start | bytes 1769480 | tf_op jit(solution)/shard_map/ppermute | solution.py:706
  122.7 2.8 %collective-permute-start.11 = (bf16[768,384]{1,0:T(8,128)(2,1)}, bf16[768,384]{1,0:T(8,128)(2,1)S(1)}, u32[]{:S(2)}, u32[]{:S(2)}) collective-permute-start(bf16[768,384]{1,0:T(8,128)(2,1)} %get-tuple-element.121), channel_id=1, source_target_pairs={{1,16},{3,18},{5,20},{7,22},{9,24},{11,26},{13,28},{15,30},{16,1},... | collective-permute-start | bytes 1769480 | tf_op jit(solution)/shard_map/ppermute | solution.py:706
  125.5 1.2 copy-done.29
  126.7 10.2 %shard_map.225 = (bf16[1024,768]{1,0:T(8,128)(2,1)}, bf16[1024,384]{1,0:T(8,128)(2,1)}, bf16[768,384]{1,0:T(8,128)(2,1)}, f32[8,768]{1,0:T(8,128)}) custom-call(s32[4]{0:T(128)} %pad_add_fusion.flags.refs_0_, bf16[1024,768]{1,0:T(8,128)(2,1)} %maximum_select_fusion.rows_ref.refs_2_, bf16[1024,768]{1,0:T(8,128)(2,1)} %copy-done.3, ...), custom_call_target="tpu_custom_call" | custom-call | bytes 24000000 | tf_op jit(solution)/shard_map/pallas_call | solution.py:240
  137.0 19.6 %shard_map.226.grad_ref = bf16[3,1024,384]{2,1,0:T(8,128)(2,1)} custom-call(bf16[1024,128]{1,0:T(8,128)(2,1)} %select_convert_fusion.apart_ref, bf16[1024,128]{1,0:T(8,128)(2,1)} %fusion.2.member_ref, f32[1024,128]{1,0:T(8,128)} %get-tuple-element.103.cos_ref, f32[1024,128]{1,0:T(8,128)} %get-tuple-element.104.sin_ref, ...), custom_call_target="tpu_custom_call" | custom-call | bytes 66000000 | tf_op jit(solution)/shard_map/pallas_call | solution.py:189
  156.8 7.6 %shard_map.227 = (bf16[768,384]{1,0:T(8,128)(2,1)}, bf16[768,384]{1,0:T(8,128)(2,1)}, bf16[768,384]{1,0:T(8,128)(2,1)}, bf16[768,384]{1,0:T(8,128)(2,1)}) custom-call(s32[4]{0:T(128)} %pad_add_fusion.flags.refs_0_, bf16[768,1024]{1,0:T(8,128)(2,1)} %get-tuple-element.126.turned_ref, bf16[768,384]{1,0:T(8,128)(2,1)} %get-tuple-element.127.out_grad_ref, ...), custom_call_target="tpu_custom_call" | custom-call | bytes 12000000 | tf_op jit(solution)/shard_map/pallas_call | solution.py:240
  164.4 3.2 %collective-permute-start.15 = (bf16[768,384]{1,0:T(8,128)(2,1)}, bf16[768,384]{1,0:T(8,128)(2,1)}, u32[]{:S(2)}, u32[]{:S(2)}) collective-permute-start(bf16[768,384]{1,0:T(8,128)(2,1)} %get-tuple-element.128), channel_id=1, source_target_pairs={{1,16},{3,18},{5,20},{7,22},{9,24},{11,26},{13,28},{15,30},{16,1},... | collective-permute-start | bytes 1769480 | tf_op jit(solution)/shard_map/ppermute | solution.py:706
  167.6 1.5 collective-permute-start.17
  169.5 3.0 %add_convert_fusion = bf16[768,384]{1,0:T(8,128)(2,1)} fusion(bf16[768,384]{1,0:T(8,128)(2,1)} %copy-done.36, bf16[768,384]{1,0:T(8,128)(2,1)} %copy-done.35, bf16[768,384]{1,0:T(8,128)(2,1)} %copy-done.34, bf16[768,384]{1,0:T(8,128)(2,1)} %get-tuple-element.121, bf16[768,384]{1,0:T(8,128)(2,1)} %copy-done.37, pred[]{:T(512)S(6)} %eq.35), kind=kLoop, calls=%fused_computation.6 | loop fusion | flops 2654208 | bytes 3538945 | tf_op jit(solution)/shard_map/convert_element_type | solution.py:744
  173.3 1.7 copy-done.1
  175.0 1.2 copy-done.10
  176.2 1.2 copy-done.12
  177.4 6.2 %shard_map.228 = (f32[512,768]{1,0:T(8,128)S(1)}, bf16[256,768]{1,0:T(8,128)(2,1)}, bf16[256,768]{1,0:T(8,128)(2,1)}, f32[8,768]{1,0:T(8,128)S(1)}) custom-call(s32[4]{0:T(128)S(1)} %copy-done.20, bf16[3,1024,384]{2,1,0:T(8,128)(2,1)S(1)} %copy-done.1, bf16[1024,768]{1,0:T(8,128)(2,1)S(1)} %copy-done, bf16[3,768,384]{2,1,0:T(8,128)(2,1)S(1)} %copy-done.7, ...), custom_call_target="tpu_custom_call" | custom-call | bytes 15000000 | tf_op jit(solution)/shard_map/pallas_call | solution.py:240
  183.5 1.2 copy-done.14
  184.7 1.4 copy-done.17
  186.1 1.3 copy-done.19
  187.4 6.9 %shard_map.229 = (f32[512,768]{1,0:T(8,128)S(1)}, bf16[256,768]{1,0:T(8,128)(2,1)S(1)}, bf16[256,768]{1,0:T(8,128)(2,1)S(1)}, f32[8,768]{1,0:T(8,128)S(1)}) custom-call(s32[4]{0:T(128)S(1)} %copy-done.20, bf16[1024,768]{1,0:T(8,128)(2,1)S(1)} %copy-done.16, bf16[1024,768]{1,0:T(8,128)(2,1)S(1)} %copy-done.17, bf16[1024,768]{1,0:T(8,128)(2,1)S(1)} %copy-done, ...), custom_call_target="tpu_custom_call" | custom-call | bytes 18000000 | tf_op jit(solution)/shard_map/pallas_call | solution.py:240
  194.4 1.9 collective-permute-done.18
  197.4 2.0 add_convert_fusion.1
  200.2 2.4 collective-permute-start.28
  202.6 2.2 collective-permute-start.27
  204.8 3.4 %collective-permute-start.26 = (bf16[192,384]{1,0:T(8,128)(2,1)}, bf16[192,384]{1,0:T(8,128)(2,1)S(1)}, u32[]{:S(2)}, u32[]{:S(2)}) collective-permute-start(bf16[192,384]{1,0:T(8,128)(2,1)} %reduce-scatter.8.cloned.1.call-done), channel_id=1, source_target_pairs={{1,16},{3,18},{5,20},{7,22},{9,24},{11,26},{13,28},{15,30},{16,1},... | collective-permute-start | bytes 442376 | tf_op jit(solution)/shard_map/ppermute | solution.py:702
  209.0 5.4 %shard_map.230.own_ref = bf16[2,512,768]{2,1,0:T(8,128)(2,1)} custom-call(s32[4]{0:T(128)} %pad_add_fusion.flags.refs_0_, bf16[1024,768]{1,0:T(8,128)(2,1)} %maximum_select_fusion.rows_ref.refs_2_, bf16[1024,768]{1,0:T(8,128)(2,1)} %get-tuple-element.118.resid_ref, f32[512,768]{1,0:T(8,128)} %copy-done.14, f32[512,768]{1,0:T(8,128)} %copy-done.15, ...), custom_call_target="tpu_custom_call" | custom-call | bytes 9000000 | tf_op jit(solution)/shard_map/pallas_call | solution.py:240
  214.4 2.9 %collective-permute-done.24 = f32[9,768]{1,0:T(8,128)S(1)} collective-permute-done((f32[9,768]{1,0:T(8,128)S(1)}, f32[9,768]{1,0:T(8,128)S(1)}, u32[]{:S(2)}, u32[]{:S(2)}) %collective-permute-start.24) | collective-permute-done | bytes 27680 | tf_op jit(solution)/shard_map/ppermute | solution.py:772
  217.4 1.4 collective-permute-start.25
  218.8 2.0 collective-permute-done.25
  220.8 4.3 %collective-permute-start.23 = (bf16[2,512,768]{2,1,0:T(8,128)(2,1)}, bf16[2,512,768]{2,1,0:T(8,128)(2,1)S(1)}, u32[]{:S(2)}, u32[]{:S(2)}) collective-permute-start(bf16[2,512,768]{2,1,0:T(8,128)(2,1)} %shard_map.230.own_ref), channel_id=1, source_target_pairs={{1,16},{3,18},{5,20},{7,22},{9,24},{11,26},{13,28},{15,30},{16,1},... | collective-permute-start | bytes 4718600 | tf_op jit(solution)/shard_map/ppermute | solution.py:702
  225.8 1.1 add_convert_fusion.2
  227.0 1.1 fusion.9
  228.1 1.2 collective-permute-start.33
  229.3 8.5 %collective-permute-done.33 = bf16[192,1152]{1,0:T(8,128)(2,1)S(1)} collective-permute-done((bf16[192,1152]{1,0:T(8,128)(2,1)S(1)}, bf16[192,1152]{1,0:T(8,128)(2,1)S(1)}, u32[]{:S(2)}, u32[]{:S(2)}) %collective-permute-start.33) | collective-permute-done | bytes 442400 | tf_op jit(solution)/shard_map/ppermute | solution.py:721
  238.5 2.0 collective-permute-done.30
  240.6 2.9 %collective-permute-done.31 = f32[9,768]{1,0:T(8,128)S(1)} collective-permute-done((f32[9,768]{1,0:T(8,128)S(1)}, f32[9,768]{1,0:T(8,128)S(1)}, u32[]{:S(2)}, u32[]{:S(2)}) %collective-permute-start.31) | collective-permute-done | bytes 27680 | tf_op jit(solution)/shard_map/ppermute | solution.py:772
  243.5 1.2 collective-permute-start.32
  245.3 2.1 shard_map.231
  247.4 1.3 slice_reduce_fusion
  249.3 2.5 shard_map.232
  (176 shorter events, 11.1 us)
Async XLA Ops:
  7.2 8.7 %copy-start.45 = (f32[768]{0:T(1024)S(1)}, f32[768]{0:T(1024)}, u32[]{:S(2)}) copy-start(f32[768]{0:T(1024)} %param.18) | copy-start | bytes 9220
  7.2 8.8 %copy-start.46 = (f32[768]{0:T(1024)S(1)}, f32[768]{0:T(1024)}, u32[]{:S(2)}) copy-start(f32[768]{0:T(1024)} %param.19) | copy-start | bytes 9220
  7.2 8.8 %copy-start.47 = (f32[768]{0:T(1024)S(1)}, f32[768]{0:T(1024)}, u32[]{:S(2)}) copy-start(f32[768]{0:T(1024)} %param.22) | copy-start | bytes 9220
  7.2 8.8 %copy-start.48 = (f32[768]{0:T(1024)S(1)}, f32[768]{0:T(1024)}, u32[]{:S(2)}) copy-start(f32[768]{0:T(1024)} %param.23) | copy-start | bytes 9220
  7.2 149.5 %reduce-scatter.10.cloned.1.call-start = ((), (), s32[]{:S(2)}) async-start(), calls=%async_computation.5 | async-start | bytes 2949120
  7.3 21.9 %collective-permute-start.2 = (s32[1,3]{1,0:T(1,128)}, s32[1,3]{1,0:T(1,128)S(1)}, u32[]{:S(2)}, u32[]{:S(2)}) collective-permute-start(s32[1,3]{1,0:T(1,128)} %param.16), channel_id=1, source_target_pairs={{0,1},{1,0},{2,3},{3,2},{4,5},{5,4},{6,7},{7,6},{8,9},{9,8},{10,11... | collective-permute-start | bytes 44 | tf_op jit(solution)/shard_map/ppermute | solution.py:725
  8.0 21.6 %collective-permute-start = (bf16[512,768]{1,0:T(8,128)(2,1)}, bf16[512,768]{1,0:T(8,128)(2,1)}, u32[]{:S(2)}, u32[]{:S(2)}) collective-permute-start(bf16[512,768]{1,0:T(8,128)(2,1)} %bitcast.45), channel_id=1, source_target_pairs={{1,16},{3,18},{5,20},{7,22},{9,24},{11,26},{13,28},{15,30},{16,1},... | collective-permute-start | bytes 2359304 | tf_op jit(solution)/shard_map/ppermute | solution.py:702
  13.2 20.7 %collective-permute-start.3 = (bf16[3,384,384]{2,1,0:T(8,128)(2,1)}, bf16[3,384,384]{2,1,0:T(8,128)(2,1)S(1)}, u32[]{:S(2)}, u32[]{:S(2)}) collective-permute-start(bf16[3,384,384]{2,1,0:T(8,128)(2,1)} %constant_dynamic-slice_fusion), channel_id=1, source_target_pairs={{1,16},{3,18},{5,20},{7,22},{9,24},{11,26},{13,28},{15,30},{16,1},... | collective-permute-start | bytes 2654216 | tf_op jit(solution)/shard_map/ppermute | solution.py:702
  23.6 6.0 %copy-start.30 = (bf16[896,768]{1,0:T(8,128)(2,1)S(1)}, bf16[896,768]{1,0:T(8,128)(2,1)}, u32[]{:S(2)}) copy-start(bf16[896,768]{1,0:T(8,128)(2,1)} %pad_maximum_fusion.2) | copy-start | bytes 4128772
  23.6 9.1 %copy-start.31 = (bf16[1,512,768]{2,1,0:T(8,128)(2,1)S(1)}, bf16[1,512,768]{2,1,0:T(8,128)(2,1)}, u32[]{:S(2)}) copy-start(bf16[1,512,768]{2,1,0:T(8,128)(2,1)} %param.13) | copy-start | bytes 2359300
  29.6 45.1 %collective-permute-start.5 = (bf16[896,768]{1,0:T(8,128)(2,1)S(1)}, bf16[896,768]{1,0:T(8,128)(2,1)}, u32[]{:S(2)}, u32[]{:S(2)}) collective-permute-start(bf16[896,768]{1,0:T(8,128)(2,1)S(1)} %copy-done.30), channel_id=1, source_target_pairs={{1,16},{3,18},{5,20},{7,22},{9,24},{11,26},{13,28},{15,30},{16,1},... | collective-permute-start | bytes 4128776 | tf_op jit(solution)/shard_map/ppermute | solution.py:702
  33.9 10.9 %collective-permute-start.1 = (bf16[512,768]{1,0:T(8,128)(2,1)S(1)}, bf16[512,768]{1,0:T(8,128)(2,1)S(1)}, u32[]{:S(2)}, u32[]{:S(2)}) collective-permute-start(bf16[512,768]{1,0:T(8,128)(2,1)S(1)} %broadcast_select_fusion.1), channel_id=1, source_target_pairs={{0,1},{1,0},{2,3},{3,2},{4,5},{5,4},{6,7},{7,6},{8,9},{9,8},{10,11... | collective-permute-start | bytes 2359304 | tf_op jit(solution)/shard_map/ppermute | solution.py:725
  34.0 12.7 %copy-start.9 = (bf16[3,384,384]{2,1,0:T(8,128)(2,1)}, bf16[3,384,384]{2,1,0:T(8,128)(2,1)S(1)}, u32[]{:S(2)}) copy-start(bf16[3,384,384]{2,1,0:T(8,128)(2,1)S(1)} %collective-permute-done.3.w_near) | copy-start | bytes 2654212
  34.0 13.8 %collective-permute-start.4 = (bf16[3,384,384]{2,1,0:T(8,128)(2,1)S(1)}, bf16[3,384,384]{2,1,0:T(8,128)(2,1)S(1)}, u32[]{:S(2)}, u32[]{:S(2)}) collective-permute-start(bf16[3,384,384]{2,1,0:T(8,128)(2,1)S(1)} %collective-permute-done.3.w_near), channel_id=1, source_target_pairs={{1,3},{3,1},{5,7},{7,5},{9,11},{11,9},{13,15},{15,13},{16,18},{18,... | collective-permute-start | bytes 2654216 | tf_op jit(solution)/shard_map/ppermute | solution.py:717
  42.0 40.9 %collective-permute-start.8 = (bf16[1536,768]{1,0:T(8,128)(2,1)}, bf16[1536,768]{1,0:T(8,128)(2,1)}, u32[]{:S(2)}, u32[]{:S(2)}) collective-permute-start(bf16[1536,768]{1,0:T(8,128)(2,1)} %pad_maximum_fusion), channel_id=1, source_target_pairs={{1,16},{3,18},{5,20},{7,22},{9,24},{11,26},{13,28},{15,30},{16,1},... | collective-permute-start | bytes 7077896 | tf_op jit(solution)/shard_map/ppermute | solution.py:702
  57.7 17.1 %copy-start.25 = (bf16[1,512,768]{2,1,0:T(8,128)(2,1)S(1)}, bf16[1,512,768]{2,1,0:T(8,128)(2,1)}, u32[]{:S(2)}) copy-start(bf16[1,512,768]{2,1,0:T(8,128)(2,1)} %param.15) | copy-start | bytes 2359300
  57.7 17.1 %copy-start.28 = (bf16[384,768]{1,0:T(8,128)(2,1)S(1)}, bf16[384,768]{1,0:T(8,128)(2,1)}, u32[]{:S(2)}) copy-start(bf16[384,768]{1,0:T(8,128)(2,1)} %param.21) | copy-start | bytes 1769476
  70.8 32.4 %collective-permute-start.9 = (bf16[1536,768]{1,0:T(8,128)(2,1)}, bf16[1536,768]{1,0:T(8,128)(2,1)}, u32[]{:S(2)}, u32[]{:S(2)}) collective-permute-start(bf16[1536,768]{1,0:T(8,128)(2,1)} %pad_maximum_fusion.1), channel_id=1, source_target_pairs={{1,16},{3,18},{5,20},{7,22},{9,24},{11,26},{13,28},{15,30},{16,1},... | collective-permute-start | bytes 7077896 | tf_op jit(solution)/shard_map/ppermute | solution.py:702
  77.4 5.5 %collective-permute-start.6 = (bf16[1024,768]{1,0:T(8,128)(2,1)S(1)}, bf16[1024,768]{1,0:T(8,128)(2,1)S(1)}, u32[]{:S(2)}, u32[]{:S(2)}) collective-permute-start(bf16[1024,768]{1,0:T(8,128)(2,1)S(1)} %convolution_convert_fusion.refs_3_.own_ref), channel_id=1, source_target_pairs={{0,1},{1,0},{2,3},{3,2},{4,5},{5,4},{6,7},{7,6},{8,9},{9,8},{10,11... | collective-permute-start | bytes 4718600 | tf_op jit(solution)/shard_map/ppermute | solution.py:725
  77.6 4.4 %collective-permute-start.7 = (bf16[512,768]{1,0:T(8,128)(2,1)S(1)}, bf16[512,768]{1,0:T(8,128)(2,1)S(1)}, u32[]{:S(2)}, u32[]{:S(2)}) collective-permute-start(bf16[512,768]{1,0:T(8,128)(2,1)S(1)} %slice.53.refs_5_), channel_id=1, source_target_pairs={{0,1},{1,0},{2,3},{3,2},{4,5},{5,4},{6,7},{7,6},{8,9},{9,8},{10,11... | collective-permute-start | bytes 2359304 | tf_op jit(solution)/shard_map/ppermute | solution.py:725
  103.2 97.1 %reduce-scatter.8.cloned.1.call-start = ((), (), s32[]{:S(2)}) async-start(), calls=%async_computation.4 | async-start | bytes 737280 | tf_op jit(solution)/shard_map/reduce_scatter | solution.py:752
  119.5 5.9 %collective-permute-start.10 = (bf16[1024,768]{1,0:T(8,128)(2,1)}, bf16[1024,768]{1,0:T(8,128)(2,1)S(1)}, u32[]{:S(2)}, u32[]{:S(2)}) collective-permute-start(bf16[1024,768]{1,0:T(8,128)(2,1)} %get-tuple-element.117.back_own), channel_id=1, source_target_pairs={{0,1},{1,0},{2,3},{3,2},{4,5},{5,4},{6,7},{7,6},{8,9},{9,8},{10,11... | collective-permute-start | bytes 4718600 | tf_op jit(solution)/shard_map/ppermute | solution.py:725
  119.7 36.8 %collective-permute-start.12 = (bf16[768,384]{1,0:T(8,128)(2,1)}, bf16[768,384]{1,0:T(8,128)(2,1)S(1)}, u32[]{:S(2)}, u32[]{:S(2)}) collective-permute-start(bf16[768,384]{1,0:T(8,128)(2,1)} %get-tuple-element.122), channel_id=1, source_target_pairs={{0,1},{1,17},{2,3},{3,19},{4,5},{5,21},{6,7},{7,23},{8,9},{9,25},{... | collective-permute-start | bytes 1769480 | tf_op jit(solution)/shard_map/ppermute | solution.py:706
  119.8 36.9 %collective-permute-start.13 = (bf16[768,384]{1,0:T(8,128)(2,1)}, bf16[768,384]{1,0:T(8,128)(2,1)S(1)}, u32[]{:S(2)}, u32[]{:S(2)}) collective-permute-start(bf16[768,384]{1,0:T(8,128)(2,1)} %get-tuple-element.123), channel_id=1, source_target_pairs={{0,2},{1,18},{2,0},{3,16},{4,6},{5,22},{6,4},{7,20},{8,10},{9,26},... | collective-permute-start | bytes 1769480 | tf_op jit(solution)/shard_map/ppermute | solution.py:706
  122.7 34.0 %collective-permute-start.14 = (bf16[768,384]{1,0:T(8,128)(2,1)}, bf16[768,384]{1,0:T(8,128)(2,1)S(1)}, u32[]{:S(2)}, u32[]{:S(2)}) collective-permute-start(bf16[768,384]{1,0:T(8,128)(2,1)} %get-tuple-element.124), channel_id=1, source_target_pairs={{0,3},{1,19},{2,1},{3,17},{4,7},{5,23},{6,5},{7,21},{8,11},{9,27},... | collective-permute-start | bytes 1769480 | tf_op jit(solution)/shard_map/ppermute | solution.py:706
  122.7 34.0 %collective-permute-start.11 = (bf16[768,384]{1,0:T(8,128)(2,1)}, bf16[768,384]{1,0:T(8,128)(2,1)S(1)}, u32[]{:S(2)}, u32[]{:S(2)}) collective-permute-start(bf16[768,384]{1,0:T(8,128)(2,1)} %get-tuple-element.121), channel_id=1, source_target_pairs={{1,16},{3,18},{5,20},{7,22},{9,24},{11,26},{13,28},{15,30},{16,1},... | collective-permute-start | bytes 1769480 | tf_op jit(solution)/shard_map/ppermute | solution.py:706
  156.6 7.8 %copy-start.34 = (bf16[768,384]{1,0:T(8,128)(2,1)}, bf16[768,384]{1,0:T(8,128)(2,1)S(1)}, u32[]{:S(2)}) copy-start(bf16[768,384]{1,0:T(8,128)(2,1)S(1)} %collective-permute-done.12) | copy-start | bytes 1769476
  156.6 7.8 %copy-start.35 = (bf16[768,384]{1,0:T(8,128)(2,1)}, bf16[768,384]{1,0:T(8,128)(2,1)S(1)}, u32[]{:S(2)}) copy-start(bf16[768,384]{1,0:T(8,128)(2,1)S(1)} %collective-permute-done.13) | copy-start | bytes 1769476
  156.6 7.8 %copy-start.36 = (bf16[768,384]{1,0:T(8,128)(2,1)}, bf16[768,384]{1,0:T(8,128)(2,1)S(1)}, u32[]{:S(2)}) copy-start(bf16[768,384]{1,0:T(8,128)(2,1)S(1)} %collective-permute-done.14) | copy-start | bytes 1769476
  156.7 7.8 %copy-start.37 = (bf16[768,384]{1,0:T(8,128)(2,1)}, bf16[768,384]{1,0:T(8,128)(2,1)S(1)}, u32[]{:S(2)}) copy-start(bf16[768,384]{1,0:T(8,128)(2,1)S(1)} %collective-permute-done.11) | copy-start | bytes 1769476
  156.7 69.0 %reduce-scatter.6.cloned.1.call-start = ((), (), s32[]{:S(2)}) async-start(), calls=%async_computation.3 | async-start | bytes 737280 | tf_op jit(solution)/shard_map/reduce_scatter | solution.py:752
  164.4 31.9 %collective-permute-start.15 = (bf16[768,384]{1,0:T(8,128)(2,1)}, bf16[768,384]{1,0:T(8,128)(2,1)}, u32[]{:S(2)}, u32[]{:S(2)}) collective-permute-start(bf16[768,384]{1,0:T(8,128)(2,1)} %get-tuple-element.128), channel_id=1, source_target_pairs={{1,16},{3,18},{5,20},{7,22},{9,24},{11,26},{13,28},{15,30},{16,1},... | collective-permute-start | bytes 1769480 | tf_op jit(solution)/shard_map/ppermute | solution.py:706
  167.6 26.8 %collective-permute-start.16 = (bf16[768,384]{1,0:T(8,128)(2,1)}, bf16[768,384]{1,0:T(8,128)(2,1)}, u32[]{:S(2)}, u32[]{:S(2)}) collective-permute-start(bf16[768,384]{1,0:T(8,128)(2,1)} %get-tuple-element.141), channel_id=1, source_target_pairs={{0,1},{1,17},{2,3},{3,19},{4,5},{5,21},{6,7},{7,23},{8,9},{9,25},{... | collective-permute-start | bytes 1769480 | tf_op jit(solution)/shard_map/ppermute | solution.py:706
  167.6 26.8 %collective-permute-start.17 = (bf16[768,384]{1,0:T(8,128)(2,1)}, bf16[768,384]{1,0:T(8,128)(2,1)}, u32[]{:S(2)}, u32[]{:S(2)}) collective-permute-start(bf16[768,384]{1,0:T(8,128)(2,1)} %get-tuple-element.142), channel_id=1, source_target_pairs={{0,2},{1,18},{2,0},{3,16},{4,6},{5,22},{6,4},{7,20},{8,10},{9,26},... | collective-permute-start | bytes 1769480 | tf_op jit(solution)/shard_map/ppermute | solution.py:706
  169.1 27.2 %collective-permute-start.18 = (bf16[768,384]{1,0:T(8,128)(2,1)}, bf16[768,384]{1,0:T(8,128)(2,1)}, u32[]{:S(2)}, u32[]{:S(2)}) collective-permute-start(bf16[768,384]{1,0:T(8,128)(2,1)} %get-tuple-element.143), channel_id=1, source_target_pairs={{0,3},{1,19},{2,1},{3,17},{4,7},{5,23},{6,5},{7,21},{8,11},{9,27},... | collective-permute-start | bytes 1769480 | tf_op jit(solution)/shard_map/ppermute | solution.py:706
  177.3 7.4 %copy-start.2 = (bf16[1024,768]{1,0:T(8,128)(2,1)S(1)}, bf16[1024,768]{1,0:T(8,128)(2,1)}, u32[]{:S(2)}) copy-start(bf16[1024,768]{1,0:T(8,128)(2,1)} %get-tuple-element.133.refs_3_.cot_ref) | copy-start | bytes 4718596
  177.3 7.4 %copy-start.4 = (bf16[1024,768]{1,0:T(8,128)(2,1)S(1)}, bf16[1024,768]{1,0:T(8,128)(2,1)}, u32[]{:S(2)}) copy-start(bf16[1024,768]{1,0:T(8,128)(2,1)} %copy-done.3) | copy-start | bytes 4718596
  177.3 7.4 %copy-start.6 = (bf16[1024,768]{1,0:T(8,128)(2,1)S(1)}, bf16[1024,768]{1,0:T(8,128)(2,1)}, u32[]{:S(2)}) copy-start(bf16[1024,768]{1,0:T(8,128)(2,1)} %copy-done.5) | copy-start | bytes 4718596
  177.3 7.4 %copy-start.16 = (bf16[1024,768]{1,0:T(8,128)(2,1)S(1)}, bf16[1024,768]{1,0:T(8,128)(2,1)}, u32[]{:S(2)}) copy-start(bf16[1024,768]{1,0:T(8,128)(2,1)} %get-tuple-element.131.act_early) | copy-start | bytes 4718596
  177.4 7.4 %copy-start.18 = (bf16[768,768]{1,0:T(8,128)(2,1)S(1)}, bf16[768,768]{1,0:T(8,128)(2,1)}, u32[]{:S(2)}) copy-start(bf16[768,768]{1,0:T(8,128)(2,1)} %get-tuple-element.134.early_ref) | copy-start | bytes 3538948
  187.4 9.9 %copy-start.33 = (bf16[768,384]{1,0:T(8,128)(2,1)S(1)}, bf16[768,384]{1,0:T(8,128)(2,1)}, u32[]{:S(2)}) copy-start(bf16[768,384]{1,0:T(8,128)(2,1)} %get-tuple-element.128) | copy-start | bytes 1769476
  196.3 3.9 %collective-permute-start.19 = (bf16[256,768]{1,0:T(8,128)(2,1)}, bf16[256,768]{1,0:T(8,128)(2,1)S(1)}, u32[]{:S(2)}, u32[]{:S(2)}) collective-permute-start(bf16[256,768]{1,0:T(8,128)(2,1)} %get-tuple-element.151), channel_id=1, source_target_pairs={{0,1},{1,0},{2,3},{3,2},{4,5},{5,4},{6,7},{7,6},{8,9},{9,8},{10,11... | collective-permute-start | bytes 1179656 | tf_op jit(solution)/shard_map/ppermute | solution.py:725
  196.7 5.9 %collective-permute-start.20 = (bf16[256,768]{1,0:T(8,128)(2,1)}, bf16[256,768]{1,0:T(8,128)(2,1)S(1)}, u32[]{:S(2)}, u32[]{:S(2)}) collective-permute-start(bf16[256,768]{1,0:T(8,128)(2,1)} %get-tuple-element.152), channel_id=1, source_target_pairs={{0,1},{1,0},{2,3},{3,2},{4,5},{5,4},{6,7},{7,6},{8,9},{9,8},{10,11... | collective-permute-start | bytes 1179656 | tf_op jit(solution)/shard_map/ppermute | solution.py:725
  196.8 7.9 %collective-permute-start.21 = (bf16[256,768]{1,0:T(8,128)(2,1)S(1)}, bf16[256,768]{1,0:T(8,128)(2,1)S(1)}, u32[]{:S(2)}, u32[]{:S(2)}) collective-permute-start(bf16[256,768]{1,0:T(8,128)(2,1)S(1)} %get-tuple-element.153), channel_id=1, source_target_pairs={{0,1},{1,0},{2,3},{3,2},{4,5},{5,4},{6,7},{7,6},{8,9},{9,8},{10,11... | collective-permute-start | bytes 1179656 | tf_op jit(solution)/shard_map/ppermute | solution.py:725
  197.2 11.1 %collective-permute-start.22 = (bf16[256,768]{1,0:T(8,128)(2,1)S(1)}, bf16[256,768]{1,0:T(8,128)(2,1)S(1)}, u32[]{:S(2)}, u32[]{:S(2)}) collective-permute-start(bf16[256,768]{1,0:T(8,128)(2,1)S(1)} %get-tuple-element.154), channel_id=1, source_target_pairs={{0,1},{1,0},{2,3},{3,2},{4,5},{5,4},{6,7},{7,6},{8,9},{9,8},{10,11... | collective-permute-start | bytes 1179656 | tf_op jit(solution)/shard_map/ppermute | solution.py:725
  200.1 25.0 %collective-permute-start.29 = (bf16[192,384]{1,0:T(8,128)(2,1)}, bf16[192,384]{1,0:T(8,128)(2,1)}, u32[]{:S(2)}, u32[]{:S(2)}) collective-permute-start(bf16[192,384]{1,0:T(8,128)(2,1)} %get-tuple-element.228), channel_id=1, source_target_pairs={{0,12},{4,0},{8,4},{12,8},{1,13},{5,1},{9,5},{13,9},{2,14},{6,2},{... | collective-permute-start | bytes 442376 | tf_op jit(solution)/shard_map/ppermute | solution.py:764
  200.2 8.0 %copy-start.38 = (bf16[256,768]{1,0:T(8,128)(2,1)}, bf16[256,768]{1,0:T(8,128)(2,1)S(1)}, u32[]{:S(2)}) copy-start(bf16[256,768]{1,0:T(8,128)(2,1)S(1)} %collective-permute-done.19.got_first) | copy-start | bytes 1179652
  200.2 24.8 %collective-permute-start.28 = (bf16[192,384]{1,0:T(8,128)(2,1)S(1)}, bf16[192,384]{1,0:T(8,128)(2,1)S(1)}, u32[]{:S(2)}, u32[]{:S(2)}) collective-permute-start(bf16[192,384]{1,0:T(8,128)(2,1)S(1)} %get-tuple-element.229), channel_id=1, source_target_pairs={{0,8},{4,12},{8,0},{12,4},{1,9},{5,13},{9,1},{13,5},{2,10},{6,14},... | collective-permute-start | bytes 442376 | tf_op jit(solution)/shard_map/ppermute | solution.py:764
  202.6 5.7 %copy-start.39 = (bf16[256,768]{1,0:T(8,128)(2,1)}, bf16[256,768]{1,0:T(8,128)(2,1)S(1)}, u32[]{:S(2)}) copy-start(bf16[256,768]{1,0:T(8,128)(2,1)S(1)} %collective-permute-done.20.got_second) | copy-start | bytes 1179652
  202.6 23.2 %collective-permute-start.27 = (bf16[192,384]{1,0:T(8,128)(2,1)S(1)}, bf16[192,384]{1,0:T(8,128)(2,1)}, u32[]{:S(2)}, u32[]{:S(2)}) collective-permute-start(bf16[192,384]{1,0:T(8,128)(2,1)S(1)} %get-tuple-element.230), channel_id=1, source_target_pairs={{0,4},{4,8},{8,12},{12,0},{1,5},{5,9},{9,13},{13,1},{2,6},{6,10},{... | collective-permute-start | bytes 442376 | tf_op jit(solution)/shard_map/ppermute | solution.py:764
  204.8 21.0 %collective-permute-start.26 = (bf16[192,384]{1,0:T(8,128)(2,1)}, bf16[192,384]{1,0:T(8,128)(2,1)S(1)}, u32[]{:S(2)}, u32[]{:S(2)}) collective-permute-start(bf16[192,384]{1,0:T(8,128)(2,1)} %reduce-scatter.8.cloned.1.call-done), channel_id=1, source_target_pairs={{1,16},{3,18},{5,20},{7,22},{9,24},{11,26},{13,28},{15,30},{16,1},... | collective-permute-start | bytes 442376 | tf_op jit(solution)/shard_map/ppermute | solution.py:702
  209.0 16.8 %copy-start.42 = (bf16[192,384]{1,0:T(8,128)(2,1)S(1)}, bf16[192,384]{1,0:T(8,128)(2,1)}, u32[]{:S(2)}) copy-start(bf16[192,384]{1,0:T(8,128)(2,1)} %reduce-scatter.8.cloned.1.call-done) | copy-start | bytes 442372
  214.4 2.9 %collective-permute-start.24 = (f32[9,768]{1,0:T(8,128)S(1)}, f32[9,768]{1,0:T(8,128)S(1)}, u32[]{:S(2)}, u32[]{:S(2)}) collective-permute-start(f32[9,768]{1,0:T(8,128)S(1)} %pad_maximum_fusion.5), channel_id=1, source_target_pairs={{0,16},{16,0},{1,17},{17,1},{2,18},{18,2},{3,19},{19,3},{4,20},{20... | collective-permute-start | bytes 82952 | tf_op jit(solution)/shard_map/ppermute | solution.py:772
  217.4 3.4 %collective-permute-start.25 = (f32[9,768]{1,0:T(8,128)S(1)}, f32[9,768]{1,0:T(8,128)S(1)}, u32[]{:S(2)}, u32[]{:S(2)}) collective-permute-start(f32[9,768]{1,0:T(8,128)S(1)} %add.97), channel_id=1, source_target_pairs={{0,2},{2,0},{1,3},{3,1},{4,6},{6,4},{5,7},{7,5},{8,10},{10,8},{9,1... | collective-permute-start | bytes 82952 | tf_op jit(solution)/shard_map/ppermute | solution.py:772
  220.8 24.5 %collective-permute-start.23 = (bf16[2,512,768]{2,1,0:T(8,128)(2,1)}, bf16[2,512,768]{2,1,0:T(8,128)(2,1)S(1)}, u32[]{:S(2)}, u32[]{:S(2)}) collective-permute-start(bf16[2,512,768]{2,1,0:T(8,128)(2,1)} %shard_map.230.own_ref), channel_id=1, source_target_pairs={{1,16},{3,18},{5,20},{7,22},{9,24},{11,26},{13,28},{15,30},{16,1},... | collective-permute-start | bytes 4718600 | tf_op jit(solution)/shard_map/ppermute | solution.py:702
  226.9 17.8 %copy-start.22 = (f32[5]{0:T(128)S(1)}, f32[5]{0:T(128)}, u32[]{:S(2)}) copy-start(f32[5]{0:T(128)} %weight_ref.1) | copy-start | bytes 64
  227.0 18.3 %copy-start.8 = (bf16[2,512,768]{2,1,0:T(8,128)(2,1)S(1)}, bf16[2,512,768]{2,1,0:T(8,128)(2,1)}, u32[]{:S(2)}) copy-start(bf16[2,512,768]{2,1,0:T(8,128)(2,1)} %shard_map.230.own_ref) | copy-start | bytes 4718596
  227.0 18.3 %copy-start.13 = (f32[512,768]{1,0:T(8,128)S(1)}, f32[512,768]{1,0:T(8,128)}, u32[]{:S(2)}) copy-start(f32[512,768]{1,0:T(8,128)} %get-tuple-element.99.part_ref) | copy-start | bytes 4718596
  227.0 18.3 %copy-start.21 = (s32[4]{0:T(128)S(1)}, s32[4]{0:T(128)}, u32[]{:S(2)}) copy-start(s32[4]{0:T(128)} %pad_add_fusion.flags.refs_0_) | copy-start | bytes 52
  228.1 9.7 %collective-permute-start.33 = (bf16[192,1152]{1,0:T(8,128)(2,1)S(1)}, bf16[192,1152]{1,0:T(8,128)(2,1)S(1)}, u32[]{:S(2)}, u32[]{:S(2)}) collective-permute-start(bf16[192,1152]{1,0:T(8,128)(2,1)S(1)} %get-tuple-element.233), channel_id=1, source_target_pairs={{0,2},{2,0},{1,3},{3,1},{4,6},{6,4},{5,7},{7,5},{8,10},{10,8},{9,1... | collective-permute-start | bytes 1327112 | tf_op jit(solution)/shard_map/ppermute | solution.py:721
  237.9 11.4 %collective-permute-start.34 = (bf16[2,192,1152]{2,1,0:T(8,128)(2,1)S(1)}, bf16[2,192,1152]{2,1,0:T(8,128)(2,1)S(1)}, u32[]{:S(2)}, u32[]{:S(2)}) collective-permute-start(bf16[2,192,1152]{2,1,0:T(8,128)(2,1)S(1)} %pad_maximum_fusion.3.here_ref), channel_id=1, source_target_pairs={{0,1},{1,0},{2,3},{3,2},{4,5},{5,4},{6,7},{7,6},{8,9},{9,8},{10,11... | collective-permute-start | bytes 2654216 | tf_op jit(solution)/shard_map/ppermute | solution.py:725
  238.0 2.5 collective-permute-start.30
  240.5 3.0 %collective-permute-start.31 = (f32[9,768]{1,0:T(8,128)S(1)}, f32[9,768]{1,0:T(8,128)S(1)}, u32[]{:S(2)}, u32[]{:S(2)}) collective-permute-start(f32[9,768]{1,0:T(8,128)S(1)} %add.109), channel_id=1, source_target_pairs={{0,4},{4,0},{8,12},{12,8},{1,5},{5,1},{9,13},{13,9},{2,6},{6,2},{1... | collective-permute-start | bytes 82952 | tf_op jit(solution)/shard_map/ppermute | solution.py:772
  243.5 3.9 %collective-permute-start.32 = (f32[9,768]{1,0:T(8,128)S(1)}, f32[9,768]{1,0:T(8,128)S(1)}, u32[]{:S(2)}, u32[]{:S(2)}) collective-permute-start(f32[9,768]{1,0:T(8,128)S(1)} %add.110), channel_id=1, source_target_pairs={{0,8},{4,12},{8,0},{12,4},{1,9},{5,13},{9,1},{13,5},{2,10},{6,14},... | collective-permute-start | bytes 82952 | tf_op jit(solution)/shard_map/ppermute | solution.py:772
  (24 other events, 66.5 us)
Sparse Core Ops, SparseCore 0:
  103.3 46.2 reduce-scatter.9
  156.8 18.2 reduce-scatter.7
  178.0 20.2 reduce-scatter.5

commit v11 on v10

--- a/solution.py
+++ b/solution.py
@@ -533,26 +533,25 @@
     )
 
 
-def weigh_kernel(flags, turned_ref, out_grad_ref, grad_ref, *out_refs):
-    last = grad_ref.shape[0]
-    for j, out_ref in enumerate(out_refs):
-        piece = 2 * (flags[2] ^ (j // 2)) + (flags[3] ^ (j % 2))
-
-        @pl.when(piece < last)
-        def _():
-            out_ref[...] = dot(turned_ref[...], grad_ref[jnp.minimum(piece, last - 1)]).astype(jnp.bfloat16)
-
-        @pl.when(piece == last)
-        def _():
-            out_ref[...] = out_grad_ref[...]
+def weigh_kernel(flags, turned_ref, out_grad_ref, query_ref, key_ref, value_ref, *out_refs):
+    rows = turned_ref[...]
+    fields = [dot(rows, ref[...]).astype(jnp.bfloat16) for ref in (query_ref, key_ref, value_ref)]
+    for piece, field in enumerate([*fields, out_grad_ref[...]]):
+        slot = 2 * (flags[2] ^ (piece // 2)) + (flags[3] ^ (piece % 2))
+        for j, out_ref in enumerate(out_refs):
+
+            @pl.when(slot == j)
+            def _():
+                out_ref[...] = field
 
 
 def weigh(flags, turned, grad, out_grad):
     width, columns = turned.shape[0], grad.shape[2]
     piece = ((width, columns), jnp.bfloat16, (ROWS, columns), lambda i, flags: (i, 0))
-    return streamed(
-        weigh_kernel, width // ROWS, [flags], [by_rows(turned, ROWS), by_rows(out_grad, ROWS), grad], [piece] * 4, [], 4
-    )
+    fields = [by_rows(turned, ROWS), by_rows(out_grad, ROWS)]
+    for c in range(3):
+        fields.append((grad, (None, *grad.shape[1:]), lambda i, flags, c=c: (c, 0, 0)))
+    return streamed(weigh_kernel, width // ROWS, [flags], fields, [piece] * 4, [], 4)
 
 
 def unproject_kernel(flags, grad_ref, rows_ref, w_own, w_near, w_far, keep_ref, first, second, sums_ref, weight):
@@ -880,7 +879,7 @@
         small = sum_over(small, name)
     attn_sum = add(*attn_moved)
     blocks = jnp.concatenate([attn_sum, jnp.where(same, early_sum, early_got), late_sum], axis=1)
-    here = jnp.stack([blocks, swap_far(blocks)])
+    here = after(jnp.stack([blocks, swap_far(blocks)]), small)
     output, grad_input = present(flags, dwa_weights, past_sum, ours, theirs)
     grad_w_qkv, grad_w_out, grad_w_up, grad_w_down = place(flags, here, swap_near(here))
 

time: 263 us -> 257 us (0.977); the launches traced: 258 us -> 256 us
  waiting for transfers between devices: 25.4 us -> 22 us
    ppermute x1, waiting for transfers between devices: 8.52 us -> 0.01 us  [swap_far(): return lax.ppermute(field, 'far', [(0, 1), (1, 0)])]
    ppermute x7, waiting for transfers between devices: 0.02 us -> 2.76 us  [swap_diagonal(): lax.ppermute(field, AXES, moves(away, lambda t, d, k, c: (c, d, k, t)))]
  transfers between devices with their start and end apart: 38 -> 38, of which waited for: 8 -> 9; matrix products, arithmetic and copies ran while one was open for 13% -> 13% of each run, Pallas kernels for 46% -> 47%
where the time goes in v11:
time: 257 us; the launch traced here: 256 us
  Pallas kernels  122 us (47%)
  starting transfers between devices  50.3 us (20%)
  other arithmetic  26.2 us (10%)
  waiting for transfers between devices  22 us (9%)
  local copies, waits for them, and re-layouts  19.9 us (8%)
  between operations  14.7 us (6%)
    pallas_call x10, Pallas kernels, streamed(): pl.pallas_call(kernel, grid_spec=pltpu.PrefetchScalarGridSpec(num_scalar_...  84.7 us
    ppermute x7, starting transfers between devices, swap_diagonal(): lax.ppermute(field, AXES, moves(away, lambda t, d, k, c: (c, d, k, t)))  23.2 us
    pallas_call x1, Pallas kernels, attend_back(): pl.pallas_call(functools.partial(attend_back_kernel, reach), grid=(width...  19.6 us
    unnamed x100, local copies, waits for them, and re-layouts  13.7 us
    pallas_call x1, Pallas kernels, attend(): pl.pallas_call(functools.partial(attend_kernel, reach), grid=(width // LA...  13.1 us
    ppermute x5, waiting for transfers between devices, sum_over(): lax.ppermute(field, name, [(d, d ^ bit) for d in range(size)])  12.3 us
    ppermute x8, starting transfers between devices, send_to_owner(): lax.ppermute(field, AXES, moves(away if not other_far and (not other_tp)...  10.7 us
    convert_element_type x3, other arithmetic, add(): sum((field.astype(jnp.float32) for field in fields)).astype(jnp.bfloat16)  6.11 us
  transfers between devices with their start and end apart: 38, of which 9 were waited for; matrix products, arithmetic and copies ran while one was open for 13% of the time, Pallas kernels for 47%

profile of v11, /device:TPU:9, one launch (start us, length us, event | category | flops | bytes accessed | tf_op | source)
XLA Modules:
  0.0 255.8 jit_solution(12003572322217448529)
XLA Ops:
  8.0 3.1 %collective-permute-start = (bf16[512,768]{1,0:T(8,128)(2,1)}, bf16[512,768]{1,0:T(8,128)(2,1)}, u32[]{:S(2)}, u32[]{:S(2)}) collective-permute-start(bf16[512,768]{1,0:T(8,128)(2,1)} %bitcast.45), channel_id=1, source_target_pairs={{1,16},{3,18},{5,20},{7,22},{9,24},{11,26},{13,28},{15,30},{16,1},... | collective-permute-start | bytes 2359304 | tf_op jit(solution)/shard_map/ppermute | solution.py:701
  11.1 2.2 constant_dynamic-slice_fusion
  13.2 2.6 %collective-permute-start.3 = (bf16[3,384,384]{2,1,0:T(8,128)(2,1)}, bf16[3,384,384]{2,1,0:T(8,128)(2,1)S(1)}, u32[]{:S(2)}, u32[]{:S(2)}) collective-permute-start(bf16[3,384,384]{2,1,0:T(8,128)(2,1)} %constant_dynamic-slice_fusion), channel_id=1, source_target_pairs={{1,16},{3,18},{5,20},{7,22},{9,24},{11,26},{13,28},{15,30},{16,1},... | collective-permute-start | bytes 2654216 | tf_op jit(solution)/shard_map/ppermute | solution.py:701
  16.0 2.5 pad_maximum_fusion.2
  18.5 1.9 fusion.10
  20.4 1.6 pad_maximum_fusion.1
  22.0 1.6 pad_maximum_fusion
  23.6 4.4 %shard_map.220 = (bf16[4,512,768]{2,1,0:T(8,128)(2,1)}, f32[512,768]{1,0:T(8,128)}, f32[8,768]{1,0:T(8,128)}) custom-call(f32[5]{0:T(128)} %weight_ref.1, bf16[4,512,768]{2,1,0:T(8,128)(2,1)} %bitcast.43, bf16[512,768]{1,0:T(8,128)(2,1)} %bitcast.41), custom_call_target="tpu_custom_call" | custom-call | bytes 9000000 | tf_op jit(solution)/shard_map/pallas_call | solution.py:631
  29.6 3.1 %collective-permute-start.5 = (bf16[896,768]{1,0:T(8,128)(2,1)S(1)}, bf16[896,768]{1,0:T(8,128)(2,1)}, u32[]{:S(2)}, u32[]{:S(2)}) collective-permute-start(bf16[896,768]{1,0:T(8,128)(2,1)S(1)} %copy-done.30), channel_id=1, source_target_pairs={{1,16},{3,18},{5,20},{7,22},{9,24},{11,26},{13,28},{15,30},{16,1},... | collective-permute-start | bytes 4128776 | tf_op jit(solution)/shard_map/ppermute | solution.py:701
  32.7 1.2 broadcast_select_fusion.1
  34.0 3.1 %collective-permute-start.4 = (bf16[3,384,384]{2,1,0:T(8,128)(2,1)S(1)}, bf16[3,384,384]{2,1,0:T(8,128)(2,1)S(1)}, u32[]{:S(2)}, u32[]{:S(2)}) collective-permute-start(bf16[3,384,384]{2,1,0:T(8,128)(2,1)S(1)} %collective-permute-done.3.w_near), channel_id=1, source_target_pairs={{1,3},{3,1},{5,7},{7,5},{9,11},{11,9},{13,15},{15,13},{16,18},{18,... | collective-permute-start | bytes 2654216 | tf_op jit(solution)/shard_map/ppermute | solution.py:716
  39.0 3.1 %fusion.1 = (f32[1024,128]{1,0:T(8,128)}, f32[1024,128]{1,0:T(8,128)}) fusion(f32[128]{0:T(128)S(1)} %get-tuple-element.239, f32[128]{0:T(128)S(1)} %get-tuple-element.240, f32[1024]{0:T(1024)S(1)} %subtract_convert_fusion), kind=kLoop, calls=%fused_computation.13 | loop fusion | flops 262144 | bytes 1053696 | tf_op jit(solution)/shard_map/mul | solution.py:816
  42.0 2.8 %collective-permute-start.8 = (bf16[1536,768]{1,0:T(8,128)(2,1)}, bf16[1536,768]{1,0:T(8,128)(2,1)}, u32[]{:S(2)}, u32[]{:S(2)}) collective-permute-start(bf16[1536,768]{1,0:T(8,128)(2,1)} %pad_maximum_fusion), channel_id=1, source_target_pairs={{1,16},{3,18},{5,20},{7,22},{9,24},{11,26},{13,28},{15,30},{16,1},... | collective-permute-start | bytes 7077896 | tf_op jit(solution)/shard_map/ppermute | solution.py:701
  44.8 1.9 maximum_select_fusion.rows_ref.refs_2_
  46.7 1.1 collective-permute-done.4.w_far
  47.8 0.9 copy-done.11
  48.7 9.0 %shard_map.221 = (bf16[3,1024,384]{2,1,0:T(8,128)(2,1)}, bf16[768,1024]{1,0:T(8,128)(2,1)}) custom-call(s32[4]{0:T(128)} %pad_add_fusion.flags.refs_0_, bf16[1024,768]{1,0:T(8,128)(2,1)} %maximum_select_fusion.rows_ref.refs_2_, f32[1024,128]{1,0:T(8,128)} %get-tuple-element.104.cos_ref, f32[1024,128]{1,0:T(8,128)} %get-tuple-element.105.sin_ref, ...), custom_call_target="tpu_custom_call" | custom-call | bytes 24000000 | tf_op jit(solution)/shard_map/pallas_call | solution.py:240
  57.7 13.1 %shard_map.222 = (bf16[1024,384]{1,0:T(8,128)(2,1)}, f32[3,8,1024]{2,1,0:T(8,128)}) custom-call(bf16[1024,128]{1,0:T(8,128)(2,1)} %select_convert_fusion.apart_ref, bf16[1024,128]{1,0:T(8,128)(2,1)} %fusion.2.member_ref, bf16[3,1024,384]{2,1,0:T(8,128)(2,1)} %get-tuple-element.107.q_ref.k_ref.v_ref, ...), custom_call_target="tpu_custom_call" | custom-call | bytes 36000000 | tf_op jit(solution)/shard_map/pallas_call | solution.py:104
  70.8 4.0 %collective-permute-start.9 = (bf16[1536,768]{1,0:T(8,128)(2,1)}, bf16[1536,768]{1,0:T(8,128)(2,1)}, u32[]{:S(2)}, u32[]{:S(2)}) collective-permute-start(bf16[1536,768]{1,0:T(8,128)(2,1)} %pad_maximum_fusion.1), channel_id=1, source_target_pairs={{1,16},{3,18},{5,20},{7,22},{9,24},{11,26},{13,28},{15,30},{16,1},... | collective-permute-start | bytes 7077896 | tf_op jit(solution)/shard_map/ppermute | solution.py:701
  74.8 1.7 broadcast_select_fusion.w_ref
  76.4 1.0 convolution_convert_fusion.refs_3_.own_ref
  78.1 3.9 %collective-permute-done.7.refs_6_ = bf16[512,768]{1,0:T(8,128)(2,1)S(1)} collective-permute-done((bf16[512,768]{1,0:T(8,128)(2,1)S(1)}, bf16[512,768]{1,0:T(8,128)(2,1)S(1)}, u32[]{:S(2)}, u32[]{:S(2)}) %collective-permute-start.7) | collective-permute-done | bytes 786464 | tf_op jit(solution)/shard_map/ppermute | solution.py:724
  82.9 1.2 copy-done.5
  84.1 19.0 %shard_map.223 = (bf16[1024,768]{1,0:T(8,128)(2,1)}, bf16[768,1024]{1,0:T(8,128)(2,1)}, bf16[1024,768]{1,0:T(8,128)(2,1)}, bf16[768,1024]{1,0:T(8,128)(2,1)}, bf...) custom-call(s32[4]{0:T(128)} %pad_add_fusion.flags.refs_0_, ...), custom_call_target="tpu_custom_call" | custom-call | bytes 51000000 | tf_op jit(solution)/shard_map/pallas_call | solution.py:240
  103.2 16.3 %shard_map.224 = (bf16[1024,768]{1,0:T(8,128)(2,1)}, bf16[1024,768]{1,0:T(8,128)(2,1)}, bf16[768,768]{1,0:T(8,128)(2,1)}, bf16[768,384]{1,0:T(8,128)(2,1)}, bf16...) custom-call(s32[4]{0:T(128)} %pad_add_fusion.flags.refs_0_, ...), custom_call_target="tpu_custom_call" | custom-call | bytes 51000000 | tf_op jit(solution)/shard_map/pallas_call | solution.py:240
  119.8 2.9 %collective-permute-start.13 = (bf16[768,384]{1,0:T(8,128)(2,1)}, bf16[768,384]{1,0:T(8,128)(2,1)S(1)}, u32[]{:S(2)}, u32[]{:S(2)}) collective-permute-start(bf16[768,384]{1,0:T(8,128)(2,1)} %get-tuple-element.124), channel_id=1, source_target_pairs={{0,2},{1,18},{2,0},{3,16},{4,6},{5,22},{6,4},{7,20},{8,10},{9,26},... | collective-permute-start | bytes 1769480 | tf_op jit(solution)/shard_map/ppermute | solution.py:705
  122.7 2.8 %collective-permute-start.11 = (bf16[768,384]{1,0:T(8,128)(2,1)}, bf16[768,384]{1,0:T(8,128)(2,1)S(1)}, u32[]{:S(2)}, u32[]{:S(2)}) collective-permute-start(bf16[768,384]{1,0:T(8,128)(2,1)} %get-tuple-element.122), channel_id=1, source_target_pairs={{1,16},{3,18},{5,20},{7,22},{9,24},{11,26},{13,28},{15,30},{16,1},... | collective-permute-start | bytes 1769480 | tf_op jit(solution)/shard_map/ppermute | solution.py:705
  125.5 1.2 copy-done.29
  126.7 10.2 %shard_map.225 = (bf16[1024,768]{1,0:T(8,128)(2,1)}, bf16[1024,384]{1,0:T(8,128)(2,1)}, bf16[768,384]{1,0:T(8,128)(2,1)}, f32[8,768]{1,0:T(8,128)}) custom-call(s32[4]{0:T(128)} %pad_add_fusion.flags.refs_0_, bf16[1024,768]{1,0:T(8,128)(2,1)} %maximum_select_fusion.rows_ref.refs_2_, bf16[1024,768]{1,0:T(8,128)(2,1)} %copy-done.3, ...), custom_call_target="tpu_custom_call" | custom-call | bytes 24000000 | tf_op jit(solution)/shard_map/pallas_call | solution.py:240
  137.0 19.6 %shard_map.226.query_ref.key_ref.value_ref.grad_ref = bf16[3,1024,384]{2,1,0:T(8,128)(2,1)} custom-call(bf16[1024,128]{1,0:T(8,128)(2,1)} %select_convert_fusion.apart_ref, bf16[1024,128]{1,0:T(8,128)(2,1)} %fusion.2.member_ref, f32[1024,128]{1,0:T(8,128)} %get-tuple-element.104.cos_ref, f32[1024,128]{1,0:T(8,128)} %get-tuple-element.105.sin_ref, ...), custom_call_target="tpu_custom_call" | custom-call | bytes 66000000 | tf_op jit(solution)/shard_map/pallas_call | solution.py:189
  156.8 7.1 %shard_map.227 = (bf16[768,384]{1,0:T(8,128)(2,1)}, bf16[768,384]{1,0:T(8,128)(2,1)}, bf16[768,384]{1,0:T(8,128)(2,1)}, bf16[768,384]{1,0:T(8,128)(2,1)}) custom-call(s32[4]{0:T(128)} %pad_add_fusion.flags.refs_0_, bf16[768,1024]{1,0:T(8,128)(2,1)} %get-tuple-element.127.turned_ref, bf16[768,384]{1,0:T(8,128)(2,1)} %get-tuple-element.128.out_grad_ref, ...), custom_call_target="tpu_custom_call" | custom-call | bytes 12000000 | tf_op jit(solution)/shard_map/pallas_call | solution.py:240
  163.9 3.2 %collective-permute-start.15 = (bf16[768,384]{1,0:T(8,128)(2,1)}, bf16[768,384]{1,0:T(8,128)(2,1)}, u32[]{:S(2)}, u32[]{:S(2)}) collective-permute-start(bf16[768,384]{1,0:T(8,128)(2,1)} %get-tuple-element.129), channel_id=1, source_target_pairs={{1,16},{3,18},{5,20},{7,22},{9,24},{11,26},{13,28},{15,30},{16,1},... | collective-permute-start | bytes 1769480 | tf_op jit(solution)/shard_map/ppermute | solution.py:705
  167.1 1.5 collective-permute-start.17
  168.9 3.0 %add_convert_fusion = bf16[768,384]{1,0:T(8,128)(2,1)} fusion(bf16[768,384]{1,0:T(8,128)(2,1)} %copy-done.36, bf16[768,384]{1,0:T(8,128)(2,1)} %copy-done.35, bf16[768,384]{1,0:T(8,128)(2,1)} %copy-done.34, bf16[768,384]{1,0:T(8,128)(2,1)} %get-tuple-element.122, bf16[768,384]{1,0:T(8,128)(2,1)} %copy-done.37, pred[]{:T(512)S(6)} %eq.35), kind=kLoop, calls=%fused_computation.6 | loop fusion | flops 2654208 | bytes 3538945 | tf_op jit(solution)/shard_map/convert_element_type | solution.py:743
  172.8 1.7 copy-done.1
  174.4 1.2 copy-done.10
  175.6 1.2 copy-done.12
  176.8 6.2 %shard_map.228 = (f32[512,768]{1,0:T(8,128)S(1)}, bf16[256,768]{1,0:T(8,128)(2,1)}, bf16[256,768]{1,0:T(8,128)(2,1)}, f32[8,768]{1,0:T(8,128)S(1)}) custom-call(s32[4]{0:T(128)S(1)} %copy-done.20, bf16[3,1024,384]{2,1,0:T(8,128)(2,1)S(1)} %copy-done.1, bf16[1024,768]{1,0:T(8,128)(2,1)S(1)} %copy-done, bf16[3,768,384]{2,1,0:T(8,128)(2,1)S(1)} %copy-done.7, ...), custom_call_target="tpu_custom_call" | custom-call | bytes 15000000 | tf_op jit(solution)/shard_map/pallas_call | solution.py:240
  183.0 1.2 copy-done.14
  184.2 1.4 copy-done.17
  185.6 1.3 copy-done.19
  186.9 6.9 %shard_map.229 = (f32[512,768]{1,0:T(8,128)S(1)}, bf16[256,768]{1,0:T(8,128)(2,1)S(1)}, bf16[256,768]{1,0:T(8,128)(2,1)S(1)}, f32[8,768]{1,0:T(8,128)S(1)}) custom-call(s32[4]{0:T(128)S(1)} %copy-done.20, bf16[1024,768]{1,0:T(8,128)(2,1)S(1)} %copy-done.16, bf16[1024,768]{1,0:T(8,128)(2,1)S(1)} %copy-done.17, bf16[1024,768]{1,0:T(8,128)(2,1)S(1)} %copy-done, ...), custom_call_target="tpu_custom_call" | custom-call | bytes 18000000 | tf_op jit(solution)/shard_map/pallas_call | solution.py:240
  193.9 1.9 collective-permute-done.18
  196.8 2.0 add_convert_fusion.1
  199.8 2.2 collective-permute-start.28
  202.0 2.2 collective-permute-start.27
  204.2 3.4 %collective-permute-start.26 = (bf16[192,384]{1,0:T(8,128)(2,1)}, bf16[192,384]{1,0:T(8,128)(2,1)S(1)}, u32[]{:S(2)}, u32[]{:S(2)}) collective-permute-start(bf16[192,384]{1,0:T(8,128)(2,1)} %reduce-scatter.8.cloned.1.call-done), channel_id=1, source_target_pairs={{1,16},{3,18},{5,20},{7,22},{9,24},{11,26},{13,28},{15,30},{16,1},... | collective-permute-start | bytes 442376 | tf_op jit(solution)/shard_map/ppermute | solution.py:701
  208.4 5.4 %shard_map.230.own_ref = bf16[2,512,768]{2,1,0:T(8,128)(2,1)} custom-call(s32[4]{0:T(128)} %pad_add_fusion.flags.refs_0_, bf16[1024,768]{1,0:T(8,128)(2,1)} %maximum_select_fusion.rows_ref.refs_2_, bf16[1024,768]{1,0:T(8,128)(2,1)} %get-tuple-element.119.resid_ref, f32[512,768]{1,0:T(8,128)} %copy-done.14, f32[512,768]{1,0:T(8,128)} %copy-done.15, ...), custom_call_target="tpu_custom_call" | custom-call | bytes 9000000 | tf_op jit(solution)/shard_map/pallas_call | solution.py:240
  213.8 2.9 %collective-permute-done.24 = f32[9,768]{1,0:T(8,128)S(1)} collective-permute-done((f32[9,768]{1,0:T(8,128)S(1)}, f32[9,768]{1,0:T(8,128)S(1)}, u32[]{:S(2)}, u32[]{:S(2)}) %collective-permute-start.24) | collective-permute-done | bytes 27680 | tf_op jit(solution)/shard_map/ppermute | solution.py:771
  216.8 1.4 collective-permute-start.25
  218.2 2.0 collective-permute-done.25
  220.2 4.3 %collective-permute-start.23 = (bf16[2,512,768]{2,1,0:T(8,128)(2,1)}, bf16[2,512,768]{2,1,0:T(8,128)(2,1)S(1)}, u32[]{:S(2)}, u32[]{:S(2)}) collective-permute-start(bf16[2,512,768]{2,1,0:T(8,128)(2,1)} %shard_map.230.own_ref), channel_id=1, source_target_pairs={{1,16},{3,18},{5,20},{7,22},{9,24},{11,26},{13,28},{15,30},{16,1},... | collective-permute-start | bytes 4718600 | tf_op jit(solution)/shard_map/ppermute | solution.py:701
  225.2 1.1 add_convert_fusion.2
  226.4 1.1 fusion.9
  227.5 1.2 collective-permute-start.33
  228.7 1.2 collective-permute-done.30
  230.0 3.2 %collective-permute-done.31 = f32[9,768]{1,0:T(8,128)S(1)} collective-permute-done((f32[9,768]{1,0:T(8,128)S(1)}, f32[9,768]{1,0:T(8,128)S(1)}, u32[]{:S(2)}, u32[]{:S(2)}) %collective-permute-start.31) | collective-permute-done | bytes 27680 | tf_op jit(solution)/shard_map/ppermute | solution.py:771
  233.3 1.0 collective-permute-start.32
  234.3 2.9 %collective-permute-done.32 = f32[9,768]{1,0:T(8,128)S(1)} collective-permute-done((f32[9,768]{1,0:T(8,128)S(1)}, f32[9,768]{1,0:T(8,128)S(1)}, u32[]{:S(2)}, u32[]{:S(2)}) %collective-permute-start.32) | collective-permute-done | bytes 27680 | tf_op jit(solution)/shard_map/ppermute | solution.py:771
  237.3 2.1 collective-permute-start.34
  240.0 2.7 %collective-permute-done.23.got_ref = bf16[2,512,768]{2,1,0:T(8,128)(2,1)S(1)} collective-permute-done((bf16[2,512,768]{2,1,0:T(8,128)(2,1)}, bf16[2,512,768]{2,1,0:T(8,128)(2,1)S(1)}, u32[]{:S(2)}, u32[]{:S(2)}) %collective-permute-start.23) | collective-permute-done | bytes 1572896 | tf_op jit(solution)/shard_map/ppermute | solution.py:701
  242.8 2.1 shard_map.231
  244.9 1.3 slice_reduce_fusion
  246.8 2.5 shard_map.232
  (176 shorter events, 12.4 us)
Async XLA Ops:
  7.2 8.7 %copy-start.45 = (f32[768]{0:T(1024)S(1)}, f32[768]{0:T(1024)}, u32[]{:S(2)}) copy-start(f32[768]{0:T(1024)} %param.18) | copy-start | bytes 9220
  7.2 8.8 %copy-start.46 = (f32[768]{0:T(1024)S(1)}, f32[768]{0:T(1024)}, u32[]{:S(2)}) copy-start(f32[768]{0:T(1024)} %param.19) | copy-start | bytes 9220
  7.2 8.8 %copy-start.47 = (f32[768]{0:T(1024)S(1)}, f32[768]{0:T(1024)}, u32[]{:S(2)}) copy-start(f32[768]{0:T(1024)} %param.22) | copy-start | bytes 9220
  7.2 8.8 %copy-start.48 = (f32[768]{0:T(1024)S(1)}, f32[768]{0:T(1024)}, u32[]{:S(2)}) copy-start(f32[768]{0:T(1024)} %param.23) | copy-start | bytes 9220
  7.2 149.5 %reduce-scatter.10.cloned.1.call-start = ((), (), s32[]{:S(2)}) async-start(), calls=%async_computation.5 | async-start | bytes 2949120
  7.3 21.9 %collective-permute-start.2 = (s32[1,3]{1,0:T(1,128)}, s32[1,3]{1,0:T(1,128)S(1)}, u32[]{:S(2)}, u32[]{:S(2)}) collective-permute-start(s32[1,3]{1,0:T(1,128)} %param.16), channel_id=1, source_target_pairs={{0,1},{1,0},{2,3},{3,2},{4,5},{5,4},{6,7},{7,6},{8,9},{9,8},{10,11... | collective-permute-start | bytes 44 | tf_op jit(solution)/shard_map/ppermute | solution.py:724
  8.0 21.6 %collective-permute-start = (bf16[512,768]{1,0:T(8,128)(2,1)}, bf16[512,768]{1,0:T(8,128)(2,1)}, u32[]{:S(2)}, u32[]{:S(2)}) collective-permute-start(bf16[512,768]{1,0:T(8,128)(2,1)} %bitcast.45), channel_id=1, source_target_pairs={{1,16},{3,18},{5,20},{7,22},{9,24},{11,26},{13,28},{15,30},{16,1},... | collective-permute-start | bytes 2359304 | tf_op jit(solution)/shard_map/ppermute | solution.py:701
  13.2 20.7 %collective-permute-start.3 = (bf16[3,384,384]{2,1,0:T(8,128)(2,1)}, bf16[3,384,384]{2,1,0:T(8,128)(2,1)S(1)}, u32[]{:S(2)}, u32[]{:S(2)}) collective-permute-start(bf16[3,384,384]{2,1,0:T(8,128)(2,1)} %constant_dynamic-slice_fusion), channel_id=1, source_target_pairs={{1,16},{3,18},{5,20},{7,22},{9,24},{11,26},{13,28},{15,30},{16,1},... | collective-permute-start | bytes 2654216 | tf_op jit(solution)/shard_map/ppermute | solution.py:701
  23.6 6.0 %copy-start.30 = (bf16[896,768]{1,0:T(8,128)(2,1)S(1)}, bf16[896,768]{1,0:T(8,128)(2,1)}, u32[]{:S(2)}) copy-start(bf16[896,768]{1,0:T(8,128)(2,1)} %pad_maximum_fusion.2) | copy-start | bytes 4128772
  23.6 9.1 %copy-start.31 = (bf16[1,512,768]{2,1,0:T(8,128)(2,1)S(1)}, bf16[1,512,768]{2,1,0:T(8,128)(2,1)}, u32[]{:S(2)}) copy-start(bf16[1,512,768]{2,1,0:T(8,128)(2,1)} %param.13) | copy-start | bytes 2359300
  29.6 45.1 %collective-permute-start.5 = (bf16[896,768]{1,0:T(8,128)(2,1)S(1)}, bf16[896,768]{1,0:T(8,128)(2,1)}, u32[]{:S(2)}, u32[]{:S(2)}) collective-permute-start(bf16[896,768]{1,0:T(8,128)(2,1)S(1)} %copy-done.30), channel_id=1, source_target_pairs={{1,16},{3,18},{5,20},{7,22},{9,24},{11,26},{13,28},{15,30},{16,1},... | collective-permute-start | bytes 4128776 | tf_op jit(solution)/shard_map/ppermute | solution.py:701
  33.9 10.9 %collective-permute-start.1 = (bf16[512,768]{1,0:T(8,128)(2,1)S(1)}, bf16[512,768]{1,0:T(8,128)(2,1)S(1)}, u32[]{:S(2)}, u32[]{:S(2)}) collective-permute-start(bf16[512,768]{1,0:T(8,128)(2,1)S(1)} %broadcast_select_fusion.1), channel_id=1, source_target_pairs={{0,1},{1,0},{2,3},{3,2},{4,5},{5,4},{6,7},{7,6},{8,9},{9,8},{10,11... | collective-permute-start | bytes 2359304 | tf_op jit(solution)/shard_map/ppermute | solution.py:724
  34.0 12.7 %copy-start.9 = (bf16[3,384,384]{2,1,0:T(8,128)(2,1)}, bf16[3,384,384]{2,1,0:T(8,128)(2,1)S(1)}, u32[]{:S(2)}) copy-start(bf16[3,384,384]{2,1,0:T(8,128)(2,1)S(1)} %collective-permute-done.3.w_near) | copy-start | bytes 2654212
  34.0 13.8 %collective-permute-start.4 = (bf16[3,384,384]{2,1,0:T(8,128)(2,1)S(1)}, bf16[3,384,384]{2,1,0:T(8,128)(2,1)S(1)}, u32[]{:S(2)}, u32[]{:S(2)}) collective-permute-start(bf16[3,384,384]{2,1,0:T(8,128)(2,1)S(1)} %collective-permute-done.3.w_near), channel_id=1, source_target_pairs={{1,3},{3,1},{5,7},{7,5},{9,11},{11,9},{13,15},{15,13},{16,18},{18,... | collective-permute-start | bytes 2654216 | tf_op jit(solution)/shard_map/ppermute | solution.py:716
  42.0 40.9 %collective-permute-start.8 = (bf16[1536,768]{1,0:T(8,128)(2,1)}, bf16[1536,768]{1,0:T(8,128)(2,1)}, u32[]{:S(2)}, u32[]{:S(2)}) collective-permute-start(bf16[1536,768]{1,0:T(8,128)(2,1)} %pad_maximum_fusion), channel_id=1, source_target_pairs={{1,16},{3,18},{5,20},{7,22},{9,24},{11,26},{13,28},{15,30},{16,1},... | collective-permute-start | bytes 7077896 | tf_op jit(solution)/shard_map/ppermute | solution.py:701
  57.7 17.1 %copy-start.25 = (bf16[1,512,768]{2,1,0:T(8,128)(2,1)S(1)}, bf16[1,512,768]{2,1,0:T(8,128)(2,1)}, u32[]{:S(2)}) copy-start(bf16[1,512,768]{2,1,0:T(8,128)(2,1)} %param.15) | copy-start | bytes 2359300
  57.7 17.1 %copy-start.28 = (bf16[384,768]{1,0:T(8,128)(2,1)S(1)}, bf16[384,768]{1,0:T(8,128)(2,1)}, u32[]{:S(2)}) copy-start(bf16[384,768]{1,0:T(8,128)(2,1)} %param.21) | copy-start | bytes 1769476
  70.8 32.4 %collective-permute-start.9 = (bf16[1536,768]{1,0:T(8,128)(2,1)}, bf16[1536,768]{1,0:T(8,128)(2,1)}, u32[]{:S(2)}, u32[]{:S(2)}) collective-permute-start(bf16[1536,768]{1,0:T(8,128)(2,1)} %pad_maximum_fusion.1), channel_id=1, source_target_pairs={{1,16},{3,18},{5,20},{7,22},{9,24},{11,26},{13,28},{15,30},{16,1},... | collective-permute-start | bytes 7077896 | tf_op jit(solution)/shard_map/ppermute | solution.py:701
  77.4 5.5 %collective-permute-start.6 = (bf16[1024,768]{1,0:T(8,128)(2,1)S(1)}, bf16[1024,768]{1,0:T(8,128)(2,1)S(1)}, u32[]{:S(2)}, u32[]{:S(2)}) collective-permute-start(bf16[1024,768]{1,0:T(8,128)(2,1)S(1)} %convolution_convert_fusion.refs_3_.own_ref), channel_id=1, source_target_pairs={{0,1},{1,0},{2,3},{3,2},{4,5},{5,4},{6,7},{7,6},{8,9},{9,8},{10,11... | collective-permute-start | bytes 4718600 | tf_op jit(solution)/shard_map/ppermute | solution.py:724
  77.6 4.4 %collective-permute-start.7 = (bf16[512,768]{1,0:T(8,128)(2,1)S(1)}, bf16[512,768]{1,0:T(8,128)(2,1)S(1)}, u32[]{:S(2)}, u32[]{:S(2)}) collective-permute-start(bf16[512,768]{1,0:T(8,128)(2,1)S(1)} %slice.53.refs_5_), channel_id=1, source_target_pairs={{0,1},{1,0},{2,3},{3,2},{4,5},{5,4},{6,7},{7,6},{8,9},{9,8},{10,11... | collective-permute-start | bytes 2359304 | tf_op jit(solution)/shard_map/ppermute | solution.py:724
  103.2 96.6 %reduce-scatter.8.cloned.1.call-start = ((), (), s32[]{:S(2)}) async-start(), calls=%async_computation.4 | async-start | bytes 737280 | tf_op jit(solution)/shard_map/reduce_scatter | solution.py:751
  119.5 5.9 %collective-permute-start.10 = (bf16[1024,768]{1,0:T(8,128)(2,1)}, bf16[1024,768]{1,0:T(8,128)(2,1)S(1)}, u32[]{:S(2)}, u32[]{:S(2)}) collective-permute-start(bf16[1024,768]{1,0:T(8,128)(2,1)} %get-tuple-element.118.back_own), channel_id=1, source_target_pairs={{0,1},{1,0},{2,3},{3,2},{4,5},{5,4},{6,7},{7,6},{8,9},{9,8},{10,11... | collective-permute-start | bytes 4718600 | tf_op jit(solution)/shard_map/ppermute | solution.py:724
  119.7 36.8 %collective-permute-start.12 = (bf16[768,384]{1,0:T(8,128)(2,1)}, bf16[768,384]{1,0:T(8,128)(2,1)S(1)}, u32[]{:S(2)}, u32[]{:S(2)}) collective-permute-start(bf16[768,384]{1,0:T(8,128)(2,1)} %get-tuple-element.123), channel_id=1, source_target_pairs={{0,1},{1,17},{2,3},{3,19},{4,5},{5,21},{6,7},{7,23},{8,9},{9,25},{... | collective-permute-start | bytes 1769480 | tf_op jit(solution)/shard_map/ppermute | solution.py:705
  119.8 36.9 %collective-permute-start.13 = (bf16[768,384]{1,0:T(8,128)(2,1)}, bf16[768,384]{1,0:T(8,128)(2,1)S(1)}, u32[]{:S(2)}, u32[]{:S(2)}) collective-permute-start(bf16[768,384]{1,0:T(8,128)(2,1)} %get-tuple-element.124), channel_id=1, source_target_pairs={{0,2},{1,18},{2,0},{3,16},{4,6},{5,22},{6,4},{7,20},{8,10},{9,26},... | collective-permute-start | bytes 1769480 | tf_op jit(solution)/shard_map/ppermute | solution.py:705
  122.7 34.0 %collective-permute-start.14 = (bf16[768,384]{1,0:T(8,128)(2,1)}, bf16[768,384]{1,0:T(8,128)(2,1)S(1)}, u32[]{:S(2)}, u32[]{:S(2)}) collective-permute-start(bf16[768,384]{1,0:T(8,128)(2,1)} %get-tuple-element.125), channel_id=1, source_target_pairs={{0,3},{1,19},{2,1},{3,17},{4,7},{5,23},{6,5},{7,21},{8,11},{9,27},... | collective-permute-start | bytes 1769480 | tf_op jit(solution)/shard_map/ppermute | solution.py:705
  122.7 34.0 %collective-permute-start.11 = (bf16[768,384]{1,0:T(8,128)(2,1)}, bf16[768,384]{1,0:T(8,128)(2,1)S(1)}, u32[]{:S(2)}, u32[]{:S(2)}) collective-permute-start(bf16[768,384]{1,0:T(8,128)(2,1)} %get-tuple-element.122), channel_id=1, source_target_pairs={{1,16},{3,18},{5,20},{7,22},{9,24},{11,26},{13,28},{15,30},{16,1},... | collective-permute-start | bytes 1769480 | tf_op jit(solution)/shard_map/ppermute | solution.py:705
  156.6 7.2 %copy-start.34 = (bf16[768,384]{1,0:T(8,128)(2,1)}, bf16[768,384]{1,0:T(8,128)(2,1)S(1)}, u32[]{:S(2)}) copy-start(bf16[768,384]{1,0:T(8,128)(2,1)S(1)} %collective-permute-done.12) | copy-start | bytes 1769476
  156.6 7.2 %copy-start.35 = (bf16[768,384]{1,0:T(8,128)(2,1)}, bf16[768,384]{1,0:T(8,128)(2,1)S(1)}, u32[]{:S(2)}) copy-start(bf16[768,384]{1,0:T(8,128)(2,1)S(1)} %collective-permute-done.13) | copy-start | bytes 1769476
  156.6 7.2 %copy-start.36 = (bf16[768,384]{1,0:T(8,128)(2,1)}, bf16[768,384]{1,0:T(8,128)(2,1)S(1)}, u32[]{:S(2)}) copy-start(bf16[768,384]{1,0:T(8,128)(2,1)S(1)} %collective-permute-done.14) | copy-start | bytes 1769476
  156.7 7.2 %copy-start.37 = (bf16[768,384]{1,0:T(8,128)(2,1)}, bf16[768,384]{1,0:T(8,128)(2,1)S(1)}, u32[]{:S(2)}) copy-start(bf16[768,384]{1,0:T(8,128)(2,1)S(1)} %collective-permute-done.11) | copy-start | bytes 1769476
  156.7 68.5 %reduce-scatter.6.cloned.1.call-start = ((), (), s32[]{:S(2)}) async-start(), calls=%async_computation.3 | async-start | bytes 737280 | tf_op jit(solution)/shard_map/reduce_scatter | solution.py:751
  163.9 31.9 %collective-permute-start.15 = (bf16[768,384]{1,0:T(8,128)(2,1)}, bf16[768,384]{1,0:T(8,128)(2,1)}, u32[]{:S(2)}, u32[]{:S(2)}) collective-permute-start(bf16[768,384]{1,0:T(8,128)(2,1)} %get-tuple-element.129), channel_id=1, source_target_pairs={{1,16},{3,18},{5,20},{7,22},{9,24},{11,26},{13,28},{15,30},{16,1},... | collective-permute-start | bytes 1769480 | tf_op jit(solution)/shard_map/ppermute | solution.py:705
  167.0 26.9 %collective-permute-start.16 = (bf16[768,384]{1,0:T(8,128)(2,1)}, bf16[768,384]{1,0:T(8,128)(2,1)}, u32[]{:S(2)}, u32[]{:S(2)}) collective-permute-start(bf16[768,384]{1,0:T(8,128)(2,1)} %get-tuple-element.142), channel_id=1, source_target_pairs={{0,1},{1,17},{2,3},{3,19},{4,5},{5,21},{6,7},{7,23},{8,9},{9,25},{... | collective-permute-start | bytes 1769480 | tf_op jit(solution)/shard_map/ppermute | solution.py:705
  167.1 26.8 %collective-permute-start.17 = (bf16[768,384]{1,0:T(8,128)(2,1)}, bf16[768,384]{1,0:T(8,128)(2,1)}, u32[]{:S(2)}, u32[]{:S(2)}) collective-permute-start(bf16[768,384]{1,0:T(8,128)(2,1)} %get-tuple-element.143), channel_id=1, source_target_pairs={{0,2},{1,18},{2,0},{3,16},{4,6},{5,22},{6,4},{7,20},{8,10},{9,26},... | collective-permute-start | bytes 1769480 | tf_op jit(solution)/shard_map/ppermute | solution.py:705
  168.6 27.2 %collective-permute-start.18 = (bf16[768,384]{1,0:T(8,128)(2,1)}, bf16[768,384]{1,0:T(8,128)(2,1)}, u32[]{:S(2)}, u32[]{:S(2)}) collective-permute-start(bf16[768,384]{1,0:T(8,128)(2,1)} %get-tuple-element.144), channel_id=1, source_target_pairs={{0,3},{1,19},{2,1},{3,17},{4,7},{5,23},{6,5},{7,21},{8,11},{9,27},... | collective-permute-start | bytes 1769480 | tf_op jit(solution)/shard_map/ppermute | solution.py:705
  176.8 7.4 %copy-start.2 = (bf16[1024,768]{1,0:T(8,128)(2,1)S(1)}, bf16[1024,768]{1,0:T(8,128)(2,1)}, u32[]{:S(2)}) copy-start(bf16[1024,768]{1,0:T(8,128)(2,1)} %get-tuple-element.134.refs_3_.cot_ref) | copy-start | bytes 4718596
  176.8 7.4 %copy-start.4 = (bf16[1024,768]{1,0:T(8,128)(2,1)S(1)}, bf16[1024,768]{1,0:T(8,128)(2,1)}, u32[]{:S(2)}) copy-start(bf16[1024,768]{1,0:T(8,128)(2,1)} %copy-done.3) | copy-start | bytes 4718596
  176.8 7.4 %copy-start.6 = (bf16[1024,768]{1,0:T(8,128)(2,1)S(1)}, bf16[1024,768]{1,0:T(8,128)(2,1)}, u32[]{:S(2)}) copy-start(bf16[1024,768]{1,0:T(8,128)(2,1)} %copy-done.5) | copy-start | bytes 4718596
  176.8 7.4 %copy-start.16 = (bf16[1024,768]{1,0:T(8,128)(2,1)S(1)}, bf16[1024,768]{1,0:T(8,128)(2,1)}, u32[]{:S(2)}) copy-start(bf16[1024,768]{1,0:T(8,128)(2,1)} %get-tuple-element.132.act_early) | copy-start | bytes 4718596
  176.8 7.4 %copy-start.18 = (bf16[768,768]{1,0:T(8,128)(2,1)S(1)}, bf16[768,768]{1,0:T(8,128)(2,1)}, u32[]{:S(2)}) copy-start(bf16[768,768]{1,0:T(8,128)(2,1)} %get-tuple-element.135.early_ref) | copy-start | bytes 3538948
  186.9 9.9 %copy-start.33 = (bf16[768,384]{1,0:T(8,128)(2,1)S(1)}, bf16[768,384]{1,0:T(8,128)(2,1)}, u32[]{:S(2)}) copy-start(bf16[768,384]{1,0:T(8,128)(2,1)} %get-tuple-element.129) | copy-start | bytes 1769476
  195.8 4.0 %collective-permute-start.19 = (bf16[256,768]{1,0:T(8,128)(2,1)}, bf16[256,768]{1,0:T(8,128)(2,1)S(1)}, u32[]{:S(2)}, u32[]{:S(2)}) collective-permute-start(bf16[256,768]{1,0:T(8,128)(2,1)} %get-tuple-element.152), channel_id=1, source_target_pairs={{0,1},{1,0},{2,3},{3,2},{4,5},{5,4},{6,7},{7,6},{8,9},{9,8},{10,11... | collective-permute-start | bytes 1179656 | tf_op jit(solution)/shard_map/ppermute | solution.py:724
  196.1 5.9 %collective-permute-start.20 = (bf16[256,768]{1,0:T(8,128)(2,1)}, bf16[256,768]{1,0:T(8,128)(2,1)S(1)}, u32[]{:S(2)}, u32[]{:S(2)}) collective-permute-start(bf16[256,768]{1,0:T(8,128)(2,1)} %get-tuple-element.153), channel_id=1, source_target_pairs={{0,1},{1,0},{2,3},{3,2},{4,5},{5,4},{6,7},{7,6},{8,9},{9,8},{10,11... | collective-permute-start | bytes 1179656 | tf_op jit(solution)/shard_map/ppermute | solution.py:724
  196.3 7.9 %collective-permute-start.21 = (bf16[256,768]{1,0:T(8,128)(2,1)S(1)}, bf16[256,768]{1,0:T(8,128)(2,1)S(1)}, u32[]{:S(2)}, u32[]{:S(2)}) collective-permute-start(bf16[256,768]{1,0:T(8,128)(2,1)S(1)} %get-tuple-element.154), channel_id=1, source_target_pairs={{0,1},{1,0},{2,3},{3,2},{4,5},{5,4},{6,7},{7,6},{8,9},{9,8},{10,11... | collective-permute-start | bytes 1179656 | tf_op jit(solution)/shard_map/ppermute | solution.py:724
  196.6 11.1 %collective-permute-start.22 = (bf16[256,768]{1,0:T(8,128)(2,1)S(1)}, bf16[256,768]{1,0:T(8,128)(2,1)S(1)}, u32[]{:S(2)}, u32[]{:S(2)}) collective-permute-start(bf16[256,768]{1,0:T(8,128)(2,1)S(1)} %get-tuple-element.155), channel_id=1, source_target_pairs={{0,1},{1,0},{2,3},{3,2},{4,5},{5,4},{6,7},{7,6},{8,9},{9,8},{10,11... | collective-permute-start | bytes 1179656 | tf_op jit(solution)/shard_map/ppermute | solution.py:724
  199.5 25.0 %collective-permute-start.29 = (bf16[192,384]{1,0:T(8,128)(2,1)}, bf16[192,384]{1,0:T(8,128)(2,1)}, u32[]{:S(2)}, u32[]{:S(2)}) collective-permute-start(bf16[192,384]{1,0:T(8,128)(2,1)} %get-tuple-element.230), channel_id=1, source_target_pairs={{0,12},{4,0},{8,4},{12,8},{1,13},{5,1},{9,5},{13,9},{2,14},{6,2},{... | collective-permute-start | bytes 442376 | tf_op jit(solution)/shard_map/ppermute | solution.py:763
  199.8 7.9 %copy-start.38 = (bf16[256,768]{1,0:T(8,128)(2,1)}, bf16[256,768]{1,0:T(8,128)(2,1)S(1)}, u32[]{:S(2)}) copy-start(bf16[256,768]{1,0:T(8,128)(2,1)S(1)} %collective-permute-done.19.got_first) | copy-start | bytes 1179652
  199.8 24.7 %collective-permute-start.28 = (bf16[192,384]{1,0:T(8,128)(2,1)S(1)}, bf16[192,384]{1,0:T(8,128)(2,1)S(1)}, u32[]{:S(2)}, u32[]{:S(2)}) collective-permute-start(bf16[192,384]{1,0:T(8,128)(2,1)S(1)} %get-tuple-element.231), channel_id=1, source_target_pairs={{0,8},{4,12},{8,0},{12,4},{1,9},{5,13},{9,1},{13,5},{2,10},{6,14},... | collective-permute-start | bytes 442376 | tf_op jit(solution)/shard_map/ppermute | solution.py:763
  202.0 5.7 %copy-start.39 = (bf16[256,768]{1,0:T(8,128)(2,1)}, bf16[256,768]{1,0:T(8,128)(2,1)S(1)}, u32[]{:S(2)}) copy-start(bf16[256,768]{1,0:T(8,128)(2,1)S(1)} %collective-permute-done.20.got_second) | copy-start | bytes 1179652
  202.0 23.2 %collective-permute-start.27 = (bf16[192,384]{1,0:T(8,128)(2,1)S(1)}, bf16[192,384]{1,0:T(8,128)(2,1)}, u32[]{:S(2)}, u32[]{:S(2)}) collective-permute-start(bf16[192,384]{1,0:T(8,128)(2,1)S(1)} %get-tuple-element.232), channel_id=1, source_target_pairs={{0,4},{4,8},{8,12},{12,0},{1,5},{5,9},{9,13},{13,1},{2,6},{6,10},{... | collective-permute-start | bytes 442376 | tf_op jit(solution)/shard_map/ppermute | solution.py:763
  204.2 21.0 %collective-permute-start.26 = (bf16[192,384]{1,0:T(8,128)(2,1)}, bf16[192,384]{1,0:T(8,128)(2,1)S(1)}, u32[]{:S(2)}, u32[]{:S(2)}) collective-permute-start(bf16[192,384]{1,0:T(8,128)(2,1)} %reduce-scatter.8.cloned.1.call-done), channel_id=1, source_target_pairs={{1,16},{3,18},{5,20},{7,22},{9,24},{11,26},{13,28},{15,30},{16,1},... | collective-permute-start | bytes 442376 | tf_op jit(solution)/shard_map/ppermute | solution.py:701
  208.4 16.8 %copy-start.42 = (bf16[192,384]{1,0:T(8,128)(2,1)S(1)}, bf16[192,384]{1,0:T(8,128)(2,1)}, u32[]{:S(2)}) copy-start(bf16[192,384]{1,0:T(8,128)(2,1)} %reduce-scatter.8.cloned.1.call-done) | copy-start | bytes 442372
  213.8 2.9 %collective-permute-start.24 = (f32[9,768]{1,0:T(8,128)S(1)}, f32[9,768]{1,0:T(8,128)S(1)}, u32[]{:S(2)}, u32[]{:S(2)}) collective-permute-start(f32[9,768]{1,0:T(8,128)S(1)} %pad_maximum_fusion.5), channel_id=1, source_target_pairs={{0,16},{16,0},{1,17},{17,1},{2,18},{18,2},{3,19},{19,3},{4,20},{20... | collective-permute-start | bytes 82952 | tf_op jit(solution)/shard_map/ppermute | solution.py:771
  216.8 3.4 %collective-permute-start.25 = (f32[9,768]{1,0:T(8,128)S(1)}, f32[9,768]{1,0:T(8,128)S(1)}, u32[]{:S(2)}, u32[]{:S(2)}) collective-permute-start(f32[9,768]{1,0:T(8,128)S(1)} %add.97), channel_id=1, source_target_pairs={{0,2},{2,0},{1,3},{3,1},{4,6},{6,4},{5,7},{7,5},{8,10},{10,8},{9,1... | collective-permute-start | bytes 82952 | tf_op jit(solution)/shard_map/ppermute | solution.py:771
  220.2 22.6 %collective-permute-start.23 = (bf16[2,512,768]{2,1,0:T(8,128)(2,1)}, bf16[2,512,768]{2,1,0:T(8,128)(2,1)S(1)}, u32[]{:S(2)}, u32[]{:S(2)}) collective-permute-start(bf16[2,512,768]{2,1,0:T(8,128)(2,1)} %shard_map.230.own_ref), channel_id=1, source_target_pairs={{1,16},{3,18},{5,20},{7,22},{9,24},{11,26},{13,28},{15,30},{16,1},... | collective-permute-start | bytes 4718600 | tf_op jit(solution)/shard_map/ppermute | solution.py:701
  226.4 13.1 %copy-start.22 = (f32[5]{0:T(128)S(1)}, f32[5]{0:T(128)}, u32[]{:S(2)}) copy-start(f32[5]{0:T(128)} %weight_ref.1) | copy-start | bytes 64
  226.4 16.4 %copy-start.8 = (bf16[2,512,768]{2,1,0:T(8,128)(2,1)S(1)}, bf16[2,512,768]{2,1,0:T(8,128)(2,1)}, u32[]{:S(2)}) copy-start(bf16[2,512,768]{2,1,0:T(8,128)(2,1)} %shard_map.230.own_ref) | copy-start | bytes 4718596
  226.4 16.4 %copy-start.13 = (f32[512,768]{1,0:T(8,128)S(1)}, f32[512,768]{1,0:T(8,128)}, u32[]{:S(2)}) copy-start(f32[512,768]{1,0:T(8,128)} %get-tuple-element.100.part_ref) | copy-start | bytes 4718596
  226.4 16.4 %copy-start.21 = (s32[4]{0:T(128)S(1)}, s32[4]{0:T(128)}, u32[]{:S(2)}) copy-start(s32[4]{0:T(128)} %pad_add_fusion.flags.refs_0_) | copy-start | bytes 52
  227.5 9.7 %collective-permute-start.33 = (bf16[192,1152]{1,0:T(8,128)(2,1)S(1)}, bf16[192,1152]{1,0:T(8,128)(2,1)S(1)}, u32[]{:S(2)}, u32[]{:S(2)}) collective-permute-start(bf16[192,1152]{1,0:T(8,128)(2,1)S(1)} %get-tuple-element.235), channel_id=1, source_target_pairs={{0,2},{2,0},{1,3},{3,1},{4,6},{6,4},{5,7},{7,5},{8,10},{10,8},{9,1... | collective-permute-start | bytes 1327112 | tf_op jit(solution)/shard_map/ppermute | solution.py:720
  228.7 1.2 collective-permute-start.30
  230.0 3.3 %collective-permute-start.31 = (f32[9,768]{1,0:T(8,128)S(1)}, f32[9,768]{1,0:T(8,128)S(1)}, u32[]{:S(2)}, u32[]{:S(2)}) collective-permute-start(f32[9,768]{1,0:T(8,128)S(1)} %add.109), channel_id=1, source_target_pairs={{0,4},{4,0},{8,12},{12,8},{1,5},{5,1},{9,13},{13,9},{2,6},{6,2},{1... | collective-permute-start | bytes 82952 | tf_op jit(solution)/shard_map/ppermute | solution.py:771
  233.3 3.9 %collective-permute-start.32 = (f32[9,768]{1,0:T(8,128)S(1)}, f32[9,768]{1,0:T(8,128)S(1)}, u32[]{:S(2)}, u32[]{:S(2)}) collective-permute-start(f32[9,768]{1,0:T(8,128)S(1)} %add.110), channel_id=1, source_target_pairs={{0,8},{4,12},{8,0},{12,4},{1,9},{5,13},{9,1},{13,5},{2,10},{6,14},... | collective-permute-start | bytes 82952 | tf_op jit(solution)/shard_map/ppermute | solution.py:771
  237.3 9.4 %collective-permute-start.34 = (bf16[2,192,1152]{2,1,0:T(8,128)(2,1)S(1)}, bf16[2,192,1152]{2,1,0:T(8,128)(2,1)S(1)}, u32[]{:S(2)}, u32[]{:S(2)}) collective-permute-start(bf16[2,192,1152]{2,1,0:T(8,128)(2,1)S(1)} %pad_maximum_fusion.3.here_ref), channel_id=1, source_target_pairs={{0,1},{1,0},{2,3},{3,2},{4,5},{5,4},{6,7},{7,6},{8,9},{9,8},{10,11... | collective-permute-start | bytes 2654216 | tf_op jit(solution)/shard_map/ppermute | solution.py:724
  (24 other events, 66.5 us)
Sparse Core Ops, SparseCore 0:
  103.3 46.2 reduce-scatter.9
  156.8 18.3 reduce-scatter.7
  178.1 20.2 reduce-scatter.5

commit v12 on v11

--- a/solution.py
+++ b/solution.py
@@ -325,7 +325,7 @@
 def feed_kernel(early, *refs):
     if early:
         flags, weight_ref, rows_ref, own_ref, got_ref, cot_here, cot_there, vectors, up_own, down_own, got = refs[:11]
-        norm, norm_t, grad, grad_t, back_ref, act_ref, down_ref, pieces = refs[11:19]
+        norm, norm_t, grad, grad_t, resid_ref, back_ref, act_ref, down_ref, pieces = refs[11:20]
     else:
         flags, norm, norm_t, grad, grad_t, back_early, up_own, down_own, got = refs[:9]
         back_ref, act_ref, down_ref, *pieces = refs[9:16]
@@ -342,7 +342,9 @@
     if early:
 
         def head(i, at):
-            unit, unused = norm_parts(wide(rows_ref, at) + wide(own_ref, at) + wide(got_ref, at))
+            resid = wide(rows_ref, at) + wide(own_ref, at) + wide(got_ref, at)
+            resid_ref[at, :] = resid.astype(jnp.bfloat16)
+            unit, unused = norm_parts(resid)
             field = unit * vectors[2:3, :] + vectors[3:4, :]
             norm[at, :] = field.astype(jnp.bfloat16)
             norm_t[:, at] = field.T.astype(jnp.bfloat16)
@@ -402,7 +404,7 @@
     turned = ((width, whole), low, (width, rows), across)
     if early:
         operands = [by_rows(field, rows) for field in fields[:3]] + [*fields[3:]]
-        outs = [tokens, turned, tokens, turned]
+        outs = [tokens, turned, tokens, turned, tokens]
         pieces = [((4, width, hidden // 2), low)]
     else:
         operands = [by_rows(fields[0], rows), (fields[1], (width, rows), across)]
@@ -422,7 +424,7 @@
 
 
 def lower_kernel(
-    flags, act_early, act_late, rows_ref, own_ref, got_ref, cot_ref, early_ref, late_ref, keep_ref, first, second, sums_ref
+    flags, act_early, act_late, resid_ref, cot_ref, early_ref, late_ref, keep_ref, first, second, sums_ref
 ):
     step = pl.program_id(0)
     total = dot(act_early[...], early_ref[...]) + dot(act_late[...], late_ref[...])
@@ -432,15 +434,9 @@
     def _():
         sums_ref[...] = jnp.zeros_like(sums_ref)
 
-    send_or_keep(
-        total,
-        total + sum(ref[...].astype(jnp.float32) for ref in (rows_ref, own_ref, got_ref)),
-        first,
-        second,
-        keep_ref,
-    )
     mine = jnp.where(step < pl.num_programs(0) // 2, 0.0, 1.0)
-    block = total + mine * sum(ref[...].astype(jnp.float32) for ref in (rows_ref, own_ref, got_ref))
+    block = total + mine * resid_ref[...].astype(jnp.float32)
+    send_or_keep(block, block, first, second, keep_ref)
     sums_ref[0:1, :] += jnp.sum(block * cot, axis=0, keepdims=True)
 
 
@@ -454,7 +450,7 @@
 
     @pl.when(step >= 2)
     def _():
-        keep_ref[...] = kept
+        keep_ref[...] = kept.astype(keep_ref.dtype)
 
 
 def theirs_first(i, flags, *more):
@@ -463,25 +459,25 @@
 
 def sent_and_kept(whole, width):
     rows = whole // 4
-    keep = ((2 * rows, width), jnp.float32, (rows, width), lambda i, *scalars: (jnp.maximum(i - 2, 0), 0))
+    keep = ((2 * rows, width), jnp.bfloat16, (rows, width), lambda i, *scalars: (jnp.maximum(i - 2, 0), 0))
     send = ((rows, width), jnp.bfloat16)
     return [keep, send, send, ((8, width), jnp.float32)]
 
 
-def lower(flags, act_early, act_late, down_early, down_late, rows, own, got, cot):
-    whole, width = rows.shape
-    fields = [by_rows(field, whole // 4, theirs_first) for field in (act_early, act_late, rows, own, got, cot)]
+def lower(flags, act_early, act_late, down_early, down_late, resid, cot):
+    whole, width = resid.shape
+    fields = [by_rows(field, whole // 4, theirs_first) for field in (act_early, act_late, resid, cot)]
     return streamed(
         lower_kernel, 4, [flags], fields + [down_early, down_late], sent_and_kept(whole, width), [], 6, SNUG
     )
 
 
 def middle_kernel(
-    flags, rows_ref, own_ref, got_ref, cot_ref, back_own, back_got, mixed_ref,
+    flags, resid_ref, cot_ref, back_own, back_got, mixed_ref,
     vectors, w_ref, grad_ref, gmixed_ref, gout_ref, sums_ref, gout,
 ):
     step, last = pl.program_id(0), pl.num_programs(0) - 1
-    unit, scale = norm_parts(sum(ref[...].astype(jnp.float32) for ref in (rows_ref, own_ref, got_ref)))
+    unit, scale = norm_parts(resid_ref[...].astype(jnp.float32))
     back = sum(ref[...].astype(jnp.float32) for ref in (back_own, back_got))
     inner = back * vectors[2:3, :]
     mean = jnp.mean(inner, axis=-1, keepdims=True)
@@ -588,13 +584,13 @@
     first = pl.program_id(0) == 0
     unit, scale = norm_parts(rows_ref[...].astype(jnp.float32))
     got = jnp.where(first, got_first[...], got_second[...]).astype(jnp.float32)
-    inner = (keep_ref[...] + got) * vectors[0:1, :]
+    inner = (keep_ref[...].astype(jnp.float32) + got) * vectors[0:1, :]
     mean = jnp.mean(inner, axis=-1, keepdims=True)
     slant = jnp.mean(inner * unit, axis=-1, keepdims=True)
     grad = resid_ref[...].astype(jnp.float32) + scale * (inner - mean - unit * slant)
     out_ref[0] = grad.astype(jnp.bfloat16)
     got = jnp.where(first, block_first[...], block_second[...]).astype(jnp.float32)
-    out_ref[1] = (block_keep[...] + got).astype(jnp.bfloat16)
+    out_ref[1] = (block_keep[...].astype(jnp.float32) + got).astype(jnp.bfloat16)
 
 
 def last(flags, rows, resid, keep, block_keep, got, vectors):
@@ -835,14 +831,14 @@
     cot_half = last_got[w_out.shape[0] :]
     scalars = [flags, dwa_weights]
     fields = [layer_rows, attn, attn_got, cot_half, swap_near(cot_half), vectors]
-    *kept, back, act_early, down_early, early_pieces = feed(True, scalars, fields, w_up, w_down, early_got)
+    *kept, resid, back, act_early, down_early, early_pieces = feed(True, scalars, fields, w_up, w_down, early_got)
     early_sum = scatter_plane(after(early_pieces, late_got))
     back, act_late, down_late, *late_owned = feed(
         False, [flags], [*kept, back], w_up, w_down, late_got
     )
     late_moved = [send_to_owner(late_owned[j], j // 2, j % 2) for j in range(4)]
     grad_down = kept[2]
-    fields = [layer_rows, attn, attn_got, grad_down, back, swap_near(back)]
+    fields = [resid, grad_down, back, swap_near(back)]
     grad_attn, grad_mixed, grad_out, sums_two = middle(flags, fields, mixed, vectors, last_got)
     grad_qkv = attend_back(
         apart, member, cos_table, sin_table, projected, grad_mixed, mixed, logs, LONGEST
@@ -856,7 +852,7 @@
         flags, after(grad_qkv, owned[0]), (w_qkv, qkv_near, qkv_far), layer_rows
     )
     block_keep, *block_send, sums_now = lower(
-        flags, act_early, act_late, down_early, down_late, layer_rows, attn, attn_got, after(grad_down, keep)
+        flags, act_early, act_late, down_early, down_late, resid, after(grad_down, keep)
     )
     sent = [*send, *block_send]
     keep, block_keep, *arrived = lax.optimization_barrier((keep, block_keep, *sent, *moved))

time: 257 us -> 255 us (level)
  waiting for transfers between devices: 22 us -> 32.1 us
  starting transfers between devices: 50.3 us -> 46 us
  local copies, waits for them, and re-layouts: 19.9 us -> 16.5 us
  Pallas kernels: 122 us -> 119 us
    ppermute x8, waiting for transfers between devices: 1.87 us -> 5.6 us  [send_to_owner(): lax.ppermute(field, AXES, moves(away if not other_far and (not other_tp)...]
    ppermute x7, waiting for transfers between devices: 2.76 us -> 5.65 us  [swap_diagonal(): lax.ppermute(field, AXES, moves(away, lambda t, d, k, c: (c, d, k, t)))]
    unnamed x100 -> x94, local copies, waits for them, and re-layouts: 13.7 us -> 10.9 us
    pallas_call x10, Pallas kernels: 84.7 us -> 81.9 us  [streamed(): pl.pallas_call(kernel, grid_spec=pltpu.PrefetchScalarGridSpec(num_scalar_...]
  transfers between devices with their start and end apart: 38 -> 38, of which waited for: 9 -> 11; matrix products, arithmetic and copies ran while one was open for 13% -> 12% of each run, Pallas kernels for 47% -> 46%
where the time goes in v12:
time: 255 us; the launch traced here: 254 us
  Pallas kernels  119 us (47%)
  starting transfers between devices  46 us (18%)
  waiting for transfers between devices  32.1 us (13%)
  other arithmetic  25.1 us (10%)
  local copies, waits for them, and re-layouts  16.5 us (6%)
  between operations  14.6 us (6%)
    pallas_call x10, Pallas kernels, streamed(): pl.pallas_call(kernel, grid_spec=pltpu.PrefetchScalarGridSpec(num_scalar_...  81.9 us
    ppermute x7, starting transfers between devices, swap_diagonal(): lax.ppermute(field, AXES, moves(away, lambda t, d, k, c: (c, d, k, t)))  23 us
    pallas_call x1, Pallas kernels, attend_back(): pl.pallas_call(functools.partial(attend_back_kernel, reach), grid=(width...  19.6 us
    ppermute x5, waiting for transfers between devices, sum_over(): lax.ppermute(field, name, [(d, d ^ bit) for d in range(size)])  14 us
    pallas_call x1, Pallas kernels, attend(): pl.pallas_call(functools.partial(attend_kernel, reach), grid=(width // LA...  13.1 us
    unnamed x94, local copies, waits for them, and re-layouts  10.9 us
    ppermute x8, starting transfers between devices, send_to_owner(): lax.ppermute(field, AXES, moves(away if not other_far and (not other_tp)...  10.7 us
    ppermute x7, waiting for transfers between devices, swap_diagonal(): lax.ppermute(field, AXES, moves(away, lambda t, d, k, c: (c, d, k, t)))  5.65 us
  transfers between devices with their start and end apart: 38, of which 11 were waited for; matrix products, arithmetic and copies ran while one was open for 12% of the time, Pallas kernels for 46%

profile of v12, /device:TPU:9, one launch (start us, length us, event | category | flops | bytes accessed | tf_op | source)
XLA Modules:
  0.0 254.2 jit_solution(2082732933461657247)
XLA Ops:
  7.3 0.7 collective-permute-start.2
  8.0 3.1 %collective-permute-start = (bf16[512,768]{1,0:T(8,128)(2,1)}, bf16[512,768]{1,0:T(8,128)(2,1)}, u32[]{:S(2)}, u32[]{:S(2)}) collective-permute-start(bf16[512,768]{1,0:T(8,128)(2,1)} %bitcast.45), channel_id=1, source_target_pairs={{1,16},{3,18},{5,20},{7,22},{9,24},{11,26},{13,28},{15,30},{16,1},... | collective-permute-start | bytes 2359304 | tf_op jit(solution)/shard_map/ppermute | solution.py:697
  11.1 2.2 constant_dynamic-slice_fusion
  13.2 2.6 %collective-permute-start.3 = (bf16[3,384,384]{2,1,0:T(8,128)(2,1)}, bf16[3,384,384]{2,1,0:T(8,128)(2,1)S(1)}, u32[]{:S(2)}, u32[]{:S(2)}) collective-permute-start(bf16[3,384,384]{2,1,0:T(8,128)(2,1)} %constant_dynamic-slice_fusion), channel_id=1, source_target_pairs={{1,16},{3,18},{5,20},{7,22},{9,24},{11,26},{13,28},{15,30},{16,1},... | collective-permute-start | bytes 2654216 | tf_op jit(solution)/shard_map/ppermute | solution.py:697
  16.0 2.5 pad_maximum_fusion.2
  18.5 1.9 fusion.10
  20.5 1.6 pad_maximum_fusion.1
  22.1 1.5 pad_maximum_fusion
  23.6 4.3 %shard_map.220 = (bf16[4,512,768]{2,1,0:T(8,128)(2,1)}, f32[512,768]{1,0:T(8,128)}, f32[8,768]{1,0:T(8,128)}) custom-call(f32[5]{0:T(128)} %weight_ref.1, bf16[4,512,768]{2,1,0:T(8,128)(2,1)} %bitcast.43, bf16[512,768]{1,0:T(8,128)(2,1)} %bitcast.41), custom_call_target="tpu_custom_call" | custom-call | bytes 9000000 | tf_op jit(solution)/shard_map/pallas_call | solution.py:627
  29.5 3.1 %collective-permute-start.5 = (bf16[896,768]{1,0:T(8,128)(2,1)}, bf16[896,768]{1,0:T(8,128)(2,1)}, u32[]{:S(2)}, u32[]{:S(2)}) collective-permute-start(bf16[896,768]{1,0:T(8,128)(2,1)} %pad_maximum_fusion.2), channel_id=1, source_target_pairs={{1,16},{3,18},{5,20},{7,22},{9,24},{11,26},{13,28},{15,30},{16,1},... | collective-permute-start | bytes 4128776 | tf_op jit(solution)/shard_map/ppermute | solution.py:697
  32.6 1.2 broadcast_select_fusion.1
  33.9 3.1 %collective-permute-start.4 = (bf16[3,384,384]{2,1,0:T(8,128)(2,1)S(1)}, bf16[3,384,384]{2,1,0:T(8,128)(2,1)S(1)}, u32[]{:S(2)}, u32[]{:S(2)}) collective-permute-start(bf16[3,384,384]{2,1,0:T(8,128)(2,1)S(1)} %collective-permute-done.3.w_near), channel_id=1, source_target_pairs={{1,3},{3,1},{5,7},{7,5},{9,11},{11,9},{13,15},{15,13},{16,18},{18,... | collective-permute-start | bytes 2654216 | tf_op jit(solution)/shard_map/ppermute | solution.py:712
  37.1 0.9 fusion.2.member_ref
  38.0 0.9 select_convert_fusion.apart_ref
  38.9 3.1 %fusion.1 = (f32[1024,128]{1,0:T(8,128)}, f32[1024,128]{1,0:T(8,128)}) fusion(f32[128]{0:T(128)S(1)} %get-tuple-element.241, f32[128]{0:T(128)S(1)} %get-tuple-element.242, f32[1024]{0:T(1024)S(1)} %subtract_convert_fusion), kind=kLoop, calls=%fused_computation.13 | loop fusion | flops 262144 | bytes 1053696 | tf_op jit(solution)/shard_map/mul | solution.py:812
  41.9 2.8 %collective-permute-start.8 = (bf16[1536,768]{1,0:T(8,128)(2,1)}, bf16[1536,768]{1,0:T(8,128)(2,1)}, u32[]{:S(2)}, u32[]{:S(2)}) collective-permute-start(bf16[1536,768]{1,0:T(8,128)(2,1)} %pad_maximum_fusion), channel_id=1, source_target_pairs={{1,16},{3,18},{5,20},{7,22},{9,24},{11,26},{13,28},{15,30},{16,1},... | collective-permute-start | bytes 7077896 | tf_op jit(solution)/shard_map/ppermute | solution.py:697
  44.7 1.8 maximum_select_fusion.rows_ref.refs_2_
  46.6 1.1 collective-permute-done.4.w_far
  47.7 0.9 copy-done.8
  48.6 9.0 %shard_map.221 = (bf16[3,1024,384]{2,1,0:T(8,128)(2,1)}, bf16[768,1024]{1,0:T(8,128)(2,1)}) custom-call(s32[4]{0:T(128)} %pad_add_fusion.flags.refs_0_, bf16[1024,768]{1,0:T(8,128)(2,1)} %maximum_select_fusion.rows_ref.refs_2_, f32[1024,128]{1,0:T(8,128)} %get-tuple-element.105.cos_ref, f32[1024,128]{1,0:T(8,128)} %get-tuple-element.106.sin_ref, ...), custom_call_target="tpu_custom_call" | custom-call | bytes 24000000 | tf_op jit(solution)/shard_map/pallas_call | solution.py:240
  57.6 13.1 %shard_map.222 = (bf16[1024,384]{1,0:T(8,128)(2,1)}, f32[3,8,1024]{2,1,0:T(8,128)}) custom-call(bf16[1024,128]{1,0:T(8,128)(2,1)} %select_convert_fusion.apart_ref, bf16[1024,128]{1,0:T(8,128)(2,1)} %fusion.2.member_ref, bf16[3,1024,384]{2,1,0:T(8,128)(2,1)} %get-tuple-element.108.q_ref.k_ref.v_ref, ...), custom_call_target="tpu_custom_call" | custom-call | bytes 36000000 | tf_op jit(solution)/shard_map/pallas_call | solution.py:104
  70.8 4.0 %collective-permute-start.9 = (bf16[1536,768]{1,0:T(8,128)(2,1)S(1)}, bf16[1536,768]{1,0:T(8,128)(2,1)}, u32[]{:S(2)}, u32[]{:S(2)}) collective-permute-start(bf16[1536,768]{1,0:T(8,128)(2,1)S(1)} %copy-done.26), channel_id=1, source_target_pairs={{1,16},{3,18},{5,20},{7,22},{9,24},{11,26},{13,28},{15,30},{16,1},... | collective-permute-start | bytes 7077896 | tf_op jit(solution)/shard_map/ppermute | solution.py:697
  74.8 1.7 broadcast_select_fusion.w_ref
  76.5 1.0 convolution_convert_fusion.refs_3_
  78.2 3.9 %collective-permute-done.7.refs_6_ = bf16[512,768]{1,0:T(8,128)(2,1)S(1)} collective-permute-done((bf16[512,768]{1,0:T(8,128)(2,1)S(1)}, bf16[512,768]{1,0:T(8,128)(2,1)S(1)}, u32[]{:S(2)}, u32[]{:S(2)}) %collective-permute-start.7) | collective-permute-done | bytes 786464 | tf_op jit(solution)/shard_map/ppermute | solution.py:720
  82.1 0.9 copy-done.30
  82.9 19.3 %shard_map.223 = (bf16[1024,768]{1,0:T(8,128)(2,1)}, bf16[768,1024]{1,0:T(8,128)(2,1)}, bf16[1024,768]{1,0:T(8,128)(2,1)}, bf16[768,1024]{1,0:T(8,128)(2,1)}, bf...) custom-call(s32[4]{0:T(128)} %pad_add_fusion.flags.refs_0_, ...), custom_call_target="tpu_custom_call" | custom-call | bytes 51000000 | tf_op jit(solution)/shard_map/pallas_call | solution.py:240
  102.4 16.3 %shard_map.224 = (bf16[1024,768]{1,0:T(8,128)(2,1)}, bf16[1024,768]{1,0:T(8,128)(2,1)}, bf16[768,768]{1,0:T(8,128)(2,1)}, bf16[768,384]{1,0:T(8,128)(2,1)}, bf16...) custom-call(s32[4]{0:T(128)} %pad_add_fusion.flags.refs_0_, ...), custom_call_target="tpu_custom_call" | custom-call | bytes 51000000 | tf_op jit(solution)/shard_map/pallas_call | solution.py:240
  119.5 2.3 collective-permute-start.13
  121.8 2.8 %collective-permute-start.11 = (bf16[768,384]{1,0:T(8,128)(2,1)}, bf16[768,384]{1,0:T(8,128)(2,1)S(1)}, u32[]{:S(2)}, u32[]{:S(2)}) collective-permute-start(bf16[768,384]{1,0:T(8,128)(2,1)} %get-tuple-element.124), channel_id=1, source_target_pairs={{1,16},{3,18},{5,20},{7,22},{9,24},{11,26},{13,28},{15,30},{16,1},... | collective-permute-start | bytes 1769480 | tf_op jit(solution)/shard_map/ppermute | solution.py:701
  124.7 1.1 copy-done.27
  125.8 9.3 %shard_map.225 = (bf16[1024,768]{1,0:T(8,128)(2,1)}, bf16[1024,384]{1,0:T(8,128)(2,1)}, bf16[768,384]{1,0:T(8,128)(2,1)}, f32[8,768]{1,0:T(8,128)}) custom-call(s32[4]{0:T(128)} %pad_add_fusion.flags.refs_0_, bf16[1024,768]{1,0:T(8,128)(2,1)} %get-tuple-element.113.resid_ref, bf16[1024,768]{1,0:T(8,128)(2,1)} %get-tuple-element.136.refs_3_.cot_ref, ...), custom_call_target="tpu_custom_call" | custom-call | bytes 24000000 | tf_op jit(solution)/shard_map/pallas_call | solution.py:240
  135.0 19.6 %shard_map.226.query_ref.key_ref.value_ref.grad_ref = bf16[3,1024,384]{2,1,0:T(8,128)(2,1)} custom-call(bf16[1024,128]{1,0:T(8,128)(2,1)} %select_convert_fusion.apart_ref, bf16[1024,128]{1,0:T(8,128)(2,1)} %fusion.2.member_ref, f32[1024,128]{1,0:T(8,128)} %get-tuple-element.105.cos_ref, f32[1024,128]{1,0:T(8,128)} %get-tuple-element.106.sin_ref, ...), custom_call_target="tpu_custom_call" | custom-call | bytes 66000000 | tf_op jit(solution)/shard_map/pallas_call | solution.py:189
  155.4 7.1 %shard_map.227 = (bf16[768,384]{1,0:T(8,128)(2,1)}, bf16[768,384]{1,0:T(8,128)(2,1)}, bf16[768,384]{1,0:T(8,128)(2,1)}, bf16[768,384]{1,0:T(8,128)(2,1)}) custom-call(s32[4]{0:T(128)} %pad_add_fusion.flags.refs_0_, bf16[768,1024]{1,0:T(8,128)(2,1)} %get-tuple-element.129.turned_ref, bf16[768,384]{1,0:T(8,128)(2,1)} %get-tuple-element.130.out_grad_ref, ...), custom_call_target="tpu_custom_call" | custom-call | bytes 12000000 | tf_op jit(solution)/shard_map/pallas_call | solution.py:240
  162.5 3.1 %collective-permute-start.15 = (bf16[768,384]{1,0:T(8,128)(2,1)}, bf16[768,384]{1,0:T(8,128)(2,1)}, u32[]{:S(2)}, u32[]{:S(2)}) collective-permute-start(bf16[768,384]{1,0:T(8,128)(2,1)} %get-tuple-element.131), channel_id=1, source_target_pairs={{1,16},{3,18},{5,20},{7,22},{9,24},{11,26},{13,28},{15,30},{16,1},... | collective-permute-start | bytes 1769480 | tf_op jit(solution)/shard_map/ppermute | solution.py:701
  165.6 1.6 collective-permute-start.17
  167.6 3.0 %add_convert_fusion = bf16[768,384]{1,0:T(8,128)(2,1)} fusion(bf16[768,384]{1,0:T(8,128)(2,1)} %copy-done.34, bf16[768,384]{1,0:T(8,128)(2,1)} %copy-done.33, bf16[768,384]{1,0:T(8,128)(2,1)} %copy-done.32, bf16[768,384]{1,0:T(8,128)(2,1)} %get-tuple-element.124, bf16[768,384]{1,0:T(8,128)(2,1)} %copy-done.35, pred[]{:T(512)S(6)} %eq.35), kind=kLoop, calls=%fused_computation.6 | loop fusion | flops 2654208 | bytes 3538945 | tf_op jit(solution)/shard_map/convert_element_type | solution.py:739
  171.4 1.4 copy-done.1
  172.8 1.5 copy-done.3
  174.3 1.2 copy-done.9
  175.5 6.1 %shard_map.228 = (bf16[512,768]{1,0:T(8,128)(2,1)S(1)}, bf16[256,768]{1,0:T(8,128)(2,1)}, bf16[256,768]{1,0:T(8,128)(2,1)}, f32[8,768]{1,0:T(8,128)S(1)}) custom-call(s32[4]{0:T(128)S(1)} %copy-done.17, bf16[3,1024,384]{2,1,0:T(8,128)(2,1)S(1)} %copy-done, bf16[1024,768]{1,0:T(8,128)(2,1)S(1)} %copy-done.1, bf16[3,768,384]{2,1,0:T(8,128)(2,1)S(1)} %copy-done.3, ...), custom_call_target="tpu_custom_call" | custom-call | bytes 15000000 | tf_op jit(solution)/shard_map/pallas_call | solution.py:240
  181.6 0.9 copy-done.15
  182.5 1.3 copy-done.14
  183.8 4.9 %shard_map.229 = (bf16[512,768]{1,0:T(8,128)(2,1)S(1)}, bf16[256,768]{1,0:T(8,128)(2,1)S(1)}, bf16[256,768]{1,0:T(8,128)(2,1)S(1)}, f32[8,768]{1,0:T(8,128)S(1)}) custom-call(s32[4]{0:T(128)S(1)} %copy-done.17, bf16[1024,768]{1,0:T(8,128)(2,1)S(1)} %copy-done.11, bf16[1024,768]{1,0:T(8,128)(2,1)S(1)} %copy-done.12, bf16[1024,768]{1,0:T(8,128)(2,1)S(1)} %copy-done.5, ...), custom_call_target="tpu_custom_call" | custom-call | bytes 18000000 | tf_op jit(solution)/shard_map/pallas_call | solution.py:240
  188.7 0.9 copy-done.16
  189.6 4.9 %collective-permute-done.18 = bf16[768,384]{1,0:T(8,128)(2,1)} collective-permute-done((bf16[768,384]{1,0:T(8,128)(2,1)}, bf16[768,384]{1,0:T(8,128)(2,1)}, u32[]{:S(2)}, u32[]{:S(2)}) %collective-permute-start.18) | collective-permute-done | bytes 589856 | tf_op jit(solution)/shard_map/ppermute | solution.py:701
  195.6 2.0 add_convert_fusion.1
  197.9 2.1 collective-permute-start.28
  199.9 2.2 collective-permute-start.27
  202.2 4.1 %collective-permute-start.26 = (bf16[192,384]{1,0:T(8,128)(2,1)}, bf16[192,384]{1,0:T(8,128)(2,1)S(1)}, u32[]{:S(2)}, u32[]{:S(2)}) collective-permute-start(bf16[192,384]{1,0:T(8,128)(2,1)} %reduce-scatter.8.cloned.1.call-done), channel_id=1, source_target_pairs={{1,16},{3,18},{5,20},{7,22},{9,24},{11,26},{13,28},{15,30},{16,1},... | collective-permute-start | bytes 442376 | tf_op jit(solution)/shard_map/ppermute | solution.py:697
  207.1 5.3 %shard_map.230.own_ref = bf16[2,512,768]{2,1,0:T(8,128)(2,1)} custom-call(s32[4]{0:T(128)} %pad_add_fusion.flags.refs_0_, bf16[1024,768]{1,0:T(8,128)(2,1)} %maximum_select_fusion.rows_ref.refs_2_, bf16[1024,768]{1,0:T(8,128)(2,1)} %get-tuple-element.121.resid_ref, bf16[512,768]{1,0:T(8,128)(2,1)} %copy-done.15, bf16[512,768]{1,0:T(8,128)(2,1)} %copy-done.16, ...), custom_call_target="tpu_custom_call" | custom-call | bytes 9000000 | tf_op jit(solution)/shard_map/pallas_call | solution.py:240
  212.4 2.9 %collective-permute-done.24 = f32[9,768]{1,0:T(8,128)S(1)} collective-permute-done((f32[9,768]{1,0:T(8,128)S(1)}, f32[9,768]{1,0:T(8,128)S(1)}, u32[]{:S(2)}, u32[]{:S(2)}) %collective-permute-start.24) | collective-permute-done | bytes 27680 | tf_op jit(solution)/shard_map/ppermute | solution.py:767
  215.5 3.7 %collective-permute-done.25 = f32[9,768]{1,0:T(8,128)S(1)} collective-permute-done((f32[9,768]{1,0:T(8,128)S(1)}, f32[9,768]{1,0:T(8,128)S(1)}, u32[]{:S(2)}, u32[]{:S(2)}) %collective-permute-start.25) | collective-permute-done | bytes 27680 | tf_op jit(solution)/shard_map/ppermute | solution.py:767
  219.2 3.4 %collective-permute-start.23 = (bf16[2,512,768]{2,1,0:T(8,128)(2,1)}, bf16[2,512,768]{2,1,0:T(8,128)(2,1)S(1)}, u32[]{:S(2)}, u32[]{:S(2)}) collective-permute-start(bf16[2,512,768]{2,1,0:T(8,128)(2,1)} %shard_map.230.own_ref), channel_id=1, source_target_pairs={{1,16},{3,18},{5,20},{7,22},{9,24},{11,26},{13,28},{15,30},{16,1},... | collective-permute-start | bytes 4718600 | tf_op jit(solution)/shard_map/ppermute | solution.py:697
  222.9 1.1 fusion.9
  224.2 1.2 collective-permute-done.30
  225.5 3.2 %collective-permute-done.31 = f32[9,768]{1,0:T(8,128)S(1)} collective-permute-done((f32[9,768]{1,0:T(8,128)S(1)}, f32[9,768]{1,0:T(8,128)S(1)}, u32[]{:S(2)}, u32[]{:S(2)}) %collective-permute-start.31) | collective-permute-done | bytes 27680 | tf_op jit(solution)/shard_map/ppermute | solution.py:767
  228.7 1.0 collective-permute-start.32
  229.8 2.9 %collective-permute-done.32 = f32[9,768]{1,0:T(8,128)S(1)} collective-permute-done((f32[9,768]{1,0:T(8,128)S(1)}, f32[9,768]{1,0:T(8,128)S(1)}, u32[]{:S(2)}, u32[]{:S(2)}) %collective-permute-start.32) | collective-permute-done | bytes 27680 | tf_op jit(solution)/shard_map/ppermute | solution.py:767
  232.7 1.6 collective-permute-done.33
  235.5 5.6 %collective-permute-done.23.got_ref = bf16[2,512,768]{2,1,0:T(8,128)(2,1)S(1)} collective-permute-done((bf16[2,512,768]{2,1,0:T(8,128)(2,1)}, bf16[2,512,768]{2,1,0:T(8,128)(2,1)S(1)}, u32[]{:S(2)}, u32[]{:S(2)}) %collective-permute-start.23) | collective-permute-done | bytes 1572896 | tf_op jit(solution)/shard_map/ppermute | solution.py:697
  241.1 2.1 shard_map.231
  243.2 1.3 slice_reduce_fusion
  245.1 2.5 shard_map.232
  (170 shorter events, 9.7 us)
Async XLA Ops:
  7.2 8.7 %copy-start.42 = (f32[768]{0:T(1024)S(1)}, f32[768]{0:T(1024)}, u32[]{:S(2)}) copy-start(f32[768]{0:T(1024)} %param.18) | copy-start | bytes 9220
  7.2 8.8 %copy-start.43 = (f32[768]{0:T(1024)S(1)}, f32[768]{0:T(1024)}, u32[]{:S(2)}) copy-start(f32[768]{0:T(1024)} %param.19) | copy-start | bytes 9220
  7.2 8.8 %copy-start.44 = (f32[768]{0:T(1024)S(1)}, f32[768]{0:T(1024)}, u32[]{:S(2)}) copy-start(f32[768]{0:T(1024)} %param.22) | copy-start | bytes 9220
  7.2 8.8 %copy-start.45 = (f32[768]{0:T(1024)S(1)}, f32[768]{0:T(1024)}, u32[]{:S(2)}) copy-start(f32[768]{0:T(1024)} %param.23) | copy-start | bytes 9220
  7.2 148.1 %reduce-scatter.10.cloned.1.call-start = ((), (), s32[]{:S(2)}) async-start(), calls=%async_computation.5 | async-start | bytes 2949120
  7.3 21.9 %collective-permute-start.2 = (s32[1,3]{1,0:T(1,128)}, s32[1,3]{1,0:T(1,128)S(1)}, u32[]{:S(2)}, u32[]{:S(2)}) collective-permute-start(s32[1,3]{1,0:T(1,128)} %param.16), channel_id=1, source_target_pairs={{0,1},{1,0},{2,3},{3,2},{4,5},{5,4},{6,7},{7,6},{8,9},{9,8},{10,11... | collective-permute-start | bytes 44 | tf_op jit(solution)/shard_map/ppermute | solution.py:720
  8.0 21.5 %collective-permute-start = (bf16[512,768]{1,0:T(8,128)(2,1)}, bf16[512,768]{1,0:T(8,128)(2,1)}, u32[]{:S(2)}, u32[]{:S(2)}) collective-permute-start(bf16[512,768]{1,0:T(8,128)(2,1)} %bitcast.45), channel_id=1, source_target_pairs={{1,16},{3,18},{5,20},{7,22},{9,24},{11,26},{13,28},{15,30},{16,1},... | collective-permute-start | bytes 2359304 | tf_op jit(solution)/shard_map/ppermute | solution.py:697
  13.2 20.7 %collective-permute-start.3 = (bf16[3,384,384]{2,1,0:T(8,128)(2,1)}, bf16[3,384,384]{2,1,0:T(8,128)(2,1)S(1)}, u32[]{:S(2)}, u32[]{:S(2)}) collective-permute-start(bf16[3,384,384]{2,1,0:T(8,128)(2,1)} %constant_dynamic-slice_fusion), channel_id=1, source_target_pairs={{1,16},{3,18},{5,20},{7,22},{9,24},{11,26},{13,28},{15,30},{16,1},... | collective-permute-start | bytes 2654216 | tf_op jit(solution)/shard_map/ppermute | solution.py:697
  23.6 9.0 %copy-start.29 = (bf16[1,512,768]{2,1,0:T(8,128)(2,1)S(1)}, bf16[1,512,768]{2,1,0:T(8,128)(2,1)}, u32[]{:S(2)}) copy-start(bf16[1,512,768]{2,1,0:T(8,128)(2,1)} %param.13) | copy-start | bytes 2359300
  29.5 45.2 %collective-permute-start.5 = (bf16[896,768]{1,0:T(8,128)(2,1)}, bf16[896,768]{1,0:T(8,128)(2,1)}, u32[]{:S(2)}, u32[]{:S(2)}) collective-permute-start(bf16[896,768]{1,0:T(8,128)(2,1)} %pad_maximum_fusion.2), channel_id=1, source_target_pairs={{1,16},{3,18},{5,20},{7,22},{9,24},{11,26},{13,28},{15,30},{16,1},... | collective-permute-start | bytes 4128776 | tf_op jit(solution)/shard_map/ppermute | solution.py:697
  33.8 10.9 %collective-permute-start.1 = (bf16[512,768]{1,0:T(8,128)(2,1)S(1)}, bf16[512,768]{1,0:T(8,128)(2,1)S(1)}, u32[]{:S(2)}, u32[]{:S(2)}) collective-permute-start(bf16[512,768]{1,0:T(8,128)(2,1)S(1)} %broadcast_select_fusion.1), channel_id=1, source_target_pairs={{0,1},{1,0},{2,3},{3,2},{4,5},{5,4},{6,7},{7,6},{8,9},{9,8},{10,11... | collective-permute-start | bytes 2359304 | tf_op jit(solution)/shard_map/ppermute | solution.py:720
  33.9 12.7 %copy-start.6 = (bf16[3,384,384]{2,1,0:T(8,128)(2,1)}, bf16[3,384,384]{2,1,0:T(8,128)(2,1)S(1)}, u32[]{:S(2)}) copy-start(bf16[3,384,384]{2,1,0:T(8,128)(2,1)S(1)} %collective-permute-done.3.w_near) | copy-start | bytes 2654212
  33.9 13.8 %collective-permute-start.4 = (bf16[3,384,384]{2,1,0:T(8,128)(2,1)S(1)}, bf16[3,384,384]{2,1,0:T(8,128)(2,1)S(1)}, u32[]{:S(2)}, u32[]{:S(2)}) collective-permute-start(bf16[3,384,384]{2,1,0:T(8,128)(2,1)S(1)} %collective-permute-done.3.w_near), channel_id=1, source_target_pairs={{1,3},{3,1},{5,7},{7,5},{9,11},{11,9},{13,15},{15,13},{16,18},{18,... | collective-permute-start | bytes 2654216 | tf_op jit(solution)/shard_map/ppermute | solution.py:712
  41.9 40.1 %collective-permute-start.8 = (bf16[1536,768]{1,0:T(8,128)(2,1)}, bf16[1536,768]{1,0:T(8,128)(2,1)}, u32[]{:S(2)}, u32[]{:S(2)}) collective-permute-start(bf16[1536,768]{1,0:T(8,128)(2,1)} %pad_maximum_fusion), channel_id=1, source_target_pairs={{1,16},{3,18},{5,20},{7,22},{9,24},{11,26},{13,28},{15,30},{16,1},... | collective-permute-start | bytes 7077896 | tf_op jit(solution)/shard_map/ppermute | solution.py:697
  57.6 13.1 %copy-start.26 = (bf16[1536,768]{1,0:T(8,128)(2,1)S(1)}, bf16[1536,768]{1,0:T(8,128)(2,1)}, u32[]{:S(2)}) copy-start(bf16[1536,768]{1,0:T(8,128)(2,1)} %pad_maximum_fusion.1) | copy-start | bytes 7077892
  57.6 17.1 %copy-start.22 = (bf16[1,512,768]{2,1,0:T(8,128)(2,1)S(1)}, bf16[1,512,768]{2,1,0:T(8,128)(2,1)}, u32[]{:S(2)}) copy-start(bf16[1,512,768]{2,1,0:T(8,128)(2,1)} %param.15) | copy-start | bytes 2359300
  57.6 17.1 %copy-start.25 = (bf16[384,768]{1,0:T(8,128)(2,1)S(1)}, bf16[384,768]{1,0:T(8,128)(2,1)}, u32[]{:S(2)}) copy-start(bf16[384,768]{1,0:T(8,128)(2,1)} %param.21) | copy-start | bytes 1769476
  70.8 31.5 %collective-permute-start.9 = (bf16[1536,768]{1,0:T(8,128)(2,1)S(1)}, bf16[1536,768]{1,0:T(8,128)(2,1)}, u32[]{:S(2)}, u32[]{:S(2)}) collective-permute-start(bf16[1536,768]{1,0:T(8,128)(2,1)S(1)} %copy-done.26), channel_id=1, source_target_pairs={{1,16},{3,18},{5,20},{7,22},{9,24},{11,26},{13,28},{15,30},{16,1},... | collective-permute-start | bytes 7077896 | tf_op jit(solution)/shard_map/ppermute | solution.py:697
  77.4 5.5 %collective-permute-start.6 = (bf16[1024,768]{1,0:T(8,128)(2,1)S(1)}, bf16[1024,768]{1,0:T(8,128)(2,1)}, u32[]{:S(2)}, u32[]{:S(2)}) collective-permute-start(bf16[1024,768]{1,0:T(8,128)(2,1)S(1)} %convolution_convert_fusion.refs_3_), channel_id=1, source_target_pairs={{0,1},{1,0},{2,3},{3,2},{4,5},{5,4},{6,7},{7,6},{8,9},{9,8},{10,11... | collective-permute-start | bytes 4718600 | tf_op jit(solution)/shard_map/ppermute | solution.py:720
  77.6 4.4 %collective-permute-start.7 = (bf16[512,768]{1,0:T(8,128)(2,1)S(1)}, bf16[512,768]{1,0:T(8,128)(2,1)S(1)}, u32[]{:S(2)}, u32[]{:S(2)}) collective-permute-start(bf16[512,768]{1,0:T(8,128)(2,1)S(1)} %slice.53.refs_5_), channel_id=1, source_target_pairs={{0,1},{1,0},{2,3},{3,2},{4,5},{5,4},{6,7},{7,6},{8,9},{9,8},{10,11... | collective-permute-start | bytes 2359304 | tf_op jit(solution)/shard_map/ppermute | solution.py:720
  102.3 95.6 %reduce-scatter.8.cloned.1.call-start = ((), (), s32[]{:S(2)}) async-start(), calls=%async_computation.4 | async-start | bytes 737280 | tf_op jit(solution)/shard_map/reduce_scatter | solution.py:747
  118.7 5.9 %collective-permute-start.10 = (bf16[1024,768]{1,0:T(8,128)(2,1)}, bf16[1024,768]{1,0:T(8,128)(2,1)S(1)}, u32[]{:S(2)}, u32[]{:S(2)}) collective-permute-start(bf16[1024,768]{1,0:T(8,128)(2,1)} %get-tuple-element.120.back_own), channel_id=1, source_target_pairs={{0,1},{1,0},{2,3},{3,2},{4,5},{5,4},{6,7},{7,6},{8,9},{9,8},{10,11... | collective-permute-start | bytes 4718600 | tf_op jit(solution)/shard_map/ppermute | solution.py:720
  118.9 35.7 %collective-permute-start.12 = (bf16[768,384]{1,0:T(8,128)(2,1)}, bf16[768,384]{1,0:T(8,128)(2,1)S(1)}, u32[]{:S(2)}, u32[]{:S(2)}) collective-permute-start(bf16[768,384]{1,0:T(8,128)(2,1)} %get-tuple-element.125), channel_id=1, source_target_pairs={{0,1},{1,17},{2,3},{3,19},{4,5},{5,21},{6,7},{7,23},{8,9},{9,25},{... | collective-permute-start | bytes 1769480 | tf_op jit(solution)/shard_map/ppermute | solution.py:701
  119.5 35.1 %collective-permute-start.13 = (bf16[768,384]{1,0:T(8,128)(2,1)}, bf16[768,384]{1,0:T(8,128)(2,1)S(1)}, u32[]{:S(2)}, u32[]{:S(2)}) collective-permute-start(bf16[768,384]{1,0:T(8,128)(2,1)} %get-tuple-element.126), channel_id=1, source_target_pairs={{0,2},{1,18},{2,0},{3,16},{4,6},{5,22},{6,4},{7,20},{8,10},{9,26},... | collective-permute-start | bytes 1769480 | tf_op jit(solution)/shard_map/ppermute | solution.py:701
  121.8 33.4 %collective-permute-start.14 = (bf16[768,384]{1,0:T(8,128)(2,1)}, bf16[768,384]{1,0:T(8,128)(2,1)S(1)}, u32[]{:S(2)}, u32[]{:S(2)}) collective-permute-start(bf16[768,384]{1,0:T(8,128)(2,1)} %get-tuple-element.127), channel_id=1, source_target_pairs={{0,3},{1,19},{2,1},{3,17},{4,7},{5,23},{6,5},{7,21},{8,11},{9,27},... | collective-permute-start | bytes 1769480 | tf_op jit(solution)/shard_map/ppermute | solution.py:701
  121.8 33.4 %collective-permute-start.11 = (bf16[768,384]{1,0:T(8,128)(2,1)}, bf16[768,384]{1,0:T(8,128)(2,1)S(1)}, u32[]{:S(2)}, u32[]{:S(2)}) collective-permute-start(bf16[768,384]{1,0:T(8,128)(2,1)} %get-tuple-element.124), channel_id=1, source_target_pairs={{1,16},{3,18},{5,20},{7,22},{9,24},{11,26},{13,28},{15,30},{16,1},... | collective-permute-start | bytes 1769480 | tf_op jit(solution)/shard_map/ppermute | solution.py:701
  154.6 7.9 %copy-start.32 = (bf16[768,384]{1,0:T(8,128)(2,1)}, bf16[768,384]{1,0:T(8,128)(2,1)S(1)}, u32[]{:S(2)}) copy-start(bf16[768,384]{1,0:T(8,128)(2,1)S(1)} %collective-permute-done.12) | copy-start | bytes 1769476
  154.6 7.9 %copy-start.33 = (bf16[768,384]{1,0:T(8,128)(2,1)}, bf16[768,384]{1,0:T(8,128)(2,1)S(1)}, u32[]{:S(2)}) copy-start(bf16[768,384]{1,0:T(8,128)(2,1)S(1)} %collective-permute-done.13) | copy-start | bytes 1769476
  155.3 7.2 %copy-start.34 = (bf16[768,384]{1,0:T(8,128)(2,1)}, bf16[768,384]{1,0:T(8,128)(2,1)S(1)}, u32[]{:S(2)}) copy-start(bf16[768,384]{1,0:T(8,128)(2,1)S(1)} %collective-permute-done.14) | copy-start | bytes 1769476
  155.3 7.2 %copy-start.35 = (bf16[768,384]{1,0:T(8,128)(2,1)}, bf16[768,384]{1,0:T(8,128)(2,1)S(1)}, u32[]{:S(2)}) copy-start(bf16[768,384]{1,0:T(8,128)(2,1)S(1)} %collective-permute-done.11) | copy-start | bytes 1769476
  155.3 67.4 %reduce-scatter.6.cloned.1.call-start = ((), (), s32[]{:S(2)}) async-start(), calls=%async_computation.3 | async-start | bytes 737280 | tf_op jit(solution)/shard_map/reduce_scatter | solution.py:747
  162.5 32.0 %collective-permute-start.15 = (bf16[768,384]{1,0:T(8,128)(2,1)}, bf16[768,384]{1,0:T(8,128)(2,1)}, u32[]{:S(2)}, u32[]{:S(2)}) collective-permute-start(bf16[768,384]{1,0:T(8,128)(2,1)} %get-tuple-element.131), channel_id=1, source_target_pairs={{1,16},{3,18},{5,20},{7,22},{9,24},{11,26},{13,28},{15,30},{16,1},... | collective-permute-start | bytes 1769480 | tf_op jit(solution)/shard_map/ppermute | solution.py:701
  165.6 24.0 %collective-permute-start.16 = (bf16[768,384]{1,0:T(8,128)(2,1)}, bf16[768,384]{1,0:T(8,128)(2,1)}, u32[]{:S(2)}, u32[]{:S(2)}) collective-permute-start(bf16[768,384]{1,0:T(8,128)(2,1)} %get-tuple-element.144), channel_id=1, source_target_pairs={{0,1},{1,17},{2,3},{3,19},{4,5},{5,21},{6,7},{7,23},{8,9},{9,25},{... | collective-permute-start | bytes 1769480 | tf_op jit(solution)/shard_map/ppermute | solution.py:701
  165.6 24.0 %collective-permute-start.17 = (bf16[768,384]{1,0:T(8,128)(2,1)}, bf16[768,384]{1,0:T(8,128)(2,1)}, u32[]{:S(2)}, u32[]{:S(2)}) collective-permute-start(bf16[768,384]{1,0:T(8,128)(2,1)} %get-tuple-element.145), channel_id=1, source_target_pairs={{0,2},{1,18},{2,0},{3,16},{4,6},{5,22},{6,4},{7,20},{8,10},{9,26},... | collective-permute-start | bytes 1769480 | tf_op jit(solution)/shard_map/ppermute | solution.py:701
  167.2 27.3 %collective-permute-start.18 = (bf16[768,384]{1,0:T(8,128)(2,1)}, bf16[768,384]{1,0:T(8,128)(2,1)}, u32[]{:S(2)}, u32[]{:S(2)}) collective-permute-start(bf16[768,384]{1,0:T(8,128)(2,1)} %get-tuple-element.146), channel_id=1, source_target_pairs={{0,3},{1,19},{2,1},{3,17},{4,7},{5,23},{6,5},{7,21},{8,11},{9,27},... | collective-permute-start | bytes 1769480 | tf_op jit(solution)/shard_map/ppermute | solution.py:701
  175.5 7.0 %copy-start.2 = (bf16[1024,768]{1,0:T(8,128)(2,1)S(1)}, bf16[1024,768]{1,0:T(8,128)(2,1)}, u32[]{:S(2)}) copy-start(bf16[1024,768]{1,0:T(8,128)(2,1)} %get-tuple-element.136.refs_3_.cot_ref) | copy-start | bytes 4718596
  175.5 7.0 %copy-start.5 = (bf16[1024,768]{1,0:T(8,128)(2,1)S(1)}, bf16[1024,768]{1,0:T(8,128)(2,1)}, u32[]{:S(2)}) copy-start(bf16[1024,768]{1,0:T(8,128)(2,1)} %get-tuple-element.113.resid_ref) | copy-start | bytes 4718596
  175.5 7.0 %copy-start.11 = (bf16[1024,768]{1,0:T(8,128)(2,1)S(1)}, bf16[1024,768]{1,0:T(8,128)(2,1)}, u32[]{:S(2)}) copy-start(bf16[1024,768]{1,0:T(8,128)(2,1)} %get-tuple-element.134.act_early) | copy-start | bytes 4718596
  175.5 7.0 %copy-start.12 = (bf16[1024,768]{1,0:T(8,128)(2,1)S(1)}, bf16[1024,768]{1,0:T(8,128)(2,1)}, u32[]{:S(2)}) copy-start(bf16[1024,768]{1,0:T(8,128)(2,1)} %get-tuple-element.135.act_late) | copy-start | bytes 4718596
  175.5 7.0 %copy-start.13 = (bf16[768,768]{1,0:T(8,128)(2,1)S(1)}, bf16[768,768]{1,0:T(8,128)(2,1)}, u32[]{:S(2)}) copy-start(bf16[768,768]{1,0:T(8,128)(2,1)} %get-tuple-element.137.early_ref) | copy-start | bytes 3538948
  183.8 11.7 %copy-start.31 = (bf16[768,384]{1,0:T(8,128)(2,1)S(1)}, bf16[768,384]{1,0:T(8,128)(2,1)}, u32[]{:S(2)}) copy-start(bf16[768,384]{1,0:T(8,128)(2,1)} %get-tuple-element.131) | copy-start | bytes 1769476
  194.5 3.3 %collective-permute-start.19 = (bf16[256,768]{1,0:T(8,128)(2,1)}, bf16[256,768]{1,0:T(8,128)(2,1)S(1)}, u32[]{:S(2)}, u32[]{:S(2)}) collective-permute-start(bf16[256,768]{1,0:T(8,128)(2,1)} %get-tuple-element.154), channel_id=1, source_target_pairs={{0,1},{1,0},{2,3},{3,2},{4,5},{5,4},{6,7},{7,6},{8,9},{9,8},{10,11... | collective-permute-start | bytes 1179656 | tf_op jit(solution)/shard_map/ppermute | solution.py:720
  194.7 5.2 %collective-permute-start.20 = (bf16[256,768]{1,0:T(8,128)(2,1)}, bf16[256,768]{1,0:T(8,128)(2,1)S(1)}, u32[]{:S(2)}, u32[]{:S(2)}) collective-permute-start(bf16[256,768]{1,0:T(8,128)(2,1)} %get-tuple-element.155), channel_id=1, source_target_pairs={{0,1},{1,0},{2,3},{3,2},{4,5},{5,4},{6,7},{7,6},{8,9},{9,8},{10,11... | collective-permute-start | bytes 1179656 | tf_op jit(solution)/shard_map/ppermute | solution.py:720
  195.0 7.1 %collective-permute-start.21 = (bf16[256,768]{1,0:T(8,128)(2,1)S(1)}, bf16[256,768]{1,0:T(8,128)(2,1)S(1)}, u32[]{:S(2)}, u32[]{:S(2)}) collective-permute-start(bf16[256,768]{1,0:T(8,128)(2,1)S(1)} %get-tuple-element.156), channel_id=1, source_target_pairs={{0,1},{1,0},{2,3},{3,2},{4,5},{5,4},{6,7},{7,6},{8,9},{9,8},{10,11... | collective-permute-start | bytes 1179656 | tf_op jit(solution)/shard_map/ppermute | solution.py:720
  195.2 11.2 %collective-permute-start.22 = (bf16[256,768]{1,0:T(8,128)(2,1)S(1)}, bf16[256,768]{1,0:T(8,128)(2,1)S(1)}, u32[]{:S(2)}, u32[]{:S(2)}) collective-permute-start(bf16[256,768]{1,0:T(8,128)(2,1)S(1)} %get-tuple-element.157), channel_id=1, source_target_pairs={{0,1},{1,0},{2,3},{3,2},{4,5},{5,4},{6,7},{7,6},{8,9},{9,8},{10,11... | collective-permute-start | bytes 1179656 | tf_op jit(solution)/shard_map/ppermute | solution.py:720
  197.6 25.0 %collective-permute-start.29 = (bf16[192,384]{1,0:T(8,128)(2,1)S(1)}, bf16[192,384]{1,0:T(8,128)(2,1)S(1)}, u32[]{:S(2)}, u32[]{:S(2)}) collective-permute-start(bf16[192,384]{1,0:T(8,128)(2,1)S(1)} %get-tuple-element.232), channel_id=1, source_target_pairs={{0,12},{4,0},{8,4},{12,8},{1,13},{5,1},{9,5},{13,9},{2,14},{6,2},{... | collective-permute-start | bytes 442376 | tf_op jit(solution)/shard_map/ppermute | solution.py:759
  197.9 8.5 %copy-start.36 = (bf16[256,768]{1,0:T(8,128)(2,1)}, bf16[256,768]{1,0:T(8,128)(2,1)S(1)}, u32[]{:S(2)}) copy-start(bf16[256,768]{1,0:T(8,128)(2,1)S(1)} %collective-permute-done.19.got_first) | copy-start | bytes 1179652
  197.9 24.8 %collective-permute-start.28 = (bf16[192,384]{1,0:T(8,128)(2,1)S(1)}, bf16[192,384]{1,0:T(8,128)(2,1)S(1)}, u32[]{:S(2)}, u32[]{:S(2)}) collective-permute-start(bf16[192,384]{1,0:T(8,128)(2,1)S(1)} %get-tuple-element.233), channel_id=1, source_target_pairs={{0,8},{4,12},{8,0},{12,4},{1,9},{5,13},{9,1},{13,5},{2,10},{6,14},... | collective-permute-start | bytes 442376 | tf_op jit(solution)/shard_map/ppermute | solution.py:759
  199.9 6.5 %copy-start.37 = (bf16[256,768]{1,0:T(8,128)(2,1)}, bf16[256,768]{1,0:T(8,128)(2,1)S(1)}, u32[]{:S(2)}) copy-start(bf16[256,768]{1,0:T(8,128)(2,1)S(1)} %collective-permute-done.20.got_second) | copy-start | bytes 1179652
  199.9 22.7 %collective-permute-start.27 = (bf16[192,384]{1,0:T(8,128)(2,1)S(1)}, bf16[192,384]{1,0:T(8,128)(2,1)S(1)}, u32[]{:S(2)}, u32[]{:S(2)}) collective-permute-start(bf16[192,384]{1,0:T(8,128)(2,1)S(1)} %get-tuple-element.234), channel_id=1, source_target_pairs={{0,4},{4,8},{8,12},{12,0},{1,5},{5,9},{9,13},{13,1},{2,6},{6,10},{... | collective-permute-start | bytes 442376 | tf_op jit(solution)/shard_map/ppermute | solution.py:759
  202.2 20.5 %collective-permute-start.26 = (bf16[192,384]{1,0:T(8,128)(2,1)}, bf16[192,384]{1,0:T(8,128)(2,1)S(1)}, u32[]{:S(2)}, u32[]{:S(2)}) collective-permute-start(bf16[192,384]{1,0:T(8,128)(2,1)} %reduce-scatter.8.cloned.1.call-done), channel_id=1, source_target_pairs={{1,16},{3,18},{5,20},{7,22},{9,24},{11,26},{13,28},{15,30},{16,1},... | collective-permute-start | bytes 442376 | tf_op jit(solution)/shard_map/ppermute | solution.py:697
  207.1 15.6 %copy-start.40 = (bf16[192,384]{1,0:T(8,128)(2,1)S(1)}, bf16[192,384]{1,0:T(8,128)(2,1)}, u32[]{:S(2)}) copy-start(bf16[192,384]{1,0:T(8,128)(2,1)} %reduce-scatter.8.cloned.1.call-done) | copy-start | bytes 442372
  212.4 2.9 %collective-permute-start.24 = (f32[9,768]{1,0:T(8,128)S(1)}, f32[9,768]{1,0:T(8,128)S(1)}, u32[]{:S(2)}, u32[]{:S(2)}) collective-permute-start(f32[9,768]{1,0:T(8,128)S(1)} %pad_maximum_fusion.5), channel_id=1, source_target_pairs={{0,16},{16,0},{1,17},{17,1},{2,18},{18,2},{3,19},{19,3},{4,20},{20... | collective-permute-start | bytes 82952 | tf_op jit(solution)/shard_map/ppermute | solution.py:767
  215.4 3.8 %collective-permute-start.25 = (f32[9,768]{1,0:T(8,128)S(1)}, f32[9,768]{1,0:T(8,128)S(1)}, u32[]{:S(2)}, u32[]{:S(2)}) collective-permute-start(f32[9,768]{1,0:T(8,128)S(1)} %add.97), channel_id=1, source_target_pairs={{0,2},{2,0},{1,3},{3,1},{4,6},{6,4},{5,7},{7,5},{8,10},{10,8},{9,1... | collective-permute-start | bytes 82952 | tf_op jit(solution)/shard_map/ppermute | solution.py:767
  219.2 21.9 %collective-permute-start.23 = (bf16[2,512,768]{2,1,0:T(8,128)(2,1)}, bf16[2,512,768]{2,1,0:T(8,128)(2,1)S(1)}, u32[]{:S(2)}, u32[]{:S(2)}) collective-permute-start(bf16[2,512,768]{2,1,0:T(8,128)(2,1)} %shard_map.230.own_ref), channel_id=1, source_target_pairs={{1,16},{3,18},{5,20},{7,22},{9,24},{11,26},{13,28},{15,30},{16,1},... | collective-permute-start | bytes 4718600 | tf_op jit(solution)/shard_map/ppermute | solution.py:697
  222.8 12.1 %copy-start.19 = (f32[5]{0:T(128)S(1)}, f32[5]{0:T(128)}, u32[]{:S(2)}) copy-start(f32[5]{0:T(128)} %weight_ref.1) | copy-start | bytes 64
  222.8 18.3 %copy-start.4 = (bf16[2,512,768]{2,1,0:T(8,128)(2,1)S(1)}, bf16[2,512,768]{2,1,0:T(8,128)(2,1)}, u32[]{:S(2)}) copy-start(bf16[2,512,768]{2,1,0:T(8,128)(2,1)} %shard_map.230.own_ref) | copy-start | bytes 4718596
  222.8 18.3 %copy-start.10 = (f32[512,768]{1,0:T(8,128)S(1)}, f32[512,768]{1,0:T(8,128)}, u32[]{:S(2)}) copy-start(f32[512,768]{1,0:T(8,128)} %get-tuple-element.101.part_ref) | copy-start | bytes 4718596
  222.8 18.3 %copy-start.18 = (s32[4]{0:T(128)S(1)}, s32[4]{0:T(128)}, u32[]{:S(2)}) copy-start(s32[4]{0:T(128)} %pad_add_fusion.flags.refs_0_) | copy-start | bytes 52
  224.0 10.3 %collective-permute-start.33 = (bf16[192,1152]{1,0:T(8,128)(2,1)S(1)}, bf16[192,1152]{1,0:T(8,128)(2,1)S(1)}, u32[]{:S(2)}, u32[]{:S(2)}) collective-permute-start(bf16[192,1152]{1,0:T(8,128)(2,1)S(1)} %get-tuple-element.237), channel_id=1, source_target_pairs={{0,2},{2,0},{1,3},{3,1},{4,6},{6,4},{5,7},{7,5},{8,10},{10,8},{9,1... | collective-permute-start | bytes 1327112 | tf_op jit(solution)/shard_map/ppermute | solution.py:716
  224.2 1.2 collective-permute-start.30
  225.4 3.3 %collective-permute-start.31 = (f32[9,768]{1,0:T(8,128)S(1)}, f32[9,768]{1,0:T(8,128)S(1)}, u32[]{:S(2)}, u32[]{:S(2)}) collective-permute-start(f32[9,768]{1,0:T(8,128)S(1)} %add.109), channel_id=1, source_target_pairs={{0,4},{4,0},{8,12},{12,8},{1,5},{5,1},{9,13},{13,9},{2,6},{6,2},{1... | collective-permute-start | bytes 82952 | tf_op jit(solution)/shard_map/ppermute | solution.py:767
  228.7 3.9 %collective-permute-start.32 = (f32[9,768]{1,0:T(8,128)S(1)}, f32[9,768]{1,0:T(8,128)S(1)}, u32[]{:S(2)}, u32[]{:S(2)}) collective-permute-start(f32[9,768]{1,0:T(8,128)S(1)} %add.110), channel_id=1, source_target_pairs={{0,8},{4,12},{8,0},{12,4},{1,9},{5,13},{9,1},{13,5},{2,10},{6,14},... | collective-permute-start | bytes 82952 | tf_op jit(solution)/shard_map/ppermute | solution.py:767
  234.4 10.7 %collective-permute-start.34 = (bf16[2,192,1152]{2,1,0:T(8,128)(2,1)S(1)}, bf16[2,192,1152]{2,1,0:T(8,128)(2,1)S(1)}, u32[]{:S(2)}, u32[]{:S(2)}) collective-permute-start(bf16[2,192,1152]{2,1,0:T(8,128)(2,1)S(1)} %pad_maximum_fusion.3.here_ref), channel_id=1, source_target_pairs={{0,1},{1,0},{2,3},{3,2},{4,5},{5,4},{6,7},{7,6},{8,9},{9,8},{10,11... | collective-permute-start | bytes 2654216 | tf_op jit(solution)/shard_map/ppermute | solution.py:720
  (21 other events, 58.6 us)
Sparse Core Ops, SparseCore 0:
  102.4 46.3 reduce-scatter.9
  155.4 18.4 reduce-scatter.7
  176.2 20.2 reduce-scatter.5

commit v13 on v12

--- a/solution.py
+++ b/solution.py
@@ -651,6 +651,21 @@
     out = ((rows, width), jnp.bfloat16, (ROWS, width), lambda i, *scalars: (i, 0))
     fields = [by_rows(part, ROWS), (own, *both), (got, *both)]
     return streamed(present_kernel, rows // ROWS, [flags, weight], fields, [out] * 2, [], 2, SNUG)
+
+
+def blocks_kernel(flags, early_own, early_got, late_ref, *refs):
+    parts, out_ref = refs[:-1], refs[-1]
+    part = late_ref.shape[1]
+    total = sum(ref[...].astype(jnp.float32) for ref in parts)
+    out_ref[:, :part] = total.astype(jnp.bfloat16)
+    out_ref[:, part : 2 * part] = jnp.where(flags[0] == 1, early_own[...], early_got[...])
+    out_ref[:, 2 * part :] = late_ref[...]
+
+
+def blocks_of(flags, early_own, early_got, late, parts):
+    rows, part = late.shape
+    out = ((rows, 3 * part), jnp.bfloat16)
+    return streamed(blocks_kernel, 1, [flags], [early_own, early_got, late, *parts], [out], [], 1, SNUG)[0]
 
 
 def place_kernel(flags, here_ref, there_ref, qkv_ref, out_ref, up_ref, down_ref):
@@ -873,11 +888,10 @@
     )
     for name in ("near", "dp"):
         small = sum_over(small, name)
-    attn_sum = add(*attn_moved)
-    blocks = jnp.concatenate([attn_sum, jnp.where(same, early_sum, early_got), late_sum], axis=1)
+    blocks = blocks_of(flags, early_sum, early_got, late_sum, attn_moved)
     here = after(jnp.stack([blocks, swap_far(blocks)]), small)
-    output, grad_input = present(flags, dwa_weights, past_sum, ours, theirs)
     grad_w_qkv, grad_w_out, grad_w_up, grad_w_down = place(flags, here, swap_near(here))
+    output, grad_input = present(flags, dwa_weights, past_sum, ours, after(theirs, grad_w_up))
 
     return (
         output[None],

time: 255 us -> 253 us (level)
  waiting for transfers between devices: 32.1 us -> 26.3 us
  starting transfers between devices: 46 us -> 48.6 us
    ppermute x7, waiting for transfers between devices: 5.65 us -> 2.28 us  [swap_diagonal(): lax.ppermute(field, AXES, moves(away, lambda t, d, k, c: (c, d, k, t)))]
    pallas_call x10 -> x11, Pallas kernels: 81.9 us -> 82.6 us  [streamed(): pl.pallas_call(kernel, grid_spec=pltpu.PrefetchScalarGridSpec(num_scalar_...]
  transfers between devices with their start and end apart: 38 -> 38, of which waited for: 11 -> 10; matrix products, arithmetic and copies ran while one was open for 12% -> 13% of each run, Pallas kernels for 46% -> 46%
where the time goes in v13:
time: 253 us; the launch traced here: 252 us
  Pallas kernels  120 us (47%)
  starting transfers between devices  48.6 us (19%)
  waiting for transfers between devices  26.3 us (10%)
  other arithmetic  23.8 us (9%)
  local copies, waits for them, and re-layouts  17.9 us (7%)
  between operations  14.6 us (6%)
    pallas_call x11, Pallas kernels, streamed(): pl.pallas_call(kernel, grid_spec=pltpu.PrefetchScalarGridSpec(num_scalar_...  82.6 us
    ppermute x7, starting transfers between devices, swap_diagonal(): lax.ppermute(field, AXES, moves(away, lambda t, d, k, c: (c, d, k, t)))  23.6 us
    pallas_call x1, Pallas kernels, attend_back(): pl.pallas_call(functools.partial(attend_back_kernel, reach), grid=(width...  19.6 us
    ppermute x5, waiting for transfers between devices, sum_over(): lax.ppermute(field, name, [(d, d ^ bit) for d in range(size)])  13.9 us
    pallas_call x1, Pallas kernels, attend(): pl.pallas_call(functools.partial(attend_kernel, reach), grid=(width // LA...  13.1 us
    unnamed x94, local copies, waits for them, and re-layouts  11.1 us
    ppermute x8, starting transfers between devices, send_to_owner(): lax.ppermute(field, AXES, moves(away if not other_far and (not other_tp)...  10.7 us
  transfers between devices with their start and end apart: 38, of which 10 were waited for; matrix products, arithmetic and copies ran while one was open for 13% of the time, Pallas kernels for 46%

profile of v13, /device:TPU:9, one launch (start us, length us, event | category | flops | bytes accessed | tf_op | source)
XLA Modules:
  0.0 251.8 jit_solution(16064704785891874787)
XLA Ops:
  8.0 3.1 %collective-permute-start = (bf16[512,768]{1,0:T(8,128)(2,1)}, bf16[512,768]{1,0:T(8,128)(2,1)}, u32[]{:S(2)}, u32[]{:S(2)}) collective-permute-start(bf16[512,768]{1,0:T(8,128)(2,1)} %bitcast.45), channel_id=1, source_target_pairs={{1,16},{3,18},{5,20},{7,22},{9,24},{11,26},{13,28},{15,30},{16,1},... | collective-permute-start | bytes 2359304 | tf_op jit(solution)/shard_map/ppermute | solution.py:712
  11.1 2.2 constant_dynamic-slice_fusion
  13.2 2.6 %collective-permute-start.3 = (bf16[3,384,384]{2,1,0:T(8,128)(2,1)}, bf16[3,384,384]{2,1,0:T(8,128)(2,1)S(1)}, u32[]{:S(2)}, u32[]{:S(2)}) collective-permute-start(bf16[3,384,384]{2,1,0:T(8,128)(2,1)} %constant_dynamic-slice_fusion), channel_id=1, source_target_pairs={{1,16},{3,18},{5,20},{7,22},{9,24},{11,26},{13,28},{15,30},{16,1},... | collective-permute-start | bytes 2654216 | tf_op jit(solution)/shard_map/ppermute | solution.py:712
  16.0 2.5 pad_maximum_fusion.2
  18.5 1.9 fusion.9
  20.4 1.6 pad_maximum_fusion.1
  22.0 1.5 pad_maximum_fusion
  23.6 4.3 %shard_map.220 = (bf16[4,512,768]{2,1,0:T(8,128)(2,1)}, f32[512,768]{1,0:T(8,128)}, f32[8,768]{1,0:T(8,128)}) custom-call(f32[5]{0:T(128)} %weight_ref.1, bf16[4,512,768]{2,1,0:T(8,128)(2,1)} %bitcast.43, bf16[512,768]{1,0:T(8,128)(2,1)} %bitcast.41), custom_call_target="tpu_custom_call" | custom-call | bytes 9000000 | tf_op jit(solution)/shard_map/pallas_call | solution.py:627
  29.5 3.1 %collective-permute-start.5 = (bf16[896,768]{1,0:T(8,128)(2,1)}, bf16[896,768]{1,0:T(8,128)(2,1)}, u32[]{:S(2)}, u32[]{:S(2)}) collective-permute-start(bf16[896,768]{1,0:T(8,128)(2,1)} %pad_maximum_fusion.2), channel_id=1, source_target_pairs={{1,16},{3,18},{5,20},{7,22},{9,24},{11,26},{13,28},{15,30},{16,1},... | collective-permute-start | bytes 4128776 | tf_op jit(solution)/shard_map/ppermute | solution.py:712
  32.5 1.2 broadcast_select_fusion.1
  33.9 3.1 %collective-permute-start.4 = (bf16[3,384,384]{2,1,0:T(8,128)(2,1)S(1)}, bf16[3,384,384]{2,1,0:T(8,128)(2,1)S(1)}, u32[]{:S(2)}, u32[]{:S(2)}) collective-permute-start(bf16[3,384,384]{2,1,0:T(8,128)(2,1)S(1)} %collective-permute-done.3.w_near), channel_id=1, source_target_pairs={{1,3},{3,1},{5,7},{7,5},{9,11},{11,9},{13,15},{15,13},{16,18},{18,... | collective-permute-start | bytes 2654216 | tf_op jit(solution)/shard_map/ppermute | solution.py:727
  37.0 0.9 fusion.2.member_ref
  37.9 0.9 select_convert_fusion.apart_ref
  38.8 3.1 %fusion.1 = (f32[1024,128]{1,0:T(8,128)}, f32[1024,128]{1,0:T(8,128)}) fusion(f32[128]{0:T(128)S(1)} %get-tuple-element.241, f32[128]{0:T(128)S(1)} %get-tuple-element.242, f32[1024]{0:T(1024)S(1)} %subtract_convert_fusion), kind=kLoop, calls=%fused_computation.13 | loop fusion | flops 262144 | bytes 1053696 | tf_op jit(solution)/shard_map/mul | solution.py:827
  41.9 2.8 %collective-permute-start.8 = (bf16[1536,768]{1,0:T(8,128)(2,1)}, bf16[1536,768]{1,0:T(8,128)(2,1)}, u32[]{:S(2)}, u32[]{:S(2)}) collective-permute-start(bf16[1536,768]{1,0:T(8,128)(2,1)} %pad_maximum_fusion), channel_id=1, source_target_pairs={{1,16},{3,18},{5,20},{7,22},{9,24},{11,26},{13,28},{15,30},{16,1},... | collective-permute-start | bytes 7077896 | tf_op jit(solution)/shard_map/ppermute | solution.py:712
  44.7 1.8 maximum_select_fusion.rows_ref.refs_2_
  46.5 1.2 collective-permute-done.4.w_far
  47.7 0.9 copy-done.8
  48.6 9.0 %shard_map.221 = (bf16[3,1024,384]{2,1,0:T(8,128)(2,1)}, bf16[768,1024]{1,0:T(8,128)(2,1)}) custom-call(s32[4]{0:T(128)} %pad_add_fusion.flags.refs_0_, bf16[1024,768]{1,0:T(8,128)(2,1)} %maximum_select_fusion.rows_ref.refs_2_, f32[1024,128]{1,0:T(8,128)} %get-tuple-element.106.cos_ref, f32[1024,128]{1,0:T(8,128)} %get-tuple-element.107.sin_ref, ...), custom_call_target="tpu_custom_call" | custom-call | bytes 24000000 | tf_op jit(solution)/shard_map/pallas_call | solution.py:240
  57.6 13.1 %shard_map.222 = (bf16[1024,384]{1,0:T(8,128)(2,1)}, f32[3,8,1024]{2,1,0:T(8,128)}) custom-call(bf16[1024,128]{1,0:T(8,128)(2,1)} %select_convert_fusion.apart_ref, bf16[1024,128]{1,0:T(8,128)(2,1)} %fusion.2.member_ref, bf16[3,1024,384]{2,1,0:T(8,128)(2,1)} %get-tuple-element.109.q_ref.k_ref.v_ref, ...), custom_call_target="tpu_custom_call" | custom-call | bytes 36000000 | tf_op jit(solution)/shard_map/pallas_call | solution.py:104
  70.7 4.0 %collective-permute-start.9 = (bf16[1536,768]{1,0:T(8,128)(2,1)S(1)}, bf16[1536,768]{1,0:T(8,128)(2,1)}, u32[]{:S(2)}, u32[]{:S(2)}) collective-permute-start(bf16[1536,768]{1,0:T(8,128)(2,1)S(1)} %copy-done.28), channel_id=1, source_target_pairs={{1,16},{3,18},{5,20},{7,22},{9,24},{11,26},{13,28},{15,30},{16,1},... | collective-permute-start | bytes 7077896 | tf_op jit(solution)/shard_map/ppermute | solution.py:712
  74.7 1.7 broadcast_select_fusion.w_ref
  76.4 1.0 convolution_convert_fusion.refs_3_
  78.1 3.9 %collective-permute-done.7.refs_6_ = bf16[512,768]{1,0:T(8,128)(2,1)S(1)} collective-permute-done((bf16[512,768]{1,0:T(8,128)(2,1)S(1)}, bf16[512,768]{1,0:T(8,128)(2,1)S(1)}, u32[]{:S(2)}, u32[]{:S(2)}) %collective-permute-start.7) | collective-permute-done | bytes 786464 | tf_op jit(solution)/shard_map/ppermute | solution.py:735
  82.0 0.9 copy-done.32
  82.9 19.3 %shard_map.223 = (bf16[1024,768]{1,0:T(8,128)(2,1)}, bf16[768,1024]{1,0:T(8,128)(2,1)}, bf16[1024,768]{1,0:T(8,128)(2,1)}, bf16[768,1024]{1,0:T(8,128)(2,1)}, bf...) custom-call(s32[4]{0:T(128)} %pad_add_fusion.flags.refs_0_, ...), custom_call_target="tpu_custom_call" | custom-call | bytes 51000000 | tf_op jit(solution)/shard_map/pallas_call | solution.py:240
  102.3 16.3 %shard_map.224 = (bf16[1024,768]{1,0:T(8,128)(2,1)}, bf16[1024,768]{1,0:T(8,128)(2,1)}, bf16[768,768]{1,0:T(8,128)(2,1)}, bf16[768,384]{1,0:T(8,128)(2,1)}, bf16...) custom-call(s32[4]{0:T(128)} %pad_add_fusion.flags.refs_0_, ...), custom_call_target="tpu_custom_call" | custom-call | bytes 51000000 | tf_op jit(solution)/shard_map/pallas_call | solution.py:240
  119.4 2.3 collective-permute-start.13
  121.7 2.8 %collective-permute-start.11 = (bf16[768,384]{1,0:T(8,128)(2,1)}, bf16[768,384]{1,0:T(8,128)(2,1)S(1)}, u32[]{:S(2)}, u32[]{:S(2)}) collective-permute-start(bf16[768,384]{1,0:T(8,128)(2,1)} %get-tuple-element.125), channel_id=1, source_target_pairs={{1,16},{3,18},{5,20},{7,22},{9,24},{11,26},{13,28},{15,30},{16,1},... | collective-permute-start | bytes 1769480 | tf_op jit(solution)/shard_map/ppermute | solution.py:716
  124.6 1.1 copy-done.29
  125.7 9.3 %shard_map.225 = (bf16[1024,768]{1,0:T(8,128)(2,1)}, bf16[1024,384]{1,0:T(8,128)(2,1)}, bf16[768,384]{1,0:T(8,128)(2,1)}, f32[8,768]{1,0:T(8,128)}) custom-call(s32[4]{0:T(128)} %pad_add_fusion.flags.refs_0_, bf16[1024,768]{1,0:T(8,128)(2,1)} %get-tuple-element.114.resid_ref, bf16[1024,768]{1,0:T(8,128)(2,1)} %get-tuple-element.137.refs_3_.cot_ref, ...), custom_call_target="tpu_custom_call" | custom-call | bytes 24000000 | tf_op jit(solution)/shard_map/pallas_call | solution.py:240
  134.9 19.6 %shard_map.226.query_ref.key_ref.value_ref.grad_ref = bf16[3,1024,384]{2,1,0:T(8,128)(2,1)} custom-call(bf16[1024,128]{1,0:T(8,128)(2,1)} %select_convert_fusion.apart_ref, bf16[1024,128]{1,0:T(8,128)(2,1)} %fusion.2.member_ref, f32[1024,128]{1,0:T(8,128)} %get-tuple-element.106.cos_ref, f32[1024,128]{1,0:T(8,128)} %get-tuple-element.107.sin_ref, ...), custom_call_target="tpu_custom_call" | custom-call | bytes 66000000 | tf_op jit(solution)/shard_map/pallas_call | solution.py:189
  155.3 7.1 %shard_map.227 = (bf16[768,384]{1,0:T(8,128)(2,1)}, bf16[768,384]{1,0:T(8,128)(2,1)}, bf16[768,384]{1,0:T(8,128)(2,1)}, bf16[768,384]{1,0:T(8,128)(2,1)}) custom-call(s32[4]{0:T(128)} %pad_add_fusion.flags.refs_0_, bf16[768,1024]{1,0:T(8,128)(2,1)} %get-tuple-element.130.turned_ref, bf16[768,384]{1,0:T(8,128)(2,1)} %get-tuple-element.131.out_grad_ref, ...), custom_call_target="tpu_custom_call" | custom-call | bytes 12000000 | tf_op jit(solution)/shard_map/pallas_call | solution.py:240
  162.4 3.1 %collective-permute-start.15 = (bf16[768,384]{1,0:T(8,128)(2,1)}, bf16[768,384]{1,0:T(8,128)(2,1)}, u32[]{:S(2)}, u32[]{:S(2)}) collective-permute-start(bf16[768,384]{1,0:T(8,128)(2,1)} %get-tuple-element.132), channel_id=1, source_target_pairs={{1,16},{3,18},{5,20},{7,22},{9,24},{11,26},{13,28},{15,30},{16,1},... | collective-permute-start | bytes 1769480 | tf_op jit(solution)/shard_map/ppermute | solution.py:716
  165.5 1.6 collective-permute-start.17
  167.5 3.0 %add_convert_fusion = bf16[768,384]{1,0:T(8,128)(2,1)} fusion(bf16[768,384]{1,0:T(8,128)(2,1)} %copy-done.36, bf16[768,384]{1,0:T(8,128)(2,1)} %copy-done.35, bf16[768,384]{1,0:T(8,128)(2,1)} %copy-done.34, bf16[768,384]{1,0:T(8,128)(2,1)} %get-tuple-element.125, bf16[768,384]{1,0:T(8,128)(2,1)} %copy-done.37, pred[]{:T(512)S(6)} %eq.35), kind=kLoop, calls=%fused_computation.6 | loop fusion | flops 2654208 | bytes 3538945 | tf_op jit(solution)/shard_map/convert_element_type | solution.py:754
  170.6 1.3 slice.42
  171.9 1.4 copy-done.1
  173.3 1.5 copy-done.3
  174.8 1.2 copy-done.9
  176.0 6.1 %shard_map.228 = (bf16[512,768]{1,0:T(8,128)(2,1)S(1)}, bf16[256,768]{1,0:T(8,128)(2,1)}, bf16[256,768]{1,0:T(8,128)(2,1)}, f32[8,768]{1,0:T(8,128)S(1)}) custom-call(s32[4]{0:T(128)S(1)} %copy-done.19, bf16[3,1024,384]{2,1,0:T(8,128)(2,1)S(1)} %copy-done, bf16[1024,768]{1,0:T(8,128)(2,1)S(1)} %copy-done.1, bf16[3,768,384]{2,1,0:T(8,128)(2,1)S(1)} %copy-done.3, ...), custom_call_target="tpu_custom_call" | custom-call | bytes 15000000 | tf_op jit(solution)/shard_map/pallas_call | solution.py:240
  182.2 0.9 copy-done.15
  183.1 1.3 copy-done.14
  184.3 4.9 %shard_map.229 = (bf16[512,768]{1,0:T(8,128)(2,1)S(1)}, bf16[256,768]{1,0:T(8,128)(2,1)S(1)}, bf16[256,768]{1,0:T(8,128)(2,1)S(1)}, f32[8,768]{1,0:T(8,128)S(1)}) custom-call(s32[4]{0:T(128)S(1)} %copy-done.19, bf16[1024,768]{1,0:T(8,128)(2,1)S(1)} %copy-done.11, bf16[1024,768]{1,0:T(8,128)(2,1)S(1)} %copy-done.12, bf16[1024,768]{1,0:T(8,128)(2,1)S(1)} %copy-done.5, ...), custom_call_target="tpu_custom_call" | custom-call | bytes 18000000 | tf_op jit(solution)/shard_map/pallas_call | solution.py:240
  189.2 0.9 copy-done.16
  190.1 4.3 %collective-permute-done.18 = bf16[768,384]{1,0:T(8,128)(2,1)} collective-permute-done((bf16[768,384]{1,0:T(8,128)(2,1)}, bf16[768,384]{1,0:T(8,128)(2,1)}, u32[]{:S(2)}, u32[]{:S(2)}) %collective-permute-start.18) | collective-permute-done | bytes 589856 | tf_op jit(solution)/shard_map/ppermute | solution.py:716
  195.5 2.0 add_convert_fusion.1
  198.4 2.1 collective-permute-start.28
  200.5 2.3 collective-permute-start.27
  202.7 4.5 %collective-permute-start.26 = (bf16[192,384]{1,0:T(8,128)(2,1)}, bf16[192,384]{1,0:T(8,128)(2,1)S(1)}, u32[]{:S(2)}, u32[]{:S(2)}) collective-permute-start(bf16[192,384]{1,0:T(8,128)(2,1)} %reduce-scatter.8.cloned.1.call-done.early_own), channel_id=1, source_target_pairs={{1,16},{3,18},{5,20},{7,22},{9,24},{11,26},{13,28},{15,30},{16,1},... | collective-permute-start | bytes 442376 | tf_op jit(solution)/shard_map/ppermute | solution.py:712
  207.3 5.3 %shard_map.230.own_ref = bf16[2,512,768]{2,1,0:T(8,128)(2,1)} custom-call(s32[4]{0:T(128)} %pad_add_fusion.flags.refs_0_, bf16[1024,768]{1,0:T(8,128)(2,1)} %maximum_select_fusion.rows_ref.refs_2_, bf16[1024,768]{1,0:T(8,128)(2,1)} %get-tuple-element.122.resid_ref, bf16[512,768]{1,0:T(8,128)(2,1)} %copy-done.15, bf16[512,768]{1,0:T(8,128)(2,1)} %copy-done.16, ...), custom_call_target="tpu_custom_call" | custom-call | bytes 9000000 | tf_op jit(solution)/shard_map/pallas_call | solution.py:240
  212.7 2.9 %collective-permute-done.24 = f32[9,768]{1,0:T(8,128)S(1)} collective-permute-done((f32[9,768]{1,0:T(8,128)S(1)}, f32[9,768]{1,0:T(8,128)S(1)}, u32[]{:S(2)}, u32[]{:S(2)}) %collective-permute-start.24) | collective-permute-done | bytes 27680 | tf_op jit(solution)/shard_map/ppermute | solution.py:782
  215.9 3.5 %collective-permute-done.25 = f32[9,768]{1,0:T(8,128)S(1)} collective-permute-done((f32[9,768]{1,0:T(8,128)S(1)}, f32[9,768]{1,0:T(8,128)S(1)}, u32[]{:S(2)}, u32[]{:S(2)}) %collective-permute-start.25) | collective-permute-done | bytes 27680 | tf_op jit(solution)/shard_map/ppermute | solution.py:782
  219.5 0.9 copy-done.18
  221.4 3.7 %collective-permute-start.23 = (bf16[2,512,768]{2,1,0:T(8,128)(2,1)S(1)}, bf16[2,512,768]{2,1,0:T(8,128)(2,1)S(1)}, u32[]{:S(2)}, u32[]{:S(2)}) collective-permute-start(bf16[2,512,768]{2,1,0:T(8,128)(2,1)S(1)} %copy-done.4), channel_id=1, source_target_pairs={{1,16},{3,18},{5,20},{7,22},{9,24},{11,26},{13,28},{15,30},{16,1},... | collective-permute-start | bytes 4718600 | tf_op jit(solution)/shard_map/ppermute | solution.py:712
  225.1 1.2 collective-permute-done.31
  226.4 3.2 %collective-permute-done.32 = f32[9,768]{1,0:T(8,128)S(1)} collective-permute-done((f32[9,768]{1,0:T(8,128)S(1)}, f32[9,768]{1,0:T(8,128)S(1)}, u32[]{:S(2)}, u32[]{:S(2)}) %collective-permute-start.32) | collective-permute-done | bytes 27680 | tf_op jit(solution)/shard_map/ppermute | solution.py:782
  229.7 0.9 collective-permute-start.33
  230.6 3.0 %collective-permute-done.33 = f32[9,768]{1,0:T(8,128)S(1)} collective-permute-done((f32[9,768]{1,0:T(8,128)S(1)}, f32[9,768]{1,0:T(8,128)S(1)}, u32[]{:S(2)}, u32[]{:S(2)}) %collective-permute-start.33) | collective-permute-done | bytes 27680 | tf_op jit(solution)/shard_map/ppermute | solution.py:782
  233.8 2.1 collective-permute-start.34
  236.5 1.3 slice_reduce_fusion
  238.4 2.5 shard_map.232
  240.9 2.3 collective-permute-done.23.got_ref
  243.2 2.1 shard_map.233
  (168 shorter events, 10.1 us)
Async XLA Ops:
  7.2 8.7 %copy-start.42 = (f32[768]{0:T(1024)S(1)}, f32[768]{0:T(1024)}, u32[]{:S(2)}) copy-start(f32[768]{0:T(1024)} %param.18) | copy-start | bytes 9220
  7.2 8.8 %copy-start.43 = (f32[768]{0:T(1024)S(1)}, f32[768]{0:T(1024)}, u32[]{:S(2)}) copy-start(f32[768]{0:T(1024)} %param.19) | copy-start | bytes 9220
  7.2 8.8 %copy-start.44 = (f32[768]{0:T(1024)S(1)}, f32[768]{0:T(1024)}, u32[]{:S(2)}) copy-start(f32[768]{0:T(1024)} %param.22) | copy-start | bytes 9220
  7.2 8.8 %copy-start.45 = (f32[768]{0:T(1024)S(1)}, f32[768]{0:T(1024)}, u32[]{:S(2)}) copy-start(f32[768]{0:T(1024)} %param.23) | copy-start | bytes 9220
  7.2 148.0 %reduce-scatter.10.cloned.1.call-start = ((), (), s32[]{:S(2)}) async-start(), calls=%async_computation.5 | async-start | bytes 2949120
  7.3 21.8 %collective-permute-start.2 = (s32[1,3]{1,0:T(1,128)}, s32[1,3]{1,0:T(1,128)S(1)}, u32[]{:S(2)}, u32[]{:S(2)}) collective-permute-start(s32[1,3]{1,0:T(1,128)} %param.16), channel_id=1, source_target_pairs={{0,1},{1,0},{2,3},{3,2},{4,5},{5,4},{6,7},{7,6},{8,9},{9,8},{10,11... | collective-permute-start | bytes 44 | tf_op jit(solution)/shard_map/ppermute | solution.py:735
  8.0 21.4 %collective-permute-start = (bf16[512,768]{1,0:T(8,128)(2,1)}, bf16[512,768]{1,0:T(8,128)(2,1)}, u32[]{:S(2)}, u32[]{:S(2)}) collective-permute-start(bf16[512,768]{1,0:T(8,128)(2,1)} %bitcast.45), channel_id=1, source_target_pairs={{1,16},{3,18},{5,20},{7,22},{9,24},{11,26},{13,28},{15,30},{16,1},... | collective-permute-start | bytes 2359304 | tf_op jit(solution)/shard_map/ppermute | solution.py:712
  13.2 20.6 %collective-permute-start.3 = (bf16[3,384,384]{2,1,0:T(8,128)(2,1)}, bf16[3,384,384]{2,1,0:T(8,128)(2,1)S(1)}, u32[]{:S(2)}, u32[]{:S(2)}) collective-permute-start(bf16[3,384,384]{2,1,0:T(8,128)(2,1)} %constant_dynamic-slice_fusion), channel_id=1, source_target_pairs={{1,16},{3,18},{5,20},{7,22},{9,24},{11,26},{13,28},{15,30},{16,1},... | collective-permute-start | bytes 2654216 | tf_op jit(solution)/shard_map/ppermute | solution.py:712
  23.6 9.0 %copy-start.31 = (bf16[1,512,768]{2,1,0:T(8,128)(2,1)S(1)}, bf16[1,512,768]{2,1,0:T(8,128)(2,1)}, u32[]{:S(2)}) copy-start(bf16[1,512,768]{2,1,0:T(8,128)(2,1)} %param.13) | copy-start | bytes 2359300
  29.5 45.2 %collective-permute-start.5 = (bf16[896,768]{1,0:T(8,128)(2,1)}, bf16[896,768]{1,0:T(8,128)(2,1)}, u32[]{:S(2)}, u32[]{:S(2)}) collective-permute-start(bf16[896,768]{1,0:T(8,128)(2,1)} %pad_maximum_fusion.2), channel_id=1, source_target_pairs={{1,16},{3,18},{5,20},{7,22},{9,24},{11,26},{13,28},{15,30},{16,1},... | collective-permute-start | bytes 4128776 | tf_op jit(solution)/shard_map/ppermute | solution.py:712
  33.8 10.9 %collective-permute-start.1 = (bf16[512,768]{1,0:T(8,128)(2,1)S(1)}, bf16[512,768]{1,0:T(8,128)(2,1)S(1)}, u32[]{:S(2)}, u32[]{:S(2)}) collective-permute-start(bf16[512,768]{1,0:T(8,128)(2,1)S(1)} %broadcast_select_fusion.1), channel_id=1, source_target_pairs={{0,1},{1,0},{2,3},{3,2},{4,5},{5,4},{6,7},{7,6},{8,9},{9,8},{10,11... | collective-permute-start | bytes 2359304 | tf_op jit(solution)/shard_map/ppermute | solution.py:735
  33.9 12.6 %copy-start.6 = (bf16[3,384,384]{2,1,0:T(8,128)(2,1)}, bf16[3,384,384]{2,1,0:T(8,128)(2,1)S(1)}, u32[]{:S(2)}) copy-start(bf16[3,384,384]{2,1,0:T(8,128)(2,1)S(1)} %collective-permute-done.3.w_near) | copy-start | bytes 2654212
  33.9 13.8 %collective-permute-start.4 = (bf16[3,384,384]{2,1,0:T(8,128)(2,1)S(1)}, bf16[3,384,384]{2,1,0:T(8,128)(2,1)S(1)}, u32[]{:S(2)}, u32[]{:S(2)}) collective-permute-start(bf16[3,384,384]{2,1,0:T(8,128)(2,1)S(1)} %collective-permute-done.3.w_near), channel_id=1, source_target_pairs={{1,3},{3,1},{5,7},{7,5},{9,11},{11,9},{13,15},{15,13},{16,18},{18,... | collective-permute-start | bytes 2654216 | tf_op jit(solution)/shard_map/ppermute | solution.py:727
  41.9 40.1 %collective-permute-start.8 = (bf16[1536,768]{1,0:T(8,128)(2,1)}, bf16[1536,768]{1,0:T(8,128)(2,1)}, u32[]{:S(2)}, u32[]{:S(2)}) collective-permute-start(bf16[1536,768]{1,0:T(8,128)(2,1)} %pad_maximum_fusion), channel_id=1, source_target_pairs={{1,16},{3,18},{5,20},{7,22},{9,24},{11,26},{13,28},{15,30},{16,1},... | collective-permute-start | bytes 7077896 | tf_op jit(solution)/shard_map/ppermute | solution.py:712
  57.5 13.1 %copy-start.28 = (bf16[1536,768]{1,0:T(8,128)(2,1)S(1)}, bf16[1536,768]{1,0:T(8,128)(2,1)}, u32[]{:S(2)}) copy-start(bf16[1536,768]{1,0:T(8,128)(2,1)} %pad_maximum_fusion.1) | copy-start | bytes 7077892
  57.5 17.1 %copy-start.24 = (bf16[1,512,768]{2,1,0:T(8,128)(2,1)S(1)}, bf16[1,512,768]{2,1,0:T(8,128)(2,1)}, u32[]{:S(2)}) copy-start(bf16[1,512,768]{2,1,0:T(8,128)(2,1)} %param.15) | copy-start | bytes 2359300
  57.5 17.1 %copy-start.27 = (bf16[384,768]{1,0:T(8,128)(2,1)S(1)}, bf16[384,768]{1,0:T(8,128)(2,1)}, u32[]{:S(2)}) copy-start(bf16[384,768]{1,0:T(8,128)(2,1)} %param.21) | copy-start | bytes 1769476
  70.7 31.5 %collective-permute-start.9 = (bf16[1536,768]{1,0:T(8,128)(2,1)S(1)}, bf16[1536,768]{1,0:T(8,128)(2,1)}, u32[]{:S(2)}, u32[]{:S(2)}) collective-permute-start(bf16[1536,768]{1,0:T(8,128)(2,1)S(1)} %copy-done.28), channel_id=1, source_target_pairs={{1,16},{3,18},{5,20},{7,22},{9,24},{11,26},{13,28},{15,30},{16,1},... | collective-permute-start | bytes 7077896 | tf_op jit(solution)/shard_map/ppermute | solution.py:712
  77.4 5.5 %collective-permute-start.6 = (bf16[1024,768]{1,0:T(8,128)(2,1)S(1)}, bf16[1024,768]{1,0:T(8,128)(2,1)}, u32[]{:S(2)}, u32[]{:S(2)}) collective-permute-start(bf16[1024,768]{1,0:T(8,128)(2,1)S(1)} %convolution_convert_fusion.refs_3_), channel_id=1, source_target_pairs={{0,1},{1,0},{2,3},{3,2},{4,5},{5,4},{6,7},{7,6},{8,9},{9,8},{10,11... | collective-permute-start | bytes 4718600 | tf_op jit(solution)/shard_map/ppermute | solution.py:735
  77.5 4.4 %collective-permute-start.7 = (bf16[512,768]{1,0:T(8,128)(2,1)S(1)}, bf16[512,768]{1,0:T(8,128)(2,1)S(1)}, u32[]{:S(2)}, u32[]{:S(2)}) collective-permute-start(bf16[512,768]{1,0:T(8,128)(2,1)S(1)} %slice.53.refs_5_), channel_id=1, source_target_pairs={{0,1},{1,0},{2,3},{3,2},{4,5},{5,4},{6,7},{7,6},{8,9},{9,8},{10,11... | collective-permute-start | bytes 2359304 | tf_op jit(solution)/shard_map/ppermute | solution.py:735
  102.2 96.2 %reduce-scatter.8.cloned.1.call-start = ((), (), s32[]{:S(2)}) async-start(), calls=%async_computation.4 | async-start | bytes 737280 | tf_op jit(solution)/shard_map/reduce_scatter | solution.py:762
  118.6 5.9 %collective-permute-start.10 = (bf16[1024,768]{1,0:T(8,128)(2,1)}, bf16[1024,768]{1,0:T(8,128)(2,1)S(1)}, u32[]{:S(2)}, u32[]{:S(2)}) collective-permute-start(bf16[1024,768]{1,0:T(8,128)(2,1)} %get-tuple-element.121.back_own), channel_id=1, source_target_pairs={{0,1},{1,0},{2,3},{3,2},{4,5},{5,4},{6,7},{7,6},{8,9},{9,8},{10,11... | collective-permute-start | bytes 4718600 | tf_op jit(solution)/shard_map/ppermute | solution.py:735
  118.8 35.7 %collective-permute-start.12 = (bf16[768,384]{1,0:T(8,128)(2,1)}, bf16[768,384]{1,0:T(8,128)(2,1)S(1)}, u32[]{:S(2)}, u32[]{:S(2)}) collective-permute-start(bf16[768,384]{1,0:T(8,128)(2,1)} %get-tuple-element.126), channel_id=1, source_target_pairs={{0,1},{1,17},{2,3},{3,19},{4,5},{5,21},{6,7},{7,23},{8,9},{9,25},{... | collective-permute-start | bytes 1769480 | tf_op jit(solution)/shard_map/ppermute | solution.py:716
  119.4 35.1 %collective-permute-start.13 = (bf16[768,384]{1,0:T(8,128)(2,1)}, bf16[768,384]{1,0:T(8,128)(2,1)S(1)}, u32[]{:S(2)}, u32[]{:S(2)}) collective-permute-start(bf16[768,384]{1,0:T(8,128)(2,1)} %get-tuple-element.127), channel_id=1, source_target_pairs={{0,2},{1,18},{2,0},{3,16},{4,6},{5,22},{6,4},{7,20},{8,10},{9,26},... | collective-permute-start | bytes 1769480 | tf_op jit(solution)/shard_map/ppermute | solution.py:716
  121.7 33.4 %collective-permute-start.14 = (bf16[768,384]{1,0:T(8,128)(2,1)}, bf16[768,384]{1,0:T(8,128)(2,1)S(1)}, u32[]{:S(2)}, u32[]{:S(2)}) collective-permute-start(bf16[768,384]{1,0:T(8,128)(2,1)} %get-tuple-element.128), channel_id=1, source_target_pairs={{0,3},{1,19},{2,1},{3,17},{4,7},{5,23},{6,5},{7,21},{8,11},{9,27},... | collective-permute-start | bytes 1769480 | tf_op jit(solution)/shard_map/ppermute | solution.py:716
  121.7 33.4 %collective-permute-start.11 = (bf16[768,384]{1,0:T(8,128)(2,1)}, bf16[768,384]{1,0:T(8,128)(2,1)S(1)}, u32[]{:S(2)}, u32[]{:S(2)}) collective-permute-start(bf16[768,384]{1,0:T(8,128)(2,1)} %get-tuple-element.125), channel_id=1, source_target_pairs={{1,16},{3,18},{5,20},{7,22},{9,24},{11,26},{13,28},{15,30},{16,1},... | collective-permute-start | bytes 1769480 | tf_op jit(solution)/shard_map/ppermute | solution.py:716
  154.5 7.9 %copy-start.34 = (bf16[768,384]{1,0:T(8,128)(2,1)}, bf16[768,384]{1,0:T(8,128)(2,1)S(1)}, u32[]{:S(2)}) copy-start(bf16[768,384]{1,0:T(8,128)(2,1)S(1)} %collective-permute-done.12) | copy-start | bytes 1769476
  154.6 7.8 %copy-start.35 = (bf16[768,384]{1,0:T(8,128)(2,1)}, bf16[768,384]{1,0:T(8,128)(2,1)S(1)}, u32[]{:S(2)}) copy-start(bf16[768,384]{1,0:T(8,128)(2,1)S(1)} %collective-permute-done.13) | copy-start | bytes 1769476
  155.2 7.2 %copy-start.36 = (bf16[768,384]{1,0:T(8,128)(2,1)}, bf16[768,384]{1,0:T(8,128)(2,1)S(1)}, u32[]{:S(2)}) copy-start(bf16[768,384]{1,0:T(8,128)(2,1)S(1)} %collective-permute-done.14) | copy-start | bytes 1769476
  155.2 7.2 %copy-start.37 = (bf16[768,384]{1,0:T(8,128)(2,1)}, bf16[768,384]{1,0:T(8,128)(2,1)S(1)}, u32[]{:S(2)}) copy-start(bf16[768,384]{1,0:T(8,128)(2,1)S(1)} %collective-permute-done.11) | copy-start | bytes 1769476
  155.2 64.2 %reduce-scatter.6.cloned.1.call-start = ((), (), s32[]{:S(2)}) async-start(), calls=%async_computation.3 | async-start | bytes 737280 | tf_op jit(solution)/shard_map/reduce_scatter | solution.py:762
  162.4 32.0 %collective-permute-start.15 = (bf16[768,384]{1,0:T(8,128)(2,1)}, bf16[768,384]{1,0:T(8,128)(2,1)}, u32[]{:S(2)}, u32[]{:S(2)}) collective-permute-start(bf16[768,384]{1,0:T(8,128)(2,1)} %get-tuple-element.132), channel_id=1, source_target_pairs={{1,16},{3,18},{5,20},{7,22},{9,24},{11,26},{13,28},{15,30},{16,1},... | collective-permute-start | bytes 1769480 | tf_op jit(solution)/shard_map/ppermute | solution.py:716
  165.5 24.6 %collective-permute-start.16 = (bf16[768,384]{1,0:T(8,128)(2,1)}, bf16[768,384]{1,0:T(8,128)(2,1)}, u32[]{:S(2)}, u32[]{:S(2)}) collective-permute-start(bf16[768,384]{1,0:T(8,128)(2,1)} %get-tuple-element.145), channel_id=1, source_target_pairs={{0,1},{1,17},{2,3},{3,19},{4,5},{5,21},{6,7},{7,23},{8,9},{9,25},{... | collective-permute-start | bytes 1769480 | tf_op jit(solution)/shard_map/ppermute | solution.py:716
  165.5 24.6 %collective-permute-start.17 = (bf16[768,384]{1,0:T(8,128)(2,1)}, bf16[768,384]{1,0:T(8,128)(2,1)}, u32[]{:S(2)}, u32[]{:S(2)}) collective-permute-start(bf16[768,384]{1,0:T(8,128)(2,1)} %get-tuple-element.146), channel_id=1, source_target_pairs={{0,2},{1,18},{2,0},{3,16},{4,6},{5,22},{6,4},{7,20},{8,10},{9,26},... | collective-permute-start | bytes 1769480 | tf_op jit(solution)/shard_map/ppermute | solution.py:716
  167.1 27.3 %collective-permute-start.18 = (bf16[768,384]{1,0:T(8,128)(2,1)}, bf16[768,384]{1,0:T(8,128)(2,1)}, u32[]{:S(2)}, u32[]{:S(2)}) collective-permute-start(bf16[768,384]{1,0:T(8,128)(2,1)} %get-tuple-element.147), channel_id=1, source_target_pairs={{0,3},{1,19},{2,1},{3,17},{4,7},{5,23},{6,5},{7,21},{8,11},{9,27},... | collective-permute-start | bytes 1769480 | tf_op jit(solution)/shard_map/ppermute | solution.py:716
  176.0 7.1 %copy-start.2 = (bf16[1024,768]{1,0:T(8,128)(2,1)S(1)}, bf16[1024,768]{1,0:T(8,128)(2,1)}, u32[]{:S(2)}) copy-start(bf16[1024,768]{1,0:T(8,128)(2,1)} %get-tuple-element.137.refs_3_.cot_ref) | copy-start | bytes 4718596
  176.0 7.1 %copy-start.5 = (bf16[1024,768]{1,0:T(8,128)(2,1)S(1)}, bf16[1024,768]{1,0:T(8,128)(2,1)}, u32[]{:S(2)}) copy-start(bf16[1024,768]{1,0:T(8,128)(2,1)} %get-tuple-element.114.resid_ref) | copy-start | bytes 4718596
  176.0 7.1 %copy-start.11 = (bf16[1024,768]{1,0:T(8,128)(2,1)S(1)}, bf16[1024,768]{1,0:T(8,128)(2,1)}, u32[]{:S(2)}) copy-start(bf16[1024,768]{1,0:T(8,128)(2,1)} %get-tuple-element.135.act_early) | copy-start | bytes 4718596
  176.0 7.1 %copy-start.12 = (bf16[1024,768]{1,0:T(8,128)(2,1)S(1)}, bf16[1024,768]{1,0:T(8,128)(2,1)}, u32[]{:S(2)}) copy-start(bf16[1024,768]{1,0:T(8,128)(2,1)} %get-tuple-element.136.act_late) | copy-start | bytes 4718596
  176.0 7.1 %copy-start.13 = (bf16[768,768]{1,0:T(8,128)(2,1)S(1)}, bf16[768,768]{1,0:T(8,128)(2,1)}, u32[]{:S(2)}) copy-start(bf16[768,768]{1,0:T(8,128)(2,1)} %get-tuple-element.138.early_ref) | copy-start | bytes 3538948
  184.3 11.2 %copy-start.33 = (bf16[768,384]{1,0:T(8,128)(2,1)S(1)}, bf16[768,384]{1,0:T(8,128)(2,1)}, u32[]{:S(2)}) copy-start(bf16[768,384]{1,0:T(8,128)(2,1)} %get-tuple-element.132) | copy-start | bytes 1769476
  194.5 12.8 %copy-start.40 = (f32[2,768]{1,0:T(2,128)S(1)}, f32[2,768]{1,0:T(2,128)}, u32[]{:S(2)}) copy-start(f32[2,768]{1,0:T(2,128)} %slice.42) | copy-start | bytes 18436
  194.5 3.9 %collective-permute-start.19 = (bf16[256,768]{1,0:T(8,128)(2,1)}, bf16[256,768]{1,0:T(8,128)(2,1)S(1)}, u32[]{:S(2)}, u32[]{:S(2)}) collective-permute-start(bf16[256,768]{1,0:T(8,128)(2,1)} %get-tuple-element.155), channel_id=1, source_target_pairs={{0,1},{1,0},{2,3},{3,2},{4,5},{5,4},{6,7},{7,6},{8,9},{9,8},{10,11... | collective-permute-start | bytes 1179656 | tf_op jit(solution)/shard_map/ppermute | solution.py:735
  194.7 5.8 %collective-permute-start.20 = (bf16[256,768]{1,0:T(8,128)(2,1)}, bf16[256,768]{1,0:T(8,128)(2,1)S(1)}, u32[]{:S(2)}, u32[]{:S(2)}) collective-permute-start(bf16[256,768]{1,0:T(8,128)(2,1)} %get-tuple-element.156), channel_id=1, source_target_pairs={{0,1},{1,0},{2,3},{3,2},{4,5},{5,4},{6,7},{7,6},{8,9},{9,8},{10,11... | collective-permute-start | bytes 1179656 | tf_op jit(solution)/shard_map/ppermute | solution.py:735
  195.0 7.8 %collective-permute-start.21 = (bf16[256,768]{1,0:T(8,128)(2,1)S(1)}, bf16[256,768]{1,0:T(8,128)(2,1)}, u32[]{:S(2)}, u32[]{:S(2)}) collective-permute-start(bf16[256,768]{1,0:T(8,128)(2,1)S(1)} %get-tuple-element.157), channel_id=1, source_target_pairs={{0,1},{1,0},{2,3},{3,2},{4,5},{5,4},{6,7},{7,6},{8,9},{9,8},{10,11... | collective-permute-start | bytes 1179656 | tf_op jit(solution)/shard_map/ppermute | solution.py:735
  195.2 12.1 %collective-permute-start.22 = (bf16[256,768]{1,0:T(8,128)(2,1)S(1)}, bf16[256,768]{1,0:T(8,128)(2,1)}, u32[]{:S(2)}, u32[]{:S(2)}) collective-permute-start(bf16[256,768]{1,0:T(8,128)(2,1)S(1)} %get-tuple-element.158), channel_id=1, source_target_pairs={{0,1},{1,0},{2,3},{3,2},{4,5},{5,4},{6,7},{7,6},{8,9},{9,8},{10,11... | collective-permute-start | bytes 1179656 | tf_op jit(solution)/shard_map/ppermute | solution.py:735
  198.2 21.2 %collective-permute-start.29 = (bf16[192,384]{1,0:T(8,128)(2,1)}, bf16[192,384]{1,0:T(8,128)(2,1)S(1)}, u32[]{:S(2)}, u32[]{:S(2)}) collective-permute-start(bf16[192,384]{1,0:T(8,128)(2,1)} %get-tuple-element.234), channel_id=1, source_target_pairs={{0,12},{4,0},{8,4},{12,8},{1,13},{5,1},{9,5},{13,9},{2,14},{6,2},{... | collective-permute-start | bytes 442376 | tf_op jit(solution)/shard_map/ppermute | solution.py:774
  198.4 8.9 %copy-start.38 = (bf16[256,768]{1,0:T(8,128)(2,1)}, bf16[256,768]{1,0:T(8,128)(2,1)S(1)}, u32[]{:S(2)}) copy-start(bf16[256,768]{1,0:T(8,128)(2,1)S(1)} %collective-permute-done.19.got_first) | copy-start | bytes 1179652
  198.4 21.0 %collective-permute-start.28 = (bf16[192,384]{1,0:T(8,128)(2,1)S(1)}, bf16[192,384]{1,0:T(8,128)(2,1)S(1)}, u32[]{:S(2)}, u32[]{:S(2)}) collective-permute-start(bf16[192,384]{1,0:T(8,128)(2,1)S(1)} %get-tuple-element.235), channel_id=1, source_target_pairs={{0,8},{4,12},{8,0},{12,4},{1,9},{5,13},{9,1},{13,5},{2,10},{6,14},... | collective-permute-start | bytes 442376 | tf_op jit(solution)/shard_map/ppermute | solution.py:774
  200.5 19.0 %collective-permute-start.27 = (bf16[192,384]{1,0:T(8,128)(2,1)S(1)}, bf16[192,384]{1,0:T(8,128)(2,1)S(1)}, u32[]{:S(2)}, u32[]{:S(2)}) collective-permute-start(bf16[192,384]{1,0:T(8,128)(2,1)S(1)} %get-tuple-element.236), channel_id=1, source_target_pairs={{0,4},{4,8},{8,12},{12,0},{1,5},{5,9},{9,13},{13,1},{2,6},{6,10},{... | collective-permute-start | bytes 442376 | tf_op jit(solution)/shard_map/ppermute | solution.py:774
  202.7 16.7 %collective-permute-start.26 = (bf16[192,384]{1,0:T(8,128)(2,1)}, bf16[192,384]{1,0:T(8,128)(2,1)S(1)}, u32[]{:S(2)}, u32[]{:S(2)}) collective-permute-start(bf16[192,384]{1,0:T(8,128)(2,1)} %reduce-scatter.8.cloned.1.call-done.early_own), channel_id=1, source_target_pairs={{1,16},{3,18},{5,20},{7,22},{9,24},{11,26},{13,28},{15,30},{16,1},... | collective-permute-start | bytes 442376 | tf_op jit(solution)/shard_map/ppermute | solution.py:712
  207.3 12.2 %copy-start.17 = (bf16[192,384]{1,0:T(8,128)(2,1)S(1)}, bf16[192,384]{1,0:T(8,128)(2,1)}, u32[]{:S(2)}) copy-start(bf16[192,384]{1,0:T(8,128)(2,1)} %reduce-scatter.8.cloned.1.call-done.early_own) | copy-start | bytes 442372
  207.3 12.2 %copy-start.20 = (s32[4]{0:T(128)S(1)}, s32[4]{0:T(128)}, u32[]{:S(2)}) copy-start(s32[4]{0:T(128)} %pad_add_fusion.flags.refs_0_) | copy-start | bytes 52
  212.6 8.7 %copy-start.4 = (bf16[2,512,768]{2,1,0:T(8,128)(2,1)S(1)}, bf16[2,512,768]{2,1,0:T(8,128)(2,1)}, u32[]{:S(2)}) copy-start(bf16[2,512,768]{2,1,0:T(8,128)(2,1)} %shard_map.230.own_ref) | copy-start | bytes 4718596
  212.6 2.9 %collective-permute-start.24 = (f32[9,768]{1,0:T(8,128)S(1)}, f32[9,768]{1,0:T(8,128)S(1)}, u32[]{:S(2)}, u32[]{:S(2)}) collective-permute-start(f32[9,768]{1,0:T(8,128)S(1)} %pad_maximum_fusion.4), channel_id=1, source_target_pairs={{0,16},{16,0},{1,17},{17,1},{2,18},{18,2},{3,19},{19,3},{4,20},{20... | collective-permute-start | bytes 82952 | tf_op jit(solution)/shard_map/ppermute | solution.py:782
  215.6 3.8 %collective-permute-start.25 = (f32[9,768]{1,0:T(8,128)S(1)}, f32[9,768]{1,0:T(8,128)S(1)}, u32[]{:S(2)}, u32[]{:S(2)}) collective-permute-start(f32[9,768]{1,0:T(8,128)S(1)} %add.88), channel_id=1, source_target_pairs={{0,2},{2,0},{1,3},{3,1},{4,6},{6,4},{5,7},{7,5},{8,10},{10,8},{9,1... | collective-permute-start | bytes 82952 | tf_op jit(solution)/shard_map/ppermute | solution.py:782
  220.4 15.5 %copy-start.21 = (f32[5]{0:T(128)S(1)}, f32[5]{0:T(128)}, u32[]{:S(2)}) copy-start(f32[5]{0:T(128)} %weight_ref.1) | copy-start | bytes 64
  221.0 12.6 %collective-permute-start.30 = (bf16[192,1152]{1,0:T(8,128)(2,1)S(1)}, bf16[192,1152]{1,0:T(8,128)(2,1)S(1)}, u32[]{:S(2)}, u32[]{:S(2)}) collective-permute-start(bf16[192,1152]{1,0:T(8,128)(2,1)S(1)} %shard_map.231), channel_id=1, source_target_pairs={{0,2},{2,0},{1,3},{3,1},{4,6},{6,4},{5,7},{7,5},{8,10},{10,8},{9,1... | collective-permute-start | bytes 1327112 | tf_op jit(solution)/shard_map/ppermute | solution.py:731
  221.4 21.8 %collective-permute-start.23 = (bf16[2,512,768]{2,1,0:T(8,128)(2,1)S(1)}, bf16[2,512,768]{2,1,0:T(8,128)(2,1)S(1)}, u32[]{:S(2)}, u32[]{:S(2)}) collective-permute-start(bf16[2,512,768]{2,1,0:T(8,128)(2,1)S(1)} %copy-done.4), channel_id=1, source_target_pairs={{1,16},{3,18},{5,20},{7,22},{9,24},{11,26},{13,28},{15,30},{16,1},... | collective-permute-start | bytes 4718600 | tf_op jit(solution)/shard_map/ppermute | solution.py:712
  225.1 1.3 collective-permute-start.31
  226.4 3.3 %collective-permute-start.32 = (f32[9,768]{1,0:T(8,128)S(1)}, f32[9,768]{1,0:T(8,128)S(1)}, u32[]{:S(2)}, u32[]{:S(2)}) collective-permute-start(f32[9,768]{1,0:T(8,128)S(1)} %add.100), channel_id=1, source_target_pairs={{0,4},{4,0},{8,12},{12,8},{1,5},{5,1},{9,13},{13,9},{2,6},{6,2},{1... | collective-permute-start | bytes 82952 | tf_op jit(solution)/shard_map/ppermute | solution.py:782
  229.7 3.9 %collective-permute-start.33 = (f32[9,768]{1,0:T(8,128)S(1)}, f32[9,768]{1,0:T(8,128)S(1)}, u32[]{:S(2)}, u32[]{:S(2)}) collective-permute-start(f32[9,768]{1,0:T(8,128)S(1)} %add.101), channel_id=1, source_target_pairs={{0,8},{4,12},{8,0},{12,4},{1,9},{5,13},{9,1},{13,5},{2,10},{6,14},... | collective-permute-start | bytes 82952 | tf_op jit(solution)/shard_map/ppermute | solution.py:782
  233.6 9.5 %copy-start.10 = (f32[512,768]{1,0:T(8,128)S(1)}, f32[512,768]{1,0:T(8,128)}, u32[]{:S(2)}) copy-start(f32[512,768]{1,0:T(8,128)} %get-tuple-element.102.part_ref) | copy-start | bytes 4718596
  233.8 4.6 %collective-permute-start.34 = (bf16[2,192,1152]{2,1,0:T(8,128)(2,1)S(1)}, bf16[2,192,1152]{2,1,0:T(8,128)(2,1)S(1)}, u32[]{:S(2)}, u32[]{:S(2)}) collective-permute-start(bf16[2,192,1152]{2,1,0:T(8,128)(2,1)S(1)} %pad_maximum_fusion.3.here_ref), channel_id=1, source_target_pairs={{0,1},{1,0},{2,3},{3,2},{4,5},{5,4},{6,7},{7,6},{8,9},{9,8},{10,11... | collective-permute-start | bytes 2654216 | tf_op jit(solution)/shard_map/ppermute | solution.py:735
  (21 other events, 63.0 us)
Sparse Core Ops, SparseCore 0:
  102.3 46.4 reduce-scatter.9
  155.4 18.4 reduce-scatter.7
  176.1 20.2 reduce-scatter.5

commit v14 on v13

--- a/solution.py
+++ b/solution.py
@@ -668,6 +668,23 @@
     return streamed(blocks_kernel, 1, [flags], [early_own, early_got, late, *parts], [out], [], 1, SNUG)[0]
 
 
+def deal_kernel(flags, place_ref, own_ref, *refs):
+    moved, outs, total = refs[:4], refs[4:-1], refs[-1]
+    first = jnp.where(flags[0] == 1, own_ref[...], moved[0][...]).astype(jnp.float32)
+    total[...] = (first + sum(ref[...].astype(jnp.float32) for ref in moved[1:])).astype(jnp.bfloat16)
+    rows = outs[0].shape[0]
+    for step, out_ref in enumerate(outs):
+        at = lax.rem(place_ref[0] + step, len(outs)) * rows
+        out_ref[...] = total[pl.ds(pl.multiple_of(at, rows), rows), :]
+
+
+def deal(flags, own, moved, dps):
+    depth, columns = own.shape
+    place = lax.axis_index("dp")[None].astype(jnp.int32)
+    outs = [((depth // dps, columns), jnp.bfloat16)] * dps
+    return streamed(deal_kernel, 1, [flags, place], [own, *moved], outs, [(own.shape, jnp.bfloat16)], 1, SNUG)
+
+
 def place_kernel(flags, here_ref, there_ref, qkv_ref, out_ref, up_ref, down_ref):
     near, far = flags[1], flags[2]
     part = out_ref.shape[1]
@@ -762,17 +779,14 @@
     return lax.psum_scatter(piece, "dp", scatter_dimension=0, tiled=True)
 
 
-def move_rows(block):
+def move_rows(flags, own, moved):
     dps = lax.axis_size("dp")
     if dps > 8:
-        return [scatter_rows(block)]
-    block = block.reshape(dps, block.shape[0] // dps, block.shape[1])
-    place = lax.axis_index("dp")
-    moved = [lax.dynamic_index_in_dim(block, place, 0, keepdims=False)]
-    for step in range(1, dps):
-        sent = lax.dynamic_index_in_dim(block, lax.rem(place + step, dps), 0, keepdims=False)
-        moved.append(lax.ppermute(sent, "dp", [(d, (d + step) % dps) for d in range(dps)]))
-    return moved
+        return [scatter_rows(add(jnp.where(flags[0] == 1, own, moved[0]), *moved[1:]))]
+    first, *rest = deal(flags, own, moved, dps)
+    return [first] + [
+        lax.ppermute(field, "dp", [(d, (d + step + 1) % dps) for d in range(dps)]) for step, field in enumerate(rest)
+    ]
 
 
 def sum_over(field, name):
@@ -872,8 +886,8 @@
     sent = [*send, *block_send]
     keep, block_keep, *arrived = lax.optimization_barrier((keep, block_keep, *sent, *moved))
     sent, moved = arrived[:4], arrived[4:]
-    attn_one = add(jnp.where(same, owned[0], moved[0]), *moved[1:])
-    attn_moved = move_rows(attn_one)
+    attn_moved = move_rows(flags, owned[0], moved)
+    attn_one = attn_moved[0]
     got = [swap_near(field) for field in sent]
     ours = last(flags, layer_rows, grad_attn, after(keep, attn_one), block_keep, got, vectors)
     early_sum = after(early_sum, attn_one)

time: 253 us -> 261 us (1.032)
  local copies, waits for them, and re-layouts: 17.9 us -> 24.1 us
    unnamed x94 -> x106, local copies, waits for them, and re-layouts: 11.1 us -> 18.6 us
    pallas_call x11 -> x12, Pallas kernels: 82.6 us -> 84.3 us  [streamed(): pl.pallas_call(kernel, grid_spec=pltpu.PrefetchScalarGridSpec(num_scalar_...]
  transfers between devices with their start and end apart: 38 -> 38, of which waited for: 10 -> 11; matrix products, arithmetic and copies ran while one was open for 13% -> 11% of each run, Pallas kernels for 46% -> 46%
where the time goes in v14:
time: 261 us; the launch traced here: 258 us
  Pallas kernels  121 us (46%)
  starting transfers between devices  49.9 us (19%)
  waiting for transfers between devices  25.1 us (10%)
  local copies, waits for them, and re-layouts  24.1 us (9%)
  other arithmetic  21.9 us (8%)
  between operations  14.6 us (6%)
    pallas_call x12, Pallas kernels, streamed(): pl.pallas_call(kernel, grid_spec=pltpu.PrefetchScalarGridSpec(num_scalar_...  84.3 us
    ppermute x7, starting transfers between devices, swap_diagonal(): lax.ppermute(field, AXES, moves(away, lambda t, d, k, c: (c, d, k, t)))  24 us
    pallas_call x1, Pallas kernels, attend_back(): pl.pallas_call(functools.partial(attend_back_kernel, reach), grid=(width...  19.6 us
    unnamed x106, local copies, waits for them, and re-layouts  18.6 us
    ppermute x5, waiting for transfers between devices, sum_over(): lax.ppermute(field, name, [(d, d ^ bit) for d in range(size)])  14 us
    pallas_call x1, Pallas kernels, attend(): pl.pallas_call(functools.partial(attend_kernel, reach), grid=(width // LA...  13.1 us
    ppermute x8, starting transfers between devices, send_to_owner(): lax.ppermute(field, AXES, moves(away if not other_far and (not other_tp)...  12.4 us
  transfers between devices with their start and end apart: 38, of which 11 were waited for; matrix products, arithmetic and copies ran while one was open for 11% of the time, Pallas kernels for 46%

profile of v14, /device:TPU:9, one launch (start us, length us, event | category | flops | bytes accessed | tf_op | source)
XLA Modules:
  0.0 257.8 jit_solution(14515431809826833095)
XLA Ops:
  8.0 3.1 %collective-permute-start = (bf16[512,768]{1,0:T(8,128)(2,1)}, bf16[512,768]{1,0:T(8,128)(2,1)}, u32[]{:S(2)}, u32[]{:S(2)}) collective-permute-start(bf16[512,768]{1,0:T(8,128)(2,1)} %bitcast.36), channel_id=1, source_target_pairs={{1,16},{3,18},{5,20},{7,22},{9,24},{11,26},{13,28},{15,30},{16,1},... | collective-permute-start | bytes 2359304 | tf_op jit(solution)/shard_map/ppermute | solution.py:729
  11.1 2.2 constant_dynamic-slice_fusion
  13.2 2.6 %collective-permute-start.3 = (bf16[3,384,384]{2,1,0:T(8,128)(2,1)}, bf16[3,384,384]{2,1,0:T(8,128)(2,1)S(1)}, u32[]{:S(2)}, u32[]{:S(2)}) collective-permute-start(bf16[3,384,384]{2,1,0:T(8,128)(2,1)} %constant_dynamic-slice_fusion), channel_id=1, source_target_pairs={{1,16},{3,18},{5,20},{7,22},{9,24},{11,26},{13,28},{15,30},{16,1},... | collective-permute-start | bytes 2654216 | tf_op jit(solution)/shard_map/ppermute | solution.py:729
  16.0 2.5 pad_maximum_fusion.2
  18.5 1.9 fusion.9
  20.4 1.6 pad_maximum_fusion.1
  22.0 1.6 pad_maximum_fusion
  23.6 4.3 %shard_map.220 = (bf16[4,512,768]{2,1,0:T(8,128)(2,1)}, f32[512,768]{1,0:T(8,128)}, f32[8,768]{1,0:T(8,128)}) custom-call(f32[5]{0:T(128)} %weight_ref.1, bf16[4,512,768]{2,1,0:T(8,128)(2,1)} %bitcast.35, bf16[512,768]{1,0:T(8,128)(2,1)} %bitcast.33), custom_call_target="tpu_custom_call" | custom-call | bytes 9000000 | tf_op jit(solution)/shard_map/pallas_call | solution.py:627
  29.5 3.1 %collective-permute-start.5 = (bf16[896,768]{1,0:T(8,128)(2,1)}, bf16[896,768]{1,0:T(8,128)(2,1)}, u32[]{:S(2)}, u32[]{:S(2)}) collective-permute-start(bf16[896,768]{1,0:T(8,128)(2,1)} %pad_maximum_fusion.2), channel_id=1, source_target_pairs={{1,16},{3,18},{5,20},{7,22},{9,24},{11,26},{13,28},{15,30},{16,1},... | collective-permute-start | bytes 4128776 | tf_op jit(solution)/shard_map/ppermute | solution.py:729
  32.6 1.2 broadcast_select_fusion.1
  33.9 3.1 %collective-permute-start.4 = (bf16[3,384,384]{2,1,0:T(8,128)(2,1)S(1)}, bf16[3,384,384]{2,1,0:T(8,128)(2,1)S(1)}, u32[]{:S(2)}, u32[]{:S(2)}) collective-permute-start(bf16[3,384,384]{2,1,0:T(8,128)(2,1)S(1)} %collective-permute-done.3.w_near), channel_id=1, source_target_pairs={{1,3},{3,1},{5,7},{7,5},{9,11},{11,9},{13,15},{15,13},{16,18},{18,... | collective-permute-start | bytes 2654216 | tf_op jit(solution)/shard_map/ppermute | solution.py:744
  37.9 0.9 select_convert_fusion.apart_ref
  38.9 3.1 %fusion.1 = (f32[1024,128]{1,0:T(8,128)}, f32[1024,128]{1,0:T(8,128)}) fusion(f32[128]{0:T(128)S(1)} %get-tuple-element.245, f32[128]{0:T(128)S(1)} %get-tuple-element.246, f32[1024]{0:T(1024)S(1)} %subtract_convert_fusion), kind=kLoop, calls=%fused_computation.12 | loop fusion | flops 262144 | bytes 1053696 | tf_op jit(solution)/shard_map/mul | solution.py:841
  41.9 2.8 %collective-permute-start.8 = (bf16[1536,768]{1,0:T(8,128)(2,1)}, bf16[1536,768]{1,0:T(8,128)(2,1)}, u32[]{:S(2)}, u32[]{:S(2)}) collective-permute-start(bf16[1536,768]{1,0:T(8,128)(2,1)} %pad_maximum_fusion), channel_id=1, source_target_pairs={{1,16},{3,18},{5,20},{7,22},{9,24},{11,26},{13,28},{15,30},{16,1},... | collective-permute-start | bytes 7077896 | tf_op jit(solution)/shard_map/ppermute | solution.py:729
  44.7 1.9 maximum_select_fusion.rows_ref.refs_2_
  46.6 1.1 collective-permute-done.4.w_far
  47.7 1.0 copy-done.8
  48.7 9.0 %shard_map.221 = (bf16[3,1024,384]{2,1,0:T(8,128)(2,1)}, bf16[768,1024]{1,0:T(8,128)(2,1)}) custom-call(s32[4]{0:T(128)} %pad_add_fusion.flags.refs_0_, bf16[1024,768]{1,0:T(8,128)(2,1)} %maximum_select_fusion.rows_ref.refs_2_, f32[1024,128]{1,0:T(8,128)} %get-tuple-element.110.cos_ref, f32[1024,128]{1,0:T(8,128)} %get-tuple-element.111.sin_ref, ...), custom_call_target="tpu_custom_call" | custom-call | bytes 24000000 | tf_op jit(solution)/shard_map/pallas_call | solution.py:240
  57.6 13.1 %shard_map.222 = (bf16[1024,384]{1,0:T(8,128)(2,1)}, f32[3,8,1024]{2,1,0:T(8,128)}) custom-call(bf16[1024,128]{1,0:T(8,128)(2,1)} %select_convert_fusion.apart_ref, bf16[1024,128]{1,0:T(8,128)(2,1)} %fusion.2.member_ref, bf16[3,1024,384]{2,1,0:T(8,128)(2,1)} %get-tuple-element.113.q_ref.k_ref.v_ref, ...), custom_call_target="tpu_custom_call" | custom-call | bytes 36000000 | tf_op jit(solution)/shard_map/pallas_call | solution.py:104
  70.7 4.0 %collective-permute-start.9 = (bf16[1536,768]{1,0:T(8,128)(2,1)}, bf16[1536,768]{1,0:T(8,128)(2,1)}, u32[]{:S(2)}, u32[]{:S(2)}) collective-permute-start(bf16[1536,768]{1,0:T(8,128)(2,1)} %pad_maximum_fusion.1), channel_id=1, source_target_pairs={{1,16},{3,18},{5,20},{7,22},{9,24},{11,26},{13,28},{15,30},{16,1},... | collective-permute-start | bytes 7077896 | tf_op jit(solution)/shard_map/ppermute | solution.py:729
  74.7 1.7 broadcast_select_fusion.w_ref
  76.4 1.0 convolution_convert_fusion.refs_3_
  78.1 3.9 %collective-permute-done.7.refs_6_ = bf16[512,768]{1,0:T(8,128)(2,1)S(1)} collective-permute-done((bf16[512,768]{1,0:T(8,128)(2,1)S(1)}, bf16[512,768]{1,0:T(8,128)(2,1)S(1)}, u32[]{:S(2)}, u32[]{:S(2)}) %collective-permute-start.7) | collective-permute-done | bytes 786464 | tf_op jit(solution)/shard_map/ppermute | solution.py:752
  82.8 19.3 %shard_map.223 = (bf16[1024,768]{1,0:T(8,128)(2,1)}, bf16[768,1024]{1,0:T(8,128)(2,1)}, bf16[1024,768]{1,0:T(8,128)(2,1)}, bf16[768,1024]{1,0:T(8,128)(2,1)}, bf...) custom-call(s32[4]{0:T(128)} %pad_add_fusion.flags.refs_0_, ...), custom_call_target="tpu_custom_call" | custom-call | bytes 51000000 | tf_op jit(solution)/shard_map/pallas_call | solution.py:240
  102.3 16.4 %shard_map.224 = (bf16[1024,768]{1,0:T(8,128)(2,1)}, bf16[1024,768]{1,0:T(8,128)(2,1)}, bf16[768,768]{1,0:T(8,128)(2,1)}, bf16[768,384]{1,0:T(8,128)(2,1)}, bf16...) custom-call(s32[4]{0:T(128)} %pad_add_fusion.flags.refs_0_, ...), custom_call_target="tpu_custom_call" | custom-call | bytes 51000000 | tf_op jit(solution)/shard_map/pallas_call | solution.py:240
  119.7 2.1 collective-permute-start.13
  121.7 2.8 %collective-permute-start.11 = (bf16[768,384]{1,0:T(8,128)(2,1)}, bf16[768,384]{1,0:T(8,128)(2,1)S(1)}, u32[]{:S(2)}, u32[]{:S(2)}) collective-permute-start(bf16[768,384]{1,0:T(8,128)(2,1)} %get-tuple-element.129), channel_id=1, source_target_pairs={{1,16},{3,18},{5,20},{7,22},{9,24},{11,26},{13,28},{15,30},{16,1},... | collective-permute-start | bytes 1769480 | tf_op jit(solution)/shard_map/ppermute | solution.py:733
  124.6 1.2 copy-done.37
  125.7 9.3 %shard_map.225 = (bf16[1024,768]{1,0:T(8,128)(2,1)}, bf16[1024,384]{1,0:T(8,128)(2,1)}, bf16[768,384]{1,0:T(8,128)(2,1)}, f32[8,768]{1,0:T(8,128)}) custom-call(s32[4]{0:T(128)} %pad_add_fusion.flags.refs_0_, bf16[1024,768]{1,0:T(8,128)(2,1)} %get-tuple-element.118.resid_ref, bf16[1024,768]{1,0:T(8,128)(2,1)} %get-tuple-element.141.refs_3_.cot_ref, ...), custom_call_target="tpu_custom_call" | custom-call | bytes 24000000 | tf_op jit(solution)/shard_map/pallas_call | solution.py:240
  135.0 19.6 %shard_map.226.query_ref.key_ref.value_ref.grad_ref = bf16[3,1024,384]{2,1,0:T(8,128)(2,1)} custom-call(bf16[1024,128]{1,0:T(8,128)(2,1)} %select_convert_fusion.apart_ref, bf16[1024,128]{1,0:T(8,128)(2,1)} %fusion.2.member_ref, f32[1024,128]{1,0:T(8,128)} %get-tuple-element.110.cos_ref, f32[1024,128]{1,0:T(8,128)} %get-tuple-element.111.sin_ref, ...), custom_call_target="tpu_custom_call" | custom-call | bytes 66000000 | tf_op jit(solution)/shard_map/pallas_call | solution.py:189
  155.5 7.1 %shard_map.227 = (bf16[768,384]{1,0:T(8,128)(2,1)}, bf16[768,384]{1,0:T(8,128)(2,1)}, bf16[768,384]{1,0:T(8,128)(2,1)}, bf16[768,384]{1,0:T(8,128)(2,1)}) custom-call(s32[4]{0:T(128)} %pad_add_fusion.flags.refs_0_, bf16[768,1024]{1,0:T(8,128)(2,1)} %get-tuple-element.134.turned_ref, bf16[768,384]{1,0:T(8,128)(2,1)} %get-tuple-element.135.out_grad_ref, ...), custom_call_target="tpu_custom_call" | custom-call | bytes 12000000 | tf_op jit(solution)/shard_map/pallas_call | solution.py:240
  162.7 3.0 %add_convert_fusion = bf16[768,384]{1,0:T(8,128)(2,1)} fusion(bf16[768,384]{1,0:T(8,128)(2,1)} %copy-done.43, bf16[768,384]{1,0:T(8,128)(2,1)} %copy-done.42, bf16[768,384]{1,0:T(8,128)(2,1)} %copy-done.41, bf16[768,384]{1,0:T(8,128)(2,1)} %get-tuple-element.129, bf16[768,384]{1,0:T(8,128)(2,1)} %copy-done.44, pred[]{:T(512)S(6)} %eq.35), kind=kLoop, calls=%fused_computation.6 | loop fusion | flops 2654208 | bytes 3538945 | tf_op jit(solution)/shard_map/convert_element_type | solution.py:771
  165.7 1.2 collective-permute-start.16
  166.8 2.1 collective-permute-start.17
  168.9 3.4 %collective-permute-start.15 = (bf16[768,384]{1,0:T(8,128)(2,1)}, bf16[768,384]{1,0:T(8,128)(2,1)S(1)}, u32[]{:S(2)}, u32[]{:S(2)}) collective-permute-start(bf16[768,384]{1,0:T(8,128)(2,1)} %get-tuple-element.136.own_ref), channel_id=1, source_target_pairs={{1,16},{3,18},{5,20},{7,22},{9,24},{11,26},{13,28},{15,30},{16,1},... | collective-permute-start | bytes 1769480 | tf_op jit(solution)/shard_map/ppermute | solution.py:733
  172.4 1.4 copy-done.1
  173.8 1.5 copy-done.3
  175.3 1.2 copy-done.9
  176.5 6.1 %shard_map.228 = (bf16[512,768]{1,0:T(8,128)(2,1)S(1)}, bf16[256,768]{1,0:T(8,128)(2,1)}, bf16[256,768]{1,0:T(8,128)(2,1)}, f32[8,768]{1,0:T(8,128)S(1)}) custom-call(s32[4]{0:T(128)S(1)} %copy-done.28, bf16[3,1024,384]{2,1,0:T(8,128)(2,1)S(1)} %copy-done, bf16[1024,768]{1,0:T(8,128)(2,1)S(1)} %copy-done.1, bf16[3,768,384]{2,1,0:T(8,128)(2,1)S(1)} %copy-done.3, ...), custom_call_target="tpu_custom_call" | custom-call | bytes 15000000 | tf_op jit(solution)/shard_map/pallas_call | solution.py:240
  183.4 1.3 copy-done.14
  184.7 4.8 %shard_map.229 = (bf16[512,768]{1,0:T(8,128)(2,1)S(1)}, bf16[256,768]{1,0:T(8,128)(2,1)S(1)}, bf16[256,768]{1,0:T(8,128)(2,1)S(1)}, f32[8,768]{1,0:T(8,128)S(1)}) custom-call(s32[4]{0:T(128)S(1)} %copy-done.28, bf16[1024,768]{1,0:T(8,128)(2,1)S(1)} %copy-done.11, bf16[1024,768]{1,0:T(8,128)(2,1)S(1)} %copy-done.12, bf16[1024,768]{1,0:T(8,128)(2,1)S(1)} %copy-done.5, ...), custom_call_target="tpu_custom_call" | custom-call | bytes 18000000 | tf_op jit(solution)/shard_map/pallas_call | solution.py:240
  192.1 2.9 %collective-permute-done.18.refs_3_ = bf16[768,384]{1,0:T(8,128)(2,1)S(1)} collective-permute-done((bf16[768,384]{1,0:T(8,128)(2,1)}, bf16[768,384]{1,0:T(8,128)(2,1)S(1)}, u32[]{:S(2)}, u32[]{:S(2)}) %collective-permute-start.18) | collective-permute-done | bytes 589856 | tf_op jit(solution)/shard_map/ppermute | solution.py:733
  198.5 1.1 copy-done.19
  199.6 1.1 copy-done.21
  200.6 1.1 copy-done.23
  201.7 1.1 copy-done.25
  202.8 1.8 shard_map.230
  204.6 1.4 collective-permute-start.27
  206.0 1.2 collective-permute-start.28
  207.2 1.2 collective-permute-start.29
  208.4 4.9 %collective-permute-start.26 = (bf16[192,384]{1,0:T(8,128)(2,1)}, bf16[192,384]{1,0:T(8,128)(2,1)S(1)}, u32[]{:S(2)}, u32[]{:S(2)}) collective-permute-start(bf16[192,384]{1,0:T(8,128)(2,1)} %reduce-scatter.8.cloned.1.call-done.early_own), channel_id=1, source_target_pairs={{1,16},{3,18},{5,20},{7,22},{9,24},{11,26},{13,28},{15,30},{16,1},... | collective-permute-start | bytes 442376 | tf_op jit(solution)/shard_map/ppermute | solution.py:729
  213.4 5.3 %shard_map.231.own_ref = bf16[2,512,768]{2,1,0:T(8,128)(2,1)} custom-call(s32[4]{0:T(128)} %pad_add_fusion.flags.refs_0_, bf16[1024,768]{1,0:T(8,128)(2,1)} %maximum_select_fusion.rows_ref.refs_2_, bf16[1024,768]{1,0:T(8,128)(2,1)} %get-tuple-element.126.resid_ref, bf16[512,768]{1,0:T(8,128)(2,1)} %copy-done.15, bf16[512,768]{1,0:T(8,128)(2,1)} %copy-done.16, ...), custom_call_target="tpu_custom_call" | custom-call | bytes 9000000 | tf_op jit(solution)/shard_map/pallas_call | solution.py:240
  218.7 2.9 %collective-permute-done.24 = f32[9,768]{1,0:T(8,128)S(1)} collective-permute-done((f32[9,768]{1,0:T(8,128)S(1)}, f32[9,768]{1,0:T(8,128)S(1)}, u32[]{:S(2)}, u32[]{:S(2)}) %collective-permute-start.24) | collective-permute-done | bytes 27680 | tf_op jit(solution)/shard_map/ppermute | solution.py:796
  222.0 3.5 %collective-permute-done.25 = f32[9,768]{1,0:T(8,128)S(1)} collective-permute-done((f32[9,768]{1,0:T(8,128)S(1)}, f32[9,768]{1,0:T(8,128)S(1)}, u32[]{:S(2)}, u32[]{:S(2)}) %collective-permute-start.25) | collective-permute-done | bytes 27680 | tf_op jit(solution)/shard_map/ppermute | solution.py:796
  225.6 0.9 copy-done.27
  227.5 3.7 %collective-permute-start.23 = (bf16[2,512,768]{2,1,0:T(8,128)(2,1)S(1)}, bf16[2,512,768]{2,1,0:T(8,128)(2,1)S(1)}, u32[]{:S(2)}, u32[]{:S(2)}) collective-permute-start(bf16[2,512,768]{2,1,0:T(8,128)(2,1)S(1)} %copy-done.4), channel_id=1, source_target_pairs={{1,16},{3,18},{5,20},{7,22},{9,24},{11,26},{13,28},{15,30},{16,1},... | collective-permute-start | bytes 4718600 | tf_op jit(solution)/shard_map/ppermute | solution.py:729
  231.2 1.2 collective-permute-done.31
  233.3 2.5 collective-permute-done.32
  235.9 3.9 %collective-permute-done.33 = f32[9,768]{1,0:T(8,128)S(1)} collective-permute-done((f32[9,768]{1,0:T(8,128)S(1)}, f32[9,768]{1,0:T(8,128)S(1)}, u32[]{:S(2)}, u32[]{:S(2)}) %collective-permute-start.33) | collective-permute-done | bytes 27680 | tf_op jit(solution)/shard_map/ppermute | solution.py:796
  239.9 2.2 collective-permute-start.34
  242.6 1.3 slice_reduce_fusion
  244.6 2.5 shard_map.233
  247.1 2.2 collective-permute-done.23.got_ref
  249.2 2.0 shard_map.234
  (179 shorter events, 17.6 us)
Async XLA Ops:
  7.2 8.7 %copy-start.48 = (f32[768]{0:T(1024)S(1)}, f32[768]{0:T(1024)}, u32[]{:S(2)}) copy-start(f32[768]{0:T(1024)} %param.18) | copy-start | bytes 9220
  7.2 8.8 %copy-start.49 = (f32[768]{0:T(1024)S(1)}, f32[768]{0:T(1024)}, u32[]{:S(2)}) copy-start(f32[768]{0:T(1024)} %param.19) | copy-start | bytes 9220
  7.2 8.8 %copy-start.50 = (f32[768]{0:T(1024)S(1)}, f32[768]{0:T(1024)}, u32[]{:S(2)}) copy-start(f32[768]{0:T(1024)} %param.22) | copy-start | bytes 9220
  7.2 8.8 %copy-start.51 = (f32[768]{0:T(1024)S(1)}, f32[768]{0:T(1024)}, u32[]{:S(2)}) copy-start(f32[768]{0:T(1024)} %param.23) | copy-start | bytes 9220
  7.2 148.2 %reduce-scatter.10.cloned.1.call-start = ((), (), s32[]{:S(2)}) async-start(), calls=%async_computation.5 | async-start | bytes 2949120
  7.3 21.8 %collective-permute-start.2 = (s32[1,3]{1,0:T(1,128)}, s32[1,3]{1,0:T(1,128)S(1)}, u32[]{:S(2)}, u32[]{:S(2)}) collective-permute-start(s32[1,3]{1,0:T(1,128)} %param.16), channel_id=1, source_target_pairs={{0,1},{1,0},{2,3},{3,2},{4,5},{5,4},{6,7},{7,6},{8,9},{9,8},{10,11... | collective-permute-start | bytes 44 | tf_op jit(solution)/shard_map/ppermute | solution.py:752
  8.0 21.5 %collective-permute-start = (bf16[512,768]{1,0:T(8,128)(2,1)}, bf16[512,768]{1,0:T(8,128)(2,1)}, u32[]{:S(2)}, u32[]{:S(2)}) collective-permute-start(bf16[512,768]{1,0:T(8,128)(2,1)} %bitcast.36), channel_id=1, source_target_pairs={{1,16},{3,18},{5,20},{7,22},{9,24},{11,26},{13,28},{15,30},{16,1},... | collective-permute-start | bytes 2359304 | tf_op jit(solution)/shard_map/ppermute | solution.py:729
  13.2 20.6 %collective-permute-start.3 = (bf16[3,384,384]{2,1,0:T(8,128)(2,1)}, bf16[3,384,384]{2,1,0:T(8,128)(2,1)S(1)}, u32[]{:S(2)}, u32[]{:S(2)}) collective-permute-start(bf16[3,384,384]{2,1,0:T(8,128)(2,1)} %constant_dynamic-slice_fusion), channel_id=1, source_target_pairs={{1,16},{3,18},{5,20},{7,22},{9,24},{11,26},{13,28},{15,30},{16,1},... | collective-permute-start | bytes 2654216 | tf_op jit(solution)/shard_map/ppermute | solution.py:729
  23.6 9.0 %copy-start.39 = (bf16[1,512,768]{2,1,0:T(8,128)(2,1)S(1)}, bf16[1,512,768]{2,1,0:T(8,128)(2,1)}, u32[]{:S(2)}) copy-start(bf16[1,512,768]{2,1,0:T(8,128)(2,1)} %param.13) | copy-start | bytes 2359300
  29.5 45.2 %collective-permute-start.5 = (bf16[896,768]{1,0:T(8,128)(2,1)}, bf16[896,768]{1,0:T(8,128)(2,1)}, u32[]{:S(2)}, u32[]{:S(2)}) collective-permute-start(bf16[896,768]{1,0:T(8,128)(2,1)} %pad_maximum_fusion.2), channel_id=1, source_target_pairs={{1,16},{3,18},{5,20},{7,22},{9,24},{11,26},{13,28},{15,30},{16,1},... | collective-permute-start | bytes 4128776 | tf_op jit(solution)/shard_map/ppermute | solution.py:729
  33.8 10.9 %collective-permute-start.1 = (bf16[512,768]{1,0:T(8,128)(2,1)S(1)}, bf16[512,768]{1,0:T(8,128)(2,1)S(1)}, u32[]{:S(2)}, u32[]{:S(2)}) collective-permute-start(bf16[512,768]{1,0:T(8,128)(2,1)S(1)} %broadcast_select_fusion.1), channel_id=1, source_target_pairs={{0,1},{1,0},{2,3},{3,2},{4,5},{5,4},{6,7},{7,6},{8,9},{9,8},{10,11... | collective-permute-start | bytes 2359304 | tf_op jit(solution)/shard_map/ppermute | solution.py:752
  33.9 12.7 %copy-start.6 = (bf16[3,384,384]{2,1,0:T(8,128)(2,1)}, bf16[3,384,384]{2,1,0:T(8,128)(2,1)S(1)}, u32[]{:S(2)}) copy-start(bf16[3,384,384]{2,1,0:T(8,128)(2,1)S(1)} %collective-permute-done.3.w_near) | copy-start | bytes 2654212
  33.9 13.8 %collective-permute-start.4 = (bf16[3,384,384]{2,1,0:T(8,128)(2,1)S(1)}, bf16[3,384,384]{2,1,0:T(8,128)(2,1)S(1)}, u32[]{:S(2)}, u32[]{:S(2)}) collective-permute-start(bf16[3,384,384]{2,1,0:T(8,128)(2,1)S(1)} %collective-permute-done.3.w_near), channel_id=1, source_target_pairs={{1,3},{3,1},{5,7},{7,5},{9,11},{11,9},{13,15},{15,13},{16,18},{18,... | collective-permute-start | bytes 2654216 | tf_op jit(solution)/shard_map/ppermute | solution.py:744
  41.9 40.0 %collective-permute-start.8 = (bf16[1536,768]{1,0:T(8,128)(2,1)}, bf16[1536,768]{1,0:T(8,128)(2,1)}, u32[]{:S(2)}, u32[]{:S(2)}) collective-permute-start(bf16[1536,768]{1,0:T(8,128)(2,1)} %pad_maximum_fusion), channel_id=1, source_target_pairs={{1,16},{3,18},{5,20},{7,22},{9,24},{11,26},{13,28},{15,30},{16,1},... | collective-permute-start | bytes 7077896 | tf_op jit(solution)/shard_map/ppermute | solution.py:729
  57.6 17.0 %copy-start.33 = (bf16[1,512,768]{2,1,0:T(8,128)(2,1)S(1)}, bf16[1,512,768]{2,1,0:T(8,128)(2,1)}, u32[]{:S(2)}) copy-start(bf16[1,512,768]{2,1,0:T(8,128)(2,1)} %param.15) | copy-start | bytes 2359300
  57.6 17.1 %copy-start.36 = (bf16[384,768]{1,0:T(8,128)(2,1)S(1)}, bf16[384,768]{1,0:T(8,128)(2,1)}, u32[]{:S(2)}) copy-start(bf16[384,768]{1,0:T(8,128)(2,1)} %param.21) | copy-start | bytes 1769476
  70.7 31.5 %collective-permute-start.9 = (bf16[1536,768]{1,0:T(8,128)(2,1)}, bf16[1536,768]{1,0:T(8,128)(2,1)}, u32[]{:S(2)}, u32[]{:S(2)}) collective-permute-start(bf16[1536,768]{1,0:T(8,128)(2,1)} %pad_maximum_fusion.1), channel_id=1, source_target_pairs={{1,16},{3,18},{5,20},{7,22},{9,24},{11,26},{13,28},{15,30},{16,1},... | collective-permute-start | bytes 7077896 | tf_op jit(solution)/shard_map/ppermute | solution.py:729
  77.4 4.6 %collective-permute-start.6 = (bf16[1024,768]{1,0:T(8,128)(2,1)S(1)}, bf16[1024,768]{1,0:T(8,128)(2,1)}, u32[]{:S(2)}, u32[]{:S(2)}) collective-permute-start(bf16[1024,768]{1,0:T(8,128)(2,1)S(1)} %convolution_convert_fusion.refs_3_), channel_id=1, source_target_pairs={{0,1},{1,0},{2,3},{3,2},{4,5},{5,4},{6,7},{7,6},{8,9},{9,8},{10,11... | collective-permute-start | bytes 4718600 | tf_op jit(solution)/shard_map/ppermute | solution.py:752
  77.5 4.4 %collective-permute-start.7 = (bf16[512,768]{1,0:T(8,128)(2,1)S(1)}, bf16[512,768]{1,0:T(8,128)(2,1)S(1)}, u32[]{:S(2)}, u32[]{:S(2)}) collective-permute-start(bf16[512,768]{1,0:T(8,128)(2,1)S(1)} %slice.53.refs_5_), channel_id=1, source_target_pairs={{0,1},{1,0},{2,3},{3,2},{4,5},{5,4},{6,7},{7,6},{8,9},{9,8},{10,11... | collective-permute-start | bytes 2359304 | tf_op jit(solution)/shard_map/ppermute | solution.py:752
  102.2 103.8 %reduce-scatter.8.cloned.1.call-start = ((), (), s32[]{:S(2)}) async-start(), calls=%async_computation.4 | async-start | bytes 737280 | tf_op jit(solution)/shard_map/reduce_scatter | solution.py:779
  118.6 5.9 %collective-permute-start.10 = (bf16[1024,768]{1,0:T(8,128)(2,1)}, bf16[1024,768]{1,0:T(8,128)(2,1)S(1)}, u32[]{:S(2)}, u32[]{:S(2)}) collective-permute-start(bf16[1024,768]{1,0:T(8,128)(2,1)} %get-tuple-element.125.back_own), channel_id=1, source_target_pairs={{0,1},{1,0},{2,3},{3,2},{4,5},{5,4},{6,7},{7,6},{8,9},{9,8},{10,11... | collective-permute-start | bytes 4718600 | tf_op jit(solution)/shard_map/ppermute | solution.py:752
  118.8 35.8 %collective-permute-start.12 = (bf16[768,384]{1,0:T(8,128)(2,1)}, bf16[768,384]{1,0:T(8,128)(2,1)S(1)}, u32[]{:S(2)}, u32[]{:S(2)}) collective-permute-start(bf16[768,384]{1,0:T(8,128)(2,1)} %get-tuple-element.130), channel_id=1, source_target_pairs={{0,1},{1,17},{2,3},{3,19},{4,5},{5,21},{6,7},{7,23},{8,9},{9,25},{... | collective-permute-start | bytes 1769480 | tf_op jit(solution)/shard_map/ppermute | solution.py:733
  119.7 35.0 %collective-permute-start.13 = (bf16[768,384]{1,0:T(8,128)(2,1)}, bf16[768,384]{1,0:T(8,128)(2,1)S(1)}, u32[]{:S(2)}, u32[]{:S(2)}) collective-permute-start(bf16[768,384]{1,0:T(8,128)(2,1)} %get-tuple-element.131), channel_id=1, source_target_pairs={{0,2},{1,18},{2,0},{3,16},{4,6},{5,22},{6,4},{7,20},{8,10},{9,26},... | collective-permute-start | bytes 1769480 | tf_op jit(solution)/shard_map/ppermute | solution.py:733
  121.7 33.7 %collective-permute-start.14 = (bf16[768,384]{1,0:T(8,128)(2,1)}, bf16[768,384]{1,0:T(8,128)(2,1)S(1)}, u32[]{:S(2)}, u32[]{:S(2)}) collective-permute-start(bf16[768,384]{1,0:T(8,128)(2,1)} %get-tuple-element.132), channel_id=1, source_target_pairs={{0,3},{1,19},{2,1},{3,17},{4,7},{5,23},{6,5},{7,21},{8,11},{9,27},... | collective-permute-start | bytes 1769480 | tf_op jit(solution)/shard_map/ppermute | solution.py:733
  121.7 33.7 %collective-permute-start.11 = (bf16[768,384]{1,0:T(8,128)(2,1)}, bf16[768,384]{1,0:T(8,128)(2,1)S(1)}, u32[]{:S(2)}, u32[]{:S(2)}) collective-permute-start(bf16[768,384]{1,0:T(8,128)(2,1)} %get-tuple-element.129), channel_id=1, source_target_pairs={{1,16},{3,18},{5,20},{7,22},{9,24},{11,26},{13,28},{15,30},{16,1},... | collective-permute-start | bytes 1769480 | tf_op jit(solution)/shard_map/ppermute | solution.py:733
  154.6 8.0 %copy-start.41 = (bf16[768,384]{1,0:T(8,128)(2,1)}, bf16[768,384]{1,0:T(8,128)(2,1)S(1)}, u32[]{:S(2)}) copy-start(bf16[768,384]{1,0:T(8,128)(2,1)S(1)} %collective-permute-done.12) | copy-start | bytes 1769476
  154.6 8.0 %copy-start.42 = (bf16[768,384]{1,0:T(8,128)(2,1)}, bf16[768,384]{1,0:T(8,128)(2,1)S(1)}, u32[]{:S(2)}) copy-start(bf16[768,384]{1,0:T(8,128)(2,1)S(1)} %collective-permute-done.13) | copy-start | bytes 1769476
  155.4 7.2 %copy-start.43 = (bf16[768,384]{1,0:T(8,128)(2,1)}, bf16[768,384]{1,0:T(8,128)(2,1)S(1)}, u32[]{:S(2)}) copy-start(bf16[768,384]{1,0:T(8,128)(2,1)S(1)} %collective-permute-done.14) | copy-start | bytes 1769476
  155.4 7.3 %copy-start.44 = (bf16[768,384]{1,0:T(8,128)(2,1)}, bf16[768,384]{1,0:T(8,128)(2,1)S(1)}, u32[]{:S(2)}) copy-start(bf16[768,384]{1,0:T(8,128)(2,1)S(1)} %collective-permute-done.11) | copy-start | bytes 1769476
  155.5 70.1 %reduce-scatter.6.cloned.1.call-start = ((), (), s32[]{:S(2)}) async-start(), calls=%async_computation.3 | async-start | bytes 737280 | tf_op jit(solution)/shard_map/reduce_scatter | solution.py:779
  162.7 9.7 %copy-start = (bf16[3,1024,384]{2,1,0:T(8,128)(2,1)S(1)}, bf16[3,1024,384]{2,1,0:T(8,128)(2,1)}, u32[]{:S(2)}) copy-start(bf16[3,1024,384]{2,1,0:T(8,128)(2,1)} %shard_map.226.query_ref.key_ref.value_ref.grad_ref) | copy-start | bytes 7077892
  162.7 9.7 %copy-start.7 = (bf16[3,384,384]{2,1,0:T(8,128)(2,1)S(1)}, bf16[3,384,384]{2,1,0:T(8,128)(2,1)}, u32[]{:S(2)}) copy-start(bf16[3,384,384]{2,1,0:T(8,128)(2,1)} %copy-done.6) | copy-start | bytes 2654212
  162.7 9.7 %copy-start.28 = (s32[4]{0:T(128)S(1)}, s32[4]{0:T(128)}, u32[]{:S(2)}) copy-start(s32[4]{0:T(128)} %pad_add_fusion.flags.refs_0_) | copy-start | bytes 52
  165.7 24.7 %collective-permute-start.16 = (bf16[768,384]{1,0:T(8,128)(2,1)}, bf16[768,384]{1,0:T(8,128)(2,1)S(1)}, u32[]{:S(2)}, u32[]{:S(2)}) collective-permute-start(bf16[768,384]{1,0:T(8,128)(2,1)} %get-tuple-element.149), channel_id=1, source_target_pairs={{0,1},{1,17},{2,3},{3,19},{4,5},{5,21},{6,7},{7,23},{8,9},{9,25},{... | collective-permute-start | bytes 1769480 | tf_op jit(solution)/shard_map/ppermute | solution.py:733
  166.8 24.4 %collective-permute-start.17 = (bf16[768,384]{1,0:T(8,128)(2,1)}, bf16[768,384]{1,0:T(8,128)(2,1)S(1)}, u32[]{:S(2)}, u32[]{:S(2)}) collective-permute-start(bf16[768,384]{1,0:T(8,128)(2,1)} %get-tuple-element.150), channel_id=1, source_target_pairs={{0,2},{1,18},{2,0},{3,16},{4,6},{5,22},{6,4},{7,20},{8,10},{9,26},... | collective-permute-start | bytes 1769480 | tf_op jit(solution)/shard_map/ppermute | solution.py:733
  168.9 26.1 %collective-permute-start.18 = (bf16[768,384]{1,0:T(8,128)(2,1)}, bf16[768,384]{1,0:T(8,128)(2,1)S(1)}, u32[]{:S(2)}, u32[]{:S(2)}) collective-permute-start(bf16[768,384]{1,0:T(8,128)(2,1)} %get-tuple-element.151), channel_id=1, source_target_pairs={{0,3},{1,19},{2,1},{3,17},{4,7},{5,23},{6,5},{7,21},{8,11},{9,27},... | collective-permute-start | bytes 1769480 | tf_op jit(solution)/shard_map/ppermute | solution.py:733
  168.9 27.0 %collective-permute-start.15 = (bf16[768,384]{1,0:T(8,128)(2,1)}, bf16[768,384]{1,0:T(8,128)(2,1)S(1)}, u32[]{:S(2)}, u32[]{:S(2)}) collective-permute-start(bf16[768,384]{1,0:T(8,128)(2,1)} %get-tuple-element.136.own_ref), channel_id=1, source_target_pairs={{1,16},{3,18},{5,20},{7,22},{9,24},{11,26},{13,28},{15,30},{16,1},... | collective-permute-start | bytes 1769480 | tf_op jit(solution)/shard_map/ppermute | solution.py:733
  176.4 7.0 %copy-start.11 = (bf16[1024,768]{1,0:T(8,128)(2,1)S(1)}, bf16[1024,768]{1,0:T(8,128)(2,1)}, u32[]{:S(2)}) copy-start(bf16[1024,768]{1,0:T(8,128)(2,1)} %get-tuple-element.139.act_early) | copy-start | bytes 4718596
  176.4 7.0 %copy-start.12 = (bf16[1024,768]{1,0:T(8,128)(2,1)S(1)}, bf16[1024,768]{1,0:T(8,128)(2,1)}, u32[]{:S(2)}) copy-start(bf16[1024,768]{1,0:T(8,128)(2,1)} %get-tuple-element.140.act_late) | copy-start | bytes 4718596
  176.4 7.0 %copy-start.13 = (bf16[768,768]{1,0:T(8,128)(2,1)S(1)}, bf16[768,768]{1,0:T(8,128)(2,1)}, u32[]{:S(2)}) copy-start(bf16[768,768]{1,0:T(8,128)(2,1)} %get-tuple-element.142.early_ref) | copy-start | bytes 3538948
  184.7 13.1 %copy-start.47 = (f32[8,768]{1,0:T(8,128)S(1)}, f32[8,768]{1,0:T(8,128)}, u32[]{:S(2)}) copy-start(f32[8,768]{1,0:T(8,128)} %get-tuple-element.167) | copy-start | bytes 73732
  184.7 13.8 %copy-start.17 = (bf16[768,384]{1,0:T(8,128)(2,1)S(1)}, bf16[768,384]{1,0:T(8,128)(2,1)}, u32[]{:S(2)}) copy-start(bf16[768,384]{1,0:T(8,128)(2,1)} %get-tuple-element.136.own_ref) | copy-start | bytes 1769476
  196.7 9.3 %collective-permute-start.19 = (bf16[256,768]{1,0:T(8,128)(2,1)}, bf16[256,768]{1,0:T(8,128)(2,1)S(1)}, u32[]{:S(2)}, u32[]{:S(2)}) collective-permute-start(bf16[256,768]{1,0:T(8,128)(2,1)} %get-tuple-element.160), channel_id=1, source_target_pairs={{0,1},{1,0},{2,3},{3,2},{4,5},{5,4},{6,7},{7,6},{8,9},{9,8},{10,11... | collective-permute-start | bytes 1179656 | tf_op jit(solution)/shard_map/ppermute | solution.py:752
  197.0 10.2 %collective-permute-start.20 = (bf16[256,768]{1,0:T(8,128)(2,1)}, bf16[256,768]{1,0:T(8,128)(2,1)S(1)}, u32[]{:S(2)}, u32[]{:S(2)}) collective-permute-start(bf16[256,768]{1,0:T(8,128)(2,1)} %get-tuple-element.161), channel_id=1, source_target_pairs={{0,1},{1,0},{2,3},{3,2},{4,5},{5,4},{6,7},{7,6},{8,9},{9,8},{10,11... | collective-permute-start | bytes 1179656 | tf_op jit(solution)/shard_map/ppermute | solution.py:752
  197.2 11.2 %collective-permute-start.21 = (bf16[256,768]{1,0:T(8,128)(2,1)S(1)}, bf16[256,768]{1,0:T(8,128)(2,1)}, u32[]{:S(2)}, u32[]{:S(2)}) collective-permute-start(bf16[256,768]{1,0:T(8,128)(2,1)S(1)} %get-tuple-element.162), channel_id=1, source_target_pairs={{0,1},{1,0},{2,3},{3,2},{4,5},{5,4},{6,7},{7,6},{8,9},{9,8},{10,11... | collective-permute-start | bytes 1179656 | tf_op jit(solution)/shard_map/ppermute | solution.py:752
  197.5 15.8 %collective-permute-start.22 = (bf16[256,768]{1,0:T(8,128)(2,1)S(1)}, bf16[256,768]{1,0:T(8,128)(2,1)}, u32[]{:S(2)}, u32[]{:S(2)}) collective-permute-start(bf16[256,768]{1,0:T(8,128)(2,1)S(1)} %get-tuple-element.163), channel_id=1, source_target_pairs={{0,1},{1,0},{2,3},{3,2},{4,5},{5,4},{6,7},{7,6},{8,9},{9,8},{10,11... | collective-permute-start | bytes 1179656 | tf_op jit(solution)/shard_map/ppermute | solution.py:752
  204.6 20.9 %collective-permute-start.27 = (bf16[192,384]{1,0:T(8,128)(2,1)}, bf16[192,384]{1,0:T(8,128)(2,1)S(1)}, u32[]{:S(2)}, u32[]{:S(2)}) collective-permute-start(bf16[192,384]{1,0:T(8,128)(2,1)} %get-tuple-element.178), channel_id=1, source_target_pairs={{0,4},{4,8},{8,12},{12,0},{1,5},{5,9},{9,13},{13,1},{2,6},{6,10},{... | collective-permute-start | bytes 442376 | tf_op jit(solution)/shard_map/ppermute | solution.py:788
  206.0 7.3 %copy-start.45 = (bf16[256,768]{1,0:T(8,128)(2,1)}, bf16[256,768]{1,0:T(8,128)(2,1)S(1)}, u32[]{:S(2)}) copy-start(bf16[256,768]{1,0:T(8,128)(2,1)S(1)} %collective-permute-done.19.got_first) | copy-start | bytes 1179652
  206.0 19.5 %collective-permute-start.28 = (bf16[192,384]{1,0:T(8,128)(2,1)S(1)}, bf16[192,384]{1,0:T(8,128)(2,1)S(1)}, u32[]{:S(2)}, u32[]{:S(2)}) collective-permute-start(bf16[192,384]{1,0:T(8,128)(2,1)S(1)} %get-tuple-element.179), channel_id=1, source_target_pairs={{0,8},{4,12},{8,0},{12,4},{1,9},{5,13},{9,1},{13,5},{2,10},{6,14},... | collective-permute-start | bytes 442376 | tf_op jit(solution)/shard_map/ppermute | solution.py:788
  207.2 18.3 %collective-permute-start.29 = (bf16[192,384]{1,0:T(8,128)(2,1)S(1)}, bf16[192,384]{1,0:T(8,128)(2,1)S(1)}, u32[]{:S(2)}, u32[]{:S(2)}) collective-permute-start(bf16[192,384]{1,0:T(8,128)(2,1)S(1)} %get-tuple-element.180), channel_id=1, source_target_pairs={{0,12},{4,0},{8,4},{12,8},{1,13},{5,1},{9,5},{13,9},{2,14},{6,2},{... | collective-permute-start | bytes 442376 | tf_op jit(solution)/shard_map/ppermute | solution.py:788
  208.4 17.1 %collective-permute-start.26 = (bf16[192,384]{1,0:T(8,128)(2,1)}, bf16[192,384]{1,0:T(8,128)(2,1)S(1)}, u32[]{:S(2)}, u32[]{:S(2)}) collective-permute-start(bf16[192,384]{1,0:T(8,128)(2,1)} %reduce-scatter.8.cloned.1.call-done.early_own), channel_id=1, source_target_pairs={{1,16},{3,18},{5,20},{7,22},{9,24},{11,26},{13,28},{15,30},{16,1},... | collective-permute-start | bytes 442376 | tf_op jit(solution)/shard_map/ppermute | solution.py:729
  213.4 12.2 %copy-start.26 = (bf16[192,384]{1,0:T(8,128)(2,1)S(1)}, bf16[192,384]{1,0:T(8,128)(2,1)}, u32[]{:S(2)}) copy-start(bf16[192,384]{1,0:T(8,128)(2,1)} %reduce-scatter.8.cloned.1.call-done.early_own) | copy-start | bytes 442372
  213.4 12.2 %copy-start.29 = (s32[4]{0:T(128)S(1)}, s32[4]{0:T(128)}, u32[]{:S(2)}) copy-start(s32[4]{0:T(128)} %pad_add_fusion.flags.refs_0_) | copy-start | bytes 52
  218.7 8.7 %copy-start.4 = (bf16[2,512,768]{2,1,0:T(8,128)(2,1)S(1)}, bf16[2,512,768]{2,1,0:T(8,128)(2,1)}, u32[]{:S(2)}) copy-start(bf16[2,512,768]{2,1,0:T(8,128)(2,1)} %shard_map.231.own_ref) | copy-start | bytes 4718596
  218.7 2.9 %collective-permute-start.24 = (f32[9,768]{1,0:T(8,128)S(1)}, f32[9,768]{1,0:T(8,128)S(1)}, u32[]{:S(2)}, u32[]{:S(2)}) collective-permute-start(f32[9,768]{1,0:T(8,128)S(1)} %pad_maximum_fusion.4), channel_id=1, source_target_pairs={{0,16},{16,0},{1,17},{17,1},{2,18},{18,2},{3,19},{19,3},{4,20},{20... | collective-permute-start | bytes 82952 | tf_op jit(solution)/shard_map/ppermute | solution.py:796
  221.7 3.8 %collective-permute-start.25 = (f32[9,768]{1,0:T(8,128)S(1)}, f32[9,768]{1,0:T(8,128)S(1)}, u32[]{:S(2)}, u32[]{:S(2)}) collective-permute-start(f32[9,768]{1,0:T(8,128)S(1)} %add.54), channel_id=1, source_target_pairs={{0,2},{2,0},{1,3},{3,1},{4,6},{6,4},{5,7},{7,5},{8,10},{10,8},{9,1... | collective-permute-start | bytes 82952 | tf_op jit(solution)/shard_map/ppermute | solution.py:796
  226.5 15.6 %copy-start.30 = (f32[5]{0:T(128)S(1)}, f32[5]{0:T(128)}, u32[]{:S(2)}) copy-start(f32[5]{0:T(128)} %weight_ref.1) | copy-start | bytes 64
  227.1 12.7 %collective-permute-start.30 = (bf16[192,1152]{1,0:T(8,128)(2,1)S(1)}, bf16[192,1152]{1,0:T(8,128)(2,1)S(1)}, u32[]{:S(2)}, u32[]{:S(2)}) collective-permute-start(bf16[192,1152]{1,0:T(8,128)(2,1)S(1)} %shard_map.232), channel_id=1, source_target_pairs={{0,2},{2,0},{1,3},{3,1},{4,6},{6,4},{5,7},{7,5},{8,10},{10,8},{9,1... | collective-permute-start | bytes 1327112 | tf_op jit(solution)/shard_map/ppermute | solution.py:748
  227.5 21.8 %collective-permute-start.23 = (bf16[2,512,768]{2,1,0:T(8,128)(2,1)S(1)}, bf16[2,512,768]{2,1,0:T(8,128)(2,1)S(1)}, u32[]{:S(2)}, u32[]{:S(2)}) collective-permute-start(bf16[2,512,768]{2,1,0:T(8,128)(2,1)S(1)} %copy-done.4), channel_id=1, source_target_pairs={{1,16},{3,18},{5,20},{7,22},{9,24},{11,26},{13,28},{15,30},{16,1},... | collective-permute-start | bytes 4718600 | tf_op jit(solution)/shard_map/ppermute | solution.py:729
  231.2 1.3 collective-permute-start.31
  232.5 3.3 %collective-permute-start.32 = (f32[9,768]{1,0:T(8,128)S(1)}, f32[9,768]{1,0:T(8,128)S(1)}, u32[]{:S(2)}, u32[]{:S(2)}) collective-permute-start(f32[9,768]{1,0:T(8,128)S(1)} %add.59), channel_id=1, source_target_pairs={{0,4},{4,0},{8,12},{12,8},{1,5},{5,1},{9,13},{13,9},{2,6},{6,2},{1... | collective-permute-start | bytes 82952 | tf_op jit(solution)/shard_map/ppermute | solution.py:796
  235.8 4.0 %collective-permute-start.33 = (f32[9,768]{1,0:T(8,128)S(1)}, f32[9,768]{1,0:T(8,128)S(1)}, u32[]{:S(2)}, u32[]{:S(2)}) collective-permute-start(f32[9,768]{1,0:T(8,128)S(1)} %add.60), channel_id=1, source_target_pairs={{0,8},{4,12},{8,0},{12,4},{1,9},{5,13},{9,1},{13,5},{2,10},{6,14},... | collective-permute-start | bytes 82952 | tf_op jit(solution)/shard_map/ppermute | solution.py:796
  239.8 9.4 %copy-start.10 = (f32[512,768]{1,0:T(8,128)S(1)}, f32[512,768]{1,0:T(8,128)}, u32[]{:S(2)}) copy-start(f32[512,768]{1,0:T(8,128)} %get-tuple-element.106.part_ref) | copy-start | bytes 4718596
  239.9 4.7 %collective-permute-start.34 = (bf16[2,192,1152]{2,1,0:T(8,128)(2,1)S(1)}, bf16[2,192,1152]{2,1,0:T(8,128)(2,1)S(1)}, u32[]{:S(2)}, u32[]{:S(2)}) collective-permute-start(bf16[2,192,1152]{2,1,0:T(8,128)(2,1)S(1)} %pad_maximum_fusion.3.here_ref), channel_id=1, source_target_pairs={{0,1},{1,0},{2,3},{3,2},{4,5},{5,4},{6,7},{7,6},{8,9},{9,8},{10,11... | collective-permute-start | bytes 2654216 | tf_op jit(solution)/shard_map/ppermute | solution.py:752
  (27 other events, 65.3 us)
Sparse Core Ops, SparseCore 0:
  102.3 46.5 reduce-scatter.9
  155.6 18.3 reduce-scatter.7
  176.3 20.3 reduce-scatter.5

commit v15 on v13

--- a/solution.py
+++ b/solution.py
@@ -526,6 +526,7 @@
         ],
         [((width, columns), jnp.float32)],
         8,
+        40 << 20,
     )
 
 

time: 253 us -> 255 us (level)
  local copies, waits for them, and re-layouts: 17.9 us -> 23 us
  Pallas kernels: 120 us -> 116 us
    unnamed x94 -> x98, local copies, waits for them, and re-layouts: 11.1 us -> 16.3 us
    pallas_call x11, Pallas kernels: 82.6 us -> 79.1 us  [streamed(): pl.pallas_call(kernel, grid_spec=pltpu.PrefetchScalarGridSpec(num_scalar_...]
  transfers between devices with their start and end apart: 38 -> 38, of which waited for: 10 -> 9; matrix products, arithmetic and copies ran while one was open for 13% -> 13% of each run, Pallas kernels for 46% -> 45%
where the time goes in v15:
time: 255 us; the launch traced here: 254 us
  Pallas kernels  116 us (45%)
  starting transfers between devices  49.1 us (19%)
  waiting for transfers between devices  25.6 us (10%)
  other arithmetic  24.5 us (10%)
  local copies, waits for them, and re-layouts  23 us (9%)
  between operations  14.6 us (6%)
    pallas_call x11, Pallas kernels, streamed(): pl.pallas_call(kernel, grid_spec=pltpu.PrefetchScalarGridSpec(num_scalar_...  79.1 us
    ppermute x7, starting transfers between devices, swap_diagonal(): lax.ppermute(field, AXES, moves(away, lambda t, d, k, c: (c, d, k, t)))  23.3 us
    pallas_call x1, Pallas kernels, attend_back(): pl.pallas_call(functools.partial(attend_back_kernel, reach), grid=(width...  19.6 us
    unnamed x98, local copies, waits for them, and re-layouts  16.3 us
    ppermute x5, waiting for transfers between devices, sum_over(): lax.ppermute(field, name, [(d, d ^ bit) for d in range(size)])  13.4 us
    pallas_call x1, Pallas kernels, attend(): pl.pallas_call(functools.partial(attend_kernel, reach), grid=(width // LA...  13 us
    ppermute x8, starting transfers between devices, send_to_owner(): lax.ppermute(field, AXES, moves(away if not other_far and (not other_tp)...  10.7 us
  transfers between devices with their start and end apart: 38, of which 9 were waited for; matrix products, arithmetic and copies ran while one was open for 13% of the time, Pallas kernels for 45%

profile of v15, /device:TPU:9, one launch (start us, length us, event | category | flops | bytes accessed | tf_op | source)
XLA Modules:
  0.0 253.9 jit_solution(9010331160171301880)
XLA Ops:
  8.0 3.1 %collective-permute-start = (bf16[512,768]{1,0:T(8,128)(2,1)}, bf16[512,768]{1,0:T(8,128)(2,1)}, u32[]{:S(2)}, u32[]{:S(2)}) collective-permute-start(bf16[512,768]{1,0:T(8,128)(2,1)} %bitcast.45), channel_id=1, source_target_pairs={{1,16},{3,18},{5,20},{7,22},{9,24},{11,26},{13,28},{15,30},{16,1},... | collective-permute-start | bytes 2359304 | tf_op jit(solution)/shard_map/ppermute | solution.py:713
  11.1 2.2 constant_dynamic-slice_fusion
  13.2 2.6 %collective-permute-start.3 = (bf16[3,384,384]{2,1,0:T(8,128)(2,1)}, bf16[3,384,384]{2,1,0:T(8,128)(2,1)S(1)}, u32[]{:S(2)}, u32[]{:S(2)}) collective-permute-start(bf16[3,384,384]{2,1,0:T(8,128)(2,1)} %constant_dynamic-slice_fusion), channel_id=1, source_target_pairs={{1,16},{3,18},{5,20},{7,22},{9,24},{11,26},{13,28},{15,30},{16,1},... | collective-permute-start | bytes 2654216 | tf_op jit(solution)/shard_map/ppermute | solution.py:713
  16.0 2.5 pad_maximum_fusion.2
  18.5 1.9 fusion.9
  20.4 1.6 pad_maximum_fusion.1
  22.0 1.5 pad_maximum_fusion
  23.6 4.3 %shard_map.220 = (bf16[4,512,768]{2,1,0:T(8,128)(2,1)}, f32[512,768]{1,0:T(8,128)}, f32[8,768]{1,0:T(8,128)}) custom-call(f32[5]{0:T(128)} %weight_ref.1, bf16[4,512,768]{2,1,0:T(8,128)(2,1)} %bitcast.43, bf16[512,768]{1,0:T(8,128)(2,1)} %bitcast.41), custom_call_target="tpu_custom_call" | custom-call | bytes 9000000 | tf_op jit(solution)/shard_map/pallas_call | solution.py:628
  29.5 3.1 %collective-permute-start.5 = (bf16[896,768]{1,0:T(8,128)(2,1)}, bf16[896,768]{1,0:T(8,128)(2,1)}, u32[]{:S(2)}, u32[]{:S(2)}) collective-permute-start(bf16[896,768]{1,0:T(8,128)(2,1)} %pad_maximum_fusion.2), channel_id=1, source_target_pairs={{1,16},{3,18},{5,20},{7,22},{9,24},{11,26},{13,28},{15,30},{16,1},... | collective-permute-start | bytes 4128776 | tf_op jit(solution)/shard_map/ppermute | solution.py:713
  32.6 1.2 broadcast_select_fusion.1
  33.9 3.1 %collective-permute-start.4 = (bf16[3,384,384]{2,1,0:T(8,128)(2,1)S(1)}, bf16[3,384,384]{2,1,0:T(8,128)(2,1)S(1)}, u32[]{:S(2)}, u32[]{:S(2)}) collective-permute-start(bf16[3,384,384]{2,1,0:T(8,128)(2,1)S(1)} %collective-permute-done.3.w_near), channel_id=1, source_target_pairs={{1,3},{3,1},{5,7},{7,5},{9,11},{11,9},{13,15},{15,13},{16,18},{18,... | collective-permute-start | bytes 2654216 | tf_op jit(solution)/shard_map/ppermute | solution.py:728
  37.0 0.9 fusion.2.member_ref
  37.9 0.9 select_convert_fusion.apart_ref
  38.8 3.1 %fusion.1 = (f32[1024,128]{1,0:T(8,128)}, f32[1024,128]{1,0:T(8,128)}) fusion(f32[128]{0:T(128)S(1)} %get-tuple-element.241, f32[128]{0:T(128)S(1)} %get-tuple-element.242, f32[1024]{0:T(1024)S(1)} %subtract_convert_fusion), kind=kLoop, calls=%fused_computation.13 | loop fusion | flops 262144 | bytes 1053696 | tf_op jit(solution)/shard_map/mul | solution.py:828
  41.9 2.8 %collective-permute-start.8 = (bf16[1536,768]{1,0:T(8,128)(2,1)}, bf16[1536,768]{1,0:T(8,128)(2,1)}, u32[]{:S(2)}, u32[]{:S(2)}) collective-permute-start(bf16[1536,768]{1,0:T(8,128)(2,1)} %pad_maximum_fusion), channel_id=1, source_target_pairs={{1,16},{3,18},{5,20},{7,22},{9,24},{11,26},{13,28},{15,30},{16,1},... | collective-permute-start | bytes 7077896 | tf_op jit(solution)/shard_map/ppermute | solution.py:713
  44.7 1.8 maximum_select_fusion.rows_ref.refs_2_
  46.5 1.2 collective-permute-done.4.w_far
  47.7 0.9 copy-done.10
  48.6 9.0 %shard_map.221 = (bf16[3,1024,384]{2,1,0:T(8,128)(2,1)}, bf16[768,1024]{1,0:T(8,128)(2,1)}) custom-call(s32[4]{0:T(128)} %pad_add_fusion.flags.refs_0_, bf16[1024,768]{1,0:T(8,128)(2,1)} %maximum_select_fusion.rows_ref.refs_2_, f32[1024,128]{1,0:T(8,128)} %get-tuple-element.106.cos_ref, f32[1024,128]{1,0:T(8,128)} %get-tuple-element.107.sin_ref, ...), custom_call_target="tpu_custom_call" | custom-call | bytes 24000000 | tf_op jit(solution)/shard_map/pallas_call | solution.py:240
  57.6 13.0 %shard_map.222 = (bf16[1024,384]{1,0:T(8,128)(2,1)}, f32[3,8,1024]{2,1,0:T(8,128)}) custom-call(bf16[1024,128]{1,0:T(8,128)(2,1)} %select_convert_fusion.apart_ref, bf16[1024,128]{1,0:T(8,128)(2,1)} %fusion.2.member_ref, bf16[3,1024,384]{2,1,0:T(8,128)(2,1)} %get-tuple-element.109.q_ref.k_ref.v_ref, ...), custom_call_target="tpu_custom_call" | custom-call | bytes 36000000 | tf_op jit(solution)/shard_map/pallas_call | solution.py:104
  70.6 4.0 %collective-permute-start.9 = (bf16[1536,768]{1,0:T(8,128)(2,1)}, bf16[1536,768]{1,0:T(8,128)(2,1)}, u32[]{:S(2)}, u32[]{:S(2)}) collective-permute-start(bf16[1536,768]{1,0:T(8,128)(2,1)} %pad_maximum_fusion.1), channel_id=1, source_target_pairs={{1,16},{3,18},{5,20},{7,22},{9,24},{11,26},{13,28},{15,30},{16,1},... | collective-permute-start | bytes 7077896 | tf_op jit(solution)/shard_map/ppermute | solution.py:713
  74.6 1.7 broadcast_select_fusion.w_ref
  76.3 1.0 convolution_convert_fusion.refs_3_
  78.0 3.9 %collective-permute-done.7.refs_6_ = bf16[512,768]{1,0:T(8,128)(2,1)S(1)} collective-permute-done((bf16[512,768]{1,0:T(8,128)(2,1)S(1)}, bf16[512,768]{1,0:T(8,128)(2,1)S(1)}, u32[]{:S(2)}, u32[]{:S(2)}) %collective-permute-start.7) | collective-permute-done | bytes 786464 | tf_op jit(solution)/shard_map/ppermute | solution.py:736
  82.8 19.3 %shard_map.223 = (bf16[1024,768]{1,0:T(8,128)(2,1)}, bf16[768,1024]{1,0:T(8,128)(2,1)}, bf16[1024,768]{1,0:T(8,128)(2,1)}, bf16[768,1024]{1,0:T(8,128)(2,1)}, bf...) custom-call(s32[4]{0:T(128)} %pad_add_fusion.flags.refs_0_, ...), custom_call_target="tpu_custom_call" | custom-call | bytes 51000000 | tf_op jit(solution)/shard_map/pallas_call | solution.py:240
  102.2 16.5 %shard_map.224 = (bf16[1024,768]{1,0:T(8,128)(2,1)}, bf16[1024,768]{1,0:T(8,128)(2,1)}, bf16[768,768]{1,0:T(8,128)(2,1)}, bf16[768,384]{1,0:T(8,128)(2,1)}, bf16...) custom-call(s32[4]{0:T(128)} %pad_add_fusion.flags.refs_0_, ...), custom_call_target="tpu_custom_call" | custom-call | bytes 51000000 | tf_op jit(solution)/shard_map/pallas_call | solution.py:240
  118.8 0.9 collective-permute-start.12
  119.7 2.0 collective-permute-start.13
  121.8 2.8 %collective-permute-start.11 = (bf16[768,384]{1,0:T(8,128)(2,1)}, bf16[768,384]{1,0:T(8,128)(2,1)}, u32[]{:S(2)}, u32[]{:S(2)}) collective-permute-start(bf16[768,384]{1,0:T(8,128)(2,1)} %get-tuple-element.125), channel_id=1, source_target_pairs={{1,16},{3,18},{5,20},{7,22},{9,24},{11,26},{13,28},{15,30},{16,1},... | collective-permute-start | bytes 1769480 | tf_op jit(solution)/shard_map/ppermute | solution.py:717
  124.6 1.4 copy-done.6
  126.0 1.4 copy-done.14
  127.5 5.9 %shard_map.225 = (bf16[1024,768]{1,0:T(8,128)(2,1)S(1)}, bf16[1024,384]{1,0:T(8,128)(2,1)S(1)}, bf16[768,384]{1,0:T(8,128)(2,1)S(1)}, f32[8,768]{1,0:T(8,128)S(1)}) custom-call(s32[4]{0:T(128)S(1)} %copy-done.27, bf16[1024,768]{1,0:T(8,128)(2,1)S(1)} %copy-done.6, bf16[1024,768]{1,0:T(8,128)(2,1)S(1)} %copy-done.2, bf16[1024,768]{1,0:T(8,128)(2,1)S(1)} %copy-done.14, ...), custom_call_target="tpu_custom_call" | custom-call | bytes 24000000 | tf_op jit(solution)/shard_map/pallas_call | solution.py:240
  133.3 1.1 copy-done.15
  134.5 0.9 copy-done.22
  136.2 19.6 %shard_map.226.query_ref.key_ref.value_ref.grad_ref = bf16[3,1024,384]{2,1,0:T(8,128)(2,1)} custom-call(bf16[1024,128]{1,0:T(8,128)(2,1)} %select_convert_fusion.apart_ref, bf16[1024,128]{1,0:T(8,128)(2,1)} %fusion.2.member_ref, f32[1024,128]{1,0:T(8,128)} %get-tuple-element.106.cos_ref, f32[1024,128]{1,0:T(8,128)} %get-tuple-element.107.sin_ref, ...), custom_call_target="tpu_custom_call" | custom-call | bytes 66000000 | tf_op jit(solution)/shard_map/pallas_call | solution.py:189
  155.9 7.1 %shard_map.227 = (bf16[768,384]{1,0:T(8,128)(2,1)}, bf16[768,384]{1,0:T(8,128)(2,1)}, bf16[768,384]{1,0:T(8,128)(2,1)}, bf16[768,384]{1,0:T(8,128)(2,1)}) custom-call(s32[4]{0:T(128)} %pad_add_fusion.flags.refs_0_, bf16[768,1024]{1,0:T(8,128)(2,1)} %get-tuple-element.130.turned_ref, bf16[768,384]{1,0:T(8,128)(2,1)} %copy-done.23, ...), custom_call_target="tpu_custom_call" | custom-call | bytes 12000000 | tf_op jit(solution)/shard_map/pallas_call | solution.py:240
  162.9 2.9 %collective-permute-start.15 = (bf16[768,384]{1,0:T(8,128)(2,1)}, bf16[768,384]{1,0:T(8,128)(2,1)}, u32[]{:S(2)}, u32[]{:S(2)}) collective-permute-start(bf16[768,384]{1,0:T(8,128)(2,1)} %get-tuple-element.132), channel_id=1, source_target_pairs={{1,16},{3,18},{5,20},{7,22},{9,24},{11,26},{13,28},{15,30},{16,1},... | collective-permute-start | bytes 1769480 | tf_op jit(solution)/shard_map/ppermute | solution.py:717
  165.9 1.7 collective-permute-start.17
  168.0 3.0 %add_convert_fusion = bf16[768,384]{1,0:T(8,128)(2,1)} fusion(bf16[768,384]{1,0:T(8,128)(2,1)} %collective-permute-done.14, bf16[768,384]{1,0:T(8,128)(2,1)} %collective-permute-done.13, bf16[768,384]{1,0:T(8,128)(2,1)} %collective-permute-done.12, bf16[768,384]{1,0:T(8,128)(2,1)} %get-tuple-element.125, bf16[768,384]{1,0:T(8,128)(2,1)} %collective-permute-done.11, ...), kind=kLoop, calls=%fused_computation.6 | loop fusion | flops 2654208 | bytes 3538945 | tf_op jit(solution)/shard_map/convert_element_type | solution.py:755
  171.7 1.4 copy-done.1
  173.1 1.5 copy-done.4
  174.6 1.2 copy-done.11
  175.8 6.1 %shard_map.228 = (bf16[512,768]{1,0:T(8,128)(2,1)S(1)}, bf16[256,768]{1,0:T(8,128)(2,1)}, bf16[256,768]{1,0:T(8,128)(2,1)}, f32[8,768]{1,0:T(8,128)S(1)}) custom-call(s32[4]{0:T(128)S(1)} %copy-done.28, bf16[3,1024,384]{2,1,0:T(8,128)(2,1)S(1)} %copy-done, bf16[1024,768]{1,0:T(8,128)(2,1)S(1)} %copy-done.1, bf16[3,768,384]{2,1,0:T(8,128)(2,1)S(1)} %copy-done.4, ...), custom_call_target="tpu_custom_call" | custom-call | bytes 15000000 | tf_op jit(solution)/shard_map/pallas_call | solution.py:240
  182.8 1.3 copy-done.19
  184.0 4.8 %shard_map.229 = (bf16[512,768]{1,0:T(8,128)(2,1)S(1)}, bf16[256,768]{1,0:T(8,128)(2,1)S(1)}, bf16[256,768]{1,0:T(8,128)(2,1)S(1)}, f32[8,768]{1,0:T(8,128)S(1)}) custom-call(s32[4]{0:T(128)S(1)} %copy-done.28, bf16[1024,768]{1,0:T(8,128)(2,1)S(1)} %copy-done.16, bf16[1024,768]{1,0:T(8,128)(2,1)S(1)} %copy-done.17, bf16[1024,768]{1,0:T(8,128)(2,1)S(1)} %copy-done.7, ...), custom_call_target="tpu_custom_call" | custom-call | bytes 18000000 | tf_op jit(solution)/shard_map/pallas_call | solution.py:240
  190.4 4.7 %collective-permute-done.18 = bf16[768,384]{1,0:T(8,128)(2,1)} collective-permute-done((bf16[768,384]{1,0:T(8,128)(2,1)}, bf16[768,384]{1,0:T(8,128)(2,1)}, u32[]{:S(2)}, u32[]{:S(2)}) %collective-permute-start.18) | collective-permute-done | bytes 589856 | tf_op jit(solution)/shard_map/ppermute | solution.py:717
  196.1 2.0 add_convert_fusion.1
  199.0 2.4 collective-permute-start.28
  201.4 2.1 collective-permute-start.27
  203.5 4.0 %collective-permute-start.26 = (bf16[192,384]{1,0:T(8,128)(2,1)}, bf16[192,384]{1,0:T(8,128)(2,1)S(1)}, u32[]{:S(2)}, u32[]{:S(2)}) collective-permute-start(bf16[192,384]{1,0:T(8,128)(2,1)} %reduce-scatter.8.cloned.1.call-done.early_own), channel_id=1, source_target_pairs={{1,16},{3,18},{5,20},{7,22},{9,24},{11,26},{13,28},{15,30},{16,1},... | collective-permute-start | bytes 442376 | tf_op jit(solution)/shard_map/ppermute | solution.py:713
  209.0 5.3 %shard_map.230.own_ref = bf16[2,512,768]{2,1,0:T(8,128)(2,1)} custom-call(s32[4]{0:T(128)} %pad_add_fusion.flags.refs_0_, bf16[1024,768]{1,0:T(8,128)(2,1)} %maximum_select_fusion.rows_ref.refs_2_, bf16[1024,768]{1,0:T(8,128)(2,1)} %copy-done.15, bf16[512,768]{1,0:T(8,128)(2,1)} %copy-done.20, bf16[512,768]{1,0:T(8,128)(2,1)} %copy-done.21, ...), custom_call_target="tpu_custom_call" | custom-call | bytes 9000000 | tf_op jit(solution)/shard_map/pallas_call | solution.py:240
  214.3 2.9 %collective-permute-done.24 = f32[9,768]{1,0:T(8,128)S(1)} collective-permute-done((f32[9,768]{1,0:T(8,128)S(1)}, f32[9,768]{1,0:T(8,128)S(1)}, u32[]{:S(2)}, u32[]{:S(2)}) %collective-permute-start.24) | collective-permute-done | bytes 27680 | tf_op jit(solution)/shard_map/ppermute | solution.py:783
  217.9 3.1 %collective-permute-done.25 = f32[9,768]{1,0:T(8,128)S(1)} collective-permute-done((f32[9,768]{1,0:T(8,128)S(1)}, f32[9,768]{1,0:T(8,128)S(1)}, u32[]{:S(2)}, u32[]{:S(2)}) %collective-permute-start.25) | collective-permute-done | bytes 27680 | tf_op jit(solution)/shard_map/ppermute | solution.py:783
  221.2 0.9 copy-done.26
  223.3 3.8 %collective-permute-start.23 = (bf16[2,512,768]{2,1,0:T(8,128)(2,1)S(1)}, bf16[2,512,768]{2,1,0:T(8,128)(2,1)S(1)}, u32[]{:S(2)}, u32[]{:S(2)}) collective-permute-start(bf16[2,512,768]{2,1,0:T(8,128)(2,1)S(1)} %copy-done.5), channel_id=1, source_target_pairs={{1,16},{3,18},{5,20},{7,22},{9,24},{11,26},{13,28},{15,30},{16,1},... | collective-permute-start | bytes 4718600 | tf_op jit(solution)/shard_map/ppermute | solution.py:713
  227.2 1.2 collective-permute-done.31
  228.5 3.2 %collective-permute-done.32 = f32[9,768]{1,0:T(8,128)S(1)} collective-permute-done((f32[9,768]{1,0:T(8,128)S(1)}, f32[9,768]{1,0:T(8,128)S(1)}, u32[]{:S(2)}, u32[]{:S(2)}) %collective-permute-start.32) | collective-permute-done | bytes 27680 | tf_op jit(solution)/shard_map/ppermute | solution.py:783
  231.8 1.0 collective-permute-start.33
  232.8 2.9 %collective-permute-done.33 = f32[9,768]{1,0:T(8,128)S(1)} collective-permute-done((f32[9,768]{1,0:T(8,128)S(1)}, f32[9,768]{1,0:T(8,128)S(1)}, u32[]{:S(2)}, u32[]{:S(2)}) %collective-permute-start.33) | collective-permute-done | bytes 27680 | tf_op jit(solution)/shard_map/ppermute | solution.py:783
  235.9 2.1 collective-permute-start.34
  238.6 1.3 slice_reduce_fusion
  240.5 2.5 shard_map.232
  243.0 2.3 collective-permute-done.23.got_ref
  245.3 2.1 shard_map.233
  (172 shorter events, 15.5 us)
Async XLA Ops:
  7.2 8.7 %copy-start.44 = (f32[768]{0:T(1024)S(1)}, f32[768]{0:T(1024)}, u32[]{:S(2)}) copy-start(f32[768]{0:T(1024)} %param.18) | copy-start | bytes 9220
  7.2 8.8 %copy-start.45 = (f32[768]{0:T(1024)S(1)}, f32[768]{0:T(1024)}, u32[]{:S(2)}) copy-start(f32[768]{0:T(1024)} %param.19) | copy-start | bytes 9220
  7.2 8.8 %copy-start.46 = (f32[768]{0:T(1024)S(1)}, f32[768]{0:T(1024)}, u32[]{:S(2)}) copy-start(f32[768]{0:T(1024)} %param.22) | copy-start | bytes 9220
  7.2 8.8 %copy-start.47 = (f32[768]{0:T(1024)S(1)}, f32[768]{0:T(1024)}, u32[]{:S(2)}) copy-start(f32[768]{0:T(1024)} %param.23) | copy-start | bytes 9220
  7.2 148.6 %reduce-scatter.10.cloned.1.call-start = ((), (), s32[]{:S(2)}) async-start(), calls=%async_computation.5 | async-start | bytes 2949120
  7.3 21.8 %collective-permute-start.2 = (s32[1,3]{1,0:T(1,128)}, s32[1,3]{1,0:T(1,128)S(1)}, u32[]{:S(2)}, u32[]{:S(2)}) collective-permute-start(s32[1,3]{1,0:T(1,128)} %param.16), channel_id=1, source_target_pairs={{0,1},{1,0},{2,3},{3,2},{4,5},{5,4},{6,7},{7,6},{8,9},{9,8},{10,11... | collective-permute-start | bytes 44 | tf_op jit(solution)/shard_map/ppermute | solution.py:736
  8.0 21.5 %collective-permute-start = (bf16[512,768]{1,0:T(8,128)(2,1)}, bf16[512,768]{1,0:T(8,128)(2,1)}, u32[]{:S(2)}, u32[]{:S(2)}) collective-permute-start(bf16[512,768]{1,0:T(8,128)(2,1)} %bitcast.45), channel_id=1, source_target_pairs={{1,16},{3,18},{5,20},{7,22},{9,24},{11,26},{13,28},{15,30},{16,1},... | collective-permute-start | bytes 2359304 | tf_op jit(solution)/shard_map/ppermute | solution.py:713
  13.2 20.6 %collective-permute-start.3 = (bf16[3,384,384]{2,1,0:T(8,128)(2,1)}, bf16[3,384,384]{2,1,0:T(8,128)(2,1)S(1)}, u32[]{:S(2)}, u32[]{:S(2)}) collective-permute-start(bf16[3,384,384]{2,1,0:T(8,128)(2,1)} %constant_dynamic-slice_fusion), channel_id=1, source_target_pairs={{1,16},{3,18},{5,20},{7,22},{9,24},{11,26},{13,28},{15,30},{16,1},... | collective-permute-start | bytes 2654216 | tf_op jit(solution)/shard_map/ppermute | solution.py:713
  23.6 5.5 %copy-start.48 = (s32[1,3]{1,0:T(1,128)S(1)}, s32[1,3]{1,0:T(1,128)}, u32[]{:S(2)}) copy-start(s32[1,3]{1,0:T(1,128)} %param.16) | copy-start | bytes 40
  23.6 9.0 %copy-start.36 = (bf16[1,512,768]{2,1,0:T(8,128)(2,1)S(1)}, bf16[1,512,768]{2,1,0:T(8,128)(2,1)}, u32[]{:S(2)}) copy-start(bf16[1,512,768]{2,1,0:T(8,128)(2,1)} %param.13) | copy-start | bytes 2359300
  29.5 45.1 %collective-permute-start.5 = (bf16[896,768]{1,0:T(8,128)(2,1)}, bf16[896,768]{1,0:T(8,128)(2,1)}, u32[]{:S(2)}, u32[]{:S(2)}) collective-permute-start(bf16[896,768]{1,0:T(8,128)(2,1)} %pad_maximum_fusion.2), channel_id=1, source_target_pairs={{1,16},{3,18},{5,20},{7,22},{9,24},{11,26},{13,28},{15,30},{16,1},... | collective-permute-start | bytes 4128776 | tf_op jit(solution)/shard_map/ppermute | solution.py:713
  33.8 10.9 %collective-permute-start.1 = (bf16[512,768]{1,0:T(8,128)(2,1)S(1)}, bf16[512,768]{1,0:T(8,128)(2,1)S(1)}, u32[]{:S(2)}, u32[]{:S(2)}) collective-permute-start(bf16[512,768]{1,0:T(8,128)(2,1)S(1)} %broadcast_select_fusion.1), channel_id=1, source_target_pairs={{0,1},{1,0},{2,3},{3,2},{4,5},{5,4},{6,7},{7,6},{8,9},{9,8},{10,11... | collective-permute-start | bytes 2359304 | tf_op jit(solution)/shard_map/ppermute | solution.py:736
  33.9 12.6 %copy-start.8 = (bf16[3,384,384]{2,1,0:T(8,128)(2,1)}, bf16[3,384,384]{2,1,0:T(8,128)(2,1)S(1)}, u32[]{:S(2)}) copy-start(bf16[3,384,384]{2,1,0:T(8,128)(2,1)S(1)} %collective-permute-done.3.w_near) | copy-start | bytes 2654212
  33.9 13.8 %collective-permute-start.4 = (bf16[3,384,384]{2,1,0:T(8,128)(2,1)S(1)}, bf16[3,384,384]{2,1,0:T(8,128)(2,1)S(1)}, u32[]{:S(2)}, u32[]{:S(2)}) collective-permute-start(bf16[3,384,384]{2,1,0:T(8,128)(2,1)S(1)} %collective-permute-done.3.w_near), channel_id=1, source_target_pairs={{1,3},{3,1},{5,7},{7,5},{9,11},{11,9},{13,15},{15,13},{16,18},{18,... | collective-permute-start | bytes 2654216 | tf_op jit(solution)/shard_map/ppermute | solution.py:728
  41.9 40.0 %collective-permute-start.8 = (bf16[1536,768]{1,0:T(8,128)(2,1)}, bf16[1536,768]{1,0:T(8,128)(2,1)}, u32[]{:S(2)}, u32[]{:S(2)}) collective-permute-start(bf16[1536,768]{1,0:T(8,128)(2,1)} %pad_maximum_fusion), channel_id=1, source_target_pairs={{1,16},{3,18},{5,20},{7,22},{9,24},{11,26},{13,28},{15,30},{16,1},... | collective-permute-start | bytes 7077896 | tf_op jit(solution)/shard_map/ppermute | solution.py:713
  57.6 17.0 %copy-start.32 = (bf16[1,512,768]{2,1,0:T(8,128)(2,1)S(1)}, bf16[1,512,768]{2,1,0:T(8,128)(2,1)}, u32[]{:S(2)}) copy-start(bf16[1,512,768]{2,1,0:T(8,128)(2,1)} %param.15) | copy-start | bytes 2359300
  57.6 17.0 %copy-start.34 = (bf16[384,768]{1,0:T(8,128)(2,1)S(1)}, bf16[384,768]{1,0:T(8,128)(2,1)}, u32[]{:S(2)}) copy-start(bf16[384,768]{1,0:T(8,128)(2,1)} %param.21) | copy-start | bytes 1769476
  70.6 5.7 %copy-start.12 = (bf16[1024,384]{1,0:T(8,128)(2,1)S(1)}, bf16[1024,384]{1,0:T(8,128)(2,1)}, u32[]{:S(2)}) copy-start(bf16[1024,384]{1,0:T(8,128)(2,1)} %get-tuple-element.110.mixed_ref) | copy-start | bytes 2359300
  70.6 31.4 %collective-permute-start.9 = (bf16[1536,768]{1,0:T(8,128)(2,1)}, bf16[1536,768]{1,0:T(8,128)(2,1)}, u32[]{:S(2)}, u32[]{:S(2)}) collective-permute-start(bf16[1536,768]{1,0:T(8,128)(2,1)} %pad_maximum_fusion.1), channel_id=1, source_target_pairs={{1,16},{3,18},{5,20},{7,22},{9,24},{11,26},{13,28},{15,30},{16,1},... | collective-permute-start | bytes 7077896 | tf_op jit(solution)/shard_map/ppermute | solution.py:713
  77.3 4.6 %collective-permute-start.6 = (bf16[1024,768]{1,0:T(8,128)(2,1)S(1)}, bf16[1024,768]{1,0:T(8,128)(2,1)}, u32[]{:S(2)}, u32[]{:S(2)}) collective-permute-start(bf16[1024,768]{1,0:T(8,128)(2,1)S(1)} %convolution_convert_fusion.refs_3_), channel_id=1, source_target_pairs={{0,1},{1,0},{2,3},{3,2},{4,5},{5,4},{6,7},{7,6},{8,9},{9,8},{10,11... | collective-permute-start | bytes 4718600 | tf_op jit(solution)/shard_map/ppermute | solution.py:736
  77.4 4.4 %collective-permute-start.7 = (bf16[512,768]{1,0:T(8,128)(2,1)S(1)}, bf16[512,768]{1,0:T(8,128)(2,1)S(1)}, u32[]{:S(2)}, u32[]{:S(2)}) collective-permute-start(bf16[512,768]{1,0:T(8,128)(2,1)S(1)} %slice.53.refs_5_), channel_id=1, source_target_pairs={{0,1},{1,0},{2,3},{3,2},{4,5},{5,4},{6,7},{7,6},{8,9},{9,8},{10,11... | collective-permute-start | bytes 2359304 | tf_op jit(solution)/shard_map/ppermute | solution.py:736
  102.1 96.9 %reduce-scatter.8.cloned.1.call-start = ((), (), s32[]{:S(2)}) async-start(), calls=%async_computation.4 | async-start | bytes 737280 | tf_op jit(solution)/shard_map/reduce_scatter | solution.py:763
  102.1 22.4 %copy-start.2 = (bf16[1024,768]{1,0:T(8,128)(2,1)S(1)}, bf16[1024,768]{1,0:T(8,128)(2,1)}, u32[]{:S(2)}) copy-start(bf16[1024,768]{1,0:T(8,128)(2,1)} %get-tuple-element.137.refs_3_.cot_ref) | copy-start | bytes 4718596
  102.2 22.4 %copy-start.24 = (f32[4,768]{1,0:T(4,128)S(1)}, f32[4,768]{1,0:T(4,128)}, u32[]{:S(2)}) copy-start(f32[4,768]{1,0:T(4,128)} %pad_maximum_fusion.5.vectors.refs_7_) | copy-start | bytes 36868
  102.2 22.4 %copy-start.27 = (s32[4]{0:T(128)S(1)}, s32[4]{0:T(128)}, u32[]{:S(2)}) copy-start(s32[4]{0:T(128)} %pad_add_fusion.flags.refs_0_) | copy-start | bytes 52
  118.6 5.9 %collective-permute-start.10 = (bf16[1024,768]{1,0:T(8,128)(2,1)}, bf16[1024,768]{1,0:T(8,128)(2,1)S(1)}, u32[]{:S(2)}, u32[]{:S(2)}) collective-permute-start(bf16[1024,768]{1,0:T(8,128)(2,1)} %get-tuple-element.121.back_own), channel_id=1, source_target_pairs={{0,1},{1,0},{2,3},{3,2},{4,5},{5,4},{6,7},{7,6},{8,9},{9,8},{10,11... | collective-permute-start | bytes 4718600 | tf_op jit(solution)/shard_map/ppermute | solution.py:736
  118.8 36.9 %collective-permute-start.12 = (bf16[768,384]{1,0:T(8,128)(2,1)}, bf16[768,384]{1,0:T(8,128)(2,1)}, u32[]{:S(2)}, u32[]{:S(2)}) collective-permute-start(bf16[768,384]{1,0:T(8,128)(2,1)} %get-tuple-element.126), channel_id=1, source_target_pairs={{0,1},{1,17},{2,3},{3,19},{4,5},{5,21},{6,7},{7,23},{8,9},{9,25},{... | collective-permute-start | bytes 1769480 | tf_op jit(solution)/shard_map/ppermute | solution.py:717
  119.7 36.0 %collective-permute-start.13 = (bf16[768,384]{1,0:T(8,128)(2,1)}, bf16[768,384]{1,0:T(8,128)(2,1)}, u32[]{:S(2)}, u32[]{:S(2)}) collective-permute-start(bf16[768,384]{1,0:T(8,128)(2,1)} %get-tuple-element.127), channel_id=1, source_target_pairs={{0,2},{1,18},{2,0},{3,16},{4,6},{5,22},{6,4},{7,20},{8,10},{9,26},... | collective-permute-start | bytes 1769480 | tf_op jit(solution)/shard_map/ppermute | solution.py:717
  121.8 34.0 %collective-permute-start.14 = (bf16[768,384]{1,0:T(8,128)(2,1)}, bf16[768,384]{1,0:T(8,128)(2,1)}, u32[]{:S(2)}, u32[]{:S(2)}) collective-permute-start(bf16[768,384]{1,0:T(8,128)(2,1)} %get-tuple-element.128), channel_id=1, source_target_pairs={{0,3},{1,19},{2,1},{3,17},{4,7},{5,23},{6,5},{7,21},{8,11},{9,27},... | collective-permute-start | bytes 1769480 | tf_op jit(solution)/shard_map/ppermute | solution.py:717
  121.8 34.0 %collective-permute-start.11 = (bf16[768,384]{1,0:T(8,128)(2,1)}, bf16[768,384]{1,0:T(8,128)(2,1)}, u32[]{:S(2)}, u32[]{:S(2)}) collective-permute-start(bf16[768,384]{1,0:T(8,128)(2,1)} %get-tuple-element.125), channel_id=1, source_target_pairs={{1,16},{3,18},{5,20},{7,22},{9,24},{11,26},{13,28},{15,30},{16,1},... | collective-permute-start | bytes 1769480 | tf_op jit(solution)/shard_map/ppermute | solution.py:717
  155.8 65.3 %reduce-scatter.6.cloned.1.call-start = ((), (), s32[]{:S(2)}) async-start(), calls=%async_computation.3 | async-start | bytes 737280 | tf_op jit(solution)/shard_map/reduce_scatter | solution.py:763
  162.9 32.1 %collective-permute-start.15 = (bf16[768,384]{1,0:T(8,128)(2,1)}, bf16[768,384]{1,0:T(8,128)(2,1)}, u32[]{:S(2)}, u32[]{:S(2)}) collective-permute-start(bf16[768,384]{1,0:T(8,128)(2,1)} %get-tuple-element.132), channel_id=1, source_target_pairs={{1,16},{3,18},{5,20},{7,22},{9,24},{11,26},{13,28},{15,30},{16,1},... | collective-permute-start | bytes 1769480 | tf_op jit(solution)/shard_map/ppermute | solution.py:717
  165.9 24.5 %collective-permute-start.16 = (bf16[768,384]{1,0:T(8,128)(2,1)}, bf16[768,384]{1,0:T(8,128)(2,1)}, u32[]{:S(2)}, u32[]{:S(2)}) collective-permute-start(bf16[768,384]{1,0:T(8,128)(2,1)} %get-tuple-element.145), channel_id=1, source_target_pairs={{0,1},{1,17},{2,3},{3,19},{4,5},{5,21},{6,7},{7,23},{8,9},{9,25},{... | collective-permute-start | bytes 1769480 | tf_op jit(solution)/shard_map/ppermute | solution.py:717
  165.9 24.5 %collective-permute-start.17 = (bf16[768,384]{1,0:T(8,128)(2,1)}, bf16[768,384]{1,0:T(8,128)(2,1)}, u32[]{:S(2)}, u32[]{:S(2)}) collective-permute-start(bf16[768,384]{1,0:T(8,128)(2,1)} %get-tuple-element.146), channel_id=1, source_target_pairs={{0,2},{1,18},{2,0},{3,16},{4,6},{5,22},{6,4},{7,20},{8,10},{9,26},... | collective-permute-start | bytes 1769480 | tf_op jit(solution)/shard_map/ppermute | solution.py:717
  167.6 27.4 %collective-permute-start.18 = (bf16[768,384]{1,0:T(8,128)(2,1)}, bf16[768,384]{1,0:T(8,128)(2,1)}, u32[]{:S(2)}, u32[]{:S(2)}) collective-permute-start(bf16[768,384]{1,0:T(8,128)(2,1)} %get-tuple-element.147), channel_id=1, source_target_pairs={{0,3},{1,19},{2,1},{3,17},{4,7},{5,23},{6,5},{7,21},{8,11},{9,27},... | collective-permute-start | bytes 1769480 | tf_op jit(solution)/shard_map/ppermute | solution.py:717
  175.7 7.0 %copy-start.3 = (bf16[1024,768]{1,0:T(8,128)(2,1)S(1)}, bf16[1024,768]{1,0:T(8,128)(2,1)}, u32[]{:S(2)}) copy-start(bf16[1024,768]{1,0:T(8,128)(2,1)} %get-tuple-element.137.refs_3_.cot_ref) | copy-start | bytes 4718596
  175.7 7.0 %copy-start.7 = (bf16[1024,768]{1,0:T(8,128)(2,1)S(1)}, bf16[1024,768]{1,0:T(8,128)(2,1)}, u32[]{:S(2)}) copy-start(bf16[1024,768]{1,0:T(8,128)(2,1)} %get-tuple-element.114.resid_ref) | copy-start | bytes 4718596
  175.7 7.0 %copy-start.16 = (bf16[1024,768]{1,0:T(8,128)(2,1)S(1)}, bf16[1024,768]{1,0:T(8,128)(2,1)}, u32[]{:S(2)}) copy-start(bf16[1024,768]{1,0:T(8,128)(2,1)} %get-tuple-element.135.act_early) | copy-start | bytes 4718596
  175.7 7.0 %copy-start.17 = (bf16[1024,768]{1,0:T(8,128)(2,1)S(1)}, bf16[1024,768]{1,0:T(8,128)(2,1)}, u32[]{:S(2)}) copy-start(bf16[1024,768]{1,0:T(8,128)(2,1)} %get-tuple-element.136.act_late) | copy-start | bytes 4718596
  175.7 7.0 %copy-start.18 = (bf16[768,768]{1,0:T(8,128)(2,1)S(1)}, bf16[768,768]{1,0:T(8,128)(2,1)}, u32[]{:S(2)}) copy-start(bf16[768,768]{1,0:T(8,128)(2,1)} %get-tuple-element.138.early_ref) | copy-start | bytes 3538948
  184.0 12.1 %copy-start.38 = (bf16[768,384]{1,0:T(8,128)(2,1)S(1)}, bf16[768,384]{1,0:T(8,128)(2,1)}, u32[]{:S(2)}) copy-start(bf16[768,384]{1,0:T(8,128)(2,1)} %get-tuple-element.132) | copy-start | bytes 1769476
  195.1 3.9 %collective-permute-start.19 = (bf16[256,768]{1,0:T(8,128)(2,1)}, bf16[256,768]{1,0:T(8,128)(2,1)S(1)}, u32[]{:S(2)}, u32[]{:S(2)}) collective-permute-start(bf16[256,768]{1,0:T(8,128)(2,1)} %get-tuple-element.155), channel_id=1, source_target_pairs={{0,1},{1,0},{2,3},{3,2},{4,5},{5,4},{6,7},{7,6},{8,9},{9,8},{10,11... | collective-permute-start | bytes 1179656 | tf_op jit(solution)/shard_map/ppermute | solution.py:736
  195.1 6.3 %collective-permute-start.20 = (bf16[256,768]{1,0:T(8,128)(2,1)}, bf16[256,768]{1,0:T(8,128)(2,1)S(1)}, u32[]{:S(2)}, u32[]{:S(2)}) collective-permute-start(bf16[256,768]{1,0:T(8,128)(2,1)} %get-tuple-element.156), channel_id=1, source_target_pairs={{0,1},{1,0},{2,3},{3,2},{4,5},{5,4},{6,7},{7,6},{8,9},{9,8},{10,11... | collective-permute-start | bytes 1179656 | tf_op jit(solution)/shard_map/ppermute | solution.py:736
  195.6 7.9 %collective-permute-start.21 = (bf16[256,768]{1,0:T(8,128)(2,1)S(1)}, bf16[256,768]{1,0:T(8,128)(2,1)S(1)}, u32[]{:S(2)}, u32[]{:S(2)}) collective-permute-start(bf16[256,768]{1,0:T(8,128)(2,1)S(1)} %get-tuple-element.157), channel_id=1, source_target_pairs={{0,1},{1,0},{2,3},{3,2},{4,5},{5,4},{6,7},{7,6},{8,9},{9,8},{10,11... | collective-permute-start | bytes 1179656 | tf_op jit(solution)/shard_map/ppermute | solution.py:736
  195.7 12.6 %collective-permute-start.22 = (bf16[256,768]{1,0:T(8,128)(2,1)S(1)}, bf16[256,768]{1,0:T(8,128)(2,1)S(1)}, u32[]{:S(2)}, u32[]{:S(2)}) collective-permute-start(bf16[256,768]{1,0:T(8,128)(2,1)S(1)} %get-tuple-element.158), channel_id=1, source_target_pairs={{0,1},{1,0},{2,3},{3,2},{4,5},{5,4},{6,7},{7,6},{8,9},{9,8},{10,11... | collective-permute-start | bytes 1179656 | tf_op jit(solution)/shard_map/ppermute | solution.py:736
  198.8 22.3 %collective-permute-start.29 = (bf16[192,384]{1,0:T(8,128)(2,1)}, bf16[192,384]{1,0:T(8,128)(2,1)S(1)}, u32[]{:S(2)}, u32[]{:S(2)}) collective-permute-start(bf16[192,384]{1,0:T(8,128)(2,1)} %get-tuple-element.234), channel_id=1, source_target_pairs={{0,12},{4,0},{8,4},{12,8},{1,13},{5,1},{9,5},{13,9},{2,14},{6,2},{... | collective-permute-start | bytes 442376 | tf_op jit(solution)/shard_map/ppermute | solution.py:775
  199.0 9.3 %copy-start.39 = (bf16[256,768]{1,0:T(8,128)(2,1)}, bf16[256,768]{1,0:T(8,128)(2,1)S(1)}, u32[]{:S(2)}) copy-start(bf16[256,768]{1,0:T(8,128)(2,1)S(1)} %collective-permute-done.19.got_first) | copy-start | bytes 1179652
  199.0 22.1 %collective-permute-start.28 = (bf16[192,384]{1,0:T(8,128)(2,1)S(1)}, bf16[192,384]{1,0:T(8,128)(2,1)S(1)}, u32[]{:S(2)}, u32[]{:S(2)}) collective-permute-start(bf16[192,384]{1,0:T(8,128)(2,1)S(1)} %get-tuple-element.235), channel_id=1, source_target_pairs={{0,8},{4,12},{8,0},{12,4},{1,9},{5,13},{9,1},{13,5},{2,10},{6,14},... | collective-permute-start | bytes 442376 | tf_op jit(solution)/shard_map/ppermute | solution.py:775
  201.4 6.8 %copy-start.40 = (bf16[256,768]{1,0:T(8,128)(2,1)}, bf16[256,768]{1,0:T(8,128)(2,1)S(1)}, u32[]{:S(2)}) copy-start(bf16[256,768]{1,0:T(8,128)(2,1)S(1)} %collective-permute-done.20.got_second) | copy-start | bytes 1179652
  201.4 19.7 %collective-permute-start.27 = (bf16[192,384]{1,0:T(8,128)(2,1)S(1)}, bf16[192,384]{1,0:T(8,128)(2,1)S(1)}, u32[]{:S(2)}, u32[]{:S(2)}) collective-permute-start(bf16[192,384]{1,0:T(8,128)(2,1)S(1)} %get-tuple-element.236), channel_id=1, source_target_pairs={{0,4},{4,8},{8,12},{12,0},{1,5},{5,9},{9,13},{13,1},{2,6},{6,10},{... | collective-permute-start | bytes 442376 | tf_op jit(solution)/shard_map/ppermute | solution.py:775
  203.5 17.6 %collective-permute-start.26 = (bf16[192,384]{1,0:T(8,128)(2,1)}, bf16[192,384]{1,0:T(8,128)(2,1)S(1)}, u32[]{:S(2)}, u32[]{:S(2)}) collective-permute-start(bf16[192,384]{1,0:T(8,128)(2,1)} %reduce-scatter.8.cloned.1.call-done.early_own), channel_id=1, source_target_pairs={{1,16},{3,18},{5,20},{7,22},{9,24},{11,26},{13,28},{15,30},{16,1},... | collective-permute-start | bytes 442376 | tf_op jit(solution)/shard_map/ppermute | solution.py:713
  209.0 12.1 %copy-start.25 = (bf16[192,384]{1,0:T(8,128)(2,1)S(1)}, bf16[192,384]{1,0:T(8,128)(2,1)}, u32[]{:S(2)}) copy-start(bf16[192,384]{1,0:T(8,128)(2,1)} %reduce-scatter.8.cloned.1.call-done.early_own) | copy-start | bytes 442372
  209.0 12.2 %copy-start.29 = (s32[4]{0:T(128)S(1)}, s32[4]{0:T(128)}, u32[]{:S(2)}) copy-start(s32[4]{0:T(128)} %pad_add_fusion.flags.refs_0_) | copy-start | bytes 52
  214.3 9.0 %copy-start.5 = (bf16[2,512,768]{2,1,0:T(8,128)(2,1)S(1)}, bf16[2,512,768]{2,1,0:T(8,128)(2,1)}, u32[]{:S(2)}) copy-start(bf16[2,512,768]{2,1,0:T(8,128)(2,1)} %shard_map.230.own_ref) | copy-start | bytes 4718596
  214.3 2.9 %collective-permute-start.24 = (f32[9,768]{1,0:T(8,128)S(1)}, f32[9,768]{1,0:T(8,128)S(1)}, u32[]{:S(2)}, u32[]{:S(2)}) collective-permute-start(f32[9,768]{1,0:T(8,128)S(1)} %pad_maximum_fusion.4), channel_id=1, source_target_pairs={{0,16},{16,0},{1,17},{17,1},{2,18},{18,2},{3,19},{19,3},{4,20},{20... | collective-permute-start | bytes 82952 | tf_op jit(solution)/shard_map/ppermute | solution.py:783
  217.3 3.8 %collective-permute-start.25 = (f32[9,768]{1,0:T(8,128)S(1)}, f32[9,768]{1,0:T(8,128)S(1)}, u32[]{:S(2)}, u32[]{:S(2)}) collective-permute-start(f32[9,768]{1,0:T(8,128)S(1)} %add.88), channel_id=1, source_target_pairs={{0,2},{2,0},{1,3},{3,1},{4,6},{6,4},{5,7},{7,5},{8,10},{10,8},{9,1... | collective-permute-start | bytes 82952 | tf_op jit(solution)/shard_map/ppermute | solution.py:783
  222.1 15.9 %copy-start.30 = (f32[5]{0:T(128)S(1)}, f32[5]{0:T(128)}, u32[]{:S(2)}) copy-start(f32[5]{0:T(128)} %weight_ref.1) | copy-start | bytes 64
  222.7 13.0 %collective-permute-start.30 = (bf16[192,1152]{1,0:T(8,128)(2,1)S(1)}, bf16[192,1152]{1,0:T(8,128)(2,1)S(1)}, u32[]{:S(2)}, u32[]{:S(2)}) collective-permute-start(bf16[192,1152]{1,0:T(8,128)(2,1)S(1)} %shard_map.231), channel_id=1, source_target_pairs={{0,2},{2,0},{1,3},{3,1},{4,6},{6,4},{5,7},{7,5},{8,10},{10,8},{9,1... | collective-permute-start | bytes 1327112 | tf_op jit(solution)/shard_map/ppermute | solution.py:732
  223.3 21.9 %collective-permute-start.23 = (bf16[2,512,768]{2,1,0:T(8,128)(2,1)S(1)}, bf16[2,512,768]{2,1,0:T(8,128)(2,1)S(1)}, u32[]{:S(2)}, u32[]{:S(2)}) collective-permute-start(bf16[2,512,768]{2,1,0:T(8,128)(2,1)S(1)} %copy-done.5), channel_id=1, source_target_pairs={{1,16},{3,18},{5,20},{7,22},{9,24},{11,26},{13,28},{15,30},{16,1},... | collective-permute-start | bytes 4718600 | tf_op jit(solution)/shard_map/ppermute | solution.py:713
  227.2 1.3 collective-permute-start.31
  228.5 3.3 %collective-permute-start.32 = (f32[9,768]{1,0:T(8,128)S(1)}, f32[9,768]{1,0:T(8,128)S(1)}, u32[]{:S(2)}, u32[]{:S(2)}) collective-permute-start(f32[9,768]{1,0:T(8,128)S(1)} %add.100), channel_id=1, source_target_pairs={{0,4},{4,0},{8,12},{12,8},{1,5},{5,1},{9,13},{13,9},{2,6},{6,2},{1... | collective-permute-start | bytes 82952 | tf_op jit(solution)/shard_map/ppermute | solution.py:783
  231.8 3.9 %collective-permute-start.33 = (f32[9,768]{1,0:T(8,128)S(1)}, f32[9,768]{1,0:T(8,128)S(1)}, u32[]{:S(2)}, u32[]{:S(2)}) collective-permute-start(f32[9,768]{1,0:T(8,128)S(1)} %add.101), channel_id=1, source_target_pairs={{0,8},{4,12},{8,0},{12,4},{1,9},{5,13},{9,1},{13,5},{2,10},{6,14},... | collective-permute-start | bytes 82952 | tf_op jit(solution)/shard_map/ppermute | solution.py:783
  235.7 9.5 %copy-start.13 = (f32[512,768]{1,0:T(8,128)S(1)}, f32[512,768]{1,0:T(8,128)}, u32[]{:S(2)}) copy-start(f32[512,768]{1,0:T(8,128)} %get-tuple-element.102.part_ref) | copy-start | bytes 4718596
  235.9 4.6 %collective-permute-start.34 = (bf16[2,192,1152]{2,1,0:T(8,128)(2,1)S(1)}, bf16[2,192,1152]{2,1,0:T(8,128)(2,1)S(1)}, u32[]{:S(2)}, u32[]{:S(2)}) collective-permute-start(bf16[2,192,1152]{2,1,0:T(8,128)(2,1)S(1)} %pad_maximum_fusion.3.here_ref), channel_id=1, source_target_pairs={{0,1},{1,0},{2,3},{3,2},{4,5},{5,4},{6,7},{7,6},{8,9},{9,8},{10,11... | collective-permute-start | bytes 2654216 | tf_op jit(solution)/shard_map/ppermute | solution.py:736
  (23 other events, 50.9 us)
Sparse Core Ops, SparseCore 0:
  102.2 46.5 reduce-scatter.9
  155.9 18.1 reduce-scatter.7
  176.5 20.2 reduce-scatter.5
